TPU v7x, 32 devices: a whole 2x2x4 slice. The times are simulated.
32 devices in a mesh: dp: 2 (over y), row: 4 (over z), col: 4 (over x, core).
Axes of the slice: x: 2, y: 2, z: 4, core: 2. Of those that a mesh axis runs over, the one named last changes fastest.
Arguments:
- inputs: bfloat16 [18464, 1024], P(('dp', 'row'), 'col'), may hold values from -30 to 30
- query_weight: bfloat16 [1024, 1024], P('row', 'col'), may hold values from -7 to 7
- key_weight: bfloat16 [1024, 1024], P('row', 'col'), may hold values from -7 to 7
- value_weight: bfloat16 [1024, 1024], P('row', 'col'), may hold values from -0.1875 to 0.1875
- query_bias: float32 [1024], P('col'), may hold values from -3 to 3
- value_bias: float32 [1024], P('col'), may hold values from -0.3 to 0.3
- out_weight: bfloat16 [1024, 1024], P('col', 'row'), may hold values from -1.5 to 1.5
- out_bias: float32 [1024], P('col'), may hold values from -3 to 3
- up_weight: bfloat16 [1024, 4096], P('row', 'col'), may hold values from -0.1875 to 0.1875
- up_bias: float32 [4096], P('col'), may hold values from -3 to 3
- down_weight: bfloat16 [4096, 1024], P('col', 'row'), may hold values from -0.09375 to 0.09375
- down_bias: float32 [1024], P('col'), may hold values from -3 to 3
- first_gain: float32 [1024], P('col'), may hold values from 0.1 to 1.9
- first_shift: float32 [1024], P('col'), may hold values from -2 to 2
- second_gain: float32 [1024], P('col'), may hold values from 0.1 to 1.9
- second_shift: float32 [1024], P('col'), may hold values from -2 to 2
- cotangent: bfloat16 [18464, 1024], P(('dp', 'row'), 'col'), may hold values from -6 to 6
Outputs:
- outputs: bfloat16 [18464, 1024], P(('dp', 'row'), 'col')
- input_grad: float32 [18464, 1024], P(('dp', 'row'), 'col')
- query_weight_grad: float32 [1024, 1024], P('row', 'col')
- key_weight_grad: float32 [1024, 1024], P('row', 'col')
- value_weight_grad: float32 [1024, 1024], P('row', 'col')
- query_bias_grad: float32 [1024], P('col')
- value_bias_grad: float32 [1024], P('col')
- out_weight_grad: float32 [1024, 1024], P('col', 'row')
- out_bias_grad: float32 [1024], P('col')
- up_weight_grad: float32 [1024, 4096], P('row', 'col')
- up_bias_grad: float32 [4096], P('col')
- down_weight_grad: float32 [4096, 1024], P('col', 'row')
- down_bias_grad: float32 [1024], P('col')
- first_gain_grad: float32 [1024], P('col')
- first_shift_grad: float32 [1024], P('col')
- second_gain_grad: float32 [1024], P('col')
- second_shift_grad: float32 [1024], P('col')
All inputs are finite; a program needn't handle non-finite values.
Results may differ from a plain program's by a relative error of at most 0.012.
The roundings to bfloat16 on the way count: a program that leaves them out, or rounds other values in their place, can miss the bound.
Values may be sent and summed in bfloat16 or wider, within the bound.
No kernel may reach another device: no remote copies, remote signals or barrier semaphores. Data moves between devices by JAX's collectives and lax.ppermute only.
A program may use at most 192 MiB of HBM per device.

v0:
```python
import jax
import jax.numpy as jnp
from jax import lax
from jax.sharding import PartitionSpec as P

D = 1024
HD = 64
SEQ = 577


def matmul(left_side, right_side):
    return jnp.dot(left_side, right_side, preferred_element_type=jnp.float32)


def matmul_tn(left_side, right_side):
    return lax.dot_general(
        left_side, right_side, (((0,), (0,)), ((), ())), preferred_element_type=jnp.float32
    )


def matmul_nt(left_side, right_side):
    return lax.dot_general(
        left_side, right_side, (((1,), (1,)), ((), ())), preferred_element_type=jnp.float32
    )


def feature_totals(first, second):
    return lax.psum(
        (jnp.sum(first, axis=1, keepdims=True), jnp.sum(second, axis=1, keepdims=True)), "col"
    )


def gather_normed(values):
    return lax.all_gather(values, "col", axis=1, tiled=True)


def gather_grads(values):
    return lax.all_gather(values, "col", axis=1, tiled=True)


def scatter_partial(values):
    return lax.psum_scatter(values, "col", scatter_dimension=1, tiled=True)


def norm_forward(inputs_rows, gain_vector, shift_vector):
    row_total, squares = feature_totals(inputs_rows, inputs_rows * inputs_rows)
    middle = row_total / D
    spread = squares / D - middle * middle
    scaled = lax.rsqrt(spread + 1e-06)
    centred = (inputs_rows - middle) * scaled
    return (centred * gain_vector + shift_vector, centred, scaled)


def norm_backward(upstream, gain_vector, centred, scaled):
    dcentred = upstream * gain_vector
    first, second = feature_totals(dcentred, dcentred * centred)
    return scaled * (dcentred - first / D - centred * second / D)


def attend_image(operands):
    query_rows, key_rows, value_rows = operands
    scores = (
        jnp.einsum("qhd,khd->hqk", query_rows, key_rows, preferred_element_type=jnp.float32) * 0.125
    )
    row_peak = jnp.max(scores, axis=-1, keepdims=True)
    exponent = jnp.exp(scores - row_peak)
    row_total = jnp.sum(exponent, axis=-1, keepdims=True)
    soft_weights = (exponent / row_total).astype(jnp.bfloat16)
    mixed_rows = jnp.einsum(
        "hqk,khd->qhd", soft_weights, value_rows, preferred_element_type=jnp.float32
    )
    return (mixed_rows.astype(jnp.bfloat16), row_peak + jnp.log(row_total))


def attend_back(operands):
    query_rows, key_rows, value_rows, grad_rows, logsum = operands
    scores = (
        jnp.einsum("qhd,khd->hqk", query_rows, key_rows, preferred_element_type=jnp.float32) * 0.125
    )
    soft_weights = jnp.exp(scores - logsum)
    dprobs = jnp.einsum("qhd,khd->hqk", grad_rows, value_rows, preferred_element_type=jnp.float32)
    dvalues = jnp.einsum(
        "hqk,qhd->khd",
        soft_weights.astype(jnp.bfloat16),
        grad_rows,
        preferred_element_type=jnp.float32,
    )
    row_dot = jnp.sum(soft_weights * dprobs, axis=-1, keepdims=True)
    dscores = (soft_weights * (dprobs - row_dot)).astype(jnp.bfloat16)
    dqueries = (
        jnp.einsum("hqk,khd->qhd", dscores, key_rows, preferred_element_type=jnp.float32) * 0.125
    )
    key_grads = (
        jnp.einsum("hqk,qhd->khd", dscores, query_rows, preferred_element_type=jnp.float32) * 0.125
    )
    return (
        dqueries.astype(jnp.bfloat16),
        key_grads.astype(jnp.bfloat16),
        dvalues.astype(jnp.bfloat16),
    )


def gelu_exact(values):
    return jax.nn.gelu(values, approximate=False)


def local(
    inputs,
    query_weight,
    key_weight,
    value_weight,
    query_bias,
    value_bias,
    out_weight,
    out_bias,
    up_weight,
    up_bias,
    down_weight,
    down_bias,
    first_gain,
    first_shift,
    second_gain,
    second_shift,
    cotangent,
):
    tokens_here = inputs.shape[0]
    feature_width = inputs.shape[1]
    images = tokens_here // SEQ
    heads_here = feature_width // HD
    head_shape = (images, SEQ, heads_here, HD)
    residual = inputs.astype(jnp.float32)
    query_full, key_full, value_full, out_full, up_full, down_full = (
        lax.all_gather(query_weight, "row", axis=0, tiled=True),
        lax.all_gather(key_weight, "row", axis=0, tiled=True),
        lax.all_gather(value_weight, "row", axis=0, tiled=True),
        lax.all_gather(out_weight, "row", axis=1, tiled=True),
        lax.all_gather(up_weight, "row", axis=0, tiled=True),
        lax.all_gather(down_weight, "row", axis=1, tiled=True),
    )
    normed_one, centred_one, scaled_one = norm_forward(residual, first_gain, first_shift)
    wide_one = gather_normed(normed_one.astype(jnp.bfloat16))
    queries = (matmul(wide_one, query_full) + query_bias).astype(jnp.bfloat16)
    key_rows = matmul(wide_one, key_full).astype(jnp.bfloat16)
    values = (matmul(wide_one, value_full) + value_bias).astype(jnp.bfloat16)
    query_heads = queries.reshape(head_shape)
    key_heads = key_rows.reshape(head_shape)
    value_heads = values.reshape(head_shape)
    attended, logsums = lax.map(attend_image, (query_heads, key_heads, value_heads))
    attended = attended.reshape(tokens_here, feature_width)
    branch_attn = (
        lax.psum_scatter(matmul(attended, out_full), "col", scatter_dimension=1, tiled=True)
        + out_bias
    )
    middle_sum = residual + branch_attn
    normed_two, centred_two, scaled_two = norm_forward(middle_sum, second_gain, second_shift)
    wide_two = gather_normed(normed_two.astype(jnp.bfloat16))
    up_values = matmul(wide_two, up_full) + up_bias
    gelu_value, gelu_back = jax.vjp(gelu_exact, up_values)
    hidden = gelu_value.astype(jnp.bfloat16)
    branch_mlp = (
        lax.psum_scatter(
            matmul(hidden, down_full).astype(jnp.bfloat16), "col", scatter_dimension=1, tiled=True
        ).astype(jnp.float32)
        + down_bias
    )
    outputs = (middle_sum + branch_mlp).astype(jnp.bfloat16)
    grad_top = cotangent.astype(jnp.float32)
    down_bias_grad = jnp.sum(grad_top, axis=0)
    wide_grad = gather_grads(cotangent)
    down_grad_full = matmul_tn(hidden, wide_grad)
    hidden_grad = matmul_nt(wide_grad, down_full)
    pre_grad = gelu_back(hidden_grad)[0].astype(jnp.bfloat16)
    up_bias_grad = jnp.sum(pre_grad.astype(jnp.float32), axis=0)
    up_grad_full = matmul_tn(wide_two, pre_grad)
    normed_grad_two = scatter_partial(matmul_nt(pre_grad, up_full))
    second_gain_grad = jnp.sum(normed_grad_two * centred_two, axis=0)
    second_shift_grad = jnp.sum(normed_grad_two, axis=0)
    middle_grad = grad_top + norm_backward(normed_grad_two, second_gain, centred_two, scaled_two)
    attn_grad = middle_grad.astype(jnp.bfloat16)
    out_bias_grad = jnp.sum(attn_grad.astype(jnp.float32), axis=0)
    wide_attn_grad = gather_grads(attn_grad)
    out_grad_full = matmul_tn(attended, wide_attn_grad)
    head_grad = matmul_nt(wide_attn_grad, out_full).astype(jnp.bfloat16)
    dqueries, key_grads, dvalues = lax.map(
        attend_back, (query_heads, key_heads, value_heads, head_grad.reshape(head_shape), logsums)
    )
    dqueries = dqueries.reshape(tokens_here, feature_width)
    key_grads = key_grads.reshape(tokens_here, feature_width)
    dvalues = dvalues.reshape(tokens_here, feature_width)
    query_bias_grad = jnp.sum(dqueries.astype(jnp.float32), axis=0)
    value_bias_grad = jnp.sum(dvalues.astype(jnp.float32), axis=0)
    query_grad_full = matmul_tn(wide_one, dqueries)
    key_grad_full = matmul_tn(wide_one, key_grads)
    value_grad_full = matmul_tn(wide_one, dvalues)
    partial_one = (
        matmul_nt(dqueries, query_full)
        + matmul_nt(key_grads, key_full)
        + matmul_nt(dvalues, value_full)
    )
    normed_grad_one = scatter_partial(partial_one)
    first_gain_grad = jnp.sum(normed_grad_one * centred_one, axis=0)
    first_shift_grad = jnp.sum(normed_grad_one, axis=0)
    input_grad = middle_grad + norm_backward(normed_grad_one, first_gain, centred_one, scaled_one)
    vectors = jnp.concatenate(
        [
            query_bias_grad,
            value_bias_grad,
            out_bias_grad,
            down_bias_grad,
            first_gain_grad,
            first_shift_grad,
            second_gain_grad,
            second_shift_grad,
            up_bias_grad,
        ]
    )
    summed = lax.psum(
        (
            query_grad_full,
            key_grad_full,
            value_grad_full,
            out_grad_full,
            up_grad_full,
            down_grad_full,
            vectors,
        ),
        ("dp", "row"),
    )
    row_index = lax.axis_index("row")
    query_grad = lax.dynamic_slice_in_dim(
        summed[0], row_index * query_weight.shape[0], query_weight.shape[0], 0
    )
    key_grad = lax.dynamic_slice_in_dim(
        summed[1], row_index * key_weight.shape[0], key_weight.shape[0], 0
    )
    value_grad = lax.dynamic_slice_in_dim(
        summed[2], row_index * value_weight.shape[0], value_weight.shape[0], 0
    )
    out_grad = lax.dynamic_slice_in_dim(
        summed[3], row_index * out_weight.shape[1], out_weight.shape[1], 1
    )
    up_grad = lax.dynamic_slice_in_dim(
        summed[4], row_index * up_weight.shape[0], up_weight.shape[0], 0
    )
    down_grad = lax.dynamic_slice_in_dim(
        summed[5], row_index * down_weight.shape[1], down_weight.shape[1], 1
    )
    vector_sums = summed[6]
    pieces = [
        vector_sums[feature_width * place : feature_width * (place + 1)] for place in range(8)
    ]
    up_bias_sum = vector_sums[8 * feature_width :]
    return (
        outputs,
        input_grad,
        query_grad,
        key_grad,
        value_grad,
        pieces[0],
        pieces[1],
        out_grad,
        pieces[2],
        up_grad,
        up_bias_sum,
        down_grad,
        pieces[3],
        pieces[4],
        pieces[5],
        pieces[6],
        pieces[7],
    )


def solution(mesh):
    in_specs = (
        P(("dp", "row"), "col"),
        P("row", "col"),
        P("row", "col"),
        P("row", "col"),
        P("col"),
        P("col"),
        P("col", "row"),
        P("col"),
        P("row", "col"),
        P("col"),
        P("col", "row"),
        P("col"),
        P("col"),
        P("col"),
        P("col"),
        P("col"),
        P(("dp", "row"), "col"),
    )
    out_specs = (
        P(("dp", "row"), "col"),
        P(("dp", "row"), "col"),
        P("row", "col"),
        P("row", "col"),
        P("row", "col"),
        P("col"),
        P("col"),
        P("col", "row"),
        P("col"),
        P("row", "col"),
        P("col"),
        P("col", "row"),
        P("col"),
        P("col"),
        P("col"),
        P("col"),
        P("col"),
    )
    return jax.shard_map(local, mesh=mesh, in_specs=in_specs, out_specs=out_specs, check_vma=False)
```

profile of v0, /device:TPU:0, one launch (start us, length us, event | category | flops | bytes accessed | tf_op | source)
XLA Modules:
  0.0 1232.9 jit_solution(17970794028962596964)
XLA Ops:
  10.2 12.9 %all-reduce.4 = (f32[2308,1]{0,1:T(1,128)S(1)}, f32[2308,1]{0,1:T(1,128)S(1)}) all-reduce(f32[2308,1]{0,1:T(1,128)S(1)} %broadcast_in_dim.57, f32[2308,1]{0,1:T(1,128)S(1)} %broadcast_in_dim.58), channel_id=1, replica_groups=mesh['dp'=2,'row'=4,'col'=4] {'col'}, use_global_device_ids=true, to_apply=%region_1.0 | all-reduce | flops 4616 | bytes 36928 | tf_op jit(solution)/shard_map/psum | solution.py:28
  23.9 3.2 fusion.71
  27.2 15.0 %all_gather.31 = bf16[1024,256]{1,0:T(8,128)(2,1)S(1)} all-gather(bf16[256,256]{1,0:T(8,128)(2,1)S(1)} %copy-done.27), channel_id=1, replica_groups=mesh['dp'=2,'row'=4,'col'=4] {'row'}, dimensions={0}, use_global_device_ids=true | all-gather | bytes 655360 | tf_op jit(solution)/shard_map/all_gather | solution.py:135
  42.2 17.4 %all_gather.32 = bf16[1024,256]{1,0:T(8,128)(2,1)S(1)} all-gather(bf16[256,256]{1,0:T(8,128)(2,1)S(1)} %copy-done.28), channel_id=1, replica_groups=mesh['dp'=2,'row'=4,'col'=4] {'row'}, dimensions={0}, use_global_device_ids=true | all-gather | bytes 655360 | tf_op jit(solution)/shard_map/all_gather | solution.py:133
  59.7 14.8 %all_gather.33 = bf16[1024,256]{1,0:T(8,128)(2,1)S(1)} all-gather(bf16[256,256]{1,0:T(8,128)(2,1)S(1)} %copy-done.29), channel_id=1, replica_groups=mesh['dp'=2,'row'=4,'col'=4] {'row'}, dimensions={0}, use_global_device_ids=true | all-gather | bytes 655360 | tf_op jit(solution)/shard_map/all_gather | solution.py:134
  74.5 15.8 %all_gather.34 = bf16[256,1024]{1,0:T(8,128)(2,1)} all-gather(bf16[256,256]{1,0:T(8,128)(2,1)S(1)} %copy-done.30), channel_id=1, replica_groups=mesh['dp'=2,'row'=4,'col'=4] {'row'}, dimensions={1}, use_global_device_ids=true | all-gather | bytes 655360 | tf_op jit(solution)/shard_map/all_gather | solution.py:136
  90.3 4.8 fusion.63
  95.0 3.8 reshape.104
  101.4 3.8 fusion.64
  107.5 3.2 copy.53
  110.7 3.8 convolution_convert_fusion.2
  116.8 3.2 copy.54
  121.2 23.7 %while.26 = (s32[]{:T(128)}, bf16[4,577,4,64]{1,3,2,0:T(8,128)(2,1)}, f32[4,4,577,1]{2,1,3,0:T(4,128)}, bf16[4,577,4,64]{1,3,2,0:T(8,128)(2,1)}, bf16[4,577,4,64...) while((s32[]{:T(128)}, bf16[4,577,4,64]{1,3,2,0:T(8,128)(2,1)}, ...), condition=%wide.region_7.8_spmd, body=%wide.region_4.7_spmd.sunk | while | flops 353050112 | bytes 17368812 | solution.py:148
  145.0 4.4 copy.55
  149.3 3.9 reshape.96
  153.3 6.3 fusion.82
  160.3 78.4 %reduce-scatter.5.cloned.1.call-done = f32[2308,256]{1,0:T(8,128)} async-done(((f32[2308,1024]{1,0:T(8,128)}), f32[2308,256]{1,0:T(8,128)}) %reduce-scatter.5.cloned.1.call-update) | async-done | bytes 2363408 | tf_op jit(solution)/shard_map/reduce_scatter | solution.py:151
  241.2 10.2 all-reduce.3
  256.3 37.3 %all-gather.9.cloned.1.call-done = bf16[2308,1024]{1,0:T(8,128)(2,1)} async-done(((bf16[2308,256]{1,0:T(8,128)(2,1)}), bf16[2308,1024]{1,0:T(8,128)(2,1)}) %all-gather.9.cloned.1.call-update) | async-done | bytes 4726800 | tf_op jit(solution)/shard_map/all_gather | solution.py:34
  293.6 10.1 fusion.83
  303.7 37.5 %all-gather.13.cloned.1.call-done = bf16[1024,1024]{1,0:T(8,128)(2,1)} async-done(((bf16[1024,256]{1,0:T(8,128)(2,1)}), bf16[1024,1024]{1,0:T(8,128)(2,1)}) %all-gather.13.cloned.1.call-update) | async-done | bytes 2097168 | tf_op jit(solution)/shard_map/all_gather | solution.py:138
  341.2 37.8 %all-gather.15.cloned.1.call-done = bf16[2308,1024]{1,0:T(8,128)(2,1)} async-done(((bf16[2308,256]{1,0:T(8,128)(2,1)}), bf16[2308,1024]{1,0:T(8,128)(2,1)}) %all-gather.15.cloned.1.call-update) | async-done | bytes 4726800 | tf_op jit(solution)/shard_map/all_gather | solution.py:38
  379.0 32.0 %convert_reduce_fusion = (f32[1024]{0:T(1024)}, bf16[2308,1024]{1,0:T(8,128)(2,1)S(1)}, f32[2308,1024]{1,0:T(8,128)}) fusion(f32[2308,1024]{1,0:T(8,128)} %fusion.83, f32[1024]{0:T(1024)S(1)} %copy-done.36, bf16[2308,1024]{1,0:T(8,128)(2,1)} %all-gather.15.cloned.1.call-done, bf16[1024,1024]{1,0:T(8,128)(2,1)} %all-gather.13.cloned.1.call-done), kind=kOutput, calls=%fused_computation.62 | convolution fusion | flops 5017480192 | bytes 30466048 | tf_op jit(solution)/shard_map/dot_general | solution.py:22
  413.2 8.0 fusion.84
  421.4 13.0 %multiply_convert_fusion.1 = bf16[2308,1024]{1,0:T(8,128)(2,1)} fusion(f32[2308,1024]{1,0:T(8,128)} %get-tuple-element.196, f32[2308,1024]{1,0:T(8,128)} %fusion.83, f32[1024]{0:T(1024)S(1)} %copy-done.36), kind=kLoop, calls=%fused_computation.65 | loop fusion | flops 9453568 | bytes 23638016 | tf_op jit(solution)/shard_map/convert_element_type | solution.py:159
  434.5 10.1 convolution_convert_fusion
  444.6 54.6 %reduce-scatter.9.cloned.1.call-done = f32[2308,256]{1,0:T(8,128)} async-done(((f32[2308,1024]{1,0:T(8,128)}), f32[2308,256]{1,0:T(8,128)}) %reduce-scatter.9.cloned.1.call-update) | async-done | bytes 2363408 | tf_op jit(solution)/shard_map/reduce_scatter | solution.py:42
  499.2 3.7 multiply_reduce_fusion.2
  503.5 11.4 all-reduce.2
  516.3 33.3 %reduce-scatter.7.cloned.1.call-done = bf16[2308,256]{1,0:T(8,128)(2,1)} async-done(((bf16[2308,1024]{1,0:T(8,128)(2,1)}), bf16[2308,256]{1,0:T(8,128)(2,1)}) %reduce-scatter.7.cloned.1.call-update) | async-done | bytes 1181712 | tf_op jit(solution)/shard_map/reduce_scatter | solution.py:161
  549.6 6.5 convert_reduce_fusion.5
  556.2 10.4 fusion.91
  566.6 8.9 fusion.92
  575.6 18.9 %all-gather.17.cloned.1.call-done = bf16[2308,1024]{1,0:T(8,128)(2,1)} async-done(((bf16[2308,256]{1,0:T(8,128)(2,1)}), bf16[2308,1024]{1,0:T(8,128)(2,1)}) %all-gather.17.cloned.1.call-update) | async-done | bytes 4726800 | tf_op jit(solution)/shard_map/all_gather | solution.py:38
  594.4 3.8 convolution_convert_fusion.1
  600.6 4.4 copy.59
  608.8 43.5 %while.27 = (s32[]{:T(128)}, bf16[4,577,4,64]{1,3,2,0:T(8,128)(2,1)}, bf16[4,577,4,64]{1,3,2,0:T(8,128)(2,1)}, bf16[4,577,4,64]{1,3,2,0:T(8,128)(2,1)}, bf16[4,5...) while((s32[]{:T(128)}, ...), condition=%wide.region_21.22_spmd, body=%wide.region_19.21_spmd.sunk | while | flops 869015040 | bytes 49986844 | solution.py:184
  659.4 3.5 copy.63
  662.9 3.9 reshape.100
  666.9 5.0 fusion.90
  671.9 5.2 fusion.87
  687.2 5.1 add_add_fusion
  699.5 378.4 %all-reduce.7.cloned.1.call-done = (f32[1024,256]{1,0:T(8,128)}, f32[1024,256]{1,0:T(8,128)}, f32[1024,256]{1,0:T(8,128)}, f32[256,1024]{1,0:T(8,128)}, f32[1024,1024]{1,0:T(8,128)}, /*index=5*/f32[1024,1024]{1,0:T(8,128)}) async-done(((f32[1024,256]{1,0:T(8,128)}, f32[1024,256]{1,0:T(8,128)}, f32[1024,256]{1,0:T(8,128)}, f32[256,1024]{1,0:T(8,128)}, f32[1024,1024]{1,0:T(8,128)}, ...) | async-done | bytes 12582928 | tf_op jit(solution)/shard_map/psum | solution.py:217
  1086.8 70.7 %reduce-scatter.11.cloned.1.call-done = f32[2308,256]{1,0:T(8,128)} async-done(((f32[2308,1024]{1,0:T(8,128)}), f32[2308,256]{1,0:T(8,128)}) %reduce-scatter.11.cloned.1.call-update) | async-done | bytes 2363408 | tf_op jit(solution)/shard_map/reduce_scatter | solution.py:42
  1157.5 3.7 fusion.77
  1166.9 37.3 %psum.116 = f32[3072]{0:T(1024)} all-reduce(f32[3072]{0:T(1024)} %constant_dynamic-update-slice_fusion), channel_id=1, replica_groups=mesh['dp'=2,'row'=4,'col'=4] {'dp','row'}, use_global_device_ids=true, to_apply=%region_39.40 | all-reduce | flops 3072 | bytes 24576 | tf_op jit(solution)/shard_map/psum | solution.py:217
  1208.2 11.6 all-reduce.1
  1220.6 5.0 fusion.76
  (215 shorter events, 140.6 us)
Async XLA Ops:
  8.0 19.1 %copy-start.27 = (bf16[256,256]{1,0:T(8,128)(2,1)S(1)}, bf16[256,256]{1,0:T(8,128)(2,1)}, u32[]{:S(2)}) copy-start(bf16[256,256]{1,0:T(8,128)(2,1)} %param.24) | copy-start | bytes 393220
  8.0 34.2 %copy-start.28 = (bf16[256,256]{1,0:T(8,128)(2,1)S(1)}, bf16[256,256]{1,0:T(8,128)(2,1)}, u32[]{:S(2)}) copy-start(bf16[256,256]{1,0:T(8,128)(2,1)} %param.22) | copy-start | bytes 393220
  8.0 51.6 %copy-start.29 = (bf16[256,256]{1,0:T(8,128)(2,1)S(1)}, bf16[256,256]{1,0:T(8,128)(2,1)}, u32[]{:S(2)}) copy-start(bf16[256,256]{1,0:T(8,128)(2,1)} %param.23) | copy-start | bytes 393220
  8.1 82.2 %all-gather.7.cloned.1.call-start = ((), (), s32[]{:S(2)}) async-start(), calls=%async_computation.4 | async-start | bytes 5918720 | tf_op jit(solution)/shard_map/all_gather | solution.py:34
  10.2 64.3 %copy-start.30 = (bf16[256,256]{1,0:T(8,128)(2,1)S(1)}, bf16[256,256]{1,0:T(8,128)(2,1)}, u32[]{:S(2)}) copy-start(bf16[256,256]{1,0:T(8,128)(2,1)} %param.27) | copy-start | bytes 393220
  23.9 66.4 %copy-start.38 = (f32[256]{0:T(256)S(1)}, f32[256]{0:T(256)}, u32[]{:S(2)}) copy-start(f32[256]{0:T(256)} %param.26) | copy-start | bytes 3076
  27.1 211.6 %reduce-scatter.5.cloned.1.call-start = ((), (), s32[]{:S(2)}) async-start(), calls=%async_computation.5 | async-start | bytes 11837440 | tf_op jit(solution)/shard_map/reduce_scatter | solution.py:151
  42.2 48.0 %copy-start.16 = (bf16[1024,256]{1,0:T(8,128)(2,1)}, bf16[1024,256]{1,0:T(8,128)(2,1)S(1)}, u32[]{:S(2)}) copy-start(bf16[1024,256]{1,0:T(8,128)(2,1)S(1)} %all_gather.31) | copy-start | bytes 1572868
  59.7 41.7 %copy-start.18 = (bf16[1024,256]{1,0:T(8,128)(2,1)}, bf16[1024,256]{1,0:T(8,128)(2,1)S(1)}, u32[]{:S(2)}) copy-start(bf16[1024,256]{1,0:T(8,128)(2,1)S(1)} %all_gather.32) | copy-start | bytes 1572868
  74.5 36.2 %copy-start.20 = (bf16[1024,256]{1,0:T(8,128)(2,1)}, bf16[1024,256]{1,0:T(8,128)(2,1)S(1)}, u32[]{:S(2)}) copy-start(bf16[1024,256]{1,0:T(8,128)(2,1)S(1)} %all_gather.33) | copy-start | bytes 1572868
  95.0 6.3 copy-start.39
  145.0 14.6 %copy-start.2 = (bf16[4,577,4,64]{1,3,2,0:T(8,128)(2,1)}, bf16[4,577,4,64]{1,3,2,0:T(8,128)(2,1)S(1)}, u32[]{:S(2)}) copy-start(bf16[4,577,4,64]{1,3,2,0:T(8,128)(2,1)S(1)} %get-tuple-element.398) | copy-start | bytes 3545092
  145.0 14.6 %copy-start.4 = (bf16[4,577,4,64]{1,3,2,0:T(8,128)(2,1)}, bf16[4,577,4,64]{1,3,2,0:T(8,128)(2,1)S(1)}, u32[]{:S(2)}) copy-start(bf16[4,577,4,64]{1,3,2,0:T(8,128)(2,1)S(1)} %get-tuple-element.399) | copy-start | bytes 3545092
  145.0 8.3 copy-start.21
  159.6 79.1 %copy-start = (bf16[2308,256]{1,0:T(8,128)(2,1)S(1)}, bf16[2308,256]{1,0:T(8,128)(2,1)}, u32[]{:S(2)}) copy-start(bf16[2308,256]{1,0:T(8,128)(2,1)} %param.21) | copy-start | bytes 3545092
  159.6 96.7 %all-gather.11.cloned.1.call-start = ((), (), s32[]{:S(2)}) async-start(), calls=%async_computation.7 | async-start | bytes 2621440 | tf_op jit(solution)/shard_map/all_gather | solution.py:137
  160.2 91.9 %copy-start.32 = (f32[256]{0:T(256)S(1)}, f32[256]{0:T(256)}, u32[]{:S(2)}) copy-start(f32[256]{0:T(256)} %param.35) | copy-start | bytes 3076
  160.2 133.4 %all-gather.9.cloned.1.call-start = ((), (), s32[]{:S(2)}) async-start(), calls=%async_computation.6 | async-start | bytes 5918720 | tf_op jit(solution)/shard_map/all_gather | solution.py:34
  254.9 86.3 %all-gather.13.cloned.1.call-start = ((), (), s32[]{:S(2)}) async-start(), calls=%async_computation.8 | async-start | bytes 2621440 | tf_op jit(solution)/shard_map/all_gather | solution.py:138
  255.5 123.5 %all-gather.15.cloned.1.call-start = ((), (), s32[]{:S(2)}) async-start(), calls=%async_computation.10 | async-start | bytes 5918720 | tf_op jit(solution)/shard_map/all_gather | solution.py:38
  256.2 122.8 %copy-start.36 = (f32[1024]{0:T(1024)S(1)}, f32[1024]{0:T(1024)}, u32[]{:S(2)}) copy-start(f32[1024]{0:T(1024)} %param.30) | copy-start | bytes 12292
  256.3 243.0 %reduce-scatter.9.cloned.1.call-start = ((), (), s32[]{:S(2)}) async-start(), calls=%async_computation.11 | async-start | bytes 11837440 | tf_op jit(solution)/shard_map/reduce_scatter | solution.py:42
  379.0 34.2 %copy-start.37 = (bf16[1024,1024]{1,0:T(8,128)(2,1)S(1)}, bf16[1024,1024]{1,0:T(8,128)(2,1)}, u32[]{:S(2)}) copy-start(bf16[1024,1024]{1,0:T(8,128)(2,1)} %all-gather.11.cloned.1.call-done) | copy-start | bytes 6291460
  421.2 128.4 %reduce-scatter.7.cloned.1.call-start = ((), (), s32[]{:S(2)}) async-start(), calls=%async_computation.9 | async-start | bytes 5918720 | tf_op jit(solution)/shard_map/reduce_scatter | solution.py:161
  444.6 105.0 %copy-start.15 = (bf16[2308,256]{1,0:T(8,128)(2,1)S(1)}, bf16[2308,256]{1,0:T(8,128)(2,1)}, u32[]{:S(2)}) copy-start(bf16[2308,256]{1,0:T(8,128)(2,1)} %param.37) | copy-start | bytes 3545092
  444.6 149.8 %all-gather.17.cloned.1.call-start = ((), (), s32[]{:S(2)}) async-start(), calls=%async_computation.12 | async-start | bytes 5918720 | tf_op jit(solution)/shard_map/all_gather | solution.py:38
  556.1 10.5 slice-start
  556.1 521.8 %all-reduce.7.cloned.1.call-start = ((), (), s32[]{:S(2)}) async-start(), calls=%async_computation.14 | async-start | bytes 25165824 | tf_op jit(solution)/shard_map/psum | solution.py:217
  556.2 10.4 slice-start.1
  566.6 27.8 %copy-start.22 = (bf16[256,1024]{1,0:T(8,128)(2,1)S(1)}, bf16[256,1024]{1,0:T(8,128)(2,1)}, u32[]{:S(2)}) copy-start(bf16[256,1024]{1,0:T(8,128)(2,1)} %all_gather.34) | copy-start | bytes 1572868
  600.6 8.2 copy-start.3
  600.6 8.2 copy-start.5
  652.3 4.3 copy-start.7
  659.4 7.5 copy-start.9
  666.9 5.0 copy-start.11
  666.9 10.2 slice-start.2
  671.9 5.2 copy-start.10
  671.9 5.2 slice-start.3
  677.1 2.8 copy-start.13
  682.8 2.9 copy-start.19
  682.8 474.7 %reduce-scatter.11.cloned.1.call-start = ((), (), s32[]{:S(2)}) async-start(), calls=%async_computation.13 | async-start | bytes 11837440 | tf_op jit(solution)/shard_map/reduce_scatter | solution.py:42
  683.0 2.7 copy-start.12
  692.4 4.6 copy-start.34
  692.4 5.9 copy-start.33
  1077.9 79.5 %copy-start.1 = (bf16[2308,256]{1,0:T(8,128)(2,1)S(1)}, bf16[2308,256]{1,0:T(8,128)(2,1)}, u32[]{:S(2)}) copy-start(bf16[2308,256]{1,0:T(8,128)(2,1)} %param.21) | copy-start | bytes 3545092
  1077.9 79.5 %copy-start.31 = (f32[256]{0:T(256)S(1)}, f32[256]{0:T(256)}, u32[]{:S(2)}) copy-start(f32[256]{0:T(256)} %param.33) | copy-start | bytes 3076
  1084.0 136.6 %copy-start.8 = (f32[2308,256]{1,0:T(8,128)S(1)}, f32[2308,256]{1,0:T(8,128)}, u32[]{:S(2)}) copy-start(f32[2308,256]{1,0:T(8,128)} %get-tuple-element.199) | copy-start | bytes 7090180
  1157.5 8.9 copy-start.35
  (11 other events, 15.1 us)
Sparse Core Ops, SparseCore 0:
  27.2 38.4 all-gather.6
  159.8 78.8 reduce-scatter.4
  556.2 38.1 all-gather.16
  682.9 395.0 all-reduce.6
  1080.4 77.0 reduce-scatter.10
Sparse Core Ops, SparseCore 1:
  161.7 46.4 all-gather.10
  255.0 38.5 all-gather.8
  295.0 46.1 all-gather.12
  342.8 36.2 all-gather.14
  421.3 77.8 reduce-scatter.8
  501.8 47.8 reduce-scatter.6
where the time goes:
time: 1240 us; the launch traced here: 1230 us
  waiting for transfers between devices  749 us (60%)
  matrix products  179 us (14%)
  blocking collectives  147 us (12%)
  local copies, waits for them, and re-layouts  83 us (7%)
  other arithmetic  58.7 us (5%)
  between operations  16 us (1%)
    psum x1, waiting for transfers between devices, local(): lax.psum((query_grad_full, key_grad_full, value_grad_full, out_grad_full,...  378 us
    reduce_scatter x2, waiting for transfers between devices, scatter_partial(): return lax.psum_scatter(values, 'col', scatter_dimension=1, tiled=True)  125 us
    reduce_scatter x1, waiting for transfers between devices, local(): lax.psum_scatter(matmul(attended, out_full), 'col', scatter_dimension=1,...  78.4 us
    all_gather x2, waiting for transfers between devices, gather_grads(): return lax.all_gather(values, 'col', axis=1, tiled=True)  56.6 us
    dot_general x6, matrix products, matmul_nt(): lax.dot_general(left_side, right_side, (((1,), (1,)), ((), ())), preferre...  53.1 us
    psum x4, blocking collectives, feature_totals(): lax.psum((jnp.sum(first, axis=1, keepdims=True), jnp.sum(second, axis=1,...  46.3 us
    dot_general x6, matrix products, matmul(): return jnp.dot(left_side, right_side, preferred_element_type=jnp.float32)  38.8 us
    all_gather x1, waiting for transfers between devices, local(): lax.all_gather(down_weight, 'row', axis=1, tiled=True)  37.5 us
  transfers between devices with their start and end apart: 11, of which 9 were waited for; matrix products, arithmetic and copies ran while one was open for 7% of the time, Pallas kernels for 0%

commit v1 on v0

v1 whole, which is shorter than its diff:
```python
import functools

import jax
import jax.numpy as jnp
from jax import lax
from jax.sharding import Mesh, PartitionSpec as P

D = 1024
HD = 64
SEQ = 577
PAD = 592
EPS = 1e-06
F32 = jnp.float32
BF16 = jnp.bfloat16


def mm(left_side, right_side):
    return jnp.dot(left_side, right_side, preferred_element_type=F32)


def mm_tn(left_side, right_side):
    return lax.dot_general(
        left_side, right_side, (((0,), (0,)), ((), ())), preferred_element_type=F32
    )


def mm_nt(left_side, right_side):
    return lax.dot_general(
        left_side, right_side, (((1,), (1,)), ((), ())), preferred_element_type=F32
    )


def swap(value, axis, size):
    return lax.ppermute(value, axis, [(place, place ^ 1) for place in range(size)])


def row_mean(values):
    return jnp.sum(values, axis=1, keepdims=True) / D


def norm_forward(rows, gain, shift):
    middle = row_mean(rows)
    spread = row_mean(rows * rows) - middle * middle
    scaled = lax.rsqrt(spread + EPS)
    centred = (rows - middle) * scaled
    return centred * gain + shift, centred, scaled


def norm_backward(upstream, gain, centred, scaled):
    lifted = upstream * gain
    return scaled * (lifted - row_mean(lifted) - centred * row_mean(lifted * centred))


def attend_image(operands):
    query_rows, key_rows, value_rows = operands
    scores = jnp.einsum("qhd,khd->hqk", query_rows, key_rows, preferred_element_type=F32) * 0.125
    live = lax.broadcasted_iota(jnp.int32, (1, 1, PAD), 2) < SEQ
    scores = jnp.where(live, scores, -1e30)
    row_peak = jnp.max(scores, axis=-1, keepdims=True)
    exponent = jnp.exp(scores - row_peak)
    row_total = jnp.sum(exponent, axis=-1, keepdims=True)
    soft_weights = (exponent / row_total).astype(BF16)
    mixed_rows = jnp.einsum("hqk,khd->qhd", soft_weights, value_rows, preferred_element_type=F32)
    return (mixed_rows.astype(BF16), row_peak + jnp.log(row_total))


def attend_back(operands):
    query_rows, key_rows, value_rows, grad_rows, logsum = operands
    scores = jnp.einsum("qhd,khd->hqk", query_rows, key_rows, preferred_element_type=F32) * 0.125
    live = lax.broadcasted_iota(jnp.int32, (1, 1, PAD), 2) < SEQ
    soft_weights = jnp.where(live, jnp.exp(scores - logsum), 0.0)
    dprobs = jnp.einsum("qhd,khd->hqk", grad_rows, value_rows, preferred_element_type=F32)
    dvalues = jnp.einsum(
        "hqk,qhd->khd", soft_weights.astype(BF16), grad_rows, preferred_element_type=F32
    )
    row_dot = jnp.sum(soft_weights * dprobs, axis=-1, keepdims=True)
    dscores = (soft_weights * (dprobs - row_dot)).astype(BF16)
    dqueries = jnp.einsum("hqk,khd->qhd", dscores, key_rows, preferred_element_type=F32) * 0.125
    key_grads = jnp.einsum("hqk,qhd->khd", dscores, query_rows, preferred_element_type=F32) * 0.125
    return dqueries.astype(BF16), key_grads.astype(BF16), dvalues.astype(BF16)


def gelu_exact(values):
    return jax.nn.gelu(values, approximate=False)


def local(
    sizes,
    inputs,
    query_weight,
    key_weight,
    value_weight,
    query_bias,
    value_bias,
    out_weight,
    out_bias,
    up_weight,
    up_bias,
    down_weight,
    down_bias,
    first_gain,
    first_shift,
    second_gain,
    second_shift,
    cotangent,
):
    n_dp, n_row, n_xa, n_core = sizes
    my_x = lax.axis_index("xa")
    my_core = lax.axis_index("core")
    tokens_here, width = inputs.shape
    images = tokens_here // SEQ
    held = images // n_xa
    rows = held * PAD
    hidden = up_weight.shape[1]

    def across(value):
        return swap(value, "xa", n_xa)

    def beside(value):
        return swap(value, "core", n_core)

    def image_halves(value):
        padded = jnp.pad(value.reshape(images, SEQ, -1), ((0, 0), (0, PAD - SEQ), (0, 0)))
        halves = padded.reshape(n_xa, rows, -1)
        mine = lax.dynamic_index_in_dim(halves, my_x, 0, keepdims=False)
        theirs = lax.dynamic_index_in_dim(halves, my_x ^ 1, 0, keepdims=False)
        return mine, theirs

    def in_order(mine, other, place):
        first = jnp.where(place == 0, mine, other)
        second = jnp.where(place == 0, other, mine)
        return first, second

    def wide_tokens(value):
        mine, theirs = image_halves(value)
        got = across(theirs)
        pair = jnp.stack(in_order(mine, got, my_x))
        other = beside(pair)
        left, right = in_order(pair, other, my_core)
        return jnp.concatenate([left[0], right[0], left[1], right[1]], axis=1)

    small = jnp.concatenate(
        [
            out_bias,
            down_bias,
            first_gain,
            first_shift,
            second_gain,
            second_shift,
            query_bias,
            value_bias,
            up_bias,
        ]
    )
    small_far = across(small)
    small_pair = jnp.stack(in_order(small, small_far, my_x))
    small_other = beside(small_pair)
    small_left, small_right = in_order(small_pair, small_other, my_core)

    def whole_vector(place):
        cut = slice(width * place, width * (place + 1))
        return jnp.concatenate(
            [small_left[0, cut], small_right[0, cut], small_left[1, cut], small_right[1, cut]]
        )

    out_bias_all, down_bias_all, gain_one, shift_one, gain_two, shift_two = (
        whole_vector(place) for place in range(6)
    )
    query_bias_far = small_far[6 * width : 7 * width]
    value_bias_far = small_far[7 * width : 8 * width]
    up_bias_far = small_far[8 * width :]

    def gather_rows(value):
        return lax.all_gather(value, "row", axis=0, tiled=True)

    qkv_near = gather_rows(jnp.concatenate([query_weight, key_weight, value_weight], axis=1))
    qkv_far = across(qkv_near)
    out_near = gather_rows(out_weight.T)
    out_far = across(out_near)
    up_near = gather_rows(up_weight)
    up_far = across(up_near)
    down_near = gather_rows(down_weight.T)
    down_far = across(down_near)

    wide_input = wide_tokens(inputs)
    wide_grad = wide_tokens(cotangent)
    residual = wide_input.astype(F32)

    normed_one, centred_one, scaled_one = norm_forward(residual, gain_one, shift_one)
    wide_one = normed_one.astype(BF16)

    zeros = jnp.zeros_like(query_bias)
    bias_near = jnp.concatenate([query_bias, zeros, value_bias])
    bias_far = jnp.concatenate([query_bias_far, zeros, value_bias_far])
    near = (mm(wide_one, qkv_near) + bias_near).astype(BF16)
    far = (mm(wide_one, qkv_far) + bias_far).astype(BF16)
    heads_here = 2 * width // HD
    head_shape = (held, PAD, heads_here, HD)

    def heads(place):
        cut = slice(width * place, width * (place + 1))
        return jnp.concatenate([near[:, cut], far[:, cut]], axis=1).reshape(head_shape)

    query_heads, key_heads, value_heads = heads(0), heads(1), heads(2)
    attended, logsums = lax.map(attend_image, (query_heads, key_heads, value_heads))
    attended = attended.reshape(rows, 2 * width)
    mixed = mm_nt(attended[:, :width], out_near) + mm_nt(attended[:, width:], out_far)
    mixed = mixed.astype(BF16)
    middle_sum = residual + (mixed.astype(F32) + beside(mixed).astype(F32)) + out_bias_all

    normed_two, centred_two, scaled_two = norm_forward(middle_sum, gain_two, shift_two)
    wide_two = normed_two.astype(BF16)

    def mlp(up_block, up_bias_block, down_block):
        up_values = mm(wide_two, up_block) + up_bias_block
        gelu_value, gelu_back = jax.vjp(gelu_exact, up_values)
        gate = gelu_value.astype(BF16)
        pre_grad = gelu_back(mm(wide_grad, down_block))[0].astype(BF16)
        return gate, pre_grad

    gate_near, pre_near = mlp(up_near, up_bias, down_near)
    gate_far, pre_far = mlp(up_far, up_bias_far, down_far)

    def feature_split(value):
        blocks = value.reshape(rows, n_xa, 2, width)
        mine = lax.dynamic_index_in_dim(blocks, my_core, 2, keepdims=False)
        theirs = lax.dynamic_index_in_dim(blocks, my_core ^ 1, 2, keepdims=False)
        return mine.reshape(rows, -1), theirs.reshape(rows, -1)

    def to_feature_blocks(value):
        blocks = value.reshape(rows, n_xa, width)
        mine = lax.dynamic_index_in_dim(blocks, my_x, 1, keepdims=False)
        theirs = lax.dynamic_index_in_dim(blocks, my_x ^ 1, 1, keepdims=False)
        got = across(theirs)
        first, second = in_order(mine, got, my_x)
        both = jnp.concatenate([first, second]).reshape(images, PAD, width)
        return both[:, :SEQ].reshape(tokens_here, width)

    lowered = mm_nt(gate_near, down_near) + mm_nt(gate_far, down_far)
    lowered_mine, lowered_theirs = feature_split(lowered)
    middle_mine, _ = feature_split(middle_sum)
    down_bias_mine, _ = feature_split(jnp.broadcast_to(down_bias_all, (rows, D)))
    branch = lowered_mine + beside(lowered_theirs.astype(BF16)).astype(F32)
    outputs = to_feature_blocks((middle_mine + branch + down_bias_mine).astype(BF16))

    def reduce_grad(near_grad, far_grad):
        total = (near_grad + across(far_grad.astype(BF16)).astype(F32)).astype(BF16)
        piece = lax.psum_scatter(total, "row", scatter_dimension=0, tiled=True)
        return piece.astype(F32) + swap(piece, "dp", n_dp).astype(F32) if n_dp == 2 else (
            lax.psum(piece.astype(F32), "dp")
        )

    down_grad = reduce_grad(mm_tn(wide_grad, gate_near), mm_tn(wide_grad, gate_far)).T
    up_grad = reduce_grad(mm_tn(wide_two, pre_near), mm_tn(wide_two, pre_far))
    lifted_two = (mm_nt(pre_near, up_near) + mm_nt(pre_far, up_far)).astype(BF16)
    normed_grad_two = lifted_two.astype(F32) + beside(lifted_two).astype(F32)
    grad_top = wide_grad.astype(F32)
    middle_grad = grad_top + norm_backward(normed_grad_two, gain_two, centred_two, scaled_two)
    attn_grad = middle_grad.astype(BF16)
    out_grad = reduce_grad(
        mm_tn(attn_grad, attended[:, :width]), mm_tn(attn_grad, attended[:, width:])
    ).T
    head_grad = jnp.concatenate([mm(attn_grad, out_near), mm(attn_grad, out_far)], axis=1)
    head_grad = head_grad.astype(BF16).reshape(head_shape)
    dqueries, key_grads, dvalues = lax.map(
        attend_back, (query_heads, key_heads, value_heads, head_grad, logsums)
    )
    dqueries, key_grads, dvalues = (
        item.reshape(rows, 2 * width) for item in (dqueries, key_grads, dvalues)
    )
    grads_near = jnp.concatenate([item[:, :width] for item in (dqueries, key_grads, dvalues)], axis=1)
    grads_far = jnp.concatenate([item[:, width:] for item in (dqueries, key_grads, dvalues)], axis=1)
    qkv_grad = reduce_grad(mm_tn(wide_one, grads_near), mm_tn(wide_one, grads_far))
    lifted_one = (mm_nt(grads_near, qkv_near) + mm_nt(grads_far, qkv_far)).astype(BF16)
    normed_grad_one = lifted_one.astype(F32) + beside(lifted_one).astype(F32)
    input_wide = middle_grad + norm_backward(normed_grad_one, gain_one, centred_one, scaled_one)
    input_mine, _ = feature_split(input_wide)
    input_grad = to_feature_blocks(input_mine.astype(BF16)).astype(F32)

    def column_sum(value):
        return jnp.sum(value.astype(F32), axis=0)

    def own_features(value):
        blocks = value.reshape(n_xa, 2, width)
        return lax.dynamic_index_in_dim(blocks, my_core, 1, keepdims=False)

    def by_x(near_sum, far_sum):
        return jnp.stack(in_order(near_sum, far_sum, my_x))

    near_sums, far_sums = column_sum(grads_near), column_sum(grads_far)
    vectors = jnp.concatenate(
        [
            by_x(near_sums[:width], far_sums[:width]),
            by_x(near_sums[2 * width :], far_sums[2 * width :]),
            own_features(column_sum(attn_grad)),
            own_features(column_sum(grad_top)),
            own_features(column_sum(normed_grad_one * centred_one)),
            own_features(column_sum(normed_grad_one)),
            own_features(column_sum(normed_grad_two * centred_two)),
            own_features(column_sum(normed_grad_two)),
            by_x(column_sum(pre_near), column_sum(pre_far)),
        ],
        axis=1,
    )
    vector_sums = lax.dynamic_index_in_dim(
        lax.psum(vectors, ("dp", "row", "xa")), my_x, 0, keepdims=False
    )
    pieces = [vector_sums[width * place : width * (place + 1)] for place in range(8)]
    up_bias_sum = vector_sums[8 * width :]
    return (
        outputs,
        input_grad,
        qkv_grad[:, :width],
        qkv_grad[:, width : 2 * width],
        qkv_grad[:, 2 * width :],
        pieces[0],
        pieces[1],
        out_grad,
        pieces[2],
        up_grad,
        up_bias_sum,
        down_grad,
        pieces[3],
        pieces[4],
        pieces[5],
        pieces[6],
        pieces[7],
    )


def solution(mesh):
    n_dp, n_row, n_col = (mesh.shape[name] for name in ("dp", "row", "col"))
    sizes = (n_dp, n_row, n_col // 2, 2)
    split = Mesh(mesh.devices.reshape(sizes), ("dp", "row", "xa", "core"))
    col = ("xa", "core")
    tokens, rows, cols, vec = P(("dp", "row"), col), P("row", col), P(col, "row"), P(col)
    in_specs = (
        tokens, rows, rows, rows, vec, vec, cols, vec, rows, vec, cols, vec, vec, vec, vec, vec, tokens,
    )
    out_specs = (
        tokens, tokens, rows, rows, rows, vec, vec, cols, vec, rows, vec, cols, vec, vec, vec, vec, vec,
    )
    return jax.shard_map(
        functools.partial(local, sizes),
        mesh=split,
        in_specs=in_specs,
        out_specs=out_specs,
        check_vma=False,
    )
```

time: 1240 us -> 759 us (0.61)
  waiting for transfers between devices: 749 us -> 223 us
  local copies, waits for them, and re-layouts: 83 us -> 157 us
  blocking collectives: 147 us -> 105 us
  matrix products: 179 us -> 157 us
  starting transfers between devices: 0.8 us -> 17.9 us
  other arithmetic: 58.7 us -> 71.8 us
    psum x1 -> x0, waiting for transfers between devices: 378 us -> none  [local(): lax.psum((query_grad_full, key_grad_full, value_grad_full, out_grad_full,...]
    reduce_scatter x4, waiting for transfers between devices: 237 us -> 0.03 us  [reduce_grad(): piece = lax.psum_scatter(total, 'row', scatter_dimension=0, tiled=True)]
    ppermute x0 -> x24, waiting for transfers between devices: none -> 222 us  [swap(): lax.ppermute(value, axis, [(place, place ^ 1) for place in range(size)])]
    all_gather x6 -> x3, waiting for transfers between devices: 131 us -> 0.02 us  [gather_rows(): return lax.all_gather(value, 'row', axis=0, tiled=True)]
    all_gather x4 -> x1, blocking collectives: 63.1 us -> 23.6 us  [gather_rows(): return lax.all_gather(value, 'row', axis=0, tiled=True)]
    reshape x8 -> x20, local copies, waits for them, and re-layouts: 22.4 us -> 50.3 us  [the longest x3 21 us: feature_split(): blocks = value.reshape(rows, n_xa, 2, width)]
    dynamic_slice x4 -> x12, local copies, waits for them, and re-layouts: 8.83 us -> 30.3 us  [the longest x4 21.3 us: feature_split(): mine = lax.dynamic_index_in_dim(blocks, my_core, 2, keepdims=False)]
    dot_general x38 -> x34, matrix products: 156 us -> 137 us  [the longest x8 50.8 us: mm(): return jnp.dot(left_side, right_side, preferred_element_type=F32)]
  transfers between devices with their start and end apart: 11 -> 31, of which waited for: 9 -> 11; matrix products, arithmetic and copies ran while one was open for 7% -> 49% of each run, Pallas kernels for 0% -> 0%
where the time goes in v1:
time: 759 us; the launch traced here: 749 us
  waiting for transfers between devices  223 us (29%)
  local copies, waits for them, and re-layouts  157 us (21%)
  matrix products  157 us (21%)
  blocking collectives  105 us (14%)
  other arithmetic  71.8 us (9%)
  starting transfers between devices  17.9 us (2%)
  between operations  16.5 us (2%)
    ppermute x24, waiting for transfers between devices, swap(): lax.ppermute(value, axis, [(place, place ^ 1) for place in range(size)])  222 us
    psum x1, blocking collectives, local(): lax.psum(vectors, ('dp', 'row', 'xa'))  81.5 us
    dot_general x8, matrix products, mm(): return jnp.dot(left_side, right_side, preferred_element_type=F32)  50.8 us
    dot_general x8, matrix products, mm_tn(): lax.dot_general(left_side, right_side, (((0,), (0,)), ((), ())), preferre...  39.4 us
    dot_general x8, matrix products, mm_nt(): lax.dot_general(left_side, right_side, (((1,), (1,)), ((), ())), preferre...  26.2 us
    all_gather x1, blocking collectives, gather_rows(): return lax.all_gather(value, 'row', axis=0, tiled=True)  23.6 us
    dynamic_slice x4, local copies, waits for them, and re-layouts, feature_split(): mine = lax.dynamic_index_in_dim(blocks, my_core, 2, keepdims=False)  21.3 us
    reshape x3, local copies, waits for them, and re-layouts, feature_split(): blocks = value.reshape(rows, n_xa, 2, width)  21 us
  transfers between devices with their start and end apart: 31, of which 11 were waited for; matrix products, arithmetic and copies ran while one was open for 49% of the time, Pallas kernels for 0%

profile of v1, /device:TPU:0, one launch (start us, length us, event | category | flops | bytes accessed | tf_op | source)
XLA Modules:
  0.0 748.7 jit_solution(13739585852261563856)
XLA Ops:
  19.0 23.6 %all_gather.13 = bf16[1024,256]{0,1:T(8,128)(2,1)} all-gather(bf16[256,256]{0,1:T(8,128)(2,1)} %bitcast.283), channel_id=1, replica_groups=mesh['dp'=2,'row'=4,'xa'=2,'core'=2] {'row'}, dimensions={0}, use_global_device_ids=true | all-gather | bytes 655360 | tf_op jit(solution)/shard_map/all_gather | solution.py:174
  53.5 17.2 %collective-permute-done = bf16[1184,256]{1,0:T(8,128)(2,1)} collective-permute-done((bf16[1184,256]{1,0:T(8,128)(2,1)}, bf16[1184,256]{1,0:T(8,128)(2,1)}, u32[]{:S(2)}, u32[]{:S(2)}) %collective-permute-start) | collective-permute-done | bytes 606240 | tf_op jit(solution)/shard_map/ppermute | solution.py:34
  73.3 8.1 %collective-permute-done.11 = bf16[1184,256]{1,0:T(8,128)(2,1)} collective-permute-done((bf16[1184,256]{1,0:T(8,128)(2,1)S(1)}, bf16[1184,256]{1,0:T(8,128)(2,1)}, u32[]{:S(2)}, u32[]{:S(2)}) %collective-permute-start.11) | collective-permute-done | bytes 606240 | tf_op jit(solution)/shard_map/ppermute | solution.py:34
  87.4 4.2 fusion.91
  92.8 29.3 %collective-permute-done.4 = bf16[1024,768]{1,0:T(8,128)(2,1)S(1)} collective-permute-done((bf16[1024,768]{1,0:T(8,128)(2,1)}, bf16[1024,768]{1,0:T(8,128)(2,1)S(1)}, u32[]{:S(2)}, u32[]{:S(2)}) %collective-permute-start.4) | collective-permute-done | bytes 1572896 | tf_op jit(solution)/shard_map/ppermute | solution.py:34
  148.9 20.0 %while.26 = (s32[]{:T(128)}, bf16[2,592,8,64]{1,3,2,0:T(8,128)(2,1)}, f32[2,8,592,1]{2,1,3,0:T(8,128)S(1)}, bf16[2,592,8,64]{1,3,2,0:T(8,128)(2,1)}, bf16[2,592,...) while((s32[]{:T(128)}, bf16[2,592,8,64]{1,3,2,0:T(8,128)(2,1)}, ...), condition=%wide.region_5.6_spmd, body=%wide.region_2.5_spmd.sunk | while | flops 751693824 | bytes 51888972 | solution.py:205
  168.9 4.6 copy.80
  173.6 4.2 reshape.279
  180.2 3.4 add_convert_fusion.5
  188.7 4.5 fusion.116
  196.4 14.3 %multiply_convert_fusion.2 = (bf16[1184,1024]{1,0:T(8,128)(2,1)}, f32[1184,1024]{1,0:T(8,128)S(1)}, f32[1184,1024]{1,0:T(8,128)S(1)}) fusion(f32[1024]{0:T(1024)S(1)} %copy-done.86, bf16[1184,1024]{1,0:T(8,128)(2,1)S(1)} %add_convert_fusion.4, bf16[1024,1024]{1,0:T(8,128)(2,1)S(1)} %copy-done.101), kind=kOutput, calls=%fused_computation.112 | convolution fusion | flops 2563047424 | bytes 16650240 | tf_op jit(solution)/shard_map/dot_general | solution.py:18
  210.7 4.7 convert_reduce_fusion.3
  218.2 61.6 %collective-permute-done.7 = bf16[1024,1024]{1,0:T(8,128)(2,1)S(1)} collective-permute-done((bf16[1024,1024]{1,0:T(8,128)(2,1)}, bf16[1024,1024]{1,0:T(8,128)(2,1)S(1)}, u32[]{:S(2)}, u32[]{:S(2)}) %collective-permute-start.7) | collective-permute-done | bytes 2097184 | tf_op jit(solution)/shard_map/ppermute | solution.py:34
  279.8 14.2 %multiply_convert_fusion.1 = (bf16[1184,1024]{1,0:T(8,128)(2,1)}, f32[1184,1024]{1,0:T(8,128)S(1)}, f32[1184,1024]{1,0:T(8,128)S(1)}) fusion(f32[1024]{0:T(1024)S(1)} %slice-done.4, bf16[1184,1024]{1,0:T(8,128)(2,1)S(1)} %add_convert_fusion.4, bf16[1024,1024]{1,0:T(8,128)(2,1)S(1)} %collective-permute-done.7), kind=kOutput, calls=%fused_computation.99 | convolution fusion | flops 2563047424 | bytes 16650240 | tf_op jit(solution)/shard_map/dot_general | solution.py:18
  294.0 6.5 convert_reduce_fusion.2
  303.8 7.6 %reshape.280 = f32[1184,2,2,256]{3,2,1,0:T(2,128)} reshape(f32[1184,1024]{1,0:T(8,128)} %copy-done) | data formatting | bytes 9699328 | tf_op jit(solution)/shard_map/reshape | solution.py:225
  311.4 6.8 convolution_convert_fusion.2
  321.3 4.6 multiply_reduce_fusion.1
  326.0 6.2 convert_reduce_fusion.4
  335.0 6.0 convolution_add_fusion
  341.0 7.7 %reshape.282 = f32[1184,2,2,256]{3,2,1,0:T(2,128)} reshape(f32[1184,1024]{1,0:T(8,128)} %convolution_add_fusion) | data formatting | bytes 9699328 | tf_op jit(solution)/shard_map/reshape | solution.py:225
  348.7 29.0 %collective-permute-done.18 = bf16[1024,256]{1,0:T(8,128)(2,1)S(1)} collective-permute-done((bf16[1024,256]{1,0:T(8,128)(2,1)S(1)}, bf16[1024,256]{1,0:T(8,128)(2,1)S(1)}, u32[]{:S(2)}, u32[]{:S(2)}) %collective-permute-start.18) | collective-permute-done | bytes 524320 | tf_op jit(solution)/shard_map/ppermute | solution.py:34
  377.7 3.4 add_convert_fusion.10
  381.2 5.2 constant_dynamic-slice_fusion.11
  390.9 5.6 add_convert_fusion.6
  396.5 10.3 %dynamic-slice_reduce_fusion.1 = f32[1184,2,256]{2,1,0:T(2,128)S(1)} fusion(f32[1184,2,2,256]{3,2,1,0:T(2,128)} %reshape.280, s32[]{:T(128)S(6)} %select_n.186), kind=kLoop, calls=%fused_computation.157 | loop fusion | bytes 4849668 | tf_op jit(solution)/shard_map/jit(dynamic_index_in_dim)/dynamic_slice | solution.py:226
  407.1 4.2 convolution_convert_fusion.3
  411.6 8.4 %dynamic-slice_reduce_fusion = f32[1184,2,256]{2,1,0:T(2,128)S(1)} fusion(f32[1184,2,2,256]{3,2,1,0:T(2,128)S(1)} %bitcast.269, s32[]{:T(128)S(6)} %select_n.186), kind=kLoop, calls=%fused_computation.156 | loop fusion | bytes 4849668 | tf_op jit(solution)/shard_map/jit(dynamic_index_in_dim)/dynamic_slice | solution.py:226
  427.7 44.8 %collective-permute-done.10 = bf16[1184,256]{1,0:T(8,128)(2,1)S(1)} collective-permute-done((bf16[1184,256]{1,0:T(8,128)(2,1)S(1)}, bf16[1184,256]{1,0:T(8,128)(2,1)S(1)}, u32[]{:S(2)}, u32[]{:S(2)}) %collective-permute-start.10) | collective-permute-done | bytes 606240 | tf_op jit(solution)/shard_map/ppermute | solution.py:34
  474.1 7.5 add_convert_fusion.7
  488.9 4.7 reshape.301
  493.6 4.1 copy.85
  501.6 44.1 %while.27 = (s32[]{:T(128)}, bf16[2,592,8,64]{1,3,2,0:T(8,128)(2,1)}, bf16[2,592,8,64]{1,3,2,0:T(8,128)(2,1)}, bf16[2,592,8,64]{1,3,2,0:T(8,128)(2,1)}, bf16[2,5...) while((s32[]{:T(128)}, ...), condition=%wide.region_12.13_spmd, body=%wide.region_10.12_spmd.sunk | while | flops 1837942784 | bytes 132334592 | solution.py:265
  505.9 6.5 multiply_reduce_fusion.5
  512.4 6.8 multiply_convert_fusion.4
  527.9 6.5 multiply_reduce_fusion.5
  534.4 6.8 multiply_convert_fusion.4
  545.6 3.8 copy.89
  559.4 3.7 copy.88
  563.1 4.2 reshape.290
  568.8 5.4 convolution_convert_fusion.4
  576.9 3.9 add_convert_fusion
  586.5 23.9 %collective-permute-done.16 = bf16[1024,768]{1,0:T(8,128)(2,1)} collective-permute-done((bf16[1024,768]{1,0:T(8,128)(2,1)}, bf16[1024,768]{1,0:T(8,128)(2,1)}, u32[]{:S(2)}, u32[]{:S(2)}) %collective-permute-start.16) | collective-permute-done | bytes 1572896 | tf_op jit(solution)/shard_map/ppermute | solution.py:34
  610.4 5.7 add_convert_fusion.8
  617.1 5.6 fusion.72
  622.7 6.0 fusion.71
  628.7 5.7 reshape.292
  638.1 81.5 %psum.7 = f32[2,3072]{1,0:T(2,128)S(1)} all-reduce(f32[2,3072]{1,0:T(2,128)S(1)} %constant_dynamic-update-slice_fusion.1), channel_id=1, replica_groups=mesh['dp'=2,'row'=4,'xa'=2,'core'=2] {'dp','row','xa'}, use_global_device_ids=true, to_apply=%region_26.27 | all-reduce | flops 6144 | bytes 49152 | tf_op jit(solution)/shard_map/psum | solution.py:306
  (472 shorter events, 188.8 us)
Async XLA Ops:
  7.2 77.8 %all-gather.4.cloned.1.call-start = ((), (), s32[]{:S(2)}) async-start(), calls=%async_computation.4 | async-start | bytes 1966080 | tf_op jit(solution)/shard_map/all_gather | solution.py:174
  9.1 177.5 %all-gather.8.cloned.1.call-start = ((), (), s32[]{:S(2)}) async-start(), calls=%async_computation.6 | async-start | bytes 2621440 | tf_op jit(solution)/shard_map/all_gather | solution.py:174
  9.8 177.1 %all-gather.6.cloned.1.call-start = ((), (), s32[]{:S(2)}) async-start(), calls=%async_computation.5 | async-start | bytes 2621440 | tf_op jit(solution)/shard_map/all_gather | solution.py:174
  16.0 36.0 %collective-permute-start.2 = (f32[3072]{0:T(1024)S(1)}, f32[3072]{0:T(1024)S(1)}, u32[]{:S(2)}, u32[]{:S(2)}) collective-permute-start(f32[3072]{0:T(1024)S(1)} %constant_dynamic-update-slice_fusion.10), channel_id=1, source_target_pairs={{0,2},{2,0},{1,3},{3,1},{4,6},{6,4},{5,7},{7,5},{8,10},{10,8},{9,1... | collective-permute-start | bytes 36872 | tf_op jit(solution)/shard_map/ppermute | solution.py:34
  42.6 137.5 %collective-permute-start.5 = (bf16[1024,256]{0,1:T(8,128)(2,1)}, bf16[1024,256]{0,1:T(8,128)(2,1)}, u32[]{:S(2)}, u32[]{:S(2)}) collective-permute-start(bf16[1024,256]{0,1:T(8,128)(2,1)} %all_gather.13), channel_id=1, source_target_pairs={{0,2},{2,0},{1,3},{3,1},{4,6},{6,4},{5,7},{7,5},{8,10},{10,8},{9,1... | collective-permute-start | bytes 1572872 | tf_op jit(solution)/shard_map/ppermute | solution.py:34
  45.9 24.8 %collective-permute-start = (bf16[1184,256]{1,0:T(8,128)(2,1)}, bf16[1184,256]{1,0:T(8,128)(2,1)}, u32[]{:S(2)}, u32[]{:S(2)}) collective-permute-start(bf16[1184,256]{1,0:T(8,128)(2,1)} %dynamic-slice_bitcast_fusion.3), channel_id=1, source_target_pairs={{0,2},{2,0},{1,3},{3,1},{4,6},{6,4},{5,7},{7,5},{8,10},{10,8},{9,1... | collective-permute-start | bytes 1818632 | tf_op jit(solution)/shard_map/ppermute | solution.py:34
  51.2 30.2 %collective-permute-start.11 = (bf16[1184,256]{1,0:T(8,128)(2,1)S(1)}, bf16[1184,256]{1,0:T(8,128)(2,1)}, u32[]{:S(2)}, u32[]{:S(2)}) collective-permute-start(bf16[1184,256]{1,0:T(8,128)(2,1)S(1)} %dynamic-slice_bitcast_fusion.2), channel_id=1, source_target_pairs={{0,2},{2,0},{1,3},{3,1},{4,6},{6,4},{5,7},{7,5},{8,10},{10,8},{9,1... | collective-permute-start | bytes 1818632 | tf_op jit(solution)/shard_map/ppermute | solution.py:34
  52.0 533.0 %reduce-scatter.7.cloned.1.call-start = ((), (), s32[]{:S(2)}) async-start(), calls=%async_computation.8 | async-start | bytes 655360 | tf_op jit(solution)/shard_map/reduce_scatter | solution.py:248
  52.2 1.3 collective-permute-start.3
  72.0 12.6 %collective-permute-start.1 = (bf16[2,1184,256]{2,1,0:T(8,128)(2,1)S(1)}, bf16[2,1184,256]{2,1,0:T(8,128)(2,1)S(1)}, u32[]{:S(2)}, u32[]{:S(2)}) collective-permute-start(bf16[2,1184,256]{2,1,0:T(8,128)(2,1)S(1)} %pad_maximum_fusion.4), channel_id=1, source_target_pairs={{0,1},{1,0},{2,3},{3,2},{4,5},{5,4},{6,7},{7,6},{8,9},{9,8},{10,11... | collective-permute-start | bytes 3637256 | tf_op jit(solution)/shard_map/ppermute | solution.py:34
  73.3 48.8 %copy-start.65 = (f32[1024]{0:T(1024)}, f32[1024]{0:T(1024)S(1)}, u32[]{:S(2)}) copy-start(f32[1024]{0:T(1024)S(1)} %get-tuple-element.350) | copy-start | bytes 12292
  73.3 48.8 %copy-start.87 = (f32[1024]{0:T(1024)}, f32[1024]{0:T(1024)S(1)}, u32[]{:S(2)}) copy-start(f32[1024]{0:T(1024)S(1)} %get-tuple-element.351) | copy-start | bytes 12292
  84.6 99.1 %collective-permute-start.12 = (bf16[2,1184,256]{2,1,0:T(8,128)(2,1)}, bf16[2,1184,256]{2,1,0:T(8,128)(2,1)}, u32[]{:S(2)}, u32[]{:S(2)}) collective-permute-start(bf16[2,1184,256]{2,1,0:T(8,128)(2,1)} %pad_maximum_fusion.9), channel_id=1, source_target_pairs={{0,1},{1,0},{2,3},{3,2},{4,5},{5,4},{6,7},{7,6},{8,9},{9,8},{10,11... | collective-permute-start | bytes 3637256 | tf_op jit(solution)/shard_map/ppermute | solution.py:34
  85.0 37.2 %copy-start.10 = (bf16[1184,256]{1,0:T(8,128)(2,1)}, bf16[1184,256]{1,0:T(8,128)(2,1)S(1)}, u32[]{:S(2)}) copy-start(bf16[1184,256]{1,0:T(8,128)(2,1)S(1)} %get-tuple-element.288) | copy-start | bytes 1818628
  85.0 37.1 %copy-start.13 = (bf16[1184,256]{1,0:T(8,128)(2,1)}, bf16[1184,256]{1,0:T(8,128)(2,1)S(1)}, u32[]{:S(2)}) copy-start(bf16[1184,256]{1,0:T(8,128)(2,1)S(1)} %get-tuple-element.348) | copy-start | bytes 1818628
  85.0 37.1 %copy-start.16 = (bf16[1184,256]{1,0:T(8,128)(2,1)}, bf16[1184,256]{1,0:T(8,128)(2,1)S(1)}, u32[]{:S(2)}) copy-start(bf16[1184,256]{1,0:T(8,128)(2,1)S(1)} %get-tuple-element.349) | copy-start | bytes 1818628
  85.0 103.6 %copy-start.8 = (bf16[1184,256]{1,0:T(8,128)(2,1)}, bf16[1184,256]{1,0:T(8,128)(2,1)S(1)}, u32[]{:S(2)}) copy-start(bf16[1184,256]{1,0:T(8,128)(2,1)S(1)} %get-tuple-element.287) | copy-start | bytes 1818628
  85.0 37.1 %collective-permute-start.4 = (bf16[1024,768]{1,0:T(8,128)(2,1)}, bf16[1024,768]{1,0:T(8,128)(2,1)S(1)}, u32[]{:S(2)}, u32[]{:S(2)}) collective-permute-start(bf16[1024,768]{1,0:T(8,128)(2,1)} %all-gather.4.cloned.1.call-done), channel_id=1, source_target_pairs={{0,2},{2,0},{1,3},{3,1},{4,6},{6,4},{5,7},{7,5},{8,10},{10,8},{9,1... | collective-permute-start | bytes 4718600 | tf_op jit(solution)/shard_map/ppermute | solution.py:34
  87.4 34.7 %copy-start.61 = (f32[1184]{0:T(1024)}, f32[1184]{0:T(1024)S(1)}, u32[]{:S(2)}) copy-start(f32[1184]{0:T(1024)S(1)} %get-tuple-element.338) | copy-start | bytes 14212
  87.4 34.7 %copy-start.63 = (f32[1184]{0:T(1024)}, f32[1184]{0:T(1024)S(1)}, u32[]{:S(2)}) copy-start(f32[1184]{0:T(1024)S(1)} %get-tuple-element.339) | copy-start | bytes 14212
  183.6 5.1 collective-permute-start.6
  186.6 107.4 %copy-start.39 = (bf16[1184,256]{1,0:T(8,128)(2,1)}, bf16[1184,256]{1,0:T(8,128)(2,1)S(1)}, u32[]{:S(2)}) copy-start(bf16[1184,256]{1,0:T(8,128)(2,1)S(1)} %get-tuple-element.281) | copy-start | bytes 1818628
  186.6 107.4 %collective-permute-start.8 = (bf16[1024,1024]{0,1:T(8,128)(2,1)}, bf16[1024,1024]{0,1:T(8,128)(2,1)}, u32[]{:S(2)}, u32[]{:S(2)}) collective-permute-start(bf16[1024,1024]{0,1:T(8,128)(2,1)} %all-gather.8.cloned.1.call-done), channel_id=1, source_target_pairs={{0,2},{2,0},{1,3},{3,1},{4,6},{6,4},{5,7},{7,5},{8,10},{10,8},{9,1... | collective-permute-start | bytes 6291464 | tf_op jit(solution)/shard_map/ppermute | solution.py:34
  186.9 92.9 %collective-permute-start.7 = (bf16[1024,1024]{1,0:T(8,128)(2,1)}, bf16[1024,1024]{1,0:T(8,128)(2,1)S(1)}, u32[]{:S(2)}, u32[]{:S(2)}) collective-permute-start(bf16[1024,1024]{1,0:T(8,128)(2,1)} %all-gather.6.cloned.1.call-done), channel_id=1, source_target_pairs={{0,2},{2,0},{1,3},{3,1},{4,6},{6,4},{5,7},{7,5},{8,10},{10,8},{9,1... | collective-permute-start | bytes 6291464 | tf_op jit(solution)/shard_map/ppermute | solution.py:34
  193.1 17.5 %copy-start = (f32[1184,1024]{1,0:T(8,128)}, f32[1184,1024]{1,0:T(8,128)S(1)}, u32[]{:S(2)}) copy-start(f32[1184,1024]{1,0:T(8,128)S(1)} %get-tuple-element.249) | copy-start | bytes 14548996
  196.4 83.4 %copy-start.51 = (bf16[1184,1024]{1,0:T(8,128)(2,1)}, bf16[1184,1024]{1,0:T(8,128)(2,1)S(1)}, u32[]{:S(2)}) copy-start(bf16[1184,1024]{1,0:T(8,128)(2,1)S(1)} %add_convert_fusion.4) | copy-start | bytes 7274500
  196.4 14.3 %copy-start.48 = (bf16[1184,256]{1,0:T(8,128)(2,1)S(1)}, bf16[1184,256]{1,0:T(8,128)(2,1)}, u32[]{:S(2)}) copy-start(bf16[1184,256]{1,0:T(8,128)(2,1)} %get-tuple-element.355) | copy-start | bytes 1818628
  196.4 14.3 %copy-start.99 = (bf16[1024,1024]{0,1:T(8,128)(2,1)S(1)}, bf16[1024,1024]{0,1:T(8,128)(2,1)}, u32[]{:S(2)}) copy-start(bf16[1024,1024]{0,1:T(8,128)(2,1)} %all-gather.8.cloned.1.call-done) | copy-start | bytes 6291460
  215.4 64.4 %slice-start.4 = ((f32[3072]{0:T(1024)}), f32[1024]{0:T(1024)S(1)}, s32[]{:S(2)}) async-start(f32[3072]{0:T(1024)} %copy-done.69), calls=%async_computation.15 | async-start | bytes 8192 | tf_op jit(solution)/shard_map/slice | solution.py:171
  303.6 17.7 %collective-permute-start.13 = (bf16[1184,1024]{1,0:T(8,128)(2,1)S(1)}, bf16[1184,1024]{1,0:T(8,128)(2,1)}, u32[]{:S(2)}, u32[]{:S(2)}) collective-permute-start(bf16[1184,1024]{1,0:T(8,128)(2,1)S(1)} %add_convert_fusion.1), channel_id=1, source_target_pairs={{0,1},{1,0},{2,3},{3,2},{4,5},{5,4},{6,7},{7,6},{8,9},{9,8},{10,11... | collective-permute-start | bytes 7274504 | tf_op jit(solution)/shard_map/ppermute | solution.py:34
  303.8 17.5 %slice-start = ((s8[4849664]{0:T(1024)(128)(4,1)}), s8[655360]{0:T(1024)(128)(4,1)S(1)}, s32[]{:S(2)}) async-start(s8[4849664]{0:T(1024)(128)(4,1)} %bitcast.266), calls=%async_computation.11 | async-start | bytes 1310720
  318.3 72.6 %collective-permute-start.22 = (bf16[1024,1024]{1,0:T(8,128)(2,1)}, bf16[1024,1024]{1,0:T(8,128)(2,1)}, u32[]{:S(2)}, u32[]{:S(2)}) collective-permute-start(bf16[1024,1024]{1,0:T(8,128)(2,1)} %convolution_convert_fusion.2), channel_id=1, source_target_pairs={{0,2},{2,0},{1,3},{3,1},{4,6},{6,4},{5,7},{7,5},{8,10},{10,8},{9,1... | collective-permute-start | bytes 6291464 | tf_op jit(solution)/shard_map/ppermute | solution.py:34
  333.2 44.5 %collective-permute-start.18 = (bf16[1024,256]{1,0:T(8,128)(2,1)S(1)}, bf16[1024,256]{1,0:T(8,128)(2,1)S(1)}, u32[]{:S(2)}, u32[]{:S(2)}) collective-permute-start(bf16[1024,256]{1,0:T(8,128)(2,1)S(1)} %convolution_convert_fusion.5), channel_id=1, source_target_pairs={{0,2},{2,0},{1,3},{3,1},{4,6},{6,4},{5,7},{7,5},{8,10},{10,8},{9,1... | collective-permute-start | bytes 1572872 | tf_op jit(solution)/shard_map/ppermute | solution.py:34
  341.0 36.7 %copy-start.21 = (bf16[1184,512]{0,1:T(8,128)(2,1)S(1)}, bf16[1184,512]{0,1:T(8,128)(2,1)}, u32[]{:S(2)}) copy-start(bf16[1184,512]{0,1:T(8,128)(2,1)} %reshape.279) | copy-start | bytes 3637252
  381.2 339.9 %reduce-scatter.11.cloned.1.call-start = ((), (), s32[]{:S(2)}) async-start(), calls=%async_computation.10 | async-start | bytes 2621440 | tf_op jit(solution)/shard_map/reduce_scatter | solution.py:248
  390.8 29.4 %collective-permute-start.9 = (bf16[1184,512]{1,0:T(8,128)(2,1)}, bf16[1184,512]{1,0:T(8,128)(2,1)}, u32[]{:S(2)}, u32[]{:S(2)}) collective-permute-start(bf16[1184,512]{1,0:T(8,128)(2,1)} %bitcast.105), channel_id=1, source_target_pairs={{0,1},{1,0},{2,3},{3,2},{4,5},{5,4},{6,7},{7,6},{8,9},{9,8},{10,11... | collective-permute-start | bytes 3637256 | tf_op jit(solution)/shard_map/ppermute | solution.py:34
  396.5 326.4 %reduce-scatter.9.cloned.1.call-start = ((), (), s32[]{:S(2)}) async-start(), calls=%async_computation.9 | async-start | bytes 2621440 | tf_op jit(solution)/shard_map/reduce_scatter | solution.py:248
  411.2 62.9 %collective-permute-start.20 = (bf16[1024,1024]{1,0:T(8,128)(2,1)}, bf16[1024,1024]{1,0:T(8,128)(2,1)}, u32[]{:S(2)}, u32[]{:S(2)}) collective-permute-start(bf16[1024,1024]{1,0:T(8,128)(2,1)} %convolution_convert_fusion.3), channel_id=1, source_target_pairs={{0,2},{2,0},{1,3},{3,1},{4,6},{6,4},{5,7},{7,5},{8,10},{10,8},{9,1... | collective-permute-start | bytes 6291464 | tf_op jit(solution)/shard_map/ppermute | solution.py:34
  425.3 47.2 %collective-permute-start.10 = (bf16[1184,256]{1,0:T(8,128)(2,1)S(1)}, bf16[1184,256]{1,0:T(8,128)(2,1)S(1)}, u32[]{:S(2)}, u32[]{:S(2)}) collective-permute-start(bf16[1184,256]{1,0:T(8,128)(2,1)S(1)} %bitcast.281), channel_id=1, source_target_pairs={{0,2},{2,0},{1,3},{3,1},{4,6},{6,4},{5,7},{7,5},{8,10},{10,8},{9,1... | collective-permute-start | bytes 1818632 | tf_op jit(solution)/shard_map/ppermute | solution.py:34
  481.6 246.0 %reduce-scatter.5.cloned.1.call-start = ((), (), s32[]{:S(2)}) async-start(), calls=%async_computation.7 | async-start | bytes 1966080 | tf_op jit(solution)/shard_map/reduce_scatter | solution.py:248
  574.2 36.2 %collective-permute-start.16 = (bf16[1024,768]{1,0:T(8,128)(2,1)}, bf16[1024,768]{1,0:T(8,128)(2,1)}, u32[]{:S(2)}, u32[]{:S(2)}) collective-permute-start(bf16[1024,768]{1,0:T(8,128)(2,1)} %convolution_convert_fusion.4), channel_id=1, source_target_pairs={{0,2},{2,0},{1,3},{3,1},{4,6},{6,4},{5,7},{7,5},{8,10},{10,8},{9,1... | collective-permute-start | bytes 4718600 | tf_op jit(solution)/shard_map/ppermute | solution.py:34
  580.7 36.3 %collective-permute-start.14 = (bf16[1184,1024]{1,0:T(8,128)(2,1)}, bf16[1184,1024]{1,0:T(8,128)(2,1)}, u32[]{:S(2)}, u32[]{:S(2)}) collective-permute-start(bf16[1184,1024]{1,0:T(8,128)(2,1)} %add_convert_fusion), channel_id=1, source_target_pairs={{0,1},{1,0},{2,3},{3,2},{4,5},{5,4},{6,7},{7,6},{8,9},{9,8},{10,11... | collective-permute-start | bytes 7274504 | tf_op jit(solution)/shard_map/ppermute | solution.py:34
  585.0 31.2 %copy-start.60 = (bf16[256,256]{1,0:T(8,128)(2,1)S(1)}, bf16[256,256]{1,0:T(8,128)(2,1)}, u32[]{:S(2)}) copy-start(bf16[256,256]{1,0:T(8,128)(2,1)} %reduce-scatter.7.cloned.1.call-done) | copy-start | bytes 393220
  585.0 31.1 %collective-permute-start.19 = (bf16[256,256]{1,0:T(8,128)(2,1)}, bf16[256,256]{1,0:T(8,128)(2,1)S(1)}, u32[]{:S(2)}, u32[]{:S(2)}) collective-permute-start(bf16[256,256]{1,0:T(8,128)(2,1)} %reduce-scatter.7.cloned.1.call-done), channel_id=1, source_target_pairs={{0,16},{16,0},{1,17},{17,1},{2,18},{18,2},{3,19},{19,3},{4,20},{20... | collective-permute-start | bytes 393224 | tf_op jit(solution)/shard_map/ppermute | solution.py:34
  637.3 83.6 %collective-permute-start.15 = (bf16[1184,256]{1,0:T(8,128)(2,1)S(1)}, bf16[1184,256]{1,0:T(8,128)(2,1)S(1)}, u32[]{:S(2)}, u32[]{:S(2)}) collective-permute-start(bf16[1184,256]{1,0:T(8,128)(2,1)S(1)} %dynamic-slice_bitcast_fusion.1), channel_id=1, source_target_pairs={{0,2},{2,0},{1,3},{3,1},{4,6},{6,4},{5,7},{7,5},{8,10},{10,8},{9,1... | collective-permute-start | bytes 1818632 | tf_op jit(solution)/shard_map/ppermute | solution.py:34
  721.1 9.6 %collective-permute-start.23 = (bf16[256,1024]{1,0:T(8,128)(2,1)}, bf16[256,1024]{1,0:T(8,128)(2,1)}, u32[]{:S(2)}, u32[]{:S(2)}) collective-permute-start(bf16[256,1024]{1,0:T(8,128)(2,1)} %reduce-scatter.11.cloned.1.call-done), channel_id=1, source_target_pairs={{0,16},{16,0},{1,17},{17,1},{2,18},{18,2},{3,19},{19,3},{4,20},{20... | collective-permute-start | bytes 1572872 | tf_op jit(solution)/shard_map/ppermute | solution.py:34
  722.9 13.4 %collective-permute-start.21 = (bf16[256,1024]{1,0:T(8,128)(2,1)}, bf16[256,1024]{1,0:T(8,128)(2,1)}, u32[]{:S(2)}, u32[]{:S(2)}) collective-permute-start(bf16[256,1024]{1,0:T(8,128)(2,1)} %reduce-scatter.9.cloned.1.call-done), channel_id=1, source_target_pairs={{0,16},{16,0},{1,17},{17,1},{2,18},{18,2},{3,19},{19,3},{4,20},{20... | collective-permute-start | bytes 1572872 | tf_op jit(solution)/shard_map/ppermute | solution.py:34
  727.6 12.8 %collective-permute-start.17 = (bf16[256,768]{1,0:T(8,128)(2,1)}, bf16[256,768]{1,0:T(8,128)(2,1)S(1)}, u32[]{:S(2)}, u32[]{:S(2)}) collective-permute-start(bf16[256,768]{1,0:T(8,128)(2,1)} %reduce-scatter.5.cloned.1.call-done), channel_id=1, source_target_pairs={{0,16},{16,0},{1,17},{17,1},{2,18},{18,2},{3,19},{19,3},{4,20},{20... | collective-permute-start | bytes 1179656 | tf_op jit(solution)/shard_map/ppermute | solution.py:34
  (110 other events, 623.4 us)
Sparse Core Ops, SparseCore 0:
  10.1 48.1 all-gather.3
  59.9 44.6 all-gather.7
  106.2 43.8 all-gather.5
  381.3 21.3 reduce-scatter.6
  404.8 41.8 reduce-scatter.10
  481.7 43.1 reduce-scatter.8
  616.3 35.0 reduce-scatter.4

commit v2 on v1

v2 whole, which is shorter than its diff:
```python
import functools
import math
import jax
import jax.numpy as jnp
from jax import lax
from jax.sharding import Mesh, PartitionSpec as P
from jax.experimental import pallas as pl
from jax.experimental.pallas import tpu as pltpu

D = 1024
HD = 64
SEQ = 577
PAD = 592
EPS = 1e-06
F32 = jnp.float32
BF16 = jnp.bfloat16
VM = 60 * 1024 * 1024


def mm(a, b):
    return lax.dot_general(a, b, (((1,), (0,)), ((), ())), preferred_element_type=F32)

def mm_nt(a, b):
    return lax.dot_general(a, b, (((1,), (1,)), ((), ())), preferred_element_type=F32)

def mm_tn(a, b):
    return lax.dot_general(a, b, (((0,), (0,)), ((), ())), preferred_element_type=F32)

def row_mean(v):
    return jnp.sum(v, axis=1, keepdims=True) * (1.0 / D)

def stats(rows):
    middle = row_mean(rows)
    spread = row_mean(rows * rows) - middle * middle
    return middle, lax.rsqrt(spread + EPS)

def params(n, **kw):
    return pltpu.CompilerParams(dimension_semantics=("arbitrary",) * n, vmem_limit_bytes=VM, **kw)

def qkv_kernel(x_ref, gain_ref, shift_ref, wn_ref, wf_ref, bn_ref, bf_ref, n_ref, o_ref):
    x = x_ref[...].astype(F32)
    middle, scaled = stats(x)
    n = (((x - middle) * scaled) * gain_ref[...] + shift_ref[...]).astype(BF16)
    n_ref[...] = n
    w = bn_ref.shape[1]
    o_ref[:, :w] = (mm(n, wn_ref[...]) + bn_ref[...]).astype(BF16)
    o_ref[:, w:] = (mm(n, wf_ref[...]) + bf_ref[...]).astype(BF16)

def norm_qkv(x, gain, shift, wn, wf, bn, bf, tm=296):
    rows = x.shape[0]; w = bn.shape[1]
    row = lambda c: pl.BlockSpec((tm, c), lambda i: (i, 0))
    vec = lambda c: pl.BlockSpec((1, c), lambda i: (0, 0))
    whole = lambda s: pl.BlockSpec((D, w), lambda i: (0, 0), pipeline_mode=pl.Buffered(1))
    return pl.pallas_call(qkv_kernel, grid=(rows // tm,), name="norm_qkv",
        in_specs=[row(D), vec(D), vec(D), whole(wn.shape), whole(wf.shape), vec(w), vec(w)],
        out_specs=[row(D), row(2 * w)],
        out_shape=[jax.ShapeDtypeStruct((rows, D), BF16), jax.ShapeDtypeStruct((rows, 2 * w), BF16)],
        compiler_params=params(1))(x, gain, shift, wn, wf, bn, bf)

def attend_kernel(q_ref, k_ref, v_ref, o_ref, p_ref):
    live = lax.broadcasted_iota(jnp.int32, (1, PAD), 1) < SEQ
    for h in range(2):
        cut = slice(HD * h, HD * (h + 1))
        s = mm_nt(q_ref[:, cut] * jnp.asarray(0.125, BF16), k_ref[:, cut])
        s = jnp.where(live, s, -1e30)
        peak = jnp.max(s, axis=1, keepdims=True)
        e = jnp.exp(s - peak)
        total = jnp.sum(e, axis=1, keepdims=True)
        p = (e * (1.0 / total)).astype(BF16)
        p_ref[h] = p
        o_ref[:, cut] = mm(p, v_ref[:, cut]).astype(BF16)

def head_spec(which, pairs):
    return pl.BlockSpec((PAD, 2 * HD), lambda i, p: (i, (p // pairs) * 3 * pairs + which * pairs + p % pairs))

def attend(qkv):
    rows, w3 = qkv.shape
    pairs = w3 // (6 * 2 * HD)
    held = rows // PAD
    return pl.pallas_call(attend_kernel, grid=(held, 2 * pairs), name="attend",
        in_specs=[head_spec(0, pairs), head_spec(1, pairs), head_spec(2, pairs)],
        out_specs=[pl.BlockSpec((PAD, 2 * HD), lambda i, p: (i, p)),
                   pl.BlockSpec((None, 2, PAD, PAD), lambda i, p: (i, p, 0, 0))],
        out_shape=[jax.ShapeDtypeStruct((rows, w3 // 3), BF16),
                   jax.ShapeDtypeStruct((held, 4 * pairs, PAD, PAD), BF16)],
        compiler_params=params(2))(qkv, qkv, qkv)

def attend_back_kernel(q_ref, k_ref, v_ref, p_ref, g_ref, dq_ref, dk_ref, dv_ref):
    for h in range(2):
        cut = slice(HD * h, HD * (h + 1))
        g = g_ref[:, cut]
        pb = p_ref[h]
        p = pb.astype(F32)
        dp = mm_nt(g, v_ref[:, cut])
        z = jnp.sum(p * dp, axis=1, keepdims=True)
        ds = (p * (dp - z)).astype(BF16)
        dq_ref[:, cut] = (mm(ds, k_ref[:, cut]) * 0.125).astype(BF16)
        dk_ref[:, cut] = (mm_tn(ds, q_ref[:, cut]) * 0.125).astype(BF16)
        dv_ref[:, cut] = mm_tn(pb, g).astype(BF16)

def attend_back(qkv, probs, grads):
    rows, w3 = qkv.shape
    pairs = w3 // (6 * 2 * HD)
    held = rows // PAD
    pair = pl.BlockSpec((PAD, 2 * HD), lambda i, p: (i, p))
    out = jax.ShapeDtypeStruct((rows, w3 // 3), BF16)
    return pl.pallas_call(attend_back_kernel, grid=(held, 2 * pairs), name="attend_back",
        in_specs=[head_spec(0, pairs), head_spec(1, pairs), head_spec(2, pairs),
                  pl.BlockSpec((None, 2, PAD, PAD), lambda i, p: (i, p, 0, 0)), pair],
        out_specs=[pair, pair, pair], out_shape=[out, out, out],
        compiler_params=params(2))(qkv, qkv, qkv, probs, grads)

def middle_kernel(x_ref, a_ref, b_ref, bias_ref, gain_ref, shift_ref, h_ref, n_ref):
    h = x_ref[...].astype(F32) + (a_ref[...].astype(F32) + b_ref[...].astype(F32)) + bias_ref[...]
    h_ref[...] = h
    middle, scaled = stats(h)
    n_ref[...] = (((h - middle) * scaled) * gain_ref[...] + shift_ref[...]).astype(BF16)

def middle(x, a, b, bias, gain, shift, tm=296):
    rows = x.shape[0]
    row = pl.BlockSpec((tm, D), lambda i: (i, 0))
    vec = pl.BlockSpec((1, D), lambda i: (0, 0))
    return pl.pallas_call(middle_kernel, grid=(rows // tm,), name="middle",
        in_specs=[row, row, row, vec, vec, vec], out_specs=[row, row],
        out_shape=[jax.ShapeDtypeStruct((rows, D), F32), jax.ShapeDtypeStruct((rows, D), BF16)],
        compiler_params=params(1))(x, a, b, bias, gain, shift)

ROOT_HALF = math.sqrt(0.5)
DENSITY = 1.0 / math.sqrt(2.0 * math.pi)

def mlp_kernel(tiles, n_ref, dy_ref, *refs):
    ups, downs, biases = refs[0:4], refs[4:8], refs[8:12]
    g_ref, du_ref, low_ref, lift_ref, bsum_ref, low_acc, lift_acc = refs[12:]
    j = pl.program_id(0)

    @pl.when(j == 0)
    def _():
        low_acc[...] = jnp.zeros_like(low_acc)
        lift_acc[...] = jnp.zeros_like(lift_acc)

    def step(up_ref, down_ref, bias_ref):
        u = mm(n_ref[...], up_ref[...]) + bias_ref[...]
        cdf = 0.5 * (1.0 + lax.erf(u * ROOT_HALF))
        g = (u * cdf).astype(BF16)
        slope = cdf + u * (jnp.exp(-0.5 * u * u) * DENSITY)
        g_ref[...] = g
        du = (mm(dy_ref[...], down_ref[...]) * slope).astype(BF16)
        du_ref[...] = du
        bsum_ref[...] = jnp.sum(du.astype(F32), axis=0, keepdims=True)
        low_acc[...] += mm_nt(g, down_ref[...])
        lift_acc[...] += mm_nt(du, up_ref[...])

    for block in range(4):

        @pl.when((j >= block * tiles) & (j < (block + 1) * tiles))
        def _(block=block):
            step(ups[block], downs[block], biases[block])

    @pl.when(j == 4 * tiles - 1)
    def _():
        low_ref[...] = low_acc[...].astype(BF16)
        lift_ref[...] = lift_acc[...].astype(BF16)


def mlp(n2, dy, packs, biases, tn=256):
    rows = n2.shape[0]
    half = packs[0].shape[1] // 2
    tiles = half // tn
    hid = 4 * half
    whole = pl.BlockSpec((rows, D), lambda j: (0, 0), pipeline_mode=pl.Buffered(1))

    def part(height, block, skip):
        return pl.BlockSpec(
            (height, tn), lambda j: (0, jnp.clip(j - block * tiles, 0, tiles - 1) + skip)
        )

    tile = pl.BlockSpec((rows, tn), lambda j: (0, j))
    return pl.pallas_call(
        functools.partial(mlp_kernel, tiles),
        grid=(4 * tiles,),
        name="mlp",
        in_specs=[whole, whole]
        + [part(D, block, 0) for block in range(4)]
        + [part(D, block, tiles) for block in range(4)]
        + [part(1, block, 0) for block in range(4)],
        out_specs=[tile, tile, whole, whole, pl.BlockSpec((1, tn), lambda j: (0, j))],
        out_shape=[
            jax.ShapeDtypeStruct((rows, hid), BF16),
            jax.ShapeDtypeStruct((rows, hid), BF16),
            jax.ShapeDtypeStruct((rows, D), BF16),
            jax.ShapeDtypeStruct((rows, D), BF16),
            jax.ShapeDtypeStruct((1, hid), F32),
        ],
        scratch_shapes=[pltpu.VMEM((rows, D), F32), pltpu.VMEM((rows, D), F32)],
        compiler_params=params(1),
    )(n2, dy, *packs, *packs, *biases)


def turn_kernel(h_ref, dy_ref, a_ref, b_ref, gain_ref, wn_ref, wf_ref, dh_ref, da_ref, do_ref, sums_ref):
    i = pl.program_id(0)
    h = h_ref[...]
    middle, scaled = stats(h)
    c = (h - middle) * scaled
    dn = a_ref[...].astype(F32) + b_ref[...].astype(F32)
    dy = dy_ref[...].astype(F32)
    e = dn * gain_ref[...]
    dh = dy + scaled * (e - row_mean(e) - c * row_mean(e * c))
    dh_ref[...] = dh
    da = dh.astype(BF16)
    da_ref[...] = da
    w = wn_ref.shape[1]
    do_ref[:, :w] = mm(da, wn_ref[...]).astype(BF16)
    do_ref[:, w:] = mm(da, wf_ref[...]).astype(BF16)
    col = lambda v: jnp.sum(v, axis=0, keepdims=True)
    part = jnp.concatenate([col(dn * c), col(dn), col(da.astype(F32)), col(dy)], axis=0)
    @pl.when(i == 0)
    def _(): sums_ref[...] = part
    @pl.when(i > 0)
    def _(): sums_ref[...] += part

def turn(h, dy, a, b, gain, wn, wf, tm=296):
    rows = h.shape[0]; w = wn.shape[1] // 4
    row = lambda c: pl.BlockSpec((tm, c), lambda i: (i, 0))
    vec = pl.BlockSpec((1, D), lambda i: (0, 0))
    whole = pl.BlockSpec((D, w), lambda i: (0, 3), pipeline_mode=pl.Buffered(1))
    return pl.pallas_call(turn_kernel, grid=(rows // tm,), name="turn",
        in_specs=[row(D), row(D), row(D), row(D), vec, whole, whole],
        out_specs=[row(D), row(D), row(2 * w), pl.BlockSpec((4, D), lambda i: (0, 0))],
        out_shape=[jax.ShapeDtypeStruct((rows, D), F32), jax.ShapeDtypeStruct((rows, D), BF16),
                   jax.ShapeDtypeStruct((rows, 2 * w), BF16), jax.ShapeDtypeStruct((4, D), F32)],
        compiler_params=params(1))(h, dy, a, b, gain, wn, wf)

def last_kernel(x_ref, dh_ref, a_ref, b_ref, gain_ref, o_ref, sums_ref):
    i = pl.program_id(0)
    x = x_ref[...].astype(F32)
    middle, scaled = stats(x)
    c = (x - middle) * scaled
    dn = a_ref[...].astype(F32) + b_ref[...].astype(F32)
    e = dn * gain_ref[...]
    o_ref[...] = (dh_ref[...] + scaled * (e - row_mean(e) - c * row_mean(e * c))).astype(BF16)
    part = jnp.concatenate([jnp.sum(dn * c, axis=0, keepdims=True), jnp.sum(dn, axis=0, keepdims=True)], axis=0)
    @pl.when(i == 0)
    def _(): sums_ref[...] = part
    @pl.when(i > 0)
    def _(): sums_ref[...] += part

def last(x, dh, a, b, gain, tm=296):
    rows = x.shape[0]
    row = pl.BlockSpec((tm, D), lambda i: (i, 0))
    vec = pl.BlockSpec((1, D), lambda i: (0, 0))
    return pl.pallas_call(last_kernel, grid=(rows // tm,), name="last",
        in_specs=[row, row, row, row, vec], out_specs=[row, pl.BlockSpec((2, D), lambda i: (0, 0))],
        out_shape=[jax.ShapeDtypeStruct((rows, D), BF16), jax.ShapeDtypeStruct((2, D), F32)],
        compiler_params=params(1))(x, dh, a, b, gain)


def local(
    sizes,
    inputs,
    query_weight,
    key_weight,
    value_weight,
    query_bias,
    value_bias,
    out_weight,
    out_bias,
    up_weight,
    up_bias,
    down_weight,
    down_bias,
    first_gain,
    first_shift,
    second_gain,
    second_shift,
    cotangent,
):
    n_dp, n_row, n_xa, n_core = sizes
    my_x = lax.axis_index("xa")
    my_core = lax.axis_index("core")
    my_row = lax.axis_index("row")
    my_half = lax.axis_index("dp") % 2
    tokens_here, width = inputs.shape
    images = tokens_here // SEQ
    held = images // n_xa
    rows = held * PAD
    hidden = up_weight.shape[1]
    half = hidden // 2

    def swap(value, axis, size, bit=1):
        return lax.ppermute(value, axis, [(place, place ^ bit) for place in range(size)])

    def across(value):
        return swap(value, "xa", n_xa)

    def beside(value):
        return swap(value, "core", n_core)

    def over(value):
        return swap(value, "dp", n_dp)

    def pick(value, place, axis):
        return lax.dynamic_index_in_dim(value, place, axis, keepdims=False)

    def in_order(mine, other, place):
        return jnp.where(place == 0, mine, other), jnp.where(place == 0, other, mine)

    def wide_tokens(value):
        padded = jnp.pad(value.reshape(images, SEQ, -1), ((0, 0), (0, PAD - SEQ), (0, 0)))
        halves = padded.reshape(n_xa, rows, -1)
        mine, theirs = pick(halves, my_x, 0), pick(halves, my_x ^ 1, 0)
        got = across(theirs)
        pair = jnp.concatenate([mine, got], axis=1)
        other = beside(pair)
        left, right = in_order(pair, other, my_core)
        first_left, second_left = in_order(left[:, :width], left[:, width:], my_x)
        first_right, second_right = in_order(right[:, :width], right[:, width:], my_x)
        return jnp.concatenate([first_left, first_right, second_left, second_right], axis=1)

    small = jnp.concatenate(
        [
            out_bias,
            down_bias,
            first_gain,
            first_shift,
            second_gain,
            second_shift,
            query_bias,
            value_bias,
            up_bias,
        ]
    )
    small_far = across(small)
    small_pair = jnp.stack(in_order(small, small_far, my_x))
    small_left, small_right = in_order(small_pair, beside(small_pair), my_core)

    def whole_vector(place):
        cut = slice(width * place, width * (place + 1))
        return jnp.concatenate(
            [small_left[0, cut], small_right[0, cut], small_left[1, cut], small_right[1, cut]]
        )[None]

    out_bias_all, down_bias_all, gain_one, shift_one, gain_two, shift_two = (
        whole_vector(place) for place in range(6)
    )
    query_bias_far = small_far[6 * width : 7 * width]
    value_bias_far = small_far[7 * width : 8 * width]
    up_bias_far = small_far[8 * width :]

    shard = jnp.concatenate([query_weight, key_weight, value_weight, out_weight.T], axis=1)
    near = jnp.zeros((D, 4 * width), BF16)
    far = jnp.zeros((D, 4 * width), BF16)
    for shift in range(n_row):
        piece = shard
        if shift:
            piece = lax.ppermute(
                shard, "row", [(place, (place + shift) % n_row) for place in range(n_row)]
            )
        start = (my_row - shift) % n_row * (D // n_row)
        near = lax.dynamic_update_slice(near, piece, (start, 0))
        far = lax.dynamic_update_slice(far, across(piece), (start, 0))

    def halves(value, axis):
        shape = value.shape[:axis] + (2, half) + value.shape[axis + 1 :]
        both = value.reshape(shape)
        return pick(both, my_half, axis), pick(both, my_half ^ 1, axis)

    up_own, _ = halves(up_weight, 1)
    down_own, _ = halves(down_weight, 0)
    own_shard = jnp.concatenate([up_own, down_own.T], axis=1)
    near_own = lax.all_gather(own_shard, "row", axis=0, tiled=True)
    near_oth = over(near_own)
    far_own = across(near_own)
    far_oth = across(near_oth)
    bias_near_own, bias_near_oth = halves(up_bias[None], 1)
    bias_far_own, bias_far_oth = halves(up_bias_far[None], 1)

    wide_input = wide_tokens(inputs)
    wide_grad = wide_tokens(cotangent)

    zeros = jnp.zeros_like(query_bias)
    bias_near = jnp.concatenate([query_bias, zeros, value_bias])[None]
    bias_far = jnp.concatenate([query_bias_far, zeros, value_bias_far])[None]
    wide_one, qkv = norm_qkv(wide_input, gain_one, shift_one, near, far, bias_near, bias_far)
    attended, probs = attend(qkv)
    mixed = mm_nt(attended[:, :width], near[:, 3 * width :])
    mixed = (mixed + mm_nt(attended[:, width:], far[:, 3 * width :])).astype(BF16)
    middle_sum, wide_two = middle(
        wide_input, mixed, beside(mixed), out_bias_all, gain_two, shift_two
    )
    gate, pre, lowered, lifted_two, up_sums = mlp(
        wide_two,
        wide_grad,
        (near_own, near_oth, far_own, far_oth),
        (bias_near_own, bias_near_oth, bias_far_own, bias_far_oth),
    )

    def block(value, place):
        return value[:, half * place : half * (place + 1)]

    def to_wire(value):
        return value.astype(BF16)

    def wide_add(mine, got):
        return (mine.astype(F32) + got.astype(F32)).astype(BF16)

    lifted_other = beside(lifted_two)
    down_far = to_wire(mm_tn(wide_grad, gate[:, 2 * half :]))
    down_near = wide_add(mm_tn(wide_grad, gate[:, : 2 * half]), across(down_far))
    down_sum = wide_add(block(down_near, 0), over(block(down_near, 1)))
    up_oth = jnp.concatenate(
        [to_wire(mm_tn(wide_two, block(pre, 1))), to_wire(mm_tn(wide_two, block(pre, 3)))], axis=1
    )
    up_got = over(up_oth)
    up_far = wide_add(mm_tn(wide_two, block(pre, 2)), block(up_got, 1))
    up_near = wide_add(mm_tn(wide_two, block(pre, 0)), block(up_got, 0))
    up_sum = wide_add(up_near, across(up_far))
    mlp_piece = lax.psum_scatter(
        jnp.concatenate([up_sum, down_sum], axis=1), "row", scatter_dimension=0, tiled=True
    )
    if n_dp > 2:
        pairs = [[place + bit for place in range(0, n_dp, 2)] for bit in range(2)]
        mlp_piece = lax.psum(mlp_piece.astype(F32), "dp", axis_index_groups=pairs).astype(BF16)
    mlp_other = over(mlp_piece)
    up_first, up_second = in_order(mlp_piece[:, :half], mlp_other[:, :half], my_half)
    down_first, down_second = in_order(mlp_piece[:, half:], mlp_other[:, half:], my_half)
    up_grad = jnp.concatenate([up_first, up_second], axis=1).astype(F32)
    down_grad = jnp.concatenate([down_first, down_second], axis=1).astype(F32).T

    def to_feature_blocks(pair):
        mine, theirs = pick(pair, my_x, 1), pick(pair, my_x ^ 1, 1)
        got = across(theirs)
        first, second = in_order(mine, got, my_x)
        both = jnp.concatenate([first, second]).reshape(images, PAD, width)
        return both[:, :SEQ].reshape(tokens_here, width)

    def feature_split(value):
        return value.reshape(value.shape[0], n_xa, 2, width)

    low_parts = feature_split(lowered)
    branch = pick(low_parts, my_core, 2).astype(F32) + beside(
        pick(low_parts, my_core ^ 1, 2)
    ).astype(F32)
    total = pick(feature_split(middle_sum), my_core, 2) + branch
    total = total + pick(feature_split(down_bias_all), my_core, 2)
    outputs = to_feature_blocks(total.astype(BF16))

    middle_grad, attn_grad, head_grad, turn_sums = turn(
        middle_sum, wide_grad, lifted_two, lifted_other, gain_two, near, far
    )
    dqueries, key_grads, dvalues = attend_back(qkv, probs, head_grad)

    def column_block(value, place):
        return value[:, width * place : width * (place + 1)]

    def four(place):
        out_part = to_wire(mm_tn(attn_grad, column_block(attended, place)))
        return jnp.concatenate(
            [
                to_wire(mm_tn(wide_one, column_block(item, place)))
                for item in (dqueries, key_grads, dvalues)
            ]
            + [out_part],
            axis=1,
        )

    attn_far = four(1)
    attn_sum = wide_add(four(0), across(attn_far))
    attn_piece = lax.psum_scatter(attn_sum, "row", scatter_dimension=0, tiled=True)
    if n_dp > 2:
        attn_weights = lax.psum(attn_piece.astype(F32), "dp")
    else:
        attn_weights = attn_piece.astype(F32) + over(attn_piece).astype(F32)

    lifted_one = mm_nt(dqueries[:, :width], near[:, :width])
    for place, (item, part) in enumerate(
        (item, part) for item in (dqueries, key_grads, dvalues) for part in range(2)
    ):
        if place:
            side = (near, far)[part]
            lifted_one = lifted_one + mm_nt(
                column_block(item, part), column_block(side, place // 2)
            )
    lifted_one = to_wire(lifted_one)
    input_wide, last_sums = last(wide_input, middle_grad, lifted_one, beside(lifted_one), gain_one)
    input_grad = to_feature_blocks(pick(feature_split(input_wide), my_core, 2)).astype(F32)

    def own_features(value):
        return pick(value.reshape(-1, n_xa, 2, width), my_core, 2)

    def column_sum(value):
        return jnp.sum(value.astype(F32), axis=0)

    def by_x(near_sum, far_sum):
        return jnp.stack(in_order(near_sum, far_sum, my_x))

    def everywhere(value):
        value = value + across(value)
        bit = 1
        while bit < n_row:
            value = value + swap(value, "row", n_row, bit)
            bit *= 2
        bit = 1
        while bit < n_dp:
            value = value + swap(value, "dp", n_dp, bit)
            bit *= 2
        return pick(value, my_x, 0)

    query_sums, value_sums = column_sum(dqueries), column_sum(dvalues)
    turn_own = own_features(turn_sums)
    up_sums = up_sums[0].reshape(2, 2, half)
    up_ordered = jnp.concatenate(
        in_order(up_sums[:, 0], up_sums[:, 1], my_half), axis=1
    )
    early = everywhere(
        jnp.concatenate(
            [
                by_x(query_sums[:width], query_sums[width:]),
                by_x(value_sums[:width], value_sums[width:]),
                turn_own[2],
                turn_own[3],
                turn_own[0],
                turn_own[1],
                by_x(up_ordered[0], up_ordered[1]),
            ],
            axis=1,
        )
    )
    last_own = own_features(last_sums)
    late = everywhere(jnp.concatenate([last_own[0], last_own[1]], axis=1))

    def piece_of(value, place):
        return value[width * place : width * (place + 1)]

    return (
        outputs,
        input_grad,
        column_block(attn_weights, 0),
        column_block(attn_weights, 1),
        column_block(attn_weights, 2),
        piece_of(early, 0),
        piece_of(early, 1),
        column_block(attn_weights, 3).T,
        piece_of(early, 2),
        up_grad,
        early[6 * width :],
        down_grad,
        piece_of(early, 3),
        piece_of(late, 0),
        piece_of(late, 1),
        piece_of(early, 4),
        piece_of(early, 5),
    )


def solution(mesh):
    n_dp, n_row, n_col = (mesh.shape[name] for name in ("dp", "row", "col"))
    sizes = (n_dp, n_row, n_col // 2, 2)
    split = Mesh(mesh.devices.reshape(sizes), ("dp", "row", "xa", "core"))
    col = ("xa", "core")
    tokens, rows, cols, vec = P(("dp", "row"), col), P("row", col), P(col, "row"), P(col)
    in_specs = (
        (tokens, rows, rows, rows, vec, vec, cols, vec, rows, vec, cols)
        + (vec,) * 5
        + (tokens,)
    )
    out_specs = (
        (tokens, tokens, rows, rows, rows, vec, vec, cols, vec, rows, vec, cols) + (vec,) * 5
    )
    return jax.shard_map(
        functools.partial(local, sizes),
        mesh=split,
        in_specs=in_specs,
        out_specs=out_specs,
        check_vma=False,
    )
```

time: 759 us -> 574 us (0.76)
  Pallas kernels: 0 us -> 118 us
  matrix products: 157 us -> 48.9 us
  blocking collectives: 105 us -> 0 us
  local copies, waits for them, and re-layouts: 157 us -> 92.6 us
  other arithmetic: 71.8 us -> 39 us
  starting transfers between devices: 17.9 us -> 49.7 us
  waiting for transfers between devices: 223 us -> 204 us
    pallas_call x0 -> x7, Pallas kernels: none -> 118 us  [the longest x1 35.1 us: mlp(): pl.pallas_call(functools.partial(mlp_kernel, tiles), grid=(4 * tiles,), n...]
    dot_general x38 -> x22, matrix products: 157 us -> 48.9 us  [the longest x14 31.3 us: mm_tn(): lax.dot_general(a, b, (((0,), (0,)), ((), ())), preferred_element_type=F32)]
    psum x1 -> x0, blocking collectives: 81.5 us -> none  [local(): lax.psum(vectors, ('dp', 'row', 'xa'))]
    while x52 -> x0, local copies, waits for them, and re-layouts: 31.7 us -> none  [the longest x4 14.3 us: local(): lax.map(attend_image, (query_heads, key_heads, value_heads))]
    ppermute x24 -> x37, starting transfers between devices: 17.6 us -> 49.1 us  [the longest x34 42.1 us: swap(): lax.ppermute(value, axis, [(place, place ^ bit) for place in range(size)])]
    all_gather x1 -> x0, blocking collectives: 23.6 us -> none  [gather_rows(): return lax.all_gather(value, 'row', axis=0, tiled=True)]
    reshape x19 -> x8, local copies, waits for them, and re-layouts: 48.9 us -> 26.4 us  [the longest x3 19 us: feature_split(): return value.reshape(value.shape[0], n_xa, 2, width)]
    ppermute x24 -> x37, waiting for transfers between devices: 222 us -> 204 us  [the longest x34 204 us: swap(): lax.ppermute(value, axis, [(place, place ^ bit) for place in range(size)])]
  transfers between devices with their start and end apart: 31 -> 40, of which waited for: 11 -> 17; matrix products, arithmetic and copies ran while one was open for 49% -> 28% of each run, Pallas kernels for 0% -> 15%
where the time goes in v2:
time: 574 us; the launch traced here: 567 us
  waiting for transfers between devices  204 us (36%)
  Pallas kernels  118 us (21%)
  local copies, waits for them, and re-layouts  92.6 us (16%)
  starting transfers between devices  49.7 us (9%)
  matrix products  48.9 us (9%)
  other arithmetic  39 us (7%)
  between operations  15.4 us (3%)
    ppermute x34, waiting for transfers between devices, swap(): lax.ppermute(value, axis, [(place, place ^ bit) for place in range(size)])  204 us
    ppermute x34, starting transfers between devices, swap(): lax.ppermute(value, axis, [(place, place ^ bit) for place in range(size)])  42.1 us
    pallas_call x1, Pallas kernels, mlp(): pl.pallas_call(functools.partial(mlp_kernel, tiles), grid=(4 * tiles,), n...  35.1 us
    dot_general x14, matrix products, mm_tn(): lax.dot_general(a, b, (((0,), (0,)), ((), ())), preferred_element_type=F32)  31.3 us
    pallas_call x1, Pallas kernels, attend_back(): pl.pallas_call(attend_back_kernel, grid=(held, 2 * pairs), name='attend_b...  26.6 us
    pallas_call x1, Pallas kernels, attend(): pl.pallas_call(attend_kernel, grid=(held, 2 * pairs), name='attend', in_s...  20.6 us
    unnamed x188, local copies, waits for them, and re-layouts  20.4 us
    reshape x3, local copies, waits for them, and re-layouts, feature_split(): return value.reshape(value.shape[0], n_xa, 2, width)  19 us
  transfers between devices with their start and end apart: 40, of which 17 were waited for; matrix products, arithmetic and copies ran while one was open for 28% of the time, Pallas kernels for 15%

profile of v2, /device:TPU:0, one launch (start us, length us, event | category | flops | bytes accessed | tf_op | source)
XLA Modules:
  0.0 567.2 jit_solution(8557865001906192824)
XLA Ops:
  9.8 3.1 collective-permute-start.4
  12.8 2.6 collective-permute-start.5
  33.0 2.6 reshape.119
  35.6 2.6 reshape.122
  38.2 2.5 pad.7
  50.5 12.9 %collective-permute-done = bf16[1184,256]{1,0:T(8,128)(2,1)S(1)} collective-permute-done((bf16[1184,256]{1,0:T(8,128)(2,1)}, bf16[1184,256]{1,0:T(8,128)(2,1)S(1)}, u32[]{:S(2)}, u32[]{:S(2)}) %collective-permute-start) | collective-permute-done | bytes 606240 | tf_op jit(solution)/shard_map/ppermute | solution.py:290
  76.3 3.9 collective-permute-done.12
  81.3 10.1 %collective-permute-done.8 = bf16[256,1024]{1,0:T(8,128)(2,1)S(1)} collective-permute-done((bf16[256,1024]{1,0:T(8,128)(2,1)}, bf16[256,1024]{1,0:T(8,128)(2,1)S(1)}, u32[]{:S(2)}, u32[]{:S(2)}) %collective-permute-start.8) | collective-permute-done | bytes 524320 | tf_op jit(solution)/shard_map/ppermute | solution.py:290
  92.3 10.4 %collective-permute-done.9 = bf16[256,1024]{1,0:T(8,128)(2,1)S(1)} collective-permute-done((bf16[256,1024]{1,0:T(8,128)(2,1)}, bf16[256,1024]{1,0:T(8,128)(2,1)S(1)}, u32[]{:S(2)}, u32[]{:S(2)}) %collective-permute-start.9) | collective-permute-done | bytes 524320 | tf_op jit(solution)/shard_map/ppermute | solution.py:290
  103.5 9.2 %collective-permute-done.10 = bf16[256,1024]{1,0:T(8,128)(2,1)S(1)} collective-permute-done((bf16[256,1024]{1,0:T(8,128)(2,1)}, bf16[256,1024]{1,0:T(8,128)(2,1)S(1)}, u32[]{:S(2)}, u32[]{:S(2)}) %collective-permute-start.10) | collective-permute-done | bytes 524320 | tf_op jit(solution)/shard_map/ppermute | solution.py:290
  117.6 8.8 %norm_qkv.1 = (bf16[1184,1024]{1,0:T(8,128)(2,1)}, bf16[1184,1536]{1,0:T(8,128)(2,1)}) custom-call(bf16[1184,1024]{1,0:T(8,128)(2,1)} %pad_maximum_fusion.x_ref, f32[1,1024]{1,0:T(1,128)} %bitcast.151, f32[1,1024]{1,0:T(1,128)} %bitcast.159, bf16[1024,1024]{1,0:T(8,128)(2,1)} %copy-done.2, bf16[1024,1024]{1,0:T(8,128)(2,1)} %constant_dynamic-update-slice_fusion.8.wf_ref, ...), custom_call_target="tpu_custom_call" | custom-call | tf_op jit(solution)/shard_map/norm_qkv/pallas_call | solution.py:54
  126.3 20.6 %attend.1 = (bf16[1184,512]{1,0:T(8,128)(2,1)}, bf16[2,8,592,592]{3,2,1,0:T(8,128)(2,1)}) custom-call(bf16[1184,1536]{1,0:T(8,128)(2,1)} %get-tuple-element.37.q_ref.k_ref.v_ref, bf16[1184,1536]{1,0:T(8,128)(2,1)} %get-tuple-element.37.q_ref.k_ref.v_ref, bf16[1184,1536]{1,0:T(8,128)(2,1)} %get-tuple-element.37.q_ref.k_ref.v_ref), custom_call_target="tpu_custom_call" | custom-call | tf_op jit(solution)/shard_map/attend/pallas_call | solution.py:80
  155.5 5.4 collective-permute-done.14.refs_1_.refs_5_
  167.7 6.7 %middle.1 = (f32[1184,1024]{1,0:T(8,128)}, bf16[1184,1024]{1,0:T(8,128)(2,1)}) custom-call(bf16[1184,1024]{1,0:T(8,128)(2,1)} %pad_maximum_fusion.x_ref, bf16[1184,1024]{1,0:T(8,128)(2,1)} %copy-done.6, bf16[1184,1024]{1,0:T(8,128)(2,1)} %collective-permute-done.11.b_ref, f32[1,1024]{1,0:T(1,128)} %bitcast.157, f32[1,1024]{1,0:T(1,128)} %bitcast.147, ...), custom_call_target="tpu_custom_call" | custom-call | tf_op jit(solution)/shard_map/middle/pallas_call | solution.py:123
  174.4 7.6 %reshape.121 = f32[1184,2,2,256]{3,2,1,0:T(2,128)} reshape(f32[1184,1024]{1,0:T(8,128)} %get-tuple-element.39.h_ref) | data formatting | bytes 9699328 | tf_op jit(solution)/shard_map/reshape | solution.py:437
  182.0 6.1 %constant_dynamic-slice_fusion.19 = f32[1184,2,1,256]{3,2,1,0:T(1,128)} fusion(f32[1184,2,2,256]{3,2,1,0:T(2,128)} %reshape.121, s32[]{:T(128)S(6)} %select_n.284), kind=kLoop, calls=%fused_computation.140 | loop fusion | bytes 4849668 | tf_op jit(solution)/shard_map/jit(dynamic_index_in_dim)/dynamic_slice | solution.py:302
  188.1 14.7 %collective-permute-done.15.refs_2_.refs_6_ = bf16[1024,1024]{1,0:T(8,128)(2,1)} collective-permute-done((bf16[1024,1024]{1,0:T(8,128)(2,1)}, bf16[1024,1024]{1,0:T(8,128)(2,1)}, u32[]{:S(2)}, u32[]{:S(2)}) %collective-permute-start.15) | collective-permute-done | bytes 2097184 | tf_op jit(solution)/shard_map/ppermute | solution.py:290
  202.9 44.3 %collective-permute-done.16.refs_3_.refs_7_ = bf16[1024,1024]{1,0:T(8,128)(2,1)} collective-permute-done((bf16[1024,1024]{1,0:T(8,128)(2,1)}, bf16[1024,1024]{1,0:T(8,128)(2,1)}, u32[]{:S(2)}, u32[]{:S(2)}) %collective-permute-start.16) | collective-permute-done | bytes 2097184 | tf_op jit(solution)/shard_map/ppermute | solution.py:290
  247.2 35.1 %mlp.1 = (bf16[1184,2048]{1,0:T(8,128)(2,1)}, bf16[1184,2048]{1,0:T(8,128)(2,1)}, bf16[1184,1024]{1,0:T(8,128)(2,1)}, bf16[1184,1024]{1,0:T(8,128)(2,1)}, f32[1,2048]{1,0:T(1,128)}) custom-call(bf16[1184,1024]{1,0:T(8,128)(2,1)} %get-tuple-element.40.n_ref, bf16[1184,1024]{1,0:T(8,128)(2,1)} %pad_maximum_fusion.1.dy_ref, ...), custom_call_target="tpu_custom_call" | custom-call | tf_op jit(solution)/shard_map/mlp/pallas_call | solution.py:178
  282.3 5.7 %reshape.126 = bf16[1184,2,2,256]{3,2,1,0:T(2,128)(2,1)S(1)} reshape(bf16[1184,1024]{1,0:T(8,128)(2,1)} %get-tuple-element.41) | data formatting | bytes 4849664 | tf_op jit(solution)/shard_map/reshape | solution.py:437
  288.0 5.9 %constant_dynamic-slice_fusion.12 = (bf16[1184,2,1,256]{3,2,1,0:T(2,128)(2,1)}, bf16[1184,2,1,256]{3,2,1,0:T(2,128)(2,1)S(1)}) fusion(bf16[1184,2,2,256]{3,2,1,0:T(2,128)(2,1)S(1)} %reshape.126, s32[]{:T(128)S(6)} %select_n.284, s32[]{:T(128)S(6)} %select_n.294), kind=kLoop, calls=%fused_computation.133 | loop fusion | bytes 4849672 | tf_op jit(solution)/shard_map/jit(dynamic_index_in_dim)/dynamic_slice | solution.py:302
  295.8 4.4 fusion.7
  301.7 2.6 convolution_convert_fusion
  304.2 2.6 convolution_convert_fusion.1
  311.8 2.6 fusion.2
  316.8 32.1 %collective-permute-done.30 = bf16[1024,1024]{0,1:T(8,128)(2,1)} collective-permute-done((bf16[1024,1024]{0,1:T(8,128)(2,1)}, bf16[1024,1024]{0,1:T(8,128)(2,1)}, u32[]{:S(2)}, u32[]{:S(2)}) %collective-permute-start.30) | collective-permute-done | bytes 2097184 | tf_op jit(solution)/shard_map/ppermute | solution.py:290
  349.0 5.6 add_convert_fusion.2
  356.3 2.2 collective-permute-done.28
  358.5 2.6 add_convert_fusion.6
  361.1 2.6 add_convert_fusion.7
  363.7 11.1 %turn.1 = (f32[1184,1024]{1,0:T(8,128)}, bf16[1184,1024]{1,0:T(8,128)(2,1)}, bf16[1184,512]{1,0:T(8,128)(2,1)}, f32[4,1024]{1,0:T(4,128)}) custom-call(f32[1184,1024]{1,0:T(8,128)} %get-tuple-element.39.h_ref, bf16[1184,1024]{1,0:T(8,128)(2,1)} %pad_maximum_fusion.1.dy_ref, bf16[1184,1024]{1,0:T(8,128)(2,1)} %get-tuple-element.42.a_ref, ...), custom_call_target="tpu_custom_call" | custom-call | tf_op jit(solution)/shard_map/turn/pallas_call | solution.py:226
  374.8 26.6 %attend_back.1 = (bf16[1184,512]{1,0:T(8,128)(2,1)}, bf16[1184,512]{1,0:T(8,128)(2,1)}, bf16[1184,512]{1,0:T(8,128)(2,1)}) custom-call(bf16[1184,1536]{1,0:T(8,128)(2,1)} %get-tuple-element.37.q_ref.k_ref.v_ref, bf16[1184,1536]{1,0:T(8,128)(2,1)} %get-tuple-element.37.q_ref.k_ref.v_ref, bf16[1184,1536]{1,0:T(8,128)(2,1)} %get-tuple-element.37.q_ref.k_ref.v_ref, ...), custom_call_target="tpu_custom_call" | custom-call | tf_op jit(solution)/shard_map/attend_back/pallas_call | solution.py:107
  407.8 3.1 fusion.19
  411.7 4.7 add_convert_fusion.a_ref
  416.5 2.8 add_convert_fusion.4
  423.0 2.8 convolution_convert_fusion.4
  432.9 2.8 convolution_convert_fusion.6
  439.5 38.4 %collective-permute-done.22 = bf16[1024,1024]{0,1:T(8,128)(2,1)} collective-permute-done((bf16[1024,1024]{0,1:T(8,128)(2,1)}, bf16[1024,1024]{0,1:T(8,128)(2,1)}, u32[]{:S(2)}, u32[]{:S(2)}) %collective-permute-start.22) | collective-permute-done | bytes 2097184 | tf_op jit(solution)/shard_map/ppermute | solution.py:290
  477.8 4.0 add_convert_fusion.3
  485.8 9.8 %collective-permute-start.25 = (f32[2,2560]{1,0:T(2,128)S(1)}, f32[2,2560]{1,0:T(2,128)S(1)}, u32[]{:S(2)}, u32[]{:S(2)}) collective-permute-start(f32[2,2560]{1,0:T(2,128)S(1)} %add.205), channel_id=1, source_target_pairs={{0,4},{4,0},{8,12},{12,8},{1,5},{5,1},{9,13},{13,9},{2,6},{6,2},{1... | collective-permute-start | bytes 61448 | tf_op jit(solution)/shard_map/ppermute | solution.py:290
  495.6 2.4 bitcast_select_fusion.1
  498.0 3.5 collective-permute-start.26
  501.5 8.7 %last.1 = (bf16[1184,1024]{1,0:T(8,128)(2,1)}, f32[2,1024]{1,0:T(2,128)}) custom-call(bf16[1184,1024]{1,0:T(8,128)(2,1)} %pad_maximum_fusion.x_ref, f32[1184,1024]{1,0:T(8,128)} %get-tuple-element.43.dh_ref, bf16[1184,1024]{1,0:T(8,128)(2,1)} %copy-done.4, bf16[1184,1024]{1,0:T(8,128)(2,1)} %collective-permute-done.20.b_ref, f32[1,1024]{1,0:T(1,128)} %bitcast.152), custom_call_target="tpu_custom_call" | custom-call | tf_op jit(solution)/shard_map/last/pallas_call | solution.py:251
  514.7 5.7 %reshape.129 = bf16[1184,2,2,256]{3,2,1,0:T(2,128)(2,1)S(1)} reshape(bf16[1184,1024]{1,0:T(8,128)(2,1)} %get-tuple-element.49) | data formatting | bytes 4849664 | tf_op jit(solution)/shard_map/reshape | solution.py:437
  522.3 2.5 constant_dynamic-slice_fusion.9
  525.4 4.8 collective-permute-done.35
  530.2 2.7 collective-permute-start.36
  540.2 10.3 %collective-permute-done.32 = bf16[256,1024]{0,1:T(8,128)(2,1)} collective-permute-done((bf16[256,1024]{0,1:T(8,128)(2,1)}, bf16[256,1024]{0,1:T(8,128)(2,1)}, u32[]{:S(2)}, u32[]{:S(2)}) %collective-permute-start.32) | collective-permute-done | bytes 524320 | tf_op jit(solution)/shard_map/ppermute | solution.py:290
  (366 shorter events, 127.3 us)
Async XLA Ops:
  7.3 106.7 %all-gather.2.cloned.1.call-start = ((), (), s32[]{:S(2)}) async-start(), calls=%async_computation.2 | async-start | bytes 2621440 | tf_op jit(solution)/shard_map/all_gather | solution.py:370
  9.8 56.3 %collective-permute-start.4 = (bf16[256,1024]{1,0:T(8,128)(2,1)}, bf16[256,1024]{1,0:T(8,128)(2,1)}, u32[]{:S(2)}, u32[]{:S(2)}) collective-permute-start(bf16[256,1024]{1,0:T(8,128)(2,1)} %get-tuple-element.125), channel_id=1, source_target_pairs={{0,4},{4,8},{8,12},{12,0},{1,5},{5,9},{9,13},{13,1},{2,6},{6,10},{... | collective-permute-start | bytes 1572872 | tf_op jit(solution)/shard_map/ppermute | solution.py:355
  12.8 55.0 %collective-permute-start.5 = (bf16[256,1024]{1,0:T(8,128)(2,1)}, bf16[256,1024]{1,0:T(8,128)(2,1)}, u32[]{:S(2)}, u32[]{:S(2)}) collective-permute-start(bf16[256,1024]{1,0:T(8,128)(2,1)} %get-tuple-element.125), channel_id=1, source_target_pairs={{0,8},{4,12},{8,0},{12,4},{1,9},{5,13},{9,1},{13,5},{2,10},{6,14},... | collective-permute-start | bytes 1572872 | tf_op jit(solution)/shard_map/ppermute | solution.py:355
  15.4 54.1 %collective-permute-start.6 = (bf16[256,1024]{1,0:T(8,128)(2,1)}, bf16[256,1024]{1,0:T(8,128)(2,1)}, u32[]{:S(2)}, u32[]{:S(2)}) collective-permute-start(bf16[256,1024]{1,0:T(8,128)(2,1)} %get-tuple-element.125), channel_id=1, source_target_pairs={{0,12},{4,0},{8,4},{12,8},{1,13},{5,1},{9,5},{13,9},{2,14},{6,2},{... | collective-permute-start | bytes 1572872 | tf_op jit(solution)/shard_map/ppermute | solution.py:355
  16.8 55.4 %collective-permute-start.7 = (bf16[256,1024]{1,0:T(8,128)(2,1)}, bf16[256,1024]{1,0:T(8,128)(2,1)}, u32[]{:S(2)}, u32[]{:S(2)}) collective-permute-start(bf16[256,1024]{1,0:T(8,128)(2,1)} %get-tuple-element.125), channel_id=1, source_target_pairs={{0,2},{2,0},{1,3},{3,1},{4,6},{6,4},{5,7},{7,5},{8,10},{10,8},{9,1... | collective-permute-start | bytes 1572872 | tf_op jit(solution)/shard_map/ppermute | solution.py:290
  29.3 15.1 %collective-permute-start.2 = (f32[3072]{0:T(1024)}, f32[3072]{0:T(1024)}, u32[]{:S(2)}, u32[]{:S(2)}) collective-permute-start(f32[3072]{0:T(1024)} %constant_dynamic-update-slice_fusion.22), channel_id=1, source_target_pairs={{0,2},{2,0},{1,3},{3,1},{4,6},{6,4},{5,7},{7,5},{8,10},{10,8},{9,1... | collective-permute-start | bytes 36872 | tf_op jit(solution)/shard_map/ppermute | solution.py:290
  32.9 503.1 %reduce-scatter.5.cloned.1.call-start = ((), (), s32[]{:S(2)}) async-start(), calls=%async_computation.4 | async-start | bytes 2621440 | tf_op jit(solution)/shard_map/reduce_scatter | solution.py:417
  45.1 2.0 collective-permute-start.3
  47.1 16.3 %collective-permute-start = (bf16[1184,256]{1,0:T(8,128)(2,1)}, bf16[1184,256]{1,0:T(8,128)(2,1)S(1)}, u32[]{:S(2)}, u32[]{:S(2)}) collective-permute-start(bf16[1184,256]{1,0:T(8,128)(2,1)} %get-tuple-element.116), channel_id=1, source_target_pairs={{0,2},{2,0},{1,3},{3,1},{4,6},{6,4},{5,7},{7,5},{8,10},{10,8},{9,1... | collective-permute-start | bytes 1818632 | tf_op jit(solution)/shard_map/ppermute | solution.py:290
  63.4 16.8 %collective-permute-start.12 = (bf16[1184,256]{1,0:T(8,128)(2,1)}, bf16[1184,256]{1,0:T(8,128)(2,1)S(1)}, u32[]{:S(2)}, u32[]{:S(2)}) collective-permute-start(bf16[1184,256]{1,0:T(8,128)(2,1)} %get-tuple-element.110), channel_id=1, source_target_pairs={{0,2},{2,0},{1,3},{3,1},{4,6},{6,4},{5,7},{7,5},{8,10},{10,8},{9,1... | collective-permute-start | bytes 1818632 | tf_op jit(solution)/shard_map/ppermute | solution.py:290
  66.1 47.4 %collective-permute-start.1 = (bf16[1184,512]{1,0:T(8,128)(2,1)S(1)}, bf16[1184,512]{1,0:T(8,128)(2,1)S(1)}, u32[]{:S(2)}, u32[]{:S(2)}) collective-permute-start(bf16[1184,512]{1,0:T(8,128)(2,1)S(1)} %pad_maximum_fusion.5), channel_id=1, source_target_pairs={{0,1},{1,0},{2,3},{3,2},{4,5},{5,4},{6,7},{7,6},{8,9},{9,8},{10,11... | collective-permute-start | bytes 3637256 | tf_op jit(solution)/shard_map/ppermute | solution.py:290
  67.9 23.6 %collective-permute-start.8 = (bf16[256,1024]{1,0:T(8,128)(2,1)}, bf16[256,1024]{1,0:T(8,128)(2,1)S(1)}, u32[]{:S(2)}, u32[]{:S(2)}) collective-permute-start(bf16[256,1024]{1,0:T(8,128)(2,1)} %collective-permute-done.4), channel_id=1, source_target_pairs={{0,2},{2,0},{1,3},{3,1},{4,6},{6,4},{5,7},{7,5},{8,10},{10,8},{9,1... | collective-permute-start | bytes 1572872 | tf_op jit(solution)/shard_map/ppermute | solution.py:290
  69.6 33.1 %collective-permute-start.9 = (bf16[256,1024]{1,0:T(8,128)(2,1)}, bf16[256,1024]{1,0:T(8,128)(2,1)S(1)}, u32[]{:S(2)}, u32[]{:S(2)}) collective-permute-start(bf16[256,1024]{1,0:T(8,128)(2,1)} %collective-permute-done.5), channel_id=1, source_target_pairs={{0,2},{2,0},{1,3},{3,1},{4,6},{6,4},{5,7},{7,5},{8,10},{10,8},{9,1... | collective-permute-start | bytes 1572872 | tf_op jit(solution)/shard_map/ppermute | solution.py:290
  72.2 40.5 %collective-permute-start.10 = (bf16[256,1024]{1,0:T(8,128)(2,1)}, bf16[256,1024]{1,0:T(8,128)(2,1)S(1)}, u32[]{:S(2)}, u32[]{:S(2)}) collective-permute-start(bf16[256,1024]{1,0:T(8,128)(2,1)} %collective-permute-done.6), channel_id=1, source_target_pairs={{0,2},{2,0},{1,3},{3,1},{4,6},{6,4},{5,7},{7,5},{8,10},{10,8},{9,1... | collective-permute-start | bytes 1572872 | tf_op jit(solution)/shard_map/ppermute | solution.py:290
  81.3 82.3 %collective-permute-start.13 = (bf16[1184,512]{1,0:T(8,128)(2,1)}, bf16[1184,512]{1,0:T(8,128)(2,1)}, u32[]{:S(2)}, u32[]{:S(2)}) collective-permute-start(bf16[1184,512]{1,0:T(8,128)(2,1)} %pad_maximum_fusion.6), channel_id=1, source_target_pairs={{0,1},{1,0},{2,3},{3,2},{4,5},{5,4},{6,7},{7,6},{8,9},{9,8},{10,11... | collective-permute-start | bytes 3637256 | tf_op jit(solution)/shard_map/ppermute | solution.py:290
  114.1 46.8 %collective-permute-start.14 = (bf16[1024,1024]{1,0:T(8,128)(2,1)}, bf16[1024,1024]{1,0:T(8,128)(2,1)}, u32[]{:S(2)}, u32[]{:S(2)}) collective-permute-start(bf16[1024,1024]{1,0:T(8,128)(2,1)} %all-gather.2.cloned.1.call-done.refs_0_.refs_4_), channel_id=1, source_target_pairs={{0,16},{16,0},{1,17},{17,1},{2,18},{18,2},{3,19},{19,3},{4,20},{20... | collective-permute-start | bytes 6291464 | tf_op jit(solution)/shard_map/ppermute | solution.py:290
  151.2 16.6 %collective-permute-start.11 = (bf16[1184,1024]{1,0:T(8,128)(2,1)S(1)}, bf16[1184,1024]{1,0:T(8,128)(2,1)}, u32[]{:S(2)}, u32[]{:S(2)}) collective-permute-start(bf16[1184,1024]{1,0:T(8,128)(2,1)S(1)} %add_convert_fusion.1.a_ref), channel_id=1, source_target_pairs={{0,1},{1,0},{2,3},{3,2},{4,5},{5,4},{6,7},{7,6},{8,9},{9,8},{10,11... | collective-permute-start | bytes 7274504 | tf_op jit(solution)/shard_map/ppermute | solution.py:290
  154.0 48.8 %collective-permute-start.15 = (bf16[1024,1024]{1,0:T(8,128)(2,1)}, bf16[1024,1024]{1,0:T(8,128)(2,1)}, u32[]{:S(2)}, u32[]{:S(2)}) collective-permute-start(bf16[1024,1024]{1,0:T(8,128)(2,1)} %all-gather.2.cloned.1.call-done.refs_0_.refs_4_), channel_id=1, source_target_pairs={{0,2},{2,0},{1,3},{3,1},{4,6},{6,4},{5,7},{7,5},{8,10},{10,8},{9,1... | collective-permute-start | bytes 6291464 | tf_op jit(solution)/shard_map/ppermute | solution.py:290
  160.9 86.3 %collective-permute-start.16 = (bf16[1024,1024]{1,0:T(8,128)(2,1)}, bf16[1024,1024]{1,0:T(8,128)(2,1)}, u32[]{:S(2)}, u32[]{:S(2)}) collective-permute-start(bf16[1024,1024]{1,0:T(8,128)(2,1)} %collective-permute-done.14.refs_1_.refs_5_), channel_id=1, source_target_pairs={{0,2},{2,0},{1,3},{3,1},{4,6},{6,4},{5,7},{7,5},{8,10},{10,8},{9,1... | collective-permute-start | bytes 6291464 | tf_op jit(solution)/shard_map/ppermute | solution.py:290
  295.2 16.6 %collective-permute-start.17 = (bf16[1184,2,256]{2,0,1:T(8,128)(2,1)}, bf16[1184,2,256]{2,0,1:T(8,128)(2,1)}, u32[]{:S(2)}, u32[]{:S(2)}) collective-permute-start(bf16[1184,2,256]{2,0,1:T(8,128)(2,1)} %bitcast.127), channel_id=1, source_target_pairs={{0,1},{1,0},{2,3},{3,2},{4,5},{5,4},{6,7},{7,6},{8,9},{9,8},{10,11... | collective-permute-start | bytes 3637256 | tf_op jit(solution)/shard_map/ppermute | solution.py:290
  300.2 48.8 %collective-permute-start.30 = (bf16[1024,1024]{0,1:T(8,128)(2,1)}, bf16[1024,1024]{0,1:T(8,128)(2,1)}, u32[]{:S(2)}, u32[]{:S(2)}) collective-permute-start(bf16[1024,1024]{0,1:T(8,128)(2,1)} %fusion.7), channel_id=1, source_target_pairs={{0,2},{2,0},{1,3},{3,1},{4,6},{6,4},{5,7},{7,5},{8,10},{10,8},{9,1... | collective-permute-start | bytes 6291464 | tf_op jit(solution)/shard_map/ppermute | solution.py:290
  306.8 56.9 %collective-permute-start.19 = (bf16[1184,1024]{1,0:T(8,128)(2,1)}, bf16[1184,1024]{1,0:T(8,128)(2,1)}, u32[]{:S(2)}, u32[]{:S(2)}) collective-permute-start(bf16[1184,1024]{1,0:T(8,128)(2,1)} %get-tuple-element.42.a_ref), channel_id=1, source_target_pairs={{0,1},{1,0},{2,3},{3,2},{4,5},{5,4},{6,7},{7,6},{8,9},{9,8},{10,11... | collective-permute-start | bytes 7274504 | tf_op jit(solution)/shard_map/ppermute | solution.py:290
  309.9 48.6 %collective-permute-start.28 = (bf16[1024,1024]{0,1:T(8,128)(2,1)S(1)}, bf16[1024,1024]{0,1:T(8,128)(2,1)S(1)}, u32[]{:S(2)}, u32[]{:S(2)}) collective-permute-start(bf16[1024,1024]{0,1:T(8,128)(2,1)S(1)} %pad_maximum_fusion.3), channel_id=1, source_target_pairs={{0,16},{16,0},{1,17},{17,1},{2,18},{18,2},{3,19},{19,3},{4,20},{20... | collective-permute-start | bytes 6291464 | tf_op jit(solution)/shard_map/ppermute | solution.py:290
  311.7 37.2 %copy-start.23 = (bf16[1184,256]{1,0:T(8,128)(2,1)S(1)}, bf16[1184,256]{1,0:T(8,128)(2,1)}, u32[]{:S(2)}) copy-start(bf16[1184,256]{1,0:T(8,128)(2,1)} %copy-done.21) | copy-start | bytes 1818628
  311.7 37.2 %copy-start.26 = (bf16[1184,256]{1,0:T(8,128)(2,1)S(1)}, bf16[1184,256]{1,0:T(8,128)(2,1)}, u32[]{:S(2)}) copy-start(bf16[1184,256]{1,0:T(8,128)(2,1)} %copy-done.24) | copy-start | bytes 1818628
  311.7 37.2 %copy-start.29 = (bf16[1184,256]{1,0:T(8,128)(2,1)S(1)}, bf16[1184,256]{1,0:T(8,128)(2,1)}, u32[]{:S(2)}) copy-start(bf16[1184,256]{1,0:T(8,128)(2,1)} %copy-done.27) | copy-start | bytes 1818628
  315.4 43.1 %slice-start.2 = ((s8[4849664]{0:T(1024)(128)(4,1)}), s8[4194304]{0:T(1024)(128)(4,1)S(1)}, s32[]{:S(2)}) async-start(s8[4849664]{0:T(1024)(128)(4,1)} %bitcast.200), calls=%async_computation.7 | async-start | bytes 8388608
  316.3 42.2 %copy-start.19 = (bf16[1184,1024]{1,0:T(8,128)(2,1)S(1)}, bf16[1184,1024]{1,0:T(8,128)(2,1)}, u32[]{:S(2)}) copy-start(bf16[1184,1024]{1,0:T(8,128)(2,1)} %get-tuple-element.40.n_ref) | copy-start | bytes 7274500
  316.3 42.2 %slice-start.3 = ((s8[4849664]{0:T(1024)(128)(4,1)}), s8[655360]{0:T(1024)(128)(4,1)S(1)}, s32[]{:S(2)}) async-start(s8[4849664]{0:T(1024)(128)(4,1)} %bitcast.200), calls=%async_computation.8 | async-start | bytes 1310720
  316.3 179.3 %collective-permute-start.18 = (bf16[1184,256]{1,0:T(8,128)(2,1)}, bf16[1184,256]{1,0:T(8,128)(2,1)}, u32[]{:S(2)}, u32[]{:S(2)}) collective-permute-start(bf16[1184,256]{1,0:T(8,128)(2,1)} %dynamic-slice_bitcast_fusion), channel_id=1, source_target_pairs={{0,2},{2,0},{1,3},{3,1},{4,6},{6,4},{5,7},{7,5},{8,10},{10,8},{9,1... | collective-permute-start | bytes 1818632 | tf_op jit(solution)/shard_map/ppermute | solution.py:290
  355.8 60.7 %collective-permute-start.31 = (bf16[1024,512]{0,1:T(8,128)(2,1)}, bf16[1024,512]{0,1:T(8,128)(2,1)}, u32[]{:S(2)}, u32[]{:S(2)}) collective-permute-start(bf16[1024,512]{0,1:T(8,128)(2,1)} %slice.496), channel_id=1, source_target_pairs={{0,16},{16,0},{1,17},{17,1},{2,18},{18,2},{3,19},{19,3},{4,20},{20... | collective-permute-start | bytes 3145736 | tf_op jit(solution)/shard_map/ppermute | solution.py:290
  361.1 58.2 %collective-permute-start.29 = (bf16[1024,512]{0,1:T(8,128)(2,1)}, bf16[1024,512]{0,1:T(8,128)(2,1)}, u32[]{:S(2)}, u32[]{:S(2)}) collective-permute-start(bf16[1024,512]{0,1:T(8,128)(2,1)} %add_convert_fusion.6), channel_id=1, source_target_pairs={{0,2},{2,0},{1,3},{3,1},{4,6},{6,4},{5,7},{7,5},{8,10},{10,8},{9,1... | collective-permute-start | bytes 3145736 | tf_op jit(solution)/shard_map/ppermute | solution.py:290
  422.4 117.0 %reduce-scatter.3.cloned.1.call-start = ((), (), s32[]{:S(2)}) async-start(), calls=%async_computation.3 | async-start | bytes 2621440 | tf_op jit(solution)/shard_map/reduce_scatter | solution.py:468
  425.9 75.6 %collective-permute-start.20 = (bf16[1184,1024]{1,0:T(8,128)(2,1)S(1)}, bf16[1184,1024]{1,0:T(8,128)(2,1)}, u32[]{:S(2)}, u32[]{:S(2)}) collective-permute-start(bf16[1184,1024]{1,0:T(8,128)(2,1)S(1)} %add_convert_fusion.a_ref), channel_id=1, source_target_pairs={{0,1},{1,0},{2,3},{3,2},{4,5},{5,4},{6,7},{7,6},{8,9},{9,8},{10,11... | collective-permute-start | bytes 7274504 | tf_op jit(solution)/shard_map/ppermute | solution.py:290
  430.3 47.5 %collective-permute-start.22 = (bf16[1024,1024]{0,1:T(8,128)(2,1)}, bf16[1024,1024]{0,1:T(8,128)(2,1)}, u32[]{:S(2)}, u32[]{:S(2)}) collective-permute-start(bf16[1024,1024]{0,1:T(8,128)(2,1)} %pad_maximum_fusion.2), channel_id=1, source_target_pairs={{0,2},{2,0},{1,3},{3,1},{4,6},{6,4},{5,7},{7,5},{8,10},{10,8},{9,1... | collective-permute-start | bytes 6291464 | tf_op jit(solution)/shard_map/ppermute | solution.py:290
  439.4 42.4 %copy-start.44 = (f32[1,1024]{1,0:T(1,128)S(1)}, f32[1,1024]{1,0:T(1,128)}, u32[]{:S(2)}) copy-start(f32[1,1024]{1,0:T(1,128)} %get-tuple-element.91) | copy-start | bytes 12292
  439.4 42.4 %copy-start.45 = (f32[1,1024]{1,0:T(1,128)S(1)}, f32[1,1024]{1,0:T(1,128)}, u32[]{:S(2)}) copy-start(f32[1,1024]{1,0:T(1,128)} %broadcast_select_fusion.21) | copy-start | bytes 12292
  481.9 3.8 collective-permute-start.24
  485.8 12.2 %collective-permute-start.25 = (f32[2,2560]{1,0:T(2,128)S(1)}, f32[2,2560]{1,0:T(2,128)S(1)}, u32[]{:S(2)}, u32[]{:S(2)}) collective-permute-start(f32[2,2560]{1,0:T(2,128)S(1)} %add.205), channel_id=1, source_target_pairs={{0,4},{4,0},{8,12},{12,8},{1,5},{5,1},{9,13},{13,9},{2,6},{6,2},{1... | collective-permute-start | bytes 61448 | tf_op jit(solution)/shard_map/ppermute | solution.py:290
  498.0 16.4 %collective-permute-start.26 = (f32[2,2560]{1,0:T(2,128)S(1)}, f32[2,2560]{1,0:T(2,128)S(1)}, u32[]{:S(2)}, u32[]{:S(2)}) collective-permute-start(f32[2,2560]{1,0:T(2,128)S(1)} %add.206), channel_id=1, source_target_pairs={{0,8},{4,12},{8,0},{12,4},{1,9},{5,13},{9,1},{13,5},{2,10},{6,14},... | collective-permute-start | bytes 61448 | tf_op jit(solution)/shard_map/ppermute | solution.py:290
  510.9 9.5 %collective-permute-start.33 = (f32[2,512]{1,0:T(2,128)S(1)}, f32[2,512]{1,0:T(2,128)S(1)}, u32[]{:S(2)}, u32[]{:S(2)}) collective-permute-start(f32[2,512]{1,0:T(2,128)S(1)} %pad_maximum_fusion.21), channel_id=1, source_target_pairs={{0,2},{2,0},{1,3},{3,1},{4,6},{6,4},{5,7},{7,5},{8,10},{10,8},{9,1... | collective-permute-start | bytes 12296 | tf_op jit(solution)/shard_map/ppermute | solution.py:290
  514.4 11.0 %collective-permute-start.27 = (f32[2,2560]{1,0:T(2,128)S(1)}, f32[2,2560]{1,0:T(2,128)S(1)}, u32[]{:S(2)}, u32[]{:S(2)}) collective-permute-start(f32[2,2560]{1,0:T(2,128)S(1)} %add.207), channel_id=1, source_target_pairs={{0,16},{16,0},{1,17},{17,1},{2,18},{18,2},{3,19},{19,3},{4,20},{20... | collective-permute-start | bytes 61448 | tf_op jit(solution)/shard_map/ppermute | solution.py:290
  520.5 4.7 collective-permute-start.34
  525.0 10.9 %collective-permute-start.21 = (bf16[1184,256]{1,0:T(8,128)(2,1)S(1)}, bf16[1184,256]{1,0:T(8,128)(2,1)S(1)}, u32[]{:S(2)}, u32[]{:S(2)}) collective-permute-start(bf16[1184,256]{1,0:T(8,128)(2,1)S(1)} %bitcast.141), channel_id=1, source_target_pairs={{0,2},{2,0},{1,3},{3,1},{4,6},{6,4},{5,7},{7,5},{8,10},{10,8},{9,1... | collective-permute-start | bytes 1818632 | tf_op jit(solution)/shard_map/ppermute | solution.py:290
  525.2 5.0 collective-permute-start.35
  530.2 4.3 collective-permute-start.36
  536.0 14.4 %collective-permute-start.32 = (bf16[256,1024]{0,1:T(8,128)(2,1)}, bf16[256,1024]{0,1:T(8,128)(2,1)}, u32[]{:S(2)}, u32[]{:S(2)}) collective-permute-start(bf16[256,1024]{0,1:T(8,128)(2,1)} %reduce-scatter.5.cloned.1.call-done), channel_id=1, source_target_pairs={{0,16},{16,0},{1,17},{17,1},{2,18},{18,2},{3,19},{19,3},{4,20},{20... | collective-permute-start | bytes 1572872 | tf_op jit(solution)/shard_map/ppermute | solution.py:290
  539.4 16.6 %collective-permute-start.23 = (bf16[256,1024]{0,1:T(8,128)(2,1)}, bf16[256,1024]{0,1:T(8,128)(2,1)}, u32[]{:S(2)}, u32[]{:S(2)}) collective-permute-start(bf16[256,1024]{0,1:T(8,128)(2,1)} %reduce-scatter.3.cloned.1.call-done), channel_id=1, source_target_pairs={{0,16},{16,0},{1,17},{17,1},{2,18},{18,2},{3,19},{19,3},{4,20},{20... | collective-permute-start | bytes 1572872 | tf_op jit(solution)/shard_map/ppermute | solution.py:290
  (74 other events, 567.3 us)
Sparse Core Ops, SparseCore 0:
  33.1 60.9 all-gather.1
  422.6 53.3 reduce-scatter.4
  482.0 53.5 reduce-scatter.2

commit v3 on v2

v3 whole, which is shorter than its diff:
```python
import functools
import math

import jax
import jax.numpy as jnp
from jax import lax
from jax.experimental import pallas as pl
from jax.experimental.pallas import tpu as pltpu
from jax.sharding import Mesh, PartitionSpec as P

D = 1024
HD = 64
SEQ = 577
PAD = 592
TM = 296
EPS = 1e-06
F32 = jnp.float32
BF16 = jnp.bfloat16
VMEM_LIMIT = 60 * 1024 * 1024
ROOT_HALF = math.sqrt(0.5)
DENSITY = 1.0 / math.sqrt(2.0 * math.pi)


def mm(a, b):
    return lax.dot_general(a, b, (((1,), (0,)), ((), ())), preferred_element_type=F32)


def mm_nt(a, b):
    return lax.dot_general(a, b, (((1,), (1,)), ((), ())), preferred_element_type=F32)


def mm_tn(a, b):
    return lax.dot_general(a, b, (((0,), (0,)), ((), ())), preferred_element_type=F32)


def row_mean(v):
    return jnp.sum(v, axis=1, keepdims=True) * (1.0 / D)


def col_sum(v):
    return jnp.sum(v, axis=0, keepdims=True)


def stats(rows):
    middle = row_mean(rows)
    spread = row_mean(rows * rows) - middle * middle
    return middle, lax.rsqrt(spread + EPS)


def params(n):
    return pltpu.CompilerParams(
        dimension_semantics=("arbitrary",) * n, vmem_limit_bytes=VMEM_LIMIT
    )


def cost(flops, moved, exps=0):
    return pl.CostEstimate(flops=int(flops), bytes_accessed=int(moved), transcendentals=int(exps))


def like(shape, dtype):
    return jax.ShapeDtypeStruct(shape, dtype)


def row_spec(cols):
    return pl.BlockSpec((TM, cols), lambda i, *_: (i, 0))


def fixed(shape):
    return pl.BlockSpec(shape, lambda *_: (0,) * len(shape))


def held_once(shape):
    return pl.BlockSpec(shape, lambda *_: (0,) * len(shape), pipeline_mode=pl.Buffered(1))


def add_up(ref, first, part):
    @pl.when(first)
    def _():
        ref[...] = part

    @pl.when(jnp.logical_not(first))
    def _():
        ref[...] += part


def norm_qkv_kernel(x_ref, gain_ref, shift_ref, bias_ref, a_ref, b_ref, c_ref, d_ref, n_ref, o_ref, w_ref):
    wide = a_ref.shape[1]
    three = wide // 4 * 3

    @pl.when(pl.program_id(0) == 0)
    def _():
        for place, ref in enumerate((a_ref, b_ref, c_ref, d_ref)):
            w_ref[:, three * place : three * (place + 1)] = ref[:, :three]
            low = 4 * three + (wide - three) * place
            w_ref[:, low : low + wide - three] = ref[:, three:]

    x = x_ref[...].astype(F32)
    middle, scaled = stats(x)
    n = (((x - middle) * scaled) * gain_ref[...] + shift_ref[...]).astype(BF16)
    n_ref[...] = n
    o_ref[...] = (mm(n, w_ref[:, : 4 * three]) + bias_ref[...]).astype(BF16)


def norm_qkv(x, gain, shift, bias, blocks):
    rows = x.shape[0]
    wide = blocks[0].shape[1]
    out = 3 * wide
    return pl.pallas_call(
        norm_qkv_kernel,
        grid=(rows // TM,),
        name="norm_qkv",
        in_specs=[row_spec(D), fixed((1, D)), fixed((1, D)), fixed((1, out))]
        + [held_once((D, wide))] * 4,
        out_specs=[row_spec(D), row_spec(out), held_once((D, 4 * wide))],
        out_shape=[like((rows, D), BF16), like((rows, out), BF16), like((D, 4 * wide), BF16)],
        compiler_params=params(1),
        cost_estimate=cost(2 * rows * D * out, 16 * rows * D),
    )(x, gain, shift, bias, *blocks)


def attend_kernel(qkv_ref, o_ref, p_ref):
    live = lax.broadcasted_iota(jnp.int32, (1, PAD), 1) < SEQ
    step = 2 * HD
    for h in range(2):
        q, k, v = (qkv_ref[:, step * w + HD * h : step * w + HD * (h + 1)] for w in range(3))
        s = mm_nt(q * jnp.asarray(0.125, BF16), k)
        s = jnp.where(live, s, -1e30)
        e = jnp.exp(s - jnp.max(s, axis=1, keepdims=True))
        p = (e * (1.0 / jnp.sum(e, axis=1, keepdims=True))).astype(BF16)
        p_ref[h] = p
        o_ref[:, HD * h : HD * (h + 1)] = mm(p, v).astype(BF16)


def attend(qkv):
    rows, cols = qkv.shape
    pairs = cols // (6 * HD)
    held = rows // PAD
    return pl.pallas_call(
        attend_kernel,
        grid=(pairs, held),
        name="attend",
        in_specs=[pl.BlockSpec((PAD, 6 * HD), lambda p, i: (i, p))],
        out_specs=[
            pl.BlockSpec((PAD, 2 * HD), lambda p, i: (i, p)),
            pl.BlockSpec((None, 2, PAD, PAD), lambda p, i: (i, p, 0, 0)),
        ],
        out_shape=[like((rows, cols // 3), BF16), like((held, 2 * pairs, PAD, PAD), BF16)],
        compiler_params=params(2),
        cost_estimate=cost(16 * rows * PAD * cols, 40 * rows * D, 4 * rows * PAD * pairs),
    )(qkv)


def attend_back_kernel(qkv_ref, p_ref, g_ref, d_ref, sum_ref):
    step = 2 * HD
    for h in range(2):
        q, k, v = (qkv_ref[:, step * w + HD * h : step * w + HD * (h + 1)] for w in range(3))
        g = g_ref[:, HD * h : HD * (h + 1)]
        pb = p_ref[h]
        p = pb.astype(F32)
        dp = mm_nt(g, v)
        z = jnp.sum(p * dp, axis=1, keepdims=True)
        ds = (p * (dp - z)).astype(BF16)
        parts = (mm(ds, k) * 0.125, mm_tn(ds, q) * 0.125, mm_tn(pb, g))
        for w, part in enumerate(parts):
            d_ref[:, step * w + HD * h : step * w + HD * (h + 1)] = part.astype(BF16)
    add_up(sum_ref, pl.program_id(1) == 0, col_sum(d_ref[...].astype(F32)))


def attend_back(qkv, probs, grads):
    rows, cols = qkv.shape
    pairs = cols // (6 * HD)
    held = rows // PAD
    three = pl.BlockSpec((PAD, 6 * HD), lambda p, i: (i, p))
    return pl.pallas_call(
        attend_back_kernel,
        grid=(pairs, held),
        name="attend_back",
        in_specs=[
            three,
            pl.BlockSpec((None, 2, PAD, PAD), lambda p, i: (i, p, 0, 0)),
            pl.BlockSpec((PAD, 2 * HD), lambda p, i: (i, p)),
        ],
        out_specs=[three, pl.BlockSpec((1, 6 * HD), lambda p, i: (0, p))],
        out_shape=[like((rows, cols), BF16), like((1, cols), F32)],
        compiler_params=params(2),
        cost_estimate=cost(20 * rows * PAD * cols, 50 * rows * D),
    )(qkv, probs, grads)


def middle_kernel(x_ref, a_ref, b_ref, bias_ref, gain_ref, shift_ref, h_ref, n_ref):
    h = x_ref[...].astype(F32) + (a_ref[...].astype(F32) + b_ref[...].astype(F32)) + bias_ref[...]
    h_ref[...] = h
    middle, scaled = stats(h)
    n_ref[...] = (((h - middle) * scaled) * gain_ref[...] + shift_ref[...]).astype(BF16)


def middle(x, a, b, bias, gain, shift):
    rows = x.shape[0]
    vec = fixed((1, D))
    return pl.pallas_call(
        middle_kernel,
        grid=(rows // TM,),
        name="middle",
        in_specs=[row_spec(D)] * 3 + [vec] * 3,
        out_specs=[row_spec(D)] * 2,
        out_shape=[like((rows, D), F32), like((rows, D), BF16)],
        compiler_params=params(1),
        cost_estimate=cost(20 * rows * D, 12 * rows * D),
    )(x, a, b, bias, gain, shift)


def mlp_kernel(tiles, place_ref, n_ref, dy_ref, *refs):
    ups, downs, biases = refs[0:4], refs[4:8], refs[8:12]
    g_ref, du_ref, mine_ref, theirs_ref, lift_ref, bsum_ref, low_acc, lift_acc = refs[12:]
    j = pl.program_id(0)

    @pl.when(j == 0)
    def _():
        low_acc[...] = jnp.zeros_like(low_acc)
        lift_acc[...] = jnp.zeros_like(lift_acc)

    def step(up_ref, down_ref, bias_ref):
        u = mm(n_ref[...], up_ref[...]) + bias_ref[...]
        cdf = 0.5 * (1.0 + lax.erf(u * ROOT_HALF))
        g = (u * cdf).astype(BF16)
        slope = cdf + u * (jnp.exp(-0.5 * u * u) * DENSITY)
        g_ref[...] = g
        du = (mm(dy_ref[...], down_ref[...]) * slope).astype(BF16)
        du_ref[...] = du
        bsum_ref[...] = col_sum(du.astype(F32))
        low_acc[...] += mm_nt(g, down_ref[...])
        lift_acc[...] += mm_nt(du, up_ref[...])

    for block in range(4):

        @pl.when((j >= block * tiles) & (j < (block + 1) * tiles))
        def _(block=block):
            step(ups[block], downs[block], biases[block])

    @pl.when(j == 4 * tiles - 1)
    def _():
        lift_ref[...] = lift_acc[...].astype(BF16)
        width = D // 4
        core = place_ref[0]
        for far in range(2):
            low = pl.multiple_of((2 * far + core) * width, width)
            other = pl.multiple_of((2 * far + 1 - core) * width, width)
            mine_ref[:, far * width : (far + 1) * width] = low_acc[:, pl.ds(low, width)]
            theirs_ref[:, far * width : (far + 1) * width] = low_acc[:, pl.ds(other, width)].astype(
                BF16
            )


def mlp(place, n2, dy, ups, downs, biases, half, tn=256):
    rows = n2.shape[0]
    tiles = half // tn
    hid = 4 * half
    whole = held_once((rows, D))

    def part(height, block, start):
        return pl.BlockSpec(
            (height, tn), lambda j, *_: (0, jnp.clip(j - block * tiles, 0, tiles - 1) + start // tn)
        )

    tile = pl.BlockSpec((rows, tn), lambda j, *_: (0, j))
    return pl.pallas_call(
        functools.partial(mlp_kernel, tiles),
        name="mlp",
        grid_spec=pltpu.PrefetchScalarGridSpec(
            num_scalar_prefetch=1,
            grid=(4 * tiles,),
            in_specs=[whole, whole]
            + [part(D, block, item[1]) for block, item in enumerate(ups)]
            + [part(D, block, item[1]) for block, item in enumerate(downs)]
            + [part(1, block, 0) for block in range(4)],
            out_specs=[
                tile,
                tile,
                held_once((rows, D // 2)),
                held_once((rows, D // 2)),
                whole,
                pl.BlockSpec((1, tn), lambda j, *_: (0, j)),
            ],
            scratch_shapes=[pltpu.VMEM((rows, D), F32), pltpu.VMEM((rows, D), F32)],
        ),
        out_shape=[
            like((rows, hid), BF16),
            like((rows, hid), BF16),
            like((rows, D // 2), F32),
            like((rows, D // 2), BF16),
            like((rows, D), BF16),
            like((1, hid), F32),
        ],
        compiler_params=params(1),
        cost_estimate=cost(8 * rows * D * hid, 24 * rows * D, 2 * rows * hid),
    )(place, n2, dy, *[item[0] for item in ups], *[item[0] for item in downs], *biases)


def finish_kernel(place_ref, h_ref, a_ref, b_ref, bias_ref, mine_ref, theirs_ref):
    value = h_ref[...] + (a_ref[...] + b_ref[...].astype(F32)) + bias_ref[...]
    value = value.astype(BF16)

    @pl.when(pl.program_id(0) == 0)
    def _():
        theirs_ref[...] = value

    @pl.when(pl.program_id(0) == 1)
    def _():
        mine_ref[...] = value


def finish(place, h, a, b, bias):
    rows = h.shape[0]
    width = D // 4
    n = rows // TM

    def block(k, s):
        return jnp.where(k == 0, 1 - s[1], s[1])

    return pl.pallas_call(
        finish_kernel,
        name="finish",
        grid_spec=pltpu.PrefetchScalarGridSpec(
            num_scalar_prefetch=1,
            grid=(2, n),
            in_specs=[
                pl.BlockSpec((TM, width), lambda k, i, s: (i, 2 * block(k, s) + s[0])),
                pl.BlockSpec((TM, width), lambda k, i, s: (i, block(k, s))),
                pl.BlockSpec((TM, width), lambda k, i, s: (i, block(k, s))),
                pl.BlockSpec((1, width), lambda k, i, s: (0, 2 * block(k, s) + s[0])),
            ],
            out_specs=[
                pl.BlockSpec((TM, width), lambda k, i, s: (jnp.where(k == 0, 0, i), 0)),
                pl.BlockSpec((TM, width), lambda k, i, s: (jnp.where(k == 0, i, n - 1), 0)),
            ],
        ),
        out_shape=[like((rows, width), BF16), like((rows, width), BF16)],
        compiler_params=params(2),
        cost_estimate=cost(2 * rows * D, 6 * rows * D),
    )(place, h, a, b, bias)


def turn_kernel(h_ref, dy_ref, a_ref, b_ref, gain_ref, w_ref, dh_ref, da_ref, do_ref, sums_ref):
    h = h_ref[...]
    middle, scaled = stats(h)
    c = (h - middle) * scaled
    dn = a_ref[...].astype(F32) + b_ref[...].astype(F32)
    dy = dy_ref[...].astype(F32)
    e = dn * gain_ref[...]
    dh = dy + scaled * (e - row_mean(e) - c * row_mean(e * c))
    dh_ref[...] = dh
    da = dh.astype(BF16)
    da_ref[...] = da
    do_ref[...] = mm(da, w_ref[...]).astype(BF16)
    part = jnp.concatenate(
        [col_sum(dn * c), col_sum(dn), col_sum(da.astype(F32)), col_sum(dy)], axis=0
    )
    add_up(sums_ref, pl.program_id(0) == 0, part)


def turn(h, dy, a, b, gain, weights):
    rows = h.shape[0]
    wide = weights.shape[1] // 4
    return pl.pallas_call(
        turn_kernel,
        grid=(rows // TM,),
        name="turn",
        in_specs=[row_spec(D)] * 4
        + [fixed((1, D)), pl.BlockSpec((D, wide), lambda i: (0, 3), pipeline_mode=pl.Buffered(1))],
        out_specs=[row_spec(D), row_spec(D), row_spec(wide), fixed((4, D))],
        out_shape=[
            like((rows, D), F32),
            like((rows, D), BF16),
            like((rows, wide), BF16),
            like((4, D), F32),
        ],
        compiler_params=params(1),
        cost_estimate=cost(2 * rows * D * wide, 18 * rows * D),
    )(h, dy, a, b, gain, weights)


def last_kernel(place_ref, x_ref, dh_ref, a_ref, b_ref, gain_ref, mine_ref, theirs_ref, sums_ref, held):
    x = x_ref[...].astype(F32)
    middle, scaled = stats(x)
    c = (x - middle) * scaled
    dn = a_ref[...].astype(F32) + b_ref[...].astype(F32)
    e = dn * gain_ref[...]
    held[...] = dh_ref[...] + scaled * (e - row_mean(e) - c * row_mean(e * c))
    width = D // 4
    core, side = place_ref[0], place_ref[1]
    mine_ref[...] = held[:, pl.ds(pl.multiple_of((2 * side + core) * width, width), width)]
    theirs_ref[...] = held[
        :, pl.ds(pl.multiple_of((2 * (1 - side) + core) * width, width), width)
    ].astype(BF16)
    add_up(
        sums_ref,
        pl.program_id(0) == 0,
        jnp.concatenate([col_sum(dn * c), col_sum(dn)], axis=0),
    )


def last(place, x, dh, a, b, gain):
    rows = x.shape[0]
    width = D // 4
    return pl.pallas_call(
        last_kernel,
        name="last",
        grid_spec=pltpu.PrefetchScalarGridSpec(
            num_scalar_prefetch=1,
            grid=(rows // TM,),
            in_specs=[row_spec(D)] * 4 + [fixed((1, D))],
            out_specs=[row_spec(width), row_spec(width), fixed((2, D))],
            scratch_shapes=[pltpu.VMEM((TM, D), F32)],
        ),
        out_shape=[like((rows, width), F32), like((rows, width), BF16), like((2, D), F32)],
        compiler_params=params(1),
        cost_estimate=cost(20 * rows * D, 12 * rows * D),
    )(place, x, dh, a, b, gain)


def local(
    sizes,
    inputs,
    query_weight,
    key_weight,
    value_weight,
    query_bias,
    value_bias,
    out_weight,
    out_bias,
    up_weight,
    up_bias,
    down_weight,
    down_bias,
    first_gain,
    first_shift,
    second_gain,
    second_shift,
    cotangent,
):
    n_dp, n_row, n_xa, n_core = sizes
    my_x = lax.axis_index("xa")
    my_core = lax.axis_index("core")
    my_row = lax.axis_index("row")
    my_half = lax.axis_index("dp") % 2
    place = jnp.stack([my_core, my_x]).astype(jnp.int32)
    tokens_here, width = inputs.shape
    images = tokens_here // SEQ
    held = images // n_xa
    rows = held * PAD
    hidden = up_weight.shape[1]
    half = hidden // 2
    heads_half = width // 2
    three = 3 * heads_half

    def swap(value, axis, size, bit=1):
        return lax.ppermute(value, axis, [(at, at ^ bit) for at in range(size)])

    def across(value):
        return swap(value, "xa", n_xa)

    def beside(value):
        return swap(value, "core", n_core)

    def over(value):
        return swap(value, "dp", n_dp)

    def pick(value, at, axis):
        return lax.dynamic_index_in_dim(value, at, axis, keepdims=False)

    def in_order(mine, other, at):
        return jnp.where(at == 0, mine, other), jnp.where(at == 0, other, mine)

    def after(value, *others):
        return lax.optimization_barrier((value, *others))[0]

    def halves(value, axis):
        cut = value.shape[axis] // 2
        both = value.reshape(value.shape[:axis] + (2, cut) + value.shape[axis + 1 :])
        return pick(both, my_half, axis), pick(both, my_half ^ 1, axis)

    attn_shard = jnp.concatenate(
        [halves(item, 1)[0] for item in (query_weight, key_weight, value_weight)]
        + [halves(out_weight, 0)[0].T],
        axis=1,
    )
    pieces = [attn_shard] + [
        lax.ppermute(attn_shard, "row", [(at, (at + shift) % n_row) for at in range(n_row)])
        for shift in range(1, n_row)
    ]

    count = held * SEQ

    def send_tokens(value):
        theirs = lax.dynamic_slice_in_dim(value, (my_x ^ 1) * count, count, 0)
        return across(theirs)

    def wide_tokens(value, got):
        mine = lax.dynamic_slice_in_dim(value, my_x * count, count, 0)
        pair = jnp.concatenate([mine, got], axis=1)
        other = beside(pair)
        left, right = in_order(pair, other, my_core)
        first_left, second_left = in_order(left[:, :width], left[:, width:], my_x)
        first_right, second_right = in_order(right[:, :width], right[:, width:], my_x)
        whole = jnp.concatenate([first_left, first_right, second_left, second_right], axis=1)
        whole = jnp.pad(whole.reshape(held, SEQ, D), ((0, 0), (0, PAD - SEQ), (0, 0)))
        return whole.reshape(rows, D)

    wide_input = wide_tokens(inputs, send_tokens(inputs))

    small = jnp.concatenate(
        [
            out_bias,
            down_bias,
            first_gain,
            first_shift,
            second_gain,
            second_shift,
            query_bias,
            value_bias,
            up_bias,
        ]
    )
    small_far = across(small)
    small_pair = jnp.stack(in_order(small, small_far, my_x))
    small_left, small_right = in_order(small_pair, beside(small_pair), my_core)

    def whole_vector(at):
        cut = slice(width * at, width * (at + 1))
        return jnp.concatenate(
            [small_left[0, cut], small_right[0, cut], small_left[1, cut], small_right[1, cut]]
        )[None]

    out_bias_all, down_bias_all, gain_one, shift_one, gain_two, shift_two = (
        whole_vector(at) for at in range(6)
    )

    attn_own = jnp.zeros((D, 4 * heads_half), BF16)
    for shift, piece in enumerate(pieces):
        start = (my_row - shift) % n_row * (D // n_row)
        attn_own = lax.dynamic_update_slice(attn_own, piece, (start, 0))
    attn_oth, attn_far = over(attn_own), across(attn_own)
    cut = 2 * heads_half
    attn_far_oth = jnp.concatenate([over(attn_far[:, :cut]), across(attn_oth[:, cut:])], axis=1)

    down_own = halves(down_weight, 0)[0].T
    mlp_shard = jnp.concatenate([halves(up_weight, 1)[0], down_own], axis=1)
    mlp_shard = after(mlp_shard, attn_own)
    mlp_own = lax.all_gather(mlp_shard, "row", axis=0, tiled=True)
    mlp_oth, mlp_far = over(mlp_own), across(mlp_own)
    up_far_oth, down_far_oth = over(mlp_far[:, :half]), across(mlp_oth[:, half:])
    grad_here = after(cotangent, attn_far_oth)
    wide_grad = wide_tokens(grad_here, send_tokens(grad_here))

    def four(near_vector, far_vector):
        near_own, near_oth = halves(near_vector, 0)
        far_own, far_oth = halves(far_vector, 0)
        return near_own, far_own, near_oth, far_oth

    zeros = jnp.zeros((heads_half,), F32)
    query_parts = four(query_bias, small_far[6 * width : 7 * width])
    value_parts = four(value_bias, small_far[7 * width : 8 * width])
    qkv_bias = jnp.concatenate(
        [item for q, v in zip(query_parts, value_parts) for item in (q, zeros, v)]
    )[None]
    up_biases = [item[None] for item in four(up_bias, small_far[8 * width :])]

    wide_one, qkv, attn_weights = norm_qkv(
        wide_input, gain_one, shift_one, qkv_bias, (attn_own, attn_far, attn_oth, attn_far_oth)
    )
    attended, probs = attend(qkv)
    mixed = mm_nt(attended, attn_weights[:, 4 * three :]).astype(BF16)
    middle_sum, wide_two = middle(
        wide_input, mixed, beside(mixed), out_bias_all, gain_two, shift_two
    )
    gate, pre, low_mine, low_theirs, lifted_two, up_sums = mlp(
        place,
        wide_two,
        wide_grad,
        ((mlp_own, 0), (mlp_far, 0), (mlp_oth, 0), (up_far_oth, 0)),
        ((mlp_own, half), (mlp_far, half), (mlp_oth, half), (down_far_oth, 0)),
        up_biases,
        half,
    )

    def wide_add(mine, got):
        return (mine.astype(F32) + got.astype(F32)).astype(BF16)

    def same_half(value):
        if n_dp == 2:
            return value
        groups = [[at + bit for at in range(0, n_dp, 2)] for bit in range(2)]
        return lax.psum(value.astype(F32), "dp", axis_index_groups=groups).astype(BF16)

    def scatter(value):
        return lax.psum_scatter(value, "row", scatter_dimension=0, tiled=True)

    lifted_other = beside(lifted_two)
    down_all = mm_tn(wide_grad, gate).astype(BF16)
    down_piece = scatter(down_all)
    up_oth_got = over(mm_tn(wide_two, pre[:, 2 * half :]).astype(BF16))

    middle_grad, attn_grad, head_grad, turn_sums = turn(
        middle_sum, wide_grad, lifted_two, lifted_other, gain_two, attn_weights
    )
    dqkv, qkv_sums = attend_back(qkv, probs, head_grad)

    def feature_split(value):
        return value.reshape(value.shape[0], n_xa, 2, width)

    def to_feature_blocks(mine, got, dtype):
        first, second = in_order(mine.astype(dtype), got.astype(dtype), my_x)
        both = jnp.concatenate([first, second]).reshape(images, PAD, width)
        return both[:, :SEQ].reshape(tokens_here, width)

    out_mine, out_theirs = finish(place, middle_sum, low_mine, beside(low_theirs), down_bias_all)
    outputs = to_feature_blocks(out_mine, across(out_theirs), BF16)

    far_oth_got = over(mm_tn(wide_one, dqkv[:, 3 * three :]).astype(BF16))
    near_oth_got = over(mm_tn(wide_one, dqkv[:, 2 * three : 3 * three]).astype(BF16))
    lifted_one = mm_nt(dqkv, attn_weights[:, : 4 * three]).astype(BF16)
    lifted_one_other = beside(lifted_one)
    far_own = wide_add(mm_tn(wide_one, dqkv[:, three : 2 * three]), far_oth_got)
    far_own_got = across(far_own)
    near_own = wide_add(mm_tn(wide_one, dqkv[:, :three]), near_oth_got)
    qkv_piece = same_half(scatter(wide_add(near_own, far_own_got)))
    qkv_other = over(qkv_piece)

    input_mine, input_theirs, last_sums = last(
        place, wide_input, middle_grad, lifted_one, lifted_one_other, gain_one
    )
    input_grad = to_feature_blocks(input_mine, across(input_theirs), F32)

    out_all = mm_tn(attn_grad, attended).astype(BF16)
    out_got = over(out_all[:, 2 * heads_half :])
    out_own = wide_add(out_all[:, : 2 * heads_half], out_got)
    up_own = wide_add(mm_tn(wide_two, pre[:, : 2 * half]), up_oth_got)
    far_part = jnp.concatenate([up_own[:, half:], out_own[:, heads_half:]], axis=1)
    near_part = jnp.concatenate([up_own[:, :half], out_own[:, :heads_half]], axis=1)
    up_piece = same_half(scatter(wide_add(near_part, across(far_part))))
    up_other = over(up_piece)

    down_x = wide_add(
        jnp.concatenate([down_piece[:, :half], down_piece[:, 2 * half : 3 * half]], axis=1),
        across(
            jnp.concatenate([down_piece[:, half : 2 * half], down_piece[:, 3 * half :]], axis=1)
        ),
    )
    down_got = over(down_x)
    down_total = down_x.astype(F32) + jnp.concatenate(
        [down_got[:, half:], down_got[:, :half]], axis=1
    ).astype(F32)
    if n_dp > 2:
        groups = [[at + bit for at in range(0, n_dp, 2)] for bit in range(2)]
        down_total = lax.psum(down_total, "dp", axis_index_groups=groups)
    down_first, down_second = in_order(down_total[:, :half], down_total[:, half:], my_half)
    down_grad = jnp.concatenate([down_first, down_second], axis=1).T

    def both_halves(mine, other, low, high):
        first, second = in_order(mine[:, low:high], other[:, low:high], my_half)
        return jnp.concatenate([first, second], axis=1).astype(F32)

    up_grad = both_halves(up_piece, up_other, 0, half)
    out_grad = both_halves(up_piece, up_other, half, half + heads_half).T
    query_grad, key_grad, value_grad = (
        both_halves(qkv_piece, qkv_other, heads_half * at, heads_half * (at + 1))
        for at in range(3)
    )

    def own_features(value):
        return pick(value.reshape(-1, n_xa, 2, width), my_core, 2)

    def by_x(parts):
        near_own, far_own, near_oth, far_oth = parts
        near = jnp.concatenate(in_order(near_own, near_oth, my_half))
        far = jnp.concatenate(in_order(far_own, far_oth, my_half))
        return jnp.stack(in_order(near, far, my_x))

    def everywhere(value):
        value = value + across(value)
        bit = 1
        while bit < n_row:
            value = value + swap(value, "row", n_row, bit)
            bit *= 2
        bit = 1
        while bit < n_dp:
            value = value + swap(value, "dp", n_dp, bit)
            bit *= 2
        return pick(value, my_x, 0)

    turn_own = own_features(turn_sums)
    qkv_parts = qkv_sums.reshape(4, 3, heads_half)
    early = everywhere(
        jnp.concatenate(
            [
                by_x(qkv_parts[:, 0]),
                by_x(qkv_parts[:, 2]),
                turn_own[2],
                turn_own[3],
                turn_own[0],
                turn_own[1],
                by_x(up_sums.reshape(4, half)),
            ],
            axis=1,
        )
    )
    last_own = own_features(last_sums)
    late = everywhere(jnp.concatenate([last_own[0], last_own[1]], axis=1))

    def piece_of(value, at):
        return value[width * at : width * (at + 1)]

    return (
        outputs,
        input_grad,
        query_grad,
        key_grad,
        value_grad,
        piece_of(early, 0),
        piece_of(early, 1),
        out_grad,
        piece_of(early, 2),
        up_grad,
        early[6 * width :],
        down_grad,
        piece_of(early, 3),
        piece_of(late, 0),
        piece_of(late, 1),
        piece_of(early, 4),
        piece_of(early, 5),
    )


def solution(mesh):
    n_dp, n_row, n_col = (mesh.shape[name] for name in ("dp", "row", "col"))
    sizes = (n_dp, n_row, n_col // 2, 2)
    split = Mesh(mesh.devices.reshape(sizes), ("dp", "row", "xa", "core"))
    col = ("xa", "core")
    tokens, rows, cols, vec = P(("dp", "row"), col), P("row", col), P(col, "row"), P(col)
    in_specs = (
        (tokens, rows, rows, rows, vec, vec, cols, vec, rows, vec, cols)
        + (vec,) * 5
        + (tokens,)
    )
    out_specs = (
        (tokens, tokens, rows, rows, rows, vec, vec, cols, vec, rows, vec, cols) + (vec,) * 5
    )
    return jax.shard_map(
        functools.partial(local, sizes),
        mesh=split,
        in_specs=in_specs,
        out_specs=out_specs,
        check_vma=False,
    )
```

time: 574 us -> 483 us (0.84)
  local copies, waits for them, and re-layouts: 92.6 us -> 46.5 us
  waiting for transfers between devices: 204 us -> 163 us
  other arithmetic: 39 us -> 26 us
  Pallas kernels: 118 us -> 127 us
  starting transfers between devices: 49.7 us -> 57.2 us
    ppermute x37 -> x41, waiting for transfers between devices: 204 us -> 156 us  [the longest x38 149 us: swap(): return lax.ppermute(value, axis, [(at, at ^ bit) for at in range(size)])]
    reshape x6 -> x8, local copies, waits for them, and re-layouts: 25.7 us -> 8.57 us  [the longest x2 4.29 us: wide_tokens(): whole.reshape(held, SEQ, D)]
    dynamic_slice x7 -> x10, local copies, waits for them, and re-layouts: 16.4 us -> 4.6 us  [the longest x8 3.16 us: pick(): return lax.dynamic_index_in_dim(value, at, axis, keepdims=False)]
    unnamed x188 -> x122, local copies, waits for them, and re-layouts: 20.4 us -> 8.9 us
    pallas_call x7 -> x8, Pallas kernels: 118 us -> 127 us  [the longest x1 36.1 us: mlp(): pl.pallas_call(functools.partial(mlp_kernel, tiles), name='mlp', grid_spe...]
    dot_general x8 -> x2, matrix products: 17.6 us -> 8.83 us  [mm_nt(): lax.dot_general(a, b, (((1,), (1,)), ((), ())), preferred_element_type=F32)]
    ppermute x37 -> x41, starting transfers between devices: 49.1 us -> 56.5 us  [the longest x38 48.6 us: swap(): return lax.ppermute(value, axis, [(at, at ^ bit) for at in range(size)])]
    reduce_scatter x2 -> x3, waiting for transfers between devices: 0.02 us -> 6.96 us  [scatter(): return lax.psum_scatter(value, 'row', scatter_dimension=0, tiled=True)]
  transfers between devices with their start and end apart: 40 -> 45, of which waited for: 17 -> 23; matrix products, arithmetic and copies ran while one was open for 28% -> 20% of each run, Pallas kernels for 15% -> 11%
where the time goes in v3:
time: 483 us; the launch traced here: 478 us
  waiting for transfers between devices  163 us (34%)
  Pallas kernels  127 us (26%)
  starting transfers between devices  57.2 us (12%)
  local copies, waits for them, and re-layouts  46.5 us (10%)
  matrix products  43.2 us (9%)
  other arithmetic  26 us (5%)
  between operations  15.1 us (3%)
    ppermute x38, waiting for transfers between devices, swap(): return lax.ppermute(value, axis, [(at, at ^ bit) for at in range(size)])  149 us
    ppermute x38, starting transfers between devices, swap(): return lax.ppermute(value, axis, [(at, at ^ bit) for at in range(size)])  48.6 us
    pallas_call x1, Pallas kernels, mlp(): pl.pallas_call(functools.partial(mlp_kernel, tiles), name='mlp', grid_spe...  36.1 us
    dot_general x8, matrix products, mm_tn(): lax.dot_general(a, b, (((0,), (0,)), ((), ())), preferred_element_type=F32)  34.4 us
    pallas_call x1, Pallas kernels, attend_back(): pl.pallas_call(attend_back_kernel, grid=(pairs, held), name='attend_back'...  26.8 us
    pallas_call x1, Pallas kernels, attend(): pl.pallas_call(attend_kernel, grid=(pairs, held), name='attend', in_specs...  20.2 us
    pallas_call x1, Pallas kernels, turn(): pl.pallas_call(turn_kernel, grid=(rows // TM,), name='turn', in_specs=[ro...  11 us
    pallas_call x1, Pallas kernels, norm_qkv(): pl.pallas_call(norm_qkv_kernel, grid=(rows // TM,), name='norm_qkv', in_s...  9.85 us
  transfers between devices with their start and end apart: 45, of which 23 were waited for; matrix products, arithmetic and copies ran while one was open for 20% of the time, Pallas kernels for 11%

profile of v3, /device:TPU:0, one launch (start us, length us, event | category | flops | bytes accessed | tf_op | source)
XLA Modules:
  0.0 478.0 jit_solution(3092152288516122776)
XLA Ops:
  13.7 4.1 collective-permute-start.5
  19.3 2.2 collective-permute-start.6
  28.2 4.1 collective-permute-done.4
  34.0 2.4 collective-permute-done.5
  38.9 1.8 collective-permute-start.8
  46.3 16.3 %collective-permute-done.8.c_ref = bf16[1024,512]{1,0:T(8,128)(2,1)} collective-permute-done((bf16[1024,512]{1,0:T(8,128)(2,1)}, bf16[1024,512]{1,0:T(8,128)(2,1)}, u32[]{:S(2)}, u32[]{:S(2)}) %collective-permute-start.8) | collective-permute-done | bytes 1048608 | tf_op jit(solution)/shard_map/ppermute | solution.py:457
  68.3 8.4 %collective-permute-done.9 = bf16[1024,256]{1,0:T(8,128)(2,1)S(1)} collective-permute-done((bf16[1024,256]{1,0:T(8,128)(2,1)S(1)}, bf16[1024,256]{1,0:T(8,128)(2,1)S(1)}, u32[]{:S(2)}, u32[]{:S(2)}) %collective-permute-start.9) | collective-permute-done | bytes 524320 | tf_op jit(solution)/shard_map/ppermute | solution.py:457
  81.0 2.2 reshape.545
  84.9 9.8 %norm_qkv.1 = (bf16[1184,1024]{1,0:T(8,128)(2,1)}, bf16[1184,1536]{1,0:T(8,128)(2,1)}, bf16[1024,2048]{1,0:T(8,128)(2,1)}) custom-call(bf16[1184,1024]{1,0:T(8,128)(2,1)} %bitcast.160, f32[1,1024]{1,0:T(1,128)} %bitcast.185, f32[1,1024]{1,0:T(1,128)} %bitcast.191, f32[1,1536]{1,0:T(1,128)} %broadcast_in_dim.34.bias_ref, ...), custom_call_target="tpu_custom_call" | custom-call | flops 3724541952 | bytes 19398656 | tf_op jit(solution)/shard_map/norm_qkv/pallas_call | solution.py:108
  98.4 20.2 %attend.1 = (bf16[1184,512]{1,0:T(8,128)(2,1)}, bf16[2,8,592,592]{3,2,1,0:T(8,128)(2,1)}) custom-call(bf16[1184,1536]{1,0:T(8,128)(2,1)} %get-tuple-element.43.qkv_ref), custom_call_target="tpu_custom_call" | custom-call | flops 17226006528 | bytes 48496640 | tf_op jit(solution)/shard_map/attend/pallas_call | solution.py:138
  118.7 4.6 convolution_convert_fusion.a_ref
  127.0 17.3 %collective-permute-done.15.refs_2_.refs_6_ = bf16[1024,1024]{1,0:T(8,128)(2,1)} collective-permute-done((bf16[1024,1024]{1,0:T(8,128)(2,1)}, bf16[1024,1024]{1,0:T(8,128)(2,1)}, u32[]{:S(2)}, u32[]{:S(2)}) %collective-permute-start.15) | collective-permute-done | bytes 2097184 | tf_op jit(solution)/shard_map/ppermute | solution.py:457
  144.3 2.3 slice.482
  147.4 2.3 slice.481
  154.6 2.1 reshape.553
  158.4 6.7 %middle.1 = (f32[1184,1024]{1,0:T(8,128)}, bf16[1184,1024]{1,0:T(8,128)(2,1)}) custom-call(bf16[1184,1024]{1,0:T(8,128)(2,1)} %bitcast.161, bf16[1184,1024]{1,0:T(8,128)(2,1)} %convolution_convert_fusion.a_ref, bf16[1184,1024]{1,0:T(8,128)(2,1)} %collective-permute-done.11.b_ref, f32[1,1024]{1,0:T(1,128)} %bitcast.188, f32[1,1024]{1,0:T(1,128)} %bitcast.178, ...), custom_call_target="tpu_custom_call" | custom-call | flops 24248320 | bytes 14548992 | tf_op jit(solution)/shard_map/middle/pallas_call | solution.py:200
  165.1 6.4 %collective-permute-done.17.refs_7_ = bf16[1024,512]{1,0:T(8,128)(2,1)} collective-permute-done((bf16[1024,512]{1,0:T(8,128)(2,1)}, bf16[1024,512]{1,0:T(8,128)(2,1)}, u32[]{:S(2)}, u32[]{:S(2)}) %collective-permute-start.17) | collective-permute-done | bytes 1048608 | tf_op jit(solution)/shard_map/ppermute | solution.py:457
  171.5 2.8 collective-permute-done.16.refs_3_
  174.3 36.1 %mlp.1 = (bf16[1184,2048]{1,0:T(8,128)(2,1)}, bf16[1184,2048]{1,0:T(8,128)(2,1)}, f32[1184,512]{1,0:T(8,128)}, bf16[1184,512]{1,0:T(8,128)(2,1)}, bf16[1184,1024]{1,0:T(8,128)(2,1)}, /*index=5*/f32[1,2048]{1,0:T(1,128)}) custom-call(s32[2]{0:T(128)} %pad_add_fusion.place_ref, bf16[1184,1024]{1,0:T(8,128)(2,1)} %get-tuple-element.47.n_ref, ...), custom_call_target="tpu_custom_call" | custom-call | flops 19864223744 | bytes 29097984 | tf_op jit(solution)/shard_map/mlp/pallas_call | solution.py:266
  210.5 4.8 %collective-permute-done.20.b_ref = bf16[1184,1024]{1,0:T(8,128)(2,1)S(1)} collective-permute-done((bf16[1184,1024]{1,0:T(8,128)(2,1)}, bf16[1184,1024]{1,0:T(8,128)(2,1)S(1)}, u32[]{:S(2)}, u32[]{:S(2)}) %collective-permute-start.20) | collective-permute-done | bytes 2424864 | tf_op jit(solution)/shard_map/ppermute | solution.py:457
  216.7 11.0 %turn.1 = (f32[1184,1024]{1,0:T(8,128)}, bf16[1184,1024]{1,0:T(8,128)(2,1)}, bf16[1184,512]{1,0:T(8,128)(2,1)}, f32[4,1024]{1,0:T(4,128)}) custom-call(f32[1184,1024]{1,0:T(8,128)} %get-tuple-element.46.h_ref, bf16[1184,1024]{1,0:T(8,128)(2,1)} %bitcast.164, bf16[1184,1024]{1,0:T(8,128)(2,1)} %get-tuple-element.54.a_ref, bf16[1184,1024]{1,0:T(8,128)(2,1)} %copy-done.6, ...), custom_call_target="tpu_custom_call" | custom-call | flops 1241513984 | bytes 21823488 | tf_op jit(solution)/shard_map/turn/pallas_call | solution.py:364
  227.8 26.8 %attend_back.1 = (bf16[1184,1536]{1,0:T(8,128)(2,1)}, f32[1,1536]{1,0:T(1,128)}) custom-call(bf16[1184,1536]{1,0:T(8,128)(2,1)} %get-tuple-element.43.qkv_ref, bf16[2,8,592,592]{3,2,1,0:T(8,128)(2,1)} %get-tuple-element.56.p_ref, bf16[1184,512]{1,0:T(8,128)(2,1)} %get-tuple-element.57.g_ref), custom_call_target="tpu_custom_call" | custom-call | flops 21532508160 | bytes 60620800 | tf_op jit(solution)/shard_map/attend_back/pallas_call | solution.py:174
  254.5 2.9 convolution_convert_fusion.4
  261.2 16.7 %collective-permute-done.24 = bf16[1024,384]{1,0:T(8,128)(2,1)S(1)} collective-permute-done((bf16[1024,384]{1,0:T(8,128)(2,1)S(1)}, bf16[1024,384]{1,0:T(8,128)(2,1)S(1)}, u32[]{:S(2)}, u32[]{:S(2)}) %collective-permute-start.24) | collective-permute-done | bytes 786464 | tf_op jit(solution)/shard_map/ppermute | solution.py:457
  280.7 13.2 %collective-permute-done.23 = bf16[1024,384]{1,0:T(8,128)(2,1)S(1)} collective-permute-done((bf16[1024,384]{1,0:T(8,128)(2,1)S(1)}, bf16[1024,384]{1,0:T(8,128)(2,1)S(1)}, u32[]{:S(2)}, u32[]{:S(2)}) %collective-permute-start.23) | collective-permute-done | bytes 786464 | tf_op jit(solution)/shard_map/ppermute | solution.py:457
  295.5 1.9 collective-permute-done.25
  298.7 6.4 %fusion.5 = bf16[1024,1024]{1,0:T(8,128)(2,1)} fusion(bf16[1184,1024]{1,0:T(8,128)(2,1)S(1)} %copy-done.38, bf16[1184,2048]{1,0:T(8,128)(2,1)} %get-tuple-element.65), kind=kOutput, calls=%fused_computation.13 | convolution fusion | flops 2484076544 | bytes 6946816 | tf_op jit(solution)/shard_map/dot_general | solution.py:33
  306.6 9.6 %convolution_convert_fusion.1 = bf16[1024,2048]{1,0:T(8,128)(2,1)} fusion(bf16[1184,1024]{1,0:T(8,128)(2,1)S(1)} %bitcast.165, bf16[1184,2048]{1,0:T(8,128)(2,1)} %get-tuple-element.67), kind=kOutput, calls=%fused_computation.2 | convolution fusion | flops 4968153088 | bytes 11468800 | tf_op jit(solution)/shard_map/dot_general | solution.py:33
  318.1 2.3 collective-permute-done.18.b_ref
  321.4 7.2 %finish.1 = (bf16[1184,256]{1,0:T(8,128)(2,1)}, bf16[1184,256]{1,0:T(8,128)(2,1)}) custom-call(s32[2]{0:T(128)} %pad_add_fusion.place_ref, f32[1184,1024]{1,0:T(8,128)} %get-tuple-element.46.h_ref, f32[1184,512]{1,0:T(8,128)} %get-tuple-element.50.a_ref, bf16[1184,512]{1,0:T(8,128)(2,1)} %copy-done.9, f32[1,1024]{1,0:T(1,128)} %bitcast.189), custom_call_target="tpu_custom_call" | custom-call | flops 2424832 | bytes 7274496 | tf_op jit(solution)/shard_map/finish/pallas_call | solution.py:320
  329.2 21.8 %collective-permute-done.31 = bf16[1024,1024]{1,0:T(8,128)(2,1)} collective-permute-done((bf16[1024,1024]{1,0:T(8,128)(2,1)}, bf16[1024,1024]{1,0:T(8,128)(2,1)}, u32[]{:S(2)}, u32[]{:S(2)}) %collective-permute-start.31) | collective-permute-done | bytes 2097184 | tf_op jit(solution)/shard_map/ppermute | solution.py:457
  351.0 7.3 %add_convert_fusion = bf16[1024,1024]{1,0:T(8,128)(2,1)} fusion(bf16[1024,1024]{1,0:T(8,128)(2,1)} %collective-permute-done.31, bf16[1184,1024]{1,0:T(8,128)(2,1)} %get-tuple-element.47.n_ref, bf16[1184,2048]{1,0:T(8,128)(2,1)} %get-tuple-element.65), kind=kOutput, calls=%fused_computation | convolution fusion | flops 2486173696 | bytes 9043968 | tf_op jit(solution)/shard_map/dot_general | solution.py:33
  358.4 3.4 convolution_convert_fusion.3
  363.5 4.2 convolution_convert_fusion.2.a_ref
  368.8 3.1 collective-permute-done.27
  371.9 11.3 %collective-permute-start.28 = (f32[2,2560]{1,0:T(2,128)S(1)}, f32[2,2560]{1,0:T(2,128)S(1)}, u32[]{:S(2)}, u32[]{:S(2)}) collective-permute-start(f32[2,2560]{1,0:T(2,128)S(1)} %add.153), channel_id=1, source_target_pairs={{0,4},{4,0},{8,12},{12,8},{1,5},{5,1},{9,13},{13,9},{2,6},{6,2},{1... | collective-permute-start | bytes 61448 | tf_op jit(solution)/shard_map/ppermute | solution.py:457
  387.2 3.1 collective-permute-start.29
  391.8 9.2 %last.1 = (f32[1184,256]{1,0:T(8,128)}, bf16[1184,256]{1,0:T(8,128)(2,1)}, f32[2,1024]{1,0:T(2,128)}) custom-call(s32[2]{0:T(128)} %pad_add_fusion.place_ref, bf16[1184,1024]{1,0:T(8,128)(2,1)} %bitcast.162, f32[1184,1024]{1,0:T(8,128)} %get-tuple-element.55.dh_ref, bf16[1184,1024]{1,0:T(8,128)(2,1)} %copy-done.4, bf16[1184,1024]{1,0:T(8,128)(2,1)} %copy-done.5, ...), custom_call_target="tpu_custom_call" | custom-call | flops 24248320 | bytes 14548992 | tf_op jit(solution)/shard_map/last/pallas_call | solution.py:405
  406.3 8.7 %collective-permute-done.37 = f32[2,512]{1,0:T(2,128)S(1)} collective-permute-done((f32[2,512]{1,0:T(2,128)S(1)}, f32[2,512]{1,0:T(2,128)S(1)}, u32[]{:S(2)}, u32[]{:S(2)}) %collective-permute-start.37) | collective-permute-done | bytes 4128 | tf_op jit(solution)/shard_map/ppermute | solution.py:457
  415.3 2.8 add_convert_fusion.1
  418.8 3.7 collective-permute-start.39
  425.8 1.9 collective-permute-done.40
  428.3 4.1 collective-permute-done.22
  433.0 1.8 reshape.561
  437.3 3.3 collective-permute-done.26
  442.1 7.0 %reduce-scatter.6.cloned.1.call-done = bf16[256,640]{1,0:T(8,128)(2,1)} async-done(((bf16[1024,640]{1,0:T(8,128)(2,1)}), bf16[256,640]{1,0:T(8,128)(2,1)}) %reduce-scatter.6.cloned.1.call-update) | async-done | bytes 327696 | tf_op jit(solution)/shard_map/reduce_scatter | solution.py:596
  452.1 7.8 %collective-permute-done.34 = bf16[256,640]{1,0:T(8,128)(2,1)S(1)} collective-permute-done((bf16[256,640]{1,0:T(8,128)(2,1)}, bf16[256,640]{1,0:T(8,128)(2,1)S(1)}, u32[]{:S(2)}, u32[]{:S(2)}) %collective-permute-start.34) | collective-permute-done | bytes 327712 | tf_op jit(solution)/shard_map/ppermute | solution.py:457
  462.7 6.9 %collective-permute-done.36 = bf16[256,1024]{1,0:T(8,128)(2,1)S(1)} collective-permute-done((bf16[256,1024]{1,0:T(8,128)(2,1)S(1)}, bf16[256,1024]{1,0:T(8,128)(2,1)S(1)}, u32[]{:S(2)}, u32[]{:S(2)}) %collective-permute-start.36) | collective-permute-done | bytes 524320 | tf_op jit(solution)/shard_map/ppermute | solution.py:457
  (300 shorter events, 96.8 us)
Async XLA Ops:
  7.3 88.7 %all-gather.2.cloned.1.call-start = ((), (), s32[]{:S(2)}) async-start(), calls=%async_computation.3 | async-start | bytes 2621440 | tf_op jit(solution)/shard_map/all_gather | solution.py:549
  13.7 22.7 %collective-permute-start.5 = (bf16[256,512]{1,0:T(8,128)(2,1)}, bf16[256,512]{1,0:T(8,128)(2,1)S(1)}, u32[]{:S(2)}, u32[]{:S(2)}) collective-permute-start(bf16[256,512]{1,0:T(8,128)(2,1)} %get-tuple-element.145), channel_id=1, source_target_pairs={{0,8},{4,12},{8,0},{12,4},{1,9},{5,13},{9,1},{13,5},{2,10},{6,14},... | collective-permute-start | bytes 786440 | tf_op jit(solution)/shard_map/ppermute | solution.py:488
  17.8 14.5 %collective-permute-start.4 = (bf16[256,512]{1,0:T(8,128)(2,1)}, bf16[256,512]{1,0:T(8,128)(2,1)}, u32[]{:S(2)}, u32[]{:S(2)}) collective-permute-start(bf16[256,512]{1,0:T(8,128)(2,1)} %get-tuple-element.145), channel_id=1, source_target_pairs={{0,4},{4,8},{8,12},{12,0},{1,5},{5,9},{9,13},{13,1},{2,6},{6,10},{... | collective-permute-start | bytes 786440 | tf_op jit(solution)/shard_map/ppermute | solution.py:488
  19.3 17.9 %collective-permute-start.6 = (bf16[256,512]{1,0:T(8,128)(2,1)}, bf16[256,512]{1,0:T(8,128)(2,1)}, u32[]{:S(2)}, u32[]{:S(2)}) collective-permute-start(bf16[256,512]{1,0:T(8,128)(2,1)} %get-tuple-element.145), channel_id=1, source_target_pairs={{0,12},{4,0},{8,4},{12,8},{1,13},{5,1},{9,5},{13,9},{2,14},{6,2},{... | collective-permute-start | bytes 786440 | tf_op jit(solution)/shard_map/ppermute | solution.py:488
  21.8 5.6 %collective-permute-start.2 = (f32[3072]{0:T(1024)S(1)}, f32[3072]{0:T(1024)S(1)}, u32[]{:S(2)}, u32[]{:S(2)}) collective-permute-start(f32[3072]{0:T(1024)S(1)} %constant_dynamic-update-slice_fusion.26), channel_id=1, source_target_pairs={{0,2},{2,0},{1,3},{3,1},{4,6},{6,4},{5,7},{7,5},{8,10},{10,8},{9,1... | collective-permute-start | bytes 36872 | tf_op jit(solution)/shard_map/ppermute | solution.py:457
  23.6 18.5 %collective-permute-start = (bf16[1154,256]{1,0:T(8,128)(2,1)S(1)}, bf16[1154,256]{1,0:T(8,128)(2,1)S(1)}, u32[]{:S(2)}, u32[]{:S(2)}) collective-permute-start(bf16[1154,256]{1,0:T(8,128)(2,1)S(1)} %get-tuple-element.124), channel_id=1, source_target_pairs={{0,2},{2,0},{1,3},{3,1},{4,6},{6,4},{5,7},{7,5},{8,10},{10,8},{9,1... | collective-permute-start | bytes 1772552 | tf_op jit(solution)/shard_map/ppermute | solution.py:457
  28.2 15.1 %collective-permute-start.3 = (f32[2,3072]{1,0:T(2,128)S(1)}, f32[2,3072]{1,0:T(2,128)S(1)}, u32[]{:S(2)}, u32[]{:S(2)}) collective-permute-start(f32[2,3072]{1,0:T(2,128)S(1)} %pad_maximum_fusion.10), channel_id=1, source_target_pairs={{0,1},{1,0},{2,3},{3,2},{4,5},{5,4},{6,7},{7,6},{8,9},{9,8},{10,11... | collective-permute-start | bytes 73736 | tf_op jit(solution)/shard_map/ppermute | solution.py:457
  38.9 23.7 %collective-permute-start.8 = (bf16[1024,512]{1,0:T(8,128)(2,1)}, bf16[1024,512]{1,0:T(8,128)(2,1)}, u32[]{:S(2)}, u32[]{:S(2)}) collective-permute-start(bf16[1024,512]{1,0:T(8,128)(2,1)} %constant_dynamic-update-slice_fusion.13.a_ref), channel_id=1, source_target_pairs={{0,16},{16,0},{1,17},{17,1},{2,18},{18,2},{3,19},{19,3},{4,20},{20... | collective-permute-start | bytes 3145736 | tf_op jit(solution)/shard_map/ppermute | solution.py:457
  40.6 24.4 %collective-permute-start.7 = (bf16[1024,512]{1,0:T(8,128)(2,1)}, bf16[1024,512]{1,0:T(8,128)(2,1)}, u32[]{:S(2)}, u32[]{:S(2)}) collective-permute-start(bf16[1024,512]{1,0:T(8,128)(2,1)} %constant_dynamic-update-slice_fusion.13.a_ref), channel_id=1, source_target_pairs={{0,2},{2,0},{1,3},{3,1},{4,6},{6,4},{5,7},{7,5},{8,10},{10,8},{9,1... | collective-permute-start | bytes 3145736 | tf_op jit(solution)/shard_map/ppermute | solution.py:457
  43.2 24.5 %collective-permute-start.1 = (bf16[1154,512]{1,0:T(8,128)(2,1)}, bf16[1154,512]{1,0:T(8,128)(2,1)S(1)}, u32[]{:S(2)}, u32[]{:S(2)}) collective-permute-start(bf16[1154,512]{1,0:T(8,128)(2,1)} %pad_maximum_fusion.5), channel_id=1, source_target_pairs={{0,1},{1,0},{2,3},{3,2},{4,5},{5,4},{6,7},{7,6},{8,9},{9,8},{10,11... | collective-permute-start | bytes 3545096 | tf_op jit(solution)/shard_map/ppermute | solution.py:457
  43.9 390.9 %reduce-scatter.4.cloned.1.call-start = ((), (), s32[]{:S(2)}) async-start(), calls=%async_computation.4 | async-start | bytes 983040 | tf_op jit(solution)/shard_map/reduce_scatter | solution.py:596
  63.7 13.1 %collective-permute-start.10 = (bf16[1024,256]{1,0:T(8,128)(2,1)S(1)}, bf16[1024,256]{1,0:T(8,128)(2,1)S(1)}, u32[]{:S(2)}, u32[]{:S(2)}) collective-permute-start(bf16[1024,256]{1,0:T(8,128)(2,1)S(1)} %slice.464), channel_id=1, source_target_pairs={{0,2},{2,0},{1,3},{3,1},{4,6},{6,4},{5,7},{7,5},{8,10},{10,8},{9,1... | collective-permute-start | bytes 1572872 | tf_op jit(solution)/shard_map/ppermute | solution.py:457
  66.1 10.6 %collective-permute-start.9 = (bf16[1024,256]{1,0:T(8,128)(2,1)S(1)}, bf16[1024,256]{1,0:T(8,128)(2,1)S(1)}, u32[]{:S(2)}, u32[]{:S(2)}) collective-permute-start(bf16[1024,256]{1,0:T(8,128)(2,1)S(1)} %slice.463), channel_id=1, source_target_pairs={{0,16},{16,0},{1,17},{17,1},{2,18},{18,2},{3,19},{19,3},{4,20},{20... | collective-permute-start | bytes 1572872 | tf_op jit(solution)/shard_map/ppermute | solution.py:457
  78.0 16.7 %collective-permute-start.12 = (bf16[1154,256]{1,0:T(8,128)(2,1)}, bf16[1154,256]{1,0:T(8,128)(2,1)}, u32[]{:S(2)}, u32[]{:S(2)}) collective-permute-start(bf16[1154,256]{1,0:T(8,128)(2,1)} %get-tuple-element.122), channel_id=1, source_target_pairs={{0,2},{2,0},{1,3},{3,1},{4,6},{6,4},{5,7},{7,5},{8,10},{10,8},{9,1... | collective-permute-start | bytes 1772552 | tf_op jit(solution)/shard_map/ppermute | solution.py:457
  95.9 55.3 %collective-permute-start.13 = (bf16[1154,512]{1,0:T(8,128)(2,1)S(1)}, bf16[1154,512]{1,0:T(8,128)(2,1)S(1)}, u32[]{:S(2)}, u32[]{:S(2)}) collective-permute-start(bf16[1154,512]{1,0:T(8,128)(2,1)S(1)} %pad_maximum_fusion.6), channel_id=1, source_target_pairs={{0,1},{1,0},{2,3},{3,2},{4,5},{5,4},{6,7},{7,6},{8,9},{9,8},{10,11... | collective-permute-start | bytes 3545096 | tf_op jit(solution)/shard_map/ppermute | solution.py:457
  96.0 48.3 %collective-permute-start.15 = (bf16[1024,1024]{1,0:T(8,128)(2,1)}, bf16[1024,1024]{1,0:T(8,128)(2,1)}, u32[]{:S(2)}, u32[]{:S(2)}) collective-permute-start(bf16[1024,1024]{1,0:T(8,128)(2,1)} %all-gather.2.cloned.1.call-done.refs_0_.refs_4_), channel_id=1, source_target_pairs={{0,16},{16,0},{1,17},{17,1},{2,18},{18,2},{3,19},{19,3},{4,20},{20... | collective-permute-start | bytes 6291464 | tf_op jit(solution)/shard_map/ppermute | solution.py:457
  96.9 50.5 %collective-permute-start.14 = (bf16[1024,1024]{1,0:T(8,128)(2,1)}, bf16[1024,1024]{1,0:T(8,128)(2,1)}, u32[]{:S(2)}, u32[]{:S(2)}) collective-permute-start(bf16[1024,1024]{1,0:T(8,128)(2,1)} %all-gather.2.cloned.1.call-done.refs_0_.refs_4_), channel_id=1, source_target_pairs={{0,2},{2,0},{1,3},{3,1},{4,6},{6,4},{5,7},{7,5},{8,10},{10,8},{9,1... | collective-permute-start | bytes 6291464 | tf_op jit(solution)/shard_map/ppermute | solution.py:457
  123.3 35.2 %collective-permute-start.11 = (bf16[1184,1024]{1,0:T(8,128)(2,1)}, bf16[1184,1024]{1,0:T(8,128)(2,1)}, u32[]{:S(2)}, u32[]{:S(2)}) collective-permute-start(bf16[1184,1024]{1,0:T(8,128)(2,1)} %convolution_convert_fusion.a_ref), channel_id=1, source_target_pairs={{0,1},{1,0},{2,3},{3,2},{4,5},{5,4},{6,7},{7,6},{8,9},{9,8},{10,11... | collective-permute-start | bytes 7274504 | tf_op jit(solution)/shard_map/ppermute | solution.py:457
  146.6 24.9 %collective-permute-start.17 = (bf16[1024,512]{1,0:T(8,128)(2,1)}, bf16[1024,512]{1,0:T(8,128)(2,1)}, u32[]{:S(2)}, u32[]{:S(2)}) collective-permute-start(bf16[1024,512]{1,0:T(8,128)(2,1)} %slice.482), channel_id=1, source_target_pairs={{0,2},{2,0},{1,3},{3,1},{4,6},{6,4},{5,7},{7,5},{8,10},{10,8},{9,1... | collective-permute-start | bytes 3145736 | tf_op jit(solution)/shard_map/ppermute | solution.py:457
  149.7 24.6 %collective-permute-start.16 = (bf16[1024,512]{1,0:T(8,128)(2,1)}, bf16[1024,512]{1,0:T(8,128)(2,1)}, u32[]{:S(2)}, u32[]{:S(2)}) collective-permute-start(bf16[1024,512]{1,0:T(8,128)(2,1)} %slice.481), channel_id=1, source_target_pairs={{0,16},{16,0},{1,17},{17,1},{2,18},{18,2},{3,19},{19,3},{4,20},{20... | collective-permute-start | bytes 3145736 | tf_op jit(solution)/shard_map/ppermute | solution.py:457
  210.4 4.9 %collective-permute-start.20 = (bf16[1184,1024]{1,0:T(8,128)(2,1)}, bf16[1184,1024]{1,0:T(8,128)(2,1)S(1)}, u32[]{:S(2)}, u32[]{:S(2)}) collective-permute-start(bf16[1184,1024]{1,0:T(8,128)(2,1)} %get-tuple-element.54.a_ref), channel_id=1, source_target_pairs={{0,1},{1,0},{2,3},{3,2},{4,5},{5,4},{6,7},{7,6},{8,9},{9,8},{10,11... | collective-permute-start | bytes 7274504 | tf_op jit(solution)/shard_map/ppermute | solution.py:457
  257.4 20.5 %collective-permute-start.24 = (bf16[1024,384]{1,0:T(8,128)(2,1)S(1)}, bf16[1024,384]{1,0:T(8,128)(2,1)S(1)}, u32[]{:S(2)}, u32[]{:S(2)}) collective-permute-start(bf16[1024,384]{1,0:T(8,128)(2,1)S(1)} %convolution_convert_fusion.4), channel_id=1, source_target_pairs={{0,16},{16,0},{1,17},{17,1},{2,18},{18,2},{3,19},{19,3},{4,20},{20... | collective-permute-start | bytes 2359304 | tf_op jit(solution)/shard_map/ppermute | solution.py:457
  260.6 33.3 %collective-permute-start.23 = (bf16[1024,384]{1,0:T(8,128)(2,1)S(1)}, bf16[1024,384]{1,0:T(8,128)(2,1)S(1)}, u32[]{:S(2)}, u32[]{:S(2)}) collective-permute-start(bf16[1024,384]{1,0:T(8,128)(2,1)S(1)} %convolution_convert_fusion.5), channel_id=1, source_target_pairs={{0,16},{16,0},{1,17},{17,1},{2,18},{18,2},{3,19},{19,3},{4,20},{20... | collective-permute-start | bytes 2359304 | tf_op jit(solution)/shard_map/ppermute | solution.py:457
  279.5 18.0 %collective-permute-start.25 = (bf16[1024,384]{1,0:T(8,128)(2,1)S(1)}, bf16[1024,384]{1,0:T(8,128)(2,1)S(1)}, u32[]{:S(2)}, u32[]{:S(2)}) collective-permute-start(bf16[1024,384]{1,0:T(8,128)(2,1)S(1)} %add_convert_fusion.3), channel_id=1, source_target_pairs={{0,2},{2,0},{1,3},{3,1},{4,6},{6,4},{5,7},{7,5},{8,10},{10,8},{9,1... | collective-permute-start | bytes 2359304 | tf_op jit(solution)/shard_map/ppermute | solution.py:457
  298.6 136.7 %reduce-scatter.8.cloned.1.call-start = ((), (), s32[]{:S(2)}) async-start(), calls=%async_computation.6 | async-start | bytes 5242880 | tf_op jit(solution)/shard_map/reduce_scatter | solution.py:596
  305.1 45.9 %collective-permute-start.31 = (bf16[1024,1024]{1,0:T(8,128)(2,1)}, bf16[1024,1024]{1,0:T(8,128)(2,1)}, u32[]{:S(2)}, u32[]{:S(2)}) collective-permute-start(bf16[1024,1024]{1,0:T(8,128)(2,1)} %fusion.5), channel_id=1, source_target_pairs={{0,16},{16,0},{1,17},{17,1},{2,18},{18,2},{3,19},{19,3},{4,20},{20... | collective-permute-start | bytes 6291464 | tf_op jit(solution)/shard_map/ppermute | solution.py:457
  316.2 132.8 %reduce-scatter.6.cloned.1.call-start = ((), (), s32[]{:S(2)}) async-start(), calls=%async_computation.5 | async-start | bytes 1638400 | tf_op jit(solution)/shard_map/reduce_scatter | solution.py:596
  317.5 2.9 collective-permute-start.18
  328.6 29.7 %copy-start.20 = (f32[1,1536]{1,0:T(1,128)S(1)}, f32[1,1536]{1,0:T(1,128)}, u32[]{:S(2)}) copy-start(f32[1,1536]{1,0:T(1,128)} %get-tuple-element.62) | copy-start | bytes 18436
  328.6 29.8 %copy-start.17 = (f32[4,1024]{1,0:T(4,128)S(1)}, f32[4,1024]{1,0:T(4,128)}, u32[]{:S(2)}) copy-start(f32[4,1024]{1,0:T(4,128)} %get-tuple-element.63) | copy-start | bytes 49156
  328.6 29.8 %copy-start.43 = (bf16[1184,512]{1,0:T(8,128)(2,1)S(1)}, bf16[1184,512]{1,0:T(8,128)(2,1)}, u32[]{:S(2)}) copy-start(bf16[1184,512]{1,0:T(8,128)(2,1)} %get-tuple-element.44) | copy-start | bytes 3637252
  328.6 56.5 %collective-permute-start.19 = (bf16[1184,256]{1,0:T(8,128)(2,1)}, bf16[1184,256]{1,0:T(8,128)(2,1)S(1)}, u32[]{:S(2)}, u32[]{:S(2)}) collective-permute-start(bf16[1184,256]{1,0:T(8,128)(2,1)} %get-tuple-element.53), channel_id=1, source_target_pairs={{0,2},{2,0},{1,3},{3,1},{4,6},{6,4},{5,7},{7,5},{8,10},{10,8},{9,1... | collective-permute-start | bytes 1818632 | tf_op jit(solution)/shard_map/ppermute | solution.py:457
  361.9 21.2 %collective-permute-start.32 = (bf16[1024,256]{1,0:T(8,128)(2,1)S(1)}, bf16[1024,256]{1,0:T(8,128)(2,1)S(1)}, u32[]{:S(2)}, u32[]{:S(2)}) collective-permute-start(bf16[1024,256]{1,0:T(8,128)(2,1)S(1)} %slice.500), channel_id=1, source_target_pairs={{0,16},{16,0},{1,17},{17,1},{2,18},{18,2},{3,19},{19,3},{4,20},{20... | collective-permute-start | bytes 1572872 | tf_op jit(solution)/shard_map/ppermute | solution.py:457
  367.7 22.5 %collective-permute-start.21 = (bf16[1184,1024]{1,0:T(8,128)(2,1)S(1)}, bf16[1184,1024]{1,0:T(8,128)(2,1)S(1)}, u32[]{:S(2)}, u32[]{:S(2)}) collective-permute-start(bf16[1184,1024]{1,0:T(8,128)(2,1)S(1)} %convolution_convert_fusion.2.a_ref), channel_id=1, source_target_pairs={{0,1},{1,0},{2,3},{3,2},{4,5},{5,4},{6,7},{7,6},{8,9},{9,8},{10,11... | collective-permute-start | bytes 7274504 | tf_op jit(solution)/shard_map/ppermute | solution.py:457
  368.0 3.8 collective-permute-start.27
  371.9 15.3 %collective-permute-start.28 = (f32[2,2560]{1,0:T(2,128)S(1)}, f32[2,2560]{1,0:T(2,128)S(1)}, u32[]{:S(2)}, u32[]{:S(2)}) collective-permute-start(f32[2,2560]{1,0:T(2,128)S(1)} %add.153), channel_id=1, source_target_pairs={{0,4},{4,0},{8,12},{12,8},{1,5},{5,1},{9,13},{13,9},{2,6},{6,2},{1... | collective-permute-start | bytes 61448 | tf_op jit(solution)/shard_map/ppermute | solution.py:457
  384.5 30.8 %collective-permute-start.33 = (bf16[1024,640]{1,0:T(8,128)(2,1)}, bf16[1024,640]{1,0:T(8,128)(2,1)}, u32[]{:S(2)}, u32[]{:S(2)}) collective-permute-start(bf16[1024,640]{1,0:T(8,128)(2,1)} %pad_maximum_fusion.3), channel_id=1, source_target_pairs={{0,2},{2,0},{1,3},{3,1},{4,6},{6,4},{5,7},{7,5},{8,10},{10,8},{9,1... | collective-permute-start | bytes 3932168 | tf_op jit(solution)/shard_map/ppermute | solution.py:457
  387.2 17.5 %collective-permute-start.29 = (f32[2,2560]{1,0:T(2,128)S(1)}, f32[2,2560]{1,0:T(2,128)S(1)}, u32[]{:S(2)}, u32[]{:S(2)}) collective-permute-start(f32[2,2560]{1,0:T(2,128)S(1)} %add.154), channel_id=1, source_target_pairs={{0,8},{4,12},{8,0},{12,4},{1,9},{5,13},{9,1},{13,5},{2,10},{6,14},... | collective-permute-start | bytes 61448 | tf_op jit(solution)/shard_map/ppermute | solution.py:457
  401.7 13.3 %collective-permute-start.37 = (f32[2,512]{1,0:T(2,128)S(1)}, f32[2,512]{1,0:T(2,128)S(1)}, u32[]{:S(2)}, u32[]{:S(2)}) collective-permute-start(f32[2,512]{1,0:T(2,128)S(1)} %pad_maximum_fusion.19), channel_id=1, source_target_pairs={{0,2},{2,0},{1,3},{3,1},{4,6},{6,4},{5,7},{7,5},{8,10},{10,8},{9,1... | collective-permute-start | bytes 12296 | tf_op jit(solution)/shard_map/ppermute | solution.py:457
  404.7 17.8 %collective-permute-start.30 = (f32[2,2560]{1,0:T(2,128)S(1)}, f32[2,2560]{1,0:T(2,128)S(1)}, u32[]{:S(2)}, u32[]{:S(2)}) collective-permute-start(f32[2,2560]{1,0:T(2,128)S(1)} %add.155), channel_id=1, source_target_pairs={{0,16},{16,0},{1,17},{17,1},{2,18},{18,2},{3,19},{19,3},{4,20},{20... | collective-permute-start | bytes 61448 | tf_op jit(solution)/shard_map/ppermute | solution.py:457
  415.0 3.8 collective-permute-start.38
  418.2 14.2 %collective-permute-start.22 = (bf16[1184,256]{1,0:T(8,128)(2,1)}, bf16[1184,256]{1,0:T(8,128)(2,1)S(1)}, u32[]{:S(2)}, u32[]{:S(2)}) collective-permute-start(bf16[1184,256]{1,0:T(8,128)(2,1)} %get-tuple-element.60), channel_id=1, source_target_pairs={{0,2},{2,0},{1,3},{3,1},{4,6},{6,4},{5,7},{7,5},{8,10},{10,8},{9,1... | collective-permute-start | bytes 1818632 | tf_op jit(solution)/shard_map/ppermute | solution.py:457
  418.8 5.3 %collective-permute-start.39 = (f32[2,512]{1,0:T(2,128)S(1)}, f32[2,512]{1,0:T(2,128)S(1)}, u32[]{:S(2)}, u32[]{:S(2)}) collective-permute-start(f32[2,512]{1,0:T(2,128)S(1)} %add.164), channel_id=1, source_target_pairs={{0,8},{4,12},{8,0},{12,4},{1,9},{5,13},{9,1},{13,5},{2,10},{6,14},... | collective-permute-start | bytes 12296 | tf_op jit(solution)/shard_map/ppermute | solution.py:457
  424.1 3.6 collective-permute-start.40
  434.8 5.9 %collective-permute-start.26 = (bf16[256,384]{1,0:T(8,128)(2,1)}, bf16[256,384]{1,0:T(8,128)(2,1)S(1)}, u32[]{:S(2)}, u32[]{:S(2)}) collective-permute-start(bf16[256,384]{1,0:T(8,128)(2,1)} %reduce-scatter.4.cloned.1.call-done), channel_id=1, source_target_pairs={{0,16},{16,0},{1,17},{17,1},{2,18},{18,2},{3,19},{19,3},{4,20},{20... | collective-permute-start | bytes 589832 | tf_op jit(solution)/shard_map/ppermute | solution.py:457
  436.6 14.7 %collective-permute-start.35 = (bf16[256,1024]{1,0:T(8,128)(2,1)S(1)}, bf16[256,1024]{1,0:T(8,128)(2,1)S(1)}, u32[]{:S(2)}, u32[]{:S(2)}) collective-permute-start(bf16[256,1024]{1,0:T(8,128)(2,1)S(1)} %pad_maximum_fusion.8), channel_id=1, source_target_pairs={{0,2},{2,0},{1,3},{3,1},{4,6},{6,4},{5,7},{7,5},{8,10},{10,8},{9,1... | collective-permute-start | bytes 1572872 | tf_op jit(solution)/shard_map/ppermute | solution.py:457
  449.1 10.8 %collective-permute-start.34 = (bf16[256,640]{1,0:T(8,128)(2,1)}, bf16[256,640]{1,0:T(8,128)(2,1)S(1)}, u32[]{:S(2)}, u32[]{:S(2)}) collective-permute-start(bf16[256,640]{1,0:T(8,128)(2,1)} %reduce-scatter.6.cloned.1.call-done), channel_id=1, source_target_pairs={{0,16},{16,0},{1,17},{17,1},{2,18},{18,2},{3,19},{19,3},{4,20},{20... | collective-permute-start | bytes 983048 | tf_op jit(solution)/shard_map/ppermute | solution.py:457
  451.4 18.2 %collective-permute-start.36 = (bf16[256,1024]{1,0:T(8,128)(2,1)S(1)}, bf16[256,1024]{1,0:T(8,128)(2,1)S(1)}, u32[]{:S(2)}, u32[]{:S(2)}) collective-permute-start(bf16[256,1024]{1,0:T(8,128)(2,1)S(1)} %add_convert_fusion.5), channel_id=1, source_target_pairs={{0,16},{16,0},{1,17},{17,1},{2,18},{18,2},{3,19},{19,3},{4,20},{20... | collective-permute-start | bytes 1572872 | tf_op jit(solution)/shard_map/ppermute | solution.py:457
  (41 other events, 369.5 us)
Sparse Core Ops, SparseCore 0:
  44.0 50.3 all-gather.1
  298.7 32.9 reduce-scatter.3
  334.0 77.1 reduce-scatter.7
  418.3 30.7 reduce-scatter.5

commit v4 on v3

--- a/solution.py
+++ b/solution.py
@@ -209,35 +209,51 @@
     )(x, a, b, bias, gain, shift)
 
 
-def mlp_kernel(tiles, place_ref, n_ref, dy_ref, *refs):
-    ups, downs, biases = refs[0:4], refs[4:8], refs[8:12]
-    g_ref, du_ref, mine_ref, theirs_ref, lift_ref, bsum_ref, low_acc, lift_acc = refs[12:]
+def mlp_kernel(plan, place_ref, n_ref, dy_ref, bias_ref, *refs):
+    n_arrays = 1 + max(index for index, _ in plan)
+    ups, downs = refs[:n_arrays], refs[n_arrays : 2 * n_arrays]
+    g_ref, du_ref, mine_ref, theirs_ref, lift_ref, bsum_ref = refs[2 * n_arrays : 2 * n_arrays + 6]
+    low_acc, lift_acc, up_buf, down_buf, sems = refs[2 * n_arrays + 6 :]
     j = pl.program_id(0)
+    tn = up_buf.shape[2]
+    slot = lax.rem(j, 2)
+
+    def copies(tile, at):
+        index, start = plan[tile]
+        cut = (slice(None), pl.ds(start, tn))
+        return (
+            pltpu.make_async_copy(ups[index].at[cut], up_buf.at[at], sems.at[0, at]),
+            pltpu.make_async_copy(downs[index].at[cut], down_buf.at[at], sems.at[1, at]),
+        )
 
     @pl.when(j == 0)
     def _():
+        for copy in copies(0, 0):
+            copy.start()
         low_acc[...] = jnp.zeros_like(low_acc)
         lift_acc[...] = jnp.zeros_like(lift_acc)
 
-    def step(up_ref, down_ref, bias_ref):
-        u = mm(n_ref[...], up_ref[...]) + bias_ref[...]
-        cdf = 0.5 * (1.0 + lax.erf(u * ROOT_HALF))
-        g = (u * cdf).astype(BF16)
-        slope = cdf + u * (jnp.exp(-0.5 * u * u) * DENSITY)
-        g_ref[...] = g
-        du = (mm(dy_ref[...], down_ref[...]) * slope).astype(BF16)
-        du_ref[...] = du
-        bsum_ref[...] = col_sum(du.astype(F32))
-        low_acc[...] += mm_nt(g, down_ref[...])
-        lift_acc[...] += mm_nt(du, up_ref[...])
-
-    for block in range(4):
-
-        @pl.when((j >= block * tiles) & (j < (block + 1) * tiles))
-        def _(block=block):
-            step(ups[block], downs[block], biases[block])
-
-    @pl.when(j == 4 * tiles - 1)
+    for tile in range(1, len(plan)):
+
+        @pl.when(j == tile - 1)
+        def _(tile=tile):
+            for copy in copies(tile, tile % 2):
+                copy.start()
+
+    for copy in copies(0, slot):
+        copy.wait()
+    u = mm(n_ref[...], up_buf[slot]) + bias_ref[...]
+    cdf = 0.5 * (1.0 + lax.erf(u * ROOT_HALF))
+    g = (u * cdf).astype(BF16)
+    slope = cdf + u * (jnp.exp(-0.5 * u * u) * DENSITY)
+    g_ref[...] = g
+    du = (mm(dy_ref[...], down_buf[slot]) * slope).astype(BF16)
+    du_ref[...] = du
+    bsum_ref[...] = col_sum(du.astype(F32))
+    low_acc[...] += mm_nt(g, down_buf[slot])
+    lift_acc[...] += mm_nt(du, up_buf[slot])
+
+    @pl.when(j == len(plan) - 1)
     def _():
         lift_ref[...] = lift_acc[...].astype(BF16)
         width = D // 4
@@ -251,37 +267,36 @@
             )
 
 
-def mlp(place, n2, dy, ups, downs, biases, half, tn=256):
+def mlp(place, n2, dy, bias, ups, downs, plan):
     rows = n2.shape[0]
-    tiles = half // tn
-    hid = 4 * half
+    hid = bias.shape[1]
+    tn = hid // len(plan)
     whole = held_once((rows, D))
-
-    def part(height, block, start):
-        return pl.BlockSpec(
-            (height, tn), lambda j, *_: (0, jnp.clip(j - block * tiles, 0, tiles - 1) + start // tn)
-        )
-
     tile = pl.BlockSpec((rows, tn), lambda j, *_: (0, j))
+    thin = pl.BlockSpec((1, tn), lambda j, *_: (0, j))
     return pl.pallas_call(
-        functools.partial(mlp_kernel, tiles),
+        functools.partial(mlp_kernel, plan),
         name="mlp",
         grid_spec=pltpu.PrefetchScalarGridSpec(
             num_scalar_prefetch=1,
-            grid=(4 * tiles,),
-            in_specs=[whole, whole]
-            + [part(D, block, item[1]) for block, item in enumerate(ups)]
-            + [part(D, block, item[1]) for block, item in enumerate(downs)]
-            + [part(1, block, 0) for block in range(4)],
+            grid=(len(plan),),
+            in_specs=[whole, whole, thin]
+            + [pl.BlockSpec(memory_space=pl.ANY)] * (len(ups) + len(downs)),
             out_specs=[
                 tile,
                 tile,
                 held_once((rows, D // 2)),
                 held_once((rows, D // 2)),
                 whole,
-                pl.BlockSpec((1, tn), lambda j, *_: (0, j)),
+                thin,
             ],
-            scratch_shapes=[pltpu.VMEM((rows, D), F32), pltpu.VMEM((rows, D), F32)],
+            scratch_shapes=[
+                pltpu.VMEM((rows, D), F32),
+                pltpu.VMEM((rows, D), F32),
+                pltpu.VMEM((2, D, tn), BF16),
+                pltpu.VMEM((2, D, tn), BF16),
+                pltpu.SemaphoreType.DMA((2, 2)),
+            ],
         ),
         out_shape=[
             like((rows, hid), BF16),
@@ -293,7 +308,7 @@
         ],
         compiler_params=params(1),
         cost_estimate=cost(8 * rows * D * hid, 24 * rows * D, 2 * rows * hid),
-    )(place, n2, dy, *[item[0] for item in ups], *[item[0] for item in downs], *biases)
+    )(place, n2, dy, bias, *ups, *downs)
 
 
 def finish_kernel(place_ref, h_ref, a_ref, b_ref, bias_ref, mine_ref, theirs_ref):
@@ -541,14 +556,20 @@
         attn_own = lax.dynamic_update_slice(attn_own, piece, (start, 0))
     attn_oth, attn_far = over(attn_own), across(attn_own)
     cut = 2 * heads_half
-    attn_far_oth = jnp.concatenate([over(attn_far[:, :cut]), across(attn_oth[:, cut:])], axis=1)
-
-    down_own = halves(down_weight, 0)[0].T
-    mlp_shard = jnp.concatenate([halves(up_weight, 1)[0], down_own], axis=1)
-    mlp_shard = after(mlp_shard, attn_own)
-    mlp_own = lax.all_gather(mlp_shard, "row", axis=0, tiled=True)
-    mlp_oth, mlp_far = over(mlp_own), across(mlp_own)
-    up_far_oth, down_far_oth = over(mlp_far[:, :half]), across(mlp_oth[:, half:])
+    attn_far_oth = jnp.concatenate(
+        [over(after(attn_far, wide_input)[:, :cut]), across(attn_oth[:, cut:])], axis=1
+    )
+
+    def spread(shard):
+        own = lax.all_gather(shard, "row", axis=0, tiled=True)
+        oth, far = over(own), across(own)
+        cut = half // 2
+        return own, far, oth, over(far[:, :cut]), across(oth[:, cut:])
+
+    up_shard = after(halves(up_weight, 1)[0], attn_own)
+    ups = spread(up_shard)
+    down_shard = after(halves(down_weight, 0)[0].T, attn_own)
+    downs = spread(down_shard)
     grad_here = after(cotangent, attn_far_oth)
     wide_grad = wide_tokens(grad_here, send_tokens(grad_here))
 
@@ -563,7 +584,15 @@
     qkv_bias = jnp.concatenate(
         [item for q, v in zip(query_parts, value_parts) for item in (q, zeros, v)]
     )[None]
-    up_biases = [item[None] for item in four(up_bias, small_far[8 * width :])]
+    near_own, far_own, near_oth, far_oth = (
+        item.reshape(2, half // 2) for item in four(up_bias, small_far[8 * width :])
+    )
+    tile_bias = jnp.concatenate(
+        [near_own[0], far_own[0], near_oth[0], far_oth[0]]
+        + [near_own[1], near_oth[1], far_own[1], far_oth[1]]
+    )[None]
+    quarter = half // 2
+    plan = ((0, 0), (1, 0), (2, 0), (3, 0), (0, quarter), (2, quarter), (1, quarter), (4, 0))
 
     wide_one, qkv, attn_weights = norm_qkv(
         wide_input, gain_one, shift_one, qkv_bias, (attn_own, attn_far, attn_oth, attn_far_oth)
@@ -577,10 +606,10 @@
         place,
         wide_two,
         wide_grad,
-        ((mlp_own, 0), (mlp_far, 0), (mlp_oth, 0), (up_far_oth, 0)),
-        ((mlp_own, half), (mlp_far, half), (mlp_oth, half), (down_far_oth, 0)),
-        up_biases,
-        half,
+        tile_bias,
+        ups,
+        downs,
+        plan,
     )
 
     def wide_add(mine, got):
@@ -595,57 +624,99 @@
     def scatter(value):
         return lax.psum_scatter(value, "row", scatter_dimension=0, tiled=True)
 
+    def tiles(value, first, last):
+        return value[:, quarter * first : quarter * last]
+
     lifted_other = beside(lifted_two)
     down_all = mm_tn(wide_grad, gate).astype(BF16)
     down_piece = scatter(down_all)
-    up_oth_got = over(mm_tn(wide_two, pre[:, 2 * half :]).astype(BF16))
+    up_over = mm_tn(wide_two, tiles(pre, 2, 4)).astype(BF16)
+    up_across = mm_tn(wide_two, tiles(pre, 6, 8)).astype(BF16)
+    up_over_got, up_across_got = over(up_over), across(up_across)
 
     middle_grad, attn_grad, head_grad, turn_sums = turn(
-        middle_sum, wide_grad, lifted_two, lifted_other, gain_two, attn_weights
+        middle_sum,
+        wide_grad,
+        lifted_two,
+        after(lifted_other, down_all, up_over, up_across),
+        gain_two,
+        attn_weights,
     )
     dqkv, qkv_sums = attend_back(qkv, probs, head_grad)
-
-    def feature_split(value):
-        return value.reshape(value.shape[0], n_xa, 2, width)
 
     def to_feature_blocks(mine, got, dtype):
         first, second = in_order(mine.astype(dtype), got.astype(dtype), my_x)
         both = jnp.concatenate([first, second]).reshape(images, PAD, width)
         return both[:, :SEQ].reshape(tokens_here, width)
 
-    out_mine, out_theirs = finish(place, middle_sum, low_mine, beside(low_theirs), down_bias_all)
-    outputs = to_feature_blocks(out_mine, across(out_theirs), BF16)
-
-    far_oth_got = over(mm_tn(wide_one, dqkv[:, 3 * three :]).astype(BF16))
-    near_oth_got = over(mm_tn(wide_one, dqkv[:, 2 * three : 3 * three]).astype(BF16))
-    lifted_one = mm_nt(dqkv, attn_weights[:, : 4 * three]).astype(BF16)
+    far_oth = mm_tn(wide_one, dqkv[:, 3 * three :]).astype(BF16)
+    near_oth = mm_tn(wide_one, dqkv[:, 2 * three : 3 * three]).astype(BF16)
+    far_oth_got, near_oth_got = over(far_oth), over(near_oth)
+    lifted_one = mm_nt(
+        after(dqkv, far_oth, near_oth), attn_weights[:, : 4 * three]
+    ).astype(BF16)
     lifted_one_other = beside(lifted_one)
+
+    up_over_got, up_across_got, _ = lax.optimization_barrier(
+        (up_over_got, up_across_got, lifted_one)
+    )
+    up_a = wide_add(mm_tn(wide_two, tiles(pre, 0, 2)), up_over_got)
+    up_b = wide_add(mm_tn(wide_two, tiles(pre, 4, 6)), up_across_got)
+    up_a_got, up_b_got = across(up_a[:, quarter:]), over(up_b[:, quarter:])
+
+    input_mine, input_theirs, last_sums = last(
+        place, wide_input, middle_grad, lifted_one, after(lifted_one_other, up_a, up_b), gain_one
+    )
+    far_oth_got = after(far_oth_got, input_mine)
     far_own = wide_add(mm_tn(wide_one, dqkv[:, three : 2 * three]), far_oth_got)
     far_own_got = across(far_own)
     near_own = wide_add(mm_tn(wide_one, dqkv[:, :three]), near_oth_got)
-    qkv_piece = same_half(scatter(wide_add(near_own, far_own_got)))
+
+    out_all = mm_tn(after(attn_grad, far_own), attended).astype(BF16)
+    out_got = over(out_all[:, 2 * heads_half :])
+    out_mine, out_theirs = finish(
+        place, middle_sum, after(low_mine, far_own), beside(low_theirs), down_bias_all
+    )
+    outputs = to_feature_blocks(out_mine, across(out_theirs), BF16)
+    out_own = wide_add(out_all[:, : 2 * heads_half], out_got)
+    out_far_got = across(out_own[:, heads_half:])
+
+    near_sum = wide_add(near_own, after(far_own_got, out_mine))
+    strip = D // n_row
+
+    def rows_of(value, shift):
+        return lax.dynamic_slice_in_dim(value, (my_row + shift) % n_row * strip, strip, 0)
+
+    qkv_total = rows_of(near_sum, 0).astype(F32)
+    for shift in range(1, n_row):
+        got = lax.ppermute(
+            rows_of(near_sum, shift), "row", [(at, (at + shift) % n_row) for at in range(n_row)]
+        )
+        qkv_total = qkv_total + got.astype(F32)
+    qkv_piece = same_half(qkv_total.astype(BF16))
     qkv_other = over(qkv_piece)
 
-    input_mine, input_theirs, last_sums = last(
-        place, wide_input, middle_grad, lifted_one, lifted_one_other, gain_one
-    )
+    input_theirs = after(input_theirs, far_own_got)
     input_grad = to_feature_blocks(input_mine, across(input_theirs), F32)
 
-    out_all = mm_tn(attn_grad, attended).astype(BF16)
-    out_got = over(out_all[:, 2 * heads_half :])
-    out_own = wide_add(out_all[:, : 2 * heads_half], out_got)
-    up_own = wide_add(mm_tn(wide_two, pre[:, : 2 * half]), up_oth_got)
-    far_part = jnp.concatenate([up_own[:, half:], out_own[:, heads_half:]], axis=1)
-    near_part = jnp.concatenate([up_own[:, :half], out_own[:, :heads_half]], axis=1)
-    up_piece = same_half(scatter(wide_add(near_part, across(far_part))))
+    up_piece = same_half(
+        scatter(
+            jnp.concatenate(
+                [
+                    wide_add(up_a[:, :quarter], up_a_got),
+                    wide_add(up_b[:, :quarter], up_b_got),
+                    wide_add(out_own[:, :heads_half], out_far_got),
+                ],
+                axis=1,
+            )
+        )
+    )
     up_other = over(up_piece)
 
-    down_x = wide_add(
-        jnp.concatenate([down_piece[:, :half], down_piece[:, 2 * half : 3 * half]], axis=1),
-        across(
-            jnp.concatenate([down_piece[:, half : 2 * half], down_piece[:, 3 * half :]], axis=1)
-        ),
-    )
+    def some(value, *which):
+        return jnp.concatenate([tiles(value, at, at + 1) for at in which], axis=1)
+
+    down_x = wide_add(some(down_piece, 0, 4, 2, 5), across(some(down_piece, 1, 6, 3, 7)))
     down_got = over(down_x)
     down_total = down_x.astype(F32) + jnp.concatenate(
         [down_got[:, half:], down_got[:, :half]], axis=1
@@ -690,6 +761,11 @@
 
     turn_own = own_features(turn_sums)
     qkv_parts = qkv_sums.reshape(4, 3, heads_half)
+    up_tiles = up_sums.reshape(8, quarter)
+    up_parts = [
+        jnp.concatenate([up_tiles[first], up_tiles[second]])
+        for first, second in ((0, 4), (1, 6), (2, 5), (3, 7))
+    ]
     early = everywhere(
         jnp.concatenate(
             [
@@ -699,7 +775,7 @@
                 turn_own[3],
                 turn_own[0],
                 turn_own[1],
-                by_x(up_sums.reshape(4, half)),
+                by_x(up_parts),
             ],
             axis=1,
         )

time: 483 us -> 470 us (0.973)
  waiting for transfers between devices: 163 us -> 114 us
  local copies, waits for them, and re-layouts: 46.5 us -> 81.8 us
  starting transfers between devices: 57.2 us -> 50.2 us
    ppermute x38 -> x45, waiting for transfers between devices: 149 us -> 90.8 us  [swap(): return lax.ppermute(value, axis, [(at, at ^ bit) for at in range(size)])]
    unnamed x122 -> x125, local copies, waits for them, and re-layouts: 8.9 us -> 40.2 us
    all_gather x1 -> x2, waiting for transfers between devices: 0.02 us -> 15.4 us  [spread(): own = lax.all_gather(shard, 'row', axis=0, tiled=True)]
    ppermute x38 -> x45, starting transfers between devices: 48.6 us -> 37.5 us  [swap(): return lax.ppermute(value, axis, [(at, at ^ bit) for at in range(size)])]
    ppermute x3, waiting for transfers between devices: 6.63 us -> 0.01 us  [local(): lax.ppermute(attn_shard, 'row', [(at, (at + shift) % n_row) for at in ran...]
    dot_general x8 -> x10, matrix products: 34.4 us -> 39.3 us  [mm_tn(): lax.dot_general(a, b, (((0,), (0,)), ((), ())), preferred_element_type=F32)]
    slice x8 -> x14, local copies, waits for them, and re-layouts: 7.06 us -> 11.4 us  [the longest x4 5.89 us: spread(): return (own, far, oth, over(far[:, :cut]), across(oth[:, cut:]))]
  transfers between devices with their start and end apart: 45 -> 55, of which waited for: 23 -> 18; matrix products, arithmetic and copies ran while one was open for 20% -> 32% of each run, Pallas kernels for 11% -> 20%
where the time goes in v4:
time: 470 us; the launch traced here: 461 us
  Pallas kernels  126 us (27%)
  waiting for transfers between devices  114 us (24%)
  local copies, waits for them, and re-layouts  81.8 us (17%)
  starting transfers between devices  50.2 us (11%)
  matrix products  47.6 us (10%)
  other arithmetic  26 us (6%)
  between operations  15.1 us (3%)
    ppermute x45, waiting for transfers between devices, swap(): return lax.ppermute(value, axis, [(at, at ^ bit) for at in range(size)])  90.8 us
    unnamed x125, local copies, waits for them, and re-layouts  40.2 us
    dot_general x10, matrix products, mm_tn(): lax.dot_general(a, b, (((0,), (0,)), ((), ())), preferred_element_type=F32)  39.3 us
    ppermute x45, starting transfers between devices, swap(): return lax.ppermute(value, axis, [(at, at ^ bit) for at in range(size)])  37.5 us
    pallas_call x1, Pallas kernels, mlp(): pl.pallas_call(functools.partial(mlp_kernel, plan), name='mlp', grid_spec...  34 us
    pallas_call x1, Pallas kernels, attend_back(): pl.pallas_call(attend_back_kernel, grid=(pairs, held), name='attend_back'...  26.8 us
    pallas_call x1, Pallas kernels, attend(): pl.pallas_call(attend_kernel, grid=(pairs, held), name='attend', in_specs...  20.1 us
    all_gather x2, waiting for transfers between devices, spread(): own = lax.all_gather(shard, 'row', axis=0, tiled=True)  15.4 us
  transfers between devices with their start and end apart: 55, of which 18 were waited for; matrix products, arithmetic and copies ran while one was open for 32% of the time, Pallas kernels for 20%

profile of v4, /device:TPU:0, one launch (start us, length us, event | category | flops | bytes accessed | tf_op | source)
XLA Modules:
  0.0 461.5 jit_solution(10194438280748467932)
XLA Ops:
  12.7 4.1 collective-permute-start.5
  18.3 2.2 collective-permute-start.6
  67.9 1.7 pad_maximum_fusion.1
  69.6 2.2 reshape.793
  73.4 17.3 %collective-permute-done.7.b_ref = bf16[1024,512]{1,0:T(8,128)(2,1)} collective-permute-done((bf16[1024,512]{1,0:T(8,128)(2,1)}, bf16[1024,512]{1,0:T(8,128)(2,1)}, u32[]{:S(2)}, u32[]{:S(2)}) %collective-permute-start.7) | collective-permute-done | bytes 1048608 | tf_op jit(solution)/shard_map/ppermute | solution.py:472
  98.4 15.4 %all-gather.3.cloned.1.call-done.refs_0_ = bf16[1024,512]{1,0:T(8,128)(2,1)} async-done(((bf16[256,512]{1,0:T(8,128)(2,1)}), bf16[1024,512]{1,0:T(8,128)(2,1)}) %all-gather.3.cloned.1.call-update) | async-done | bytes 1048592 | tf_op jit(solution)/shard_map/all_gather | solution.py:564
  119.3 10.3 %norm_qkv.1 = (bf16[1184,1024]{1,0:T(8,128)(2,1)}, bf16[1184,1536]{1,0:T(8,128)(2,1)}, bf16[1024,2048]{1,0:T(8,128)(2,1)}) custom-call(bf16[1184,1024]{1,0:T(8,128)(2,1)} %bitcast.175, f32[1,1024]{1,0:T(1,128)} %bitcast.200, f32[1,1024]{1,0:T(1,128)} %bitcast.226, f32[1,1536]{1,0:T(1,128)} %broadcast_in_dim.33.bias_ref, bf16[1024,512]{1,0:T(8,128)(2,1)} %copy-done.10, ...), custom_call_target="tpu_custom_call" | custom-call | flops 3724541952 | bytes 19398656 | tf_op jit(solution)/shard_map/norm_qkv/pallas_call | solution.py:108
  129.6 20.1 %attend.1 = (bf16[1184,512]{1,0:T(8,128)(2,1)}, bf16[2,8,592,592]{3,2,1,0:T(8,128)(2,1)}) custom-call(bf16[1184,1536]{1,0:T(8,128)(2,1)} %get-tuple-element.56.qkv_ref), custom_call_target="tpu_custom_call" | custom-call | flops 17226006528 | bytes 48496640 | tf_op jit(solution)/shard_map/attend/pallas_call | solution.py:138
  149.8 13.9 %collective-permute-done.12 = bf16[1154,256]{1,0:T(8,128)(2,1)S(1)} collective-permute-done((bf16[1154,256]{1,0:T(8,128)(2,1)S(1)}, bf16[1154,256]{1,0:T(8,128)(2,1)S(1)}, u32[]{:S(2)}, u32[]{:S(2)}) %collective-permute-start.12) | collective-permute-done | bytes 590880 | tf_op jit(solution)/shard_map/ppermute | solution.py:472
  163.9 4.1 convolution_convert_fusion.a_ref
  181.9 1.9 slice.598
  184.3 1.9 slice.597
  187.4 1.8 pad_maximum_fusion.2
  189.1 2.1 reshape.801
  193.0 6.7 %middle.1 = (f32[1184,1024]{1,0:T(8,128)}, bf16[1184,1024]{1,0:T(8,128)(2,1)}) custom-call(bf16[1184,1024]{1,0:T(8,128)(2,1)} %bitcast.176, bf16[1184,1024]{1,0:T(8,128)(2,1)} %convolution_convert_fusion.a_ref, bf16[1184,1024]{1,0:T(8,128)(2,1)} %collective-permute-done.11.b_ref, f32[1,1024]{1,0:T(1,128)} %bitcast.204, f32[1,1024]{1,0:T(1,128)} %bitcast.193, ...), custom_call_target="tpu_custom_call" | custom-call | flops 24248320 | bytes 14548992 | tf_op jit(solution)/shard_map/middle/pallas_call | solution.py:200
  199.7 3.3 collective-permute-done.17.refs_4_
  203.0 2.4 collective-permute-done.16.refs_3_
  205.3 34.0 %mlp.1 = (bf16[1184,2048]{1,0:T(8,128)(2,1)}, bf16[1184,2048]{1,0:T(8,128)(2,1)}, f32[1184,512]{1,0:T(8,128)}, bf16[1184,512]{1,0:T(8,128)(2,1)}, bf16[1184,1024]{1,0:T(8,128)(2,1)}, /*index=5*/f32[1,2048]{1,0:T(1,128)}) custom-call(s32[2]{0:T(128)} %pad_add_fusion.place_ref, bf16[1184,1024]{1,0:T(8,128)(2,1)} %get-tuple-element.60.n_ref, ...), custom_call_target="tpu_custom_call" | custom-call | flops 19864223744 | bytes 29097984 | tf_op jit(solution)/shard_map/mlp/pallas_call | solution.py:277
  239.4 4.7 %convolution_convert_fusion.5 = bf16[1024,512]{1,0:T(8,128)(2,1)} fusion(bf16[1184,1024]{1,0:T(8,128)(2,1)} %get-tuple-element.60.n_ref, bf16[1184,2048]{1,0:T(8,128)(2,1)} %get-tuple-element.69), kind=kOutput, calls=%fused_computation.16 | convolution fusion | flops 1242038272 | bytes 4685824 | tf_op jit(solution)/shard_map/dot_general | solution.py:33
  245.6 4.4 convolution_convert_fusion.4
  250.5 7.3 %convolution_convert_fusion.2 = bf16[1024,2048]{1,0:T(8,128)(2,1)} fusion(bf16[1184,1024]{1,0:T(8,128)(2,1)S(1)} %bitcast.180, bf16[1184,2048]{1,0:T(8,128)(2,1)S(1)} %copy-done.39), kind=kOutput, calls=%fused_computation.2 | convolution fusion | flops 4968153088 | bytes 11468800 | tf_op jit(solution)/shard_map/dot_general | solution.py:33
  260.0 11.8 %turn.1 = (f32[1184,1024]{1,0:T(8,128)}, bf16[1184,1024]{1,0:T(8,128)(2,1)}, bf16[1184,512]{1,0:T(8,128)(2,1)}, f32[4,1024]{1,0:T(4,128)}) custom-call(f32[1184,1024]{1,0:T(8,128)} %get-tuple-element.59.h_ref, bf16[1184,1024]{1,0:T(8,128)(2,1)} %bitcast.179, bf16[1184,1024]{1,0:T(8,128)(2,1)} %get-tuple-element.67.a_ref, bf16[1184,1024]{1,0:T(8,128)(2,1)} %copy-done.5, ...), custom_call_target="tpu_custom_call" | custom-call | flops 1241513984 | bytes 21823488 | tf_op jit(solution)/shard_map/turn/pallas_call | solution.py:379
  271.9 26.8 %attend_back.1 = (bf16[1184,1536]{1,0:T(8,128)(2,1)}, f32[1,1536]{1,0:T(1,128)}) custom-call(bf16[1184,1536]{1,0:T(8,128)(2,1)} %get-tuple-element.56.qkv_ref, bf16[2,8,592,592]{3,2,1,0:T(8,128)(2,1)} %get-tuple-element.66.p_ref, bf16[1184,512]{1,0:T(8,128)(2,1)} %get-tuple-element.71.g_ref), custom_call_target="tpu_custom_call" | custom-call | flops 21532508160 | bytes 60620800 | tf_op jit(solution)/shard_map/attend_back/pallas_call | solution.py:174
  299.4 3.8 convolution_convert_fusion.6
  303.2 2.5 convolution_convert_fusion.7
  305.7 4.2 convolution_convert_fusion.1.a_ref
  311.7 2.3 collective-permute-done.36
  314.8 5.4 %collective-permute-done.37 = f32[2,2560]{1,0:T(2,128)S(1)} collective-permute-done((f32[2,2560]{1,0:T(2,128)S(1)}, f32[2,2560]{1,0:T(2,128)S(1)}, u32[]{:S(2)}, u32[]{:S(2)}) %collective-permute-start.37) | collective-permute-done | bytes 20512 | tf_op jit(solution)/shard_map/ppermute | solution.py:472
  320.3 4.1 add_convert_fusion.1
  324.4 2.0 collective-permute-done.38
  326.5 3.2 add_convert_fusion
  332.2 3.1 collective-permute-done.39
  336.9 7.8 %collective-permute-done.40 = bf16[1024,256]{1,0:T(8,128)(2,1)S(1)} collective-permute-done((bf16[1024,256]{1,0:T(8,128)(2,1)S(1)}, bf16[1024,256]{1,0:T(8,128)(2,1)S(1)}, u32[]{:S(2)}, u32[]{:S(2)}) %collective-permute-start.40) | collective-permute-done | bytes 524320 | tf_op jit(solution)/shard_map/ppermute | solution.py:472
  346.5 9.4 %last.1 = (f32[1184,256]{1,0:T(8,128)}, bf16[1184,256]{1,0:T(8,128)(2,1)}, f32[2,1024]{1,0:T(2,128)}) custom-call(s32[2]{0:T(128)} %pad_add_fusion.place_ref, bf16[1184,1024]{1,0:T(8,128)(2,1)} %bitcast.177, f32[1184,1024]{1,0:T(8,128)} %get-tuple-element.73.dh_ref, bf16[1184,1024]{1,0:T(8,128)(2,1)} %copy-done.4, ...), custom_call_target="tpu_custom_call" | custom-call | flops 24248320 | bytes 14548992 | tf_op jit(solution)/shard_map/last/pallas_call | solution.py:420
  358.4 2.0 collective-permute-done.47
  360.5 4.7 %add_convert_fusion.4 = bf16[1024,384]{1,0:T(8,128)(2,1)} fusion(bf16[1024,384]{1,0:T(8,128)(2,1)} %collective-permute-done.23, bf16[1184,1024]{1,0:T(8,128)(2,1)} %get-tuple-element.65, bf16[1184,1536]{1,0:T(8,128)(2,1)} %get-tuple-element.74), kind=kOutput, calls=%fused_computation.11 | convolution fusion | flops 932315136 | bytes 4907008 | tf_op jit(solution)/shard_map/dot_general | solution.py:33
  371.7 3.0 add_convert_fusion.3
  374.7 7.1 %finish.1 = (bf16[1184,256]{1,0:T(8,128)(2,1)}, bf16[1184,256]{1,0:T(8,128)(2,1)}) custom-call(s32[2]{0:T(128)} %pad_add_fusion.place_ref, f32[1184,1024]{1,0:T(8,128)} %get-tuple-element.59.h_ref, f32[1184,512]{1,0:T(8,128)} %get-tuple-element.80.a_ref, bf16[1184,512]{1,0:T(8,128)(2,1)} %collective-permute-done.27.b_ref, f32[1,1024]{1,0:T(1,128)} %bitcast.202), custom_call_target="tpu_custom_call" | custom-call | flops 2424832 | bytes 7274496 | tf_op jit(solution)/shard_map/finish/pallas_call | solution.py:335
  386.0 1.9 collective-permute-start.32
  388.0 2.0 collective-permute-start.34
  390.7 10.8 %collective-permute-done.43 = bf16[1024,128]{1,0:T(8,128)(2,1)S(1)} collective-permute-done((bf16[1024,128]{1,0:T(8,128)(2,1)S(1)}, bf16[1024,128]{1,0:T(8,128)(2,1)S(1)}, u32[]{:S(2)}, u32[]{:S(2)}) %collective-permute-start.43) | collective-permute-done | bytes 262176 | tf_op jit(solution)/shard_map/ppermute | solution.py:472
  407.6 2.1 collective-permute-done.35
  412.0 2.1 fusion.32
  416.4 6.5 %collective-permute-done.30 = bf16[1184,256]{1,0:T(8,128)(2,1)S(1)} collective-permute-done((bf16[1184,256]{1,0:T(8,128)(2,1)S(1)}, bf16[1184,256]{1,0:T(8,128)(2,1)S(1)}, u32[]{:S(2)}, u32[]{:S(2)}) %collective-permute-start.30) | collective-permute-done | bytes 606240 | tf_op jit(solution)/shard_map/ppermute | solution.py:472
  424.3 8.1 %reduce-scatter.3.cloned.1.call-done = bf16[256,640]{1,0:T(8,128)(2,1)} async-done(((bf16[1024,640]{1,0:T(8,128)(2,1)}), bf16[256,640]{1,0:T(8,128)(2,1)}) %reduce-scatter.3.cloned.1.call-update) | async-done | bytes 327696 | tf_op jit(solution)/shard_map/reduce_scatter | solution.py:625
  434.4 1.8 reshape.809
  438.8 4.6 %collective-permute-done.44 = bf16[256,640]{1,0:T(8,128)(2,1)} collective-permute-done((bf16[256,640]{1,0:T(8,128)(2,1)}, bf16[256,640]{1,0:T(8,128)(2,1)}, u32[]{:S(2)}, u32[]{:S(2)}) %collective-permute-start.44) | collective-permute-done | bytes 327712 | tf_op jit(solution)/shard_map/ppermute | solution.py:472
  447.2 5.8 %collective-permute-done.46 = bf16[256,1024]{1,0:T(8,128)(2,1)S(1)} collective-permute-done((bf16[256,1024]{1,0:T(8,128)(2,1)S(1)}, bf16[256,1024]{1,0:T(8,128)(2,1)S(1)}, u32[]{:S(2)}, u32[]{:S(2)}) %collective-permute-start.46) | collective-permute-done | bytes 524320 | tf_op jit(solution)/shard_map/ppermute | solution.py:472
  (336 shorter events, 135.5 us)
Async XLA Ops:
  7.3 89.0 %all-gather.5.cloned.1.call-start = ((), (), s32[]{:S(2)}) async-start(), calls=%async_computation.3 | async-start | bytes 1310720 | tf_op jit(solution)/shard_map/all_gather | solution.py:564
  12.7 43.1 %collective-permute-start.5 = (bf16[256,512]{1,0:T(8,128)(2,1)}, bf16[256,512]{1,0:T(8,128)(2,1)}, u32[]{:S(2)}, u32[]{:S(2)}) collective-permute-start(bf16[256,512]{1,0:T(8,128)(2,1)} %get-tuple-element.172), channel_id=1, source_target_pairs={{0,8},{4,12},{8,0},{12,4},{1,9},{5,13},{9,1},{13,5},{2,10},{6,14},... | collective-permute-start | bytes 786440 | tf_op jit(solution)/shard_map/ppermute | solution.py:503
  16.7 38.0 %collective-permute-start.4 = (bf16[256,512]{1,0:T(8,128)(2,1)}, bf16[256,512]{1,0:T(8,128)(2,1)}, u32[]{:S(2)}, u32[]{:S(2)}) collective-permute-start(bf16[256,512]{1,0:T(8,128)(2,1)} %get-tuple-element.172), channel_id=1, source_target_pairs={{0,4},{4,8},{8,12},{12,0},{1,5},{5,9},{9,13},{13,1},{2,6},{6,10},{... | collective-permute-start | bytes 786440 | tf_op jit(solution)/shard_map/ppermute | solution.py:503
  18.3 38.4 %collective-permute-start.6 = (bf16[256,512]{1,0:T(8,128)(2,1)}, bf16[256,512]{1,0:T(8,128)(2,1)}, u32[]{:S(2)}, u32[]{:S(2)}) collective-permute-start(bf16[256,512]{1,0:T(8,128)(2,1)} %get-tuple-element.172), channel_id=1, source_target_pairs={{0,12},{4,0},{8,4},{12,8},{1,13},{5,1},{9,5},{13,9},{2,14},{6,2},{... | collective-permute-start | bytes 786440 | tf_op jit(solution)/shard_map/ppermute | solution.py:503
  31.6 13.2 %collective-permute-start.2 = (f32[3072]{0:T(1024)}, f32[3072]{0:T(1024)}, u32[]{:S(2)}, u32[]{:S(2)}) collective-permute-start(f32[3072]{0:T(1024)} %constant_dynamic-update-slice_fusion.35), channel_id=1, source_target_pairs={{0,2},{2,0},{1,3},{3,1},{4,6},{6,4},{5,7},{7,5},{8,10},{10,8},{9,1... | collective-permute-start | bytes 36872 | tf_op jit(solution)/shard_map/ppermute | solution.py:472
  34.2 25.0 %collective-permute-start = (bf16[1154,256]{1,0:T(8,128)(2,1)}, bf16[1154,256]{1,0:T(8,128)(2,1)S(1)}, u32[]{:S(2)}, u32[]{:S(2)}) collective-permute-start(bf16[1154,256]{1,0:T(8,128)(2,1)} %get-tuple-element.146), channel_id=1, source_target_pairs={{0,2},{2,0},{1,3},{3,1},{4,6},{6,4},{5,7},{7,5},{8,10},{10,8},{9,1... | collective-permute-start | bytes 1772552 | tf_op jit(solution)/shard_map/ppermute | solution.py:472
  54.7 9.3 %collective-permute-start.3 = (f32[2,3072]{1,0:T(2,128)S(1)}, f32[2,3072]{1,0:T(2,128)S(1)}, u32[]{:S(2)}, u32[]{:S(2)}) collective-permute-start(f32[2,3072]{1,0:T(2,128)S(1)} %pad_maximum_fusion.9), channel_id=1, source_target_pairs={{0,1},{1,0},{2,3},{3,2},{4,5},{5,4},{6,7},{7,6},{8,9},{9,8},{10,11... | collective-permute-start | bytes 73736 | tf_op jit(solution)/shard_map/ppermute | solution.py:472
  57.7 56.0 %all-gather.3.cloned.1.call-start = ((), (), s32[]{:S(2)}) async-start(), calls=%async_computation.2 | async-start | bytes 1310720 | tf_op jit(solution)/shard_map/all_gather | solution.py:564
  60.2 7.0 %collective-permute-start.1 = (bf16[1154,512]{1,0:T(8,128)(2,1)}, bf16[1154,512]{1,0:T(8,128)(2,1)S(1)}, u32[]{:S(2)}, u32[]{:S(2)}) collective-permute-start(bf16[1154,512]{1,0:T(8,128)(2,1)} %pad_maximum_fusion.5), channel_id=1, source_target_pairs={{0,1},{1,0},{2,3},{3,2},{4,5},{5,4},{6,7},{7,6},{8,9},{9,8},{10,11... | collective-permute-start | bytes 3545096 | tf_op jit(solution)/shard_map/ppermute | solution.py:472
  64.1 28.4 %collective-permute-start.8 = (bf16[1024,512]{1,0:T(8,128)(2,1)}, bf16[1024,512]{1,0:T(8,128)(2,1)}, u32[]{:S(2)}, u32[]{:S(2)}) collective-permute-start(bf16[1024,512]{1,0:T(8,128)(2,1)} %copy-done.10), channel_id=1, source_target_pairs={{0,16},{16,0},{1,17},{17,1},{2,18},{18,2},{3,19},{19,3},{4,20},{20... | collective-permute-start | bytes 3145736 | tf_op jit(solution)/shard_map/ppermute | solution.py:472
  65.7 25.1 %collective-permute-start.7 = (bf16[1024,512]{1,0:T(8,128)(2,1)}, bf16[1024,512]{1,0:T(8,128)(2,1)}, u32[]{:S(2)}, u32[]{:S(2)}) collective-permute-start(bf16[1024,512]{1,0:T(8,128)(2,1)} %copy-done.10), channel_id=1, source_target_pairs={{0,2},{2,0},{1,3},{3,1},{4,6},{6,4},{5,7},{7,5},{8,10},{10,8},{9,1... | collective-permute-start | bytes 3145736 | tf_op jit(solution)/shard_map/ppermute | solution.py:472
  67.2 344.8 %reduce-scatter.5.cloned.1.call-start = ((), (), s32[]{:S(2)}) async-start(), calls=%async_computation.5 | async-start | bytes 5242880 | tf_op jit(solution)/shard_map/reduce_scatter | solution.py:625
  91.9 23.4 %collective-permute-start.9 = (bf16[1024,256]{1,0:T(8,128)(2,1)S(1)}, bf16[1024,256]{1,0:T(8,128)(2,1)S(1)}, u32[]{:S(2)}, u32[]{:S(2)}) collective-permute-start(bf16[1024,256]{1,0:T(8,128)(2,1)S(1)} %slice.455), channel_id=1, source_target_pairs={{0,16},{16,0},{1,17},{17,1},{2,18},{18,2},{3,19},{19,3},{4,20},{20... | collective-permute-start | bytes 1572872 | tf_op jit(solution)/shard_map/ppermute | solution.py:472
  93.6 24.0 %collective-permute-start.10 = (bf16[1024,256]{1,0:T(8,128)(2,1)S(1)}, bf16[1024,256]{1,0:T(8,128)(2,1)S(1)}, u32[]{:S(2)}, u32[]{:S(2)}) collective-permute-start(bf16[1024,256]{1,0:T(8,128)(2,1)S(1)} %slice.579), channel_id=1, source_target_pairs={{0,2},{2,0},{1,3},{3,1},{4,6},{6,4},{5,7},{7,5},{8,10},{10,8},{9,1... | collective-permute-start | bytes 1572872 | tf_op jit(solution)/shard_map/ppermute | solution.py:472
  96.3 71.7 %collective-permute-start.19 = (bf16[1024,512]{1,0:T(8,128)(2,1)}, bf16[1024,512]{1,0:T(8,128)(2,1)}, u32[]{:S(2)}, u32[]{:S(2)}) collective-permute-start(bf16[1024,512]{1,0:T(8,128)(2,1)} %all-gather.5.cloned.1.call-done.refs_5_), channel_id=1, source_target_pairs={{0,16},{16,0},{1,17},{17,1},{2,18},{18,2},{3,19},{19,3},{4,20},{20... | collective-permute-start | bytes 3145736 | tf_op jit(solution)/shard_map/ppermute | solution.py:472
  97.8 79.9 %collective-permute-start.18 = (bf16[1024,512]{1,0:T(8,128)(2,1)}, bf16[1024,512]{1,0:T(8,128)(2,1)}, u32[]{:S(2)}, u32[]{:S(2)}) collective-permute-start(bf16[1024,512]{1,0:T(8,128)(2,1)} %all-gather.5.cloned.1.call-done.refs_5_), channel_id=1, source_target_pairs={{0,2},{2,0},{1,3},{3,1},{4,6},{6,4},{5,7},{7,5},{8,10},{10,8},{9,1... | collective-permute-start | bytes 3145736 | tf_op jit(solution)/shard_map/ppermute | solution.py:472
  113.8 66.6 %collective-permute-start.15 = (bf16[1024,512]{1,0:T(8,128)(2,1)}, bf16[1024,512]{1,0:T(8,128)(2,1)}, u32[]{:S(2)}, u32[]{:S(2)}) collective-permute-start(bf16[1024,512]{1,0:T(8,128)(2,1)} %all-gather.3.cloned.1.call-done.refs_0_), channel_id=1, source_target_pairs={{0,16},{16,0},{1,17},{17,1},{2,18},{18,2},{3,19},{19,3},{4,20},{20... | collective-permute-start | bytes 3145736 | tf_op jit(solution)/shard_map/ppermute | solution.py:472
  115.2 68.6 %collective-permute-start.14 = (bf16[1024,512]{1,0:T(8,128)(2,1)}, bf16[1024,512]{1,0:T(8,128)(2,1)}, u32[]{:S(2)}, u32[]{:S(2)}) collective-permute-start(bf16[1024,512]{1,0:T(8,128)(2,1)} %all-gather.3.cloned.1.call-done.refs_0_), channel_id=1, source_target_pairs={{0,2},{2,0},{1,3},{3,1},{4,6},{6,4},{5,7},{7,5},{8,10},{10,8},{9,1... | collective-permute-start | bytes 3145736 | tf_op jit(solution)/shard_map/ppermute | solution.py:472
  118.7 45.0 %collective-permute-start.12 = (bf16[1154,256]{1,0:T(8,128)(2,1)S(1)}, bf16[1154,256]{1,0:T(8,128)(2,1)S(1)}, u32[]{:S(2)}, u32[]{:S(2)}) collective-permute-start(bf16[1154,256]{1,0:T(8,128)(2,1)S(1)} %get-tuple-element.144), channel_id=1, source_target_pairs={{0,2},{2,0},{1,3},{3,1},{4,6},{6,4},{5,7},{7,5},{8,10},{10,8},{9,1... | collective-permute-start | bytes 1772552 | tf_op jit(solution)/shard_map/ppermute | solution.py:472
  163.8 22.4 %collective-permute-start.13 = (bf16[1154,512]{1,0:T(8,128)(2,1)S(1)}, bf16[1154,512]{1,0:T(8,128)(2,1)S(1)}, u32[]{:S(2)}, u32[]{:S(2)}) collective-permute-start(bf16[1154,512]{1,0:T(8,128)(2,1)S(1)} %pad_maximum_fusion.6), channel_id=1, source_target_pairs={{0,1},{1,0},{2,3},{3,2},{4,5},{5,4},{6,7},{7,6},{8,9},{9,8},{10,11... | collective-permute-start | bytes 3545096 | tf_op jit(solution)/shard_map/ppermute | solution.py:472
  168.0 25.0 %collective-permute-start.11 = (bf16[1184,1024]{1,0:T(8,128)(2,1)}, bf16[1184,1024]{1,0:T(8,128)(2,1)}, u32[]{:S(2)}, u32[]{:S(2)}) collective-permute-start(bf16[1184,1024]{1,0:T(8,128)(2,1)} %convolution_convert_fusion.a_ref), channel_id=1, source_target_pairs={{0,1},{1,0},{2,3},{3,2},{4,5},{5,4},{6,7},{7,6},{8,9},{9,8},{10,11... | collective-permute-start | bytes 7274504 | tf_op jit(solution)/shard_map/ppermute | solution.py:472
  177.7 22.0 %collective-permute-start.21 = (bf16[1024,256]{1,0:T(8,128)(2,1)S(1)}, bf16[1024,256]{1,0:T(8,128)(2,1)}, u32[]{:S(2)}, u32[]{:S(2)}) collective-permute-start(bf16[1024,256]{1,0:T(8,128)(2,1)S(1)} %slice.600), channel_id=1, source_target_pairs={{0,2},{2,0},{1,3},{3,1},{4,6},{6,4},{5,7},{7,5},{8,10},{10,8},{9,1... | collective-permute-start | bytes 1572872 | tf_op jit(solution)/shard_map/ppermute | solution.py:472
  180.4 19.3 %collective-permute-start.20 = (bf16[1024,256]{1,0:T(8,128)(2,1)S(1)}, bf16[1024,256]{1,0:T(8,128)(2,1)}, u32[]{:S(2)}, u32[]{:S(2)}) collective-permute-start(bf16[1024,256]{1,0:T(8,128)(2,1)S(1)} %slice.599), channel_id=1, source_target_pairs={{0,16},{16,0},{1,17},{17,1},{2,18},{18,2},{3,19},{19,3},{4,20},{20... | collective-permute-start | bytes 1572872 | tf_op jit(solution)/shard_map/ppermute | solution.py:472
  183.8 19.2 %collective-permute-start.17 = (bf16[1024,256]{1,0:T(8,128)(2,1)}, bf16[1024,256]{1,0:T(8,128)(2,1)}, u32[]{:S(2)}, u32[]{:S(2)}) collective-permute-start(bf16[1024,256]{1,0:T(8,128)(2,1)} %slice.598), channel_id=1, source_target_pairs={{0,2},{2,0},{1,3},{3,1},{4,6},{6,4},{5,7},{7,5},{8,10},{10,8},{9,1... | collective-permute-start | bytes 1572872 | tf_op jit(solution)/shard_map/ppermute | solution.py:472
  186.2 19.1 %collective-permute-start.16 = (bf16[1024,256]{1,0:T(8,128)(2,1)}, bf16[1024,256]{1,0:T(8,128)(2,1)}, u32[]{:S(2)}, u32[]{:S(2)}) collective-permute-start(bf16[1024,256]{1,0:T(8,128)(2,1)} %slice.597), channel_id=1, source_target_pairs={{0,16},{16,0},{1,17},{17,1},{2,18},{18,2},{3,19},{19,3},{4,20},{20... | collective-permute-start | bytes 1572872 | tf_op jit(solution)/shard_map/ppermute | solution.py:472
  239.3 19.3 %collective-permute-start.22 = (bf16[1184,1024]{1,0:T(8,128)(2,1)}, bf16[1184,1024]{1,0:T(8,128)(2,1)S(1)}, u32[]{:S(2)}, u32[]{:S(2)}) collective-permute-start(bf16[1184,1024]{1,0:T(8,128)(2,1)} %get-tuple-element.67.a_ref), channel_id=1, source_target_pairs={{0,1},{1,0},{2,3},{3,2},{4,5},{5,4},{6,7},{7,6},{8,9},{9,8},{10,11... | collective-permute-start | bytes 7274504 | tf_op jit(solution)/shard_map/ppermute | solution.py:472
  244.1 70.7 %collective-permute-start.25 = (bf16[1024,512]{1,0:T(8,128)(2,1)}, bf16[1024,512]{1,0:T(8,128)(2,1)}, u32[]{:S(2)}, u32[]{:S(2)}) collective-permute-start(bf16[1024,512]{1,0:T(8,128)(2,1)} %convolution_convert_fusion.5), channel_id=1, source_target_pairs={{0,16},{16,0},{1,17},{17,1},{2,18},{18,2},{3,19},{19,3},{4,20},{20... | collective-permute-start | bytes 3145736 | tf_op jit(solution)/shard_map/ppermute | solution.py:472
  250.0 64.8 %collective-permute-start.26 = (bf16[1024,512]{1,0:T(8,128)(2,1)}, bf16[1024,512]{1,0:T(8,128)(2,1)}, u32[]{:S(2)}, u32[]{:S(2)}) collective-permute-start(bf16[1024,512]{1,0:T(8,128)(2,1)} %convolution_convert_fusion.4), channel_id=1, source_target_pairs={{0,2},{2,0},{1,3},{3,1},{4,6},{6,4},{5,7},{7,5},{8,10},{10,8},{9,1... | collective-permute-start | bytes 3145736 | tf_op jit(solution)/shard_map/ppermute | solution.py:472
  257.8 174.6 %reduce-scatter.3.cloned.1.call-start = ((), (), s32[]{:S(2)}) async-start(), calls=%async_computation.4 | async-start | bytes 1638400 | tf_op jit(solution)/shard_map/reduce_scatter | solution.py:625
  310.0 36.5 %collective-permute-start.24 = (bf16[1184,1024]{1,0:T(8,128)(2,1)S(1)}, bf16[1184,1024]{1,0:T(8,128)(2,1)}, u32[]{:S(2)}, u32[]{:S(2)}) collective-permute-start(bf16[1184,1024]{1,0:T(8,128)(2,1)S(1)} %convolution_convert_fusion.1.a_ref), channel_id=1, source_target_pairs={{0,1},{1,0},{2,3},{3,2},{4,5},{5,4},{6,7},{7,6},{8,9},{9,8},{10,11... | collective-permute-start | bytes 7274504 | tf_op jit(solution)/shard_map/ppermute | solution.py:472
  314.8 60.0 %collective-permute-start.27 = (bf16[1184,512]{1,0:T(8,128)(2,1)}, bf16[1184,512]{1,0:T(8,128)(2,1)}, u32[]{:S(2)}, u32[]{:S(2)}) collective-permute-start(bf16[1184,512]{1,0:T(8,128)(2,1)} %get-tuple-element.81), channel_id=1, source_target_pairs={{0,1},{1,0},{2,3},{3,2},{4,5},{5,4},{6,7},{7,6},{8,9},{9,8},{10,11... | collective-permute-start | bytes 3637256 | tf_op jit(solution)/shard_map/ppermute | solution.py:472
  314.8 43.6 %collective-permute-start.23 = (bf16[1024,384]{1,0:T(8,128)(2,1)}, bf16[1024,384]{1,0:T(8,128)(2,1)}, u32[]{:S(2)}, u32[]{:S(2)}) collective-permute-start(bf16[1024,384]{1,0:T(8,128)(2,1)} %convolution_convert_fusion.7), channel_id=1, source_target_pairs={{0,16},{16,0},{1,17},{17,1},{2,18},{18,2},{3,19},{19,3},{4,20},{20... | collective-permute-start | bytes 2359304 | tf_op jit(solution)/shard_map/ppermute | solution.py:472
  326.5 8.9 %collective-permute-start.39 = (f32[2,2560]{1,0:T(2,128)S(1)}, f32[2,2560]{1,0:T(2,128)S(1)}, u32[]{:S(2)}, u32[]{:S(2)}) collective-permute-start(f32[2,2560]{1,0:T(2,128)S(1)} %add.214), channel_id=1, source_target_pairs={{0,16},{16,0},{1,17},{17,1},{2,18},{18,2},{3,19},{19,3},{4,20},{20... | collective-permute-start | bytes 61448 | tf_op jit(solution)/shard_map/ppermute | solution.py:472
  330.7 13.9 %collective-permute-start.40 = (bf16[1024,256]{1,0:T(8,128)(2,1)S(1)}, bf16[1024,256]{1,0:T(8,128)(2,1)S(1)}, u32[]{:S(2)}, u32[]{:S(2)}) collective-permute-start(bf16[1024,256]{1,0:T(8,128)(2,1)S(1)} %slice.616), channel_id=1, source_target_pairs={{0,2},{2,0},{1,3},{3,1},{4,6},{6,4},{5,7},{7,5},{8,10},{10,8},{9,1... | collective-permute-start | bytes 1572872 | tf_op jit(solution)/shard_map/ppermute | solution.py:472
  335.4 22.9 %collective-permute-start.41 = (bf16[1024,256]{1,0:T(8,128)(2,1)}, bf16[1024,256]{1,0:T(8,128)(2,1)S(1)}, u32[]{:S(2)}, u32[]{:S(2)}) collective-permute-start(bf16[1024,256]{1,0:T(8,128)(2,1)} %slice.618), channel_id=1, source_target_pairs={{0,16},{16,0},{1,17},{17,1},{2,18},{18,2},{3,19},{19,3},{4,20},{20... | collective-permute-start | bytes 1572872 | tf_op jit(solution)/shard_map/ppermute | solution.py:472
  344.6 27.0 %collective-permute-start.31 = (bf16[1024,384]{1,0:T(8,128)(2,1)}, bf16[1024,384]{1,0:T(8,128)(2,1)}, u32[]{:S(2)}, u32[]{:S(2)}) collective-permute-start(bf16[1024,384]{1,0:T(8,128)(2,1)} %convolution_convert_fusion.6), channel_id=1, source_target_pairs={{0,16},{16,0},{1,17},{17,1},{2,18},{18,2},{3,19},{19,3},{4,20},{20... | collective-permute-start | bytes 2359304 | tf_op jit(solution)/shard_map/ppermute | solution.py:472
  365.3 20.5 %collective-permute-start.29 = (bf16[1024,384]{1,0:T(8,128)(2,1)}, bf16[1024,384]{1,0:T(8,128)(2,1)S(1)}, u32[]{:S(2)}, u32[]{:S(2)}) collective-permute-start(bf16[1024,384]{1,0:T(8,128)(2,1)} %add_convert_fusion.4), channel_id=1, source_target_pairs={{0,2},{2,0},{1,3},{3,1},{4,6},{6,4},{5,7},{7,5},{8,10},{10,8},{9,1... | collective-permute-start | bytes 2359304 | tf_op jit(solution)/shard_map/ppermute | solution.py:472
  369.6 13.4 %collective-permute-start.42 = (bf16[1024,256]{1,0:T(8,128)(2,1)}, bf16[1024,256]{1,0:T(8,128)(2,1)}, u32[]{:S(2)}, u32[]{:S(2)}) collective-permute-start(bf16[1024,256]{1,0:T(8,128)(2,1)} %slice.620), channel_id=1, source_target_pairs={{0,16},{16,0},{1,17},{17,1},{2,18},{18,2},{3,19},{19,3},{4,20},{20... | collective-permute-start | bytes 1572872 | tf_op jit(solution)/shard_map/ppermute | solution.py:472
  371.3 11.1 %collective-permute-start.50 = (f32[2,512]{1,0:T(2,128)S(1)}, f32[2,512]{1,0:T(2,128)S(1)}, u32[]{:S(2)}, u32[]{:S(2)}) collective-permute-start(f32[2,512]{1,0:T(2,128)S(1)} %add.225), channel_id=1, source_target_pairs={{0,16},{16,0},{1,17},{17,1},{2,18},{18,2},{3,19},{19,3},{4,20},{20... | collective-permute-start | bytes 12296 | tf_op jit(solution)/shard_map/ppermute | solution.py:472
  381.9 20.8 %collective-permute-start.28 = (bf16[1184,256]{1,0:T(8,128)(2,1)}, bf16[1184,256]{1,0:T(8,128)(2,1)}, u32[]{:S(2)}, u32[]{:S(2)}) collective-permute-start(bf16[1184,256]{1,0:T(8,128)(2,1)} %get-tuple-element.83), channel_id=1, source_target_pairs={{0,2},{2,0},{1,3},{3,1},{4,6},{6,4},{5,7},{7,5},{8,10},{10,8},{9,1... | collective-permute-start | bytes 1818632 | tf_op jit(solution)/shard_map/ppermute | solution.py:472
  384.2 17.2 %collective-permute-start.43 = (bf16[1024,128]{1,0:T(8,128)(2,1)S(1)}, bf16[1024,128]{1,0:T(8,128)(2,1)S(1)}, u32[]{:S(2)}, u32[]{:S(2)}) collective-permute-start(bf16[1024,128]{1,0:T(8,128)(2,1)S(1)} %slice.622), channel_id=1, source_target_pairs={{0,2},{2,0},{1,3},{3,1},{4,6},{6,4},{5,7},{7,5},{8,10},{10,8},{9,1... | collective-permute-start | bytes 786440 | tf_op jit(solution)/shard_map/ppermute | solution.py:472
  386.0 17.8 %collective-permute-start.32 = (bf16[256,384]{1,0:T(8,128)(2,1)S(1)}, bf16[256,384]{1,0:T(8,128)(2,1)S(1)}, u32[]{:S(2)}, u32[]{:S(2)}) collective-permute-start(bf16[256,384]{1,0:T(8,128)(2,1)S(1)} %get-tuple-element.157), channel_id=1, source_target_pairs={{0,4},{4,8},{8,12},{12,0},{1,5},{5,9},{9,13},{13,1},{2,6},{6,10},{... | collective-permute-start | bytes 589832 | tf_op jit(solution)/shard_map/ppermute | solution.py:692
  388.0 15.9 %collective-permute-start.34 = (bf16[256,384]{1,0:T(8,128)(2,1)S(1)}, bf16[256,384]{1,0:T(8,128)(2,1)S(1)}, u32[]{:S(2)}, u32[]{:S(2)}) collective-permute-start(bf16[256,384]{1,0:T(8,128)(2,1)S(1)} %get-tuple-element.158), channel_id=1, source_target_pairs={{0,12},{4,0},{8,4},{12,8},{1,13},{5,1},{9,5},{13,9},{2,14},{6,2},{... | collective-permute-start | bytes 589832 | tf_op jit(solution)/shard_map/ppermute | solution.py:692
  390.0 13.9 %collective-permute-start.33 = (bf16[256,384]{1,0:T(8,128)(2,1)S(1)}, bf16[256,384]{1,0:T(8,128)(2,1)S(1)}, u32[]{:S(2)}, u32[]{:S(2)}) collective-permute-start(bf16[256,384]{1,0:T(8,128)(2,1)S(1)} %get-tuple-element.159), channel_id=1, source_target_pairs={{0,8},{4,12},{8,0},{12,4},{1,9},{5,13},{9,1},{13,5},{2,10},{6,14},... | collective-permute-start | bytes 589832 | tf_op jit(solution)/shard_map/ppermute | solution.py:692
  406.3 16.6 %collective-permute-start.30 = (bf16[1184,256]{1,0:T(8,128)(2,1)S(1)}, bf16[1184,256]{1,0:T(8,128)(2,1)S(1)}, u32[]{:S(2)}, u32[]{:S(2)}) collective-permute-start(bf16[1184,256]{1,0:T(8,128)(2,1)S(1)} %copy-done.35), channel_id=1, source_target_pairs={{0,2},{2,0},{1,3},{3,1},{4,6},{6,4},{5,7},{7,5},{8,10},{10,8},{9,1... | collective-permute-start | bytes 1818632 | tf_op jit(solution)/shard_map/ppermute | solution.py:472
  414.9 21.2 %collective-permute-start.45 = (bf16[256,1024]{1,0:T(8,128)(2,1)}, bf16[256,1024]{1,0:T(8,128)(2,1)S(1)}, u32[]{:S(2)}, u32[]{:S(2)}) collective-permute-start(bf16[256,1024]{1,0:T(8,128)(2,1)} %pad_maximum_fusion.7), channel_id=1, source_target_pairs={{0,2},{2,0},{1,3},{3,1},{4,6},{6,4},{5,7},{7,5},{8,10},{10,8},{9,1... | collective-permute-start | bytes 1572872 | tf_op jit(solution)/shard_map/ppermute | solution.py:472
  432.5 10.9 %collective-permute-start.44 = (bf16[256,640]{1,0:T(8,128)(2,1)}, bf16[256,640]{1,0:T(8,128)(2,1)}, u32[]{:S(2)}, u32[]{:S(2)}) collective-permute-start(bf16[256,640]{1,0:T(8,128)(2,1)} %reduce-scatter.3.cloned.1.call-done), channel_id=1, source_target_pairs={{0,16},{16,0},{1,17},{17,1},{2,18},{18,2},{3,19},{19,3},{4,20},{20... | collective-permute-start | bytes 983048 | tf_op jit(solution)/shard_map/ppermute | solution.py:472
  438.1 14.9 %collective-permute-start.46 = (bf16[256,1024]{1,0:T(8,128)(2,1)S(1)}, bf16[256,1024]{1,0:T(8,128)(2,1)S(1)}, u32[]{:S(2)}, u32[]{:S(2)}) collective-permute-start(bf16[256,1024]{1,0:T(8,128)(2,1)S(1)} %add_convert_fusion.5), channel_id=1, source_target_pairs={{0,16},{16,0},{1,17},{17,1},{2,18},{18,2},{3,19},{19,3},{4,20},{20... | collective-permute-start | bytes 1572872 | tf_op jit(solution)/shard_map/ppermute | solution.py:472
  (49 other events, 534.6 us)
Sparse Core Ops, SparseCore 0:
  57.9 26.3 all-gather.4
  86.4 27.3 all-gather.2
  258.0 74.9 reduce-scatter.4
  402.8 29.6 reduce-scatter.2

commit v5 on v4

v5 whole, which is shorter than its diff:
```python
import functools
import math

import jax
import jax.numpy as jnp
from jax import lax
from jax.experimental import pallas as pl
from jax.experimental.pallas import tpu as pltpu
from jax.sharding import Mesh, PartitionSpec as P

D = 1024
HD = 64
SEQ = 577
PAD = 592
TM = 296
EPS = 1e-06
F32 = jnp.float32
BF16 = jnp.bfloat16
VMEM_LIMIT = 60 * 1024 * 1024
ROOT_HALF = math.sqrt(0.5)
DENSITY = 1.0 / math.sqrt(2.0 * math.pi)


def mm(a, b):
    return lax.dot_general(a, b, (((1,), (0,)), ((), ())), preferred_element_type=F32)


def mm_nt(a, b):
    return lax.dot_general(a, b, (((1,), (1,)), ((), ())), preferred_element_type=F32)


def mm_tn(a, b):
    return lax.dot_general(a, b, (((0,), (0,)), ((), ())), preferred_element_type=F32)


def row_mean(v):
    return jnp.sum(v, axis=1, keepdims=True) * (1.0 / D)


def col_sum(v):
    return jnp.sum(v, axis=0, keepdims=True)


def stats(rows):
    middle = row_mean(rows)
    spread = row_mean(rows * rows) - middle * middle
    return middle, lax.rsqrt(spread + EPS)


def params(n):
    return pltpu.CompilerParams(
        dimension_semantics=("arbitrary",) * n, vmem_limit_bytes=VMEM_LIMIT
    )


def cost(flops, moved, exps=0):
    return pl.CostEstimate(flops=int(flops), bytes_accessed=int(moved), transcendentals=int(exps))


def like(shape, dtype):
    return jax.ShapeDtypeStruct(shape, dtype)


def row_spec(cols):
    return pl.BlockSpec((TM, cols), lambda i, *_: (i, 0))


def fixed(shape):
    return pl.BlockSpec(shape, lambda *_: (0,) * len(shape))


def held_once(shape):
    return pl.BlockSpec(shape, lambda *_: (0,) * len(shape), pipeline_mode=pl.Buffered(1))


def add_up(ref, first, part):
    @pl.when(first)
    def _():
        ref[...] = part

    @pl.when(jnp.logical_not(first))
    def _():
        ref[...] += part


def norm_qkv_kernel(x_ref, gain_ref, shift_ref, bias_ref, *refs):
    blocks, (n_ref, o_ref, w_ref) = refs[:8], refs[8:]
    one = blocks[1].shape[1] // 2

    @pl.when(pl.program_id(0) == 0)
    def _():
        for place in range(4):
            first, second = blocks[2 * place], blocks[2 * place + 1]
            start = 3 * one * place
            w_ref[:, start : start + 2 * one] = first[...]
            w_ref[:, start + 2 * one : start + 3 * one] = second[:, :one]
            w_ref[:, (12 + place) * one : (13 + place) * one] = second[:, one:]

    x = x_ref[...].astype(F32)
    middle, scaled = stats(x)
    n = (((x - middle) * scaled) * gain_ref[...] + shift_ref[...]).astype(BF16)
    n_ref[...] = n
    o_ref[...] = (mm(n, w_ref[:, : 12 * one]) + bias_ref[...]).astype(BF16)


def norm_qkv(x, gain, shift, bias, blocks):
    rows = x.shape[0]
    wide = blocks[0].shape[1]
    out = 6 * wide
    return pl.pallas_call(
        norm_qkv_kernel,
        grid=(rows // TM,),
        name="norm_qkv",
        in_specs=[row_spec(D), gain[1], shift[1], fixed((1, out))] + [held_once((D, wide))] * 8,
        out_specs=[row_spec(D), row_spec(out), held_once((D, 8 * wide))],
        out_shape=[like((rows, D), BF16), like((rows, out), BF16), like((D, 8 * wide), BF16)],
        compiler_params=params(1),
        cost_estimate=cost(2 * rows * D * out, 16 * rows * D),
    )(x, gain[0], shift[0], bias, *blocks)


def attend_kernel(qkv_ref, o_ref, p_ref):
    live = lax.broadcasted_iota(jnp.int32, (1, PAD), 1) < SEQ
    step = 2 * HD
    for h in range(2):
        q, k, v = (qkv_ref[:, step * w + HD * h : step * w + HD * (h + 1)] for w in range(3))
        s = mm_nt(q * jnp.asarray(0.125, BF16), k)
        s = jnp.where(live, s, -1e30)
        e = jnp.exp(s - jnp.max(s, axis=1, keepdims=True))
        p = (e * (1.0 / jnp.sum(e, axis=1, keepdims=True))).astype(BF16)
        p_ref[h] = p
        o_ref[:, HD * h : HD * (h + 1)] = mm(p, v).astype(BF16)


def attend(qkv):
    rows, cols = qkv.shape
    pairs = cols // (6 * HD)
    held = rows // PAD
    return pl.pallas_call(
        attend_kernel,
        grid=(pairs, held),
        name="attend",
        in_specs=[pl.BlockSpec((PAD, 6 * HD), lambda p, i: (i, p))],
        out_specs=[
            pl.BlockSpec((PAD, 2 * HD), lambda p, i: (i, p)),
            pl.BlockSpec((None, 2, PAD, PAD), lambda p, i: (i, p, 0, 0)),
        ],
        out_shape=[like((rows, cols // 3), BF16), like((held, 2 * pairs, PAD, PAD), BF16)],
        compiler_params=params(2),
        cost_estimate=cost(16 * rows * PAD * cols, 40 * rows * D, 4 * rows * PAD * pairs),
    )(qkv)


def attend_back_kernel(qkv_ref, p_ref, g_ref, d_ref, sum_ref):
    step = 2 * HD
    for h in range(2):
        q, k, v = (qkv_ref[:, step * w + HD * h : step * w + HD * (h + 1)] for w in range(3))
        g = g_ref[:, HD * h : HD * (h + 1)]
        pb = p_ref[h]
        p = pb.astype(F32)
        dp = mm_nt(g, v)
        z = jnp.sum(p * dp, axis=1, keepdims=True)
        ds = (p * (dp - z)).astype(BF16)
        parts = (mm(ds, k) * 0.125, mm_tn(ds, q) * 0.125, mm_tn(pb, g))
        for w, part in enumerate(parts):
            d_ref[:, step * w + HD * h : step * w + HD * (h + 1)] = part.astype(BF16)
    add_up(sum_ref, pl.program_id(1) == 0, col_sum(d_ref[...].astype(F32)))


def attend_back(qkv, probs, grads):
    rows, cols = qkv.shape
    pairs = cols // (6 * HD)
    held = rows // PAD
    three = pl.BlockSpec((PAD, 6 * HD), lambda p, i: (i, p))
    return pl.pallas_call(
        attend_back_kernel,
        grid=(pairs, held),
        name="attend_back",
        in_specs=[
            three,
            pl.BlockSpec((None, 2, PAD, PAD), lambda p, i: (i, p, 0, 0)),
            pl.BlockSpec((PAD, 2 * HD), lambda p, i: (i, p)),
        ],
        out_specs=[three, pl.BlockSpec((1, 6 * HD), lambda p, i: (0, p))],
        out_shape=[like((rows, cols), BF16), like((1, cols), F32)],
        compiler_params=params(2),
        cost_estimate=cost(20 * rows * PAD * cols, 50 * rows * D),
    )(qkv, probs, grads)


def middle_kernel(x_ref, a_ref, b_ref, bias_ref, gain_ref, shift_ref, h_ref, n_ref):
    h = x_ref[...].astype(F32) + (a_ref[...].astype(F32) + b_ref[...].astype(F32)) + bias_ref[...]
    h_ref[...] = h
    middle, scaled = stats(h)
    n_ref[...] = (((h - middle) * scaled) * gain_ref[...] + shift_ref[...]).astype(BF16)


def middle(x, a, b, bias, gain, shift):
    rows = x.shape[0]
    return pl.pallas_call(
        middle_kernel,
        grid=(rows // TM,),
        name="middle",
        in_specs=[row_spec(D)] * 3 + [bias[1], gain[1], shift[1]],
        out_specs=[row_spec(D)] * 2,
        out_shape=[like((rows, D), F32), like((rows, D), BF16)],
        compiler_params=params(1),
        cost_estimate=cost(20 * rows * D, 12 * rows * D),
    )(x, a, b, bias[0], gain[0], shift[0])


def mlp_kernel(plan, place_ref, n_ref, dy_ref, bias_ref, *refs):
    packs = refs[: len(plan)]
    g_ref, du_ref, mine_ref, theirs_ref, lift_ref, bsum_ref = refs[len(plan) : len(plan) + 6]
    low_acc, lift_acc, buf, sems = refs[len(plan) + 6 :]
    j = pl.program_id(0)
    tn = g_ref.shape[1]
    slot = lax.rem(j, 2)

    def load(tile, at):
        return pltpu.make_async_copy(packs[plan[tile]], buf.at[at], sems.at[at])

    @pl.when(j == 0)
    def _():
        load(0, 0).start()
        low_acc[...] = jnp.zeros_like(low_acc)
        lift_acc[...] = jnp.zeros_like(lift_acc)

    for tile in range(1, len(plan)):

        @pl.when(j == tile - 1)
        def _(tile=tile):
            load(tile, tile % 2).start()

    load(0, slot).wait()
    up, down = buf[slot, :, :tn], buf[slot, :, tn:]
    u = mm(n_ref[...], up) + bias_ref[...]
    cdf = 0.5 * (1.0 + lax.erf(u * ROOT_HALF))
    g = (u * cdf).astype(BF16)
    slope = cdf + u * (jnp.exp(-0.5 * u * u) * DENSITY)
    g_ref[...] = g
    du = (mm(dy_ref[...], down) * slope).astype(BF16)
    du_ref[...] = du
    bsum_ref[...] = col_sum(du.astype(F32))
    low_acc[...] += mm_nt(g, down)
    lift_acc[...] += mm_nt(du, up)

    @pl.when(j == len(plan) - 1)
    def _():
        lift_ref[...] = lift_acc[...].astype(BF16)
        width = D // 4
        core = place_ref[0]
        for far in range(2):
            low = pl.multiple_of((2 * far + core) * width, width)
            other = pl.multiple_of((2 * far + 1 - core) * width, width)
            mine_ref[:, far * width : (far + 1) * width] = low_acc[:, pl.ds(low, width)]
            theirs_ref[:, far * width : (far + 1) * width] = low_acc[:, pl.ds(other, width)].astype(
                BF16
            )


def mlp(place, n2, dy, bias, packs, plan):
    rows = n2.shape[0]
    hid = bias.shape[1]
    tn = hid // len(plan)
    whole = held_once((rows, D))
    tile = pl.BlockSpec((rows, tn), lambda j, *_: (0, j))
    thin = pl.BlockSpec((1, tn), lambda j, *_: (0, j))
    return pl.pallas_call(
        functools.partial(mlp_kernel, plan),
        name="mlp",
        grid_spec=pltpu.PrefetchScalarGridSpec(
            num_scalar_prefetch=1,
            grid=(len(plan),),
            in_specs=[whole, whole, thin]
            + [pl.BlockSpec(memory_space=pl.ANY)] * len(packs),
            out_specs=[
                tile,
                tile,
                held_once((rows, D // 2)),
                held_once((rows, D // 2)),
                whole,
                thin,
            ],
            scratch_shapes=[
                pltpu.VMEM((rows, D), F32),
                pltpu.VMEM((rows, D), F32),
                pltpu.VMEM((2, D, 2 * tn), BF16),
                pltpu.SemaphoreType.DMA((2,)),
            ],
        ),
        out_shape=[
            like((rows, hid), BF16),
            like((rows, hid), BF16),
            like((rows, D // 2), F32),
            like((rows, D // 2), BF16),
            like((rows, D), BF16),
            like((1, hid), F32),
        ],
        compiler_params=params(1),
        cost_estimate=cost(8 * rows * D * hid, 24 * rows * D, 2 * rows * hid),
    )(place, n2, dy, bias, *packs)


def turn_kernel(
    place_ref, h_ref, dy_ref, a_ref, b_ref, low_ref, other_ref, gain_ref, bias_ref, w_ref,
    dh_ref, da_ref, do_ref, sums_ref, mine_ref, theirs_ref, held,
):
    h = h_ref[...]
    held[...] = h + bias_ref[...]
    core, side = place_ref[0], place_ref[1]
    width = D // 4
    low = low_ref[...] + other_ref[...].astype(F32)
    for far in range(2):
        at = pl.ds(pl.multiple_of((2 * far + core) * width, width), width)
        out = (held[:, at] + low[:, far * width : (far + 1) * width]).astype(BF16)

        @pl.when(side == far)
        def _(out=out):
            mine_ref[...] = out

        @pl.when(side != far)
        def _(out=out):
            theirs_ref[...] = out

    middle, scaled = stats(h)
    c = (h - middle) * scaled
    dn = a_ref[...].astype(F32) + b_ref[...].astype(F32)
    dy = dy_ref[...].astype(F32)
    e = dn * gain_ref[...]
    dh = dy + scaled * (e - row_mean(e) - c * row_mean(e * c))
    dh_ref[...] = dh
    da = dh.astype(BF16)
    da_ref[...] = da
    do_ref[...] = mm(da, w_ref[...]).astype(BF16)
    part = jnp.concatenate(
        [col_sum(da.astype(F32)), col_sum(dy), col_sum(dn * c), col_sum(dn)], axis=0
    )
    add_up(sums_ref, pl.program_id(0) == 0, part)


def turn(place, h, dy, a, b, low_mine, low_other, gain, bias, weights):
    rows = h.shape[0]
    wide = weights.shape[1] // 4
    width = D // 4
    return pl.pallas_call(
        turn_kernel,
        name="turn",
        grid_spec=pltpu.PrefetchScalarGridSpec(
            num_scalar_prefetch=1,
            grid=(rows // TM,),
            in_specs=[row_spec(D)] * 4
            + [row_spec(D // 2)] * 2
            + [gain[1], bias[1]]
            + [pl.BlockSpec((D, wide), lambda i, *_: (0, 3), pipeline_mode=pl.Buffered(1))],
            out_specs=[
                row_spec(D),
                row_spec(D),
                row_spec(wide),
                fixed((4, D)),
                row_spec(width),
                row_spec(width),
            ],
            scratch_shapes=[pltpu.VMEM((TM, D), F32)],
        ),
        out_shape=[
            like((rows, D), F32),
            like((rows, D), BF16),
            like((rows, wide), BF16),
            like((4, D), F32),
            like((rows, width), BF16),
            like((rows, width), BF16),
        ],
        compiler_params=params(1),
        cost_estimate=cost(2 * rows * D * wide, 20 * rows * D),
    )(place, h, dy, a, b, low_mine, low_other, gain[0], bias[0], weights)


def last_kernel(
    place_ref, x_ref, dh_ref, a_ref, b_ref, gain_ref, mine_ref, theirs_ref, sum_mine, sum_theirs, held, sums
):
    x = x_ref[...].astype(F32)
    middle, scaled = stats(x)
    c = (x - middle) * scaled
    dn = a_ref[...].astype(F32) + b_ref[...].astype(F32)
    e = dn * gain_ref[...]
    held[...] = dh_ref[...] + scaled * (e - row_mean(e) - c * row_mean(e * c))
    width = D // 4
    core, side = place_ref[0], place_ref[1]
    here = pl.ds(pl.multiple_of((2 * side + core) * width, width), width)
    there = pl.ds(pl.multiple_of((2 * (1 - side) + core) * width, width), width)
    mine_ref[...] = held[:, here]
    theirs_ref[...] = held[:, there].astype(BF16)
    i = pl.program_id(0)
    add_up(sums, i == 0, jnp.concatenate([col_sum(dn * c), col_sum(dn)], axis=0))

    @pl.when(i == pl.num_programs(0) - 1)
    def _():
        sum_mine[...] = sums[:, here]
        sum_theirs[...] = sums[:, there]


def last(place, x, dh, a, b, gain):
    rows = x.shape[0]
    width = D // 4
    return pl.pallas_call(
        last_kernel,
        name="last",
        grid_spec=pltpu.PrefetchScalarGridSpec(
            num_scalar_prefetch=1,
            grid=(rows // TM,),
            in_specs=[row_spec(D)] * 4 + [gain[1]],
            out_specs=[row_spec(width), row_spec(width), fixed((2, width)), fixed((2, width))],
            scratch_shapes=[pltpu.VMEM((TM, D), F32), pltpu.VMEM((2, D), F32)],
        ),
        out_shape=[
            like((rows, width), F32),
            like((rows, width), BF16),
            like((2, width), F32),
            like((2, width), F32),
        ],
        compiler_params=params(1),
        cost_estimate=cost(20 * rows * D, 12 * rows * D),
    )(place, x, dh, a, b, gain[0])


def pack_kernel(*refs):
    out_ref = refs[-1]
    width = refs[0].shape[0]
    for at, ref in enumerate(refs[:-2]):
        out_ref[at, :] = ref[...]
    for at in range(4):
        out_ref[len(refs) - 2 + at, :] = refs[-2][width * at : width * (at + 1)]


def pack(vectors, long_vector):
    width = vectors[0].shape[0]
    return pl.pallas_call(
        pack_kernel,
        name="pack",
        out_shape=like((len(vectors) + 4, width), F32),
    )(*vectors, long_vector)


def unpack_kernel(place_ref, own, far, own_other, far_other, vec_ref, qkv_ref, tile_ref):
    core, side, half = place_ref[0], place_ref[1], place_ref[2]
    width = own.shape[1]
    one = width // 2

    def put(ref, at_side, at_core):
        at = pl.multiple_of((2 * at_side + at_core) * width, width)
        for k in range(6):
            vec_ref[k, :, pl.ds(at, width)] = ref[k : k + 1, :]

    put(own, side, core)
    put(far, 1 - side, core)
    put(own_other, side, 1 - core)
    put(far_other, 1 - side, 1 - core)
    qkv_ref[...] = jnp.zeros_like(qkv_ref)
    blocks = ((own, half), (far, half), (own, 1 - half), (far, 1 - half))
    for at, (ref, which) in enumerate(blocks):
        cut = pl.ds(pl.multiple_of(which * one, one), one)
        qkv_ref[:, 3 * one * at : 3 * one * at + one] = ref[6:7, cut]
        qkv_ref[:, 3 * one * at + 2 * one : 3 * one * (at + 1)] = ref[7:8, cut]
    order = (0, 1, 2, 3), (0, 2, 1, 3)
    for part in range(2):
        for at, index in enumerate(order[part]):
            ref, which = blocks[index]
            start = width * (4 * part + at)
            tile_ref[:, start : start + width] = ref[pl.ds(8 + 2 * which + part, 1), :]


def unpack(place, own, far, own_other, far_other):
    width = own.shape[1]
    return pl.pallas_call(
        unpack_kernel,
        name="unpack",
        in_specs=[pl.BlockSpec(memory_space=pltpu.SMEM)]
        + [pl.BlockSpec(memory_space=pltpu.VMEM)] * 4,
        out_shape=[like((6, 1, D), F32), like((1, 6 * width), F32), like((1, 8 * width), F32)],
    )(place, own, far, own_other, far_other)


def collect_kernel(place_ref, turn_ref, qkv_ref, up_ref, mine_ref, theirs_ref):
    core, side, half = place_ref[0], place_ref[1], place_ref[2]
    width = mine_ref.shape[1]
    one = width // 2
    for ref, at_side in ((mine_ref, side), (theirs_ref, 1 - side)):
        at = pl.ds(pl.multiple_of((2 * at_side + core) * width, width), width)
        ref[2:6, :] = turn_ref[:, at]
    for at in range(4):
        ref = (mine_ref, theirs_ref)[at % 2]
        which = half if at < 2 else 1 - half
        cut = pl.ds(pl.multiple_of(which * one, one), one)
        ref[0:1, cut] = qkv_ref[:, 3 * one * at : 3 * one * at + one]
        ref[1:2, cut] = qkv_ref[:, 3 * one * at + 2 * one : 3 * one * (at + 1)]
    order = (0, 1, 2, 3), (0, 2, 1, 3)
    for part in range(2):
        for at, index in enumerate(order[part]):
            ref = (mine_ref, theirs_ref)[index % 2]
            which = half if index < 2 else 1 - half
            start = width * (4 * part + at)
            ref[pl.ds(6 + 2 * which + part, 1), :] = up_ref[:, start : start + width]


def collect(place, turn_sums, qkv_sums, up_sums):
    width = D // 4
    return pl.pallas_call(
        collect_kernel,
        name="collect",
        in_specs=[pl.BlockSpec(memory_space=pltpu.SMEM)]
        + [pl.BlockSpec(memory_space=pltpu.VMEM)] * 3,
        out_shape=[like((10, width), F32)] * 2,
    )(place, turn_sums, qkv_sums, up_sums)


def hand_out_kernel(a_ref, b_ref, c_ref, d_ref, *outs):
    early = a_ref[...] + b_ref[...]
    late = c_ref[...] + d_ref[...]
    width = a_ref.shape[1]
    for at in range(6):
        outs[at][...] = early[at, :]
    for at in range(4):
        outs[6][width * at : width * (at + 1)] = early[6 + at, :]
    for at in range(2):
        outs[7 + at][...] = late[at, :]


def hand_out(early, early_got, late, late_got):
    width = early.shape[1]
    one = like((width,), F32)
    return pl.pallas_call(
        hand_out_kernel,
        name="hand_out",
        out_shape=[one] * 6 + [like((4 * width,), F32)] + [one] * 2,
    )(early, early_got, late, late_got)


def local(
    sizes,
    inputs,
    query_weight,
    key_weight,
    value_weight,
    query_bias,
    value_bias,
    out_weight,
    out_bias,
    up_weight,
    up_bias,
    down_weight,
    down_bias,
    first_gain,
    first_shift,
    second_gain,
    second_shift,
    cotangent,
):
    n_dp, n_row, n_xa, n_core = sizes
    my_x = lax.axis_index("xa")
    my_core = lax.axis_index("core")
    my_row = lax.axis_index("row")
    my_half = lax.axis_index("dp") % 2
    place = jnp.stack([my_core, my_x, my_half]).astype(jnp.int32)
    tokens_here, width = inputs.shape
    images = tokens_here // SEQ
    held = images // n_xa
    rows = held * PAD
    half = up_weight.shape[1] // 2
    quarter = half // 2
    heads_half = width // 2
    three = 3 * heads_half

    def swap(value, axis, size, bit=1):
        return lax.ppermute(value, axis, [(at, at ^ bit) for at in range(size)])

    def across(value):
        return swap(value, "xa", n_xa)

    def beside(value):
        return swap(value, "core", n_core)

    def over(value):
        return swap(value, "dp", n_dp)

    def pick(value, at, axis):
        return lax.dynamic_index_in_dim(value, at, axis, keepdims=False)

    def in_order(mine, other, at):
        return jnp.where(at == 0, mine, other), jnp.where(at == 0, other, mine)

    def after(value, *others):
        return lax.optimization_barrier((value, *others))[0]

    def halves(value, axis):
        cut = value.shape[axis] // 2
        both = value.reshape(value.shape[:axis] + (2, cut) + value.shape[axis + 1 :])
        return pick(both, my_half, axis), pick(both, my_half ^ 1, axis)

    count = held * SEQ

    def send_tokens(value):
        return lax.dynamic_slice_in_dim(value, (my_x ^ 1) * count, count, 0)

    def wide_tokens(value, got):
        mine = lax.dynamic_slice_in_dim(value, my_x * count, count, 0)
        pair = jnp.concatenate([mine, got], axis=1).reshape(held, SEQ, 2 * width)
        pair = jnp.pad(pair, ((0, 0), (0, PAD - SEQ), (0, 0))).reshape(rows, 2 * width)
        other = beside(pair)
        left, right = in_order(pair, other, my_core)
        first_left, second_left = in_order(left[:, :width], left[:, width:], my_x)
        first_right, second_right = in_order(right[:, :width], right[:, width:], my_x)
        return jnp.concatenate([first_left, first_right, second_left, second_right], axis=1)

    attn_shard = jnp.concatenate(
        [halves(item, 1)[0] for item in (query_weight, key_weight, value_weight)]
        + [halves(out_weight, 0)[0].T],
        axis=1,
    )
    input_leaves = send_tokens(inputs)
    attn_shard = after(attn_shard, input_leaves)
    input_got = across(input_leaves)
    pieces = [attn_shard] + [
        lax.ppermute(attn_shard, "row", [(at, (at + shift) % n_row) for at in range(n_row)])
        for shift in range(1, n_row)
    ]
    cut = 2 * heads_half
    first_own = jnp.zeros((D, cut), BF16)
    second_own = jnp.zeros((D, cut), BF16)
    for shift, piece in enumerate(pieces):
        start = (my_row - shift) % n_row * (D // n_row)
        first_own = lax.dynamic_update_slice(first_own, piece[:, :cut], (start, 0))
        second_own = lax.dynamic_update_slice(second_own, piece[:, cut:], (start, 0))
    first_far, second_oth = across(first_own), over(second_own)
    first_oth, second_far = over(first_own), across(second_own)

    small = pack(
        (
            out_bias,
            down_bias,
            first_gain,
            first_shift,
            second_gain,
            second_shift,
            query_bias,
            value_bias,
        ),
        up_bias,
    )
    small_far = across(small)
    vectors, qkv_bias, tile_bias = unpack(
        place, small, small_far, beside(small), beside(small_far)
    )
    out_bias_all, down_bias_all, gain_one, shift_one, gain_two, shift_two = (
        (vectors, pl.BlockSpec((None, 1, D), lambda i, *_, at=at: (at, 0, 0))) for at in range(6)
    )
    wide_input = wide_tokens(inputs, input_got)
    first_far_oth = over(after(first_far, wide_input, qkv_bias))
    second_far_oth = across(after(second_oth, wide_input, qkv_bias))

    def gather(part):
        up_part = halves(up_weight, 1)[0][:, quarter * part : quarter * (part + 1)]
        down_part = halves(down_weight, 0)[0][quarter * part : quarter * (part + 1)].T
        shard = after(jnp.concatenate([up_part, down_part], axis=1), first_own, second_own)
        return lax.all_gather(shard, "row", axis=0, tiled=True)

    own_a, own_b = gather(0), gather(1)
    grad_leaves = after(send_tokens(cotangent), first_far_oth)
    wide_grad = wide_tokens(cotangent, across(grad_leaves))

    wide_one, qkv, attn_weights = norm_qkv(
        wide_input,
        gain_one,
        shift_one,
        qkv_bias,
        (
            first_own,
            second_own,
            first_far,
            second_far,
            first_oth,
            second_oth,
            first_far_oth,
            second_far_oth,
        ),
    )
    oth_a, far_a = over(own_a), across(own_a)
    oth_b, far_b = over(own_b), across(own_b)
    attended, probs = attend(qkv)
    mixed = mm_nt(attended, attn_weights[:, 4 * three :]).astype(BF16)
    far_oth_a = over(after(far_a, mixed))
    middle_sum, wide_two = middle(
        wide_input, mixed, beside(mixed), out_bias_all, gain_two, shift_two
    )
    far_oth_b = across(after(oth_b, wide_two))
    plan = (0, 1, 2, 3, 4, 6, 5, 7)
    gate, pre, low_mine, low_theirs, lifted_two, up_sums = mlp(
        place,
        wide_two,
        wide_grad,
        tile_bias,
        (own_a, far_a, oth_a, far_oth_a, own_b, far_b, oth_b, far_oth_b),
        plan,
    )

    def wide_add(mine, got):
        return (mine.astype(F32) + got.astype(F32)).astype(BF16)

    def same_half(value):
        if n_dp == 2:
            return value
        groups = [[at + bit for at in range(0, n_dp, 2)] for bit in range(2)]
        return lax.psum(value.astype(F32), "dp", axis_index_groups=groups).astype(BF16)

    def scatter(value):
        return lax.psum_scatter(value, "row", scatter_dimension=0, tiled=True)

    def tiles(value, first, end):
        return value[:, quarter * first : quarter * end]

    lifted_other = beside(lifted_two)
    low_other = beside(low_theirs)
    down_all = mm_tn(wide_grad, gate).astype(BF16)
    down_piece = scatter(down_all)
    up_over = mm_tn(after(wide_two, down_all), tiles(pre, 2, 4)).astype(BF16)
    up_across = mm_tn(after(wide_two, down_all), tiles(pre, 6, 8)).astype(BF16)
    up_over_got, up_across_got = over(up_over), across(up_across)

    middle_grad, attn_grad, head_grad, turn_sums, out_mine, out_theirs = turn(
        place,
        middle_sum,
        wide_grad,
        lifted_two,
        after(lifted_other, down_all, up_over, up_across),
        low_mine,
        low_other,
        gain_two,
        down_bias_all,
        attn_weights,
    )
    up_over_got, up_across_got, _ = lax.optimization_barrier(
        (up_over_got, up_across_got, attn_grad)
    )
    up_a = wide_add(mm_tn(wide_two, tiles(pre, 0, 2)), up_over_got)
    up_b = wide_add(mm_tn(wide_two, tiles(pre, 4, 6)), up_across_got)
    up_a_got, up_b_got = across(up_a[:, quarter:]), over(up_b[:, quarter:])
    out_got = across(after(out_theirs, up_a))
    dqkv, qkv_sums = attend_back(qkv, probs, after(head_grad, up_a, up_b))

    def to_feature_blocks(mine, got, dtype):
        first, second = in_order(mine.astype(dtype), got.astype(dtype), my_x)
        both = jnp.concatenate([first, second]).reshape(images, PAD, width)
        return both[:, :SEQ].reshape(tokens_here, width)

    far_oth = mm_tn(wide_one, dqkv[:, 3 * three :]).astype(BF16)
    near_oth = mm_tn(wide_one, dqkv[:, 2 * three : 3 * three]).astype(BF16)
    far_oth_got, near_oth_got = over(far_oth), over(near_oth)
    lifted_one = mm_nt(
        after(dqkv, far_oth, near_oth), attn_weights[:, : 4 * three]
    ).astype(BF16)
    lifted_one_other = beside(lifted_one)

    out_all = mm_tn(after(attn_grad, lifted_one), attended).astype(BF16)
    out_over_got = over(out_all[:, 2 * heads_half :])
    mine_early, theirs_early = collect(place, turn_sums, qkv_sums, up_sums)
    early = mine_early + across(theirs_early)

    far_oth_got = after(far_oth_got, out_all)
    far_own = wide_add(mm_tn(wide_one, dqkv[:, three : 2 * three]), far_oth_got)
    far_own_got = across(far_own)
    near_own = wide_add(mm_tn(wide_one, dqkv[:, :three]), near_oth_got)
    out_own = wide_add(out_all[:, : 2 * heads_half], after(out_over_got, near_own))
    out_far_got = across(out_own[:, heads_half:])
    input_mine, input_theirs, late_mine, late_theirs = last(
        place, wide_input, middle_grad, lifted_one, after(lifted_one_other, out_own), gain_one
    )
    outputs = to_feature_blocks(out_mine, after(out_got, input_mine), BF16)

    near_sum = wide_add(near_own, after(far_own_got, input_mine))
    strip = D // n_row

    def rows_of(value, shift):
        return lax.dynamic_slice_in_dim(value, (my_row + shift) % n_row * strip, strip, 0)

    qkv_total = rows_of(near_sum, 0).astype(F32)
    for shift in range(1, n_row):
        got = lax.ppermute(
            rows_of(near_sum, shift), "row", [(at, (at + shift) % n_row) for at in range(n_row)]
        )
        qkv_total = qkv_total + got.astype(F32)
    qkv_piece = same_half(qkv_total.astype(BF16))
    qkv_other = over(qkv_piece)

    input_theirs = after(input_theirs, far_own_got)
    input_grad = to_feature_blocks(input_mine, across(input_theirs), F32)

    up_piece = same_half(
        scatter(
            jnp.concatenate(
                [
                    wide_add(up_a[:, :quarter], up_a_got),
                    wide_add(up_b[:, :quarter], up_b_got),
                    wide_add(out_own[:, :heads_half], out_far_got),
                ],
                axis=1,
            )
        )
    )
    up_other = over(up_piece)

    def some(value, *which):
        return jnp.concatenate([tiles(value, at, at + 1) for at in which], axis=1)

    down_x = wide_add(some(down_piece, 0, 4, 2, 5), across(some(down_piece, 1, 6, 3, 7)))
    down_got = over(down_x)
    down_total = down_x.astype(F32) + jnp.concatenate(
        [down_got[:, half:], down_got[:, :half]], axis=1
    ).astype(F32)
    if n_dp > 2:
        groups = [[at + bit for at in range(0, n_dp, 2)] for bit in range(2)]
        down_total = lax.psum(down_total, "dp", axis_index_groups=groups)
    down_first, down_second = in_order(down_total[:, :half], down_total[:, half:], my_half)
    down_grad = jnp.concatenate([down_first, down_second], axis=1).T

    def both_halves(mine, other, low, high):
        first, second = in_order(mine[:, low:high], other[:, low:high], my_half)
        return jnp.concatenate([first, second], axis=1).astype(F32)

    up_grad = both_halves(up_piece, up_other, 0, half)
    out_grad = both_halves(up_piece, up_other, half, half + heads_half).T
    query_grad, key_grad, value_grad = (
        both_halves(qkv_piece, qkv_other, heads_half * at, heads_half * (at + 1))
        for at in range(3)
    )

    late = late_mine + across(late_theirs)
    steps = [("row", n_row, 1 << bit) for bit in range(n_row.bit_length() - 1)]
    steps += [("dp", n_dp, 1 << bit) for bit in range(n_dp.bit_length() - 1)]
    for step in steps[:-1]:
        early, late = early + swap(early, *step), late + swap(late, *step)
    sums = hand_out(early, swap(early, *steps[-1]), late, swap(late, *steps[-1]))

    return (
        outputs,
        input_grad,
        query_grad,
        key_grad,
        value_grad,
        sums[0],
        sums[1],
        out_grad,
        sums[2],
        up_grad,
        sums[6],
        down_grad,
        sums[3],
        sums[7],
        sums[8],
        sums[4],
        sums[5],
    )


def solution(mesh):
    n_dp, n_row, n_col = (mesh.shape[name] for name in ("dp", "row", "col"))
    sizes = (n_dp, n_row, n_col // 2, 2)
    split = Mesh(mesh.devices.reshape(sizes), ("dp", "row", "xa", "core"))
    col = ("xa", "core")
    tokens, rows, cols, vec = P(("dp", "row"), col), P("row", col), P(col, "row"), P(col)
    in_specs = (
        (tokens, rows, rows, rows, vec, vec, cols, vec, rows, vec, cols)
        + (vec,) * 5
        + (tokens,)
    )
    out_specs = (
        (tokens, tokens, rows, rows, rows, vec, vec, cols, vec, rows, vec, cols) + (vec,) * 5
    )
    return jax.shard_map(
        functools.partial(local, sizes),
        mesh=split,
        in_specs=in_specs,
        out_specs=out_specs,
        check_vma=False,
    )
```

time: 470 us -> 519 us (1.10)
  waiting for transfers between devices: 114 us -> 220 us
  local copies, waits for them, and re-layouts: 81.8 us -> 26.3 us
  starting transfers between devices: 50.2 us -> 57.8 us
    ppermute x45 -> x46, waiting for transfers between devices: 90.8 us -> 218 us  [swap(): return lax.ppermute(value, axis, [(at, at ^ bit) for at in range(size)])]
    unnamed x125 -> x79, local copies, waits for them, and re-layouts: 40.2 us -> 7.49 us
    all_gather x2, waiting for transfers between devices: 15.4 us -> 0.02 us  [gather(): return lax.all_gather(shard, 'row', axis=0, tiled=True)]
    slice x21 -> x4, local copies, waits for them, and re-layouts: 14.9 us -> 2.23 us  [the longest x1 1.36 us: tiles(): return value[:, quarter * first:quarter * end]]
    reduce_scatter x2, waiting for transfers between devices: 8.15 us -> 0.02 us  [scatter(): return lax.psum_scatter(value, 'row', scatter_dimension=0, tiled=True)]
    ppermute x45 -> x46, starting transfers between devices: 37.5 us -> 44.2 us  [swap(): return lax.ppermute(value, axis, [(at, at ^ bit) for at in range(size)])]
    pallas_call x2 -> x5, Pallas kernels: 19 us -> 19.5 us  [the longest x1 13.8 us: turn(): pl.pallas_call(turn_kernel, name='turn', grid_spec=pltpu.PrefetchScalarGr...]
  transfers between devices with their start and end apart: 55 -> 56, of which waited for: 18 -> 22; matrix products, arithmetic and copies ran while one was open for 32% -> 17% of each run, Pallas kernels for 20% -> 18%
where the time goes in v5:
time: 519 us; the launch traced here: 514 us
  waiting for transfers between devices  220 us (42%)
  Pallas kernels  126 us (24%)
  starting transfers between devices  57.8 us (11%)
  matrix products  46.6 us (9%)
  local copies, waits for them, and re-layouts  26.3 us (5%)
  other arithmetic  22.6 us (4%)
  between operations  14.8 us (3%)
    ppermute x46, waiting for transfers between devices, swap(): return lax.ppermute(value, axis, [(at, at ^ bit) for at in range(size)])  218 us
    ppermute x46, starting transfers between devices, swap(): return lax.ppermute(value, axis, [(at, at ^ bit) for at in range(size)])  44.2 us
    dot_general x10, matrix products, mm_tn(): lax.dot_general(a, b, (((0,), (0,)), ((), ())), preferred_element_type=F32)  37.7 us
    pallas_call x1, Pallas kernels, mlp(): pl.pallas_call(functools.partial(mlp_kernel, plan), name='mlp', grid_spec...  33.8 us
    pallas_call x1, Pallas kernels, attend_back(): pl.pallas_call(attend_back_kernel, grid=(pairs, held), name='attend_back'...  26.6 us
    pallas_call x1, Pallas kernels, attend(): pl.pallas_call(attend_kernel, grid=(pairs, held), name='attend', in_specs...  20.1 us
    pallas_call x1, Pallas kernels, turn(): pl.pallas_call(turn_kernel, name='turn', grid_spec=pltpu.PrefetchScalarGr...  13.8 us
  transfers between devices with their start and end apart: 56, of which 22 were waited for; matrix products, arithmetic and copies ran while one was open for 17% of the time, Pallas kernels for 18%

profile of v5, /device:TPU:0, one launch (start us, length us, event | category | flops | bytes accessed | tf_op | source)
XLA Modules:
  0.0 513.8 jit_solution(3099378362418405248)
XLA Ops:
  11.2 3.1 collective-permute-start.5
  14.3 2.6 collective-permute-start.6
  23.3 8.4 %collective-permute-done = bf16[1154,256]{1,0:T(8,128)(2,1)S(1)} collective-permute-done((bf16[1154,256]{1,0:T(8,128)(2,1)S(1)}, bf16[1154,256]{1,0:T(8,128)(2,1)S(1)}, u32[]{:S(2)}, u32[]{:S(2)}) %collective-permute-start) | collective-permute-done | bytes 590880 | tf_op jit(solution)/shard_map/ppermute | solution.py:575
  34.6 1.9 pad_maximum_fusion.9
  41.0 1.6 slice_dynamic-update-slice_fusion.2
  42.6 1.6 slice_dynamic-update-slice_fusion.1
  44.3 1.6 collective-permute-done.7
  45.9 1.6 slice_dynamic-update-slice_fusion
  52.1 1.8 pad_maximum_fusion.x_ref
  53.9 19.4 %collective-permute-done.11.refs_5_ = bf16[1024,256]{1,0:T(8,128)(2,1)} collective-permute-done((bf16[1024,256]{1,0:T(8,128)(2,1)S(1)}, bf16[1024,256]{1,0:T(8,128)(2,1)}, u32[]{:S(2)}, u32[]{:S(2)}) %collective-permute-start.11) | collective-permute-done | bytes 524320 | tf_op jit(solution)/shard_map/ppermute | solution.py:575
  75.6 9.7 %collective-permute-done.13.refs_7_ = bf16[1024,256]{1,0:T(8,128)(2,1)S(1)} collective-permute-done((bf16[1024,256]{1,0:T(8,128)(2,1)}, bf16[1024,256]{1,0:T(8,128)(2,1)S(1)}, u32[]{:S(2)}, u32[]{:S(2)}) %collective-permute-start.13) | collective-permute-done | bytes 524320 | tf_op jit(solution)/shard_map/ppermute | solution.py:575
  86.4 10.2 %norm_qkv.1 = (bf16[1184,1024]{1,0:T(8,128)(2,1)}, bf16[1184,1536]{1,0:T(8,128)(2,1)}, bf16[1024,2048]{1,0:T(8,128)(2,1)}) custom-call(bf16[1184,1024]{1,0:T(8,128)(2,1)} %pad_maximum_fusion.x_ref, f32[6,1,1024]{2,1,0:T(1,128)} %get-tuple-element.78.gain_ref.shift_ref.bias_ref, f32[6,1,1024]{2,1,0:T(1,128)} %get-tuple-element.78.gain_ref.shift_ref.bias_ref, ...), custom_call_target="tpu_custom_call" | custom-call | flops 3724541952 | bytes 19398656 | tf_op jit(solution)/shard_map/norm_qkv/pallas_call | solution.py:110
  96.6 20.1 %attend.1 = (bf16[1184,512]{1,0:T(8,128)(2,1)}, bf16[2,8,592,592]{3,2,1,0:T(8,128)(2,1)}) custom-call(bf16[1184,1536]{1,0:T(8,128)(2,1)} %get-tuple-element.83.qkv_ref), custom_call_target="tpu_custom_call" | custom-call | flops 17226006528 | bytes 48496640 | tf_op jit(solution)/shard_map/attend/pallas_call | solution.py:139
  116.8 4.5 convolution_convert_fusion.a_ref
  123.1 14.4 %collective-permute-done.15 = bf16[1154,256]{1,0:T(8,128)(2,1)S(1)} collective-permute-done((bf16[1154,256]{1,0:T(8,128)(2,1)S(1)}, bf16[1154,256]{1,0:T(8,128)(2,1)S(1)}, u32[]{:S(2)}, u32[]{:S(2)}) %collective-permute-start.15) | collective-permute-done | bytes 590880 | tf_op jit(solution)/shard_map/ppermute | solution.py:575
  141.6 22.3 %collective-permute-done.17.refs_1_ = bf16[1024,512]{1,0:T(8,128)(2,1)} collective-permute-done((bf16[1024,512]{1,0:T(8,128)(2,1)}, bf16[1024,512]{1,0:T(8,128)(2,1)}, u32[]{:S(2)}, u32[]{:S(2)}) %collective-permute-start.17) | collective-permute-done | bytes 1048608 | tf_op jit(solution)/shard_map/ppermute | solution.py:575
  166.9 6.7 %middle.1 = (f32[1184,1024]{1,0:T(8,128)}, bf16[1184,1024]{1,0:T(8,128)(2,1)}) custom-call(bf16[1184,1024]{1,0:T(8,128)(2,1)} %pad_maximum_fusion.x_ref, bf16[1184,1024]{1,0:T(8,128)(2,1)} %convolution_convert_fusion.a_ref, bf16[1184,1024]{1,0:T(8,128)(2,1)} %collective-permute-done.14.b_ref, f32[6,1,1024]{2,1,0:T(1,128)} %get-tuple-element.78.gain_ref.shift_ref.bias_ref, ...), custom_call_target="tpu_custom_call" | custom-call | flops 24248320 | bytes 14548992 | tf_op jit(solution)/shard_map/middle/pallas_call | solution.py:200
  175.9 2.0 pad_maximum_fusion.1.dy_ref
  177.8 10.6 %collective-permute-done.18.refs_2_ = bf16[1024,512]{1,0:T(8,128)(2,1)} collective-permute-done((bf16[1024,512]{1,0:T(8,128)(2,1)}, bf16[1024,512]{1,0:T(8,128)(2,1)}, u32[]{:S(2)}, u32[]{:S(2)}) %collective-permute-start.18) | collective-permute-done | bytes 1048608 | tf_op jit(solution)/shard_map/ppermute | solution.py:575
  188.4 1.9 collective-permute-done.20.refs_5_
  190.2 19.8 %collective-permute-done.19.refs_3_ = bf16[1024,512]{1,0:T(8,128)(2,1)} collective-permute-done((bf16[1024,512]{1,0:T(8,128)(2,1)}, bf16[1024,512]{1,0:T(8,128)(2,1)}, u32[]{:S(2)}, u32[]{:S(2)}) %collective-permute-start.19) | collective-permute-done | bytes 1048608 | tf_op jit(solution)/shard_map/ppermute | solution.py:575
  211.3 33.8 %mlp.1 = (bf16[1184,2048]{1,0:T(8,128)(2,1)}, bf16[1184,2048]{1,0:T(8,128)(2,1)}, f32[1184,512]{1,0:T(8,128)}, bf16[1184,512]{1,0:T(8,128)(2,1)}, bf16[1184,1024]{1,0:T(8,128)(2,1)}, /*index=5*/f32[1,2048]{1,0:T(1,128)}) custom-call(s32[3]{0:T(128)} %pad_add_fusion.place_ref, bf16[1184,1024]{1,0:T(8,128)(2,1)} %get-tuple-element.96.n_ref, ...), custom_call_target="tpu_custom_call" | custom-call | flops 19864223744 | bytes 29097984 | tf_op jit(solution)/shard_map/mlp/pallas_call | solution.py:269
  245.2 9.8 %convolution_convert_fusion.2 = bf16[1024,2048]{1,0:T(8,128)(2,1)} fusion(bf16[1184,2048]{1,0:T(8,128)(2,1)} %get-tuple-element.95, bf16[1184,256]{1,0:T(8,128)(2,1)} %copy-done.5, bf16[1184,256]{1,0:T(8,128)(2,1)} %copy-done.6, bf16[1184,256]{1,0:T(8,128)(2,1)S(1)} %get-tuple-element.183, bf16[1184,256]{1,0:T(8,128)(2,1)} %copy-done.7), kind=kOutput, calls=%fused_computation.2 | convolution fusion | flops 4977852416 | bytes 11468800 | tf_op jit(solution)/shard_map/dot_general | solution.py:33
  255.6 4.7 convolution_convert_fusion.4
  260.3 3.8 convolution_convert_fusion.5
  268.5 13.8 %turn.1 = (f32[1184,1024]{1,0:T(8,128)}, bf16[1184,1024]{1,0:T(8,128)(2,1)}, bf16[1184,512]{1,0:T(8,128)(2,1)}, f32[4,1024]{1,0:T(4,128)}, bf16[1184,256]{1,0:T(8,128)(2,1)}, /*index=5*/bf16[1184,256]{1,0:T(8,128)(2,1)}) custom-call(s32[3]{0:T(128)} %pad_add_fusion.place_ref, f32[1184,1024]{1,0:T(8,128)} %get-tuple-element.86.h_ref, ...), custom_call_target="tpu_custom_call" | custom-call | flops 1241513984 | bytes 24248320 | tf_op jit(solution)/shard_map/turn/pallas_call | solution.py:346
  282.3 7.2 %collective-permute-done.26 = bf16[1024,512]{1,0:T(8,128)(2,1)} collective-permute-done((bf16[1024,512]{1,0:T(8,128)(2,1)}, bf16[1024,512]{1,0:T(8,128)(2,1)}, u32[]{:S(2)}, u32[]{:S(2)}) %collective-permute-start.26) | collective-permute-done | bytes 1048608 | tf_op jit(solution)/shard_map/ppermute | solution.py:575
  290.7 4.1 add_convert_fusion.1
  294.8 4.5 add_convert_fusion
  299.3 26.6 %attend_back.1 = (bf16[1184,1536]{1,0:T(8,128)(2,1)}, f32[1,1536]{1,0:T(1,128)}) custom-call(bf16[1184,1536]{1,0:T(8,128)(2,1)} %get-tuple-element.83.qkv_ref, bf16[2,8,592,592]{3,2,1,0:T(8,128)(2,1)} %get-tuple-element.107.p_ref, bf16[1184,512]{1,0:T(8,128)(2,1)} %get-tuple-element.110.g_ref), custom_call_target="tpu_custom_call" | custom-call | flops 21532508160 | bytes 60620800 | tf_op jit(solution)/shard_map/attend_back/pallas_call | solution.py:175
  328.0 3.6 convolution_convert_fusion.6
  336.9 4.4 convolution_convert_fusion.1.a_ref
  342.0 3.4 collective-permute-start.40
  349.4 5.8 %collective-permute-done.30 = bf16[1024,384]{1,0:T(8,128)(2,1)S(1)} collective-permute-done((bf16[1024,384]{1,0:T(8,128)(2,1)S(1)}, bf16[1024,384]{1,0:T(8,128)(2,1)S(1)}, u32[]{:S(2)}, u32[]{:S(2)}) %collective-permute-start.30) | collective-permute-done | bytes 786464 | tf_op jit(solution)/shard_map/ppermute | solution.py:575
  357.5 34.6 %collective-permute-done.29 = bf16[1024,256]{1,0:T(8,128)(2,1)S(1)} collective-permute-done((bf16[1024,256]{1,0:T(8,128)(2,1)S(1)}, bf16[1024,256]{1,0:T(8,128)(2,1)S(1)}, u32[]{:S(2)}, u32[]{:S(2)}) %collective-permute-start.29) | collective-permute-done | bytes 524320 | tf_op jit(solution)/shard_map/ppermute | solution.py:575
  393.6 2.5 add_convert_fusion.3
  398.5 20.1 %collective-permute-done.48 = bf16[1024,128]{1,0:T(8,128)(2,1)S(1)} collective-permute-done((bf16[1024,128]{1,0:T(8,128)(2,1)S(1)}, bf16[1024,128]{1,0:T(8,128)(2,1)S(1)}, u32[]{:S(2)}, u32[]{:S(2)}) %collective-permute-start.48) | collective-permute-done | bytes 262176 | tf_op jit(solution)/shard_map/ppermute | solution.py:575
  419.8 9.0 %last.1 = (f32[1184,256]{1,0:T(8,128)}, bf16[1184,256]{1,0:T(8,128)(2,1)}, f32[2,256]{1,0:T(2,128)}, f32[2,256]{1,0:T(2,128)}) custom-call(s32[3]{0:T(128)} %pad_add_fusion.place_ref, bf16[1184,1024]{1,0:T(8,128)(2,1)} %pad_maximum_fusion.x_ref, f32[1184,1024]{1,0:T(8,128)} %get-tuple-element.106.dh_ref, bf16[1184,1024]{1,0:T(8,128)(2,1)} %copy-done.4, ...), custom_call_target="tpu_custom_call" | custom-call | flops 24248320 | bytes 14548992 | tf_op jit(solution)/shard_map/last/pallas_call | solution.py:406
  430.7 2.0 collective-permute-done.42
  433.8 1.7 collective-permute-start.34
  435.5 1.7 collective-permute-start.35
  437.2 2.8 collective-permute-start.36
  441.2 24.5 %collective-permute-done.44 = f32[2,256]{1,0:T(2,128)S(1)} collective-permute-done((f32[2,256]{1,0:T(2,128)S(1)}, f32[2,256]{1,0:T(2,128)S(1)}, u32[]{:S(2)}, u32[]{:S(2)}) %collective-permute-start.44) | collective-permute-done | bytes 2080 | tf_op jit(solution)/shard_map/ppermute | solution.py:575
  479.6 2.3 collective-permute-done.33
  483.4 2.0 collective-permute-start.49
  485.8 1.8 reshape.93
  487.5 4.6 collective-permute-done.50
  498.6 6.8 %collective-permute-done.51 = bf16[256,1024]{1,0:T(8,128)(2,1)S(1)} collective-permute-done((bf16[256,1024]{1,0:T(8,128)(2,1)S(1)}, bf16[256,1024]{1,0:T(8,128)(2,1)S(1)}, u32[]{:S(2)}, u32[]{:S(2)}) %collective-permute-start.51) | collective-permute-done | bytes 524320 | tf_op jit(solution)/shard_map/ppermute | solution.py:575
  (247 shorter events, 91.5 us)
Async XLA Ops:
  7.2 130.8 %all-gather.3.cloned.1.call-start = ((), (), s32[]{:S(2)}) async-start(), calls=%async_computation.2 | async-start | bytes 1310720 | tf_op jit(solution)/shard_map/all_gather | solution.py:665
  11.2 29.8 %collective-permute-start.5 = (bf16[256,512]{1,0:T(8,128)(2,1)S(1)}, bf16[256,512]{1,0:T(8,128)(2,1)}, u32[]{:S(2)}, u32[]{:S(2)}) collective-permute-start(bf16[256,512]{1,0:T(8,128)(2,1)S(1)} %pad_maximum_fusion.8), channel_id=1, source_target_pairs={{0,4},{4,8},{8,12},{12,0},{1,5},{5,9},{9,13},{13,1},{2,6},{6,10},{... | collective-permute-start | bytes 786440 | tf_op jit(solution)/shard_map/ppermute | solution.py:624
  14.3 28.3 %collective-permute-start.6 = (bf16[256,512]{1,0:T(8,128)(2,1)S(1)}, bf16[256,512]{1,0:T(8,128)(2,1)}, u32[]{:S(2)}, u32[]{:S(2)}) collective-permute-start(bf16[256,512]{1,0:T(8,128)(2,1)S(1)} %pad_maximum_fusion.8), channel_id=1, source_target_pairs={{0,8},{4,12},{8,0},{12,4},{1,9},{5,13},{9,1},{13,5},{2,10},{6,14},... | collective-permute-start | bytes 786440 | tf_op jit(solution)/shard_map/ppermute | solution.py:624
  16.9 14.8 %collective-permute-start = (bf16[1154,256]{1,0:T(8,128)(2,1)S(1)}, bf16[1154,256]{1,0:T(8,128)(2,1)S(1)}, u32[]{:S(2)}, u32[]{:S(2)}) collective-permute-start(bf16[1154,256]{1,0:T(8,128)(2,1)S(1)} %get-tuple-element.192), channel_id=1, source_target_pairs={{0,2},{2,0},{1,3},{3,1},{4,6},{6,4},{5,7},{7,5},{8,10},{10,8},{9,1... | collective-permute-start | bytes 1772552 | tf_op jit(solution)/shard_map/ppermute | solution.py:575
  19.8 16.6 %collective-permute-start.2 = (f32[12,256]{1,0:T(8,128)}, f32[12,256]{1,0:T(8,128)S(1)}, u32[]{:S(2)}, u32[]{:S(2)}) collective-permute-start(f32[12,256]{1,0:T(8,128)} %pack.1.own), channel_id=1, source_target_pairs={{0,2},{2,0},{1,3},{3,1},{4,6},{6,4},{5,7},{7,5},{8,10},{10,8},{9,1... | collective-permute-start | bytes 36872 | tf_op jit(solution)/shard_map/ppermute | solution.py:575
  20.4 17.2 %collective-permute-start.3 = (f32[12,256]{1,0:T(8,128)}, f32[12,256]{1,0:T(8,128)S(1)}, u32[]{:S(2)}, u32[]{:S(2)}) collective-permute-start(f32[12,256]{1,0:T(8,128)} %pack.1.own), channel_id=1, source_target_pairs={{0,1},{1,0},{2,3},{3,2},{4,5},{5,4},{6,7},{7,6},{8,9},{9,8},{10,11... | collective-permute-start | bytes 36872 | tf_op jit(solution)/shard_map/ppermute | solution.py:575
  32.1 19.5 %collective-permute-start.1 = (bf16[1184,512]{1,0:T(8,128)(2,1)S(1)}, bf16[1184,512]{1,0:T(8,128)(2,1)S(1)}, u32[]{:S(2)}, u32[]{:S(2)}) collective-permute-start(bf16[1184,512]{1,0:T(8,128)(2,1)S(1)} %bitcast.53), channel_id=1, source_target_pairs={{0,1},{1,0},{2,3},{3,2},{4,5},{5,4},{6,7},{7,6},{8,9},{9,8},{10,11... | collective-permute-start | bytes 3637256 | tf_op jit(solution)/shard_map/ppermute | solution.py:575
  47.6 26.3 %collective-permute-start.8 = (bf16[1024,256]{1,0:T(8,128)(2,1)}, bf16[1024,256]{1,0:T(8,128)(2,1)}, u32[]{:S(2)}, u32[]{:S(2)}) collective-permute-start(bf16[1024,256]{1,0:T(8,128)(2,1)} %get-tuple-element.223.refs_0_), channel_id=1, source_target_pairs={{0,2},{2,0},{1,3},{3,1},{4,6},{6,4},{5,7},{7,5},{8,10},{10,8},{9,1... | collective-permute-start | bytes 1572872 | tf_op jit(solution)/shard_map/ppermute | solution.py:575
  49.1 26.6 %collective-permute-start.10 = (bf16[1024,256]{1,0:T(8,128)(2,1)}, bf16[1024,256]{1,0:T(8,128)(2,1)}, u32[]{:S(2)}, u32[]{:S(2)}) collective-permute-start(bf16[1024,256]{1,0:T(8,128)(2,1)} %get-tuple-element.223.refs_0_), channel_id=1, source_target_pairs={{0,16},{16,0},{1,17},{17,1},{2,18},{18,2},{3,19},{19,3},{4,20},{20... | collective-permute-start | bytes 1572872 | tf_op jit(solution)/shard_map/ppermute | solution.py:575
  50.6 22.7 %collective-permute-start.11 = (bf16[1024,256]{1,0:T(8,128)(2,1)S(1)}, bf16[1024,256]{1,0:T(8,128)(2,1)}, u32[]{:S(2)}, u32[]{:S(2)}) collective-permute-start(bf16[1024,256]{1,0:T(8,128)(2,1)S(1)} %get-tuple-element.222.refs_1_), channel_id=1, source_target_pairs={{0,16},{16,0},{1,17},{17,1},{2,18},{18,2},{3,19},{19,3},{4,20},{20... | collective-permute-start | bytes 1572872 | tf_op jit(solution)/shard_map/ppermute | solution.py:575
  51.1 24.6 %collective-permute-start.9 = (bf16[1024,256]{1,0:T(8,128)(2,1)S(1)}, bf16[1024,256]{1,0:T(8,128)(2,1)}, u32[]{:S(2)}, u32[]{:S(2)}) collective-permute-start(bf16[1024,256]{1,0:T(8,128)(2,1)S(1)} %get-tuple-element.222.refs_1_), channel_id=1, source_target_pairs={{0,2},{2,0},{1,3},{3,1},{4,6},{6,4},{5,7},{7,5},{8,10},{10,8},{9,1... | collective-permute-start | bytes 1572872 | tf_op jit(solution)/shard_map/ppermute | solution.py:575
  51.6 87.9 %all-gather.5.cloned.1.call-start = ((), (), s32[]{:S(2)}) async-start(), calls=%async_computation.3 | async-start | bytes 1310720 | tf_op jit(solution)/shard_map/all_gather | solution.py:665
  73.3 12.1 %collective-permute-start.13 = (bf16[1024,256]{1,0:T(8,128)(2,1)}, bf16[1024,256]{1,0:T(8,128)(2,1)S(1)}, u32[]{:S(2)}, u32[]{:S(2)}) collective-permute-start(bf16[1024,256]{1,0:T(8,128)(2,1)} %collective-permute-done.11.refs_5_), channel_id=1, source_target_pairs={{0,2},{2,0},{1,3},{3,1},{4,6},{6,4},{5,7},{7,5},{8,10},{10,8},{9,1... | collective-permute-start | bytes 1572872 | tf_op jit(solution)/shard_map/ppermute | solution.py:575
  73.9 11.8 %collective-permute-start.12 = (bf16[1024,256]{1,0:T(8,128)(2,1)}, bf16[1024,256]{1,0:T(8,128)(2,1)S(1)}, u32[]{:S(2)}, u32[]{:S(2)}) collective-permute-start(bf16[1024,256]{1,0:T(8,128)(2,1)} %collective-permute-done.8.refs_2_), channel_id=1, source_target_pairs={{0,16},{16,0},{1,17},{17,1},{2,18},{18,2},{3,19},{19,3},{4,20},{20... | collective-permute-start | bytes 1572872 | tf_op jit(solution)/shard_map/ppermute | solution.py:575
  75.4 401.4 %reduce-scatter.5.cloned.1.call-start = ((), (), s32[]{:S(2)}) async-start(), calls=%async_computation.5 | async-start | bytes 5242880 | tf_op jit(solution)/shard_map/reduce_scatter | solution.py:716
  121.3 44.1 %collective-permute-start.14 = (bf16[1184,1024]{1,0:T(8,128)(2,1)}, bf16[1184,1024]{1,0:T(8,128)(2,1)}, u32[]{:S(2)}, u32[]{:S(2)}) collective-permute-start(bf16[1184,1024]{1,0:T(8,128)(2,1)} %convolution_convert_fusion.a_ref), channel_id=1, source_target_pairs={{0,1},{1,0},{2,3},{3,2},{4,5},{5,4},{6,7},{7,6},{8,9},{9,8},{10,11... | collective-permute-start | bytes 7274504 | tf_op jit(solution)/shard_map/ppermute | solution.py:575
  121.6 15.9 %collective-permute-start.15 = (bf16[1154,256]{1,0:T(8,128)(2,1)S(1)}, bf16[1154,256]{1,0:T(8,128)(2,1)S(1)}, u32[]{:S(2)}, u32[]{:S(2)}) collective-permute-start(bf16[1154,256]{1,0:T(8,128)(2,1)S(1)} %get-tuple-element.87), channel_id=1, source_target_pairs={{0,2},{2,0},{1,3},{3,1},{4,6},{6,4},{5,7},{7,5},{8,10},{10,8},{9,1... | collective-permute-start | bytes 1772552 | tf_op jit(solution)/shard_map/ppermute | solution.py:575
  137.9 36.3 %collective-permute-start.16 = (bf16[1184,512]{1,0:T(8,128)(2,1)S(1)}, bf16[1184,512]{1,0:T(8,128)(2,1)}, u32[]{:S(2)}, u32[]{:S(2)}) collective-permute-start(bf16[1184,512]{1,0:T(8,128)(2,1)S(1)} %bitcast.54), channel_id=1, source_target_pairs={{0,1},{1,0},{2,3},{3,2},{4,5},{5,4},{6,7},{7,6},{8,9},{9,8},{10,11... | collective-permute-start | bytes 3637256 | tf_op jit(solution)/shard_map/ppermute | solution.py:575
  138.0 25.8 %collective-permute-start.17 = (bf16[1024,512]{1,0:T(8,128)(2,1)}, bf16[1024,512]{1,0:T(8,128)(2,1)}, u32[]{:S(2)}, u32[]{:S(2)}) collective-permute-start(bf16[1024,512]{1,0:T(8,128)(2,1)} %all-gather.3.cloned.1.call-done.refs_0_), channel_id=1, source_target_pairs={{0,2},{2,0},{1,3},{3,1},{4,6},{6,4},{5,7},{7,5},{8,10},{10,8},{9,1... | collective-permute-start | bytes 3145736 | tf_op jit(solution)/shard_map/ppermute | solution.py:575
  139.6 34.0 %collective-permute-start.21 = (bf16[1024,512]{1,0:T(8,128)(2,1)}, bf16[1024,512]{1,0:T(8,128)(2,1)}, u32[]{:S(2)}, u32[]{:S(2)}) collective-permute-start(bf16[1024,512]{1,0:T(8,128)(2,1)} %all-gather.5.cloned.1.call-done.refs_4_), channel_id=1, source_target_pairs={{0,16},{16,0},{1,17},{17,1},{2,18},{18,2},{3,19},{19,3},{4,20},{20... | collective-permute-start | bytes 3145736 | tf_op jit(solution)/shard_map/ppermute | solution.py:575
  141.1 47.3 %collective-permute-start.18 = (bf16[1024,512]{1,0:T(8,128)(2,1)}, bf16[1024,512]{1,0:T(8,128)(2,1)}, u32[]{:S(2)}, u32[]{:S(2)}) collective-permute-start(bf16[1024,512]{1,0:T(8,128)(2,1)} %all-gather.3.cloned.1.call-done.refs_0_), channel_id=1, source_target_pairs={{0,16},{16,0},{1,17},{17,1},{2,18},{18,2},{3,19},{19,3},{4,20},{20... | collective-permute-start | bytes 3145736 | tf_op jit(solution)/shard_map/ppermute | solution.py:575
  163.9 26.3 %collective-permute-start.20 = (bf16[1024,512]{1,0:T(8,128)(2,1)}, bf16[1024,512]{1,0:T(8,128)(2,1)}, u32[]{:S(2)}, u32[]{:S(2)}) collective-permute-start(bf16[1024,512]{1,0:T(8,128)(2,1)} %all-gather.5.cloned.1.call-done.refs_4_), channel_id=1, source_target_pairs={{0,2},{2,0},{1,3},{3,1},{4,6},{6,4},{5,7},{7,5},{8,10},{10,8},{9,1... | collective-permute-start | bytes 3145736 | tf_op jit(solution)/shard_map/ppermute | solution.py:575
  165.3 44.7 %collective-permute-start.19 = (bf16[1024,512]{1,0:T(8,128)(2,1)}, bf16[1024,512]{1,0:T(8,128)(2,1)}, u32[]{:S(2)}, u32[]{:S(2)}) collective-permute-start(bf16[1024,512]{1,0:T(8,128)(2,1)} %collective-permute-done.17.refs_1_), channel_id=1, source_target_pairs={{0,16},{16,0},{1,17},{17,1},{2,18},{18,2},{3,19},{19,3},{4,20},{20... | collective-permute-start | bytes 3145736 | tf_op jit(solution)/shard_map/ppermute | solution.py:575
  173.6 37.7 %collective-permute-start.22 = (bf16[1024,512]{1,0:T(8,128)(2,1)}, bf16[1024,512]{1,0:T(8,128)(2,1)}, u32[]{:S(2)}, u32[]{:S(2)}) collective-permute-start(bf16[1024,512]{1,0:T(8,128)(2,1)} %collective-permute-done.21.refs_6_), channel_id=1, source_target_pairs={{0,2},{2,0},{1,3},{3,1},{4,6},{6,4},{5,7},{7,5},{8,10},{10,8},{9,1... | collective-permute-start | bytes 3145736 | tf_op jit(solution)/shard_map/ppermute | solution.py:575
  245.1 22.0 %collective-permute-start.23 = (bf16[1184,1024]{1,0:T(8,128)(2,1)}, bf16[1184,1024]{1,0:T(8,128)(2,1)S(1)}, u32[]{:S(2)}, u32[]{:S(2)}) collective-permute-start(bf16[1184,1024]{1,0:T(8,128)(2,1)} %get-tuple-element.94.a_ref), channel_id=1, source_target_pairs={{0,1},{1,0},{2,3},{3,2},{4,5},{5,4},{6,7},{7,6},{8,9},{9,8},{10,11... | collective-permute-start | bytes 7274504 | tf_op jit(solution)/shard_map/ppermute | solution.py:575
  255.0 228.4 %reduce-scatter.3.cloned.1.call-start = ((), (), s32[]{:S(2)}) async-start(), calls=%async_computation.4 | async-start | bytes 1638400 | tf_op jit(solution)/shard_map/reduce_scatter | solution.py:716
  255.0 12.0 %collective-permute-start.24 = (bf16[1184,512]{1,0:T(8,128)(2,1)}, bf16[1184,512]{1,0:T(8,128)(2,1)}, u32[]{:S(2)}, u32[]{:S(2)}) collective-permute-start(bf16[1184,512]{1,0:T(8,128)(2,1)} %get-tuple-element.100), channel_id=1, source_target_pairs={{0,1},{1,0},{2,3},{3,2},{4,5},{5,4},{6,7},{7,6},{8,9},{9,8},{10,11... | collective-permute-start | bytes 3637256 | tf_op jit(solution)/shard_map/ppermute | solution.py:575
  264.1 25.4 %collective-permute-start.26 = (bf16[1024,512]{1,0:T(8,128)(2,1)}, bf16[1024,512]{1,0:T(8,128)(2,1)}, u32[]{:S(2)}, u32[]{:S(2)}) collective-permute-start(bf16[1024,512]{1,0:T(8,128)(2,1)} %convolution_convert_fusion.4), channel_id=1, source_target_pairs={{0,2},{2,0},{1,3},{3,1},{4,6},{6,4},{5,7},{7,5},{8,10},{10,8},{9,1... | collective-permute-start | bytes 3145736 | tf_op jit(solution)/shard_map/ppermute | solution.py:575
  265.5 25.1 %collective-permute-start.25 = (bf16[1024,512]{1,0:T(8,128)(2,1)}, bf16[1024,512]{1,0:T(8,128)(2,1)}, u32[]{:S(2)}, u32[]{:S(2)}) collective-permute-start(bf16[1024,512]{1,0:T(8,128)(2,1)} %convolution_convert_fusion.5), channel_id=1, source_target_pairs={{0,16},{16,0},{1,17},{17,1},{2,18},{18,2},{3,19},{19,3},{4,20},{20... | collective-permute-start | bytes 3145736 | tf_op jit(solution)/shard_map/ppermute | solution.py:575
  327.4 9.1 %collective-permute-start.38 = (f32[10,256]{1,0:T(8,128)}, f32[10,256]{1,0:T(8,128)S(1)}, u32[]{:S(2)}, u32[]{:S(2)}) collective-permute-start(f32[10,256]{1,0:T(8,128)} %get-tuple-element.127), channel_id=1, source_target_pairs={{0,2},{2,0},{1,3},{3,1},{4,6},{6,4},{5,7},{7,5},{8,10},{10,8},{9,1... | collective-permute-start | bytes 30728 | tf_op jit(solution)/shard_map/ppermute | solution.py:575
  333.4 15.3 %collective-permute-start.46 = (bf16[1024,256]{1,0:T(8,128)(2,1)S(1)}, bf16[1024,256]{1,0:T(8,128)(2,1)S(1)}, u32[]{:S(2)}, u32[]{:S(2)}) collective-permute-start(bf16[1024,256]{1,0:T(8,128)(2,1)S(1)} %slice.283), channel_id=1, source_target_pairs={{0,2},{2,0},{1,3},{3,1},{4,6},{6,4},{5,7},{7,5},{8,10},{10,8},{9,1... | collective-permute-start | bytes 1572872 | tf_op jit(solution)/shard_map/ppermute | solution.py:575
  334.9 20.4 %collective-permute-start.30 = (bf16[1024,384]{1,0:T(8,128)(2,1)S(1)}, bf16[1024,384]{1,0:T(8,128)(2,1)S(1)}, u32[]{:S(2)}, u32[]{:S(2)}) collective-permute-start(bf16[1024,384]{1,0:T(8,128)(2,1)S(1)} %convolution_convert_fusion.6), channel_id=1, source_target_pairs={{0,16},{16,0},{1,17},{17,1},{2,18},{18,2},{3,19},{19,3},{4,20},{20... | collective-permute-start | bytes 2359304 | tf_op jit(solution)/shard_map/ppermute | solution.py:575
  341.4 78.4 %collective-permute-start.28 = (bf16[1184,1024]{1,0:T(8,128)(2,1)S(1)}, bf16[1184,1024]{1,0:T(8,128)(2,1)}, u32[]{:S(2)}, u32[]{:S(2)}) collective-permute-start(bf16[1184,1024]{1,0:T(8,128)(2,1)S(1)} %convolution_convert_fusion.1.a_ref), channel_id=1, source_target_pairs={{0,1},{1,0},{2,3},{3,2},{4,5},{5,4},{6,7},{7,6},{8,9},{9,8},{10,11... | collective-permute-start | bytes 7274504 | tf_op jit(solution)/shard_map/ppermute | solution.py:575
  341.5 52.1 %collective-permute-start.31 = (bf16[1024,384]{1,0:T(8,128)(2,1)S(1)}, bf16[1024,384]{1,0:T(8,128)(2,1)S(1)}, u32[]{:S(2)}, u32[]{:S(2)}) collective-permute-start(bf16[1024,384]{1,0:T(8,128)(2,1)S(1)} %convolution_convert_fusion.7), channel_id=1, source_target_pairs={{0,16},{16,0},{1,17},{17,1},{2,18},{18,2},{3,19},{19,3},{4,20},{20... | collective-permute-start | bytes 2359304 | tf_op jit(solution)/shard_map/ppermute | solution.py:575
  347.1 49.6 %collective-permute-start.47 = (bf16[1024,256]{1,0:T(8,128)(2,1)S(1)}, bf16[1024,256]{1,0:T(8,128)(2,1)S(1)}, u32[]{:S(2)}, u32[]{:S(2)}) collective-permute-start(bf16[1024,256]{1,0:T(8,128)(2,1)S(1)} %slice.285), channel_id=1, source_target_pairs={{0,16},{16,0},{1,17},{17,1},{2,18},{18,2},{3,19},{19,3},{4,20},{20... | collective-permute-start | bytes 1572872 | tf_op jit(solution)/shard_map/ppermute | solution.py:575
  348.7 43.3 %collective-permute-start.29 = (bf16[1024,256]{1,0:T(8,128)(2,1)S(1)}, bf16[1024,256]{1,0:T(8,128)(2,1)S(1)}, u32[]{:S(2)}, u32[]{:S(2)}) collective-permute-start(bf16[1024,256]{1,0:T(8,128)(2,1)S(1)} %slice.273), channel_id=1, source_target_pairs={{0,16},{16,0},{1,17},{17,1},{2,18},{18,2},{3,19},{19,3},{4,20},{20... | collective-permute-start | bytes 1572872 | tf_op jit(solution)/shard_map/ppermute | solution.py:575
  355.3 81.9 %collective-permute-start.27 = (bf16[1184,256]{1,0:T(8,128)(2,1)}, bf16[1184,256]{1,0:T(8,128)(2,1)}, u32[]{:S(2)}, u32[]{:S(2)}) collective-permute-start(bf16[1184,256]{1,0:T(8,128)(2,1)} %get-tuple-element.105), channel_id=1, source_target_pairs={{0,2},{2,0},{1,3},{3,1},{4,6},{6,4},{5,7},{7,5},{8,10},{10,8},{9,1... | collective-permute-start | bytes 1818632 | tf_op jit(solution)/shard_map/ppermute | solution.py:575
  392.0 78.9 %collective-permute-start.41 = (f32[10,256]{1,0:T(8,128)S(1)}, f32[10,256]{1,0:T(8,128)S(1)}, u32[]{:S(2)}, u32[]{:S(2)}) collective-permute-start(f32[10,256]{1,0:T(8,128)S(1)} %add.186.a_ref), channel_id=1, source_target_pairs={{0,16},{16,0},{1,17},{17,1},{2,18},{18,2},{3,19},{19,3},{4,20},{20... | collective-permute-start | bytes 30728 | tf_op jit(solution)/shard_map/ppermute | solution.py:575
  396.0 33.3 %collective-permute-start.32 = (bf16[1024,384]{1,0:T(8,128)(2,1)}, bf16[1024,384]{1,0:T(8,128)(2,1)}, u32[]{:S(2)}, u32[]{:S(2)}) collective-permute-start(bf16[1024,384]{1,0:T(8,128)(2,1)} %add_convert_fusion.3), channel_id=1, source_target_pairs={{0,2},{2,0},{1,3},{3,1},{4,6},{6,4},{5,7},{7,5},{8,10},{10,8},{9,1... | collective-permute-start | bytes 2359304 | tf_op jit(solution)/shard_map/ppermute | solution.py:575
  396.7 21.8 %collective-permute-start.48 = (bf16[1024,128]{1,0:T(8,128)(2,1)S(1)}, bf16[1024,128]{1,0:T(8,128)(2,1)S(1)}, u32[]{:S(2)}, u32[]{:S(2)}) collective-permute-start(bf16[1024,128]{1,0:T(8,128)(2,1)S(1)} %slice.287), channel_id=1, source_target_pairs={{0,2},{2,0},{1,3},{3,1},{4,6},{6,4},{5,7},{7,5},{8,10},{10,8},{9,1... | collective-permute-start | bytes 786440 | tf_op jit(solution)/shard_map/ppermute | solution.py:575
  433.8 33.4 %collective-permute-start.34 = (bf16[256,384]{1,0:T(8,128)(2,1)S(1)}, bf16[256,384]{1,0:T(8,128)(2,1)S(1)}, u32[]{:S(2)}, u32[]{:S(2)}) collective-permute-start(bf16[256,384]{1,0:T(8,128)(2,1)S(1)} %get-tuple-element.203), channel_id=1, source_target_pairs={{0,4},{4,8},{8,12},{12,0},{1,5},{5,9},{9,13},{13,1},{2,6},{6,10},{... | collective-permute-start | bytes 589832 | tf_op jit(solution)/shard_map/ppermute | solution.py:787
  435.5 33.2 %collective-permute-start.35 = (bf16[256,384]{1,0:T(8,128)(2,1)S(1)}, bf16[256,384]{1,0:T(8,128)(2,1)S(1)}, u32[]{:S(2)}, u32[]{:S(2)}) collective-permute-start(bf16[256,384]{1,0:T(8,128)(2,1)S(1)} %get-tuple-element.205), channel_id=1, source_target_pairs={{0,8},{4,12},{8,0},{12,4},{1,9},{5,13},{9,1},{13,5},{2,10},{6,14},... | collective-permute-start | bytes 589832 | tf_op jit(solution)/shard_map/ppermute | solution.py:787
  437.2 31.6 %collective-permute-start.36 = (bf16[256,384]{1,0:T(8,128)(2,1)S(1)}, bf16[256,384]{1,0:T(8,128)(2,1)S(1)}, u32[]{:S(2)}, u32[]{:S(2)}) collective-permute-start(bf16[256,384]{1,0:T(8,128)(2,1)S(1)} %get-tuple-element.204), channel_id=1, source_target_pairs={{0,12},{4,0},{8,4},{12,8},{1,13},{5,1},{9,5},{13,9},{2,14},{6,2},{... | collective-permute-start | bytes 589832 | tf_op jit(solution)/shard_map/ppermute | solution.py:787
  440.0 25.7 %collective-permute-start.44 = (f32[2,256]{1,0:T(2,128)S(1)}, f32[2,256]{1,0:T(2,128)S(1)}, u32[]{:S(2)}, u32[]{:S(2)}) collective-permute-start(f32[2,256]{1,0:T(2,128)S(1)} %add.188), channel_id=1, source_target_pairs={{0,8},{4,12},{8,0},{12,4},{1,9},{5,13},{9,1},{13,5},{2,10},{6,14},... | collective-permute-start | bytes 6152 | tf_op jit(solution)/shard_map/ppermute | solution.py:575
  465.7 16.1 %collective-permute-start.33 = (bf16[1184,256]{1,0:T(8,128)(2,1)}, bf16[1184,256]{1,0:T(8,128)(2,1)S(1)}, u32[]{:S(2)}, u32[]{:S(2)}) collective-permute-start(bf16[1184,256]{1,0:T(8,128)(2,1)} %get-tuple-element.121), channel_id=1, source_target_pairs={{0,2},{2,0},{1,3},{3,1},{4,6},{6,4},{5,7},{7,5},{8,10},{10,8},{9,1... | collective-permute-start | bytes 1818632 | tf_op jit(solution)/shard_map/ppermute | solution.py:575
  479.0 13.1 %collective-permute-start.50 = (bf16[256,1024]{1,0:T(8,128)(2,1)}, bf16[256,1024]{1,0:T(8,128)(2,1)}, u32[]{:S(2)}, u32[]{:S(2)}) collective-permute-start(bf16[256,1024]{1,0:T(8,128)(2,1)} %pad_maximum_fusion.7), channel_id=1, source_target_pairs={{0,2},{2,0},{1,3},{3,1},{4,6},{6,4},{5,7},{7,5},{8,10},{10,8},{9,1... | collective-permute-start | bytes 1572872 | tf_op jit(solution)/shard_map/ppermute | solution.py:575
  483.4 11.4 %collective-permute-start.49 = (bf16[256,640]{1,0:T(8,128)(2,1)}, bf16[256,640]{1,0:T(8,128)(2,1)}, u32[]{:S(2)}, u32[]{:S(2)}) collective-permute-start(bf16[256,640]{1,0:T(8,128)(2,1)} %reduce-scatter.3.cloned.1.call-done), channel_id=1, source_target_pairs={{0,16},{16,0},{1,17},{17,1},{2,18},{18,2},{3,19},{19,3},{4,20},{20... | collective-permute-start | bytes 983048 | tf_op jit(solution)/shard_map/ppermute | solution.py:575
  493.3 12.1 %collective-permute-start.51 = (bf16[256,1024]{1,0:T(8,128)(2,1)S(1)}, bf16[256,1024]{1,0:T(8,128)(2,1)S(1)}, u32[]{:S(2)}, u32[]{:S(2)}) collective-permute-start(bf16[256,1024]{1,0:T(8,128)(2,1)S(1)} %add_convert_fusion.5), channel_id=1, source_target_pairs={{0,16},{16,0},{1,17},{17,1},{2,18},{18,2},{3,19},{19,3},{4,20},{20... | collective-permute-start | bytes 1572872 | tf_op jit(solution)/shard_map/ppermute | solution.py:575
  (43 other events, 255.2 us)
Sparse Core Ops, SparseCore 0:
  51.8 28.7 all-gather.2
  82.7 27.3 all-gather.4
  255.1 77.6 reduce-scatter.4
  419.9 42.5 reduce-scatter.2

commit v6 on v5

--- a/solution.py
+++ b/solution.py
@@ -7,6 +7,7 @@
 from jax.experimental import pallas as pl
 from jax.experimental.pallas import tpu as pltpu
 from jax.sharding import Mesh, PartitionSpec as P
+
 
 D = 1024
 HD = 64
@@ -481,13 +482,15 @@
     )(place, own, far, own_other, far_other)
 
 
-def collect_kernel(place_ref, turn_ref, qkv_ref, up_ref, mine_ref, theirs_ref):
+def collect_kernel(place_ref, turn_ref, qkv_ref, up_ref, a_ref, b_ref, mine_ref, theirs_ref):
     core, side, half = place_ref[0], place_ref[1], place_ref[2]
     width = mine_ref.shape[1]
     one = width // 2
     for ref, at_side in ((mine_ref, side), (theirs_ref, 1 - side)):
         at = pl.ds(pl.multiple_of((2 * at_side + core) * width, width), width)
         ref[2:6, :] = turn_ref[:, at]
+    mine_ref[10:12, :] = a_ref[...]
+    theirs_ref[10:12, :] = b_ref[...]
     for at in range(4):
         ref = (mine_ref, theirs_ref)[at % 2]
         which = half if at < 2 else 1 - half
@@ -503,37 +506,36 @@
             ref[pl.ds(6 + 2 * which + part, 1), :] = up_ref[:, start : start + width]
 
 
-def collect(place, turn_sums, qkv_sums, up_sums):
+def collect(place, *sums):
     width = D // 4
     return pl.pallas_call(
         collect_kernel,
         name="collect",
         in_specs=[pl.BlockSpec(memory_space=pltpu.SMEM)]
-        + [pl.BlockSpec(memory_space=pltpu.VMEM)] * 3,
-        out_shape=[like((10, width), F32)] * 2,
-    )(place, turn_sums, qkv_sums, up_sums)
-
-
-def hand_out_kernel(a_ref, b_ref, c_ref, d_ref, *outs):
-    early = a_ref[...] + b_ref[...]
-    late = c_ref[...] + d_ref[...]
+        + [pl.BlockSpec(memory_space=pltpu.VMEM)] * 5,
+        out_shape=[like((12, width), F32)] * 2,
+    )(place, *sums)
+
+
+def hand_out_kernel(a_ref, b_ref, *outs):
+    sums = a_ref[...] + b_ref[...]
     width = a_ref.shape[1]
     for at in range(6):
-        outs[at][...] = early[at, :]
+        outs[at][...] = sums[at, :]
     for at in range(4):
-        outs[6][width * at : width * (at + 1)] = early[6 + at, :]
+        outs[6][width * at : width * (at + 1)] = sums[6 + at, :]
     for at in range(2):
-        outs[7 + at][...] = late[at, :]
-
-
-def hand_out(early, early_got, late, late_got):
-    width = early.shape[1]
+        outs[7 + at][...] = sums[10 + at, :]
+
+
+def hand_out(mine, got):
+    width = mine.shape[1]
     one = like((width,), F32)
     return pl.pallas_call(
         hand_out_kernel,
         name="hand_out",
         out_shape=[one] * 6 + [like((4 * width,), F32)] + [one] * 2,
-    )(early, early_got, late, late_got)
+    )(mine, got)
 
 
 def local(
@@ -574,6 +576,9 @@
     def swap(value, axis, size, bit=1):
         return lax.ppermute(value, axis, [(at, at ^ bit) for at in range(size)])
 
+    def shifted(value, shift):
+        return lax.ppermute(value, "row", [(at, (at + shift) % n_row) for at in range(n_row)])
+
     def across(value):
         return swap(value, "xa", n_xa)
 
@@ -620,10 +625,7 @@
     input_leaves = send_tokens(inputs)
     attn_shard = after(attn_shard, input_leaves)
     input_got = across(input_leaves)
-    pieces = [attn_shard] + [
-        lax.ppermute(attn_shard, "row", [(at, (at + shift) % n_row) for at in range(n_row)])
-        for shift in range(1, n_row)
-    ]
+    pieces = [attn_shard] + [shifted(attn_shard, shift) for shift in range(1, n_row)]
     cut = 2 * heads_half
     first_own = jnp.zeros((D, cut), BF16)
     second_own = jnp.zeros((D, cut), BF16)
@@ -649,12 +651,12 @@
     )
     small_far = across(small)
     vectors, qkv_bias, tile_bias = unpack(
-        place, small, small_far, beside(small), beside(small_far)
+        place, small, after(small_far, first_own, second_own), beside(small), beside(small_far)
     )
     out_bias_all, down_bias_all, gain_one, shift_one, gain_two, shift_two = (
         (vectors, pl.BlockSpec((None, 1, D), lambda i, *_, at=at: (at, 0, 0))) for at in range(6)
     )
-    wide_input = wide_tokens(inputs, input_got)
+    wide_input = wide_tokens(inputs, after(input_got, first_own, second_own))
     first_far_oth = over(after(first_far, wide_input, qkv_bias))
     second_far_oth = across(after(second_oth, wide_input, qkv_bias))
 
@@ -665,8 +667,7 @@
         return lax.all_gather(shard, "row", axis=0, tiled=True)
 
     own_a, own_b = gather(0), gather(1)
-    grad_leaves = after(send_tokens(cotangent), first_far_oth)
-    wide_grad = wide_tokens(cotangent, across(grad_leaves))
+    grad_got = across(after(send_tokens(cotangent), wide_input))
 
     wide_one, qkv, attn_weights = norm_qkv(
         wide_input,
@@ -688,9 +689,11 @@
     oth_b, far_b = over(own_b), across(own_b)
     attended, probs = attend(qkv)
     mixed = mm_nt(attended, attn_weights[:, 4 * three :]).astype(BF16)
+    mixed_other = beside(mixed)
+    wide_grad = wide_tokens(cotangent, after(grad_got, mixed))
     far_oth_a = over(after(far_a, mixed))
     middle_sum, wide_two = middle(
-        wide_input, mixed, beside(mixed), out_bias_all, gain_two, shift_two
+        wide_input, mixed, after(mixed_other, wide_grad), out_bias_all, gain_two, shift_two
     )
     far_oth_b = across(after(oth_b, wide_two))
     plan = (0, 1, 2, 3, 4, 6, 5, 7)
@@ -720,27 +723,27 @@
 
     lifted_other = beside(lifted_two)
     low_other = beside(low_theirs)
-    down_all = mm_tn(wide_grad, gate).astype(BF16)
+    up_over = mm_tn(wide_two, tiles(pre, 2, 4)).astype(BF16)
+    up_across = mm_tn(wide_two, tiles(pre, 6, 8)).astype(BF16)
+    up_over_got, up_across_got = over(up_over), across(up_across)
+    down_all = mm_tn(after(wide_grad, up_over, up_across), gate).astype(BF16)
     down_piece = scatter(down_all)
-    up_over = mm_tn(after(wide_two, down_all), tiles(pre, 2, 4)).astype(BF16)
-    up_across = mm_tn(after(wide_two, down_all), tiles(pre, 6, 8)).astype(BF16)
-    up_over_got, up_across_got = over(up_over), across(up_across)
 
     middle_grad, attn_grad, head_grad, turn_sums, out_mine, out_theirs = turn(
         place,
         middle_sum,
         wide_grad,
         lifted_two,
-        after(lifted_other, down_all, up_over, up_across),
+        after(lifted_other, down_all),
         low_mine,
         low_other,
         gain_two,
         down_bias_all,
         attn_weights,
     )
-    up_over_got, up_across_got, _ = lax.optimization_barrier(
-        (up_over_got, up_across_got, attn_grad)
-    )
+    out_all = mm_tn(attn_grad, attended).astype(BF16)
+    out_over_got = over(out_all[:, 2 * heads_half :])
+    up_over_got, up_across_got, _ = lax.optimization_barrier((up_over_got, up_across_got, out_all))
     up_a = wide_add(mm_tn(wide_two, tiles(pre, 0, 2)), up_over_got)
     up_b = wide_add(mm_tn(wide_two, tiles(pre, 4, 6)), up_across_got)
     up_a_got, up_b_got = across(up_a[:, quarter:]), over(up_b[:, quarter:])
@@ -752,67 +755,82 @@
         both = jnp.concatenate([first, second]).reshape(images, PAD, width)
         return both[:, :SEQ].reshape(tokens_here, width)
 
-    far_oth = mm_tn(wide_one, dqkv[:, 3 * three :]).astype(BF16)
-    near_oth = mm_tn(wide_one, dqkv[:, 2 * three : 3 * three]).astype(BF16)
-    far_oth_got, near_oth_got = over(far_oth), over(near_oth)
+    split = 3 * three + cut
+    far_oth_qk = mm_tn(wide_one, dqkv[:, 3 * three : split]).astype(BF16)
+    far_oth_v = mm_tn(wide_one, dqkv[:, split:]).astype(BF16)
+    qk_got, v_got = over(far_oth_qk), across(far_oth_v)
     lifted_one = mm_nt(
-        after(dqkv, far_oth, near_oth), attn_weights[:, : 4 * three]
+        after(dqkv, far_oth_qk, far_oth_v), attn_weights[:, : 4 * three]
     ).astype(BF16)
     lifted_one_other = beside(lifted_one)
 
-    out_all = mm_tn(after(attn_grad, lifted_one), attended).astype(BF16)
-    out_over_got = over(out_all[:, 2 * heads_half :])
-    mine_early, theirs_early = collect(place, turn_sums, qkv_sums, up_sums)
-    early = mine_early + across(theirs_early)
-
-    far_oth_got = after(far_oth_got, out_all)
-    far_own = wide_add(mm_tn(wide_one, dqkv[:, three : 2 * three]), far_oth_got)
+    out_own = wide_add(out_all[:, : 2 * heads_half], after(out_over_got, lifted_one))
+    out_far_got = across(out_own[:, heads_half:])
+    near_oth = wide_add(
+        mm_tn(wide_one, dqkv[:, 2 * three : 3 * three]),
+        jnp.pad(after(v_got, out_own), ((0, 0), (cut, 0))),
+    )
+    near_oth_got = over(near_oth)
+    far_own = wide_add(
+        mm_tn(wide_one, dqkv[:, three : 2 * three]),
+        jnp.pad(after(qk_got, near_oth), ((0, 0), (0, three - cut))),
+    )
     far_own_got = across(far_own)
-    near_own = wide_add(mm_tn(wide_one, dqkv[:, :three]), near_oth_got)
-    out_own = wide_add(out_all[:, : 2 * heads_half], after(out_over_got, near_own))
-    out_far_got = across(out_own[:, heads_half:])
+    near_own = mm_tn(after(wide_one, far_own), dqkv[:, :three])
+    up_sum = jnp.concatenate(
+        [
+            wide_add(up_a[:, :quarter], after(up_a_got, far_own)),
+            wide_add(up_b[:, :quarter], up_b_got),
+            wide_add(out_own[:, :heads_half], out_far_got),
+        ],
+        axis=1,
+    )
+    up_piece = same_half(scatter(up_sum))
     input_mine, input_theirs, late_mine, late_theirs = last(
-        place, wide_input, middle_grad, lifted_one, after(lifted_one_other, out_own), gain_one
-    )
-    outputs = to_feature_blocks(out_mine, after(out_got, input_mine), BF16)
-
-    near_sum = wide_add(near_own, after(far_own_got, input_mine))
+        place,
+        wide_input,
+        middle_grad,
+        lifted_one,
+        after(lifted_one_other, near_own, up_sum),
+        gain_one,
+    )
+    mine_sums, theirs_sums = collect(
+        place, turn_sums, qkv_sums, up_sums, late_mine, late_theirs
+    )
+
+    near_sum = (near_own + near_oth_got.astype(F32) + after(far_own_got, mine_sums).astype(F32)).astype(
+        BF16
+    )
     strip = D // n_row
 
     def rows_of(value, shift):
         return lax.dynamic_slice_in_dim(value, (my_row + shift) % n_row * strip, strip, 0)
 
+    gots = [shifted(rows_of(near_sum, shift), shift) for shift in range(1, n_row)]
+    input_got = across(after(input_theirs, near_sum))
+    sums = mine_sums + across(after(theirs_sums, near_sum))
+    steps = [("row", n_row, 1 << bit) for bit in range(n_row.bit_length() - 1)]
+    steps += [("dp", n_dp, 1 << bit) for bit in range(n_dp.bit_length() - 1)]
+    for step in steps[:-1]:
+        sums = sums + swap(sums, *step)
+    sums = hand_out(sums, swap(sums, *steps[-1]))
+    outputs = to_feature_blocks(out_mine, after(out_got, near_sum), BF16)
+
+    def some(value, *which):
+        return jnp.concatenate([tiles(value, at, at + 1) for at in which], axis=1)
+
+    down_piece = after(down_piece, near_sum)
+    down_x = wide_add(some(down_piece, 0, 4, 2, 5), across(some(down_piece, 1, 6, 3, 7)))
+
     qkv_total = rows_of(near_sum, 0).astype(F32)
-    for shift in range(1, n_row):
-        got = lax.ppermute(
-            rows_of(near_sum, shift), "row", [(at, (at + shift) % n_row) for at in range(n_row)]
-        )
+    for got in gots:
         qkv_total = qkv_total + got.astype(F32)
     qkv_piece = same_half(qkv_total.astype(BF16))
     qkv_other = over(qkv_piece)
-
-    input_theirs = after(input_theirs, far_own_got)
-    input_grad = to_feature_blocks(input_mine, across(input_theirs), F32)
-
-    up_piece = same_half(
-        scatter(
-            jnp.concatenate(
-                [
-                    wide_add(up_a[:, :quarter], up_a_got),
-                    wide_add(up_b[:, :quarter], up_b_got),
-                    wide_add(out_own[:, :heads_half], out_far_got),
-                ],
-                axis=1,
-            )
-        )
-    )
+    down_got = over(down_x)
+    input_grad = to_feature_blocks(input_mine, input_got, F32)
     up_other = over(up_piece)
 
-    def some(value, *which):
-        return jnp.concatenate([tiles(value, at, at + 1) for at in which], axis=1)
-
-    down_x = wide_add(some(down_piece, 0, 4, 2, 5), across(some(down_piece, 1, 6, 3, 7)))
-    down_got = over(down_x)
     down_total = down_x.astype(F32) + jnp.concatenate(
         [down_got[:, half:], down_got[:, :half]], axis=1
     ).astype(F32)
@@ -832,13 +850,6 @@
         both_halves(qkv_piece, qkv_other, heads_half * at, heads_half * (at + 1))
         for at in range(3)
     )
-
-    late = late_mine + across(late_theirs)
-    steps = [("row", n_row, 1 << bit) for bit in range(n_row.bit_length() - 1)]
-    steps += [("dp", n_dp, 1 << bit) for bit in range(n_dp.bit_length() - 1)]
-    for step in steps[:-1]:
-        early, late = early + swap(early, *step), late + swap(late, *step)
-    sums = hand_out(early, swap(early, *steps[-1]), late, swap(late, *steps[-1]))
 
     return (
         outputs,
@@ -875,10 +886,10 @@
     out_specs = (
         (tokens, tokens, rows, rows, rows, vec, vec, cols, vec, rows, vec, cols) + (vec,) * 5
     )
+
+    def body(*args):
+        return local(sizes, *args)
+
     return jax.shard_map(
-        functools.partial(local, sizes),
-        mesh=split,
-        in_specs=in_specs,
-        out_specs=out_specs,
-        check_vma=False,
-    )
+        body, mesh=split, in_specs=in_specs, out_specs=out_specs, check_vma=False
+    )

time: 519 us -> 495 us (0.954)
  waiting for transfers between devices: 220 us -> 204 us
  starting transfers between devices: 57.8 us -> 46.8 us
    ppermute x46 -> x43, waiting for transfers between devices: 218 us -> 187 us  [swap(): return lax.ppermute(value, axis, [(at, at ^ bit) for at in range(size)])]
    ppermute x6, waiting for transfers between devices: 1.64 us -> 16.6 us  [shifted(): lax.ppermute(value, 'row', [(at, (at + shift) % n_row) for at in range(n_...]
    ppermute x46 -> x43, starting transfers between devices: 44.2 us -> 35.9 us  [swap(): return lax.ppermute(value, axis, [(at, at ^ bit) for at in range(size)])]
    dot_general x10 -> x11, matrix products: 37.7 us -> 38.8 us  [mm_tn(): lax.dot_general(a, b, (((0,), (0,)), ((), ())), preferred_element_type=F32)]
  transfers between devices with their start and end apart: 56 -> 53, of which waited for: 22 -> 23; matrix products, arithmetic and copies ran while one was open for 17% -> 18% of each run, Pallas kernels for 18% -> 19%
where the time goes in v6:
time: 495 us; the launch traced here: 489 us
  waiting for transfers between devices  204 us (41%)
  Pallas kernels  126 us (25%)
  matrix products  48.7 us (10%)
  starting transfers between devices  46.8 us (9%)
  local copies, waits for them, and re-layouts  27.8 us (6%)
  other arithmetic  20.9 us (4%)
  between operations  14.7 us (3%)
    ppermute x43, waiting for transfers between devices, swap(): return lax.ppermute(value, axis, [(at, at ^ bit) for at in range(size)])  187 us
    dot_general x11, matrix products, mm_tn(): lax.dot_general(a, b, (((0,), (0,)), ((), ())), preferred_element_type=F32)  38.8 us
    ppermute x43, starting transfers between devices, swap(): return lax.ppermute(value, axis, [(at, at ^ bit) for at in range(size)])  35.9 us
    pallas_call x1, Pallas kernels, mlp(): pl.pallas_call(functools.partial(mlp_kernel, plan), name='mlp', grid_spec...  34 us
    pallas_call x1, Pallas kernels, attend_back(): pl.pallas_call(attend_back_kernel, grid=(pairs, held), name='attend_back'...  27 us
    pallas_call x1, Pallas kernels, attend(): pl.pallas_call(attend_kernel, grid=(pairs, held), name='attend', in_specs...  20.2 us
    ppermute x6, waiting for transfers between devices, shifted(): lax.ppermute(value, 'row', [(at, (at + shift) % n_row) for at in range(n_...  16.6 us
    pallas_call x1, Pallas kernels, turn(): pl.pallas_call(turn_kernel, name='turn', grid_spec=pltpu.PrefetchScalarGr...  13.8 us
  transfers between devices with their start and end apart: 53, of which 23 were waited for; matrix products, arithmetic and copies ran while one was open for 18% of the time, Pallas kernels for 19%

profile of v6, /device:TPU:0, one launch (start us, length us, event | category | flops | bytes accessed | tf_op | source)
XLA Modules:
  0.0 489.2 jit_solution(6649636107036605259)
XLA Ops:
  11.9 5.1 %collective-permute-start.3 = (bf16[256,512]{1,0:T(8,128)(2,1)S(1)}, bf16[256,512]{1,0:T(8,128)(2,1)S(1)}, u32[]{:S(2)}, u32[]{:S(2)}) collective-permute-start(bf16[256,512]{1,0:T(8,128)(2,1)S(1)} %pad_maximum_fusion.8), channel_id=1, source_target_pairs={{0,12},{4,0},{8,4},{12,8},{1,13},{5,1},{9,5},{13,9},{2,14},{6,2},{... | collective-permute-start | bytes 786440 | tf_op jit(solution)/shard_map/ppermute | solution.py:580
  21.1 13.8 %collective-permute-done.1 = bf16[256,512]{1,0:T(8,128)(2,1)} collective-permute-done((bf16[256,512]{1,0:T(8,128)(2,1)S(1)}, bf16[256,512]{1,0:T(8,128)(2,1)}, u32[]{:S(2)}, u32[]{:S(2)}) %collective-permute-start.1) | collective-permute-done | bytes 262176 | tf_op jit(solution)/shard_map/ppermute | solution.py:580
  36.6 2.8 collective-permute-done.2
  56.2 1.8 pad_maximum_fusion.x_ref
  58.0 7.2 %collective-permute-done.11.refs_5_ = bf16[1024,256]{1,0:T(8,128)(2,1)} collective-permute-done((bf16[1024,256]{1,0:T(8,128)(2,1)}, bf16[1024,256]{1,0:T(8,128)(2,1)}, u32[]{:S(2)}, u32[]{:S(2)}) %collective-permute-start.11) | collective-permute-done | bytes 524320 | tf_op jit(solution)/shard_map/ppermute | solution.py:577
  65.2 12.0 %collective-permute-done.8.refs_2_ = bf16[1024,256]{1,0:T(8,128)(2,1)} collective-permute-done((bf16[1024,256]{1,0:T(8,128)(2,1)}, bf16[1024,256]{1,0:T(8,128)(2,1)}, u32[]{:S(2)}, u32[]{:S(2)}) %collective-permute-start.8) | collective-permute-done | bytes 524320 | tf_op jit(solution)/shard_map/ppermute | solution.py:577
  80.7 10.0 %collective-permute-done.12.refs_6_ = bf16[1024,256]{1,0:T(8,128)(2,1)S(1)} collective-permute-done((bf16[1024,256]{1,0:T(8,128)(2,1)}, bf16[1024,256]{1,0:T(8,128)(2,1)S(1)}, u32[]{:S(2)}, u32[]{:S(2)}) %collective-permute-start.12) | collective-permute-done | bytes 524320 | tf_op jit(solution)/shard_map/ppermute | solution.py:577
  90.6 2.1 collective-permute-done.13.refs_7_
  93.5 10.1 %norm_qkv.1 = (bf16[1184,1024]{1,0:T(8,128)(2,1)}, bf16[1184,1536]{1,0:T(8,128)(2,1)}, bf16[1024,2048]{1,0:T(8,128)(2,1)}) custom-call(bf16[1184,1024]{1,0:T(8,128)(2,1)} %pad_maximum_fusion.x_ref, f32[6,1,1024]{2,1,0:T(1,128)} %get-tuple-element.89.gain_ref.shift_ref.bias_ref, f32[6,1,1024]{2,1,0:T(1,128)} %get-tuple-element.89.gain_ref.shift_ref.bias_ref, ...), custom_call_target="tpu_custom_call" | custom-call | flops 3724541952 | bytes 19398656 | tf_op jit(solution)/shard_map/norm_qkv/pallas_call | solution.py:111
  103.7 20.2 %attend.1 = (bf16[1184,512]{1,0:T(8,128)(2,1)}, bf16[2,8,592,592]{3,2,1,0:T(8,128)(2,1)}) custom-call(bf16[1184,1536]{1,0:T(8,128)(2,1)} %get-tuple-element.93.qkv_ref), custom_call_target="tpu_custom_call" | custom-call | flops 17226006528 | bytes 48496640 | tf_op jit(solution)/shard_map/attend/pallas_call | solution.py:140
  123.9 4.5 convolution_convert_fusion.a_ref
  132.6 22.7 %collective-permute-done.17.refs_1_ = bf16[1024,512]{1,0:T(8,128)(2,1)} collective-permute-done((bf16[1024,512]{1,0:T(8,128)(2,1)}, bf16[1024,512]{1,0:T(8,128)(2,1)}, u32[]{:S(2)}, u32[]{:S(2)}) %collective-permute-start.17) | collective-permute-done | bytes 1048608 | tf_op jit(solution)/shard_map/ppermute | solution.py:577
  157.7 1.8 pad_maximum_fusion.1.dy_ref
  159.5 6.7 %middle.1 = (f32[1184,1024]{1,0:T(8,128)}, bf16[1184,1024]{1,0:T(8,128)(2,1)}) custom-call(bf16[1184,1024]{1,0:T(8,128)(2,1)} %pad_maximum_fusion.x_ref, bf16[1184,1024]{1,0:T(8,128)(2,1)} %convolution_convert_fusion.a_ref, bf16[1184,1024]{1,0:T(8,128)(2,1)} %collective-permute-done.14.b_ref, f32[6,1,1024]{2,1,0:T(1,128)} %get-tuple-element.89.gain_ref.shift_ref.bias_ref, ...), custom_call_target="tpu_custom_call" | custom-call | flops 24248320 | bytes 14548992 | tf_op jit(solution)/shard_map/middle/pallas_call | solution.py:201
  166.8 10.9 %collective-permute-done.20.refs_5_ = bf16[1024,512]{1,0:T(8,128)(2,1)} collective-permute-done((bf16[1024,512]{1,0:T(8,128)(2,1)}, bf16[1024,512]{1,0:T(8,128)(2,1)}, u32[]{:S(2)}, u32[]{:S(2)}) %collective-permute-start.20) | collective-permute-done | bytes 1048608 | tf_op jit(solution)/shard_map/ppermute | solution.py:577
  177.8 3.9 collective-permute-done.18.refs_2_
  181.7 20.5 %collective-permute-done.19.refs_3_ = bf16[1024,512]{1,0:T(8,128)(2,1)} collective-permute-done((bf16[1024,512]{1,0:T(8,128)(2,1)}, bf16[1024,512]{1,0:T(8,128)(2,1)}, u32[]{:S(2)}, u32[]{:S(2)}) %collective-permute-start.19) | collective-permute-done | bytes 1048608 | tf_op jit(solution)/shard_map/ppermute | solution.py:577
  203.1 34.0 %mlp.1 = (bf16[1184,2048]{1,0:T(8,128)(2,1)}, bf16[1184,2048]{1,0:T(8,128)(2,1)}, f32[1184,512]{1,0:T(8,128)}, bf16[1184,512]{1,0:T(8,128)(2,1)}, bf16[1184,1024]{1,0:T(8,128)(2,1)}, /*index=5*/f32[1,2048]{1,0:T(1,128)}) custom-call(s32[3]{0:T(128)} %pad_add_fusion.place_ref, bf16[1184,1024]{1,0:T(8,128)(2,1)} %get-tuple-element.100.n_ref, ...), custom_call_target="tpu_custom_call" | custom-call | flops 19864223744 | bytes 29097984 | tf_op jit(solution)/shard_map/mlp/pallas_call | solution.py:270
  237.2 4.7 convolution_convert_fusion.4
  241.9 4.0 convolution_convert_fusion.5
  246.3 7.2 %convolution_convert_fusion.2 = bf16[1024,2048]{1,0:T(8,128)(2,1)} fusion(bf16[1184,1024]{1,0:T(8,128)(2,1)S(1)} %copy-done.2, bf16[1184,2048]{1,0:T(8,128)(2,1)S(1)} %copy-done.25), kind=kOutput, calls=%fused_computation.2 | convolution fusion | flops 4968153088 | bytes 11468800 | tf_op jit(solution)/shard_map/dot_general | solution.py:34
  257.2 13.8 %turn.1 = (f32[1184,1024]{1,0:T(8,128)}, bf16[1184,1024]{1,0:T(8,128)(2,1)}, bf16[1184,512]{1,0:T(8,128)(2,1)}, f32[4,1024]{1,0:T(4,128)}, bf16[1184,256]{1,0:T(8,128)(2,1)}, /*index=5*/bf16[1184,256]{1,0:T(8,128)(2,1)}) custom-call(s32[3]{0:T(128)} %pad_add_fusion.place_ref, f32[1184,1024]{1,0:T(8,128)} %get-tuple-element.99.h_ref, ...), custom_call_target="tpu_custom_call" | custom-call | flops 1241513984 | bytes 24248320 | tf_op jit(solution)/shard_map/turn/pallas_call | solution.py:347
  270.9 3.7 convolution_convert_fusion.3
  274.7 4.4 collective-permute-done.25
  280.3 3.2 add_convert_fusion.1
  283.5 3.2 add_convert_fusion
  286.7 27.0 %attend_back.1 = (bf16[1184,1536]{1,0:T(8,128)(2,1)}, f32[1,1536]{1,0:T(1,128)}) custom-call(bf16[1184,1536]{1,0:T(8,128)(2,1)} %get-tuple-element.93.qkv_ref, bf16[2,8,592,592]{3,2,1,0:T(8,128)(2,1)} %get-tuple-element.119.p_ref, bf16[1184,512]{1,0:T(8,128)(2,1)} %get-tuple-element.122.g_ref), custom_call_target="tpu_custom_call" | custom-call | flops 21532508160 | bytes 60620800 | tf_op jit(solution)/shard_map/attend_back/pallas_call | solution.py:176
  313.8 2.8 convolution_convert_fusion.7
  316.7 2.8 convolution_convert_fusion.6
  320.0 5.5 %convolution_convert_fusion.1.a_ref = bf16[1184,1024]{1,0:T(8,128)(2,1)} fusion(bf16[1184,1536]{1,0:T(8,128)(2,1)S(1)} %copy-done.23, bf16[1024,2048]{1,0:T(8,128)(2,1)S(1)} %copy-done.3), kind=kOutput, calls=%fused_computation.1 | convolution fusion | flops 3725754368 | bytes 9207808 | tf_op jit(solution)/shard_map/dot_general | solution.py:30
  330.1 4.2 collective-permute-done.30
  335.3 2.5 add_convert_fusion.4
  337.7 7.8 %collective-permute-done.28 = bf16[1024,256]{1,0:T(8,128)(2,1)S(1)} collective-permute-done((bf16[1024,256]{1,0:T(8,128)(2,1)S(1)}, bf16[1024,256]{1,0:T(8,128)(2,1)S(1)}, u32[]{:S(2)}, u32[]{:S(2)}) %collective-permute-start.28) | collective-permute-done | bytes 524320 | tf_op jit(solution)/shard_map/ppermute | solution.py:577
  345.6 2.4 add_convert_fusion.3
  348.0 2.4 fusion.6
  350.6 1.9 copy.54
  352.5 4.3 collective-permute-done.35
  358.0 23.0 %collective-permute-done.36 = bf16[1024,128]{1,0:T(8,128)(2,1)S(1)} collective-permute-done((bf16[1024,128]{1,0:T(8,128)(2,1)S(1)}, bf16[1024,128]{1,0:T(8,128)(2,1)S(1)}, u32[]{:S(2)}, u32[]{:S(2)}) %collective-permute-start.36) | collective-permute-done | bytes 262176 | tf_op jit(solution)/shard_map/ppermute | solution.py:577
  382.2 8.8 %last.1 = (f32[1184,256]{1,0:T(8,128)}, bf16[1184,256]{1,0:T(8,128)(2,1)}, f32[2,256]{1,0:T(2,128)}, f32[2,256]{1,0:T(2,128)}) custom-call(s32[3]{0:T(128)} %pad_add_fusion.place_ref, bf16[1184,1024]{1,0:T(8,128)(2,1)} %pad_maximum_fusion.x_ref, f32[1184,1024]{1,0:T(8,128)} %get-tuple-element.132.dh_ref, bf16[1184,1024]{1,0:T(8,128)(2,1)} %convolution_convert_fusion.1.a_ref, ...), custom_call_target="tpu_custom_call" | custom-call | flops 24248320 | bytes 14548992 | tf_op jit(solution)/shard_map/last/pallas_call | solution.py:407
  394.7 3.2 collective-permute-done.42
  398.0 2.7 collective-permute-start.43
  400.8 3.8 collective-permute-start.40
  404.8 2.8 collective-permute-start.44
  408.7 31.4 %collective-permute-done.44 = f32[12,256]{1,0:T(8,128)S(1)} collective-permute-done((f32[12,256]{1,0:T(8,128)S(1)}, f32[12,256]{1,0:T(8,128)S(1)}, u32[]{:S(2)}, u32[]{:S(2)}) %collective-permute-start.44) | collective-permute-done | bytes 12320 | tf_op jit(solution)/shard_map/ppermute | solution.py:577
  452.3 8.3 %collective-permute-done.37 = bf16[1184,256]{1,0:T(8,128)(2,1)S(1)} collective-permute-done((bf16[1184,256]{1,0:T(8,128)(2,1)}, bf16[1184,256]{1,0:T(8,128)(2,1)S(1)}, u32[]{:S(2)}, u32[]{:S(2)}) %collective-permute-start.37) | collective-permute-done | bytes 606240 | tf_op jit(solution)/shard_map/ppermute | solution.py:577
  464.1 1.8 reshape.93
  465.8 2.9 collective-permute-done.47
  475.2 5.5 %collective-permute-done.48 = bf16[256,1024]{1,0:T(8,128)(2,1)S(1)} collective-permute-done((bf16[256,1024]{1,0:T(8,128)(2,1)S(1)}, bf16[256,1024]{1,0:T(8,128)(2,1)S(1)}, u32[]{:S(2)}, u32[]{:S(2)}) %collective-permute-start.48) | collective-permute-done | bytes 524320 | tf_op jit(solution)/shard_map/ppermute | solution.py:577
  (222 shorter events, 82.7 us)
Async XLA Ops:
  7.2 121.7 %all-gather.3.cloned.1.call-start = ((), (), s32[]{:S(2)}) async-start(), calls=%async_computation.2 | async-start | bytes 1310720 | tf_op jit(solution)/shard_map/all_gather | solution.py:667
  11.9 28.1 %collective-permute-start.3 = (bf16[256,512]{1,0:T(8,128)(2,1)S(1)}, bf16[256,512]{1,0:T(8,128)(2,1)S(1)}, u32[]{:S(2)}, u32[]{:S(2)}) collective-permute-start(bf16[256,512]{1,0:T(8,128)(2,1)S(1)} %pad_maximum_fusion.8), channel_id=1, source_target_pairs={{0,12},{4,0},{8,4},{12,8},{1,13},{5,1},{9,5},{13,9},{2,14},{6,2},{... | collective-permute-start | bytes 786440 | tf_op jit(solution)/shard_map/ppermute | solution.py:580
  17.0 22.3 %collective-permute-start.2 = (bf16[256,512]{1,0:T(8,128)(2,1)S(1)}, bf16[256,512]{1,0:T(8,128)(2,1)S(1)}, u32[]{:S(2)}, u32[]{:S(2)}) collective-permute-start(bf16[256,512]{1,0:T(8,128)(2,1)S(1)} %pad_maximum_fusion.8), channel_id=1, source_target_pairs={{0,8},{4,12},{8,0},{12,4},{1,9},{5,13},{9,1},{13,5},{2,10},{6,14},... | collective-permute-start | bytes 786440 | tf_op jit(solution)/shard_map/ppermute | solution.py:580
  17.1 17.9 %collective-permute-start.1 = (bf16[256,512]{1,0:T(8,128)(2,1)S(1)}, bf16[256,512]{1,0:T(8,128)(2,1)}, u32[]{:S(2)}, u32[]{:S(2)}) collective-permute-start(bf16[256,512]{1,0:T(8,128)(2,1)S(1)} %pad_maximum_fusion.8), channel_id=1, source_target_pairs={{0,4},{4,8},{8,12},{12,0},{1,5},{5,9},{9,13},{13,1},{2,6},{6,10},{... | collective-permute-start | bytes 786440 | tf_op jit(solution)/shard_map/ppermute | solution.py:580
  18.1 22.7 %collective-permute-start = (bf16[1154,256]{1,0:T(8,128)(2,1)S(1)}, bf16[1154,256]{1,0:T(8,128)(2,1)S(1)}, u32[]{:S(2)}, u32[]{:S(2)}) collective-permute-start(bf16[1154,256]{1,0:T(8,128)(2,1)S(1)} %get-tuple-element.208), channel_id=1, source_target_pairs={{0,2},{2,0},{1,3},{3,1},{4,6},{6,4},{5,7},{7,5},{8,10},{10,8},{9,1... | collective-permute-start | bytes 1772552 | tf_op jit(solution)/shard_map/ppermute | solution.py:577
  41.9 13.9 %collective-permute-start.4 = (bf16[1184,512]{1,0:T(8,128)(2,1)S(1)}, bf16[1184,512]{1,0:T(8,128)(2,1)S(1)}, u32[]{:S(2)}, u32[]{:S(2)}) collective-permute-start(bf16[1184,512]{1,0:T(8,128)(2,1)S(1)} %bitcast.55), channel_id=1, source_target_pairs={{0,1},{1,0},{2,3},{3,2},{4,5},{5,4},{6,7},{7,6},{8,9},{9,8},{10,11... | collective-permute-start | bytes 3637256 | tf_op jit(solution)/shard_map/ppermute | solution.py:577
  43.4 8.8 %collective-permute-start.6 = (f32[12,256]{1,0:T(8,128)}, f32[12,256]{1,0:T(8,128)S(1)}, u32[]{:S(2)}, u32[]{:S(2)}) collective-permute-start(f32[12,256]{1,0:T(8,128)} %pack.1.own), channel_id=1, source_target_pairs={{0,1},{1,0},{2,3},{3,2},{4,5},{5,4},{6,7},{7,6},{8,9},{9,8},{10,11... | collective-permute-start | bytes 36872 | tf_op jit(solution)/shard_map/ppermute | solution.py:577
  50.1 15.1 %collective-permute-start.11 = (bf16[1024,256]{1,0:T(8,128)(2,1)}, bf16[1024,256]{1,0:T(8,128)(2,1)}, u32[]{:S(2)}, u32[]{:S(2)}) collective-permute-start(bf16[1024,256]{1,0:T(8,128)(2,1)} %copy-done.9), channel_id=1, source_target_pairs={{0,16},{16,0},{1,17},{17,1},{2,18},{18,2},{3,19},{19,3},{4,20},{20... | collective-permute-start | bytes 1572872 | tf_op jit(solution)/shard_map/ppermute | solution.py:577
  51.6 29.0 %collective-permute-start.9 = (bf16[1024,256]{1,0:T(8,128)(2,1)}, bf16[1024,256]{1,0:T(8,128)(2,1)}, u32[]{:S(2)}, u32[]{:S(2)}) collective-permute-start(bf16[1024,256]{1,0:T(8,128)(2,1)} %copy-done.9), channel_id=1, source_target_pairs={{0,2},{2,0},{1,3},{3,1},{4,6},{6,4},{5,7},{7,5},{8,10},{10,8},{9,1... | collective-permute-start | bytes 1572872 | tf_op jit(solution)/shard_map/ppermute | solution.py:577
  52.2 77.4 %all-gather.5.cloned.1.call-start = ((), (), s32[]{:S(2)}) async-start(), calls=%async_computation.3 | async-start | bytes 1310720 | tf_op jit(solution)/shard_map/all_gather | solution.py:667
  52.3 28.4 %collective-permute-start.10 = (bf16[1024,256]{1,0:T(8,128)(2,1)}, bf16[1024,256]{1,0:T(8,128)(2,1)}, u32[]{:S(2)}, u32[]{:S(2)}) collective-permute-start(bf16[1024,256]{1,0:T(8,128)(2,1)} %get-tuple-element.239.refs_0_), channel_id=1, source_target_pairs={{0,16},{16,0},{1,17},{17,1},{2,18},{18,2},{3,19},{19,3},{4,20},{20... | collective-permute-start | bytes 1572872 | tf_op jit(solution)/shard_map/ppermute | solution.py:577
  52.9 24.4 %collective-permute-start.8 = (bf16[1024,256]{1,0:T(8,128)(2,1)}, bf16[1024,256]{1,0:T(8,128)(2,1)}, u32[]{:S(2)}, u32[]{:S(2)}) collective-permute-start(bf16[1024,256]{1,0:T(8,128)(2,1)} %get-tuple-element.239.refs_0_), channel_id=1, source_target_pairs={{0,2},{2,0},{1,3},{3,1},{4,6},{6,4},{5,7},{7,5},{8,10},{10,8},{9,1... | collective-permute-start | bytes 1572872 | tf_op jit(solution)/shard_map/ppermute | solution.py:577
  77.2 13.4 %collective-permute-start.12 = (bf16[1024,256]{1,0:T(8,128)(2,1)}, bf16[1024,256]{1,0:T(8,128)(2,1)S(1)}, u32[]{:S(2)}, u32[]{:S(2)}) collective-permute-start(bf16[1024,256]{1,0:T(8,128)(2,1)} %collective-permute-done.8.refs_2_), channel_id=1, source_target_pairs={{0,16},{16,0},{1,17},{17,1},{2,18},{18,2},{3,19},{19,3},{4,20},{20... | collective-permute-start | bytes 1572872 | tf_op jit(solution)/shard_map/ppermute | solution.py:577
  77.8 15.0 %collective-permute-start.13 = (bf16[1024,256]{1,0:T(8,128)(2,1)}, bf16[1024,256]{1,0:T(8,128)(2,1)S(1)}, u32[]{:S(2)}, u32[]{:S(2)}) collective-permute-start(bf16[1024,256]{1,0:T(8,128)(2,1)} %collective-permute-done.11.refs_5_), channel_id=1, source_target_pairs={{0,2},{2,0},{1,3},{3,1},{4,6},{6,4},{5,7},{7,5},{8,10},{10,8},{9,1... | collective-permute-start | bytes 1572872 | tf_op jit(solution)/shard_map/ppermute | solution.py:577
  78.6 371.1 %reduce-scatter.5.cloned.1.call-start = ((), (), s32[]{:S(2)}) async-start(), calls=%async_computation.5 | async-start | bytes 5242880 | tf_op jit(solution)/shard_map/reduce_scatter | solution.py:719
  79.1 49.2 %collective-permute-start.15 = (bf16[1154,256]{1,0:T(8,128)(2,1)S(1)}, bf16[1154,256]{1,0:T(8,128)(2,1)S(1)}, u32[]{:S(2)}, u32[]{:S(2)}) collective-permute-start(bf16[1154,256]{1,0:T(8,128)(2,1)S(1)} %get-tuple-element.96), channel_id=1, source_target_pairs={{0,2},{2,0},{1,3},{3,1},{4,6},{6,4},{5,7},{7,5},{8,10},{10,8},{9,1... | collective-permute-start | bytes 1772552 | tf_op jit(solution)/shard_map/ppermute | solution.py:577
  128.8 28.0 %collective-permute-start.16 = (bf16[1184,512]{1,0:T(8,128)(2,1)S(1)}, bf16[1184,512]{1,0:T(8,128)(2,1)S(1)}, u32[]{:S(2)}, u32[]{:S(2)}) collective-permute-start(bf16[1184,512]{1,0:T(8,128)(2,1)S(1)} %bitcast.56), channel_id=1, source_target_pairs={{0,1},{1,0},{2,3},{3,2},{4,5},{5,4},{6,7},{7,6},{8,9},{9,8},{10,11... | collective-permute-start | bytes 3637256 | tf_op jit(solution)/shard_map/ppermute | solution.py:577
  128.9 26.4 %collective-permute-start.17 = (bf16[1024,512]{1,0:T(8,128)(2,1)}, bf16[1024,512]{1,0:T(8,128)(2,1)}, u32[]{:S(2)}, u32[]{:S(2)}) collective-permute-start(bf16[1024,512]{1,0:T(8,128)(2,1)} %all-gather.3.cloned.1.call-done.refs_0_), channel_id=1, source_target_pairs={{0,2},{2,0},{1,3},{3,1},{4,6},{6,4},{5,7},{7,5},{8,10},{10,8},{9,1... | collective-permute-start | bytes 3145736 | tf_op jit(solution)/shard_map/ppermute | solution.py:577
  129.5 30.0 %collective-permute-start.14 = (bf16[1184,1024]{1,0:T(8,128)(2,1)}, bf16[1184,1024]{1,0:T(8,128)(2,1)}, u32[]{:S(2)}, u32[]{:S(2)}) collective-permute-start(bf16[1184,1024]{1,0:T(8,128)(2,1)} %convolution_convert_fusion.a_ref), channel_id=1, source_target_pairs={{0,1},{1,0},{2,3},{3,2},{4,5},{5,4},{6,7},{7,6},{8,9},{9,8},{10,11... | collective-permute-start | bytes 7274504 | tf_op jit(solution)/shard_map/ppermute | solution.py:577
  129.6 36.6 %collective-permute-start.21 = (bf16[1024,512]{1,0:T(8,128)(2,1)}, bf16[1024,512]{1,0:T(8,128)(2,1)}, u32[]{:S(2)}, u32[]{:S(2)}) collective-permute-start(bf16[1024,512]{1,0:T(8,128)(2,1)} %all-gather.5.cloned.1.call-done.refs_4_), channel_id=1, source_target_pairs={{0,16},{16,0},{1,17},{17,1},{2,18},{18,2},{3,19},{19,3},{4,20},{20... | collective-permute-start | bytes 3145736 | tf_op jit(solution)/shard_map/ppermute | solution.py:577
  131.1 46.7 %collective-permute-start.20 = (bf16[1024,512]{1,0:T(8,128)(2,1)}, bf16[1024,512]{1,0:T(8,128)(2,1)}, u32[]{:S(2)}, u32[]{:S(2)}) collective-permute-start(bf16[1024,512]{1,0:T(8,128)(2,1)} %all-gather.5.cloned.1.call-done.refs_4_), channel_id=1, source_target_pairs={{0,2},{2,0},{1,3},{3,1},{4,6},{6,4},{5,7},{7,5},{8,10},{10,8},{9,1... | collective-permute-start | bytes 3145736 | tf_op jit(solution)/shard_map/ppermute | solution.py:577
  155.3 26.3 %collective-permute-start.18 = (bf16[1024,512]{1,0:T(8,128)(2,1)}, bf16[1024,512]{1,0:T(8,128)(2,1)}, u32[]{:S(2)}, u32[]{:S(2)}) collective-permute-start(bf16[1024,512]{1,0:T(8,128)(2,1)} %all-gather.3.cloned.1.call-done.refs_0_), channel_id=1, source_target_pairs={{0,16},{16,0},{1,17},{17,1},{2,18},{18,2},{3,19},{19,3},{4,20},{20... | collective-permute-start | bytes 3145736 | tf_op jit(solution)/shard_map/ppermute | solution.py:577
  156.8 45.3 %collective-permute-start.19 = (bf16[1024,512]{1,0:T(8,128)(2,1)}, bf16[1024,512]{1,0:T(8,128)(2,1)}, u32[]{:S(2)}, u32[]{:S(2)}) collective-permute-start(bf16[1024,512]{1,0:T(8,128)(2,1)} %collective-permute-done.17.refs_1_), channel_id=1, source_target_pairs={{0,16},{16,0},{1,17},{17,1},{2,18},{18,2},{3,19},{19,3},{4,20},{20... | collective-permute-start | bytes 3145736 | tf_op jit(solution)/shard_map/ppermute | solution.py:577
  166.2 35.9 %collective-permute-start.22 = (bf16[1024,512]{1,0:T(8,128)(2,1)}, bf16[1024,512]{1,0:T(8,128)(2,1)S(1)}, u32[]{:S(2)}, u32[]{:S(2)}) collective-permute-start(bf16[1024,512]{1,0:T(8,128)(2,1)} %collective-permute-done.21.refs_6_), channel_id=1, source_target_pairs={{0,2},{2,0},{1,3},{3,1},{4,6},{6,4},{5,7},{7,5},{8,10},{10,8},{9,1... | collective-permute-start | bytes 3145736 | tf_op jit(solution)/shard_map/ppermute | solution.py:577
  237.1 18.7 %collective-permute-start.23 = (bf16[1184,1024]{1,0:T(8,128)(2,1)}, bf16[1184,1024]{1,0:T(8,128)(2,1)S(1)}, u32[]{:S(2)}, u32[]{:S(2)}) collective-permute-start(bf16[1184,1024]{1,0:T(8,128)(2,1)} %get-tuple-element.106.a_ref), channel_id=1, source_target_pairs={{0,1},{1,0},{2,3},{3,2},{4,5},{5,4},{6,7},{7,6},{8,9},{9,8},{10,11... | collective-permute-start | bytes 7274504 | tf_op jit(solution)/shard_map/ppermute | solution.py:577
  245.8 9.9 %collective-permute-start.24 = (bf16[1184,512]{1,0:T(8,128)(2,1)}, bf16[1184,512]{1,0:T(8,128)(2,1)}, u32[]{:S(2)}, u32[]{:S(2)}) collective-permute-start(bf16[1184,512]{1,0:T(8,128)(2,1)} %get-tuple-element.112), channel_id=1, source_target_pairs={{0,1},{1,0},{2,3},{3,2},{4,5},{5,4},{6,7},{7,6},{8,9},{9,8},{10,11... | collective-permute-start | bytes 3637256 | tf_op jit(solution)/shard_map/ppermute | solution.py:577
  253.6 208.6 %reduce-scatter.3.cloned.1.call-start = ((), (), s32[]{:S(2)}) async-start(), calls=%async_computation.4 | async-start | bytes 1638400 | tf_op jit(solution)/shard_map/reduce_scatter | solution.py:719
  253.6 25.5 %collective-permute-start.25 = (bf16[1024,512]{1,0:T(8,128)(2,1)}, bf16[1024,512]{1,0:T(8,128)(2,1)}, u32[]{:S(2)}, u32[]{:S(2)}) collective-permute-start(bf16[1024,512]{1,0:T(8,128)(2,1)} %convolution_convert_fusion.5), channel_id=1, source_target_pairs={{0,16},{16,0},{1,17},{17,1},{2,18},{18,2},{3,19},{19,3},{4,20},{20... | collective-permute-start | bytes 3145736 | tf_op jit(solution)/shard_map/ppermute | solution.py:577
  255.2 25.1 %collective-permute-start.26 = (bf16[1024,512]{1,0:T(8,128)(2,1)}, bf16[1024,512]{1,0:T(8,128)(2,1)}, u32[]{:S(2)}, u32[]{:S(2)}) collective-permute-start(bf16[1024,512]{1,0:T(8,128)(2,1)} %convolution_convert_fusion.4), channel_id=1, source_target_pairs={{0,2},{2,0},{1,3},{3,1},{4,6},{6,4},{5,7},{7,5},{8,10},{10,8},{9,1... | collective-permute-start | bytes 3145736 | tf_op jit(solution)/shard_map/ppermute | solution.py:577
  319.5 14.9 %collective-permute-start.30 = (bf16[1024,256]{1,0:T(8,128)(2,1)S(1)}, bf16[1024,256]{1,0:T(8,128)(2,1)S(1)}, u32[]{:S(2)}, u32[]{:S(2)}) collective-permute-start(bf16[1024,256]{1,0:T(8,128)(2,1)S(1)} %slice.277), channel_id=1, source_target_pairs={{0,16},{16,0},{1,17},{17,1},{2,18},{18,2},{3,19},{19,3},{4,20},{20... | collective-permute-start | bytes 1572872 | tf_op jit(solution)/shard_map/ppermute | solution.py:577
  325.4 56.7 %collective-permute-start.33 = (bf16[1184,1024]{1,0:T(8,128)(2,1)}, bf16[1184,1024]{1,0:T(8,128)(2,1)}, u32[]{:S(2)}, u32[]{:S(2)}) collective-permute-start(bf16[1184,1024]{1,0:T(8,128)(2,1)} %convolution_convert_fusion.1.a_ref), channel_id=1, source_target_pairs={{0,1},{1,0},{2,3},{3,2},{4,5},{5,4},{6,7},{7,6},{8,9},{9,8},{10,11... | collective-permute-start | bytes 7274504 | tf_op jit(solution)/shard_map/ppermute | solution.py:577
  325.5 9.2 %collective-permute-start.29 = (bf16[1024,128]{1,0:T(8,128)(2,1)S(1)}, bf16[1024,128]{1,0:T(8,128)(2,1)S(1)}, u32[]{:S(2)}, u32[]{:S(2)}) collective-permute-start(bf16[1024,128]{1,0:T(8,128)(2,1)S(1)} %convolution_convert_fusion.7), channel_id=1, source_target_pairs={{0,2},{2,0},{1,3},{3,1},{4,6},{6,4},{5,7},{7,5},{8,10},{10,8},{9,1... | collective-permute-start | bytes 786440 | tf_op jit(solution)/shard_map/ppermute | solution.py:577
  327.0 18.6 %collective-permute-start.28 = (bf16[1024,256]{1,0:T(8,128)(2,1)S(1)}, bf16[1024,256]{1,0:T(8,128)(2,1)S(1)}, u32[]{:S(2)}, u32[]{:S(2)}) collective-permute-start(bf16[1024,256]{1,0:T(8,128)(2,1)S(1)} %convolution_convert_fusion.6), channel_id=1, source_target_pairs={{0,16},{16,0},{1,17},{17,1},{2,18},{18,2},{3,19},{19,3},{4,20},{20... | collective-permute-start | bytes 1572872 | tf_op jit(solution)/shard_map/ppermute | solution.py:577
  328.6 19.4 %collective-permute-start.34 = (bf16[1024,256]{1,0:T(8,128)(2,1)S(1)}, bf16[1024,256]{1,0:T(8,128)(2,1)S(1)}, u32[]{:S(2)}, u32[]{:S(2)}) collective-permute-start(bf16[1024,256]{1,0:T(8,128)(2,1)S(1)} %slice.279), channel_id=1, source_target_pairs={{0,2},{2,0},{1,3},{3,1},{4,6},{6,4},{5,7},{7,5},{8,10},{10,8},{9,1... | collective-permute-start | bytes 1572872 | tf_op jit(solution)/shard_map/ppermute | solution.py:577
  334.3 22.5 %collective-permute-start.35 = (bf16[1024,256]{1,0:T(8,128)(2,1)}, bf16[1024,256]{1,0:T(8,128)(2,1)S(1)}, u32[]{:S(2)}, u32[]{:S(2)}) collective-permute-start(bf16[1024,256]{1,0:T(8,128)(2,1)} %slice.281), channel_id=1, source_target_pairs={{0,16},{16,0},{1,17},{17,1},{2,18},{18,2},{3,19},{19,3},{4,20},{20... | collective-permute-start | bytes 1572872 | tf_op jit(solution)/shard_map/ppermute | solution.py:577
  334.8 65.9 %collective-permute-start.27 = (bf16[1184,256]{1,0:T(8,128)(2,1)}, bf16[1184,256]{1,0:T(8,128)(2,1)}, u32[]{:S(2)}, u32[]{:S(2)}) collective-permute-start(bf16[1184,256]{1,0:T(8,128)(2,1)} %get-tuple-element.117), channel_id=1, source_target_pairs={{0,2},{2,0},{1,3},{3,1},{4,6},{6,4},{5,7},{7,5},{8,10},{10,8},{9,1... | collective-permute-start | bytes 1818632 | tf_op jit(solution)/shard_map/ppermute | solution.py:577
  348.0 44.4 %collective-permute-start.32 = (bf16[1024,384]{1,0:T(8,128)(2,1)}, bf16[1024,384]{1,0:T(8,128)(2,1)}, u32[]{:S(2)}, u32[]{:S(2)}) collective-permute-start(bf16[1024,384]{1,0:T(8,128)(2,1)} %add_convert_fusion.3), channel_id=1, source_target_pairs={{0,2},{2,0},{1,3},{3,1},{4,6},{6,4},{5,7},{7,5},{8,10},{10,8},{9,1... | collective-permute-start | bytes 2359304 | tf_op jit(solution)/shard_map/ppermute | solution.py:577
  348.0 44.4 %collective-permute-start.31 = (bf16[1024,384]{1,0:T(8,128)(2,1)}, bf16[1024,384]{1,0:T(8,128)(2,1)}, u32[]{:S(2)}, u32[]{:S(2)}) collective-permute-start(bf16[1024,384]{1,0:T(8,128)(2,1)} %add_convert_fusion.4), channel_id=1, source_target_pairs={{0,16},{16,0},{1,17},{17,1},{2,18},{18,2},{3,19},{19,3},{4,20},{20... | collective-permute-start | bytes 2359304 | tf_op jit(solution)/shard_map/ppermute | solution.py:577
  356.8 24.1 %collective-permute-start.36 = (bf16[1024,128]{1,0:T(8,128)(2,1)S(1)}, bf16[1024,128]{1,0:T(8,128)(2,1)S(1)}, u32[]{:S(2)}, u32[]{:S(2)}) collective-permute-start(bf16[1024,128]{1,0:T(8,128)(2,1)S(1)} %slice.283), channel_id=1, source_target_pairs={{0,2},{2,0},{1,3},{3,1},{4,6},{6,4},{5,7},{7,5},{8,10},{10,8},{9,1... | collective-permute-start | bytes 786440 | tf_op jit(solution)/shard_map/ppermute | solution.py:577
  398.0 6.9 %collective-permute-start.43 = (f32[12,256]{1,0:T(8,128)S(1)}, f32[12,256]{1,0:T(8,128)S(1)}, u32[]{:S(2)}, u32[]{:S(2)}) collective-permute-start(f32[12,256]{1,0:T(8,128)S(1)} %add.186), channel_id=1, source_target_pairs={{0,4},{4,0},{8,12},{12,8},{1,5},{5,1},{9,13},{13,9},{2,6},{6,2},{1... | collective-permute-start | bytes 36872 | tf_op jit(solution)/shard_map/ppermute | solution.py:577
  400.7 40.9 %collective-permute-start.38 = (bf16[256,384]{1,0:T(8,128)(2,1)S(1)}, bf16[256,384]{1,0:T(8,128)(2,1)S(1)}, u32[]{:S(2)}, u32[]{:S(2)}) collective-permute-start(bf16[256,384]{1,0:T(8,128)(2,1)S(1)} %get-tuple-element.219), channel_id=1, source_target_pairs={{0,4},{4,8},{8,12},{12,0},{1,5},{5,9},{9,13},{13,1},{2,6},{6,10},{... | collective-permute-start | bytes 589832 | tf_op jit(solution)/shard_map/ppermute | solution.py:580
  400.8 40.8 %collective-permute-start.40 = (bf16[256,384]{1,0:T(8,128)(2,1)S(1)}, bf16[256,384]{1,0:T(8,128)(2,1)S(1)}, u32[]{:S(2)}, u32[]{:S(2)}) collective-permute-start(bf16[256,384]{1,0:T(8,128)(2,1)S(1)} %get-tuple-element.220), channel_id=1, source_target_pairs={{0,12},{4,0},{8,4},{12,8},{1,13},{5,1},{9,5},{13,9},{2,14},{6,2},{... | collective-permute-start | bytes 589832 | tf_op jit(solution)/shard_map/ppermute | solution.py:580
  404.6 37.0 %collective-permute-start.39 = (bf16[256,384]{1,0:T(8,128)(2,1)S(1)}, bf16[256,384]{1,0:T(8,128)(2,1)S(1)}, u32[]{:S(2)}, u32[]{:S(2)}) collective-permute-start(bf16[256,384]{1,0:T(8,128)(2,1)S(1)} %get-tuple-element.221), channel_id=1, source_target_pairs={{0,8},{4,12},{8,0},{12,4},{1,9},{5,13},{9,1},{13,5},{2,10},{6,14},... | collective-permute-start | bytes 589832 | tf_op jit(solution)/shard_map/ppermute | solution.py:580
  404.8 35.3 %collective-permute-start.44 = (f32[12,256]{1,0:T(8,128)S(1)}, f32[12,256]{1,0:T(8,128)S(1)}, u32[]{:S(2)}, u32[]{:S(2)}) collective-permute-start(f32[12,256]{1,0:T(8,128)S(1)} %add.187), channel_id=1, source_target_pairs={{0,8},{4,12},{8,0},{12,4},{1,9},{5,13},{9,1},{13,5},{2,10},{6,14},... | collective-permute-start | bytes 36872 | tf_op jit(solution)/shard_map/ppermute | solution.py:577
  443.9 16.8 %collective-permute-start.37 = (bf16[1184,256]{1,0:T(8,128)(2,1)}, bf16[1184,256]{1,0:T(8,128)(2,1)S(1)}, u32[]{:S(2)}, u32[]{:S(2)}) collective-permute-start(bf16[1184,256]{1,0:T(8,128)(2,1)} %get-tuple-element.142), channel_id=1, source_target_pairs={{0,2},{2,0},{1,3},{3,1},{4,6},{6,4},{5,7},{7,5},{8,10},{10,8},{9,1... | collective-permute-start | bytes 1818632 | tf_op jit(solution)/shard_map/ppermute | solution.py:577
  451.9 16.8 %collective-permute-start.47 = (bf16[256,1024]{1,0:T(8,128)(2,1)}, bf16[256,1024]{1,0:T(8,128)(2,1)}, u32[]{:S(2)}, u32[]{:S(2)}) collective-permute-start(bf16[256,1024]{1,0:T(8,128)(2,1)} %pad_maximum_fusion.7), channel_id=1, source_target_pairs={{0,2},{2,0},{1,3},{3,1},{4,6},{6,4},{5,7},{7,5},{8,10},{10,8},{9,1... | collective-permute-start | bytes 1572872 | tf_op jit(solution)/shard_map/ppermute | solution.py:577
  462.1 9.2 %collective-permute-start.46 = (bf16[256,640]{1,0:T(8,128)(2,1)}, bf16[256,640]{1,0:T(8,128)(2,1)}, u32[]{:S(2)}, u32[]{:S(2)}) collective-permute-start(bf16[256,640]{1,0:T(8,128)(2,1)} %reduce-scatter.3.cloned.1.call-done), channel_id=1, source_target_pairs={{0,16},{16,0},{1,17},{17,1},{2,18},{18,2},{3,19},{19,3},{4,20},{20... | collective-permute-start | bytes 983048 | tf_op jit(solution)/shard_map/ppermute | solution.py:577
  469.9 10.8 %collective-permute-start.48 = (bf16[256,1024]{1,0:T(8,128)(2,1)S(1)}, bf16[256,1024]{1,0:T(8,128)(2,1)S(1)}, u32[]{:S(2)}, u32[]{:S(2)}) collective-permute-start(bf16[256,1024]{1,0:T(8,128)(2,1)S(1)} %add_convert_fusion.5), channel_id=1, source_target_pairs={{0,16},{16,0},{1,17},{17,1},{2,18},{18,2},{3,19},{19,3},{4,20},{20... | collective-permute-start | bytes 1572872 | tf_op jit(solution)/shard_map/ppermute | solution.py:577
  (31 other events, 177.1 us)
Sparse Core Ops, SparseCore 0:
  52.3 29.2 all-gather.2
  83.7 27.3 all-gather.4
  253.7 78.0 reduce-scatter.4
  394.9 46.3 reduce-scatter.2

commit v7 on v6

--- a/solution.py
+++ b/solution.py
@@ -210,24 +210,31 @@
     )(x, a, b, bias[0], gain[0], shift[0])
 
 
-def mlp_kernel(plan, place_ref, n_ref, dy_ref, bias_ref, *refs):
-    packs = refs[: len(plan)]
-    g_ref, du_ref, mine_ref, theirs_ref, lift_ref, bsum_ref = refs[len(plan) : len(plan) + 6]
-    low_acc, lift_acc, buf, sems = refs[len(plan) + 6 :]
+def mlp_kernel(final, place_ref, n_ref, dy_ref, bias_ref, *refs):
+    packs = refs[:4]
+    before = refs[4:6] if final else ()
+    rest = refs[4 + len(before) :]
+    g_ref, du_ref, bsum_ref = rest[:3]
+    low_acc, lift_acc, buf, sems = rest[6:10] if final else rest[5:9]
     j = pl.program_id(0)
     tn = g_ref.shape[1]
     slot = lax.rem(j, 2)
 
     def load(tile, at):
-        return pltpu.make_async_copy(packs[plan[tile]], buf.at[at], sems.at[at])
+        return pltpu.make_async_copy(packs[tile], buf.at[at], sems.at[at])
+
+    def fetch(at):
+        return pltpu.make_async_copy(before[at], rest[10 + at], sems.at[2 + at])
 
     @pl.when(j == 0)
     def _():
         load(0, 0).start()
+        for at in range(len(before)):
+            fetch(at).start()
         low_acc[...] = jnp.zeros_like(low_acc)
         lift_acc[...] = jnp.zeros_like(lift_acc)
 
-    for tile in range(1, len(plan)):
+    for tile in range(1, 4):
 
         @pl.when(j == tile - 1)
         def _(tile=tile):
@@ -246,9 +253,17 @@
     low_acc[...] += mm_nt(g, down)
     lift_acc[...] += mm_nt(du, up)
 
-    @pl.when(j == len(plan) - 1)
+    @pl.when(j == 3)
     def _():
-        lift_ref[...] = lift_acc[...].astype(BF16)
+        if not final:
+            rest[3][...] = low_acc[...].astype(BF16)
+            rest[4][...] = lift_acc[...].astype(BF16)
+            return
+        mine_ref, theirs_ref, lift_ref = rest[3:6]
+        for at in range(2):
+            fetch(at).wait()
+        lift_ref[...] = (lift_acc[...] + rest[11][...].astype(F32)).astype(BF16)
+        low_acc[...] += rest[10][...].astype(F32)
         width = D // 4
         core = place_ref[0]
         for far in range(2):
@@ -260,47 +275,45 @@
             )
 
 
-def mlp(place, n2, dy, bias, packs, plan):
+def mlp(place, n2, dy, bias, packs, before=()):
     rows = n2.shape[0]
-    hid = bias.shape[1]
-    tn = hid // len(plan)
+    tn = packs[0].shape[1] // 2
+    first_tile = 4 if before else 0
     whole = held_once((rows, D))
+    half = held_once((rows, D // 2))
     tile = pl.BlockSpec((rows, tn), lambda j, *_: (0, j))
+    swapped = pl.BlockSpec(
+        (rows, tn), lambda j, *_: (0, jnp.where(j == 1, 2, jnp.where(j == 2, 1, j)))
+    )
     thin = pl.BlockSpec((1, tn), lambda j, *_: (0, j))
-    return pl.pallas_call(
-        functools.partial(mlp_kernel, plan),
-        name="mlp",
+    anywhere = pl.BlockSpec(memory_space=pl.ANY)
+    out_specs = [swapped, tile, thin] + ([half, half, whole] if before else [whole, whole])
+    out_shape = [like((rows, 4 * tn), BF16), like((rows, 4 * tn), BF16), like((1, 4 * tn), F32)]
+    if before:
+        out_shape += [like((rows, D // 2), F32), like((rows, D // 2), BF16), like((rows, D), BF16)]
+    else:
+        out_shape += [like((rows, D), BF16)] * 2
+    return pl.pallas_call(
+        functools.partial(mlp_kernel, bool(before)),
+        name="mlp_second" if before else "mlp_first",
         grid_spec=pltpu.PrefetchScalarGridSpec(
             num_scalar_prefetch=1,
-            grid=(len(plan),),
-            in_specs=[whole, whole, thin]
-            + [pl.BlockSpec(memory_space=pl.ANY)] * len(packs),
-            out_specs=[
-                tile,
-                tile,
-                held_once((rows, D // 2)),
-                held_once((rows, D // 2)),
-                whole,
-                thin,
-            ],
+            grid=(4,),
+            in_specs=[whole, whole, pl.BlockSpec((1, tn), lambda j, *_: (0, j + first_tile))]
+            + [anywhere] * (4 + len(before)),
+            out_specs=out_specs,
             scratch_shapes=[
                 pltpu.VMEM((rows, D), F32),
                 pltpu.VMEM((rows, D), F32),
                 pltpu.VMEM((2, D, 2 * tn), BF16),
-                pltpu.SemaphoreType.DMA((2,)),
-            ],
+                pltpu.SemaphoreType.DMA((4,)),
+            ]
+            + [pltpu.VMEM((rows, D), BF16)] * len(before),
         ),
-        out_shape=[
-            like((rows, hid), BF16),
-            like((rows, hid), BF16),
-            like((rows, D // 2), F32),
-            like((rows, D // 2), BF16),
-            like((rows, D), BF16),
-            like((1, hid), F32),
-        ],
+        out_shape=out_shape,
         compiler_params=params(1),
-        cost_estimate=cost(8 * rows * D * hid, 24 * rows * D, 2 * rows * hid),
-    )(place, n2, dy, bias, *packs)
+        cost_estimate=cost(32 * rows * D * tn, 20 * rows * D, 8 * rows * tn),
+    )(place, n2, dy, bias, *packs, *before)
 
 
 def turn_kernel(
@@ -482,7 +495,9 @@
     )(place, own, far, own_other, far_other)
 
 
-def collect_kernel(place_ref, turn_ref, qkv_ref, up_ref, a_ref, b_ref, mine_ref, theirs_ref):
+def collect_kernel(
+    place_ref, turn_ref, qkv_ref, up_a_ref, up_b_ref, a_ref, b_ref, mine_ref, theirs_ref
+):
     core, side, half = place_ref[0], place_ref[1], place_ref[2]
     width = mine_ref.shape[1]
     one = width // 2
@@ -502,8 +517,8 @@
         for at, index in enumerate(order[part]):
             ref = (mine_ref, theirs_ref)[index % 2]
             which = half if index < 2 else 1 - half
-            start = width * (4 * part + at)
-            ref[pl.ds(6 + 2 * which + part, 1), :] = up_ref[:, start : start + width]
+            up_ref = (up_a_ref, up_b_ref)[part]
+            ref[pl.ds(6 + 2 * which + part, 1), :] = up_ref[:, width * at : width * (at + 1)]
 
 
 def collect(place, *sums):
@@ -512,7 +527,7 @@
         collect_kernel,
         name="collect",
         in_specs=[pl.BlockSpec(memory_space=pltpu.SMEM)]
-        + [pl.BlockSpec(memory_space=pltpu.VMEM)] * 5,
+        + [pl.BlockSpec(memory_space=pltpu.VMEM)] * 6,
         out_shape=[like((12, width), F32)] * 2,
     )(place, *sums)
 
@@ -695,15 +710,25 @@
     middle_sum, wide_two = middle(
         wide_input, mixed, after(mixed_other, wide_grad), out_bias_all, gain_two, shift_two
     )
-    far_oth_b = across(after(oth_b, wide_two))
-    plan = (0, 1, 2, 3, 4, 6, 5, 7)
-    gate, pre, low_mine, low_theirs, lifted_two, up_sums = mlp(
+    far_oth_b = across(oth_b)
+
+    def tiles(value, first, end):
+        return value[:, quarter * first : quarter * end]
+
+    gate_a, pre_a, up_sums_a, low_a, lift_a = mlp(
+        place, wide_two, wide_grad, tile_bias, (own_a, far_a, oth_a, far_oth_a)
+    )
+    up_over = mm_tn(wide_two, tiles(pre_a, 2, 4)).astype(BF16)
+    down_a = mm_tn(wide_grad, gate_a).astype(BF16)
+    up_over_got = over(up_over)
+    down_piece = lax.psum_scatter(down_a, "row", scatter_dimension=0, tiled=True)
+    gate_b, pre_b, up_sums_b, low_mine, low_theirs, lifted_two = mlp(
         place,
-        wide_two,
+        after(wide_two, up_over, down_a),
         wide_grad,
         tile_bias,
-        (own_a, far_a, oth_a, far_oth_a, own_b, far_b, oth_b, far_oth_b),
-        plan,
+        (own_b, oth_b, far_b, far_oth_b),
+        (low_a, lift_a),
     )
 
     def wide_add(mine, got):
@@ -718,23 +743,18 @@
     def scatter(value):
         return lax.psum_scatter(value, "row", scatter_dimension=0, tiled=True)
 
-    def tiles(value, first, end):
-        return value[:, quarter * first : quarter * end]
-
     lifted_other = beside(lifted_two)
     low_other = beside(low_theirs)
-    up_over = mm_tn(wide_two, tiles(pre, 2, 4)).astype(BF16)
-    up_across = mm_tn(wide_two, tiles(pre, 6, 8)).astype(BF16)
-    up_over_got, up_across_got = over(up_over), across(up_across)
-    down_all = mm_tn(after(wide_grad, up_over, up_across), gate).astype(BF16)
-    down_piece = scatter(down_all)
+    up_across = mm_tn(wide_two, tiles(pre_b, 2, 4)).astype(BF16)
+    down_over = mm_tn(wide_grad, tiles(gate_b, 2, 4)).astype(BF16)
+    up_across_got, down_over_got = across(up_across), over(down_over)
 
     middle_grad, attn_grad, head_grad, turn_sums, out_mine, out_theirs = turn(
         place,
         middle_sum,
         wide_grad,
         lifted_two,
-        after(lifted_other, down_all),
+        after(lifted_other, up_across, down_over),
         low_mine,
         low_other,
         gain_two,
@@ -743,17 +763,24 @@
     )
     out_all = mm_tn(attn_grad, attended).astype(BF16)
     out_over_got = over(out_all[:, 2 * heads_half :])
-    up_over_got, up_across_got, _ = lax.optimization_barrier((up_over_got, up_across_got, out_all))
-    up_a = wide_add(mm_tn(wide_two, tiles(pre, 0, 2)), up_over_got)
-    up_b = wide_add(mm_tn(wide_two, tiles(pre, 4, 6)), up_across_got)
+    up_over_got, up_across_got, down_over_got, _ = lax.optimization_barrier(
+        (up_over_got, up_across_got, down_over_got, out_all)
+    )
+    up_a = wide_add(mm_tn(wide_two, tiles(pre_a, 0, 2)), up_over_got)
+    up_b = wide_add(mm_tn(wide_two, tiles(pre_b, 0, 2)), up_across_got)
+    down_b = wide_add(mm_tn(wide_grad, tiles(gate_b, 0, 2)), down_over_got)
     up_a_got, up_b_got = across(up_a[:, quarter:]), over(up_b[:, quarter:])
-    out_got = across(after(out_theirs, up_a))
-    dqkv, qkv_sums = attend_back(qkv, probs, after(head_grad, up_a, up_b))
+    down_b_got = across(down_b[:, quarter:])
+    out_got = across(after(out_theirs, down_b))
+    dqkv, qkv_sums = attend_back(qkv, probs, after(head_grad, up_a, up_b, down_b))
 
     def to_feature_blocks(mine, got, dtype):
         first, second = in_order(mine.astype(dtype), got.astype(dtype), my_x)
         both = jnp.concatenate([first, second]).reshape(images, PAD, width)
         return both[:, :SEQ].reshape(tokens_here, width)
+
+    down_piece = after(down_piece, dqkv)
+    down_x_got = across(down_piece[:, half:])
 
     split = 3 * three + cut
     far_oth_qk = mm_tn(wide_one, dqkv[:, 3 * three : split]).astype(BF16)
@@ -781,11 +808,14 @@
         [
             wide_add(up_a[:, :quarter], after(up_a_got, far_own)),
             wide_add(up_b[:, :quarter], up_b_got),
+            wide_add(down_b[:, :quarter], down_b_got),
             wide_add(out_own[:, :heads_half], out_far_got),
         ],
         axis=1,
     )
     up_piece = same_half(scatter(up_sum))
+    down_x = wide_add(down_piece[:, :half], after(down_x_got, far_own))
+    down_y_got = over(down_x)
     input_mine, input_theirs, late_mine, late_theirs = last(
         place,
         wide_input,
@@ -795,7 +825,7 @@
         gain_one,
     )
     mine_sums, theirs_sums = collect(
-        place, turn_sums, qkv_sums, up_sums, late_mine, late_theirs
+        place, turn_sums, qkv_sums, up_sums_a, up_sums_b, late_mine, late_theirs
     )
 
     near_sum = (near_own + near_oth_got.astype(F32) + after(far_own_got, mine_sums).astype(F32)).astype(
@@ -816,28 +846,29 @@
     sums = hand_out(sums, swap(sums, *steps[-1]))
     outputs = to_feature_blocks(out_mine, after(out_got, near_sum), BF16)
 
-    def some(value, *which):
-        return jnp.concatenate([tiles(value, at, at + 1) for at in which], axis=1)
-
-    down_piece = after(down_piece, near_sum)
-    down_x = wide_add(some(down_piece, 0, 4, 2, 5), across(some(down_piece, 1, 6, 3, 7)))
-
     qkv_total = rows_of(near_sum, 0).astype(F32)
     for got in gots:
         qkv_total = qkv_total + got.astype(F32)
     qkv_piece = same_half(qkv_total.astype(BF16))
     qkv_other = over(qkv_piece)
-    down_got = over(down_x)
     input_grad = to_feature_blocks(input_mine, input_got, F32)
     up_other = over(up_piece)
 
     down_total = down_x.astype(F32) + jnp.concatenate(
-        [down_got[:, half:], down_got[:, :half]], axis=1
+        [down_y_got[:, quarter:], down_y_got[:, :quarter]], axis=1
     ).astype(F32)
     if n_dp > 2:
         groups = [[at + bit for at in range(0, n_dp, 2)] for bit in range(2)]
         down_total = lax.psum(down_total, "dp", axis_index_groups=groups)
-    down_first, down_second = in_order(down_total[:, :half], down_total[:, half:], my_half)
+
+    def down_half(first_part, second):
+        return jnp.concatenate([first_part, tiles(second, 2, 3).astype(F32)], axis=1)
+
+    down_first, down_second = in_order(
+        down_half(down_total[:, :quarter], up_piece),
+        down_half(down_total[:, quarter:], up_other),
+        my_half,
+    )
     down_grad = jnp.concatenate([down_first, down_second], axis=1).T
 
     def both_halves(mine, other, low, high):
@@ -845,7 +876,8 @@
         return jnp.concatenate([first, second], axis=1).astype(F32)
 
     up_grad = both_halves(up_piece, up_other, 0, half)
-    out_grad = both_halves(up_piece, up_other, half, half + heads_half).T
+    start = half + quarter
+    out_grad = both_halves(up_piece, up_other, start, start + heads_half).T
     query_grad, key_grad, value_grad = (
         both_halves(qkv_piece, qkv_other, heads_half * at, heads_half * (at + 1))
         for at in range(3)

time: 495 us -> 524 us (1.059)
  starting transfers between devices: 46.8 us -> 57 us
  Pallas kernels: 126 us -> 136 us
  waiting for transfers between devices: 204 us -> 211 us
    ppermute x43 -> x45, starting transfers between devices: 35.9 us -> 46.2 us  [swap(): return lax.ppermute(value, axis, [(at, at ^ bit) for at in range(size)])]
    pallas_call x1 -> x2, Pallas kernels: 34 us -> 43 us  [mlp(): pl.pallas_call(functools.partial(mlp_kernel, bool(before)), name='mlp_sec...]
    ppermute x43 -> x45, waiting for transfers between devices: 187 us -> 194 us  [swap(): return lax.ppermute(value, axis, [(at, at ^ bit) for at in range(size)])]
    dot_general x11 -> x13, matrix products: 38.8 us -> 41.8 us  [mm_tn(): lax.dot_general(a, b, (((0,), (0,)), ((), ())), preferred_element_type=F32)]
  transfers between devices with their start and end apart: 53 -> 55, of which waited for: 23 -> 20; matrix products, arithmetic and copies ran while one was open for 18% -> 16% of each run, Pallas kernels for 19% -> 22%
where the time goes in v7:
time: 524 us; the launch traced here: 518 us
  waiting for transfers between devices  211 us (40%)
  Pallas kernels  136 us (26%)
  starting transfers between devices  57 us (11%)
  matrix products  51.8 us (10%)
  local copies, waits for them, and re-layouts  28.5 us (5%)
  other arithmetic  19.5 us (4%)
  between operations  14.9 us (3%)
    ppermute x45, waiting for transfers between devices, swap(): return lax.ppermute(value, axis, [(at, at ^ bit) for at in range(size)])  194 us
    ppermute x45, starting transfers between devices, swap(): return lax.ppermute(value, axis, [(at, at ^ bit) for at in range(size)])  46.2 us
    pallas_call x2, Pallas kernels, mlp(): pl.pallas_call(functools.partial(mlp_kernel, bool(before)), name='mlp_sec...  43 us
    dot_general x13, matrix products, mm_tn(): lax.dot_general(a, b, (((0,), (0,)), ((), ())), preferred_element_type=F32)  41.8 us
    pallas_call x1, Pallas kernels, attend_back(): pl.pallas_call(attend_back_kernel, grid=(pairs, held), name='attend_back'...  26.8 us
    pallas_call x1, Pallas kernels, attend(): pl.pallas_call(attend_kernel, grid=(pairs, held), name='attend', in_specs...  20.2 us
    ppermute x6, waiting for transfers between devices, shifted(): lax.ppermute(value, 'row', [(at, (at + shift) % n_row) for at in range(n_...  16.6 us
    pallas_call x1, Pallas kernels, turn(): pl.pallas_call(turn_kernel, name='turn', grid_spec=pltpu.PrefetchScalarGr...  14.2 us
  transfers between devices with their start and end apart: 55, of which 20 were waited for; matrix products, arithmetic and copies ran while one was open for 16% of the time, Pallas kernels for 22%

profile of v7, /device:TPU:0, one launch (start us, length us, event | category | flops | bytes accessed | tf_op | source)
XLA Modules:
  0.0 518.4 jit_solution(9687537021470978289)
XLA Ops:
  11.9 5.1 collective-permute-start.3
  21.1 13.8 %collective-permute-done.1 = bf16[256,512]{1,0:T(8,128)(2,1)} collective-permute-done((bf16[256,512]{1,0:T(8,128)(2,1)S(1)}, bf16[256,512]{1,0:T(8,128)(2,1)}, u32[]{:S(2)}, u32[]{:S(2)}) %collective-permute-start.1) | collective-permute-done | bytes 262176 | tf_op jit(solution)/shard_map/ppermute | solution.py:595
  36.6 2.8 collective-permute-done.2
  56.2 1.8 pad_maximum_fusion.x_ref
  58.0 7.2 %collective-permute-done.11.refs_5_ = bf16[1024,256]{1,0:T(8,128)(2,1)} collective-permute-done((bf16[1024,256]{1,0:T(8,128)(2,1)}, bf16[1024,256]{1,0:T(8,128)(2,1)}, u32[]{:S(2)}, u32[]{:S(2)}) %collective-permute-start.11) | collective-permute-done | bytes 524320 | tf_op jit(solution)/shard_map/ppermute | solution.py:592
  65.2 12.0 %collective-permute-done.8.refs_2_ = bf16[1024,256]{1,0:T(8,128)(2,1)} collective-permute-done((bf16[1024,256]{1,0:T(8,128)(2,1)}, bf16[1024,256]{1,0:T(8,128)(2,1)}, u32[]{:S(2)}, u32[]{:S(2)}) %collective-permute-start.8) | collective-permute-done | bytes 524320 | tf_op jit(solution)/shard_map/ppermute | solution.py:592
  80.4 10.3 %collective-permute-done.12.refs_6_ = bf16[1024,256]{1,0:T(8,128)(2,1)S(1)} collective-permute-done((bf16[1024,256]{1,0:T(8,128)(2,1)}, bf16[1024,256]{1,0:T(8,128)(2,1)S(1)}, u32[]{:S(2)}, u32[]{:S(2)}) %collective-permute-start.12) | collective-permute-done | bytes 524320 | tf_op jit(solution)/shard_map/ppermute | solution.py:592
  90.6 2.1 collective-permute-done.13.refs_7_
  93.5 10.2 %norm_qkv.1 = (bf16[1184,1024]{1,0:T(8,128)(2,1)}, bf16[1184,1536]{1,0:T(8,128)(2,1)}, bf16[1024,2048]{1,0:T(8,128)(2,1)}) custom-call(bf16[1184,1024]{1,0:T(8,128)(2,1)} %pad_maximum_fusion.x_ref, f32[6,1,1024]{2,1,0:T(1,128)} %get-tuple-element.95.gain_ref.shift_ref.bias_ref, f32[6,1,1024]{2,1,0:T(1,128)} %get-tuple-element.95.gain_ref.shift_ref.bias_ref, ...), custom_call_target="tpu_custom_call" | custom-call | flops 3724541952 | bytes 19398656 | tf_op jit(solution)/shard_map/norm_qkv/pallas_call | solution.py:111
  103.7 20.2 %attend.1 = (bf16[1184,512]{1,0:T(8,128)(2,1)}, bf16[2,8,592,592]{3,2,1,0:T(8,128)(2,1)}) custom-call(bf16[1184,1536]{1,0:T(8,128)(2,1)} %get-tuple-element.99.qkv_ref), custom_call_target="tpu_custom_call" | custom-call | flops 17226006528 | bytes 48496640 | tf_op jit(solution)/shard_map/attend/pallas_call | solution.py:140
  123.9 4.4 convolution_convert_fusion.a_ref
  132.5 22.8 %collective-permute-done.17.refs_1_ = bf16[1024,512]{1,0:T(8,128)(2,1)} collective-permute-done((bf16[1024,512]{1,0:T(8,128)(2,1)}, bf16[1024,512]{1,0:T(8,128)(2,1)}, u32[]{:S(2)}, u32[]{:S(2)}) %collective-permute-start.17) | collective-permute-done | bytes 1048608 | tf_op jit(solution)/shard_map/ppermute | solution.py:592
  158.4 2.0 pad_maximum_fusion.1.dy_ref
  160.4 6.8 %middle.1 = (f32[1184,1024]{1,0:T(8,128)}, bf16[1184,1024]{1,0:T(8,128)(2,1)}) custom-call(bf16[1184,1024]{1,0:T(8,128)(2,1)} %pad_maximum_fusion.x_ref, bf16[1184,1024]{1,0:T(8,128)(2,1)} %convolution_convert_fusion.a_ref, bf16[1184,1024]{1,0:T(8,128)(2,1)} %collective-permute-done.14.b_ref, f32[6,1,1024]{2,1,0:T(1,128)} %get-tuple-element.95.gain_ref.shift_ref.bias_ref, ...), custom_call_target="tpu_custom_call" | custom-call | flops 24248320 | bytes 14548992 | tf_op jit(solution)/shard_map/middle/pallas_call | solution.py:201
  167.2 14.4 %collective-permute-done.18.refs_2_ = bf16[1024,512]{1,0:T(8,128)(2,1)} collective-permute-done((bf16[1024,512]{1,0:T(8,128)(2,1)}, bf16[1024,512]{1,0:T(8,128)(2,1)}, u32[]{:S(2)}, u32[]{:S(2)}) %collective-permute-start.18) | collective-permute-done | bytes 1048608 | tf_op jit(solution)/shard_map/ppermute | solution.py:592
  181.6 20.5 %collective-permute-done.19.refs_3_ = bf16[1024,512]{1,0:T(8,128)(2,1)} collective-permute-done((bf16[1024,512]{1,0:T(8,128)(2,1)}, bf16[1024,512]{1,0:T(8,128)(2,1)}, u32[]{:S(2)}, u32[]{:S(2)}) %collective-permute-start.19) | collective-permute-done | bytes 1048608 | tf_op jit(solution)/shard_map/ppermute | solution.py:592
  202.1 20.6 %mlp_first.1 = (bf16[1184,1024]{1,0:T(8,128)(2,1)}, bf16[1184,1024]{1,0:T(8,128)(2,1)}, f32[1,1024]{1,0:T(1,128)}, bf16[1184,1024]{1,0:T(8,128)(2,1)}, bf16[1184,1024]{1,0:T(8,128)(2,1)}) custom-call(s32[3]{0:T(128)} %pad_add_fusion.place_ref, bf16[1184,1024]{1,0:T(8,128)(2,1)} %get-tuple-element.112.n_ref, bf16[1184,1024]{1,0:T(8,128)(2,1)} %pad_maximum_fusion.1.dy_ref, ...), custom_call_target="tpu_custom_call" | custom-call | flops 9932111872 | bytes 24248320 | tf_op jit(solution)/shard_map/mlp_first/pallas_call | solution.py:296
  222.7 4.7 convolution_convert_fusion.6
  227.4 4.3 convolution_convert_fusion.2
  231.7 22.4 %mlp_second.1 = (bf16[1184,1024]{1,0:T(8,128)(2,1)}, bf16[1184,1024]{1,0:T(8,128)(2,1)}, f32[1,1024]{1,0:T(1,128)}, f32[1184,512]{1,0:T(8,128)}, bf16[1184,512]{1,0:T(8,128)(2,1)}, /*index=5*/bf16[1184,1024]{1,0:T(8,128)(2,1)}) custom-call(s32[3]{0:T(128)} %pad_add_fusion.place_ref, bf16[1184,1024]{1,0:T(8,128)(2,1)} %get-tuple-element.112.n_ref, ...), custom_call_target="tpu_custom_call" | custom-call | flops 9932111872 | bytes 24248320 | tf_op jit(solution)/shard_map/mlp_second/pallas_call | solution.py:296
  255.9 4.5 convolution_convert_fusion.4
  260.4 2.5 convolution_convert_fusion.5
  265.5 14.2 %turn.1 = (f32[1184,1024]{1,0:T(8,128)}, bf16[1184,1024]{1,0:T(8,128)(2,1)}, bf16[1184,512]{1,0:T(8,128)(2,1)}, f32[4,1024]{1,0:T(4,128)}, bf16[1184,256]{1,0:T(8,128)(2,1)}, /*index=5*/bf16[1184,256]{1,0:T(8,128)(2,1)}) custom-call(s32[3]{0:T(128)} %pad_add_fusion.place_ref, f32[1184,1024]{1,0:T(8,128)} %get-tuple-element.105.h_ref, ...), custom_call_target="tpu_custom_call" | custom-call | flops 1241513984 | bytes 24248320 | tf_op jit(solution)/shard_map/turn/pallas_call | solution.py:360
  279.7 4.7 convolution_convert_fusion.3
  284.4 18.1 %collective-permute-done.27 = bf16[1024,512]{1,0:T(8,128)(2,1)} collective-permute-done((bf16[1024,512]{1,0:T(8,128)(2,1)}, bf16[1024,512]{1,0:T(8,128)(2,1)}, u32[]{:S(2)}, u32[]{:S(2)}) %collective-permute-start.27) | collective-permute-done | bytes 1048608 | tf_op jit(solution)/shard_map/ppermute | solution.py:592
  302.5 2.8 add_convert_fusion
  305.4 4.2 add_convert_fusion.1
  309.6 2.8 add_convert_fusion.2
  312.4 26.8 %attend_back.1 = (bf16[1184,1536]{1,0:T(8,128)(2,1)}, f32[1,1536]{1,0:T(1,128)}) custom-call(bf16[1184,1536]{1,0:T(8,128)(2,1)} %get-tuple-element.99.qkv_ref, bf16[2,8,592,592]{3,2,1,0:T(8,128)(2,1)} %get-tuple-element.128.p_ref, bf16[1184,512]{1,0:T(8,128)(2,1)} %get-tuple-element.132.g_ref), custom_call_target="tpu_custom_call" | custom-call | flops 21532508160 | bytes 60620800 | tf_op jit(solution)/shard_map/attend_back/pallas_call | solution.py:176
  341.2 2.2 convolution_convert_fusion.8
  350.0 5.5 %convolution_convert_fusion.1.a_ref = bf16[1184,1024]{1,0:T(8,128)(2,1)} fusion(bf16[1184,1536]{1,0:T(8,128)(2,1)S(1)} %copy-done.33, bf16[1024,2048]{1,0:T(8,128)(2,1)S(1)} %copy-done.2), kind=kOutput, calls=%fused_computation.1 | convolution fusion | flops 3725754368 | bytes 9207808 | tf_op jit(solution)/shard_map/dot_general | solution.py:30
  355.5 15.5 %collective-permute-done.31 = bf16[1024,256]{1,0:T(8,128)(2,1)S(1)} collective-permute-done((bf16[1024,256]{1,0:T(8,128)(2,1)S(1)}, bf16[1024,256]{1,0:T(8,128)(2,1)S(1)}, u32[]{:S(2)}, u32[]{:S(2)}) %collective-permute-start.31) | collective-permute-done | bytes 524320 | tf_op jit(solution)/shard_map/ppermute | solution.py:592
  372.7 2.5 add_convert_fusion.5
  375.7 2.4 add_convert_fusion.4
  382.2 3.7 collective-permute-done.37
  388.6 32.3 %collective-permute-done.38 = bf16[1024,128]{1,0:T(8,128)(2,1)S(1)} collective-permute-done((bf16[1024,128]{1,0:T(8,128)(2,1)}, bf16[1024,128]{1,0:T(8,128)(2,1)S(1)}, u32[]{:S(2)}, u32[]{:S(2)}) %collective-permute-start.38) | collective-permute-done | bytes 262176 | tf_op jit(solution)/shard_map/ppermute | solution.py:592
  424.0 4.9 collective-permute-done.49
  430.5 3.4 fusion.8
  437.2 8.9 %last.1 = (f32[1184,256]{1,0:T(8,128)}, bf16[1184,256]{1,0:T(8,128)(2,1)}, f32[2,256]{1,0:T(2,128)}, f32[2,256]{1,0:T(2,128)}) custom-call(s32[3]{0:T(128)} %pad_add_fusion.place_ref, bf16[1184,1024]{1,0:T(8,128)(2,1)} %pad_maximum_fusion.x_ref, f32[1184,1024]{1,0:T(8,128)} %get-tuple-element.143.dh_ref, bf16[1184,1024]{1,0:T(8,128)(2,1)} %convolution_convert_fusion.1.a_ref, ...), custom_call_target="tpu_custom_call" | custom-call | flops 24248320 | bytes 14548992 | tf_op jit(solution)/shard_map/last/pallas_call | solution.py:420
  447.5 1.7 add_convert_fusion.3
  450.8 2.2 collective-permute-done.44
  453.0 2.6 collective-permute-start.45
  455.8 4.0 collective-permute-start.42
  461.5 2.8 collective-permute-start.46
  465.5 15.8 %collective-permute-done.46 = f32[12,256]{1,0:T(8,128)S(1)} collective-permute-done((f32[12,256]{1,0:T(8,128)S(1)}, f32[12,256]{1,0:T(8,128)S(1)}, u32[]{:S(2)}, u32[]{:S(2)}) %collective-permute-start.46) | collective-permute-done | bytes 12320 | tf_op jit(solution)/shard_map/ppermute | solution.py:592
  487.1 2.2 collective-permute-done.43
  495.1 1.8 reshape.93
  496.8 8.5 %collective-permute-done.48 = bf16[256,896]{1,0:T(8,128)(2,1)} collective-permute-done((bf16[256,896]{1,0:T(8,128)(2,1)}, bf16[256,896]{1,0:T(8,128)(2,1)}, u32[]{:S(2)}, u32[]{:S(2)}) %collective-permute-start.48) | collective-permute-done | bytes 458784 | tf_op jit(solution)/shard_map/ppermute | solution.py:592
  (261 shorter events, 91.9 us)
Async XLA Ops:
  7.2 121.6 %all-gather.3.cloned.1.call-start = ((), (), s32[]{:S(2)}) async-start(), calls=%async_computation.2 | async-start | bytes 1310720 | tf_op jit(solution)/shard_map/all_gather | solution.py:682
  11.9 28.1 %collective-permute-start.3 = (bf16[256,512]{1,0:T(8,128)(2,1)S(1)}, bf16[256,512]{1,0:T(8,128)(2,1)S(1)}, u32[]{:S(2)}, u32[]{:S(2)}) collective-permute-start(bf16[256,512]{1,0:T(8,128)(2,1)S(1)} %pad_maximum_fusion.9), channel_id=1, source_target_pairs={{0,12},{4,0},{8,4},{12,8},{1,13},{5,1},{9,5},{13,9},{2,14},{6,2},{... | collective-permute-start | bytes 786440 | tf_op jit(solution)/shard_map/ppermute | solution.py:595
  17.0 22.3 %collective-permute-start.2 = (bf16[256,512]{1,0:T(8,128)(2,1)S(1)}, bf16[256,512]{1,0:T(8,128)(2,1)S(1)}, u32[]{:S(2)}, u32[]{:S(2)}) collective-permute-start(bf16[256,512]{1,0:T(8,128)(2,1)S(1)} %pad_maximum_fusion.9), channel_id=1, source_target_pairs={{0,8},{4,12},{8,0},{12,4},{1,9},{5,13},{9,1},{13,5},{2,10},{6,14},... | collective-permute-start | bytes 786440 | tf_op jit(solution)/shard_map/ppermute | solution.py:595
  17.1 17.9 %collective-permute-start.1 = (bf16[256,512]{1,0:T(8,128)(2,1)S(1)}, bf16[256,512]{1,0:T(8,128)(2,1)}, u32[]{:S(2)}, u32[]{:S(2)}) collective-permute-start(bf16[256,512]{1,0:T(8,128)(2,1)S(1)} %pad_maximum_fusion.9), channel_id=1, source_target_pairs={{0,4},{4,8},{8,12},{12,0},{1,5},{5,9},{9,13},{13,1},{2,6},{6,10},{... | collective-permute-start | bytes 786440 | tf_op jit(solution)/shard_map/ppermute | solution.py:595
  18.1 22.7 %collective-permute-start = (bf16[1154,256]{1,0:T(8,128)(2,1)S(1)}, bf16[1154,256]{1,0:T(8,128)(2,1)S(1)}, u32[]{:S(2)}, u32[]{:S(2)}) collective-permute-start(bf16[1154,256]{1,0:T(8,128)(2,1)S(1)} %get-tuple-element.220), channel_id=1, source_target_pairs={{0,2},{2,0},{1,3},{3,1},{4,6},{6,4},{5,7},{7,5},{8,10},{10,8},{9,1... | collective-permute-start | bytes 1772552 | tf_op jit(solution)/shard_map/ppermute | solution.py:592
  41.9 13.9 %collective-permute-start.4 = (bf16[1184,512]{1,0:T(8,128)(2,1)S(1)}, bf16[1184,512]{1,0:T(8,128)(2,1)S(1)}, u32[]{:S(2)}, u32[]{:S(2)}) collective-permute-start(bf16[1184,512]{1,0:T(8,128)(2,1)S(1)} %bitcast.54), channel_id=1, source_target_pairs={{0,1},{1,0},{2,3},{3,2},{4,5},{5,4},{6,7},{7,6},{8,9},{9,8},{10,11... | collective-permute-start | bytes 3637256 | tf_op jit(solution)/shard_map/ppermute | solution.py:592
  43.4 8.8 %collective-permute-start.6 = (f32[12,256]{1,0:T(8,128)}, f32[12,256]{1,0:T(8,128)S(1)}, u32[]{:S(2)}, u32[]{:S(2)}) collective-permute-start(f32[12,256]{1,0:T(8,128)} %pack.1.own), channel_id=1, source_target_pairs={{0,1},{1,0},{2,3},{3,2},{4,5},{5,4},{6,7},{7,6},{8,9},{9,8},{10,11... | collective-permute-start | bytes 36872 | tf_op jit(solution)/shard_map/ppermute | solution.py:592
  50.1 15.1 %collective-permute-start.11 = (bf16[1024,256]{1,0:T(8,128)(2,1)}, bf16[1024,256]{1,0:T(8,128)(2,1)}, u32[]{:S(2)}, u32[]{:S(2)}) collective-permute-start(bf16[1024,256]{1,0:T(8,128)(2,1)} %copy-done.20), channel_id=1, source_target_pairs={{0,16},{16,0},{1,17},{17,1},{2,18},{18,2},{3,19},{19,3},{4,20},{20... | collective-permute-start | bytes 1572872 | tf_op jit(solution)/shard_map/ppermute | solution.py:592
  51.6 28.7 %collective-permute-start.9 = (bf16[1024,256]{1,0:T(8,128)(2,1)}, bf16[1024,256]{1,0:T(8,128)(2,1)}, u32[]{:S(2)}, u32[]{:S(2)}) collective-permute-start(bf16[1024,256]{1,0:T(8,128)(2,1)} %copy-done.20), channel_id=1, source_target_pairs={{0,2},{2,0},{1,3},{3,1},{4,6},{6,4},{5,7},{7,5},{8,10},{10,8},{9,1... | collective-permute-start | bytes 1572872 | tf_op jit(solution)/shard_map/ppermute | solution.py:592
  52.2 77.3 %all-gather.5.cloned.1.call-start = ((), (), s32[]{:S(2)}) async-start(), calls=%async_computation.3 | async-start | bytes 1310720 | tf_op jit(solution)/shard_map/all_gather | solution.py:682
  52.3 28.1 %collective-permute-start.10 = (bf16[1024,256]{1,0:T(8,128)(2,1)}, bf16[1024,256]{1,0:T(8,128)(2,1)}, u32[]{:S(2)}, u32[]{:S(2)}) collective-permute-start(bf16[1024,256]{1,0:T(8,128)(2,1)} %get-tuple-element.245.refs_0_), channel_id=1, source_target_pairs={{0,16},{16,0},{1,17},{17,1},{2,18},{18,2},{3,19},{19,3},{4,20},{20... | collective-permute-start | bytes 1572872 | tf_op jit(solution)/shard_map/ppermute | solution.py:592
  52.9 24.4 %collective-permute-start.8 = (bf16[1024,256]{1,0:T(8,128)(2,1)}, bf16[1024,256]{1,0:T(8,128)(2,1)}, u32[]{:S(2)}, u32[]{:S(2)}) collective-permute-start(bf16[1024,256]{1,0:T(8,128)(2,1)} %get-tuple-element.245.refs_0_), channel_id=1, source_target_pairs={{0,2},{2,0},{1,3},{3,1},{4,6},{6,4},{5,7},{7,5},{8,10},{10,8},{9,1... | collective-permute-start | bytes 1572872 | tf_op jit(solution)/shard_map/ppermute | solution.py:592
  77.2 13.4 %collective-permute-start.12 = (bf16[1024,256]{1,0:T(8,128)(2,1)}, bf16[1024,256]{1,0:T(8,128)(2,1)S(1)}, u32[]{:S(2)}, u32[]{:S(2)}) collective-permute-start(bf16[1024,256]{1,0:T(8,128)(2,1)} %collective-permute-done.8.refs_2_), channel_id=1, source_target_pairs={{0,16},{16,0},{1,17},{17,1},{2,18},{18,2},{3,19},{19,3},{4,20},{20... | collective-permute-start | bytes 1572872 | tf_op jit(solution)/shard_map/ppermute | solution.py:592
  77.8 15.0 %collective-permute-start.13 = (bf16[1024,256]{1,0:T(8,128)(2,1)}, bf16[1024,256]{1,0:T(8,128)(2,1)S(1)}, u32[]{:S(2)}, u32[]{:S(2)}) collective-permute-start(bf16[1024,256]{1,0:T(8,128)(2,1)} %collective-permute-done.11.refs_5_), channel_id=1, source_target_pairs={{0,2},{2,0},{1,3},{3,1},{4,6},{6,4},{5,7},{7,5},{8,10},{10,8},{9,1... | collective-permute-start | bytes 1572872 | tf_op jit(solution)/shard_map/ppermute | solution.py:592
  78.6 309.0 %reduce-scatter.5.cloned.1.call-start = ((), (), s32[]{:S(2)}) async-start(), calls=%async_computation.5 | async-start | bytes 2621440 | tf_op jit(solution)/shard_map/reduce_scatter | solution.py:724
  78.8 49.5 %collective-permute-start.15 = (bf16[1154,256]{1,0:T(8,128)(2,1)S(1)}, bf16[1154,256]{1,0:T(8,128)(2,1)S(1)}, u32[]{:S(2)}, u32[]{:S(2)}) collective-permute-start(bf16[1154,256]{1,0:T(8,128)(2,1)S(1)} %get-tuple-element.102), channel_id=1, source_target_pairs={{0,2},{2,0},{1,3},{3,1},{4,6},{6,4},{5,7},{7,5},{8,10},{10,8},{9,1... | collective-permute-start | bytes 1772552 | tf_op jit(solution)/shard_map/ppermute | solution.py:592
  128.8 28.6 %collective-permute-start.16 = (bf16[1184,512]{1,0:T(8,128)(2,1)S(1)}, bf16[1184,512]{1,0:T(8,128)(2,1)S(1)}, u32[]{:S(2)}, u32[]{:S(2)}) collective-permute-start(bf16[1184,512]{1,0:T(8,128)(2,1)S(1)} %bitcast.55), channel_id=1, source_target_pairs={{0,1},{1,0},{2,3},{3,2},{4,5},{5,4},{6,7},{7,6},{8,9},{9,8},{10,11... | collective-permute-start | bytes 3637256 | tf_op jit(solution)/shard_map/ppermute | solution.py:592
  128.9 26.4 %collective-permute-start.17 = (bf16[1024,512]{1,0:T(8,128)(2,1)}, bf16[1024,512]{1,0:T(8,128)(2,1)}, u32[]{:S(2)}, u32[]{:S(2)}) collective-permute-start(bf16[1024,512]{1,0:T(8,128)(2,1)} %all-gather.3.cloned.1.call-done.refs_0_), channel_id=1, source_target_pairs={{0,2},{2,0},{1,3},{3,1},{4,6},{6,4},{5,7},{7,5},{8,10},{10,8},{9,1... | collective-permute-start | bytes 3145736 | tf_op jit(solution)/shard_map/ppermute | solution.py:592
  129.5 27.4 %collective-permute-start.20 = (bf16[1024,512]{1,0:T(8,128)(2,1)}, bf16[1024,512]{1,0:T(8,128)(2,1)}, u32[]{:S(2)}, u32[]{:S(2)}) collective-permute-start(bf16[1024,512]{1,0:T(8,128)(2,1)} %all-gather.5.cloned.1.call-done.refs_0_), channel_id=1, source_target_pairs={{0,16},{16,0},{1,17},{17,1},{2,18},{18,2},{3,19},{19,3},{4,20},{20... | collective-permute-start | bytes 3145736 | tf_op jit(solution)/shard_map/ppermute | solution.py:592
  131.0 29.5 %collective-permute-start.14 = (bf16[1184,1024]{1,0:T(8,128)(2,1)}, bf16[1184,1024]{1,0:T(8,128)(2,1)}, u32[]{:S(2)}, u32[]{:S(2)}) collective-permute-start(bf16[1184,1024]{1,0:T(8,128)(2,1)} %convolution_convert_fusion.a_ref), channel_id=1, source_target_pairs={{0,1},{1,0},{2,3},{3,2},{4,5},{5,4},{6,7},{7,6},{8,9},{9,8},{10,11... | collective-permute-start | bytes 7274504 | tf_op jit(solution)/shard_map/ppermute | solution.py:592
  131.0 100.7 %collective-permute-start.21 = (bf16[1024,512]{1,0:T(8,128)(2,1)}, bf16[1024,512]{1,0:T(8,128)(2,1)}, u32[]{:S(2)}, u32[]{:S(2)}) collective-permute-start(bf16[1024,512]{1,0:T(8,128)(2,1)} %all-gather.5.cloned.1.call-done.refs_0_), channel_id=1, source_target_pairs={{0,2},{2,0},{1,3},{3,1},{4,6},{6,4},{5,7},{7,5},{8,10},{10,8},{9,1... | collective-permute-start | bytes 3145736 | tf_op jit(solution)/shard_map/ppermute | solution.py:592
  155.3 26.3 %collective-permute-start.18 = (bf16[1024,512]{1,0:T(8,128)(2,1)}, bf16[1024,512]{1,0:T(8,128)(2,1)}, u32[]{:S(2)}, u32[]{:S(2)}) collective-permute-start(bf16[1024,512]{1,0:T(8,128)(2,1)} %all-gather.3.cloned.1.call-done.refs_0_), channel_id=1, source_target_pairs={{0,16},{16,0},{1,17},{17,1},{2,18},{18,2},{3,19},{19,3},{4,20},{20... | collective-permute-start | bytes 3145736 | tf_op jit(solution)/shard_map/ppermute | solution.py:592
  156.8 45.3 %collective-permute-start.19 = (bf16[1024,512]{1,0:T(8,128)(2,1)}, bf16[1024,512]{1,0:T(8,128)(2,1)}, u32[]{:S(2)}, u32[]{:S(2)}) collective-permute-start(bf16[1024,512]{1,0:T(8,128)(2,1)} %collective-permute-done.17.refs_1_), channel_id=1, source_target_pairs={{0,16},{16,0},{1,17},{17,1},{2,18},{18,2},{3,19},{19,3},{4,20},{20... | collective-permute-start | bytes 3145736 | tf_op jit(solution)/shard_map/ppermute | solution.py:592
  157.3 74.4 %collective-permute-start.22 = (bf16[1024,512]{1,0:T(8,128)(2,1)}, bf16[1024,512]{1,0:T(8,128)(2,1)}, u32[]{:S(2)}, u32[]{:S(2)}) collective-permute-start(bf16[1024,512]{1,0:T(8,128)(2,1)} %collective-permute-done.20.refs_1_), channel_id=1, source_target_pairs={{0,2},{2,0},{1,3},{3,1},{4,6},{6,4},{5,7},{7,5},{8,10},{10,8},{9,1... | collective-permute-start | bytes 3145736 | tf_op jit(solution)/shard_map/ppermute | solution.py:592
  254.1 10.0 %collective-permute-start.23 = (bf16[1184,1024]{1,0:T(8,128)(2,1)}, bf16[1184,1024]{1,0:T(8,128)(2,1)S(1)}, u32[]{:S(2)}, u32[]{:S(2)}) collective-permute-start(bf16[1184,1024]{1,0:T(8,128)(2,1)} %get-tuple-element.116.a_ref), channel_id=1, source_target_pairs={{0,1},{1,0},{2,3},{3,2},{4,5},{5,4},{6,7},{7,6},{8,9},{9,8},{10,11... | collective-permute-start | bytes 7274504 | tf_op jit(solution)/shard_map/ppermute | solution.py:592
  254.2 30.3 %collective-permute-start.25 = (bf16[1024,512]{1,0:T(8,128)(2,1)}, bf16[1024,512]{1,0:T(8,128)(2,1)}, u32[]{:S(2)}, u32[]{:S(2)}) collective-permute-start(bf16[1024,512]{1,0:T(8,128)(2,1)} %convolution_convert_fusion.6), channel_id=1, source_target_pairs={{0,16},{16,0},{1,17},{17,1},{2,18},{18,2},{3,19},{19,3},{4,20},{20... | collective-permute-start | bytes 3145736 | tf_op jit(solution)/shard_map/ppermute | solution.py:592
  255.7 8.3 %collective-permute-start.24 = (bf16[1184,512]{1,0:T(8,128)(2,1)}, bf16[1184,512]{1,0:T(8,128)(2,1)}, u32[]{:S(2)}, u32[]{:S(2)}) collective-permute-start(bf16[1184,512]{1,0:T(8,128)(2,1)} %get-tuple-element.121), channel_id=1, source_target_pairs={{0,1},{1,0},{2,3},{3,2},{4,5},{5,4},{6,7},{7,6},{8,9},{9,8},{10,11... | collective-permute-start | bytes 3637256 | tf_op jit(solution)/shard_map/ppermute | solution.py:592
  262.9 39.6 %collective-permute-start.27 = (bf16[1024,512]{1,0:T(8,128)(2,1)}, bf16[1024,512]{1,0:T(8,128)(2,1)}, u32[]{:S(2)}, u32[]{:S(2)}) collective-permute-start(bf16[1024,512]{1,0:T(8,128)(2,1)} %convolution_convert_fusion.4), channel_id=1, source_target_pairs={{0,16},{16,0},{1,17},{17,1},{2,18},{18,2},{3,19},{19,3},{4,20},{20... | collective-permute-start | bytes 3145736 | tf_op jit(solution)/shard_map/ppermute | solution.py:592
  263.4 39.1 %collective-permute-start.26 = (bf16[1024,512]{1,0:T(8,128)(2,1)}, bf16[1024,512]{1,0:T(8,128)(2,1)}, u32[]{:S(2)}, u32[]{:S(2)}) collective-permute-start(bf16[1024,512]{1,0:T(8,128)(2,1)} %convolution_convert_fusion.5), channel_id=1, source_target_pairs={{0,2},{2,0},{1,3},{3,1},{4,6},{6,4},{5,7},{7,5},{8,10},{10,8},{9,1... | collective-permute-start | bytes 3145736 | tf_op jit(solution)/shard_map/ppermute | solution.py:592
  264.0 229.9 %reduce-scatter.3.cloned.1.call-start = ((), (), s32[]{:S(2)}) async-start(), calls=%async_computation.4 | async-start | bytes 2293760 | tf_op jit(solution)/shard_map/reduce_scatter | solution.py:744
  343.4 27.7 %collective-permute-start.30 = (bf16[1024,128]{1,0:T(8,128)(2,1)S(1)}, bf16[1024,128]{1,0:T(8,128)(2,1)S(1)}, u32[]{:S(2)}, u32[]{:S(2)}) collective-permute-start(bf16[1024,128]{1,0:T(8,128)(2,1)S(1)} %convolution_convert_fusion.8), channel_id=1, source_target_pairs={{0,2},{2,0},{1,3},{3,1},{4,6},{6,4},{5,7},{7,5},{8,10},{10,8},{9,1... | collective-permute-start | bytes 786440 | tf_op jit(solution)/shard_map/ppermute | solution.py:592
  344.9 30.3 %collective-permute-start.29 = (bf16[1024,256]{1,0:T(8,128)(2,1)S(1)}, bf16[1024,256]{1,0:T(8,128)(2,1)S(1)}, u32[]{:S(2)}, u32[]{:S(2)}) collective-permute-start(bf16[1024,256]{1,0:T(8,128)(2,1)S(1)} %convolution_convert_fusion.7), channel_id=1, source_target_pairs={{0,16},{16,0},{1,17},{17,1},{2,18},{18,2},{3,19},{19,3},{4,20},{20... | collective-permute-start | bytes 1572872 | tf_op jit(solution)/shard_map/ppermute | solution.py:592
  346.4 24.5 %collective-permute-start.31 = (bf16[1024,256]{1,0:T(8,128)(2,1)S(1)}, bf16[1024,256]{1,0:T(8,128)(2,1)S(1)}, u32[]{:S(2)}, u32[]{:S(2)}) collective-permute-start(bf16[1024,256]{1,0:T(8,128)(2,1)S(1)} %slice.277), channel_id=1, source_target_pairs={{0,16},{16,0},{1,17},{17,1},{2,18},{18,2},{3,19},{19,3},{4,20},{20... | collective-permute-start | bytes 1572872 | tf_op jit(solution)/shard_map/ppermute | solution.py:592
  346.9 33.6 %collective-permute-start.36 = (bf16[1024,256]{1,0:T(8,128)(2,1)S(1)}, bf16[1024,256]{1,0:T(8,128)(2,1)S(1)}, u32[]{:S(2)}, u32[]{:S(2)}) collective-permute-start(bf16[1024,256]{1,0:T(8,128)(2,1)S(1)} %slice.281), channel_id=1, source_target_pairs={{0,16},{16,0},{1,17},{17,1},{2,18},{18,2},{3,19},{19,3},{4,20},{20... | collective-permute-start | bytes 1572872 | tf_op jit(solution)/shard_map/ppermute | solution.py:592
  348.5 30.4 %collective-permute-start.35 = (bf16[1024,256]{1,0:T(8,128)(2,1)S(1)}, bf16[1024,256]{1,0:T(8,128)(2,1)S(1)}, u32[]{:S(2)}, u32[]{:S(2)}) collective-permute-start(bf16[1024,256]{1,0:T(8,128)(2,1)S(1)} %slice.279), channel_id=1, source_target_pairs={{0,2},{2,0},{1,3},{3,1},{4,6},{6,4},{5,7},{7,5},{8,10},{10,8},{9,1... | collective-permute-start | bytes 1572872 | tf_op jit(solution)/shard_map/ppermute | solution.py:592
  371.0 66.2 %collective-permute-start.34 = (bf16[1184,1024]{1,0:T(8,128)(2,1)}, bf16[1184,1024]{1,0:T(8,128)(2,1)}, u32[]{:S(2)}, u32[]{:S(2)}) collective-permute-start(bf16[1184,1024]{1,0:T(8,128)(2,1)} %convolution_convert_fusion.1.a_ref), channel_id=1, source_target_pairs={{0,1},{1,0},{2,3},{3,2},{4,5},{5,4},{6,7},{7,6},{8,9},{9,8},{10,11... | collective-permute-start | bytes 7274504 | tf_op jit(solution)/shard_map/ppermute | solution.py:592
  371.1 14.9 %collective-permute-start.37 = (bf16[1024,256]{1,0:T(8,128)(2,1)S(1)}, bf16[1024,256]{1,0:T(8,128)(2,1)S(1)}, u32[]{:S(2)}, u32[]{:S(2)}) collective-permute-start(bf16[1024,256]{1,0:T(8,128)(2,1)S(1)} %slice.283), channel_id=1, source_target_pairs={{0,2},{2,0},{1,3},{3,1},{4,6},{6,4},{5,7},{7,5},{8,10},{10,8},{9,1... | collective-permute-start | bytes 1572872 | tf_op jit(solution)/shard_map/ppermute | solution.py:592
  375.2 80.5 %collective-permute-start.28 = (bf16[1184,256]{1,0:T(8,128)(2,1)}, bf16[1184,256]{1,0:T(8,128)(2,1)}, u32[]{:S(2)}, u32[]{:S(2)}) collective-permute-start(bf16[1184,256]{1,0:T(8,128)(2,1)} %get-tuple-element.126), channel_id=1, source_target_pairs={{0,2},{2,0},{1,3},{3,1},{4,6},{6,4},{5,7},{7,5},{8,10},{10,8},{9,1... | collective-permute-start | bytes 1818632 | tf_op jit(solution)/shard_map/ppermute | solution.py:592
  378.8 68.6 %collective-permute-start.33 = (bf16[1024,384]{1,0:T(8,128)(2,1)}, bf16[1024,384]{1,0:T(8,128)(2,1)}, u32[]{:S(2)}, u32[]{:S(2)}) collective-permute-start(bf16[1024,384]{1,0:T(8,128)(2,1)} %add_convert_fusion.4), channel_id=1, source_target_pairs={{0,2},{2,0},{1,3},{3,1},{4,6},{6,4},{5,7},{7,5},{8,10},{10,8},{9,1... | collective-permute-start | bytes 2359304 | tf_op jit(solution)/shard_map/ppermute | solution.py:592
  380.5 67.0 %collective-permute-start.32 = (bf16[1024,384]{1,0:T(8,128)(2,1)}, bf16[1024,384]{1,0:T(8,128)(2,1)}, u32[]{:S(2)}, u32[]{:S(2)}) collective-permute-start(bf16[1024,384]{1,0:T(8,128)(2,1)} %add_convert_fusion.5), channel_id=1, source_target_pairs={{0,16},{16,0},{1,17},{17,1},{2,18},{18,2},{3,19},{19,3},{4,20},{20... | collective-permute-start | bytes 2359304 | tf_op jit(solution)/shard_map/ppermute | solution.py:592
  386.0 35.0 %collective-permute-start.38 = (bf16[1024,128]{1,0:T(8,128)(2,1)}, bf16[1024,128]{1,0:T(8,128)(2,1)S(1)}, u32[]{:S(2)}, u32[]{:S(2)}) collective-permute-start(bf16[1024,128]{1,0:T(8,128)(2,1)} %slice.285), channel_id=1, source_target_pairs={{0,2},{2,0},{1,3},{3,1},{4,6},{6,4},{5,7},{7,5},{8,10},{10,8},{9,1... | collective-permute-start | bytes 786440 | tf_op jit(solution)/shard_map/ppermute | solution.py:592
  453.0 8.5 %collective-permute-start.45 = (f32[12,256]{1,0:T(8,128)S(1)}, f32[12,256]{1,0:T(8,128)S(1)}, u32[]{:S(2)}, u32[]{:S(2)}) collective-permute-start(f32[12,256]{1,0:T(8,128)S(1)} %add.194), channel_id=1, source_target_pairs={{0,4},{4,0},{8,12},{12,8},{1,5},{5,1},{9,13},{13,9},{2,6},{6,2},{1... | collective-permute-start | bytes 36872 | tf_op jit(solution)/shard_map/ppermute | solution.py:592
  455.7 27.1 %collective-permute-start.40 = (bf16[256,384]{1,0:T(8,128)(2,1)S(1)}, bf16[256,384]{1,0:T(8,128)(2,1)S(1)}, u32[]{:S(2)}, u32[]{:S(2)}) collective-permute-start(bf16[256,384]{1,0:T(8,128)(2,1)S(1)} %get-tuple-element.227), channel_id=1, source_target_pairs={{0,4},{4,8},{8,12},{12,0},{1,5},{5,9},{9,13},{13,1},{2,6},{6,10},{... | collective-permute-start | bytes 589832 | tf_op jit(solution)/shard_map/ppermute | solution.py:595
  455.8 27.0 %collective-permute-start.42 = (bf16[256,384]{1,0:T(8,128)(2,1)S(1)}, bf16[256,384]{1,0:T(8,128)(2,1)S(1)}, u32[]{:S(2)}, u32[]{:S(2)}) collective-permute-start(bf16[256,384]{1,0:T(8,128)(2,1)S(1)} %get-tuple-element.228), channel_id=1, source_target_pairs={{0,12},{4,0},{8,4},{12,8},{1,13},{5,1},{9,5},{13,9},{2,14},{6,2},{... | collective-permute-start | bytes 589832 | tf_op jit(solution)/shard_map/ppermute | solution.py:595
  459.8 23.0 %collective-permute-start.41 = (bf16[256,384]{1,0:T(8,128)(2,1)S(1)}, bf16[256,384]{1,0:T(8,128)(2,1)S(1)}, u32[]{:S(2)}, u32[]{:S(2)}) collective-permute-start(bf16[256,384]{1,0:T(8,128)(2,1)S(1)} %get-tuple-element.229), channel_id=1, source_target_pairs={{0,8},{4,12},{8,0},{12,4},{1,9},{5,13},{9,1},{13,5},{2,10},{6,14},... | collective-permute-start | bytes 589832 | tf_op jit(solution)/shard_map/ppermute | solution.py:595
  460.0 31.4 %collective-permute-start.39 = (bf16[1184,256]{1,0:T(8,128)(2,1)}, bf16[1184,256]{1,0:T(8,128)(2,1)S(1)}, u32[]{:S(2)}, u32[]{:S(2)}) collective-permute-start(bf16[1184,256]{1,0:T(8,128)(2,1)} %get-tuple-element.153), channel_id=1, source_target_pairs={{0,2},{2,0},{1,3},{3,1},{4,6},{6,4},{5,7},{7,5},{8,10},{10,8},{9,1... | collective-permute-start | bytes 1818632 | tf_op jit(solution)/shard_map/ppermute | solution.py:592
  461.5 19.8 %collective-permute-start.46 = (f32[12,256]{1,0:T(8,128)S(1)}, f32[12,256]{1,0:T(8,128)S(1)}, u32[]{:S(2)}, u32[]{:S(2)}) collective-permute-start(f32[12,256]{1,0:T(8,128)S(1)} %add.195), channel_id=1, source_target_pairs={{0,8},{4,12},{8,0},{12,4},{1,9},{5,13},{9,1},{13,5},{2,10},{6,14},... | collective-permute-start | bytes 36872 | tf_op jit(solution)/shard_map/ppermute | solution.py:592
  494.0 11.4 %collective-permute-start.48 = (bf16[256,896]{1,0:T(8,128)(2,1)}, bf16[256,896]{1,0:T(8,128)(2,1)}, u32[]{:S(2)}, u32[]{:S(2)}) collective-permute-start(bf16[256,896]{1,0:T(8,128)(2,1)} %reduce-scatter.3.cloned.1.call-done), channel_id=1, source_target_pairs={{0,16},{16,0},{1,17},{17,1},{2,18},{18,2},{3,19},{19,3},{4,20},{20... | collective-permute-start | bytes 1376264 | tf_op jit(solution)/shard_map/ppermute | solution.py:592
  (47 other events, 507.2 us)
Sparse Core Ops, SparseCore 0:
  52.3 29.2 all-gather.2
  83.7 27.3 all-gather.4
  264.1 45.8 reduce-scatter.4
  424.1 47.1 reduce-scatter.2

commit v8 on v7

--- a/solution.py
+++ b/solution.py
@@ -436,6 +436,34 @@
         compiler_params=params(1),
         cost_estimate=cost(20 * rows * D, 12 * rows * D),
     )(place, x, dh, a, b, gain[0])
+
+
+def join_kernel(*refs):
+    out_ref = refs[-1]
+    start = 0
+    for mine, got in zip(refs[:-1:2], refs[1:-1:2]):
+        width = got.shape[1]
+        total = mine[...].astype(F32) + got[...].astype(F32)
+        out_ref[:, start : start + width] = total.astype(BF16)
+        start += width
+
+
+def join(*parts):
+    rows = parts[0].shape[0]
+    tm = rows // 4
+    widths = [item.shape[1] for item in parts[1::2]]
+    return pl.pallas_call(
+        join_kernel,
+        grid=(4,),
+        name="join",
+        in_specs=[
+            pl.BlockSpec((tm, width), lambda i: (i, 0)) for width in widths for _ in range(2)
+        ],
+        out_specs=pl.BlockSpec((tm, sum(widths)), lambda i: (i, 0)),
+        out_shape=like((rows, sum(widths)), BF16),
+        compiler_params=params(1),
+        cost_estimate=cost(rows * sum(widths), 6 * rows * sum(widths)),
+    )(*parts)
 
 
 def pack_kernel(*refs):
@@ -641,16 +669,6 @@
     attn_shard = after(attn_shard, input_leaves)
     input_got = across(input_leaves)
     pieces = [attn_shard] + [shifted(attn_shard, shift) for shift in range(1, n_row)]
-    cut = 2 * heads_half
-    first_own = jnp.zeros((D, cut), BF16)
-    second_own = jnp.zeros((D, cut), BF16)
-    for shift, piece in enumerate(pieces):
-        start = (my_row - shift) % n_row * (D // n_row)
-        first_own = lax.dynamic_update_slice(first_own, piece[:, :cut], (start, 0))
-        second_own = lax.dynamic_update_slice(second_own, piece[:, cut:], (start, 0))
-    first_far, second_oth = across(first_own), over(second_own)
-    first_oth, second_far = over(first_own), across(second_own)
-
     small = pack(
         (
             out_bias,
@@ -664,6 +682,17 @@
         ),
         up_bias,
     )
+    pieces = [pieces[0]] + [after(piece, small) for piece in pieces[1:]]
+    cut = 2 * heads_half
+    first_own = jnp.zeros((D, cut), BF16)
+    second_own = jnp.zeros((D, cut), BF16)
+    for shift, piece in enumerate(pieces):
+        start = (my_row - shift) % n_row * (D // n_row)
+        first_own = lax.dynamic_update_slice(first_own, piece[:, :cut], (start, 0))
+        second_own = lax.dynamic_update_slice(second_own, piece[:, cut:], (start, 0))
+    first_far, second_oth = across(first_own), over(second_own)
+    first_oth, second_far = over(first_own), across(second_own)
+
     small_far = across(small)
     vectors, qkv_bias, tile_bias = unpack(
         place, small, after(small_far, first_own, second_own), beside(small), beside(small_far)
@@ -706,7 +735,7 @@
     mixed = mm_nt(attended, attn_weights[:, 4 * three :]).astype(BF16)
     mixed_other = beside(mixed)
     wide_grad = wide_tokens(cotangent, after(grad_got, mixed))
-    far_oth_a = over(after(far_a, mixed))
+    far_oth_a = over(far_a)
     middle_sum, wide_two = middle(
         wide_input, mixed, after(mixed_other, wide_grad), out_bias_all, gain_two, shift_two
     )
@@ -748,6 +777,7 @@
     up_across = mm_tn(wide_two, tiles(pre_b, 2, 4)).astype(BF16)
     down_over = mm_tn(wide_grad, tiles(gate_b, 2, 4)).astype(BF16)
     up_across_got, down_over_got = across(up_across), over(down_over)
+    down_x_got = across(after(down_piece, up_across, down_over)[:, half:])
 
     middle_grad, attn_grad, head_grad, turn_sums, out_mine, out_theirs = turn(
         place,
@@ -770,19 +800,25 @@
     up_b = wide_add(mm_tn(wide_two, tiles(pre_b, 0, 2)), up_across_got)
     down_b = wide_add(mm_tn(wide_grad, tiles(gate_b, 0, 2)), down_over_got)
     up_a_got, up_b_got = across(up_a[:, quarter:]), over(up_b[:, quarter:])
+    out_own = wide_add(out_all[:, : 2 * heads_half], after(out_over_got, down_b))
+    out_far_got = across(out_own[:, heads_half:])
+    down_x = wide_add(down_piece[:, :half], after(down_x_got, down_b))
+    down_y_got = over(down_x)
     down_b_got = across(down_b[:, quarter:])
     out_got = across(after(out_theirs, down_b))
-    dqkv, qkv_sums = attend_back(qkv, probs, after(head_grad, up_a, up_b, down_b))
+    dqkv, qkv_sums = attend_back(qkv, probs, after(head_grad, up_a, up_b, out_own, down_x))
+    up_sum = join(
+        up_a, up_a_got, up_b, up_b_got, down_b, down_b_got, out_own, after(out_far_got, dqkv)
+    )
+    up_piece = same_half(scatter(up_sum))
 
     def to_feature_blocks(mine, got, dtype):
         first, second = in_order(mine.astype(dtype), got.astype(dtype), my_x)
         both = jnp.concatenate([first, second]).reshape(images, PAD, width)
         return both[:, :SEQ].reshape(tokens_here, width)
 
-    down_piece = after(down_piece, dqkv)
-    down_x_got = across(down_piece[:, half:])
-
     split = 3 * three + cut
+    dqkv = after(dqkv, up_sum)
     far_oth_qk = mm_tn(wide_one, dqkv[:, 3 * three : split]).astype(BF16)
     far_oth_v = mm_tn(wide_one, dqkv[:, split:]).astype(BF16)
     qk_got, v_got = over(far_oth_qk), across(far_oth_v)
@@ -791,11 +827,9 @@
     ).astype(BF16)
     lifted_one_other = beside(lifted_one)
 
-    out_own = wide_add(out_all[:, : 2 * heads_half], after(out_over_got, lifted_one))
-    out_far_got = across(out_own[:, heads_half:])
     near_oth = wide_add(
         mm_tn(wide_one, dqkv[:, 2 * three : 3 * three]),
-        jnp.pad(after(v_got, out_own), ((0, 0), (cut, 0))),
+        jnp.pad(after(v_got, lifted_one), ((0, 0), (cut, 0))),
     )
     near_oth_got = over(near_oth)
     far_own = wide_add(
@@ -804,25 +838,8 @@
     )
     far_own_got = across(far_own)
     near_own = mm_tn(after(wide_one, far_own), dqkv[:, :three])
-    up_sum = jnp.concatenate(
-        [
-            wide_add(up_a[:, :quarter], after(up_a_got, far_own)),
-            wide_add(up_b[:, :quarter], up_b_got),
-            wide_add(down_b[:, :quarter], down_b_got),
-            wide_add(out_own[:, :heads_half], out_far_got),
-        ],
-        axis=1,
-    )
-    up_piece = same_half(scatter(up_sum))
-    down_x = wide_add(down_piece[:, :half], after(down_x_got, far_own))
-    down_y_got = over(down_x)
     input_mine, input_theirs, late_mine, late_theirs = last(
-        place,
-        wide_input,
-        middle_grad,
-        lifted_one,
-        after(lifted_one_other, near_own, up_sum),
-        gain_one,
+        place, wide_input, middle_grad, lifted_one, after(lifted_one_other, near_own), gain_one
     )
     mine_sums, theirs_sums = collect(
         place, turn_sums, qkv_sums, up_sums_a, up_sums_b, late_mine, late_theirs

time: 524 us -> 493 us (0.941)
  waiting for transfers between devices: 211 us -> 177 us
    ppermute x45, waiting for transfers between devices: 194 us -> 164 us  [swap(): return lax.ppermute(value, axis, [(at, at ^ bit) for at in range(size)])]
  transfers between devices with their start and end apart: 55 -> 55, of which waited for: 20 -> 24; matrix products, arithmetic and copies ran while one was open for 16% -> 14% of each run, Pallas kernels for 22% -> 23%
where the time goes in v8:
time: 493 us; the launch traced here: 487 us
  waiting for transfers between devices  177 us (36%)
  Pallas kernels  140 us (28%)
  starting transfers between devices  57.3 us (12%)
  matrix products  52.8 us (11%)
  local copies, waits for them, and re-layouts  26.4 us (5%)
  other arithmetic  18.6 us (4%)
  between operations  15 us (3%)
    ppermute x45, waiting for transfers between devices, swap(): return lax.ppermute(value, axis, [(at, at ^ bit) for at in range(size)])  164 us
    ppermute x45, starting transfers between devices, swap(): return lax.ppermute(value, axis, [(at, at ^ bit) for at in range(size)])  45.1 us
    dot_general x13, matrix products, mm_tn(): lax.dot_general(a, b, (((0,), (0,)), ((), ())), preferred_element_type=F32)  43 us
    pallas_call x2, Pallas kernels, mlp(): pl.pallas_call(functools.partial(mlp_kernel, bool(before)), name='mlp_sec...  43 us
    pallas_call x1, Pallas kernels, attend_back(): pl.pallas_call(attend_back_kernel, grid=(pairs, held), name='attend_back'...  26.6 us
    pallas_call x1, Pallas kernels, attend(): pl.pallas_call(attend_kernel, grid=(pairs, held), name='attend', in_specs...  20.2 us
    pallas_call x1, Pallas kernels, turn(): pl.pallas_call(turn_kernel, name='turn', grid_spec=pltpu.PrefetchScalarGr...  14.2 us
    ppermute x6, waiting for transfers between devices, shifted(): lax.ppermute(value, 'row', [(at, (at + shift) % n_row) for at in range(n_...  12.7 us
  transfers between devices with their start and end apart: 55, of which 24 were waited for; matrix products, arithmetic and copies ran while one was open for 14% of the time, Pallas kernels for 23%

profile of v8, /device:TPU:0, one launch (start us, length us, event | category | flops | bytes accessed | tf_op | source)
XLA Modules:
  0.0 487.1 jit_solution(12697237893400881810)
XLA Ops:
  11.2 3.1 collective-permute-start.1
  14.3 2.6 collective-permute-start.2
  21.4 2.4 collective-permute-done.1
  23.8 10.3 %collective-permute-done.2 = bf16[256,512]{1,0:T(8,128)(2,1)S(1)} collective-permute-done((bf16[256,512]{1,0:T(8,128)(2,1)S(1)}, bf16[256,512]{1,0:T(8,128)(2,1)S(1)}, u32[]{:S(2)}, u32[]{:S(2)}) %collective-permute-start.2) | collective-permute-done | bytes 262176 | tf_op jit(solution)/shard_map/ppermute | solution.py:623
  51.5 7.2 %collective-permute-done.11.refs_5_ = bf16[1024,256]{1,0:T(8,128)(2,1)} collective-permute-done((bf16[1024,256]{1,0:T(8,128)(2,1)}, bf16[1024,256]{1,0:T(8,128)(2,1)}, u32[]{:S(2)}, u32[]{:S(2)}) %collective-permute-start.11) | collective-permute-done | bytes 524320 | tf_op jit(solution)/shard_map/ppermute | solution.py:620
  62.8 7.1 %collective-permute-done.10.refs_4_ = bf16[1024,256]{1,0:T(8,128)(2,1)} collective-permute-done((bf16[1024,256]{1,0:T(8,128)(2,1)}, bf16[1024,256]{1,0:T(8,128)(2,1)}, u32[]{:S(2)}, u32[]{:S(2)}) %collective-permute-start.10) | collective-permute-done | bytes 524320 | tf_op jit(solution)/shard_map/ppermute | solution.py:620
  71.4 11.1 %collective-permute-done.13.refs_7_ = bf16[1024,256]{1,0:T(8,128)(2,1)S(1)} collective-permute-done((bf16[1024,256]{1,0:T(8,128)(2,1)}, bf16[1024,256]{1,0:T(8,128)(2,1)S(1)}, u32[]{:S(2)}, u32[]{:S(2)}) %collective-permute-start.13) | collective-permute-done | bytes 524320 | tf_op jit(solution)/shard_map/ppermute | solution.py:620
  83.5 10.2 %norm_qkv.1 = (bf16[1184,1024]{1,0:T(8,128)(2,1)}, bf16[1184,1536]{1,0:T(8,128)(2,1)}, bf16[1024,2048]{1,0:T(8,128)(2,1)}) custom-call(bf16[1184,1024]{1,0:T(8,128)(2,1)} %pad_maximum_fusion.x_ref, f32[6,1,1024]{2,1,0:T(1,128)} %get-tuple-element.101.gain_ref.shift_ref.bias_ref, f32[6,1,1024]{2,1,0:T(1,128)} %get-tuple-element.101.gain_ref.shift_ref.bias_ref, ...), custom_call_target="tpu_custom_call" | custom-call | flops 3724541952 | bytes 19398656 | tf_op jit(solution)/shard_map/norm_qkv/pallas_call | solution.py:111
  93.7 20.2 %attend.1 = (bf16[1184,512]{1,0:T(8,128)(2,1)}, bf16[2,8,592,592]{3,2,1,0:T(8,128)(2,1)}) custom-call(bf16[1184,1536]{1,0:T(8,128)(2,1)} %get-tuple-element.105.qkv_ref), custom_call_target="tpu_custom_call" | custom-call | flops 17226006528 | bytes 48496640 | tf_op jit(solution)/shard_map/attend/pallas_call | solution.py:140
  113.9 4.5 convolution_convert_fusion.a_ref
  121.5 23.3 %collective-permute-done.17.refs_1_ = bf16[1024,512]{1,0:T(8,128)(2,1)} collective-permute-done((bf16[1024,512]{1,0:T(8,128)(2,1)}, bf16[1024,512]{1,0:T(8,128)(2,1)}, u32[]{:S(2)}, u32[]{:S(2)}) %collective-permute-start.17) | collective-permute-done | bytes 1048608 | tf_op jit(solution)/shard_map/ppermute | solution.py:620
  148.2 2.0 pad_maximum_fusion.1.dy_ref
  150.2 6.8 %middle.1 = (f32[1184,1024]{1,0:T(8,128)}, bf16[1184,1024]{1,0:T(8,128)(2,1)}) custom-call(bf16[1184,1024]{1,0:T(8,128)(2,1)} %pad_maximum_fusion.x_ref, bf16[1184,1024]{1,0:T(8,128)(2,1)} %convolution_convert_fusion.a_ref, bf16[1184,1024]{1,0:T(8,128)(2,1)} %collective-permute-done.14.b_ref, f32[6,1,1024]{2,1,0:T(1,128)} %get-tuple-element.101.gain_ref.shift_ref.bias_ref, ...), custom_call_target="tpu_custom_call" | custom-call | flops 24248320 | bytes 14548992 | tf_op jit(solution)/shard_map/middle/pallas_call | solution.py:201
  157.0 11.3 %collective-permute-done.18.refs_2_ = bf16[1024,512]{1,0:T(8,128)(2,1)} collective-permute-done((bf16[1024,512]{1,0:T(8,128)(2,1)}, bf16[1024,512]{1,0:T(8,128)(2,1)}, u32[]{:S(2)}, u32[]{:S(2)}) %collective-permute-start.18) | collective-permute-done | bytes 1048608 | tf_op jit(solution)/shard_map/ppermute | solution.py:620
  168.3 21.6 %collective-permute-done.19.refs_3_ = bf16[1024,512]{1,0:T(8,128)(2,1)} collective-permute-done((bf16[1024,512]{1,0:T(8,128)(2,1)}, bf16[1024,512]{1,0:T(8,128)(2,1)}, u32[]{:S(2)}, u32[]{:S(2)}) %collective-permute-start.19) | collective-permute-done | bytes 1048608 | tf_op jit(solution)/shard_map/ppermute | solution.py:620
  189.9 20.6 %mlp_first.1 = (bf16[1184,1024]{1,0:T(8,128)(2,1)}, bf16[1184,1024]{1,0:T(8,128)(2,1)}, f32[1,1024]{1,0:T(1,128)}, bf16[1184,1024]{1,0:T(8,128)(2,1)}, bf16[1184,1024]{1,0:T(8,128)(2,1)}) custom-call(s32[3]{0:T(128)} %pad_add_fusion.place_ref, bf16[1184,1024]{1,0:T(8,128)(2,1)} %get-tuple-element.117.n_ref, bf16[1184,1024]{1,0:T(8,128)(2,1)} %pad_maximum_fusion.1.dy_ref, ...), custom_call_target="tpu_custom_call" | custom-call | flops 9932111872 | bytes 24248320 | tf_op jit(solution)/shard_map/mlp_first/pallas_call | solution.py:296
  210.5 4.7 convolution_convert_fusion.6
  215.2 4.3 convolution_convert_fusion.2
  219.5 22.4 %mlp_second.1 = (bf16[1184,1024]{1,0:T(8,128)(2,1)}, bf16[1184,1024]{1,0:T(8,128)(2,1)}, f32[1,1024]{1,0:T(1,128)}, f32[1184,512]{1,0:T(8,128)}, bf16[1184,512]{1,0:T(8,128)(2,1)}, /*index=5*/bf16[1184,1024]{1,0:T(8,128)(2,1)}) custom-call(s32[3]{0:T(128)} %pad_add_fusion.place_ref, bf16[1184,1024]{1,0:T(8,128)(2,1)} %get-tuple-element.117.n_ref, ...), custom_call_target="tpu_custom_call" | custom-call | flops 9932111872 | bytes 24248320 | tf_op jit(solution)/shard_map/mlp_second/pallas_call | solution.py:296
  242.6 4.7 convolution_convert_fusion.5
  247.3 2.5 convolution_convert_fusion.4
  254.8 14.2 %turn.1 = (f32[1184,1024]{1,0:T(8,128)}, bf16[1184,1024]{1,0:T(8,128)(2,1)}, bf16[1184,512]{1,0:T(8,128)(2,1)}, f32[4,1024]{1,0:T(4,128)}, bf16[1184,256]{1,0:T(8,128)(2,1)}, /*index=5*/bf16[1184,256]{1,0:T(8,128)(2,1)}) custom-call(s32[3]{0:T(128)} %pad_add_fusion.place_ref, f32[1184,1024]{1,0:T(8,128)} %get-tuple-element.111.h_ref, ...), custom_call_target="tpu_custom_call" | custom-call | flops 1241513984 | bytes 24248320 | tf_op jit(solution)/shard_map/turn/pallas_call | solution.py:360
  269.0 3.8 convolution_convert_fusion.3
  272.9 3.3 collective-permute-done.27
  276.2 21.5 %collective-permute-done.25 = bf16[1024,512]{1,0:T(8,128)(2,1)} collective-permute-done((bf16[1024,512]{1,0:T(8,128)(2,1)}, bf16[1024,512]{1,0:T(8,128)(2,1)}, u32[]{:S(2)}, u32[]{:S(2)}) %collective-permute-start.25) | collective-permute-done | bytes 1048608 | tf_op jit(solution)/shard_map/ppermute | solution.py:620
  298.3 2.8 add_convert_fusion.refs_2_
  303.6 2.8 add_convert_fusion.1.refs_0_
  308.8 2.8 add_convert_fusion.2.refs_4_
  317.2 21.9 %collective-permute-done.30 = bf16[256,512]{1,0:T(8,128)(2,1)S(1)} collective-permute-done((bf16[256,512]{1,0:T(8,128)(2,1)S(1)}, bf16[256,512]{1,0:T(8,128)(2,1)S(1)}, u32[]{:S(2)}, u32[]{:S(2)}) %collective-permute-start.30) | collective-permute-done | bytes 262176 | tf_op jit(solution)/shard_map/ppermute | solution.py:620
  339.2 26.6 %attend_back.1 = (bf16[1184,1536]{1,0:T(8,128)(2,1)}, f32[1,1536]{1,0:T(1,128)}) custom-call(bf16[1184,1536]{1,0:T(8,128)(2,1)} %get-tuple-element.105.qkv_ref, bf16[2,8,592,592]{3,2,1,0:T(8,128)(2,1)} %get-tuple-element.133.p_ref, bf16[1184,512]{1,0:T(8,128)(2,1)} %get-tuple-element.140.g_ref), custom_call_target="tpu_custom_call" | custom-call | flops 21532508160 | bytes 60620800 | tf_op jit(solution)/shard_map/attend_back/pallas_call | solution.py:176
  367.4 4.3 join.1
  371.7 2.7 convolution_convert_fusion.8
  374.5 2.8 convolution_convert_fusion.7
  377.5 5.3 %convolution_convert_fusion.1.a_ref = bf16[1184,1024]{1,0:T(8,128)(2,1)} fusion(bf16[1184,1536]{1,0:T(8,128)(2,1)S(1)} %copy-done.39, bf16[1024,2048]{1,0:T(8,128)(2,1)S(1)} %copy-done.2), kind=kOutput, calls=%fused_computation.1 | convolution fusion | flops 3725754368 | bytes 9207808 | tf_op jit(solution)/shard_map/dot_general | solution.py:30
  386.8 5.1 %collective-permute-done.36 = bf16[1024,128]{1,0:T(8,128)(2,1)S(1)} collective-permute-done((bf16[1024,128]{1,0:T(8,128)(2,1)S(1)}, bf16[1024,128]{1,0:T(8,128)(2,1)S(1)}, u32[]{:S(2)}, u32[]{:S(2)}) %collective-permute-start.36) | collective-permute-done | bytes 262176 | tf_op jit(solution)/shard_map/ppermute | solution.py:620
  391.9 4.4 add_convert_fusion.5
  397.1 2.0 collective-permute-done.35
  399.1 2.4 add_convert_fusion.4
  402.0 2.7 collective-permute-done.50
  404.8 2.4 fusion.8
  407.2 1.9 copy.48
  409.1 8.9 %last.1 = (f32[1184,256]{1,0:T(8,128)}, bf16[1184,256]{1,0:T(8,128)(2,1)}, f32[2,256]{1,0:T(2,128)}, f32[2,256]{1,0:T(2,128)}) custom-call(s32[3]{0:T(128)} %pad_add_fusion.place_ref, bf16[1184,1024]{1,0:T(8,128)(2,1)} %pad_maximum_fusion.x_ref, f32[1184,1024]{1,0:T(8,128)} %get-tuple-element.152.dh_ref, bf16[1184,1024]{1,0:T(8,128)(2,1)} %convolution_convert_fusion.1.a_ref, ...), custom_call_target="tpu_custom_call" | custom-call | flops 24248320 | bytes 14548992 | tf_op jit(solution)/shard_map/last/pallas_call | solution.py:420
  419.4 2.0 collective-permute-done.38
  424.5 2.2 collective-permute-done.45
  426.7 6.2 %collective-permute-start.46 = (f32[12,256]{1,0:T(8,128)S(1)}, f32[12,256]{1,0:T(8,128)S(1)}, u32[]{:S(2)}, u32[]{:S(2)}) collective-permute-start(f32[12,256]{1,0:T(8,128)S(1)} %add.179), channel_id=1, source_target_pairs={{0,4},{4,0},{8,12},{12,8},{1,5},{5,1},{9,13},{13,9},{2,6},{6,2},{1... | collective-permute-start | bytes 36872 | tf_op jit(solution)/shard_map/ppermute | solution.py:620
  434.7 3.0 collective-permute-start.43
  441.8 10.4 %collective-permute-done.47 = f32[12,256]{1,0:T(8,128)S(1)} collective-permute-done((f32[12,256]{1,0:T(8,128)S(1)}, f32[12,256]{1,0:T(8,128)S(1)}, u32[]{:S(2)}, u32[]{:S(2)}) %collective-permute-start.47) | collective-permute-done | bytes 12320 | tf_op jit(solution)/shard_map/ppermute | solution.py:620
  467.0 7.0 %collective-permute-done.49 = bf16[256,896]{1,0:T(8,128)(2,1)} collective-permute-done((bf16[256,896]{1,0:T(8,128)(2,1)}, bf16[256,896]{1,0:T(8,128)(2,1)}, u32[]{:S(2)}, u32[]{:S(2)}) %collective-permute-start.49) | collective-permute-done | bytes 458784 | tf_op jit(solution)/shard_map/ppermute | solution.py:620
  (271 shorter events, 94.0 us)
Async XLA Ops:
  7.2 111.7 %all-gather.3.cloned.1.call-start = ((), (), s32[]{:S(2)}) async-start(), calls=%async_computation.2 | async-start | bytes 1310720 | tf_op jit(solution)/shard_map/all_gather | solution.py:711
  11.2 12.5 %collective-permute-start.1 = (bf16[256,512]{1,0:T(8,128)(2,1)S(1)}, bf16[256,512]{1,0:T(8,128)(2,1)}, u32[]{:S(2)}, u32[]{:S(2)}) collective-permute-start(bf16[256,512]{1,0:T(8,128)(2,1)S(1)} %pad_maximum_fusion.8), channel_id=1, source_target_pairs={{0,4},{4,8},{8,12},{12,0},{1,5},{5,9},{9,13},{13,1},{2,6},{6,10},{... | collective-permute-start | bytes 786440 | tf_op jit(solution)/shard_map/ppermute | solution.py:623
  14.3 19.7 %collective-permute-start.2 = (bf16[256,512]{1,0:T(8,128)(2,1)S(1)}, bf16[256,512]{1,0:T(8,128)(2,1)S(1)}, u32[]{:S(2)}, u32[]{:S(2)}) collective-permute-start(bf16[256,512]{1,0:T(8,128)(2,1)S(1)} %pad_maximum_fusion.8), channel_id=1, source_target_pairs={{0,8},{4,12},{8,0},{12,4},{1,9},{5,13},{9,1},{13,5},{2,10},{6,14},... | collective-permute-start | bytes 786440 | tf_op jit(solution)/shard_map/ppermute | solution.py:623
  16.9 17.1 %collective-permute-start.3 = (bf16[256,512]{1,0:T(8,128)(2,1)S(1)}, bf16[256,512]{1,0:T(8,128)(2,1)S(1)}, u32[]{:S(2)}, u32[]{:S(2)}) collective-permute-start(bf16[256,512]{1,0:T(8,128)(2,1)S(1)} %pad_maximum_fusion.8), channel_id=1, source_target_pairs={{0,12},{4,0},{8,4},{12,8},{1,13},{5,1},{9,5},{13,9},{2,14},{6,2},{... | collective-permute-start | bytes 786440 | tf_op jit(solution)/shard_map/ppermute | solution.py:623
  18.3 16.9 %collective-permute-start = (bf16[1154,256]{1,0:T(8,128)(2,1)S(1)}, bf16[1154,256]{1,0:T(8,128)(2,1)S(1)}, u32[]{:S(2)}, u32[]{:S(2)}) collective-permute-start(bf16[1154,256]{1,0:T(8,128)(2,1)S(1)} %get-tuple-element.226), channel_id=1, source_target_pairs={{0,2},{2,0},{1,3},{3,1},{4,6},{6,4},{5,7},{7,5},{8,10},{10,8},{9,1... | collective-permute-start | bytes 1772552 | tf_op jit(solution)/shard_map/ppermute | solution.py:620
  36.5 12.7 %collective-permute-start.4 = (bf16[1184,512]{1,0:T(8,128)(2,1)S(1)}, bf16[1184,512]{1,0:T(8,128)(2,1)S(1)}, u32[]{:S(2)}, u32[]{:S(2)}) collective-permute-start(bf16[1184,512]{1,0:T(8,128)(2,1)S(1)} %bitcast.54), channel_id=1, source_target_pairs={{0,1},{1,0},{2,3},{3,2},{4,5},{5,4},{6,7},{7,6},{8,9},{9,8},{10,11... | collective-permute-start | bytes 3637256 | tf_op jit(solution)/shard_map/ppermute | solution.py:620
  43.6 15.1 %collective-permute-start.11 = (bf16[1024,256]{1,0:T(8,128)(2,1)}, bf16[1024,256]{1,0:T(8,128)(2,1)}, u32[]{:S(2)}, u32[]{:S(2)}) collective-permute-start(bf16[1024,256]{1,0:T(8,128)(2,1)} %copy-done.24), channel_id=1, source_target_pairs={{0,16},{16,0},{1,17},{17,1},{2,18},{18,2},{3,19},{19,3},{4,20},{20... | collective-permute-start | bytes 1572872 | tf_op jit(solution)/shard_map/ppermute | solution.py:620
  45.1 15.1 %collective-permute-start.8 = (bf16[1024,256]{1,0:T(8,128)(2,1)}, bf16[1024,256]{1,0:T(8,128)(2,1)}, u32[]{:S(2)}, u32[]{:S(2)}) collective-permute-start(bf16[1024,256]{1,0:T(8,128)(2,1)} %copy-done.25), channel_id=1, source_target_pairs={{0,2},{2,0},{1,3},{3,1},{4,6},{6,4},{5,7},{7,5},{8,10},{10,8},{9,1... | collective-permute-start | bytes 1572872 | tf_op jit(solution)/shard_map/ppermute | solution.py:620
  45.6 73.8 %all-gather.5.cloned.1.call-start = ((), (), s32[]{:S(2)}) async-start(), calls=%async_computation.3 | async-start | bytes 1310720 | tf_op jit(solution)/shard_map/all_gather | solution.py:711
  45.7 24.2 %collective-permute-start.10 = (bf16[1024,256]{1,0:T(8,128)(2,1)}, bf16[1024,256]{1,0:T(8,128)(2,1)}, u32[]{:S(2)}, u32[]{:S(2)}) collective-permute-start(bf16[1024,256]{1,0:T(8,128)(2,1)} %copy-done.25), channel_id=1, source_target_pairs={{0,16},{16,0},{1,17},{17,1},{2,18},{18,2},{3,19},{19,3},{4,20},{20... | collective-permute-start | bytes 1572872 | tf_op jit(solution)/shard_map/ppermute | solution.py:620
  46.3 25.1 %collective-permute-start.9 = (bf16[1024,256]{1,0:T(8,128)(2,1)}, bf16[1024,256]{1,0:T(8,128)(2,1)}, u32[]{:S(2)}, u32[]{:S(2)}) collective-permute-start(bf16[1024,256]{1,0:T(8,128)(2,1)} %copy-done.24), channel_id=1, source_target_pairs={{0,2},{2,0},{1,3},{3,1},{4,6},{6,4},{5,7},{7,5},{8,10},{10,8},{9,1... | collective-permute-start | bytes 1572872 | tf_op jit(solution)/shard_map/ppermute | solution.py:620
  58.7 23.9 %collective-permute-start.13 = (bf16[1024,256]{1,0:T(8,128)(2,1)}, bf16[1024,256]{1,0:T(8,128)(2,1)S(1)}, u32[]{:S(2)}, u32[]{:S(2)}) collective-permute-start(bf16[1024,256]{1,0:T(8,128)(2,1)} %collective-permute-done.11.refs_5_), channel_id=1, source_target_pairs={{0,2},{2,0},{1,3},{3,1},{4,6},{6,4},{5,7},{7,5},{8,10},{10,8},{9,1... | collective-permute-start | bytes 1572872 | tf_op jit(solution)/shard_map/ppermute | solution.py:620
  60.2 22.4 %collective-permute-start.12 = (bf16[1024,256]{1,0:T(8,128)(2,1)}, bf16[1024,256]{1,0:T(8,128)(2,1)S(1)}, u32[]{:S(2)}, u32[]{:S(2)}) collective-permute-start(bf16[1024,256]{1,0:T(8,128)(2,1)} %collective-permute-done.8.refs_2_), channel_id=1, source_target_pairs={{0,16},{16,0},{1,17},{17,1},{2,18},{18,2},{3,19},{19,3},{4,20},{20... | collective-permute-start | bytes 1572872 | tf_op jit(solution)/shard_map/ppermute | solution.py:620
  61.1 251.6 %reduce-scatter.3.cloned.1.call-start = ((), (), s32[]{:S(2)}) async-start(), calls=%async_computation.4 | async-start | bytes 2621440 | tf_op jit(solution)/shard_map/reduce_scatter | solution.py:753
  61.3 57.1 %collective-permute-start.15 = (bf16[1154,256]{1,0:T(8,128)(2,1)S(1)}, bf16[1154,256]{1,0:T(8,128)(2,1)S(1)}, u32[]{:S(2)}, u32[]{:S(2)}) collective-permute-start(bf16[1154,256]{1,0:T(8,128)(2,1)S(1)} %get-tuple-element.108), channel_id=1, source_target_pairs={{0,2},{2,0},{1,3},{3,1},{4,6},{6,4},{5,7},{7,5},{8,10},{10,8},{9,1... | collective-permute-start | bytes 1772552 | tf_op jit(solution)/shard_map/ppermute | solution.py:620
  118.8 27.5 %collective-permute-start.16 = (bf16[1184,512]{1,0:T(8,128)(2,1)S(1)}, bf16[1184,512]{1,0:T(8,128)(2,1)S(1)}, u32[]{:S(2)}, u32[]{:S(2)}) collective-permute-start(bf16[1184,512]{1,0:T(8,128)(2,1)S(1)} %bitcast.55), channel_id=1, source_target_pairs={{0,1},{1,0},{2,3},{3,2},{4,5},{5,4},{6,7},{7,6},{8,9},{9,8},{10,11... | collective-permute-start | bytes 3637256 | tf_op jit(solution)/shard_map/ppermute | solution.py:620
  118.9 25.9 %collective-permute-start.17 = (bf16[1024,512]{1,0:T(8,128)(2,1)}, bf16[1024,512]{1,0:T(8,128)(2,1)}, u32[]{:S(2)}, u32[]{:S(2)}) collective-permute-start(bf16[1024,512]{1,0:T(8,128)(2,1)} %all-gather.3.cloned.1.call-done.refs_0_), channel_id=1, source_target_pairs={{0,2},{2,0},{1,3},{3,1},{4,6},{6,4},{5,7},{7,5},{8,10},{10,8},{9,1... | collective-permute-start | bytes 3145736 | tf_op jit(solution)/shard_map/ppermute | solution.py:620
  119.5 26.3 %collective-permute-start.20 = (bf16[1024,512]{1,0:T(8,128)(2,1)}, bf16[1024,512]{1,0:T(8,128)(2,1)}, u32[]{:S(2)}, u32[]{:S(2)}) collective-permute-start(bf16[1024,512]{1,0:T(8,128)(2,1)} %all-gather.5.cloned.1.call-done.refs_0_), channel_id=1, source_target_pairs={{0,16},{16,0},{1,17},{17,1},{2,18},{18,2},{3,19},{19,3},{4,20},{20... | collective-permute-start | bytes 3145736 | tf_op jit(solution)/shard_map/ppermute | solution.py:620
  120.0 30.2 %collective-permute-start.14 = (bf16[1184,1024]{1,0:T(8,128)(2,1)}, bf16[1184,1024]{1,0:T(8,128)(2,1)}, u32[]{:S(2)}, u32[]{:S(2)}) collective-permute-start(bf16[1184,1024]{1,0:T(8,128)(2,1)} %convolution_convert_fusion.a_ref), channel_id=1, source_target_pairs={{0,1},{1,0},{2,3},{3,2},{4,5},{5,4},{6,7},{7,6},{8,9},{9,8},{10,11... | collective-permute-start | bytes 7274504 | tf_op jit(solution)/shard_map/ppermute | solution.py:620
  120.0 48.3 %collective-permute-start.18 = (bf16[1024,512]{1,0:T(8,128)(2,1)}, bf16[1024,512]{1,0:T(8,128)(2,1)}, u32[]{:S(2)}, u32[]{:S(2)}) collective-permute-start(bf16[1024,512]{1,0:T(8,128)(2,1)} %all-gather.3.cloned.1.call-done.refs_0_), channel_id=1, source_target_pairs={{0,16},{16,0},{1,17},{17,1},{2,18},{18,2},{3,19},{19,3},{4,20},{20... | collective-permute-start | bytes 3145736 | tf_op jit(solution)/shard_map/ppermute | solution.py:620
  144.7 74.7 %collective-permute-start.21 = (bf16[1024,512]{1,0:T(8,128)(2,1)}, bf16[1024,512]{1,0:T(8,128)(2,1)}, u32[]{:S(2)}, u32[]{:S(2)}) collective-permute-start(bf16[1024,512]{1,0:T(8,128)(2,1)} %all-gather.5.cloned.1.call-done.refs_0_), channel_id=1, source_target_pairs={{0,2},{2,0},{1,3},{3,1},{4,6},{6,4},{5,7},{7,5},{8,10},{10,8},{9,1... | collective-permute-start | bytes 3145736 | tf_op jit(solution)/shard_map/ppermute | solution.py:620
  145.8 44.1 %collective-permute-start.19 = (bf16[1024,512]{1,0:T(8,128)(2,1)}, bf16[1024,512]{1,0:T(8,128)(2,1)}, u32[]{:S(2)}, u32[]{:S(2)}) collective-permute-start(bf16[1024,512]{1,0:T(8,128)(2,1)} %collective-permute-done.17.refs_1_), channel_id=1, source_target_pairs={{0,16},{16,0},{1,17},{17,1},{2,18},{18,2},{3,19},{19,3},{4,20},{20... | collective-permute-start | bytes 3145736 | tf_op jit(solution)/shard_map/ppermute | solution.py:620
  146.3 73.2 %collective-permute-start.22 = (bf16[1024,512]{1,0:T(8,128)(2,1)}, bf16[1024,512]{1,0:T(8,128)(2,1)}, u32[]{:S(2)}, u32[]{:S(2)}) collective-permute-start(bf16[1024,512]{1,0:T(8,128)(2,1)} %collective-permute-done.20.refs_1_), channel_id=1, source_target_pairs={{0,2},{2,0},{1,3},{3,1},{4,6},{6,4},{5,7},{7,5},{8,10},{10,8},{9,1... | collective-permute-start | bytes 3145736 | tf_op jit(solution)/shard_map/ppermute | solution.py:620
  241.9 11.5 %collective-permute-start.23 = (bf16[1184,1024]{1,0:T(8,128)(2,1)}, bf16[1184,1024]{1,0:T(8,128)(2,1)S(1)}, u32[]{:S(2)}, u32[]{:S(2)}) collective-permute-start(bf16[1184,1024]{1,0:T(8,128)(2,1)} %get-tuple-element.121.a_ref), channel_id=1, source_target_pairs={{0,1},{1,0},{2,3},{3,2},{4,5},{5,4},{6,7},{7,6},{8,9},{9,8},{10,11... | collective-permute-start | bytes 7274504 | tf_op jit(solution)/shard_map/ppermute | solution.py:620
  242.0 221.6 %reduce-scatter.5.cloned.1.call-start = ((), (), s32[]{:S(2)}) async-start(), calls=%async_computation.5 | async-start | bytes 2293760 | tf_op jit(solution)/shard_map/reduce_scatter | solution.py:773
  242.1 11.4 %collective-permute-start.24 = (bf16[1184,512]{1,0:T(8,128)(2,1)}, bf16[1184,512]{1,0:T(8,128)(2,1)}, u32[]{:S(2)}, u32[]{:S(2)}) collective-permute-start(bf16[1184,512]{1,0:T(8,128)(2,1)} %get-tuple-element.126), channel_id=1, source_target_pairs={{0,1},{1,0},{2,3},{3,2},{4,5},{5,4},{6,7},{7,6},{8,9},{9,8},{10,11... | collective-permute-start | bytes 3637256 | tf_op jit(solution)/shard_map/ppermute | solution.py:620
  249.9 26.3 %collective-permute-start.27 = (bf16[1024,512]{1,0:T(8,128)(2,1)}, bf16[1024,512]{1,0:T(8,128)(2,1)}, u32[]{:S(2)}, u32[]{:S(2)}) collective-permute-start(bf16[1024,512]{1,0:T(8,128)(2,1)} %convolution_convert_fusion.4), channel_id=1, source_target_pairs={{0,16},{16,0},{1,17},{17,1},{2,18},{18,2},{3,19},{19,3},{4,20},{20... | collective-permute-start | bytes 3145736 | tf_op jit(solution)/shard_map/ppermute | solution.py:620
  250.4 25.9 %collective-permute-start.26 = (bf16[1024,512]{1,0:T(8,128)(2,1)}, bf16[1024,512]{1,0:T(8,128)(2,1)}, u32[]{:S(2)}, u32[]{:S(2)}) collective-permute-start(bf16[1024,512]{1,0:T(8,128)(2,1)} %convolution_convert_fusion.5), channel_id=1, source_target_pairs={{0,2},{2,0},{1,3},{3,1},{4,6},{6,4},{5,7},{7,5},{8,10},{10,8},{9,1... | collective-permute-start | bytes 3145736 | tf_op jit(solution)/shard_map/ppermute | solution.py:620
  251.9 45.9 %collective-permute-start.25 = (bf16[1024,512]{1,0:T(8,128)(2,1)}, bf16[1024,512]{1,0:T(8,128)(2,1)}, u32[]{:S(2)}, u32[]{:S(2)}) collective-permute-start(bf16[1024,512]{1,0:T(8,128)(2,1)} %convolution_convert_fusion.6), channel_id=1, source_target_pairs={{0,16},{16,0},{1,17},{17,1},{2,18},{18,2},{3,19},{19,3},{4,20},{20... | collective-permute-start | bytes 3145736 | tf_op jit(solution)/shard_map/ppermute | solution.py:620
  297.8 14.9 %collective-permute-start.29 = (bf16[1024,256]{1,0:T(8,128)(2,1)S(1)}, bf16[1024,256]{1,0:T(8,128)(2,1)}, u32[]{:S(2)}, u32[]{:S(2)}) collective-permute-start(bf16[1024,256]{1,0:T(8,128)(2,1)S(1)} %slice.255), channel_id=1, source_target_pairs={{0,16},{16,0},{1,17},{17,1},{2,18},{18,2},{3,19},{19,3},{4,20},{20... | collective-permute-start | bytes 1572872 | tf_op jit(solution)/shard_map/ppermute | solution.py:620
  302.0 63.9 %collective-permute-start.32 = (bf16[1024,256]{1,0:T(8,128)(2,1)}, bf16[1024,256]{1,0:T(8,128)(2,1)}, u32[]{:S(2)}, u32[]{:S(2)}) collective-permute-start(bf16[1024,256]{1,0:T(8,128)(2,1)} %slice.258), channel_id=1, source_target_pairs={{0,16},{16,0},{1,17},{17,1},{2,18},{18,2},{3,19},{19,3},{4,20},{20... | collective-permute-start | bytes 1572872 | tf_op jit(solution)/shard_map/ppermute | solution.py:620
  307.3 58.6 %collective-permute-start.31 = (bf16[1024,256]{1,0:T(8,128)(2,1)}, bf16[1024,256]{1,0:T(8,128)(2,1)}, u32[]{:S(2)}, u32[]{:S(2)}) collective-permute-start(bf16[1024,256]{1,0:T(8,128)(2,1)} %slice.257), channel_id=1, source_target_pairs={{0,2},{2,0},{1,3},{3,1},{4,6},{6,4},{5,7},{7,5},{8,10},{10,8},{9,1... | collective-permute-start | bytes 1572872 | tf_op jit(solution)/shard_map/ppermute | solution.py:620
  311.7 54.2 %collective-permute-start.33 = (bf16[1024,256]{1,0:T(8,128)(2,1)S(1)}, bf16[1024,256]{1,0:T(8,128)(2,1)S(1)}, u32[]{:S(2)}, u32[]{:S(2)}) collective-permute-start(bf16[1024,256]{1,0:T(8,128)(2,1)S(1)} %slice.259), channel_id=1, source_target_pairs={{0,2},{2,0},{1,3},{3,1},{4,6},{6,4},{5,7},{7,5},{8,10},{10,8},{9,1... | collective-permute-start | bytes 1572872 | tf_op jit(solution)/shard_map/ppermute | solution.py:620
  313.7 25.4 %collective-permute-start.30 = (bf16[256,512]{1,0:T(8,128)(2,1)S(1)}, bf16[256,512]{1,0:T(8,128)(2,1)S(1)}, u32[]{:S(2)}, u32[]{:S(2)}) collective-permute-start(bf16[256,512]{1,0:T(8,128)(2,1)S(1)} %slice.215), channel_id=1, source_target_pairs={{0,2},{2,0},{1,3},{3,1},{4,6},{6,4},{5,7},{7,5},{8,10},{10,8},{9,1... | collective-permute-start | bytes 786440 | tf_op jit(solution)/shard_map/ppermute | solution.py:620
  316.7 49.2 %collective-permute-start.34 = (bf16[1024,128]{1,0:T(8,128)(2,1)S(1)}, bf16[1024,128]{1,0:T(8,128)(2,1)S(1)}, u32[]{:S(2)}, u32[]{:S(2)}) collective-permute-start(bf16[1024,128]{1,0:T(8,128)(2,1)S(1)} %slice.260), channel_id=1, source_target_pairs={{0,2},{2,0},{1,3},{3,1},{4,6},{6,4},{5,7},{7,5},{8,10},{10,8},{9,1... | collective-permute-start | bytes 786440 | tf_op jit(solution)/shard_map/ppermute | solution.py:620
  382.7 26.3 %collective-permute-start.39 = (bf16[1184,1024]{1,0:T(8,128)(2,1)}, bf16[1184,1024]{1,0:T(8,128)(2,1)}, u32[]{:S(2)}, u32[]{:S(2)}) collective-permute-start(bf16[1184,1024]{1,0:T(8,128)(2,1)} %convolution_convert_fusion.1.a_ref), channel_id=1, source_target_pairs={{0,1},{1,0},{2,3},{3,2},{4,5},{5,4},{6,7},{7,6},{8,9},{9,8},{10,11... | collective-permute-start | bytes 7274504 | tf_op jit(solution)/shard_map/ppermute | solution.py:620
  384.3 14.8 %collective-permute-start.35 = (bf16[1024,256]{1,0:T(8,128)(2,1)S(1)}, bf16[1024,256]{1,0:T(8,128)(2,1)S(1)}, u32[]{:S(2)}, u32[]{:S(2)}) collective-permute-start(bf16[1024,256]{1,0:T(8,128)(2,1)S(1)} %convolution_convert_fusion.7), channel_id=1, source_target_pairs={{0,16},{16,0},{1,17},{17,1},{2,18},{18,2},{3,19},{19,3},{4,20},{20... | collective-permute-start | bytes 1572872 | tf_op jit(solution)/shard_map/ppermute | solution.py:620
  385.0 52.8 %collective-permute-start.28 = (bf16[1184,256]{1,0:T(8,128)(2,1)}, bf16[1184,256]{1,0:T(8,128)(2,1)}, u32[]{:S(2)}, u32[]{:S(2)}) collective-permute-start(bf16[1184,256]{1,0:T(8,128)(2,1)} %get-tuple-element.131), channel_id=1, source_target_pairs={{0,2},{2,0},{1,3},{3,1},{4,6},{6,4},{5,7},{7,5},{8,10},{10,8},{9,1... | collective-permute-start | bytes 1818632 | tf_op jit(solution)/shard_map/ppermute | solution.py:620
  385.6 19.1 %collective-permute-start.50 = (bf16[256,512]{1,0:T(8,128)(2,1)S(1)}, bf16[256,512]{1,0:T(8,128)(2,1)S(1)}, u32[]{:S(2)}, u32[]{:S(2)}) collective-permute-start(bf16[256,512]{1,0:T(8,128)(2,1)S(1)} %add_convert_fusion.7), channel_id=1, source_target_pairs={{0,16},{16,0},{1,17},{17,1},{2,18},{18,2},{3,19},{19,3},{4,20},{20... | collective-permute-start | bytes 786440 | tf_op jit(solution)/shard_map/ppermute | solution.py:620
  396.3 25.1 %collective-permute-start.37 = (bf16[1024,384]{1,0:T(8,128)(2,1)}, bf16[1024,384]{1,0:T(8,128)(2,1)S(1)}, u32[]{:S(2)}, u32[]{:S(2)}) collective-permute-start(bf16[1024,384]{1,0:T(8,128)(2,1)} %add_convert_fusion.5), channel_id=1, source_target_pairs={{0,16},{16,0},{1,17},{17,1},{2,18},{18,2},{3,19},{19,3},{4,20},{20... | collective-permute-start | bytes 2359304 | tf_op jit(solution)/shard_map/ppermute | solution.py:620
  401.5 19.9 %collective-permute-start.38 = (bf16[1024,384]{1,0:T(8,128)(2,1)}, bf16[1024,384]{1,0:T(8,128)(2,1)}, u32[]{:S(2)}, u32[]{:S(2)}) collective-permute-start(bf16[1024,384]{1,0:T(8,128)(2,1)} %add_convert_fusion.4), channel_id=1, source_target_pairs={{0,2},{2,0},{1,3},{3,1},{4,6},{6,4},{5,7},{7,5},{8,10},{10,8},{9,1... | collective-permute-start | bytes 2359304 | tf_op jit(solution)/shard_map/ppermute | solution.py:620
  426.7 12.5 %collective-permute-start.46 = (f32[12,256]{1,0:T(8,128)S(1)}, f32[12,256]{1,0:T(8,128)S(1)}, u32[]{:S(2)}, u32[]{:S(2)}) collective-permute-start(f32[12,256]{1,0:T(8,128)S(1)} %add.179), channel_id=1, source_target_pairs={{0,4},{4,0},{8,12},{12,8},{1,5},{5,1},{9,13},{13,9},{2,6},{6,2},{1... | collective-permute-start | bytes 36872 | tf_op jit(solution)/shard_map/ppermute | solution.py:620
  432.9 20.2 %collective-permute-start.41 = (bf16[256,384]{1,0:T(8,128)(2,1)S(1)}, bf16[256,384]{1,0:T(8,128)(2,1)S(1)}, u32[]{:S(2)}, u32[]{:S(2)}) collective-permute-start(bf16[256,384]{1,0:T(8,128)(2,1)S(1)} %get-tuple-element.233), channel_id=1, source_target_pairs={{0,4},{4,8},{8,12},{12,0},{1,5},{5,9},{9,13},{13,1},{2,6},{6,10},{... | collective-permute-start | bytes 589832 | tf_op jit(solution)/shard_map/ppermute | solution.py:623
  433.0 20.1 %collective-permute-start.42 = (bf16[256,384]{1,0:T(8,128)(2,1)S(1)}, bf16[256,384]{1,0:T(8,128)(2,1)S(1)}, u32[]{:S(2)}, u32[]{:S(2)}) collective-permute-start(bf16[256,384]{1,0:T(8,128)(2,1)S(1)} %get-tuple-element.235), channel_id=1, source_target_pairs={{0,8},{4,12},{8,0},{12,4},{1,9},{5,13},{9,1},{13,5},{2,10},{6,14},... | collective-permute-start | bytes 589832 | tf_op jit(solution)/shard_map/ppermute | solution.py:623
  434.7 18.4 %collective-permute-start.43 = (bf16[256,384]{1,0:T(8,128)(2,1)S(1)}, bf16[256,384]{1,0:T(8,128)(2,1)S(1)}, u32[]{:S(2)}, u32[]{:S(2)}) collective-permute-start(bf16[256,384]{1,0:T(8,128)(2,1)S(1)} %get-tuple-element.234), channel_id=1, source_target_pairs={{0,12},{4,0},{8,4},{12,8},{1,13},{5,1},{9,5},{13,9},{2,14},{6,2},{... | collective-permute-start | bytes 589832 | tf_op jit(solution)/shard_map/ppermute | solution.py:623
  437.8 23.4 %collective-permute-start.40 = (bf16[1184,256]{1,0:T(8,128)(2,1)}, bf16[1184,256]{1,0:T(8,128)(2,1)S(1)}, u32[]{:S(2)}, u32[]{:S(2)}) collective-permute-start(bf16[1184,256]{1,0:T(8,128)(2,1)} %get-tuple-element.161), channel_id=1, source_target_pairs={{0,2},{2,0},{1,3},{3,1},{4,6},{6,4},{5,7},{7,5},{8,10},{10,8},{9,1... | collective-permute-start | bytes 1818632 | tf_op jit(solution)/shard_map/ppermute | solution.py:620
  439.2 13.0 %collective-permute-start.47 = (f32[12,256]{1,0:T(8,128)S(1)}, f32[12,256]{1,0:T(8,128)S(1)}, u32[]{:S(2)}, u32[]{:S(2)}) collective-permute-start(f32[12,256]{1,0:T(8,128)S(1)} %add.180), channel_id=1, source_target_pairs={{0,8},{4,12},{8,0},{12,4},{1,9},{5,13},{9,1},{13,5},{2,10},{6,14},... | collective-permute-start | bytes 36872 | tf_op jit(solution)/shard_map/ppermute | solution.py:620
  463.6 10.4 %collective-permute-start.49 = (bf16[256,896]{1,0:T(8,128)(2,1)}, bf16[256,896]{1,0:T(8,128)(2,1)}, u32[]{:S(2)}, u32[]{:S(2)}) collective-permute-start(bf16[256,896]{1,0:T(8,128)(2,1)} %reduce-scatter.5.cloned.1.call-done), channel_id=1, source_target_pairs={{0,16},{16,0},{1,17},{17,1},{2,18},{18,2},{3,19},{19,3},{4,20},{20... | collective-permute-start | bytes 1376264 | tf_op jit(solution)/shard_map/ppermute | solution.py:620
  (54 other events, 649.1 us)
Sparse Core Ops, SparseCore 0:
  45.8 31.7 all-gather.2
  79.7 27.3 all-gather.4
  242.1 47.5 reduce-scatter.2
  386.9 43.6 reduce-scatter.4

commit v9 on v8

--- a/solution.py
+++ b/solution.py
@@ -84,18 +84,21 @@
         ref[...] += part
 
 
-def norm_qkv_kernel(x_ref, gain_ref, shift_ref, bias_ref, *refs):
-    blocks, (n_ref, o_ref, w_ref) = refs[:8], refs[8:]
-    one = blocks[1].shape[1] // 2
+def norm_qkv_kernel(place_ref, x_ref, gain_ref, shift_ref, bias_ref, *refs):
+    pieces, (n_ref, o_ref, w_ref) = refs[:-3], refs[-3:]
+    n_row = len(pieces) // 4
+    strip, wide = pieces[0].shape
+    one = wide // 4
 
     @pl.when(pl.program_id(0) == 0)
     def _():
-        for place in range(4):
-            first, second = blocks[2 * place], blocks[2 * place + 1]
-            start = 3 * one * place
-            w_ref[:, start : start + 2 * one] = first[...]
-            w_ref[:, start + 2 * one : start + 3 * one] = second[:, :one]
-            w_ref[:, (12 + place) * one : (13 + place) * one] = second[:, one:]
+        for shift in range(n_row):
+            start = lax.rem(place_ref[3] - shift + n_row, n_row) * strip
+            rows = pl.ds(pl.multiple_of(start, strip), strip)
+            for block in range(4):
+                piece = pieces[n_row * block + shift]
+                w_ref[rows, 3 * one * block : 3 * one * (block + 1)] = piece[:, : 3 * one]
+                w_ref[rows, (12 + block) * one : (13 + block) * one] = piece[:, 3 * one :]
 
     x = x_ref[...].astype(F32)
     middle, scaled = stats(x)
@@ -104,33 +107,45 @@
     o_ref[...] = (mm(n, w_ref[:, : 12 * one]) + bias_ref[...]).astype(BF16)
 
 
-def norm_qkv(x, gain, shift, bias, blocks):
+def norm_qkv(place, x, gain, shift, bias, pieces):
     rows = x.shape[0]
-    wide = blocks[0].shape[1]
-    out = 6 * wide
+    wide = pieces[0].shape[1]
+    out = 3 * wide
     return pl.pallas_call(
         norm_qkv_kernel,
-        grid=(rows // TM,),
         name="norm_qkv",
-        in_specs=[row_spec(D), gain[1], shift[1], fixed((1, out))] + [held_once((D, wide))] * 8,
-        out_specs=[row_spec(D), row_spec(out), held_once((D, 8 * wide))],
-        out_shape=[like((rows, D), BF16), like((rows, out), BF16), like((D, 8 * wide), BF16)],
+        grid_spec=pltpu.PrefetchScalarGridSpec(
+            num_scalar_prefetch=1,
+            grid=(rows // TM,),
+            in_specs=[row_spec(D), gain[1], shift[1], fixed((1, out))]
+            + [held_once(pieces[0].shape)] * len(pieces),
+            out_specs=[row_spec(D), row_spec(out), held_once((D, 4 * wide))],
+        ),
+        out_shape=[like((rows, D), BF16), like((rows, out), BF16), like((D, 4 * wide), BF16)],
         compiler_params=params(1),
         cost_estimate=cost(2 * rows * D * out, 16 * rows * D),
-    )(x, gain[0], shift[0], bias, *blocks)
+    )(place, x, gain[0], shift[0], bias, *pieces)
 
 
 def attend_kernel(qkv_ref, o_ref, p_ref):
     live = lax.broadcasted_iota(jnp.int32, (1, PAD), 1) < SEQ
     step = 2 * HD
-    for h in range(2):
-        q, k, v = (qkv_ref[:, step * w + HD * h : step * w + HD * (h + 1)] for w in range(3))
-        s = mm_nt(q * jnp.asarray(0.125, BF16), k)
-        s = jnp.where(live, s, -1e30)
+    items = [(h, slice(r, r + TM)) for h in range(2) for r in range(0, PAD, TM)]
+
+    def score(h, rows):
+        q = qkv_ref[rows, HD * h : HD * (h + 1)] * jnp.asarray(0.125, BF16)
+        return mm_nt(q, qkv_ref[:, step + HD * h : step + HD * (h + 1)])
+
+    scores = [score(*item) for item in items[:3]]
+    for at, (h, rows) in enumerate(items):
+        if at + 3 < len(items):
+            scores.append(score(*items[at + 3]))
+        s = jnp.where(live, scores[at], -1e30)
         e = jnp.exp(s - jnp.max(s, axis=1, keepdims=True))
         p = (e * (1.0 / jnp.sum(e, axis=1, keepdims=True))).astype(BF16)
-        p_ref[h] = p
-        o_ref[:, HD * h : HD * (h + 1)] = mm(p, v).astype(BF16)
+        p_ref[h, rows, :] = p
+        v = qkv_ref[:, 2 * step + HD * h : 2 * step + HD * (h + 1)]
+        o_ref[rows, HD * h : HD * (h + 1)] = mm(p, v).astype(BF16)
 
 
 def attend(qkv):
@@ -154,17 +169,21 @@
 
 def attend_back_kernel(qkv_ref, p_ref, g_ref, d_ref, sum_ref):
     step = 2 * HD
+
+    def cut(h, w):
+        return slice(step * w + HD * h, step * w + HD * (h + 1))
+
+    grads = [g_ref[:, HD * h : HD * (h + 1)] for h in range(2)]
+    dprobs = [mm_nt(grads[h], qkv_ref[:, cut(h, 2)]) for h in range(2)]
+    dscores = []
     for h in range(2):
-        q, k, v = (qkv_ref[:, step * w + HD * h : step * w + HD * (h + 1)] for w in range(3))
-        g = g_ref[:, HD * h : HD * (h + 1)]
-        pb = p_ref[h]
-        p = pb.astype(F32)
-        dp = mm_nt(g, v)
-        z = jnp.sum(p * dp, axis=1, keepdims=True)
-        ds = (p * (dp - z)).astype(BF16)
-        parts = (mm(ds, k) * 0.125, mm_tn(ds, q) * 0.125, mm_tn(pb, g))
-        for w, part in enumerate(parts):
-            d_ref[:, step * w + HD * h : step * w + HD * (h + 1)] = part.astype(BF16)
+        p = p_ref[h].astype(F32)
+        z = jnp.sum(p * dprobs[h], axis=1, keepdims=True)
+        dscores.append((p * (dprobs[h] - z)).astype(BF16))
+        d_ref[:, cut(h, 2)] = mm_tn(p_ref[h], grads[h]).astype(BF16)
+    for h in range(2):
+        d_ref[:, cut(h, 0)] = (mm(dscores[h], qkv_ref[:, cut(h, 1)]) * 0.125).astype(BF16)
+        d_ref[:, cut(h, 1)] = (mm_tn(dscores[h], qkv_ref[:, cut(h, 0)]) * 0.125).astype(BF16)
     add_up(sum_ref, pl.program_id(1) == 0, col_sum(d_ref[...].astype(F32)))
 
 
@@ -215,104 +234,89 @@
     before = refs[4:6] if final else ()
     rest = refs[4 + len(before) :]
     g_ref, du_ref, bsum_ref = rest[:3]
-    low_acc, lift_acc, buf, sems = rest[6:10] if final else rest[5:9]
-    j = pl.program_id(0)
-    tn = g_ref.shape[1]
-    slot = lax.rem(j, 2)
-
-    def load(tile, at):
-        return pltpu.make_async_copy(packs[tile], buf.at[at], sems.at[at])
-
-    def fetch(at):
-        return pltpu.make_async_copy(before[at], rest[10 + at], sems.at[2 + at])
-
-    @pl.when(j == 0)
+    buf, sem = rest[6:8] if final else rest[5:7]
+    i = pl.program_id(0)
+    tn = g_ref.shape[1] // 4
+
+    @pl.when(i == 0)
     def _():
-        load(0, 0).start()
-        for at in range(len(before)):
-            fetch(at).start()
-        low_acc[...] = jnp.zeros_like(low_acc)
-        lift_acc[...] = jnp.zeros_like(lift_acc)
-
-    for tile in range(1, 4):
-
-        @pl.when(j == tile - 1)
-        def _(tile=tile):
-            load(tile, tile % 2).start()
-
-    load(0, slot).wait()
-    up, down = buf[slot, :, :tn], buf[slot, :, tn:]
+        copies = []
+        for tile in range(4):
+            for part in range(2):
+                copies.append(
+                    pltpu.make_async_copy(
+                        packs[tile].at[:, pl.ds(part * tn, tn)],
+                        buf.at[part, :, pl.ds(tile * tn, tn)],
+                        sem.at[part, tile],
+                    )
+                )
+        for copy in copies:
+            copy.start()
+        for copy in copies:
+            copy.wait()
+
+    up, down = buf[0], buf[1]
     u = mm(n_ref[...], up) + bias_ref[...]
     cdf = 0.5 * (1.0 + lax.erf(u * ROOT_HALF))
     g = (u * cdf).astype(BF16)
     slope = cdf + u * (jnp.exp(-0.5 * u * u) * DENSITY)
-    g_ref[...] = g
+    for at, tile in enumerate((0, 2, 1, 3)):
+        g_ref[:, at * tn : (at + 1) * tn] = g[:, tile * tn : (tile + 1) * tn]
     du = (mm(dy_ref[...], down) * slope).astype(BF16)
     du_ref[...] = du
-    bsum_ref[...] = col_sum(du.astype(F32))
-    low_acc[...] += mm_nt(g, down)
-    lift_acc[...] += mm_nt(du, up)
-
-    @pl.when(j == 3)
-    def _():
-        if not final:
-            rest[3][...] = low_acc[...].astype(BF16)
-            rest[4][...] = lift_acc[...].astype(BF16)
-            return
-        mine_ref, theirs_ref, lift_ref = rest[3:6]
-        for at in range(2):
-            fetch(at).wait()
-        lift_ref[...] = (lift_acc[...] + rest[11][...].astype(F32)).astype(BF16)
-        low_acc[...] += rest[10][...].astype(F32)
-        width = D // 4
-        core = place_ref[0]
-        for far in range(2):
-            low = pl.multiple_of((2 * far + core) * width, width)
-            other = pl.multiple_of((2 * far + 1 - core) * width, width)
-            mine_ref[:, far * width : (far + 1) * width] = low_acc[:, pl.ds(low, width)]
-            theirs_ref[:, far * width : (far + 1) * width] = low_acc[:, pl.ds(other, width)].astype(
-                BF16
-            )
+    add_up(bsum_ref, i == 0, col_sum(du.astype(F32)))
+    low = mm_nt(g, down)
+    lift = mm_nt(du, up)
+    if not final:
+        rest[3][...] = low.astype(BF16)
+        rest[4][...] = lift.astype(BF16)
+        return
+    mine_ref, theirs_ref, lift_ref = rest[3:6]
+    held = rest[8]
+    lift_ref[...] = (lift + before[1][...].astype(F32)).astype(BF16)
+    held[...] = low + before[0][...].astype(F32)
+    width = D // 4
+    core = place_ref[0]
+    for far in range(2):
+        here = pl.multiple_of((2 * far + core) * width, width)
+        other = pl.multiple_of((2 * far + 1 - core) * width, width)
+        mine_ref[:, far * width : (far + 1) * width] = held[:, pl.ds(here, width)]
+        theirs_ref[:, far * width : (far + 1) * width] = held[:, pl.ds(other, width)].astype(BF16)
 
 
 def mlp(place, n2, dy, bias, packs, before=()):
     rows = n2.shape[0]
-    tn = packs[0].shape[1] // 2
-    first_tile = 4 if before else 0
-    whole = held_once((rows, D))
-    half = held_once((rows, D // 2))
-    tile = pl.BlockSpec((rows, tn), lambda j, *_: (0, j))
-    swapped = pl.BlockSpec(
-        (rows, tn), lambda j, *_: (0, jnp.where(j == 1, 2, jnp.where(j == 2, 1, j)))
-    )
-    thin = pl.BlockSpec((1, tn), lambda j, *_: (0, j))
-    anywhere = pl.BlockSpec(memory_space=pl.ANY)
-    out_specs = [swapped, tile, thin] + ([half, half, whole] if before else [whole, whole])
-    out_shape = [like((rows, 4 * tn), BF16), like((rows, 4 * tn), BF16), like((1, 4 * tn), F32)]
+    hid = 2 * packs[0].shape[1]
+    part = 1 if before else 0
+
+    def block(cols):
+        return pl.BlockSpec((PAD, cols), lambda i, *_: (i, 0))
+
+    out_specs = [block(hid), block(hid), fixed((1, hid))]
+    out_shape = [like((rows, hid), BF16), like((rows, hid), BF16), like((1, hid), F32)]
+    scratch = [pltpu.VMEM((2, D, hid), BF16), pltpu.SemaphoreType.DMA((2, 4))]
     if before:
+        out_specs += [block(D // 2), block(D // 2), block(D)]
         out_shape += [like((rows, D // 2), F32), like((rows, D // 2), BF16), like((rows, D), BF16)]
+        scratch += [pltpu.VMEM((PAD, D), F32)]
     else:
+        out_specs += [block(D), block(D)]
         out_shape += [like((rows, D), BF16)] * 2
     return pl.pallas_call(
         functools.partial(mlp_kernel, bool(before)),
         name="mlp_second" if before else "mlp_first",
         grid_spec=pltpu.PrefetchScalarGridSpec(
             num_scalar_prefetch=1,
-            grid=(4,),
-            in_specs=[whole, whole, pl.BlockSpec((1, tn), lambda j, *_: (0, j + first_tile))]
-            + [anywhere] * (4 + len(before)),
+            grid=(rows // PAD,),
+            in_specs=[block(D), block(D), pl.BlockSpec((1, hid), lambda i, *_: (0, part))]
+            + [pl.BlockSpec(memory_space=pl.ANY)] * 4
+            + [block(D)] * len(before),
             out_specs=out_specs,
-            scratch_shapes=[
-                pltpu.VMEM((rows, D), F32),
-                pltpu.VMEM((rows, D), F32),
-                pltpu.VMEM((2, D, 2 * tn), BF16),
-                pltpu.SemaphoreType.DMA((4,)),
-            ]
-            + [pltpu.VMEM((rows, D), BF16)] * len(before),
+            scratch_shapes=scratch,
         ),
         out_shape=out_shape,
         compiler_params=params(1),
-        cost_estimate=cost(32 * rows * D * tn, 20 * rows * D, 8 * rows * tn),
+        cost_estimate=cost(8 * rows * D * hid, 20 * rows * D, 2 * rows * hid),
     )(place, n2, dy, bias, *packs, *before)
 
 
@@ -606,7 +610,7 @@
     my_core = lax.axis_index("core")
     my_row = lax.axis_index("row")
     my_half = lax.axis_index("dp") % 2
-    place = jnp.stack([my_core, my_x, my_half]).astype(jnp.int32)
+    place = jnp.stack([my_core, my_x, my_half, my_row]).astype(jnp.int32)
     tokens_here, width = inputs.shape
     images = tokens_here // SEQ
     held = images // n_xa
@@ -682,52 +686,30 @@
         ),
         up_bias,
     )
-    pieces = [pieces[0]] + [after(piece, small) for piece in pieces[1:]]
-    cut = 2 * heads_half
-    first_own = jnp.zeros((D, cut), BF16)
-    second_own = jnp.zeros((D, cut), BF16)
-    for shift, piece in enumerate(pieces):
-        start = (my_row - shift) % n_row * (D // n_row)
-        first_own = lax.dynamic_update_slice(first_own, piece[:, :cut], (start, 0))
-        second_own = lax.dynamic_update_slice(second_own, piece[:, cut:], (start, 0))
-    first_far, second_oth = across(first_own), over(second_own)
-    first_oth, second_far = over(first_own), across(second_own)
-
+    fars = [across(piece) for piece in pieces]
+    oths = [over(piece) for piece in pieces]
     small_far = across(small)
     vectors, qkv_bias, tile_bias = unpack(
-        place, small, after(small_far, first_own, second_own), beside(small), beside(small_far)
+        place, small, after(small_far, pieces[-1]), beside(small), beside(small_far)
     )
     out_bias_all, down_bias_all, gain_one, shift_one, gain_two, shift_two = (
         (vectors, pl.BlockSpec((None, 1, D), lambda i, *_, at=at: (at, 0, 0))) for at in range(6)
     )
-    wide_input = wide_tokens(inputs, after(input_got, first_own, second_own))
-    first_far_oth = over(after(first_far, wide_input, qkv_bias))
-    second_far_oth = across(after(second_oth, wide_input, qkv_bias))
+    wide_input = wide_tokens(inputs, after(input_got, pieces[-1]))
+    far_oths = [over(far) for far in fars[:-1]]
+    far_oths.append(across(after(oths[-1], wide_input, qkv_bias)))
 
     def gather(part):
         up_part = halves(up_weight, 1)[0][:, quarter * part : quarter * (part + 1)]
         down_part = halves(down_weight, 0)[0][quarter * part : quarter * (part + 1)].T
-        shard = after(jnp.concatenate([up_part, down_part], axis=1), first_own, second_own)
+        shard = after(jnp.concatenate([up_part, down_part], axis=1), *pieces)
         return lax.all_gather(shard, "row", axis=0, tiled=True)
 
     own_a, own_b = gather(0), gather(1)
     grad_got = across(after(send_tokens(cotangent), wide_input))
 
     wide_one, qkv, attn_weights = norm_qkv(
-        wide_input,
-        gain_one,
-        shift_one,
-        qkv_bias,
-        (
-            first_own,
-            second_own,
-            first_far,
-            second_far,
-            first_oth,
-            second_oth,
-            first_far_oth,
-            second_far_oth,
-        ),
+        place, wide_input, gain_one, shift_one, qkv_bias, (*pieces, *fars, *oths, *far_oths)
     )
     oth_a, far_a = over(own_a), across(own_a)
     oth_b, far_b = over(own_b), across(own_b)
@@ -736,9 +718,7 @@
     mixed_other = beside(mixed)
     wide_grad = wide_tokens(cotangent, after(grad_got, mixed))
     far_oth_a = over(far_a)
-    middle_sum, wide_two = middle(
-        wide_input, mixed, after(mixed_other, wide_grad), out_bias_all, gain_two, shift_two
-    )
+    middle_sum, wide_two = middle(wide_input, mixed, mixed_other, out_bias_all, gain_two, shift_two)
     far_oth_b = across(oth_b)
 
     def tiles(value, first, end):
@@ -817,6 +797,7 @@
         both = jnp.concatenate([first, second]).reshape(images, PAD, width)
         return both[:, :SEQ].reshape(tokens_here, width)
 
+    cut = 2 * heads_half
     split = 3 * three + cut
     dqkv = after(dqkv, up_sum)
     far_oth_qk = mm_tn(wide_one, dqkv[:, 3 * three : split]).astype(BF16)

time: 493 us -> 487 us (0.988)
  Pallas kernels: 140 us -> 123 us
  waiting for transfers between devices: 177 us -> 188 us
    pallas_call x2, Pallas kernels: 43 us -> 35.6 us  [mlp(): pl.pallas_call(functools.partial(mlp_kernel, bool(before)), name='mlp_sec...]
    ppermute x45 -> x51, waiting for transfers between devices: 164 us -> 170 us  [swap(): return lax.ppermute(value, axis, [(at, at ^ bit) for at in range(size)])]
    pallas_call x1, Pallas kernels: 20.2 us -> 14.6 us  [attend(): pl.pallas_call(attend_kernel, grid=(pairs, held), name='attend', in_specs...]
    ppermute x6, waiting for transfers between devices: 12.7 us -> 17.8 us  [shifted(): lax.ppermute(value, 'row', [(at, (at + shift) % n_row) for at in range(n_...]
    ppermute x45 -> x51, starting transfers between devices: 45.1 us -> 46.9 us  [swap(): return lax.ppermute(value, axis, [(at, at ^ bit) for at in range(size)])]
  transfers between devices with their start and end apart: 55 -> 61, of which waited for: 24 -> 28; matrix products, arithmetic and copies ran while one was open for 14% -> 14% of each run, Pallas kernels for 23% -> 21%
where the time goes in v9:
time: 487 us; the launch traced here: 481 us
  waiting for transfers between devices  188 us (39%)
  Pallas kernels  123 us (25%)
  starting transfers between devices  59.5 us (12%)
  matrix products  53.4 us (11%)
  local copies, waits for them, and re-layouts  23.2 us (5%)
  other arithmetic  18.6 us (4%)
  between operations  14.9 us (3%)
    ppermute x51, waiting for transfers between devices, swap(): return lax.ppermute(value, axis, [(at, at ^ bit) for at in range(size)])  170 us
    ppermute x51, starting transfers between devices, swap(): return lax.ppermute(value, axis, [(at, at ^ bit) for at in range(size)])  46.9 us
    dot_general x13, matrix products, mm_tn(): lax.dot_general(a, b, (((0,), (0,)), ((), ())), preferred_element_type=F32)  43.5 us
    pallas_call x2, Pallas kernels, mlp(): pl.pallas_call(functools.partial(mlp_kernel, bool(before)), name='mlp_sec...  35.6 us
    pallas_call x1, Pallas kernels, attend_back(): pl.pallas_call(attend_back_kernel, grid=(pairs, held), name='attend_back'...  22.7 us
    ppermute x6, waiting for transfers between devices, shifted(): lax.ppermute(value, 'row', [(at, (at + shift) % n_row) for at in range(n_...  17.8 us
    pallas_call x1, Pallas kernels, attend(): pl.pallas_call(attend_kernel, grid=(pairs, held), name='attend', in_specs...  14.6 us
    pallas_call x1, Pallas kernels, turn(): pl.pallas_call(turn_kernel, name='turn', grid_spec=pltpu.PrefetchScalarGr...  14.2 us
  transfers between devices with their start and end apart: 61, of which 28 were waited for; matrix products, arithmetic and copies ran while one was open for 14% of the time, Pallas kernels for 21%

profile of v9, /device:TPU:0, one launch (start us, length us, event | category | flops | bytes accessed | tf_op | source)
XLA Modules:
  0.0 481.0 jit_solution(15620510854240910970)
XLA Ops:
  9.0 3.0 collective-permute-start
  12.8 3.7 collective-permute-start.1
  16.5 5.3 %collective-permute-done.1.refs_3_ = bf16[256,512]{1,0:T(8,128)(2,1)S(1)} collective-permute-done((bf16[256,512]{1,0:T(8,128)(2,1)S(1)}, bf16[256,512]{1,0:T(8,128)(2,1)S(1)}, u32[]{:S(2)}, u32[]{:S(2)}) %collective-permute-start.1) | collective-permute-done | bytes 262176 | tf_op jit(solution)/shard_map/ppermute | solution.py:627
  21.8 3.6 collective-permute-done
  30.9 2.6 collective-permute-start.7
  38.2 2.3 collective-permute-done.6.refs_1_
  40.8 10.2 %collective-permute-done.7.refs_2_ = bf16[256,512]{1,0:T(8,128)(2,1)} collective-permute-done((bf16[256,512]{1,0:T(8,128)(2,1)S(1)}, bf16[256,512]{1,0:T(8,128)(2,1)}, u32[]{:S(2)}, u32[]{:S(2)}) %collective-permute-start.7) | collective-permute-done | bytes 262176 | tf_op jit(solution)/shard_map/ppermute | solution.py:627
  58.5 6.5 %collective-permute-done.15.refs_11_ = bf16[256,512]{1,0:T(8,128)(2,1)} collective-permute-done((bf16[256,512]{1,0:T(8,128)(2,1)}, bf16[256,512]{1,0:T(8,128)(2,1)}, u32[]{:S(2)}, u32[]{:S(2)}) %collective-permute-start.15) | collective-permute-done | bytes 262176 | tf_op jit(solution)/shard_map/ppermute | solution.py:624
  75.4 4.5 collective-permute-done.14.refs_10_
  80.5 5.1 %collective-permute-done.16.refs_12_ = bf16[256,512]{1,0:T(8,128)(2,1)S(1)} collective-permute-done((bf16[256,512]{1,0:T(8,128)(2,1)}, bf16[256,512]{1,0:T(8,128)(2,1)S(1)}, u32[]{:S(2)}, u32[]{:S(2)}) %collective-permute-start.16) | collective-permute-done | bytes 262176 | tf_op jit(solution)/shard_map/ppermute | solution.py:624
  85.6 5.6 %collective-permute-done.17.refs_13_ = bf16[256,512]{1,0:T(8,128)(2,1)S(1)} collective-permute-done((bf16[256,512]{1,0:T(8,128)(2,1)}, bf16[256,512]{1,0:T(8,128)(2,1)S(1)}, u32[]{:S(2)}, u32[]{:S(2)}) %collective-permute-start.17) | collective-permute-done | bytes 262176 | tf_op jit(solution)/shard_map/ppermute | solution.py:624
  91.2 3.8 collective-permute-done.18.refs_14_
  95.7 10.8 %norm_qkv.1 = (bf16[1184,1024]{1,0:T(8,128)(2,1)}, bf16[1184,1536]{1,0:T(8,128)(2,1)}, bf16[1024,2048]{1,0:T(8,128)(2,1)}) custom-call(s32[4]{0:T(128)} %pad_add_fusion.place_ref, bf16[1184,1024]{1,0:T(8,128)(2,1)} %pad_maximum_fusion.x_ref, f32[6,1,1024]{2,1,0:T(1,128)} %get-tuple-element.93.gain_ref.shift_ref.bias_ref, ...), custom_call_target="tpu_custom_call" | custom-call | flops 3724541952 | bytes 19398656 | tf_op jit(solution)/shard_map/norm_qkv/pallas_call | solution.py:114
  106.6 14.6 %attend.1 = (bf16[1184,512]{1,0:T(8,128)(2,1)}, bf16[2,8,592,592]{3,2,1,0:T(8,128)(2,1)}) custom-call(bf16[1184,1536]{1,0:T(8,128)(2,1)} %get-tuple-element.96.qkv_ref), custom_call_target="tpu_custom_call" | custom-call | flops 17226006528 | bytes 48496640 | tf_op jit(solution)/shard_map/attend/pallas_call | solution.py:155
  121.2 4.4 convolution_convert_fusion.a_ref
  128.8 23.2 %collective-permute-done.23.refs_1_ = bf16[1024,512]{1,0:T(8,128)(2,1)} collective-permute-done((bf16[1024,512]{1,0:T(8,128)(2,1)}, bf16[1024,512]{1,0:T(8,128)(2,1)}, u32[]{:S(2)}, u32[]{:S(2)}) %collective-permute-start.23) | collective-permute-done | bytes 1048608 | tf_op jit(solution)/shard_map/ppermute | solution.py:624
  158.5 6.8 %middle.1 = (f32[1184,1024]{1,0:T(8,128)}, bf16[1184,1024]{1,0:T(8,128)(2,1)}) custom-call(bf16[1184,1024]{1,0:T(8,128)(2,1)} %pad_maximum_fusion.x_ref, bf16[1184,1024]{1,0:T(8,128)(2,1)} %convolution_convert_fusion.a_ref, bf16[1184,1024]{1,0:T(8,128)(2,1)} %collective-permute-done.20.b_ref, f32[6,1,1024]{2,1,0:T(1,128)} %get-tuple-element.93.gain_ref.shift_ref.bias_ref, ...), custom_call_target="tpu_custom_call" | custom-call | flops 24248320 | bytes 14548992 | tf_op jit(solution)/shard_map/middle/pallas_call | solution.py:220
  165.3 10.3 %collective-permute-done.24.refs_2_ = bf16[1024,512]{1,0:T(8,128)(2,1)} collective-permute-done((bf16[1024,512]{1,0:T(8,128)(2,1)}, bf16[1024,512]{1,0:T(8,128)(2,1)}, u32[]{:S(2)}, u32[]{:S(2)}) %collective-permute-start.24) | collective-permute-done | bytes 1048608 | tf_op jit(solution)/shard_map/ppermute | solution.py:624
  175.6 21.6 %collective-permute-done.25.refs_3_ = bf16[1024,512]{1,0:T(8,128)(2,1)} collective-permute-done((bf16[1024,512]{1,0:T(8,128)(2,1)}, bf16[1024,512]{1,0:T(8,128)(2,1)}, u32[]{:S(2)}, u32[]{:S(2)}) %collective-permute-start.25) | collective-permute-done | bytes 1048608 | tf_op jit(solution)/shard_map/ppermute | solution.py:624
  197.2 16.7 %mlp_first.1 = (bf16[1184,1024]{1,0:T(8,128)(2,1)}, bf16[1184,1024]{1,0:T(8,128)(2,1)}, f32[1,1024]{1,0:T(1,128)}, bf16[1184,1024]{1,0:T(8,128)(2,1)}, bf16[1184,1024]{1,0:T(8,128)(2,1)}) custom-call(s32[4]{0:T(128)} %pad_add_fusion.place_ref, bf16[1184,1024]{1,0:T(8,128)(2,1)} %get-tuple-element.107.n_ref, bf16[1184,1024]{1,0:T(8,128)(2,1)} %pad_maximum_fusion.1.dy_ref, ...), custom_call_target="tpu_custom_call" | custom-call | flops 9932111872 | bytes 24248320 | tf_op jit(solution)/shard_map/mlp_first/pallas_call | solution.py:305
  214.0 4.7 convolution_convert_fusion.6
  218.7 4.5 convolution_convert_fusion.2
  223.2 18.8 %mlp_second.1 = (bf16[1184,1024]{1,0:T(8,128)(2,1)}, bf16[1184,1024]{1,0:T(8,128)(2,1)}, f32[1,1024]{1,0:T(1,128)}, f32[1184,512]{1,0:T(8,128)}, bf16[1184,512]{1,0:T(8,128)(2,1)}, /*index=5*/bf16[1184,1024]{1,0:T(8,128)(2,1)}) custom-call(s32[4]{0:T(128)} %pad_add_fusion.place_ref, bf16[1184,1024]{1,0:T(8,128)(2,1)} %get-tuple-element.107.n_ref, ...), custom_call_target="tpu_custom_call" | custom-call | flops 9932111872 | bytes 24248320 | tf_op jit(solution)/shard_map/mlp_second/pallas_call | solution.py:305
  242.7 4.7 convolution_convert_fusion.5
  247.4 2.5 convolution_convert_fusion.4
  254.9 14.2 %turn.1 = (f32[1184,1024]{1,0:T(8,128)}, bf16[1184,1024]{1,0:T(8,128)(2,1)}, bf16[1184,512]{1,0:T(8,128)(2,1)}, f32[4,1024]{1,0:T(4,128)}, bf16[1184,256]{1,0:T(8,128)(2,1)}, /*index=5*/bf16[1184,256]{1,0:T(8,128)(2,1)}) custom-call(s32[4]{0:T(128)} %pad_add_fusion.place_ref, f32[1184,1024]{1,0:T(8,128)} %get-tuple-element.99.h_ref, ...), custom_call_target="tpu_custom_call" | custom-call | flops 1241513984 | bytes 24248320 | tf_op jit(solution)/shard_map/turn/pallas_call | solution.py:364
  269.1 3.8 convolution_convert_fusion.3
  272.9 3.4 collective-permute-done.33
  276.6 21.2 %collective-permute-done.31 = bf16[1024,512]{1,0:T(8,128)(2,1)} collective-permute-done((bf16[1024,512]{1,0:T(8,128)(2,1)}, bf16[1024,512]{1,0:T(8,128)(2,1)}, u32[]{:S(2)}, u32[]{:S(2)}) %collective-permute-start.31) | collective-permute-done | bytes 1048608 | tf_op jit(solution)/shard_map/ppermute | solution.py:624
  299.4 2.8 add_convert_fusion.refs_2_
  303.7 3.1 add_convert_fusion.1.refs_0_
  309.2 2.8 add_convert_fusion.2.refs_4_
  317.3 22.2 %collective-permute-done.36 = bf16[256,512]{1,0:T(8,128)(2,1)S(1)} collective-permute-done((bf16[256,512]{1,0:T(8,128)(2,1)S(1)}, bf16[256,512]{1,0:T(8,128)(2,1)S(1)}, u32[]{:S(2)}, u32[]{:S(2)}) %collective-permute-start.36) | collective-permute-done | bytes 262176 | tf_op jit(solution)/shard_map/ppermute | solution.py:624
  339.6 22.7 %attend_back.1 = (bf16[1184,1536]{1,0:T(8,128)(2,1)}, f32[1,1536]{1,0:T(1,128)}) custom-call(bf16[1184,1536]{1,0:T(8,128)(2,1)} %get-tuple-element.96.qkv_ref, bf16[2,8,592,592]{3,2,1,0:T(8,128)(2,1)} %get-tuple-element.123.p_ref, bf16[1184,512]{1,0:T(8,128)(2,1)} %get-tuple-element.130.g_ref), custom_call_target="tpu_custom_call" | custom-call | flops 21532508160 | bytes 60620800 | tf_op jit(solution)/shard_map/attend_back/pallas_call | solution.py:195
  363.9 4.1 join.1
  368.0 2.7 convolution_convert_fusion.8
  370.9 2.8 convolution_convert_fusion.7
  373.8 5.4 %convolution_convert_fusion.1.a_ref = bf16[1184,1024]{1,0:T(8,128)(2,1)} fusion(bf16[1184,1536]{1,0:T(8,128)(2,1)S(1)} %copy-done.46, bf16[1024,2048]{1,0:T(8,128)(2,1)S(1)} %copy-done.2), kind=kOutput, calls=%fused_computation.1 | convolution fusion | flops 3725754368 | bytes 9207808 | tf_op jit(solution)/shard_map/dot_general | solution.py:30
  383.3 5.1 %collective-permute-done.42 = bf16[1024,128]{1,0:T(8,128)(2,1)S(1)} collective-permute-done((bf16[1024,128]{1,0:T(8,128)(2,1)S(1)}, bf16[1024,128]{1,0:T(8,128)(2,1)S(1)}, u32[]{:S(2)}, u32[]{:S(2)}) %collective-permute-start.42) | collective-permute-done | bytes 262176 | tf_op jit(solution)/shard_map/ppermute | solution.py:624
  388.4 4.4 add_convert_fusion.5
  395.5 2.4 add_convert_fusion.4
  398.5 2.6 collective-permute-done.56
  401.2 2.4 fusion.8
  405.5 8.9 %last.1 = (f32[1184,256]{1,0:T(8,128)}, bf16[1184,256]{1,0:T(8,128)(2,1)}, f32[2,256]{1,0:T(2,128)}, f32[2,256]{1,0:T(2,128)}) custom-call(s32[4]{0:T(128)} %pad_add_fusion.place_ref, bf16[1184,1024]{1,0:T(8,128)(2,1)} %pad_maximum_fusion.x_ref, f32[1184,1024]{1,0:T(8,128)} %get-tuple-element.142.dh_ref, bf16[1184,1024]{1,0:T(8,128)(2,1)} %convolution_convert_fusion.1.a_ref, ...), custom_call_target="tpu_custom_call" | custom-call | flops 24248320 | bytes 14548992 | tf_op jit(solution)/shard_map/last/pallas_call | solution.py:424
  425.4 2.4 collective-permute-start.49
  432.0 11.6 %collective-permute-done.53 = f32[12,256]{1,0:T(8,128)S(1)} collective-permute-done((f32[12,256]{1,0:T(8,128)S(1)}, f32[12,256]{1,0:T(8,128)S(1)}, u32[]{:S(2)}, u32[]{:S(2)}) %collective-permute-start.53) | collective-permute-done | bytes 12320 | tf_op jit(solution)/shard_map/ppermute | solution.py:624
  449.4 2.3 collective-permute-done.50
  459.5 8.5 %collective-permute-done.55 = bf16[256,896]{1,0:T(8,128)(2,1)} collective-permute-done((bf16[256,896]{1,0:T(8,128)(2,1)}, bf16[256,896]{1,0:T(8,128)(2,1)}, u32[]{:S(2)}, u32[]{:S(2)}) %collective-permute-start.55) | collective-permute-done | bytes 458784 | tf_op jit(solution)/shard_map/ppermute | solution.py:624
  (290 shorter events, 104.3 us)
Async XLA Ops:
  7.2 118.9 %all-gather.3.cloned.1.call-start = ((), (), s32[]{:S(2)}) async-start(), calls=%async_computation.2 | async-start | bytes 1310720 | tf_op jit(solution)/shard_map/all_gather | solution.py:706
  9.0 16.4 %collective-permute-start = (bf16[1154,256]{1,0:T(8,128)(2,1)S(1)}, bf16[1154,256]{1,0:T(8,128)(2,1)S(1)}, u32[]{:S(2)}, u32[]{:S(2)}) collective-permute-start(bf16[1154,256]{1,0:T(8,128)(2,1)S(1)} %get-tuple-element.216), channel_id=1, source_target_pairs={{0,2},{2,0},{1,3},{3,1},{4,6},{6,4},{5,7},{7,5},{8,10},{10,8},{9,1... | collective-permute-start | bytes 1772552 | tf_op jit(solution)/shard_map/ppermute | solution.py:624
  25.8 29.4 %collective-permute-start.2 = (bf16[1184,512]{1,0:T(8,128)(2,1)S(1)}, bf16[1184,512]{1,0:T(8,128)(2,1)S(1)}, u32[]{:S(2)}, u32[]{:S(2)}) collective-permute-start(bf16[1184,512]{1,0:T(8,128)(2,1)S(1)} %bitcast.55), channel_id=1, source_target_pairs={{0,1},{1,0},{2,3},{3,2},{4,5},{5,4},{6,7},{7,6},{8,9},{9,8},{10,11... | collective-permute-start | bytes 3637256 | tf_op jit(solution)/shard_map/ppermute | solution.py:624
  29.1 23.5 %collective-permute-start.4 = (f32[12,256]{1,0:T(8,128)}, f32[12,256]{1,0:T(8,128)S(1)}, u32[]{:S(2)}, u32[]{:S(2)}) collective-permute-start(f32[12,256]{1,0:T(8,128)} %pack.1.own), channel_id=1, source_target_pairs={{0,1},{1,0},{2,3},{3,2},{4,5},{5,4},{6,7},{7,6},{8,9},{9,8},{10,11... | collective-permute-start | bytes 36872 | tf_op jit(solution)/shard_map/ppermute | solution.py:624
  30.9 20.1 %collective-permute-start.7 = (bf16[256,512]{1,0:T(8,128)(2,1)S(1)}, bf16[256,512]{1,0:T(8,128)(2,1)}, u32[]{:S(2)}, u32[]{:S(2)}) collective-permute-start(bf16[256,512]{1,0:T(8,128)(2,1)S(1)} %pad_maximum_fusion.8.refs_0_), channel_id=1, source_target_pairs={{0,8},{4,12},{8,0},{12,4},{1,9},{5,13},{9,1},{13,5},{2,10},{6,14},... | collective-permute-start | bytes 786440 | tf_op jit(solution)/shard_map/ppermute | solution.py:627
  37.6 15.6 %collective-permute-start.5 = (f32[12,256]{1,0:T(8,128)S(1)}, f32[12,256]{1,0:T(8,128)S(1)}, u32[]{:S(2)}, u32[]{:S(2)}) collective-permute-start(f32[12,256]{1,0:T(8,128)S(1)} %collective-permute-done.3.far), channel_id=1, source_target_pairs={{0,1},{1,0},{2,3},{3,2},{4,5},{5,4},{6,7},{7,6},{8,9},{9,8},{10,11... | collective-permute-start | bytes 36872 | tf_op jit(solution)/shard_map/ppermute | solution.py:624
  40.5 16.6 %collective-permute-start.8 = (bf16[256,512]{1,0:T(8,128)(2,1)S(1)}, bf16[256,512]{1,0:T(8,128)(2,1)}, u32[]{:S(2)}, u32[]{:S(2)}) collective-permute-start(bf16[256,512]{1,0:T(8,128)(2,1)S(1)} %pad_maximum_fusion.8.refs_0_), channel_id=1, source_target_pairs={{0,2},{2,0},{1,3},{3,1},{4,6},{6,4},{5,7},{7,5},{8,10},{10,8},{9,1... | collective-permute-start | bytes 786440 | tf_op jit(solution)/shard_map/ppermute | solution.py:624
  51.0 17.2 %collective-permute-start.12 = (bf16[256,512]{1,0:T(8,128)(2,1)S(1)}, bf16[256,512]{1,0:T(8,128)(2,1)S(1)}, u32[]{:S(2)}, u32[]{:S(2)}) collective-permute-start(bf16[256,512]{1,0:T(8,128)(2,1)S(1)} %pad_maximum_fusion.8.refs_0_), channel_id=1, source_target_pairs={{0,16},{16,0},{1,17},{17,1},{2,18},{18,2},{3,19},{19,3},{4,20},{20... | collective-permute-start | bytes 786440 | tf_op jit(solution)/shard_map/ppermute | solution.py:624
  52.6 74.2 %all-gather.5.cloned.1.call-start = ((), (), s32[]{:S(2)}) async-start(), calls=%async_computation.3 | async-start | bytes 1310720 | tf_op jit(solution)/shard_map/all_gather | solution.py:706
  52.6 12.3 %collective-permute-start.15 = (bf16[256,512]{1,0:T(8,128)(2,1)}, bf16[256,512]{1,0:T(8,128)(2,1)}, u32[]{:S(2)}, u32[]{:S(2)}) collective-permute-start(bf16[256,512]{1,0:T(8,128)(2,1)} %copy-done.36), channel_id=1, source_target_pairs={{0,16},{16,0},{1,17},{17,1},{2,18},{18,2},{3,19},{19,3},{4,20},{20... | collective-permute-start | bytes 786440 | tf_op jit(solution)/shard_map/ppermute | solution.py:624
  53.2 15.5 %collective-permute-start.9 = (bf16[256,512]{1,0:T(8,128)(2,1)}, bf16[256,512]{1,0:T(8,128)(2,1)}, u32[]{:S(2)}, u32[]{:S(2)}) collective-permute-start(bf16[256,512]{1,0:T(8,128)(2,1)} %collective-permute-done.6.refs_1_), channel_id=1, source_target_pairs={{0,2},{2,0},{1,3},{3,1},{4,6},{6,4},{5,7},{7,5},{8,10},{10,8},{9,1... | collective-permute-start | bytes 786440 | tf_op jit(solution)/shard_map/ppermute | solution.py:624
  55.3 15.0 %collective-permute-start.10 = (bf16[256,512]{1,0:T(8,128)(2,1)}, bf16[256,512]{1,0:T(8,128)(2,1)}, u32[]{:S(2)}, u32[]{:S(2)}) collective-permute-start(bf16[256,512]{1,0:T(8,128)(2,1)} %collective-permute-done.7.refs_2_), channel_id=1, source_target_pairs={{0,2},{2,0},{1,3},{3,1},{4,6},{6,4},{5,7},{7,5},{8,10},{10,8},{9,1... | collective-permute-start | bytes 786440 | tf_op jit(solution)/shard_map/ppermute | solution.py:624
  57.9 14.4 %collective-permute-start.11 = (bf16[256,512]{1,0:T(8,128)(2,1)S(1)}, bf16[256,512]{1,0:T(8,128)(2,1)S(1)}, u32[]{:S(2)}, u32[]{:S(2)}) collective-permute-start(bf16[256,512]{1,0:T(8,128)(2,1)S(1)} %copy-done.37), channel_id=1, source_target_pairs={{0,2},{2,0},{1,3},{3,1},{4,6},{6,4},{5,7},{7,5},{8,10},{10,8},{9,1... | collective-permute-start | bytes 786440 | tf_op jit(solution)/shard_map/ppermute | solution.py:624
  68.8 16.8 %collective-permute-start.16 = (bf16[256,512]{1,0:T(8,128)(2,1)}, bf16[256,512]{1,0:T(8,128)(2,1)S(1)}, u32[]{:S(2)}, u32[]{:S(2)}) collective-permute-start(bf16[256,512]{1,0:T(8,128)(2,1)} %collective-permute-done.8.refs_4_), channel_id=1, source_target_pairs={{0,16},{16,0},{1,17},{17,1},{2,18},{18,2},{3,19},{19,3},{4,20},{20... | collective-permute-start | bytes 786440 | tf_op jit(solution)/shard_map/ppermute | solution.py:624
  70.3 20.9 %collective-permute-start.17 = (bf16[256,512]{1,0:T(8,128)(2,1)}, bf16[256,512]{1,0:T(8,128)(2,1)S(1)}, u32[]{:S(2)}, u32[]{:S(2)}) collective-permute-start(bf16[256,512]{1,0:T(8,128)(2,1)} %collective-permute-done.9.refs_5_), channel_id=1, source_target_pairs={{0,16},{16,0},{1,17},{17,1},{2,18},{18,2},{3,19},{19,3},{4,20},{20... | collective-permute-start | bytes 786440 | tf_op jit(solution)/shard_map/ppermute | solution.py:624
  72.3 22.7 %collective-permute-start.18 = (bf16[256,512]{1,0:T(8,128)(2,1)}, bf16[256,512]{1,0:T(8,128)(2,1)S(1)}, u32[]{:S(2)}, u32[]{:S(2)}) collective-permute-start(bf16[256,512]{1,0:T(8,128)(2,1)} %collective-permute-done.10.refs_6_), channel_id=1, source_target_pairs={{0,16},{16,0},{1,17},{17,1},{2,18},{18,2},{3,19},{19,3},{4,20},{20... | collective-permute-start | bytes 786440 | tf_op jit(solution)/shard_map/ppermute | solution.py:624
  74.4 20.7 %collective-permute-start.19 = (bf16[256,512]{1,0:T(8,128)(2,1)}, bf16[256,512]{1,0:T(8,128)(2,1)}, u32[]{:S(2)}, u32[]{:S(2)}) collective-permute-start(bf16[256,512]{1,0:T(8,128)(2,1)} %collective-permute-done.15.refs_11_), channel_id=1, source_target_pairs={{0,2},{2,0},{1,3},{3,1},{4,6},{6,4},{5,7},{7,5},{8,10},{10,8},{9,1... | collective-permute-start | bytes 786440 | tf_op jit(solution)/shard_map/ppermute | solution.py:624
  75.2 237.5 %reduce-scatter.3.cloned.1.call-start = ((), (), s32[]{:S(2)}) async-start(), calls=%async_computation.4 | async-start | bytes 2621440 | tf_op jit(solution)/shard_map/reduce_scatter | solution.py:733
  80.0 45.6 %collective-permute-start.21 = (bf16[1154,256]{1,0:T(8,128)(2,1)S(1)}, bf16[1154,256]{1,0:T(8,128)(2,1)S(1)}, u32[]{:S(2)}, u32[]{:S(2)}) collective-permute-start(bf16[1154,256]{1,0:T(8,128)(2,1)S(1)} %get-tuple-element.100), channel_id=1, source_target_pairs={{0,2},{2,0},{1,3},{3,1},{4,6},{6,4},{5,7},{7,5},{8,10},{10,8},{9,1... | collective-permute-start | bytes 1772552 | tf_op jit(solution)/shard_map/ppermute | solution.py:624
  126.0 28.6 %collective-permute-start.22 = (bf16[1184,512]{1,0:T(8,128)(2,1)S(1)}, bf16[1184,512]{1,0:T(8,128)(2,1)S(1)}, u32[]{:S(2)}, u32[]{:S(2)}) collective-permute-start(bf16[1184,512]{1,0:T(8,128)(2,1)S(1)} %bitcast.56), channel_id=1, source_target_pairs={{0,1},{1,0},{2,3},{3,2},{4,5},{5,4},{6,7},{7,6},{8,9},{9,8},{10,11... | collective-permute-start | bytes 3637256 | tf_op jit(solution)/shard_map/ppermute | solution.py:624
  126.1 25.9 %collective-permute-start.23 = (bf16[1024,512]{1,0:T(8,128)(2,1)}, bf16[1024,512]{1,0:T(8,128)(2,1)}, u32[]{:S(2)}, u32[]{:S(2)}) collective-permute-start(bf16[1024,512]{1,0:T(8,128)(2,1)} %all-gather.3.cloned.1.call-done.refs_0_), channel_id=1, source_target_pairs={{0,2},{2,0},{1,3},{3,1},{4,6},{6,4},{5,7},{7,5},{8,10},{10,8},{9,1... | collective-permute-start | bytes 3145736 | tf_op jit(solution)/shard_map/ppermute | solution.py:624
  126.8 26.3 %collective-permute-start.26 = (bf16[1024,512]{1,0:T(8,128)(2,1)}, bf16[1024,512]{1,0:T(8,128)(2,1)}, u32[]{:S(2)}, u32[]{:S(2)}) collective-permute-start(bf16[1024,512]{1,0:T(8,128)(2,1)} %all-gather.5.cloned.1.call-done.refs_0_), channel_id=1, source_target_pairs={{0,16},{16,0},{1,17},{17,1},{2,18},{18,2},{3,19},{19,3},{4,20},{20... | collective-permute-start | bytes 3145736 | tf_op jit(solution)/shard_map/ppermute | solution.py:624
  128.3 30.3 %collective-permute-start.20 = (bf16[1184,1024]{1,0:T(8,128)(2,1)}, bf16[1184,1024]{1,0:T(8,128)(2,1)}, u32[]{:S(2)}, u32[]{:S(2)}) collective-permute-start(bf16[1184,1024]{1,0:T(8,128)(2,1)} %convolution_convert_fusion.a_ref), channel_id=1, source_target_pairs={{0,1},{1,0},{2,3},{3,2},{4,5},{5,4},{6,7},{7,6},{8,9},{9,8},{10,11... | collective-permute-start | bytes 7274504 | tf_op jit(solution)/shard_map/ppermute | solution.py:624
  128.3 47.3 %collective-permute-start.24 = (bf16[1024,512]{1,0:T(8,128)(2,1)}, bf16[1024,512]{1,0:T(8,128)(2,1)}, u32[]{:S(2)}, u32[]{:S(2)}) collective-permute-start(bf16[1024,512]{1,0:T(8,128)(2,1)} %all-gather.3.cloned.1.call-done.refs_0_), channel_id=1, source_target_pairs={{0,16},{16,0},{1,17},{17,1},{2,18},{18,2},{3,19},{19,3},{4,20},{20... | collective-permute-start | bytes 3145736 | tf_op jit(solution)/shard_map/ppermute | solution.py:624
  152.0 71.2 %collective-permute-start.27 = (bf16[1024,512]{1,0:T(8,128)(2,1)}, bf16[1024,512]{1,0:T(8,128)(2,1)}, u32[]{:S(2)}, u32[]{:S(2)}) collective-permute-start(bf16[1024,512]{1,0:T(8,128)(2,1)} %all-gather.5.cloned.1.call-done.refs_0_), channel_id=1, source_target_pairs={{0,2},{2,0},{1,3},{3,1},{4,6},{6,4},{5,7},{7,5},{8,10},{10,8},{9,1... | collective-permute-start | bytes 3145736 | tf_op jit(solution)/shard_map/ppermute | solution.py:624
  153.1 44.1 %collective-permute-start.25 = (bf16[1024,512]{1,0:T(8,128)(2,1)}, bf16[1024,512]{1,0:T(8,128)(2,1)}, u32[]{:S(2)}, u32[]{:S(2)}) collective-permute-start(bf16[1024,512]{1,0:T(8,128)(2,1)} %collective-permute-done.23.refs_1_), channel_id=1, source_target_pairs={{0,16},{16,0},{1,17},{17,1},{2,18},{18,2},{3,19},{19,3},{4,20},{20... | collective-permute-start | bytes 3145736 | tf_op jit(solution)/shard_map/ppermute | solution.py:624
  154.6 68.5 %collective-permute-start.28 = (bf16[1024,512]{1,0:T(8,128)(2,1)}, bf16[1024,512]{1,0:T(8,128)(2,1)}, u32[]{:S(2)}, u32[]{:S(2)}) collective-permute-start(bf16[1024,512]{1,0:T(8,128)(2,1)} %collective-permute-done.26.refs_1_), channel_id=1, source_target_pairs={{0,2},{2,0},{1,3},{3,1},{4,6},{6,4},{5,7},{7,5},{8,10},{10,8},{9,1... | collective-permute-start | bytes 3145736 | tf_op jit(solution)/shard_map/ppermute | solution.py:624
  242.1 214.2 %reduce-scatter.5.cloned.1.call-start = ((), (), s32[]{:S(2)}) async-start(), calls=%async_computation.5 | async-start | bytes 2293760 | tf_op jit(solution)/shard_map/reduce_scatter | solution.py:753
  250.0 26.3 %collective-permute-start.33 = (bf16[1024,512]{1,0:T(8,128)(2,1)}, bf16[1024,512]{1,0:T(8,128)(2,1)}, u32[]{:S(2)}, u32[]{:S(2)}) collective-permute-start(bf16[1024,512]{1,0:T(8,128)(2,1)} %convolution_convert_fusion.4), channel_id=1, source_target_pairs={{0,16},{16,0},{1,17},{17,1},{2,18},{18,2},{3,19},{19,3},{4,20},{20... | collective-permute-start | bytes 3145736 | tf_op jit(solution)/shard_map/ppermute | solution.py:624
  251.5 25.1 %collective-permute-start.32 = (bf16[1024,512]{1,0:T(8,128)(2,1)}, bf16[1024,512]{1,0:T(8,128)(2,1)}, u32[]{:S(2)}, u32[]{:S(2)}) collective-permute-start(bf16[1024,512]{1,0:T(8,128)(2,1)} %convolution_convert_fusion.5), channel_id=1, source_target_pairs={{0,2},{2,0},{1,3},{3,1},{4,6},{6,4},{5,7},{7,5},{8,10},{10,8},{9,1... | collective-permute-start | bytes 3145736 | tf_op jit(solution)/shard_map/ppermute | solution.py:624
  253.0 44.9 %collective-permute-start.31 = (bf16[1024,512]{1,0:T(8,128)(2,1)}, bf16[1024,512]{1,0:T(8,128)(2,1)}, u32[]{:S(2)}, u32[]{:S(2)}) collective-permute-start(bf16[1024,512]{1,0:T(8,128)(2,1)} %convolution_convert_fusion.6), channel_id=1, source_target_pairs={{0,16},{16,0},{1,17},{17,1},{2,18},{18,2},{3,19},{19,3},{4,20},{20... | collective-permute-start | bytes 3145736 | tf_op jit(solution)/shard_map/ppermute | solution.py:624
  297.9 14.9 %collective-permute-start.35 = (bf16[1024,256]{1,0:T(8,128)(2,1)S(1)}, bf16[1024,256]{1,0:T(8,128)(2,1)}, u32[]{:S(2)}, u32[]{:S(2)}) collective-permute-start(bf16[1024,256]{1,0:T(8,128)(2,1)S(1)} %slice.223), channel_id=1, source_target_pairs={{0,16},{16,0},{1,17},{17,1},{2,18},{18,2},{3,19},{19,3},{4,20},{20... | collective-permute-start | bytes 1572872 | tf_op jit(solution)/shard_map/ppermute | solution.py:624
  303.1 59.3 %collective-permute-start.38 = (bf16[1024,256]{1,0:T(8,128)(2,1)}, bf16[1024,256]{1,0:T(8,128)(2,1)}, u32[]{:S(2)}, u32[]{:S(2)}) collective-permute-start(bf16[1024,256]{1,0:T(8,128)(2,1)} %slice.226), channel_id=1, source_target_pairs={{0,16},{16,0},{1,17},{17,1},{2,18},{18,2},{3,19},{19,3},{4,20},{20... | collective-permute-start | bytes 1572872 | tf_op jit(solution)/shard_map/ppermute | solution.py:624
  307.7 54.7 %collective-permute-start.37 = (bf16[1024,256]{1,0:T(8,128)(2,1)}, bf16[1024,256]{1,0:T(8,128)(2,1)}, u32[]{:S(2)}, u32[]{:S(2)}) collective-permute-start(bf16[1024,256]{1,0:T(8,128)(2,1)} %slice.225), channel_id=1, source_target_pairs={{0,2},{2,0},{1,3},{3,1},{4,6},{6,4},{5,7},{7,5},{8,10},{10,8},{9,1... | collective-permute-start | bytes 1572872 | tf_op jit(solution)/shard_map/ppermute | solution.py:624
  312.0 50.4 %collective-permute-start.39 = (bf16[1024,256]{1,0:T(8,128)(2,1)S(1)}, bf16[1024,256]{1,0:T(8,128)(2,1)S(1)}, u32[]{:S(2)}, u32[]{:S(2)}) collective-permute-start(bf16[1024,256]{1,0:T(8,128)(2,1)S(1)} %slice.227), channel_id=1, source_target_pairs={{0,2},{2,0},{1,3},{3,1},{4,6},{6,4},{5,7},{7,5},{8,10},{10,8},{9,1... | collective-permute-start | bytes 1572872 | tf_op jit(solution)/shard_map/ppermute | solution.py:624
  313.8 25.8 %collective-permute-start.36 = (bf16[256,512]{1,0:T(8,128)(2,1)S(1)}, bf16[256,512]{1,0:T(8,128)(2,1)S(1)}, u32[]{:S(2)}, u32[]{:S(2)}) collective-permute-start(bf16[256,512]{1,0:T(8,128)(2,1)S(1)} %slice.183), channel_id=1, source_target_pairs={{0,2},{2,0},{1,3},{3,1},{4,6},{6,4},{5,7},{7,5},{8,10},{10,8},{9,1... | collective-permute-start | bytes 786440 | tf_op jit(solution)/shard_map/ppermute | solution.py:624
  316.7 45.7 %collective-permute-start.40 = (bf16[1024,128]{1,0:T(8,128)(2,1)S(1)}, bf16[1024,128]{1,0:T(8,128)(2,1)S(1)}, u32[]{:S(2)}, u32[]{:S(2)}) collective-permute-start(bf16[1024,128]{1,0:T(8,128)(2,1)S(1)} %slice.228), channel_id=1, source_target_pairs={{0,2},{2,0},{1,3},{3,1},{4,6},{6,4},{5,7},{7,5},{8,10},{10,8},{9,1... | collective-permute-start | bytes 786440 | tf_op jit(solution)/shard_map/ppermute | solution.py:624
  379.2 26.3 %collective-permute-start.45 = (bf16[1184,1024]{1,0:T(8,128)(2,1)}, bf16[1184,1024]{1,0:T(8,128)(2,1)}, u32[]{:S(2)}, u32[]{:S(2)}) collective-permute-start(bf16[1184,1024]{1,0:T(8,128)(2,1)} %convolution_convert_fusion.1.a_ref), channel_id=1, source_target_pairs={{0,1},{1,0},{2,3},{3,2},{4,5},{5,4},{6,7},{7,6},{8,9},{9,8},{10,11... | collective-permute-start | bytes 7274504 | tf_op jit(solution)/shard_map/ppermute | solution.py:624
  380.7 14.8 %collective-permute-start.41 = (bf16[1024,256]{1,0:T(8,128)(2,1)S(1)}, bf16[1024,256]{1,0:T(8,128)(2,1)S(1)}, u32[]{:S(2)}, u32[]{:S(2)}) collective-permute-start(bf16[1024,256]{1,0:T(8,128)(2,1)S(1)} %convolution_convert_fusion.7), channel_id=1, source_target_pairs={{0,16},{16,0},{1,17},{17,1},{2,18},{18,2},{3,19},{19,3},{4,20},{20... | collective-permute-start | bytes 1572872 | tf_op jit(solution)/shard_map/ppermute | solution.py:624
  382.0 45.9 %collective-permute-start.34 = (bf16[1184,256]{1,0:T(8,128)(2,1)}, bf16[1184,256]{1,0:T(8,128)(2,1)}, u32[]{:S(2)}, u32[]{:S(2)}) collective-permute-start(bf16[1184,256]{1,0:T(8,128)(2,1)} %get-tuple-element.121), channel_id=1, source_target_pairs={{0,2},{2,0},{1,3},{3,1},{4,6},{6,4},{5,7},{7,5},{8,10},{10,8},{9,1... | collective-permute-start | bytes 1818632 | tf_op jit(solution)/shard_map/ppermute | solution.py:624
  382.5 18.6 %collective-permute-start.56 = (bf16[256,512]{1,0:T(8,128)(2,1)S(1)}, bf16[256,512]{1,0:T(8,128)(2,1)S(1)}, u32[]{:S(2)}, u32[]{:S(2)}) collective-permute-start(bf16[256,512]{1,0:T(8,128)(2,1)S(1)} %add_convert_fusion.7), channel_id=1, source_target_pairs={{0,16},{16,0},{1,17},{17,1},{2,18},{18,2},{3,19},{19,3},{4,20},{20... | collective-permute-start | bytes 786440 | tf_op jit(solution)/shard_map/ppermute | solution.py:624
  392.8 25.1 %collective-permute-start.43 = (bf16[1024,384]{1,0:T(8,128)(2,1)}, bf16[1024,384]{1,0:T(8,128)(2,1)S(1)}, u32[]{:S(2)}, u32[]{:S(2)}) collective-permute-start(bf16[1024,384]{1,0:T(8,128)(2,1)} %add_convert_fusion.5), channel_id=1, source_target_pairs={{0,16},{16,0},{1,17},{17,1},{2,18},{18,2},{3,19},{19,3},{4,20},{20... | collective-permute-start | bytes 2359304 | tf_op jit(solution)/shard_map/ppermute | solution.py:624
  397.9 20.0 %collective-permute-start.44 = (bf16[1024,384]{1,0:T(8,128)(2,1)}, bf16[1024,384]{1,0:T(8,128)(2,1)}, u32[]{:S(2)}, u32[]{:S(2)}) collective-permute-start(bf16[1024,384]{1,0:T(8,128)(2,1)} %add_convert_fusion.4), channel_id=1, source_target_pairs={{0,2},{2,0},{1,3},{3,1},{4,6},{6,4},{5,7},{7,5},{8,10},{10,8},{9,1... | collective-permute-start | bytes 2359304 | tf_op jit(solution)/shard_map/ppermute | solution.py:624
  423.3 21.6 %collective-permute-start.47 = (bf16[256,384]{1,0:T(8,128)(2,1)S(1)}, bf16[256,384]{1,0:T(8,128)(2,1)S(1)}, u32[]{:S(2)}, u32[]{:S(2)}) collective-permute-start(bf16[256,384]{1,0:T(8,128)(2,1)S(1)} %get-tuple-element.223), channel_id=1, source_target_pairs={{0,4},{4,8},{8,12},{12,0},{1,5},{5,9},{9,13},{13,1},{2,6},{6,10},{... | collective-permute-start | bytes 589832 | tf_op jit(solution)/shard_map/ppermute | solution.py:627
  425.4 19.5 %collective-permute-start.48 = (bf16[256,384]{1,0:T(8,128)(2,1)S(1)}, bf16[256,384]{1,0:T(8,128)(2,1)S(1)}, u32[]{:S(2)}, u32[]{:S(2)}) collective-permute-start(bf16[256,384]{1,0:T(8,128)(2,1)S(1)} %get-tuple-element.225), channel_id=1, source_target_pairs={{0,8},{4,12},{8,0},{12,4},{1,9},{5,13},{9,1},{13,5},{2,10},{6,14},... | collective-permute-start | bytes 589832 | tf_op jit(solution)/shard_map/ppermute | solution.py:627
  425.4 19.5 %collective-permute-start.49 = (bf16[256,384]{1,0:T(8,128)(2,1)S(1)}, bf16[256,384]{1,0:T(8,128)(2,1)S(1)}, u32[]{:S(2)}, u32[]{:S(2)}) collective-permute-start(bf16[256,384]{1,0:T(8,128)(2,1)S(1)} %get-tuple-element.224), channel_id=1, source_target_pairs={{0,12},{4,0},{8,4},{12,8},{1,13},{5,1},{9,5},{13,9},{2,14},{6,2},{... | collective-permute-start | bytes 589832 | tf_op jit(solution)/shard_map/ppermute | solution.py:627
  427.8 26.0 %collective-permute-start.46 = (bf16[1184,256]{1,0:T(8,128)(2,1)}, bf16[1184,256]{1,0:T(8,128)(2,1)S(1)}, u32[]{:S(2)}, u32[]{:S(2)}) collective-permute-start(bf16[1184,256]{1,0:T(8,128)(2,1)} %get-tuple-element.151), channel_id=1, source_target_pairs={{0,2},{2,0},{1,3},{3,1},{4,6},{6,4},{5,7},{7,5},{8,10},{10,8},{9,1... | collective-permute-start | bytes 1818632 | tf_op jit(solution)/shard_map/ppermute | solution.py:624
  429.3 14.3 %collective-permute-start.53 = (f32[12,256]{1,0:T(8,128)S(1)}, f32[12,256]{1,0:T(8,128)S(1)}, u32[]{:S(2)}, u32[]{:S(2)}) collective-permute-start(f32[12,256]{1,0:T(8,128)S(1)} %add.147), channel_id=1, source_target_pairs={{0,8},{4,12},{8,0},{12,4},{1,9},{5,13},{9,1},{13,5},{2,10},{6,14},... | collective-permute-start | bytes 36872 | tf_op jit(solution)/shard_map/ppermute | solution.py:624
  (67 other events, 832.3 us)
Sparse Core Ops, SparseCore 0:
  52.7 25.3 all-gather.2
  79.7 27.3 all-gather.4
  242.2 41.9 reduce-scatter.2
  383.4 37.3 reduce-scatter.4

commit v10 on v9

--- a/solution.py
+++ b/solution.py
@@ -148,23 +148,30 @@
         o_ref[rows, HD * h : HD * (h + 1)] = mm(p, v).astype(BF16)
 
 
-def attend(qkv):
+def attend(qkv, before=()):
     rows, cols = qkv.shape
     pairs = cols // (6 * HD)
     held = rows // PAD
-    return pl.pallas_call(
-        attend_kernel,
-        grid=(pairs, held),
+    start = pairs // 2 if before else 0
+
+    def kernel(*refs):
+        attend_kernel(refs[0], refs[-2], refs[-1])
+
+    return pl.pallas_call(
+        kernel,
+        grid=(pairs // 2, held),
         name="attend",
-        in_specs=[pl.BlockSpec((PAD, 6 * HD), lambda p, i: (i, p))],
+        in_specs=[pl.BlockSpec((PAD, 6 * HD), lambda p, i: (i, p + start))]
+        + [pl.BlockSpec(memory_space=pl.ANY)] * len(before),
         out_specs=[
-            pl.BlockSpec((PAD, 2 * HD), lambda p, i: (i, p)),
-            pl.BlockSpec((None, 2, PAD, PAD), lambda p, i: (i, p, 0, 0)),
+            pl.BlockSpec((PAD, 2 * HD), lambda p, i: (i, p + start)),
+            pl.BlockSpec((None, 2, PAD, PAD), lambda p, i: (i, p + start, 0, 0)),
         ],
         out_shape=[like((rows, cols // 3), BF16), like((held, 2 * pairs, PAD, PAD), BF16)],
+        input_output_aliases={1: 0, 2: 1} if before else {},
         compiler_params=params(2),
-        cost_estimate=cost(16 * rows * PAD * cols, 40 * rows * D, 4 * rows * PAD * pairs),
-    )(qkv)
+        cost_estimate=cost(8 * rows * PAD * cols, 20 * rows * D, 2 * rows * PAD * pairs),
+    )(qkv, *before)
 
 
 def attend_back_kernel(qkv_ref, p_ref, g_ref, d_ref, sum_ref):
@@ -229,10 +236,10 @@
     )(x, a, b, bias[0], gain[0], shift[0])
 
 
-def mlp_kernel(final, place_ref, n_ref, dy_ref, bias_ref, *refs):
-    packs = refs[:4]
-    before = refs[4:6] if final else ()
-    rest = refs[4 + len(before) :]
+def mlp_kernel(final, split, place_ref, n_ref, dy_ref, bias_ref, *refs):
+    packs = refs[:5]
+    before = refs[5:7] if final else ()
+    rest = refs[5 + len(before) :]
     g_ref, du_ref, bsum_ref = rest[:3]
     buf, sem = rest[6:8] if final else rest[5:7]
     i = pl.program_id(0)
@@ -243,9 +250,13 @@
         copies = []
         for tile in range(4):
             for part in range(2):
+                if tile == 3 and split:
+                    source = packs[tile + part]
+                else:
+                    source = packs[tile].at[:, pl.ds(part * tn, tn)]
                 copies.append(
                     pltpu.make_async_copy(
-                        packs[tile].at[:, pl.ds(part * tn, tn)],
+                        source,
                         buf.at[part, :, pl.ds(tile * tn, tn)],
                         sem.at[part, tile],
                     )
@@ -285,6 +296,8 @@
 
 
 def mlp(place, n2, dy, bias, packs, before=()):
+    split = len(packs) == 5
+    packs = packs if split else (*packs, packs[-1])
     rows = n2.shape[0]
     hid = 2 * packs[0].shape[1]
     part = 1 if before else 0
@@ -303,13 +316,13 @@
         out_specs += [block(D), block(D)]
         out_shape += [like((rows, D), BF16)] * 2
     return pl.pallas_call(
-        functools.partial(mlp_kernel, bool(before)),
+        functools.partial(mlp_kernel, bool(before), split),
         name="mlp_second" if before else "mlp_first",
         grid_spec=pltpu.PrefetchScalarGridSpec(
             num_scalar_prefetch=1,
             grid=(rows // PAD,),
             in_specs=[block(D), block(D), pl.BlockSpec((1, hid), lambda i, *_: (0, part))]
-            + [pl.BlockSpec(memory_space=pl.ANY)] * 4
+            + [pl.BlockSpec(memory_space=pl.ANY)] * 5
             + [block(D)] * len(before),
             out_specs=out_specs,
             scratch_shapes=scratch,
@@ -713,13 +726,15 @@
     )
     oth_a, far_a = over(own_a), across(own_a)
     oth_b, far_b = over(own_b), across(own_b)
-    attended, probs = attend(qkv)
+    first_heads = attend(qkv)
+    attended, probs = attend(qkv, first_heads)
     mixed = mm_nt(attended, attn_weights[:, 4 * three :]).astype(BF16)
     mixed_other = beside(mixed)
     wide_grad = wide_tokens(cotangent, after(grad_got, mixed))
     far_oth_a = over(far_a)
     middle_sum, wide_two = middle(wide_input, mixed, mixed_other, out_bias_all, gain_two, shift_two)
-    far_oth_b = across(oth_b)
+    up_far_oth_b = over(far_b[:, :quarter])
+    down_far_oth_b = across(oth_b[:, quarter:])
 
     def tiles(value, first, end):
         return value[:, quarter * first : quarter * end]
@@ -736,7 +751,7 @@
         after(wide_two, up_over, down_a),
         wide_grad,
         tile_bias,
-        (own_b, oth_b, far_b, far_oth_b),
+        (own_b, oth_b, far_b, up_far_oth_b, down_far_oth_b),
         (low_a, lift_a),
     )
 
@@ -841,6 +856,7 @@
     steps += [("dp", n_dp, 1 << bit) for bit in range(n_dp.bit_length() - 1)]
     for step in steps[:-1]:
         sums = sums + swap(sums, *step)
+        sums = after(sums, up_piece)
     sums = hand_out(sums, swap(sums, *steps[-1]))
     outputs = to_feature_blocks(out_mine, after(out_got, near_sum), BF16)
 

time: 487 us -> 499 us (1.025)
  waiting for transfers between devices: 188 us -> 195 us
    ppermute x6, waiting for transfers between devices: 17.8 us -> 24.9 us  [shifted(): lax.ppermute(value, 'row', [(at, (at + shift) % n_row) for at in range(n_...]
    ppermute x51 -> x52, starting transfers between devices: 46.9 us -> 49.2 us  [swap(): return lax.ppermute(value, axis, [(at, at ^ bit) for at in range(size)])]
    pallas_call x3 -> x4, Pallas kernels: 50.2 us -> 52.3 us  [the longest x2 35.7 us: mlp(): pl.pallas_call(functools.partial(mlp_kernel, bool(before), split), name='...]
    ppermute x51 -> x52, waiting for transfers between devices: 170 us -> 170 us  [swap(): return lax.ppermute(value, axis, [(at, at ^ bit) for at in range(size)])]
  transfers between devices with their start and end apart: 61 -> 62, of which waited for: 28 -> 26; matrix products, arithmetic and copies ran while one was open for 14% -> 15% of each run, Pallas kernels for 21% -> 21%
where the time goes in v10:
time: 499 us; the launch traced here: 493 us
  waiting for transfers between devices  195 us (39%)
  Pallas kernels  126 us (25%)
  starting transfers between devices  61.3 us (12%)
  matrix products  53.6 us (11%)
  local copies, waits for them, and re-layouts  25.4 us (5%)
  other arithmetic  17.3 us (3%)
  between operations  15 us (3%)
    ppermute x52, waiting for transfers between devices, swap(): return lax.ppermute(value, axis, [(at, at ^ bit) for at in range(size)])  170 us
    ppermute x52, starting transfers between devices, swap(): return lax.ppermute(value, axis, [(at, at ^ bit) for at in range(size)])  49.2 us
    dot_general x13, matrix products, mm_tn(): lax.dot_general(a, b, (((0,), (0,)), ((), ())), preferred_element_type=F32)  43.7 us
    pallas_call x2, Pallas kernels, mlp(): pl.pallas_call(functools.partial(mlp_kernel, bool(before), split), name='...  35.7 us
    ppermute x6, waiting for transfers between devices, shifted(): lax.ppermute(value, 'row', [(at, (at + shift) % n_row) for at in range(n_...  24.9 us
    pallas_call x1, Pallas kernels, attend_back(): pl.pallas_call(attend_back_kernel, grid=(pairs, held), name='attend_back'...  22.7 us
    pallas_call x2, Pallas kernels, attend(): pl.pallas_call(kernel, grid=(pairs // 2, held), name='attend', in_specs=[...  16.6 us
    pallas_call x1, Pallas kernels, turn(): pl.pallas_call(turn_kernel, name='turn', grid_spec=pltpu.PrefetchScalarGr...  14.2 us
  transfers between devices with their start and end apart: 62, of which 26 were waited for; matrix products, arithmetic and copies ran while one was open for 15% of the time, Pallas kernels for 21%

profile of v10, /device:TPU:0, one launch (start us, length us, event | category | flops | bytes accessed | tf_op | source)
XLA Modules:
  0.0 493.2 jit_solution(7863924153018454465)
XLA Ops:
  9.0 3.0 collective-permute-start
  12.8 3.7 collective-permute-start.1
  16.5 5.3 %collective-permute-done.1.refs_3_ = bf16[256,512]{1,0:T(8,128)(2,1)S(1)} collective-permute-done((bf16[256,512]{1,0:T(8,128)(2,1)S(1)}, bf16[256,512]{1,0:T(8,128)(2,1)S(1)}, u32[]{:S(2)}, u32[]{:S(2)}) %collective-permute-start.1) | collective-permute-done | bytes 262176 | tf_op jit(solution)/shard_map/ppermute | solution.py:640
  21.8 3.6 collective-permute-done
  30.9 2.6 collective-permute-start.7
  40.8 10.2 %collective-permute-done.7.refs_2_ = bf16[256,512]{1,0:T(8,128)(2,1)} collective-permute-done((bf16[256,512]{1,0:T(8,128)(2,1)S(1)}, bf16[256,512]{1,0:T(8,128)(2,1)}, u32[]{:S(2)}, u32[]{:S(2)}) %collective-permute-start.7) | collective-permute-done | bytes 262176 | tf_op jit(solution)/shard_map/ppermute | solution.py:640
  58.5 6.5 %collective-permute-done.15.refs_11_ = bf16[256,512]{1,0:T(8,128)(2,1)} collective-permute-done((bf16[256,512]{1,0:T(8,128)(2,1)}, bf16[256,512]{1,0:T(8,128)(2,1)}, u32[]{:S(2)}, u32[]{:S(2)}) %collective-permute-start.15) | collective-permute-done | bytes 262176 | tf_op jit(solution)/shard_map/ppermute | solution.py:637
  75.4 4.5 collective-permute-done.14.refs_10_
  80.5 5.1 %collective-permute-done.16.refs_12_ = bf16[256,512]{1,0:T(8,128)(2,1)S(1)} collective-permute-done((bf16[256,512]{1,0:T(8,128)(2,1)}, bf16[256,512]{1,0:T(8,128)(2,1)S(1)}, u32[]{:S(2)}, u32[]{:S(2)}) %collective-permute-start.16) | collective-permute-done | bytes 262176 | tf_op jit(solution)/shard_map/ppermute | solution.py:637
  85.6 5.6 %collective-permute-done.17.refs_13_ = bf16[256,512]{1,0:T(8,128)(2,1)S(1)} collective-permute-done((bf16[256,512]{1,0:T(8,128)(2,1)}, bf16[256,512]{1,0:T(8,128)(2,1)S(1)}, u32[]{:S(2)}, u32[]{:S(2)}) %collective-permute-start.17) | collective-permute-done | bytes 262176 | tf_op jit(solution)/shard_map/ppermute | solution.py:637
  91.2 3.8 collective-permute-done.18.refs_14_
  95.7 10.8 %norm_qkv.1 = (bf16[1184,1024]{1,0:T(8,128)(2,1)}, bf16[1184,1536]{1,0:T(8,128)(2,1)}, bf16[1024,2048]{1,0:T(8,128)(2,1)}) custom-call(s32[4]{0:T(128)} %pad_add_fusion.place_ref, bf16[1184,1024]{1,0:T(8,128)(2,1)} %pad_maximum_fusion.x_ref, f32[6,1,1024]{2,1,0:T(1,128)} %get-tuple-element.97.gain_ref.shift_ref.bias_ref, ...), custom_call_target="tpu_custom_call" | custom-call | flops 3724541952 | bytes 19398656 | tf_op jit(solution)/shard_map/norm_qkv/pallas_call | solution.py:114
  106.5 8.3 %attend.2 = (bf16[1184,512]{1,0:T(8,128)(2,1)}, bf16[2,8,592,592]{3,2,1,0:T(8,128)(2,1)}) custom-call(bf16[1184,1536]{1,0:T(8,128)(2,1)} %get-tuple-element.100.refs_0_.qkv_ref), custom_call_target="tpu_custom_call" | custom-call | flops 8613003264 | bytes 24248320 | tf_op jit(solution)/shard_map/attend/pallas_call | solution.py:160
  114.8 8.3 %attend.3 = (bf16[1184,512]{1,0:T(8,128)(2,1)}, bf16[2,8,592,592]{3,2,1,0:T(8,128)(2,1)}) custom-call(bf16[1184,1536]{1,0:T(8,128)(2,1)} %get-tuple-element.100.refs_0_.qkv_ref, bf16[1184,512]{1,0:T(8,128)(2,1)} %get-tuple-element.101.refs_1_, bf16[2,8,592,592]{3,2,1,0:T(8,128)(2,1)} %get-tuple-element.102.refs_2_), custom_call_target="tpu_custom_call", output_to_operand_aliasing={{0}: (1, {}), {1}: (2, {})} | custom-call | flops 8613003264 | bytes 24248320 | tf_op jit(solution)/shard_map/attend/pallas_call | solution.py:160
  123.1 4.4 convolution_convert_fusion.a_ref
  131.7 22.8 %collective-permute-done.27.refs_2_ = bf16[1024,512]{1,0:T(8,128)(2,1)} collective-permute-done((bf16[1024,512]{1,0:T(8,128)(2,1)}, bf16[1024,512]{1,0:T(8,128)(2,1)}, u32[]{:S(2)}, u32[]{:S(2)}) %collective-permute-start.27) | collective-permute-done | bytes 1048608 | tf_op jit(solution)/shard_map/ppermute | solution.py:637
  160.3 16.1 %collective-permute-done.23.refs_1_ = bf16[1024,512]{1,0:T(8,128)(2,1)} collective-permute-done((bf16[1024,512]{1,0:T(8,128)(2,1)}, bf16[1024,512]{1,0:T(8,128)(2,1)}, u32[]{:S(2)}, u32[]{:S(2)}) %collective-permute-start.23) | collective-permute-done | bytes 1048608 | tf_op jit(solution)/shard_map/ppermute | solution.py:637
  180.9 6.7 %middle.1 = (f32[1184,1024]{1,0:T(8,128)}, bf16[1184,1024]{1,0:T(8,128)(2,1)}) custom-call(bf16[1184,1024]{1,0:T(8,128)(2,1)} %pad_maximum_fusion.x_ref, bf16[1184,1024]{1,0:T(8,128)(2,1)} %convolution_convert_fusion.a_ref, bf16[1184,1024]{1,0:T(8,128)(2,1)} %collective-permute-done.20.b_ref, f32[6,1,1024]{2,1,0:T(1,128)} %get-tuple-element.97.gain_ref.shift_ref.bias_ref, ...), custom_call_target="tpu_custom_call" | custom-call | flops 24248320 | bytes 14548992 | tf_op jit(solution)/shard_map/middle/pallas_call | solution.py:227
  187.6 25.0 %collective-permute-done.25.refs_3_.refs_4_ = bf16[1024,512]{1,0:T(8,128)(2,1)} collective-permute-done((bf16[1024,512]{1,0:T(8,128)(2,1)}, bf16[1024,512]{1,0:T(8,128)(2,1)}, u32[]{:S(2)}, u32[]{:S(2)}) %collective-permute-start.25) | collective-permute-done | bytes 1048608 | tf_op jit(solution)/shard_map/ppermute | solution.py:637
  212.6 17.0 %mlp_first.1 = (bf16[1184,1024]{1,0:T(8,128)(2,1)}, bf16[1184,1024]{1,0:T(8,128)(2,1)}, f32[1,1024]{1,0:T(1,128)}, bf16[1184,1024]{1,0:T(8,128)(2,1)}, bf16[1184,1024]{1,0:T(8,128)(2,1)}) custom-call(s32[4]{0:T(128)} %pad_add_fusion.place_ref, bf16[1184,1024]{1,0:T(8,128)(2,1)} %get-tuple-element.113.n_ref, bf16[1184,1024]{1,0:T(8,128)(2,1)} %pad_maximum_fusion.1.dy_ref, ...), custom_call_target="tpu_custom_call" | custom-call | flops 9932111872 | bytes 24248320 | tf_op jit(solution)/shard_map/mlp_first/pallas_call | solution.py:318
  229.6 6.0 %convolution_convert_fusion.2 = bf16[1024,1024]{1,0:T(8,128)(2,1)} fusion(bf16[1184,1024]{1,0:T(8,128)(2,1)} %get-tuple-element.112, bf16[1184,256]{1,0:T(8,128)(2,1)S(1)} %get-tuple-element.216, bf16[1184,256]{1,0:T(8,128)(2,1)S(1)} %get-tuple-element.248, bf16[1184,256]{1,0:T(8,128)(2,1)S(1)} %get-tuple-element.215, ...), kind=kOutput, calls=%fused_computation.9 | convolution fusion | flops 2493775872 | bytes 6946816 | tf_op jit(solution)/shard_map/dot_general | solution.py:34
  235.5 4.5 convolution_convert_fusion.6
  240.1 18.8 %mlp_second.1 = (bf16[1184,1024]{1,0:T(8,128)(2,1)}, bf16[1184,1024]{1,0:T(8,128)(2,1)}, f32[1,1024]{1,0:T(1,128)}, f32[1184,512]{1,0:T(8,128)}, bf16[1184,512]{1,0:T(8,128)(2,1)}, /*index=5*/bf16[1184,1024]{1,0:T(8,128)(2,1)}) custom-call(s32[4]{0:T(128)} %pad_add_fusion.place_ref, bf16[1184,1024]{1,0:T(8,128)(2,1)} %get-tuple-element.113.n_ref, ...), custom_call_target="tpu_custom_call" | custom-call | flops 9932111872 | bytes 24248320 | tf_op jit(solution)/shard_map/mlp_second/pallas_call | solution.py:318
  259.6 4.7 convolution_convert_fusion.5
  264.3 2.5 convolution_convert_fusion.4
  270.8 14.2 %turn.1 = (f32[1184,1024]{1,0:T(8,128)}, bf16[1184,1024]{1,0:T(8,128)(2,1)}, bf16[1184,512]{1,0:T(8,128)(2,1)}, f32[4,1024]{1,0:T(4,128)}, bf16[1184,256]{1,0:T(8,128)(2,1)}, /*index=5*/bf16[1184,256]{1,0:T(8,128)(2,1)}) custom-call(s32[4]{0:T(128)} %pad_add_fusion.place_ref, f32[1184,1024]{1,0:T(8,128)} %get-tuple-element.105.h_ref, ...), custom_call_target="tpu_custom_call" | custom-call | flops 1241513984 | bytes 24248320 | tf_op jit(solution)/shard_map/turn/pallas_call | solution.py:377
  285.1 3.8 convolution_convert_fusion.3
  288.9 4.3 collective-permute-done.34
  293.5 21.2 %collective-permute-done.32 = bf16[1024,512]{1,0:T(8,128)(2,1)} collective-permute-done((bf16[1024,512]{1,0:T(8,128)(2,1)}, bf16[1024,512]{1,0:T(8,128)(2,1)}, u32[]{:S(2)}, u32[]{:S(2)}) %collective-permute-start.32) | collective-permute-done | bytes 1048608 | tf_op jit(solution)/shard_map/ppermute | solution.py:637
  316.3 2.8 add_convert_fusion.refs_2_
  320.6 3.1 add_convert_fusion.1.refs_0_
  325.2 2.8 add_convert_fusion.2.refs_4_
  334.2 22.2 %collective-permute-done.37 = bf16[256,512]{1,0:T(8,128)(2,1)S(1)} collective-permute-done((bf16[256,512]{1,0:T(8,128)(2,1)S(1)}, bf16[256,512]{1,0:T(8,128)(2,1)S(1)}, u32[]{:S(2)}, u32[]{:S(2)}) %collective-permute-start.37) | collective-permute-done | bytes 262176 | tf_op jit(solution)/shard_map/ppermute | solution.py:637
  356.5 22.7 %attend_back.1 = (bf16[1184,1536]{1,0:T(8,128)(2,1)}, f32[1,1536]{1,0:T(1,128)}) custom-call(bf16[1184,1536]{1,0:T(8,128)(2,1)} %get-tuple-element.100.refs_0_.qkv_ref, bf16[2,8,592,592]{3,2,1,0:T(8,128)(2,1)} %get-tuple-element.129.p_ref, bf16[1184,512]{1,0:T(8,128)(2,1)} %get-tuple-element.136.g_ref), custom_call_target="tpu_custom_call" | custom-call | flops 21532508160 | bytes 60620800 | tf_op jit(solution)/shard_map/attend_back/pallas_call | solution.py:202
  380.8 4.1 join.1
  384.9 2.7 convolution_convert_fusion.8
  387.8 2.8 convolution_convert_fusion.7
  390.7 5.4 %convolution_convert_fusion.1.a_ref = bf16[1184,1024]{1,0:T(8,128)(2,1)} fusion(bf16[1184,1536]{1,0:T(8,128)(2,1)S(1)} %copy-done.47, bf16[1024,2048]{1,0:T(8,128)(2,1)S(1)} %copy-done.2), kind=kOutput, calls=%fused_computation.1 | convolution fusion | flops 3725754368 | bytes 9207808 | tf_op jit(solution)/shard_map/dot_general | solution.py:30
  400.3 5.0 %collective-permute-done.43 = bf16[1024,128]{1,0:T(8,128)(2,1)S(1)} collective-permute-done((bf16[1024,128]{1,0:T(8,128)(2,1)S(1)}, bf16[1024,128]{1,0:T(8,128)(2,1)S(1)}, u32[]{:S(2)}, u32[]{:S(2)}) %collective-permute-start.43) | collective-permute-done | bytes 262176 | tf_op jit(solution)/shard_map/ppermute | solution.py:637
  405.3 4.4 add_convert_fusion.5
  411.0 7.6 %collective-permute-done.42 = bf16[1024,256]{1,0:T(8,128)(2,1)S(1)} collective-permute-done((bf16[1024,256]{1,0:T(8,128)(2,1)S(1)}, bf16[1024,256]{1,0:T(8,128)(2,1)S(1)}, u32[]{:S(2)}, u32[]{:S(2)}) %collective-permute-start.42) | collective-permute-done | bytes 524320 | tf_op jit(solution)/shard_map/ppermute | solution.py:637
  424.1 8.9 %last.1 = (f32[1184,256]{1,0:T(8,128)}, bf16[1184,256]{1,0:T(8,128)(2,1)}, f32[2,256]{1,0:T(2,128)}, f32[2,256]{1,0:T(2,128)}) custom-call(s32[4]{0:T(128)} %pad_add_fusion.place_ref, bf16[1184,1024]{1,0:T(8,128)(2,1)} %pad_maximum_fusion.x_ref, f32[1184,1024]{1,0:T(8,128)} %get-tuple-element.148.dh_ref, bf16[1184,1024]{1,0:T(8,128)(2,1)} %convolution_convert_fusion.1.a_ref, ...), custom_call_target="tpu_custom_call" | custom-call | flops 24248320 | bytes 14548992 | tf_op jit(solution)/shard_map/last/pallas_call | solution.py:437
  434.5 4.5 collective-permute-done.45
  442.4 2.8 collective-permute-start.50
  451.0 4.6 collective-permute-done.49
  458.6 3.0 collective-permute-done.51
  463.9 3.2 collective-permute-start.54
  471.5 6.8 %collective-permute-done.55.b_ref = f32[12,256]{1,0:T(8,128)S(1)} collective-permute-done((f32[12,256]{1,0:T(8,128)S(1)}, f32[12,256]{1,0:T(8,128)S(1)}, u32[]{:S(2)}, u32[]{:S(2)}) %collective-permute-start.55) | collective-permute-done | bytes 12320 | tf_op jit(solution)/shard_map/ppermute | solution.py:637
  (295 shorter events, 105.5 us)
Async XLA Ops:
  7.2 120.9 %all-gather.5.cloned.1.call-start = ((), (), s32[]{:S(2)}) async-start(), calls=%async_computation.3 | async-start | bytes 1310720 | tf_op jit(solution)/shard_map/all_gather | solution.py:719
  9.0 16.4 %collective-permute-start = (bf16[1154,256]{1,0:T(8,128)(2,1)S(1)}, bf16[1154,256]{1,0:T(8,128)(2,1)S(1)}, u32[]{:S(2)}, u32[]{:S(2)}) collective-permute-start(bf16[1154,256]{1,0:T(8,128)(2,1)S(1)} %get-tuple-element.224), channel_id=1, source_target_pairs={{0,2},{2,0},{1,3},{3,1},{4,6},{6,4},{5,7},{7,5},{8,10},{10,8},{9,1... | collective-permute-start | bytes 1772552 | tf_op jit(solution)/shard_map/ppermute | solution.py:637
  25.8 29.4 %collective-permute-start.2 = (bf16[1184,512]{1,0:T(8,128)(2,1)S(1)}, bf16[1184,512]{1,0:T(8,128)(2,1)S(1)}, u32[]{:S(2)}, u32[]{:S(2)}) collective-permute-start(bf16[1184,512]{1,0:T(8,128)(2,1)S(1)} %bitcast.55), channel_id=1, source_target_pairs={{0,1},{1,0},{2,3},{3,2},{4,5},{5,4},{6,7},{7,6},{8,9},{9,8},{10,11... | collective-permute-start | bytes 3637256 | tf_op jit(solution)/shard_map/ppermute | solution.py:637
  29.1 23.5 %collective-permute-start.4 = (f32[12,256]{1,0:T(8,128)}, f32[12,256]{1,0:T(8,128)S(1)}, u32[]{:S(2)}, u32[]{:S(2)}) collective-permute-start(f32[12,256]{1,0:T(8,128)} %pack.1.own), channel_id=1, source_target_pairs={{0,1},{1,0},{2,3},{3,2},{4,5},{5,4},{6,7},{7,6},{8,9},{9,8},{10,11... | collective-permute-start | bytes 36872 | tf_op jit(solution)/shard_map/ppermute | solution.py:637
  30.9 20.1 %collective-permute-start.7 = (bf16[256,512]{1,0:T(8,128)(2,1)S(1)}, bf16[256,512]{1,0:T(8,128)(2,1)}, u32[]{:S(2)}, u32[]{:S(2)}) collective-permute-start(bf16[256,512]{1,0:T(8,128)(2,1)S(1)} %pad_maximum_fusion.8.refs_0_), channel_id=1, source_target_pairs={{0,8},{4,12},{8,0},{12,4},{1,9},{5,13},{9,1},{13,5},{2,10},{6,14},... | collective-permute-start | bytes 786440 | tf_op jit(solution)/shard_map/ppermute | solution.py:640
  37.6 15.6 %collective-permute-start.5 = (f32[12,256]{1,0:T(8,128)S(1)}, f32[12,256]{1,0:T(8,128)S(1)}, u32[]{:S(2)}, u32[]{:S(2)}) collective-permute-start(f32[12,256]{1,0:T(8,128)S(1)} %collective-permute-done.3.far), channel_id=1, source_target_pairs={{0,1},{1,0},{2,3},{3,2},{4,5},{5,4},{6,7},{7,6},{8,9},{9,8},{10,11... | collective-permute-start | bytes 36872 | tf_op jit(solution)/shard_map/ppermute | solution.py:637
  40.5 16.7 %collective-permute-start.8 = (bf16[256,512]{1,0:T(8,128)(2,1)S(1)}, bf16[256,512]{1,0:T(8,128)(2,1)}, u32[]{:S(2)}, u32[]{:S(2)}) collective-permute-start(bf16[256,512]{1,0:T(8,128)(2,1)S(1)} %pad_maximum_fusion.8.refs_0_), channel_id=1, source_target_pairs={{0,2},{2,0},{1,3},{3,1},{4,6},{6,4},{5,7},{7,5},{8,10},{10,8},{9,1... | collective-permute-start | bytes 786440 | tf_op jit(solution)/shard_map/ppermute | solution.py:637
  51.0 17.2 %collective-permute-start.12 = (bf16[256,512]{1,0:T(8,128)(2,1)S(1)}, bf16[256,512]{1,0:T(8,128)(2,1)S(1)}, u32[]{:S(2)}, u32[]{:S(2)}) collective-permute-start(bf16[256,512]{1,0:T(8,128)(2,1)S(1)} %pad_maximum_fusion.8.refs_0_), channel_id=1, source_target_pairs={{0,16},{16,0},{1,17},{17,1},{2,18},{18,2},{3,19},{19,3},{4,20},{20... | collective-permute-start | bytes 786440 | tf_op jit(solution)/shard_map/ppermute | solution.py:637
  52.6 77.7 %all-gather.3.cloned.1.call-start = ((), (), s32[]{:S(2)}) async-start(), calls=%async_computation.2 | async-start | bytes 1310720 | tf_op jit(solution)/shard_map/all_gather | solution.py:719
  52.6 12.3 %collective-permute-start.15 = (bf16[256,512]{1,0:T(8,128)(2,1)}, bf16[256,512]{1,0:T(8,128)(2,1)}, u32[]{:S(2)}, u32[]{:S(2)}) collective-permute-start(bf16[256,512]{1,0:T(8,128)(2,1)} %copy-done.37), channel_id=1, source_target_pairs={{0,16},{16,0},{1,17},{17,1},{2,18},{18,2},{3,19},{19,3},{4,20},{20... | collective-permute-start | bytes 786440 | tf_op jit(solution)/shard_map/ppermute | solution.py:637
  53.2 15.5 %collective-permute-start.9 = (bf16[256,512]{1,0:T(8,128)(2,1)}, bf16[256,512]{1,0:T(8,128)(2,1)}, u32[]{:S(2)}, u32[]{:S(2)}) collective-permute-start(bf16[256,512]{1,0:T(8,128)(2,1)} %collective-permute-done.6.refs_1_), channel_id=1, source_target_pairs={{0,2},{2,0},{1,3},{3,1},{4,6},{6,4},{5,7},{7,5},{8,10},{10,8},{9,1... | collective-permute-start | bytes 786440 | tf_op jit(solution)/shard_map/ppermute | solution.py:637
  55.3 15.0 %collective-permute-start.10 = (bf16[256,512]{1,0:T(8,128)(2,1)}, bf16[256,512]{1,0:T(8,128)(2,1)}, u32[]{:S(2)}, u32[]{:S(2)}) collective-permute-start(bf16[256,512]{1,0:T(8,128)(2,1)} %collective-permute-done.7.refs_2_), channel_id=1, source_target_pairs={{0,2},{2,0},{1,3},{3,1},{4,6},{6,4},{5,7},{7,5},{8,10},{10,8},{9,1... | collective-permute-start | bytes 786440 | tf_op jit(solution)/shard_map/ppermute | solution.py:637
  57.9 14.4 %collective-permute-start.11 = (bf16[256,512]{1,0:T(8,128)(2,1)S(1)}, bf16[256,512]{1,0:T(8,128)(2,1)S(1)}, u32[]{:S(2)}, u32[]{:S(2)}) collective-permute-start(bf16[256,512]{1,0:T(8,128)(2,1)S(1)} %copy-done.38), channel_id=1, source_target_pairs={{0,2},{2,0},{1,3},{3,1},{4,6},{6,4},{5,7},{7,5},{8,10},{10,8},{9,1... | collective-permute-start | bytes 786440 | tf_op jit(solution)/shard_map/ppermute | solution.py:637
  68.7 16.8 %collective-permute-start.16 = (bf16[256,512]{1,0:T(8,128)(2,1)}, bf16[256,512]{1,0:T(8,128)(2,1)S(1)}, u32[]{:S(2)}, u32[]{:S(2)}) collective-permute-start(bf16[256,512]{1,0:T(8,128)(2,1)} %collective-permute-done.8.refs_4_), channel_id=1, source_target_pairs={{0,16},{16,0},{1,17},{17,1},{2,18},{18,2},{3,19},{19,3},{4,20},{20... | collective-permute-start | bytes 786440 | tf_op jit(solution)/shard_map/ppermute | solution.py:637
  70.3 20.9 %collective-permute-start.17 = (bf16[256,512]{1,0:T(8,128)(2,1)}, bf16[256,512]{1,0:T(8,128)(2,1)S(1)}, u32[]{:S(2)}, u32[]{:S(2)}) collective-permute-start(bf16[256,512]{1,0:T(8,128)(2,1)} %collective-permute-done.9.refs_5_), channel_id=1, source_target_pairs={{0,16},{16,0},{1,17},{17,1},{2,18},{18,2},{3,19},{19,3},{4,20},{20... | collective-permute-start | bytes 786440 | tf_op jit(solution)/shard_map/ppermute | solution.py:637
  72.3 22.7 %collective-permute-start.18 = (bf16[256,512]{1,0:T(8,128)(2,1)}, bf16[256,512]{1,0:T(8,128)(2,1)S(1)}, u32[]{:S(2)}, u32[]{:S(2)}) collective-permute-start(bf16[256,512]{1,0:T(8,128)(2,1)} %collective-permute-done.10.refs_6_), channel_id=1, source_target_pairs={{0,16},{16,0},{1,17},{17,1},{2,18},{18,2},{3,19},{19,3},{4,20},{20... | collective-permute-start | bytes 786440 | tf_op jit(solution)/shard_map/ppermute | solution.py:637
  74.4 20.7 %collective-permute-start.19 = (bf16[256,512]{1,0:T(8,128)(2,1)}, bf16[256,512]{1,0:T(8,128)(2,1)}, u32[]{:S(2)}, u32[]{:S(2)}) collective-permute-start(bf16[256,512]{1,0:T(8,128)(2,1)} %collective-permute-done.15.refs_11_), channel_id=1, source_target_pairs={{0,2},{2,0},{1,3},{3,1},{4,6},{6,4},{5,7},{7,5},{8,10},{10,8},{9,1... | collective-permute-start | bytes 786440 | tf_op jit(solution)/shard_map/ppermute | solution.py:637
  75.2 254.4 %reduce-scatter.3.cloned.1.call-start = ((), (), s32[]{:S(2)}) async-start(), calls=%async_computation.4 | async-start | bytes 2621440 | tf_op jit(solution)/shard_map/reduce_scatter | solution.py:748
  80.0 47.6 %collective-permute-start.21 = (bf16[1154,256]{1,0:T(8,128)(2,1)S(1)}, bf16[1154,256]{1,0:T(8,128)(2,1)S(1)}, u32[]{:S(2)}, u32[]{:S(2)}) collective-permute-start(bf16[1154,256]{1,0:T(8,128)(2,1)S(1)} %get-tuple-element.106), channel_id=1, source_target_pairs={{0,2},{2,0},{1,3},{3,1},{4,6},{6,4},{5,7},{7,5},{8,10},{10,8},{9,1... | collective-permute-start | bytes 1772552 | tf_op jit(solution)/shard_map/ppermute | solution.py:637
  128.0 49.0 %collective-permute-start.22 = (bf16[1184,512]{1,0:T(8,128)(2,1)S(1)}, bf16[1184,512]{1,0:T(8,128)(2,1)S(1)}, u32[]{:S(2)}, u32[]{:S(2)}) collective-permute-start(bf16[1184,512]{1,0:T(8,128)(2,1)S(1)} %bitcast.56), channel_id=1, source_target_pairs={{0,1},{1,0},{2,3},{3,2},{4,5},{5,4},{6,7},{7,6},{8,9},{9,8},{10,11... | collective-permute-start | bytes 3637256 | tf_op jit(solution)/shard_map/ppermute | solution.py:637
  128.1 26.4 %collective-permute-start.27 = (bf16[1024,512]{1,0:T(8,128)(2,1)}, bf16[1024,512]{1,0:T(8,128)(2,1)}, u32[]{:S(2)}, u32[]{:S(2)}) collective-permute-start(bf16[1024,512]{1,0:T(8,128)(2,1)} %all-gather.5.cloned.1.call-done.refs_0_), channel_id=1, source_target_pairs={{0,2},{2,0},{1,3},{3,1},{4,6},{6,4},{5,7},{7,5},{8,10},{10,8},{9,1... | collective-permute-start | bytes 3145736 | tf_op jit(solution)/shard_map/ppermute | solution.py:637
  128.7 29.2 %collective-permute-start.26 = (bf16[1024,512]{1,0:T(8,128)(2,1)}, bf16[1024,512]{1,0:T(8,128)(2,1)}, u32[]{:S(2)}, u32[]{:S(2)}) collective-permute-start(bf16[1024,512]{1,0:T(8,128)(2,1)} %all-gather.5.cloned.1.call-done.refs_0_), channel_id=1, source_target_pairs={{0,16},{16,0},{1,17},{17,1},{2,18},{18,2},{3,19},{19,3},{4,20},{20... | collective-permute-start | bytes 3145736 | tf_op jit(solution)/shard_map/ppermute | solution.py:637
  130.2 46.2 %collective-permute-start.23 = (bf16[1024,512]{1,0:T(8,128)(2,1)}, bf16[1024,512]{1,0:T(8,128)(2,1)}, u32[]{:S(2)}, u32[]{:S(2)}) collective-permute-start(bf16[1024,512]{1,0:T(8,128)(2,1)} %all-gather.3.cloned.1.call-done.refs_0_), channel_id=1, source_target_pairs={{0,2},{2,0},{1,3},{3,1},{4,6},{6,4},{5,7},{7,5},{8,10},{10,8},{9,1... | collective-permute-start | bytes 3145736 | tf_op jit(solution)/shard_map/ppermute | solution.py:637
  131.7 49.2 %collective-permute-start.20 = (bf16[1184,1024]{1,0:T(8,128)(2,1)}, bf16[1184,1024]{1,0:T(8,128)(2,1)}, u32[]{:S(2)}, u32[]{:S(2)}) collective-permute-start(bf16[1184,1024]{1,0:T(8,128)(2,1)} %convolution_convert_fusion.a_ref), channel_id=1, source_target_pairs={{0,1},{1,0},{2,3},{3,2},{4,5},{5,4},{6,7},{7,6},{8,9},{9,8},{10,11... | collective-permute-start | bytes 7274504 | tf_op jit(solution)/shard_map/ppermute | solution.py:637
  154.5 33.1 %collective-permute-start.24 = (bf16[1024,512]{1,0:T(8,128)(2,1)}, bf16[1024,512]{1,0:T(8,128)(2,1)}, u32[]{:S(2)}, u32[]{:S(2)}) collective-permute-start(bf16[1024,512]{1,0:T(8,128)(2,1)} %all-gather.3.cloned.1.call-done.refs_0_), channel_id=1, source_target_pairs={{0,16},{16,0},{1,17},{17,1},{2,18},{18,2},{3,19},{19,3},{4,20},{20... | collective-permute-start | bytes 3145736 | tf_op jit(solution)/shard_map/ppermute | solution.py:637
  157.9 82.2 %collective-permute-start.28 = (bf16[1024,256]{1,0:T(8,128)(2,1)}, bf16[1024,256]{1,0:T(8,128)(2,1)}, u32[]{:S(2)}, u32[]{:S(2)}) collective-permute-start(bf16[1024,256]{1,0:T(8,128)(2,1)} %slice.230), channel_id=1, source_target_pairs={{0,16},{16,0},{1,17},{17,1},{2,18},{18,2},{3,19},{19,3},{4,20},{20... | collective-permute-start | bytes 1572872 | tf_op jit(solution)/shard_map/ppermute | solution.py:637
  176.4 63.7 %collective-permute-start.29 = (bf16[1024,256]{1,0:T(8,128)(2,1)}, bf16[1024,256]{1,0:T(8,128)(2,1)}, u32[]{:S(2)}, u32[]{:S(2)}) collective-permute-start(bf16[1024,256]{1,0:T(8,128)(2,1)} %slice.231), channel_id=1, source_target_pairs={{0,2},{2,0},{1,3},{3,1},{4,6},{6,4},{5,7},{7,5},{8,10},{10,8},{9,1... | collective-permute-start | bytes 1572872 | tf_op jit(solution)/shard_map/ppermute | solution.py:637
  177.0 35.6 %collective-permute-start.25 = (bf16[1024,512]{1,0:T(8,128)(2,1)}, bf16[1024,512]{1,0:T(8,128)(2,1)}, u32[]{:S(2)}, u32[]{:S(2)}) collective-permute-start(bf16[1024,512]{1,0:T(8,128)(2,1)} %collective-permute-done.23.refs_1_), channel_id=1, source_target_pairs={{0,16},{16,0},{1,17},{17,1},{2,18},{18,2},{3,19},{19,3},{4,20},{20... | collective-permute-start | bytes 3145736 | tf_op jit(solution)/shard_map/ppermute | solution.py:637
  259.0 205.0 %reduce-scatter.5.cloned.1.call-start = ((), (), s32[]{:S(2)}) async-start(), calls=%async_computation.5 | async-start | bytes 2293760 | tf_op jit(solution)/shard_map/reduce_scatter | solution.py:768
  266.9 26.3 %collective-permute-start.34 = (bf16[1024,512]{1,0:T(8,128)(2,1)}, bf16[1024,512]{1,0:T(8,128)(2,1)}, u32[]{:S(2)}, u32[]{:S(2)}) collective-permute-start(bf16[1024,512]{1,0:T(8,128)(2,1)} %convolution_convert_fusion.4), channel_id=1, source_target_pairs={{0,16},{16,0},{1,17},{17,1},{2,18},{18,2},{3,19},{19,3},{4,20},{20... | collective-permute-start | bytes 3145736 | tf_op jit(solution)/shard_map/ppermute | solution.py:637
  268.4 25.1 %collective-permute-start.33 = (bf16[1024,512]{1,0:T(8,128)(2,1)}, bf16[1024,512]{1,0:T(8,128)(2,1)}, u32[]{:S(2)}, u32[]{:S(2)}) collective-permute-start(bf16[1024,512]{1,0:T(8,128)(2,1)} %convolution_convert_fusion.5), channel_id=1, source_target_pairs={{0,2},{2,0},{1,3},{3,1},{4,6},{6,4},{5,7},{7,5},{8,10},{10,8},{9,1... | collective-permute-start | bytes 3145736 | tf_op jit(solution)/shard_map/ppermute | solution.py:637
  268.9 45.8 %collective-permute-start.32 = (bf16[1024,512]{1,0:T(8,128)(2,1)}, bf16[1024,512]{1,0:T(8,128)(2,1)}, u32[]{:S(2)}, u32[]{:S(2)}) collective-permute-start(bf16[1024,512]{1,0:T(8,128)(2,1)} %convolution_convert_fusion.6), channel_id=1, source_target_pairs={{0,16},{16,0},{1,17},{17,1},{2,18},{18,2},{3,19},{19,3},{4,20},{20... | collective-permute-start | bytes 3145736 | tf_op jit(solution)/shard_map/ppermute | solution.py:637
  314.7 14.9 %collective-permute-start.36 = (bf16[1024,256]{1,0:T(8,128)(2,1)S(1)}, bf16[1024,256]{1,0:T(8,128)(2,1)}, u32[]{:S(2)}, u32[]{:S(2)}) collective-permute-start(bf16[1024,256]{1,0:T(8,128)(2,1)S(1)} %slice.233), channel_id=1, source_target_pairs={{0,16},{16,0},{1,17},{17,1},{2,18},{18,2},{3,19},{19,3},{4,20},{20... | collective-permute-start | bytes 1572872 | tf_op jit(solution)/shard_map/ppermute | solution.py:637
  320.0 59.3 %collective-permute-start.39 = (bf16[1024,256]{1,0:T(8,128)(2,1)}, bf16[1024,256]{1,0:T(8,128)(2,1)}, u32[]{:S(2)}, u32[]{:S(2)}) collective-permute-start(bf16[1024,256]{1,0:T(8,128)(2,1)} %slice.236), channel_id=1, source_target_pairs={{0,16},{16,0},{1,17},{17,1},{2,18},{18,2},{3,19},{19,3},{4,20},{20... | collective-permute-start | bytes 1572872 | tf_op jit(solution)/shard_map/ppermute | solution.py:637
  324.6 54.7 %collective-permute-start.38 = (bf16[1024,256]{1,0:T(8,128)(2,1)}, bf16[1024,256]{1,0:T(8,128)(2,1)}, u32[]{:S(2)}, u32[]{:S(2)}) collective-permute-start(bf16[1024,256]{1,0:T(8,128)(2,1)} %slice.235), channel_id=1, source_target_pairs={{0,2},{2,0},{1,3},{3,1},{4,6},{6,4},{5,7},{7,5},{8,10},{10,8},{9,1... | collective-permute-start | bytes 1572872 | tf_op jit(solution)/shard_map/ppermute | solution.py:637
  328.0 51.3 %collective-permute-start.40 = (bf16[1024,256]{1,0:T(8,128)(2,1)S(1)}, bf16[1024,256]{1,0:T(8,128)(2,1)S(1)}, u32[]{:S(2)}, u32[]{:S(2)}) collective-permute-start(bf16[1024,256]{1,0:T(8,128)(2,1)S(1)} %slice.237), channel_id=1, source_target_pairs={{0,2},{2,0},{1,3},{3,1},{4,6},{6,4},{5,7},{7,5},{8,10},{10,8},{9,1... | collective-permute-start | bytes 1572872 | tf_op jit(solution)/shard_map/ppermute | solution.py:637
  330.7 25.7 %collective-permute-start.37 = (bf16[256,512]{1,0:T(8,128)(2,1)S(1)}, bf16[256,512]{1,0:T(8,128)(2,1)S(1)}, u32[]{:S(2)}, u32[]{:S(2)}) collective-permute-start(bf16[256,512]{1,0:T(8,128)(2,1)S(1)} %slice.191), channel_id=1, source_target_pairs={{0,2},{2,0},{1,3},{3,1},{4,6},{6,4},{5,7},{7,5},{8,10},{10,8},{9,1... | collective-permute-start | bytes 786440 | tf_op jit(solution)/shard_map/ppermute | solution.py:637
  332.7 46.6 %collective-permute-start.41 = (bf16[1024,128]{1,0:T(8,128)(2,1)S(1)}, bf16[1024,128]{1,0:T(8,128)(2,1)S(1)}, u32[]{:S(2)}, u32[]{:S(2)}) collective-permute-start(bf16[1024,128]{1,0:T(8,128)(2,1)S(1)} %slice.238), channel_id=1, source_target_pairs={{0,2},{2,0},{1,3},{3,1},{4,6},{6,4},{5,7},{7,5},{8,10},{10,8},{9,1... | collective-permute-start | bytes 786440 | tf_op jit(solution)/shard_map/ppermute | solution.py:637
  396.1 28.0 %collective-permute-start.46 = (bf16[1184,1024]{1,0:T(8,128)(2,1)}, bf16[1184,1024]{1,0:T(8,128)(2,1)}, u32[]{:S(2)}, u32[]{:S(2)}) collective-permute-start(bf16[1184,1024]{1,0:T(8,128)(2,1)} %convolution_convert_fusion.1.a_ref), channel_id=1, source_target_pairs={{0,1},{1,0},{2,3},{3,2},{4,5},{5,4},{6,7},{7,6},{8,9},{9,8},{10,11... | collective-permute-start | bytes 7274504 | tf_op jit(solution)/shard_map/ppermute | solution.py:637
  396.7 48.5 %collective-permute-start.35 = (bf16[1184,256]{1,0:T(8,128)(2,1)}, bf16[1184,256]{1,0:T(8,128)(2,1)}, u32[]{:S(2)}, u32[]{:S(2)}) collective-permute-start(bf16[1184,256]{1,0:T(8,128)(2,1)} %get-tuple-element.127), channel_id=1, source_target_pairs={{0,2},{2,0},{1,3},{3,1},{4,6},{6,4},{5,7},{7,5},{8,10},{10,8},{9,1... | collective-permute-start | bytes 1818632 | tf_op jit(solution)/shard_map/ppermute | solution.py:637
  398.2 12.8 %collective-permute-start.57 = (bf16[256,512]{1,0:T(8,128)(2,1)S(1)}, bf16[256,512]{1,0:T(8,128)(2,1)S(1)}, u32[]{:S(2)}, u32[]{:S(2)}) collective-permute-start(bf16[256,512]{1,0:T(8,128)(2,1)S(1)} %add_convert_fusion.7), channel_id=1, source_target_pairs={{0,16},{16,0},{1,17},{17,1},{2,18},{18,2},{3,19},{19,3},{4,20},{20... | collective-permute-start | bytes 786440 | tf_op jit(solution)/shard_map/ppermute | solution.py:637
  399.5 19.1 %collective-permute-start.42 = (bf16[1024,256]{1,0:T(8,128)(2,1)S(1)}, bf16[1024,256]{1,0:T(8,128)(2,1)S(1)}, u32[]{:S(2)}, u32[]{:S(2)}) collective-permute-start(bf16[1024,256]{1,0:T(8,128)(2,1)S(1)} %convolution_convert_fusion.7), channel_id=1, source_target_pairs={{0,16},{16,0},{1,17},{17,1},{2,18},{18,2},{3,19},{19,3},{4,20},{20... | collective-permute-start | bytes 1572872 | tf_op jit(solution)/shard_map/ppermute | solution.py:637
  409.7 29.3 %collective-permute-start.44 = (bf16[1024,384]{1,0:T(8,128)(2,1)}, bf16[1024,384]{1,0:T(8,128)(2,1)}, u32[]{:S(2)}, u32[]{:S(2)}) collective-permute-start(bf16[1024,384]{1,0:T(8,128)(2,1)} %add_convert_fusion.5), channel_id=1, source_target_pairs={{0,16},{16,0},{1,17},{17,1},{2,18},{18,2},{3,19},{19,3},{4,20},{20... | collective-permute-start | bytes 2359304 | tf_op jit(solution)/shard_map/ppermute | solution.py:637
  421.0 17.9 %collective-permute-start.45 = (bf16[1024,384]{1,0:T(8,128)(2,1)}, bf16[1024,384]{1,0:T(8,128)(2,1)}, u32[]{:S(2)}, u32[]{:S(2)}) collective-permute-start(bf16[1024,384]{1,0:T(8,128)(2,1)} %add_convert_fusion.4), channel_id=1, source_target_pairs={{0,2},{2,0},{1,3},{3,1},{4,6},{6,4},{5,7},{7,5},{8,10},{10,8},{9,1... | collective-permute-start | bytes 2359304 | tf_op jit(solution)/shard_map/ppermute | solution.py:637
  441.4 14.2 %collective-permute-start.49 = (bf16[256,384]{1,0:T(8,128)(2,1)S(1)}, bf16[256,384]{1,0:T(8,128)(2,1)S(1)}, u32[]{:S(2)}, u32[]{:S(2)}) collective-permute-start(bf16[256,384]{1,0:T(8,128)(2,1)S(1)} %get-tuple-element.233), channel_id=1, source_target_pairs={{0,8},{4,12},{8,0},{12,4},{1,9},{5,13},{9,1},{13,5},{2,10},{6,14},... | collective-permute-start | bytes 589832 | tf_op jit(solution)/shard_map/ppermute | solution.py:640
  442.4 13.2 %collective-permute-start.50 = (bf16[256,384]{1,0:T(8,128)(2,1)S(1)}, bf16[256,384]{1,0:T(8,128)(2,1)S(1)}, u32[]{:S(2)}, u32[]{:S(2)}) collective-permute-start(bf16[256,384]{1,0:T(8,128)(2,1)S(1)} %get-tuple-element.232), channel_id=1, source_target_pairs={{0,12},{4,0},{8,4},{12,8},{1,13},{5,1},{9,5},{13,9},{2,14},{6,2},{... | collective-permute-start | bytes 589832 | tf_op jit(solution)/shard_map/ppermute | solution.py:640
  445.2 18.5 %collective-permute-start.47 = (bf16[1184,256]{1,0:T(8,128)(2,1)}, bf16[1184,256]{1,0:T(8,128)(2,1)S(1)}, u32[]{:S(2)}, u32[]{:S(2)}) collective-permute-start(bf16[1184,256]{1,0:T(8,128)(2,1)} %get-tuple-element.157), channel_id=1, source_target_pairs={{0,2},{2,0},{1,3},{3,1},{4,6},{6,4},{5,7},{7,5},{8,10},{10,8},{9,1... | collective-permute-start | bytes 1818632 | tf_op jit(solution)/shard_map/ppermute | solution.py:637
  467.2 13.0 %collective-permute-start.56 = (bf16[256,896]{1,0:T(8,128)(2,1)}, bf16[256,896]{1,0:T(8,128)(2,1)}, u32[]{:S(2)}, u32[]{:S(2)}) collective-permute-start(bf16[256,896]{1,0:T(8,128)(2,1)} %reduce-scatter.5.cloned.1.call-done), channel_id=1, source_target_pairs={{0,16},{16,0},{1,17},{17,1},{2,18},{18,2},{3,19},{19,3},{4,20},{20... | collective-permute-start | bytes 1376264 | tf_op jit(solution)/shard_map/ppermute | solution.py:637
  (68 other events, 843.9 us)
Sparse Core Ops, SparseCore 0:
  52.7 25.3 all-gather.4
  79.7 27.3 all-gather.2
  259.1 41.0 reduce-scatter.2
  399.6 36.0 reduce-scatter.4

commit v11 on v10

--- a/solution.py
+++ b/solution.py
@@ -772,7 +772,6 @@
     up_across = mm_tn(wide_two, tiles(pre_b, 2, 4)).astype(BF16)
     down_over = mm_tn(wide_grad, tiles(gate_b, 2, 4)).astype(BF16)
     up_across_got, down_over_got = across(up_across), over(down_over)
-    down_x_got = across(after(down_piece, up_across, down_over)[:, half:])
 
     middle_grad, attn_grad, head_grad, turn_sums, out_mine, out_theirs = turn(
         place,
@@ -788,6 +787,7 @@
     )
     out_all = mm_tn(attn_grad, attended).astype(BF16)
     out_over_got = over(out_all[:, 2 * heads_half :])
+    down_x_got = across(after(down_piece, attn_grad)[:, half:])
     up_over_got, up_across_got, down_over_got, _ = lax.optimization_barrier(
         (up_over_got, up_across_got, down_over_got, out_all)
     )
@@ -802,10 +802,6 @@
     down_b_got = across(down_b[:, quarter:])
     out_got = across(after(out_theirs, down_b))
     dqkv, qkv_sums = attend_back(qkv, probs, after(head_grad, up_a, up_b, out_own, down_x))
-    up_sum = join(
-        up_a, up_a_got, up_b, up_b_got, down_b, down_b_got, out_own, after(out_far_got, dqkv)
-    )
-    up_piece = same_half(scatter(up_sum))
 
     def to_feature_blocks(mine, got, dtype):
         first, second = in_order(mine.astype(dtype), got.astype(dtype), my_x)
@@ -814,26 +810,29 @@
 
     cut = 2 * heads_half
     split = 3 * three + cut
-    dqkv = after(dqkv, up_sum)
     far_oth_qk = mm_tn(wide_one, dqkv[:, 3 * three : split]).astype(BF16)
-    far_oth_v = mm_tn(wide_one, dqkv[:, split:]).astype(BF16)
+    far_oth_v = mm_tn(after(wide_one, far_oth_qk), dqkv[:, split:]).astype(BF16)
     qk_got, v_got = over(far_oth_qk), across(far_oth_v)
+    up_sum = join(
+        up_a, up_a_got, up_b, up_b_got, down_b, down_b_got, out_own, after(out_far_got, far_oth_v)
+    )
+    up_piece = same_half(scatter(up_sum))
     lifted_one = mm_nt(
-        after(dqkv, far_oth_qk, far_oth_v), attn_weights[:, : 4 * three]
+        after(dqkv, far_oth_qk, far_oth_v, up_sum), attn_weights[:, : 4 * three]
     ).astype(BF16)
     lifted_one_other = beside(lifted_one)
 
+    far_own = wide_add(
+        mm_tn(wide_one, dqkv[:, three : 2 * three]),
+        jnp.pad(after(qk_got, lifted_one), ((0, 0), (0, three - cut))),
+    )
+    far_own_got = across(far_own)
     near_oth = wide_add(
         mm_tn(wide_one, dqkv[:, 2 * three : 3 * three]),
-        jnp.pad(after(v_got, lifted_one), ((0, 0), (cut, 0))),
+        jnp.pad(after(v_got, far_own), ((0, 0), (cut, 0))),
     )
     near_oth_got = over(near_oth)
-    far_own = wide_add(
-        mm_tn(wide_one, dqkv[:, three : 2 * three]),
-        jnp.pad(after(qk_got, near_oth), ((0, 0), (0, three - cut))),
-    )
-    far_own_got = across(far_own)
-    near_own = mm_tn(after(wide_one, far_own), dqkv[:, :three])
+    near_own = mm_tn(after(wide_one, near_oth), dqkv[:, :three])
     input_mine, input_theirs, late_mine, late_theirs = last(
         place, wide_input, middle_grad, lifted_one, after(lifted_one_other, near_own), gain_one
     )
@@ -856,7 +855,6 @@
     steps += [("dp", n_dp, 1 << bit) for bit in range(n_dp.bit_length() - 1)]
     for step in steps[:-1]:
         sums = sums + swap(sums, *step)
-        sums = after(sums, up_piece)
     sums = hand_out(sums, swap(sums, *steps[-1]))
     outputs = to_feature_blocks(out_mine, after(out_got, near_sum), BF16)
 

time: 499 us -> 500 us (level)
    ppermute x6, waiting for transfers between devices: 24.9 us -> 17.2 us  [shifted(): lax.ppermute(value, 'row', [(at, (at + shift) % n_row) for at in range(n_...]
  transfers between devices with their start and end apart: 62 -> 62, of which waited for: 26 -> 23; matrix products, arithmetic and copies ran while one was open for 15% -> 16% of each run, Pallas kernels for 21% -> 21%
where the time goes in v11:
time: 500 us; the launch traced here: 494 us
  waiting for transfers between devices  191 us (38%)
  Pallas kernels  126 us (25%)
  starting transfers between devices  61.4 us (12%)
  matrix products  58 us (12%)
  local copies, waits for them, and re-layouts  25.1 us (5%)
  other arithmetic  18.3 us (4%)
  between operations  15 us (3%)
    ppermute x52, waiting for transfers between devices, swap(): return lax.ppermute(value, axis, [(at, at ^ bit) for at in range(size)])  174 us
    ppermute x52, starting transfers between devices, swap(): return lax.ppermute(value, axis, [(at, at ^ bit) for at in range(size)])  49.2 us
    dot_general x13, matrix products, mm_tn(): lax.dot_general(a, b, (((0,), (0,)), ((), ())), preferred_element_type=F32)  45 us
    pallas_call x2, Pallas kernels, mlp(): pl.pallas_call(functools.partial(mlp_kernel, bool(before), split), name='...  35.7 us
    pallas_call x1, Pallas kernels, attend_back(): pl.pallas_call(attend_back_kernel, grid=(pairs, held), name='attend_back'...  22.7 us
    ppermute x6, waiting for transfers between devices, shifted(): lax.ppermute(value, 'row', [(at, (at + shift) % n_row) for at in range(n_...  17.2 us
    pallas_call x2, Pallas kernels, attend(): pl.pallas_call(kernel, grid=(pairs // 2, held), name='attend', in_specs=[...  16.6 us
    pallas_call x1, Pallas kernels, turn(): pl.pallas_call(turn_kernel, name='turn', grid_spec=pltpu.PrefetchScalarGr...  14.2 us
  transfers between devices with their start and end apart: 62, of which 23 were waited for; matrix products, arithmetic and copies ran while one was open for 16% of the time, Pallas kernels for 21%

profile of v11, /device:TPU:0, one launch (start us, length us, event | category | flops | bytes accessed | tf_op | source)
XLA Modules:
  0.0 494.4 jit_solution(10677156055780864377)
XLA Ops:
  9.0 3.0 collective-permute-start
  12.8 3.7 collective-permute-start.1
  16.5 5.3 %collective-permute-done.1.refs_3_ = bf16[256,512]{1,0:T(8,128)(2,1)S(1)} collective-permute-done((bf16[256,512]{1,0:T(8,128)(2,1)S(1)}, bf16[256,512]{1,0:T(8,128)(2,1)S(1)}, u32[]{:S(2)}, u32[]{:S(2)}) %collective-permute-start.1) | collective-permute-done | bytes 262176 | tf_op jit(solution)/shard_map/ppermute | solution.py:640
  21.8 3.6 collective-permute-done
  29.6 2.6 collective-permute-start.7
  37.9 11.9 %collective-permute-done.7.refs_2_ = bf16[256,512]{1,0:T(8,128)(2,1)} collective-permute-done((bf16[256,512]{1,0:T(8,128)(2,1)S(1)}, bf16[256,512]{1,0:T(8,128)(2,1)}, u32[]{:S(2)}, u32[]{:S(2)}) %collective-permute-start.7) | collective-permute-done | bytes 262176 | tf_op jit(solution)/shard_map/ppermute | solution.py:640
  57.4 3.1 collective-permute-done.8.refs_4_
  61.0 7.3 %collective-permute-done.15.refs_11_ = bf16[256,512]{1,0:T(8,128)(2,1)} collective-permute-done((bf16[256,512]{1,0:T(8,128)(2,1)}, bf16[256,512]{1,0:T(8,128)(2,1)}, u32[]{:S(2)}, u32[]{:S(2)}) %collective-permute-start.15) | collective-permute-done | bytes 262176 | tf_op jit(solution)/shard_map/ppermute | solution.py:637
  72.2 4.9 collective-permute-done.16.refs_12_
  83.4 2.7 collective-permute-done.11.refs_7_
  88.3 3.4 collective-permute-done.17.refs_13_
  91.9 10.8 %norm_qkv.1 = (bf16[1184,1024]{1,0:T(8,128)(2,1)}, bf16[1184,1536]{1,0:T(8,128)(2,1)}, bf16[1024,2048]{1,0:T(8,128)(2,1)}) custom-call(s32[4]{0:T(128)} %pad_add_fusion.place_ref, bf16[1184,1024]{1,0:T(8,128)(2,1)} %pad_maximum_fusion.x_ref, f32[6,1,1024]{2,1,0:T(1,128)} %get-tuple-element.95.gain_ref.shift_ref.bias_ref, ...), custom_call_target="tpu_custom_call" | custom-call | flops 3724541952 | bytes 19398656 | tf_op jit(solution)/shard_map/norm_qkv/pallas_call | solution.py:114
  102.7 8.3 %attend.2 = (bf16[1184,512]{1,0:T(8,128)(2,1)}, bf16[2,8,592,592]{3,2,1,0:T(8,128)(2,1)}) custom-call(bf16[1184,1536]{1,0:T(8,128)(2,1)} %get-tuple-element.98.refs_0_.qkv_ref), custom_call_target="tpu_custom_call" | custom-call | flops 8613003264 | bytes 24248320 | tf_op jit(solution)/shard_map/attend/pallas_call | solution.py:160
  111.0 8.3 %attend.3 = (bf16[1184,512]{1,0:T(8,128)(2,1)}, bf16[2,8,592,592]{3,2,1,0:T(8,128)(2,1)}) custom-call(bf16[1184,1536]{1,0:T(8,128)(2,1)} %get-tuple-element.98.refs_0_.qkv_ref, bf16[1184,512]{1,0:T(8,128)(2,1)} %get-tuple-element.99.refs_1_, bf16[2,8,592,592]{3,2,1,0:T(8,128)(2,1)} %get-tuple-element.100.refs_2_), custom_call_target="tpu_custom_call", output_to_operand_aliasing={{0}: (1, {}), {1}: (2, {})} | custom-call | flops 8613003264 | bytes 24248320 | tf_op jit(solution)/shard_map/attend/pallas_call | solution.py:160
  119.3 4.4 convolution_convert_fusion.a_ref
  128.5 22.3 %collective-permute-done.27.refs_2_ = bf16[1024,512]{1,0:T(8,128)(2,1)} collective-permute-done((bf16[1024,512]{1,0:T(8,128)(2,1)}, bf16[1024,512]{1,0:T(8,128)(2,1)}, u32[]{:S(2)}, u32[]{:S(2)}) %collective-permute-start.27) | collective-permute-done | bytes 1048608 | tf_op jit(solution)/shard_map/ppermute | solution.py:637
  155.8 16.8 %collective-permute-done.23.refs_1_ = bf16[1024,512]{1,0:T(8,128)(2,1)} collective-permute-done((bf16[1024,512]{1,0:T(8,128)(2,1)}, bf16[1024,512]{1,0:T(8,128)(2,1)}, u32[]{:S(2)}, u32[]{:S(2)}) %collective-permute-start.23) | collective-permute-done | bytes 1048608 | tf_op jit(solution)/shard_map/ppermute | solution.py:637
  177.6 6.7 %middle.1 = (f32[1184,1024]{1,0:T(8,128)}, bf16[1184,1024]{1,0:T(8,128)(2,1)}) custom-call(bf16[1184,1024]{1,0:T(8,128)(2,1)} %pad_maximum_fusion.x_ref, bf16[1184,1024]{1,0:T(8,128)(2,1)} %convolution_convert_fusion.a_ref, bf16[1184,1024]{1,0:T(8,128)(2,1)} %collective-permute-done.20.b_ref, f32[6,1,1024]{2,1,0:T(1,128)} %get-tuple-element.95.gain_ref.shift_ref.bias_ref, ...), custom_call_target="tpu_custom_call" | custom-call | flops 24248320 | bytes 14548992 | tf_op jit(solution)/shard_map/middle/pallas_call | solution.py:227
  184.4 24.7 %collective-permute-done.25.refs_3_.refs_4_ = bf16[1024,512]{1,0:T(8,128)(2,1)} collective-permute-done((bf16[1024,512]{1,0:T(8,128)(2,1)}, bf16[1024,512]{1,0:T(8,128)(2,1)}, u32[]{:S(2)}, u32[]{:S(2)}) %collective-permute-start.25) | collective-permute-done | bytes 1048608 | tf_op jit(solution)/shard_map/ppermute | solution.py:637
  209.1 17.0 %mlp_first.1 = (bf16[1184,1024]{1,0:T(8,128)(2,1)}, bf16[1184,1024]{1,0:T(8,128)(2,1)}, f32[1,1024]{1,0:T(1,128)}, bf16[1184,1024]{1,0:T(8,128)(2,1)}, bf16[1184,1024]{1,0:T(8,128)(2,1)}) custom-call(s32[4]{0:T(128)} %pad_add_fusion.place_ref, bf16[1184,1024]{1,0:T(8,128)(2,1)} %get-tuple-element.111.n_ref, bf16[1184,1024]{1,0:T(8,128)(2,1)} %pad_maximum_fusion.1.dy_ref, ...), custom_call_target="tpu_custom_call" | custom-call | flops 9932111872 | bytes 24248320 | tf_op jit(solution)/shard_map/mlp_first/pallas_call | solution.py:318
  226.1 6.0 %convolution_convert_fusion.2 = bf16[1024,1024]{1,0:T(8,128)(2,1)} fusion(bf16[1184,1024]{1,0:T(8,128)(2,1)} %get-tuple-element.110, bf16[1184,256]{1,0:T(8,128)(2,1)S(1)} %get-tuple-element.212, bf16[1184,256]{1,0:T(8,128)(2,1)S(1)} %get-tuple-element.244, bf16[1184,256]{1,0:T(8,128)(2,1)S(1)} %get-tuple-element.211, ...), kind=kOutput, calls=%fused_computation.9 | convolution fusion | flops 2493775872 | bytes 6946816 | tf_op jit(solution)/shard_map/dot_general | solution.py:34
  232.1 4.5 convolution_convert_fusion.6
  236.6 18.8 %mlp_second.1 = (bf16[1184,1024]{1,0:T(8,128)(2,1)}, bf16[1184,1024]{1,0:T(8,128)(2,1)}, f32[1,1024]{1,0:T(1,128)}, f32[1184,512]{1,0:T(8,128)}, bf16[1184,512]{1,0:T(8,128)(2,1)}, /*index=5*/bf16[1184,1024]{1,0:T(8,128)(2,1)}) custom-call(s32[4]{0:T(128)} %pad_add_fusion.place_ref, bf16[1184,1024]{1,0:T(8,128)(2,1)} %get-tuple-element.111.n_ref, ...), custom_call_target="tpu_custom_call" | custom-call | flops 9932111872 | bytes 24248320 | tf_op jit(solution)/shard_map/mlp_second/pallas_call | solution.py:318
  257.6 4.7 convolution_convert_fusion.4
  262.3 2.5 convolution_convert_fusion.5
  266.9 14.2 %turn.1 = (f32[1184,1024]{1,0:T(8,128)}, bf16[1184,1024]{1,0:T(8,128)(2,1)}, bf16[1184,512]{1,0:T(8,128)(2,1)}, f32[4,1024]{1,0:T(4,128)}, bf16[1184,256]{1,0:T(8,128)(2,1)}, /*index=5*/bf16[1184,256]{1,0:T(8,128)(2,1)}) custom-call(s32[4]{0:T(128)} %pad_add_fusion.place_ref, f32[1184,1024]{1,0:T(8,128)} %get-tuple-element.103.h_ref, ...), custom_call_target="tpu_custom_call" | custom-call | flops 1241513984 | bytes 24248320 | tf_op jit(solution)/shard_map/turn/pallas_call | solution.py:377
  281.2 3.7 convolution_convert_fusion.3
  285.0 19.0 %collective-permute-done.34 = bf16[1024,512]{1,0:T(8,128)(2,1)} collective-permute-done((bf16[1024,512]{1,0:T(8,128)(2,1)}, bf16[1024,512]{1,0:T(8,128)(2,1)}, u32[]{:S(2)}, u32[]{:S(2)}) %collective-permute-start.34) | collective-permute-done | bytes 1048608 | tf_op jit(solution)/shard_map/ppermute | solution.py:637
  305.7 2.8 add_convert_fusion.2.refs_4_
  308.6 3.2 add_convert_fusion.1.refs_0_
  313.5 2.8 add_convert_fusion.refs_2_
  324.0 25.4 %collective-permute-done.37 = bf16[256,512]{1,0:T(8,128)(2,1)S(1)} collective-permute-done((bf16[256,512]{1,0:T(8,128)(2,1)S(1)}, bf16[256,512]{1,0:T(8,128)(2,1)S(1)}, u32[]{:S(2)}, u32[]{:S(2)}) %collective-permute-start.37) | collective-permute-done | bytes 262176 | tf_op jit(solution)/shard_map/ppermute | solution.py:637
  349.5 22.7 %attend_back.1 = (bf16[1184,1536]{1,0:T(8,128)(2,1)}, f32[1,1536]{1,0:T(1,128)}) custom-call(bf16[1184,1536]{1,0:T(8,128)(2,1)} %get-tuple-element.98.refs_0_.qkv_ref, bf16[2,8,592,592]{3,2,1,0:T(8,128)(2,1)} %get-tuple-element.127.p_ref, bf16[1184,512]{1,0:T(8,128)(2,1)} %get-tuple-element.134.g_ref), custom_call_target="tpu_custom_call" | custom-call | flops 21532508160 | bytes 60620800 | tf_op jit(solution)/shard_map/attend_back/pallas_call | solution.py:202
  372.3 2.9 convolution_convert_fusion.7
  375.2 2.6 convolution_convert_fusion.8
  379.7 4.3 join.1
  383.9 8.5 %convolution_convert_fusion.1.a_ref = bf16[1184,1024]{1,0:T(8,128)(2,1)} fusion(bf16[1184,1536]{1,0:T(8,128)(2,1)} %get-tuple-element.138, bf16[1024,2048]{1,0:T(8,128)(2,1)} %get-tuple-element.102.w_ref), kind=kOutput, calls=%fused_computation.1 | convolution fusion | flops 3725754368 | bytes 9207808 | tf_op jit(solution)/shard_map/dot_general | solution.py:30
  396.6 10.7 %collective-permute-done.39 = bf16[1024,256]{1,0:T(8,128)(2,1)S(1)} collective-permute-done((bf16[1024,256]{1,0:T(8,128)(2,1)S(1)}, bf16[1024,256]{1,0:T(8,128)(2,1)S(1)}, u32[]{:S(2)}, u32[]{:S(2)}) %collective-permute-start.39) | collective-permute-done | bytes 524320 | tf_op jit(solution)/shard_map/ppermute | solution.py:637
  407.3 4.3 add_convert_fusion.5
  412.2 4.4 collective-permute-done.38
  416.6 2.5 add_convert_fusion.4
  419.4 2.5 fusion.8
  423.8 8.9 %last.1 = (f32[1184,256]{1,0:T(8,128)}, bf16[1184,256]{1,0:T(8,128)(2,1)}, f32[2,256]{1,0:T(2,128)}, f32[2,256]{1,0:T(2,128)}) custom-call(s32[4]{0:T(128)} %pad_add_fusion.place_ref, bf16[1184,1024]{1,0:T(8,128)(2,1)} %pad_maximum_fusion.x_ref, f32[1184,1024]{1,0:T(8,128)} %get-tuple-element.146.dh_ref, bf16[1184,1024]{1,0:T(8,128)(2,1)} %convolution_convert_fusion.1.a_ref, ...), custom_call_target="tpu_custom_call" | custom-call | flops 24248320 | bytes 14548992 | tf_op jit(solution)/shard_map/last/pallas_call | solution.py:437
  434.1 3.4 collective-permute-done.44
  439.6 3.2 collective-permute-done.52
  447.5 3.0 collective-permute-start.54
  451.7 9.5 %collective-permute-done.54 = f32[12,256]{1,0:T(8,128)S(1)} collective-permute-done((f32[12,256]{1,0:T(8,128)S(1)}, f32[12,256]{1,0:T(8,128)S(1)}, u32[]{:S(2)}, u32[]{:S(2)}) %collective-permute-start.54) | collective-permute-done | bytes 12320 | tf_op jit(solution)/shard_map/ppermute | solution.py:637
  476.1 5.2 %collective-permute-done.56 = bf16[256,896]{1,0:T(8,128)(2,1)} collective-permute-done((bf16[256,896]{1,0:T(8,128)(2,1)}, bf16[256,896]{1,0:T(8,128)(2,1)}, u32[]{:S(2)}, u32[]{:S(2)}) %collective-permute-start.56) | collective-permute-done | bytes 458784 | tf_op jit(solution)/shard_map/ppermute | solution.py:637
  (295 shorter events, 102.3 us)
Async XLA Ops:
  7.2 117.1 %all-gather.5.cloned.1.call-start = ((), (), s32[]{:S(2)}) async-start(), calls=%async_computation.3 | async-start | bytes 1310720 | tf_op jit(solution)/shard_map/all_gather | solution.py:719
  9.0 16.4 %collective-permute-start = (bf16[1154,256]{1,0:T(8,128)(2,1)S(1)}, bf16[1154,256]{1,0:T(8,128)(2,1)S(1)}, u32[]{:S(2)}, u32[]{:S(2)}) collective-permute-start(bf16[1154,256]{1,0:T(8,128)(2,1)S(1)} %get-tuple-element.220), channel_id=1, source_target_pairs={{0,2},{2,0},{1,3},{3,1},{4,6},{6,4},{5,7},{7,5},{8,10},{10,8},{9,1... | collective-permute-start | bytes 1772552 | tf_op jit(solution)/shard_map/ppermute | solution.py:637
  25.9 29.6 %collective-permute-start.2 = (bf16[1184,512]{1,0:T(8,128)(2,1)S(1)}, bf16[1184,512]{1,0:T(8,128)(2,1)S(1)}, u32[]{:S(2)}, u32[]{:S(2)}) collective-permute-start(bf16[1184,512]{1,0:T(8,128)(2,1)S(1)} %bitcast.55), channel_id=1, source_target_pairs={{0,1},{1,0},{2,3},{3,2},{4,5},{5,4},{6,7},{7,6},{8,9},{9,8},{10,11... | collective-permute-start | bytes 3637256 | tf_op jit(solution)/shard_map/ppermute | solution.py:637
  27.4 24.6 %collective-permute-start.4 = (f32[12,256]{1,0:T(8,128)}, f32[12,256]{1,0:T(8,128)S(1)}, u32[]{:S(2)}, u32[]{:S(2)}) collective-permute-start(f32[12,256]{1,0:T(8,128)} %pack.1.own), channel_id=1, source_target_pairs={{0,1},{1,0},{2,3},{3,2},{4,5},{5,4},{6,7},{7,6},{8,9},{9,8},{10,11... | collective-permute-start | bytes 36872 | tf_op jit(solution)/shard_map/ppermute | solution.py:637
  29.6 20.2 %collective-permute-start.7 = (bf16[256,512]{1,0:T(8,128)(2,1)S(1)}, bf16[256,512]{1,0:T(8,128)(2,1)}, u32[]{:S(2)}, u32[]{:S(2)}) collective-permute-start(bf16[256,512]{1,0:T(8,128)(2,1)S(1)} %pad_maximum_fusion.8.refs_0_), channel_id=1, source_target_pairs={{0,8},{4,12},{8,0},{12,4},{1,9},{5,13},{9,1},{13,5},{2,10},{6,14},... | collective-permute-start | bytes 786440 | tf_op jit(solution)/shard_map/ppermute | solution.py:640
  32.2 19.1 %collective-permute-start.6 = (bf16[256,512]{1,0:T(8,128)(2,1)S(1)}, bf16[256,512]{1,0:T(8,128)(2,1)}, u32[]{:S(2)}, u32[]{:S(2)}) collective-permute-start(bf16[256,512]{1,0:T(8,128)(2,1)S(1)} %pad_maximum_fusion.8.refs_0_), channel_id=1, source_target_pairs={{0,4},{4,8},{8,12},{12,0},{1,5},{5,9},{9,13},{13,1},{2,6},{6,10},{... | collective-permute-start | bytes 786440 | tf_op jit(solution)/shard_map/ppermute | solution.py:640
  37.3 15.2 %collective-permute-start.5 = (f32[12,256]{1,0:T(8,128)S(1)}, f32[12,256]{1,0:T(8,128)S(1)}, u32[]{:S(2)}, u32[]{:S(2)}) collective-permute-start(f32[12,256]{1,0:T(8,128)S(1)} %collective-permute-done.3.far), channel_id=1, source_target_pairs={{0,1},{1,0},{2,3},{3,2},{4,5},{5,4},{6,7},{7,6},{8,9},{9,8},{10,11... | collective-permute-start | bytes 36872 | tf_op jit(solution)/shard_map/ppermute | solution.py:637
  49.8 21.8 %collective-permute-start.12 = (bf16[256,512]{1,0:T(8,128)(2,1)S(1)}, bf16[256,512]{1,0:T(8,128)(2,1)S(1)}, u32[]{:S(2)}, u32[]{:S(2)}) collective-permute-start(bf16[256,512]{1,0:T(8,128)(2,1)S(1)} %pad_maximum_fusion.8.refs_0_), channel_id=1, source_target_pairs={{0,16},{16,0},{1,17},{17,1},{2,18},{18,2},{3,19},{19,3},{4,20},{20... | collective-permute-start | bytes 786440 | tf_op jit(solution)/shard_map/ppermute | solution.py:637
  51.9 75.1 %all-gather.3.cloned.1.call-start = ((), (), s32[]{:S(2)}) async-start(), calls=%async_computation.2 | async-start | bytes 1310720 | tf_op jit(solution)/shard_map/all_gather | solution.py:719
  51.9 27.9 %collective-permute-start.14 = (bf16[256,512]{1,0:T(8,128)(2,1)}, bf16[256,512]{1,0:T(8,128)(2,1)}, u32[]{:S(2)}, u32[]{:S(2)}) collective-permute-start(bf16[256,512]{1,0:T(8,128)(2,1)} %collective-permute-done.7.refs_2_), channel_id=1, source_target_pairs={{0,16},{16,0},{1,17},{17,1},{2,18},{18,2},{3,19},{19,3},{4,20},{20... | collective-permute-start | bytes 786440 | tf_op jit(solution)/shard_map/ppermute | solution.py:637
  52.5 25.3 %collective-permute-start.10 = (bf16[256,512]{1,0:T(8,128)(2,1)}, bf16[256,512]{1,0:T(8,128)(2,1)}, u32[]{:S(2)}, u32[]{:S(2)}) collective-permute-start(bf16[256,512]{1,0:T(8,128)(2,1)} %collective-permute-done.7.refs_2_), channel_id=1, source_target_pairs={{0,2},{2,0},{1,3},{3,1},{4,6},{6,4},{5,7},{7,5},{8,10},{10,8},{9,1... | collective-permute-start | bytes 786440 | tf_op jit(solution)/shard_map/ppermute | solution.py:637
  55.5 12.9 %collective-permute-start.15 = (bf16[256,512]{1,0:T(8,128)(2,1)}, bf16[256,512]{1,0:T(8,128)(2,1)}, u32[]{:S(2)}, u32[]{:S(2)}) collective-permute-start(bf16[256,512]{1,0:T(8,128)(2,1)} %copy-done.36), channel_id=1, source_target_pairs={{0,16},{16,0},{1,17},{17,1},{2,18},{18,2},{3,19},{19,3},{4,20},{20... | collective-permute-start | bytes 786440 | tf_op jit(solution)/shard_map/ppermute | solution.py:637
  60.5 19.1 %collective-permute-start.9 = (bf16[256,512]{1,0:T(8,128)(2,1)}, bf16[256,512]{1,0:T(8,128)(2,1)S(1)}, u32[]{:S(2)}, u32[]{:S(2)}) collective-permute-start(bf16[256,512]{1,0:T(8,128)(2,1)} %collective-permute-done.6.refs_1_), channel_id=1, source_target_pairs={{0,2},{2,0},{1,3},{3,1},{4,6},{6,4},{5,7},{7,5},{8,10},{10,8},{9,1... | collective-permute-start | bytes 786440 | tf_op jit(solution)/shard_map/ppermute | solution.py:637
  79.6 12.1 %collective-permute-start.17 = (bf16[256,512]{1,0:T(8,128)(2,1)S(1)}, bf16[256,512]{1,0:T(8,128)(2,1)}, u32[]{:S(2)}, u32[]{:S(2)}) collective-permute-start(bf16[256,512]{1,0:T(8,128)(2,1)S(1)} %collective-permute-done.9.refs_5_), channel_id=1, source_target_pairs={{0,16},{16,0},{1,17},{17,1},{2,18},{18,2},{3,19},{19,3},{4,20},{20... | collective-permute-start | bytes 786440 | tf_op jit(solution)/shard_map/ppermute | solution.py:637
  79.8 12.0 %collective-permute-start.19 = (bf16[256,512]{1,0:T(8,128)(2,1)}, bf16[256,512]{1,0:T(8,128)(2,1)}, u32[]{:S(2)}, u32[]{:S(2)}) collective-permute-start(bf16[256,512]{1,0:T(8,128)(2,1)} %collective-permute-done.15.refs_11_), channel_id=1, source_target_pairs={{0,2},{2,0},{1,3},{3,1},{4,6},{6,4},{5,7},{7,5},{8,10},{10,8},{9,1... | collective-permute-start | bytes 786440 | tf_op jit(solution)/shard_map/ppermute | solution.py:637
  81.5 238.1 %reduce-scatter.3.cloned.1.call-start = ((), (), s32[]{:S(2)}) async-start(), calls=%async_computation.4 | async-start | bytes 2621440 | tf_op jit(solution)/shard_map/reduce_scatter | solution.py:748
  82.7 41.1 %collective-permute-start.21 = (bf16[1154,256]{1,0:T(8,128)(2,1)S(1)}, bf16[1154,256]{1,0:T(8,128)(2,1)S(1)}, u32[]{:S(2)}, u32[]{:S(2)}) collective-permute-start(bf16[1154,256]{1,0:T(8,128)(2,1)S(1)} %get-tuple-element.104), channel_id=1, source_target_pairs={{0,2},{2,0},{1,3},{3,1},{4,6},{6,4},{5,7},{7,5},{8,10},{10,8},{9,1... | collective-permute-start | bytes 1772552 | tf_op jit(solution)/shard_map/ppermute | solution.py:637
  124.2 49.2 %collective-permute-start.22 = (bf16[1184,512]{1,0:T(8,128)(2,1)S(1)}, bf16[1184,512]{1,0:T(8,128)(2,1)S(1)}, u32[]{:S(2)}, u32[]{:S(2)}) collective-permute-start(bf16[1184,512]{1,0:T(8,128)(2,1)S(1)} %bitcast.56), channel_id=1, source_target_pairs={{0,1},{1,0},{2,3},{3,2},{4,5},{5,4},{6,7},{7,6},{8,9},{9,8},{10,11... | collective-permute-start | bytes 3637256 | tf_op jit(solution)/shard_map/ppermute | solution.py:637
  124.3 26.4 %collective-permute-start.27 = (bf16[1024,512]{1,0:T(8,128)(2,1)}, bf16[1024,512]{1,0:T(8,128)(2,1)}, u32[]{:S(2)}, u32[]{:S(2)}) collective-permute-start(bf16[1024,512]{1,0:T(8,128)(2,1)} %all-gather.5.cloned.1.call-done.refs_0_), channel_id=1, source_target_pairs={{0,2},{2,0},{1,3},{3,1},{4,6},{6,4},{5,7},{7,5},{8,10},{10,8},{9,1... | collective-permute-start | bytes 3145736 | tf_op jit(solution)/shard_map/ppermute | solution.py:637
  125.2 28.7 %collective-permute-start.26 = (bf16[1024,512]{1,0:T(8,128)(2,1)}, bf16[1024,512]{1,0:T(8,128)(2,1)}, u32[]{:S(2)}, u32[]{:S(2)}) collective-permute-start(bf16[1024,512]{1,0:T(8,128)(2,1)} %all-gather.5.cloned.1.call-done.refs_0_), channel_id=1, source_target_pairs={{0,16},{16,0},{1,17},{17,1},{2,18},{18,2},{3,19},{19,3},{4,20},{20... | collective-permute-start | bytes 3145736 | tf_op jit(solution)/shard_map/ppermute | solution.py:637
  127.0 45.7 %collective-permute-start.23 = (bf16[1024,512]{1,0:T(8,128)(2,1)}, bf16[1024,512]{1,0:T(8,128)(2,1)}, u32[]{:S(2)}, u32[]{:S(2)}) collective-permute-start(bf16[1024,512]{1,0:T(8,128)(2,1)} %all-gather.3.cloned.1.call-done.refs_0_), channel_id=1, source_target_pairs={{0,2},{2,0},{1,3},{3,1},{4,6},{6,4},{5,7},{7,5},{8,10},{10,8},{9,1... | collective-permute-start | bytes 3145736 | tf_op jit(solution)/shard_map/ppermute | solution.py:637
  128.5 49.2 %collective-permute-start.20 = (bf16[1184,1024]{1,0:T(8,128)(2,1)}, bf16[1184,1024]{1,0:T(8,128)(2,1)}, u32[]{:S(2)}, u32[]{:S(2)}) collective-permute-start(bf16[1184,1024]{1,0:T(8,128)(2,1)} %convolution_convert_fusion.a_ref), channel_id=1, source_target_pairs={{0,1},{1,0},{2,3},{3,2},{4,5},{5,4},{6,7},{7,6},{8,9},{9,8},{10,11... | collective-permute-start | bytes 7274504 | tf_op jit(solution)/shard_map/ppermute | solution.py:637
  150.7 33.7 %collective-permute-start.24 = (bf16[1024,512]{1,0:T(8,128)(2,1)}, bf16[1024,512]{1,0:T(8,128)(2,1)}, u32[]{:S(2)}, u32[]{:S(2)}) collective-permute-start(bf16[1024,512]{1,0:T(8,128)(2,1)} %all-gather.3.cloned.1.call-done.refs_0_), channel_id=1, source_target_pairs={{0,16},{16,0},{1,17},{17,1},{2,18},{18,2},{3,19},{19,3},{4,20},{20... | collective-permute-start | bytes 3145736 | tf_op jit(solution)/shard_map/ppermute | solution.py:637
  153.9 82.7 %collective-permute-start.28 = (bf16[1024,256]{1,0:T(8,128)(2,1)S(1)}, bf16[1024,256]{1,0:T(8,128)(2,1)}, u32[]{:S(2)}, u32[]{:S(2)}) collective-permute-start(bf16[1024,256]{1,0:T(8,128)(2,1)S(1)} %slice.230), channel_id=1, source_target_pairs={{0,16},{16,0},{1,17},{17,1},{2,18},{18,2},{3,19},{19,3},{4,20},{20... | collective-permute-start | bytes 1572872 | tf_op jit(solution)/shard_map/ppermute | solution.py:637
  172.6 64.0 %collective-permute-start.29 = (bf16[1024,256]{1,0:T(8,128)(2,1)}, bf16[1024,256]{1,0:T(8,128)(2,1)}, u32[]{:S(2)}, u32[]{:S(2)}) collective-permute-start(bf16[1024,256]{1,0:T(8,128)(2,1)} %slice.231), channel_id=1, source_target_pairs={{0,2},{2,0},{1,3},{3,1},{4,6},{6,4},{5,7},{7,5},{8,10},{10,8},{9,1... | collective-permute-start | bytes 1572872 | tf_op jit(solution)/shard_map/ppermute | solution.py:637
  173.4 35.7 %collective-permute-start.25 = (bf16[1024,512]{1,0:T(8,128)(2,1)}, bf16[1024,512]{1,0:T(8,128)(2,1)}, u32[]{:S(2)}, u32[]{:S(2)}) collective-permute-start(bf16[1024,512]{1,0:T(8,128)(2,1)} %collective-permute-done.23.refs_1_), channel_id=1, source_target_pairs={{0,16},{16,0},{1,17},{17,1},{2,18},{18,2},{3,19},{19,3},{4,20},{20... | collective-permute-start | bytes 3145736 | tf_op jit(solution)/shard_map/ppermute | solution.py:637
  255.5 216.7 %reduce-scatter.5.cloned.1.call-start = ((), (), s32[]{:S(2)}) async-start(), calls=%async_computation.5 | async-start | bytes 2293760 | tf_op jit(solution)/shard_map/reduce_scatter | solution.py:768
  255.6 29.5 %collective-permute-start.32 = (bf16[1024,512]{1,0:T(8,128)(2,1)}, bf16[1024,512]{1,0:T(8,128)(2,1)}, u32[]{:S(2)}, u32[]{:S(2)}) collective-permute-start(bf16[1024,512]{1,0:T(8,128)(2,1)} %convolution_convert_fusion.6), channel_id=1, source_target_pairs={{0,16},{16,0},{1,17},{17,1},{2,18},{18,2},{3,19},{19,3},{4,20},{20... | collective-permute-start | bytes 3145736 | tf_op jit(solution)/shard_map/ppermute | solution.py:637
  264.9 39.1 %collective-permute-start.34 = (bf16[1024,512]{1,0:T(8,128)(2,1)}, bf16[1024,512]{1,0:T(8,128)(2,1)}, u32[]{:S(2)}, u32[]{:S(2)}) collective-permute-start(bf16[1024,512]{1,0:T(8,128)(2,1)} %convolution_convert_fusion.4), channel_id=1, source_target_pairs={{0,16},{16,0},{1,17},{17,1},{2,18},{18,2},{3,19},{19,3},{4,20},{20... | collective-permute-start | bytes 3145736 | tf_op jit(solution)/shard_map/ppermute | solution.py:637
  265.0 39.0 %collective-permute-start.33 = (bf16[1024,512]{1,0:T(8,128)(2,1)}, bf16[1024,512]{1,0:T(8,128)(2,1)}, u32[]{:S(2)}, u32[]{:S(2)}) collective-permute-start(bf16[1024,512]{1,0:T(8,128)(2,1)} %convolution_convert_fusion.5), channel_id=1, source_target_pairs={{0,2},{2,0},{1,3},{3,1},{4,6},{6,4},{5,7},{7,5},{8,10},{10,8},{9,1... | collective-permute-start | bytes 3145736 | tf_op jit(solution)/shard_map/ppermute | solution.py:637
  304.0 15.7 %collective-permute-start.36 = (bf16[1024,256]{1,0:T(8,128)(2,1)S(1)}, bf16[1024,256]{1,0:T(8,128)(2,1)S(1)}, u32[]{:S(2)}, u32[]{:S(2)}) collective-permute-start(bf16[1024,256]{1,0:T(8,128)(2,1)S(1)} %slice.233), channel_id=1, source_target_pairs={{0,16},{16,0},{1,17},{17,1},{2,18},{18,2},{3,19},{19,3},{4,20},{20... | collective-permute-start | bytes 1572872 | tf_op jit(solution)/shard_map/ppermute | solution.py:637
  317.3 60.5 %collective-permute-start.41 = (bf16[1024,256]{1,0:T(8,128)(2,1)}, bf16[1024,256]{1,0:T(8,128)(2,1)S(1)}, u32[]{:S(2)}, u32[]{:S(2)}) collective-permute-start(bf16[1024,256]{1,0:T(8,128)(2,1)} %slice.236), channel_id=1, source_target_pairs={{0,16},{16,0},{1,17},{17,1},{2,18},{18,2},{3,19},{19,3},{4,20},{20... | collective-permute-start | bytes 1572872 | tf_op jit(solution)/shard_map/ppermute | solution.py:637
  317.6 60.2 %collective-permute-start.40 = (bf16[1024,256]{1,0:T(8,128)(2,1)}, bf16[1024,256]{1,0:T(8,128)(2,1)S(1)}, u32[]{:S(2)}, u32[]{:S(2)}) collective-permute-start(bf16[1024,256]{1,0:T(8,128)(2,1)} %slice.235), channel_id=1, source_target_pairs={{0,2},{2,0},{1,3},{3,1},{4,6},{6,4},{5,7},{7,5},{8,10},{10,8},{9,1... | collective-permute-start | bytes 1572872 | tf_op jit(solution)/shard_map/ppermute | solution.py:637
  318.1 59.7 %collective-permute-start.42 = (bf16[1024,256]{1,0:T(8,128)(2,1)}, bf16[1024,256]{1,0:T(8,128)(2,1)S(1)}, u32[]{:S(2)}, u32[]{:S(2)}) collective-permute-start(bf16[1024,256]{1,0:T(8,128)(2,1)} %slice.237), channel_id=1, source_target_pairs={{0,2},{2,0},{1,3},{3,1},{4,6},{6,4},{5,7},{7,5},{8,10},{10,8},{9,1... | collective-permute-start | bytes 1572872 | tf_op jit(solution)/shard_map/ppermute | solution.py:637
  320.7 28.8 %collective-permute-start.37 = (bf16[256,512]{1,0:T(8,128)(2,1)S(1)}, bf16[256,512]{1,0:T(8,128)(2,1)S(1)}, u32[]{:S(2)}, u32[]{:S(2)}) collective-permute-start(bf16[256,512]{1,0:T(8,128)(2,1)S(1)} %slice.191), channel_id=1, source_target_pairs={{0,2},{2,0},{1,3},{3,1},{4,6},{6,4},{5,7},{7,5},{8,10},{10,8},{9,1... | collective-permute-start | bytes 786440 | tf_op jit(solution)/shard_map/ppermute | solution.py:637
  322.5 55.3 %collective-permute-start.43 = (bf16[1024,128]{1,0:T(8,128)(2,1)S(1)}, bf16[1024,128]{1,0:T(8,128)(2,1)S(1)}, u32[]{:S(2)}, u32[]{:S(2)}) collective-permute-start(bf16[1024,128]{1,0:T(8,128)(2,1)S(1)} %slice.238), channel_id=1, source_target_pairs={{0,2},{2,0},{1,3},{3,1},{4,6},{6,4},{5,7},{7,5},{8,10},{10,8},{9,1... | collective-permute-start | bytes 786440 | tf_op jit(solution)/shard_map/ppermute | solution.py:637
  392.5 31.3 %collective-permute-start.46 = (bf16[1184,1024]{1,0:T(8,128)(2,1)}, bf16[1184,1024]{1,0:T(8,128)(2,1)}, u32[]{:S(2)}, u32[]{:S(2)}) collective-permute-start(bf16[1184,1024]{1,0:T(8,128)(2,1)} %convolution_convert_fusion.1.a_ref), channel_id=1, source_target_pairs={{0,1},{1,0},{2,3},{3,2},{4,5},{5,4},{6,7},{7,6},{8,9},{9,8},{10,11... | collective-permute-start | bytes 7274504 | tf_op jit(solution)/shard_map/ppermute | solution.py:637
  392.5 14.8 %collective-permute-start.39 = (bf16[1024,256]{1,0:T(8,128)(2,1)S(1)}, bf16[1024,256]{1,0:T(8,128)(2,1)S(1)}, u32[]{:S(2)}, u32[]{:S(2)}) collective-permute-start(bf16[1024,256]{1,0:T(8,128)(2,1)S(1)} %convolution_convert_fusion.7), channel_id=1, source_target_pairs={{0,16},{16,0},{1,17},{17,1},{2,18},{18,2},{3,19},{19,3},{4,20},{20... | collective-permute-start | bytes 1572872 | tf_op jit(solution)/shard_map/ppermute | solution.py:637
  394.2 48.7 %collective-permute-start.35 = (bf16[1184,256]{1,0:T(8,128)(2,1)}, bf16[1184,256]{1,0:T(8,128)(2,1)}, u32[]{:S(2)}, u32[]{:S(2)}) collective-permute-start(bf16[1184,256]{1,0:T(8,128)(2,1)} %get-tuple-element.125), channel_id=1, source_target_pairs={{0,2},{2,0},{1,3},{3,1},{4,6},{6,4},{5,7},{7,5},{8,10},{10,8},{9,1... | collective-permute-start | bytes 1818632 | tf_op jit(solution)/shard_map/ppermute | solution.py:637
  394.7 24.6 %collective-permute-start.57 = (bf16[256,512]{1,0:T(8,128)(2,1)S(1)}, bf16[256,512]{1,0:T(8,128)(2,1)S(1)}, u32[]{:S(2)}, u32[]{:S(2)}) collective-permute-start(bf16[256,512]{1,0:T(8,128)(2,1)S(1)} %add_convert_fusion.7), channel_id=1, source_target_pairs={{0,16},{16,0},{1,17},{17,1},{2,18},{18,2},{3,19},{19,3},{4,20},{20... | collective-permute-start | bytes 786440 | tf_op jit(solution)/shard_map/ppermute | solution.py:637
  395.1 21.5 %collective-permute-start.38 = (bf16[1024,128]{1,0:T(8,128)(2,1)S(1)}, bf16[1024,128]{1,0:T(8,128)(2,1)S(1)}, u32[]{:S(2)}, u32[]{:S(2)}) collective-permute-start(bf16[1024,128]{1,0:T(8,128)(2,1)S(1)} %copy-done.38), channel_id=1, source_target_pairs={{0,2},{2,0},{1,3},{3,1},{4,6},{6,4},{5,7},{7,5},{8,10},{10,8},{9,1... | collective-permute-start | bytes 786440 | tf_op jit(solution)/shard_map/ppermute | solution.py:637
  411.6 22.5 %collective-permute-start.45 = (bf16[1024,384]{1,0:T(8,128)(2,1)}, bf16[1024,384]{1,0:T(8,128)(2,1)S(1)}, u32[]{:S(2)}, u32[]{:S(2)}) collective-permute-start(bf16[1024,384]{1,0:T(8,128)(2,1)} %add_convert_fusion.5), channel_id=1, source_target_pairs={{0,2},{2,0},{1,3},{3,1},{4,6},{6,4},{5,7},{7,5},{8,10},{10,8},{9,1... | collective-permute-start | bytes 2359304 | tf_op jit(solution)/shard_map/ppermute | solution.py:637
  419.0 18.5 %collective-permute-start.44 = (bf16[1024,384]{1,0:T(8,128)(2,1)}, bf16[1024,384]{1,0:T(8,128)(2,1)}, u32[]{:S(2)}, u32[]{:S(2)}) collective-permute-start(bf16[1024,384]{1,0:T(8,128)(2,1)} %add_convert_fusion.4), channel_id=1, source_target_pairs={{0,16},{16,0},{1,17},{17,1},{2,18},{18,2},{3,19},{19,3},{4,20},{20... | collective-permute-start | bytes 2359304 | tf_op jit(solution)/shard_map/ppermute | solution.py:637
  442.9 18.7 %collective-permute-start.48 = (bf16[256,384]{1,0:T(8,128)(2,1)S(1)}, bf16[256,384]{1,0:T(8,128)(2,1)S(1)}, u32[]{:S(2)}, u32[]{:S(2)}) collective-permute-start(bf16[256,384]{1,0:T(8,128)(2,1)S(1)} %get-tuple-element.227), channel_id=1, source_target_pairs={{0,4},{4,8},{8,12},{12,0},{1,5},{5,9},{9,13},{13,1},{2,6},{6,10},{... | collective-permute-start | bytes 589832 | tf_op jit(solution)/shard_map/ppermute | solution.py:640
  445.0 16.7 %collective-permute-start.50 = (bf16[256,384]{1,0:T(8,128)(2,1)S(1)}, bf16[256,384]{1,0:T(8,128)(2,1)S(1)}, u32[]{:S(2)}, u32[]{:S(2)}) collective-permute-start(bf16[256,384]{1,0:T(8,128)(2,1)S(1)} %get-tuple-element.228), channel_id=1, source_target_pairs={{0,12},{4,0},{8,4},{12,8},{1,13},{5,1},{9,5},{13,9},{2,14},{6,2},{... | collective-permute-start | bytes 589832 | tf_op jit(solution)/shard_map/ppermute | solution.py:640
  447.0 14.7 %collective-permute-start.49 = (bf16[256,384]{1,0:T(8,128)(2,1)S(1)}, bf16[256,384]{1,0:T(8,128)(2,1)S(1)}, u32[]{:S(2)}, u32[]{:S(2)}) collective-permute-start(bf16[256,384]{1,0:T(8,128)(2,1)S(1)} %get-tuple-element.229), channel_id=1, source_target_pairs={{0,8},{4,12},{8,0},{12,4},{1,9},{5,13},{9,1},{13,5},{2,10},{6,14},... | collective-permute-start | bytes 589832 | tf_op jit(solution)/shard_map/ppermute | solution.py:640
  447.0 22.7 %collective-permute-start.47 = (bf16[1184,256]{1,0:T(8,128)(2,1)}, bf16[1184,256]{1,0:T(8,128)(2,1)S(1)}, u32[]{:S(2)}, u32[]{:S(2)}) collective-permute-start(bf16[1184,256]{1,0:T(8,128)(2,1)} %get-tuple-element.155), channel_id=1, source_target_pairs={{0,2},{2,0},{1,3},{3,1},{4,6},{6,4},{5,7},{7,5},{8,10},{10,8},{9,1... | collective-permute-start | bytes 1818632 | tf_op jit(solution)/shard_map/ppermute | solution.py:637
  447.5 13.7 %collective-permute-start.54 = (f32[12,256]{1,0:T(8,128)S(1)}, f32[12,256]{1,0:T(8,128)S(1)}, u32[]{:S(2)}, u32[]{:S(2)}) collective-permute-start(f32[12,256]{1,0:T(8,128)S(1)} %add.147), channel_id=1, source_target_pairs={{0,8},{4,12},{8,0},{12,4},{1,9},{5,13},{9,1},{13,5},{2,10},{6,14},... | collective-permute-start | bytes 36872 | tf_op jit(solution)/shard_map/ppermute | solution.py:637
  (68 other events, 852.6 us)
Sparse Core Ops, SparseCore 0:
  52.0 26.6 all-gather.4
  81.6 26.0 all-gather.2
  255.6 41.2 reduce-scatter.2
  396.7 36.9 reduce-scatter.4

commit v12 on v11

--- a/solution.py
+++ b/solution.py
@@ -596,6 +596,63 @@
         name="hand_out",
         out_shape=[one] * 6 + [like((4 * width,), F32)] + [one] * 2,
     )(mine, got)
+
+
+def place_mlp_kernel(swapped, place_ref, mine_ref, other_ref, a_ref, b_ref, up_ref, down_ref, out_ref):
+    half = place_ref[2]
+    width = up_ref.shape[1] // 2
+    quarter = width // 2
+    heads = out_ref.shape[0] // 2
+    for ref, at in ((mine_ref, half), (other_ref, 1 - half)):
+        up_ref[:, pl.ds(pl.multiple_of(at * width, width), width)] = ref[:, :width].astype(F32)
+        down_ref[pl.ds(pl.multiple_of(at * width + quarter, quarter), quarter), :] = (
+            ref[:, width : width + quarter].astype(F32).T
+        )
+        out_ref[pl.ds(pl.multiple_of(at * heads, heads), heads), :] = (
+            ref[:, width + quarter :].astype(F32).T
+        )
+    for part, at in ((0, half), (1, 1 - half)):
+        from_b = 1 - part if swapped else part
+        total = a_ref[:, part * quarter : (part + 1) * quarter].astype(F32)
+        total = total + b_ref[:, from_b * quarter : (from_b + 1) * quarter].astype(F32)
+        down_ref[pl.ds(pl.multiple_of(at * width, width), quarter), :] = total.T
+
+
+def place_mlp(place, mine, other, a, b, swapped):
+    strip, cols = mine.shape
+    quarter = a.shape[1] // 2
+    heads = cols - 3 * quarter
+    return pl.pallas_call(
+        functools.partial(place_mlp_kernel, swapped),
+        name="place_mlp",
+        in_specs=[pl.BlockSpec(memory_space=pltpu.SMEM)]
+        + [pl.BlockSpec(memory_space=pltpu.VMEM)] * 4,
+        out_shape=[
+            like((strip, 4 * quarter), F32),
+            like((4 * quarter, strip), F32),
+            like((2 * heads, strip), F32),
+        ],
+    )(place, mine, other, a, b)
+
+
+def place_qkv_kernel(place_ref, mine_ref, other_ref, *outs):
+    half = place_ref[2]
+    heads = outs[0].shape[1] // 2
+    for ref, at in ((mine_ref, half), (other_ref, 1 - half)):
+        here = pl.ds(pl.multiple_of(at * heads, heads), heads)
+        for w in range(3):
+            outs[w][:, here] = ref[:, heads * w : heads * (w + 1)].astype(F32)
+
+
+def place_qkv(place, mine, other):
+    strip, cols = mine.shape
+    return pl.pallas_call(
+        place_qkv_kernel,
+        name="place_qkv",
+        in_specs=[pl.BlockSpec(memory_space=pltpu.SMEM)]
+        + [pl.BlockSpec(memory_space=pltpu.VMEM)] * 2,
+        out_shape=[like((strip, cols // 3 * 2), F32)] * 3,
+    )(place, mine, other)
 
 
 def local(
@@ -817,22 +874,22 @@
         up_a, up_a_got, up_b, up_b_got, down_b, down_b_got, out_own, after(out_far_got, far_oth_v)
     )
     up_piece = same_half(scatter(up_sum))
+    near_oth = wide_add(
+        mm_tn(wide_one, dqkv[:, 2 * three : 3 * three]),
+        jnp.pad(after(v_got, up_sum), ((0, 0), (cut, 0))),
+    )
+    near_oth_got = over(near_oth)
+    far_own = wide_add(
+        mm_tn(wide_one, dqkv[:, three : 2 * three]),
+        jnp.pad(after(qk_got, near_oth), ((0, 0), (0, three - cut))),
+    )
+    far_own_got = across(far_own)
     lifted_one = mm_nt(
-        after(dqkv, far_oth_qk, far_oth_v, up_sum), attn_weights[:, : 4 * three]
+        after(dqkv, far_own), attn_weights[:, : 4 * three]
     ).astype(BF16)
     lifted_one_other = beside(lifted_one)
 
-    far_own = wide_add(
-        mm_tn(wide_one, dqkv[:, three : 2 * three]),
-        jnp.pad(after(qk_got, lifted_one), ((0, 0), (0, three - cut))),
-    )
-    far_own_got = across(far_own)
-    near_oth = wide_add(
-        mm_tn(wide_one, dqkv[:, 2 * three : 3 * three]),
-        jnp.pad(after(v_got, far_own), ((0, 0), (cut, 0))),
-    )
-    near_oth_got = over(near_oth)
-    near_own = mm_tn(after(wide_one, near_oth), dqkv[:, :three])
+    near_own = mm_tn(after(wide_one, lifted_one), dqkv[:, :three])
     input_mine, input_theirs, late_mine, late_theirs = last(
         place, wide_input, middle_grad, lifted_one, after(lifted_one_other, near_own), gain_one
     )
@@ -866,33 +923,18 @@
     input_grad = to_feature_blocks(input_mine, input_got, F32)
     up_other = over(up_piece)
 
-    down_total = down_x.astype(F32) + jnp.concatenate(
-        [down_y_got[:, quarter:], down_y_got[:, :quarter]], axis=1
-    ).astype(F32)
     if n_dp > 2:
+        down_total = down_x.astype(F32) + jnp.concatenate(
+            [down_y_got[:, quarter:], down_y_got[:, :quarter]], axis=1
+        ).astype(F32)
         groups = [[at + bit for at in range(0, n_dp, 2)] for bit in range(2)]
         down_total = lax.psum(down_total, "dp", axis_index_groups=groups)
-
-    def down_half(first_part, second):
-        return jnp.concatenate([first_part, tiles(second, 2, 3).astype(F32)], axis=1)
-
-    down_first, down_second = in_order(
-        down_half(down_total[:, :quarter], up_piece),
-        down_half(down_total[:, quarter:], up_other),
-        my_half,
-    )
-    down_grad = jnp.concatenate([down_first, down_second], axis=1).T
-
-    def both_halves(mine, other, low, high):
-        first, second = in_order(mine[:, low:high], other[:, low:high], my_half)
-        return jnp.concatenate([first, second], axis=1).astype(F32)
-
-    up_grad = both_halves(up_piece, up_other, 0, half)
-    start = half + quarter
-    out_grad = both_halves(up_piece, up_other, start, start + heads_half).T
-    query_grad, key_grad, value_grad = (
-        both_halves(qkv_piece, qkv_other, heads_half * at, heads_half * (at + 1))
-        for at in range(3)
+        parts = (down_total, jnp.zeros_like(down_total))
+    else:
+        parts = (down_x, down_y_got)
+    up_grad, down_grad, out_grad = place_mlp(place, up_piece, up_other, *parts, n_dp == 2)
+    query_grad, key_grad, value_grad = place_qkv(
+        place, qkv_piece, after(qkv_other, up_grad)
     )
 
     return (

time: 500 us -> 496 us (level)
  Pallas kernels: 126 us -> 131 us
  transfers between devices with their start and end apart: 62 -> 62, of which waited for: 23 -> 23; matrix products, arithmetic and copies ran while one was open for 16% -> 16% of each run, Pallas kernels for 21% -> 22%
where the time goes in v12:
time: 496 us; the launch traced here: 490 us
  waiting for transfers between devices  193 us (39%)
  Pallas kernels  131 us (26%)
  starting transfers between devices  61 us (12%)
  matrix products  56.3 us (11%)
  local copies, waits for them, and re-layouts  20.7 us (4%)
  between operations  14.9 us (3%)
  other arithmetic  13.6 us (3%)
    ppermute x52, waiting for transfers between devices, swap(): return lax.ppermute(value, axis, [(at, at ^ bit) for at in range(size)])  176 us
    ppermute x52, starting transfers between devices, swap(): return lax.ppermute(value, axis, [(at, at ^ bit) for at in range(size)])  49 us
    dot_general x13, matrix products, mm_tn(): lax.dot_general(a, b, (((0,), (0,)), ((), ())), preferred_element_type=F32)  47.6 us
    pallas_call x2, Pallas kernels, mlp(): pl.pallas_call(functools.partial(mlp_kernel, bool(before), split), name='...  35.8 us
    pallas_call x1, Pallas kernels, attend_back(): pl.pallas_call(attend_back_kernel, grid=(pairs, held), name='attend_back'...  22.7 us
    ppermute x6, waiting for transfers between devices, shifted(): lax.ppermute(value, 'row', [(at, (at + shift) % n_row) for at in range(n_...  17.1 us
    pallas_call x2, Pallas kernels, attend(): pl.pallas_call(kernel, grid=(pairs // 2, held), name='attend', in_specs=[...  16.6 us
    pallas_call x1, Pallas kernels, turn(): pl.pallas_call(turn_kernel, name='turn', grid_spec=pltpu.PrefetchScalarGr...  14.2 us
  transfers between devices with their start and end apart: 62, of which 23 were waited for; matrix products, arithmetic and copies ran while one was open for 16% of the time, Pallas kernels for 22%

profile of v12, /device:TPU:0, one launch (start us, length us, event | category | flops | bytes accessed | tf_op | source)
XLA Modules:
  0.0 490.3 jit_solution(6639688421972654488)
XLA Ops:
  9.0 3.0 collective-permute-start
  12.8 3.7 collective-permute-start.1
  16.5 5.3 %collective-permute-done.1.refs_3_ = bf16[256,512]{1,0:T(8,128)(2,1)S(1)} collective-permute-done((bf16[256,512]{1,0:T(8,128)(2,1)S(1)}, bf16[256,512]{1,0:T(8,128)(2,1)S(1)}, u32[]{:S(2)}, u32[]{:S(2)}) %collective-permute-start.1) | collective-permute-done | bytes 262176 | tf_op jit(solution)/shard_map/ppermute | solution.py:697
  21.8 3.6 collective-permute-done
  29.6 2.6 collective-permute-start.7
  38.0 11.8 %collective-permute-done.7.refs_2_ = bf16[256,512]{1,0:T(8,128)(2,1)} collective-permute-done((bf16[256,512]{1,0:T(8,128)(2,1)S(1)}, bf16[256,512]{1,0:T(8,128)(2,1)}, u32[]{:S(2)}, u32[]{:S(2)}) %collective-permute-start.7) | collective-permute-done | bytes 262176 | tf_op jit(solution)/shard_map/ppermute | solution.py:697
  57.4 3.1 collective-permute-done.8.refs_4_
  61.0 7.3 %collective-permute-done.15.refs_11_ = bf16[256,512]{1,0:T(8,128)(2,1)} collective-permute-done((bf16[256,512]{1,0:T(8,128)(2,1)}, bf16[256,512]{1,0:T(8,128)(2,1)}, u32[]{:S(2)}, u32[]{:S(2)}) %collective-permute-start.15) | collective-permute-done | bytes 262176 | tf_op jit(solution)/shard_map/ppermute | solution.py:694
  72.2 4.9 collective-permute-done.16.refs_12_
  83.4 2.7 collective-permute-done.11.refs_7_
  86.1 2.2 collective-permute-done.18.refs_14_
  88.3 3.4 collective-permute-done.17.refs_13_
  91.9 10.9 %norm_qkv.1 = (bf16[1184,1024]{1,0:T(8,128)(2,1)}, bf16[1184,1536]{1,0:T(8,128)(2,1)}, bf16[1024,2048]{1,0:T(8,128)(2,1)}) custom-call(s32[4]{0:T(128)} %pad_add_fusion.place_ref, bf16[1184,1024]{1,0:T(8,128)(2,1)} %pad_maximum_fusion.x_ref, f32[6,1,1024]{2,1,0:T(1,128)} %get-tuple-element.102.gain_ref.shift_ref.bias_ref, ...), custom_call_target="tpu_custom_call" | custom-call | flops 3724541952 | bytes 19398656 | tf_op jit(solution)/shard_map/norm_qkv/pallas_call | solution.py:114
  102.7 8.3 %attend.2 = (bf16[1184,512]{1,0:T(8,128)(2,1)}, bf16[2,8,592,592]{3,2,1,0:T(8,128)(2,1)}) custom-call(bf16[1184,1536]{1,0:T(8,128)(2,1)} %get-tuple-element.105.refs_0_.qkv_ref), custom_call_target="tpu_custom_call" | custom-call | flops 8613003264 | bytes 24248320 | tf_op jit(solution)/shard_map/attend/pallas_call | solution.py:160
  111.0 8.3 %attend.3 = (bf16[1184,512]{1,0:T(8,128)(2,1)}, bf16[2,8,592,592]{3,2,1,0:T(8,128)(2,1)}) custom-call(bf16[1184,1536]{1,0:T(8,128)(2,1)} %get-tuple-element.105.refs_0_.qkv_ref, bf16[1184,512]{1,0:T(8,128)(2,1)} %get-tuple-element.106.refs_1_, bf16[2,8,592,592]{3,2,1,0:T(8,128)(2,1)} %get-tuple-element.107.refs_2_), custom_call_target="tpu_custom_call", output_to_operand_aliasing={{0}: (1, {}), {1}: (2, {})} | custom-call | flops 8613003264 | bytes 24248320 | tf_op jit(solution)/shard_map/attend/pallas_call | solution.py:160
  119.3 4.4 convolution_convert_fusion.a_ref
  128.5 22.2 %collective-permute-done.27.refs_2_ = bf16[1024,512]{1,0:T(8,128)(2,1)} collective-permute-done((bf16[1024,512]{1,0:T(8,128)(2,1)}, bf16[1024,512]{1,0:T(8,128)(2,1)}, u32[]{:S(2)}, u32[]{:S(2)}) %collective-permute-start.27) | collective-permute-done | bytes 1048608 | tf_op jit(solution)/shard_map/ppermute | solution.py:694
  155.8 16.8 %collective-permute-done.23.refs_1_ = bf16[1024,512]{1,0:T(8,128)(2,1)} collective-permute-done((bf16[1024,512]{1,0:T(8,128)(2,1)}, bf16[1024,512]{1,0:T(8,128)(2,1)}, u32[]{:S(2)}, u32[]{:S(2)}) %collective-permute-start.23) | collective-permute-done | bytes 1048608 | tf_op jit(solution)/shard_map/ppermute | solution.py:694
  177.6 6.7 %middle.1 = (f32[1184,1024]{1,0:T(8,128)}, bf16[1184,1024]{1,0:T(8,128)(2,1)}) custom-call(bf16[1184,1024]{1,0:T(8,128)(2,1)} %pad_maximum_fusion.x_ref, bf16[1184,1024]{1,0:T(8,128)(2,1)} %convolution_convert_fusion.a_ref, bf16[1184,1024]{1,0:T(8,128)(2,1)} %collective-permute-done.20.b_ref, f32[6,1,1024]{2,1,0:T(1,128)} %get-tuple-element.102.gain_ref.shift_ref.bias_ref, ...), custom_call_target="tpu_custom_call" | custom-call | flops 24248320 | bytes 14548992 | tf_op jit(solution)/shard_map/middle/pallas_call | solution.py:227
  184.3 24.8 %collective-permute-done.25.refs_3_.refs_4_ = bf16[1024,512]{1,0:T(8,128)(2,1)} collective-permute-done((bf16[1024,512]{1,0:T(8,128)(2,1)}, bf16[1024,512]{1,0:T(8,128)(2,1)}, u32[]{:S(2)}, u32[]{:S(2)}) %collective-permute-start.25) | collective-permute-done | bytes 1048608 | tf_op jit(solution)/shard_map/ppermute | solution.py:694
  209.1 17.0 %mlp_first.1 = (bf16[1184,1024]{1,0:T(8,128)(2,1)}, bf16[1184,1024]{1,0:T(8,128)(2,1)}, f32[1,1024]{1,0:T(1,128)}, bf16[1184,1024]{1,0:T(8,128)(2,1)}, bf16[1184,1024]{1,0:T(8,128)(2,1)}) custom-call(s32[4]{0:T(128)} %pad_add_fusion.place_ref, bf16[1184,1024]{1,0:T(8,128)(2,1)} %get-tuple-element.118.n_ref, bf16[1184,1024]{1,0:T(8,128)(2,1)} %pad_maximum_fusion.1.dy_ref, ...), custom_call_target="tpu_custom_call" | custom-call | flops 9932111872 | bytes 24248320 | tf_op jit(solution)/shard_map/mlp_first/pallas_call | solution.py:318
  226.1 6.0 %convolution_convert_fusion.2 = bf16[1024,1024]{1,0:T(8,128)(2,1)} fusion(bf16[1184,1024]{1,0:T(8,128)(2,1)} %get-tuple-element.117, bf16[1184,256]{1,0:T(8,128)(2,1)S(1)} %get-tuple-element.192, bf16[1184,256]{1,0:T(8,128)(2,1)S(1)} %get-tuple-element.208, bf16[1184,256]{1,0:T(8,128)(2,1)S(1)} %get-tuple-element.191, ...), kind=kOutput, calls=%fused_computation.9 | convolution fusion | flops 2493775872 | bytes 6946816 | tf_op jit(solution)/shard_map/dot_general | solution.py:34
  232.1 4.5 convolution_convert_fusion.6
  236.6 18.8 %mlp_second.1 = (bf16[1184,1024]{1,0:T(8,128)(2,1)}, bf16[1184,1024]{1,0:T(8,128)(2,1)}, f32[1,1024]{1,0:T(1,128)}, f32[1184,512]{1,0:T(8,128)}, bf16[1184,512]{1,0:T(8,128)(2,1)}, /*index=5*/bf16[1184,1024]{1,0:T(8,128)(2,1)}) custom-call(s32[4]{0:T(128)} %pad_add_fusion.place_ref, bf16[1184,1024]{1,0:T(8,128)(2,1)} %get-tuple-element.118.n_ref, ...), custom_call_target="tpu_custom_call" | custom-call | flops 9932111872 | bytes 24248320 | tf_op jit(solution)/shard_map/mlp_second/pallas_call | solution.py:318
  257.6 4.7 convolution_convert_fusion.4
  262.4 2.5 convolution_convert_fusion.5
  267.0 14.2 %turn.1 = (f32[1184,1024]{1,0:T(8,128)}, bf16[1184,1024]{1,0:T(8,128)(2,1)}, bf16[1184,512]{1,0:T(8,128)(2,1)}, f32[4,1024]{1,0:T(4,128)}, bf16[1184,256]{1,0:T(8,128)(2,1)}, /*index=5*/bf16[1184,256]{1,0:T(8,128)(2,1)}) custom-call(s32[4]{0:T(128)} %pad_add_fusion.place_ref, f32[1184,1024]{1,0:T(8,128)} %get-tuple-element.110.h_ref, ...), custom_call_target="tpu_custom_call" | custom-call | flops 1241513984 | bytes 24248320 | tf_op jit(solution)/shard_map/turn/pallas_call | solution.py:377
  281.2 3.7 convolution_convert_fusion.3
  285.1 18.9 %collective-permute-done.34 = bf16[1024,512]{1,0:T(8,128)(2,1)} collective-permute-done((bf16[1024,512]{1,0:T(8,128)(2,1)}, bf16[1024,512]{1,0:T(8,128)(2,1)}, u32[]{:S(2)}, u32[]{:S(2)}) %collective-permute-start.34) | collective-permute-done | bytes 1048608 | tf_op jit(solution)/shard_map/ppermute | solution.py:694
  305.8 2.8 add_convert_fusion.2.refs_4_
  308.6 3.2 add_convert_fusion.1.refs_0_
  313.6 2.8 add_convert_fusion.refs_2_
  324.1 25.4 %collective-permute-done.37 = bf16[256,512]{1,0:T(8,128)(2,1)S(1)} collective-permute-done((bf16[256,512]{1,0:T(8,128)(2,1)S(1)}, bf16[256,512]{1,0:T(8,128)(2,1)S(1)}, u32[]{:S(2)}, u32[]{:S(2)}) %collective-permute-start.37) | collective-permute-done | bytes 262176 | tf_op jit(solution)/shard_map/ppermute | solution.py:694
  350.3 22.7 %attend_back.1 = (bf16[1184,1536]{1,0:T(8,128)(2,1)}, f32[1,1536]{1,0:T(1,128)}) custom-call(bf16[1184,1536]{1,0:T(8,128)(2,1)} %get-tuple-element.105.refs_0_.qkv_ref, bf16[2,8,592,592]{3,2,1,0:T(8,128)(2,1)} %get-tuple-element.134.p_ref, bf16[1184,512]{1,0:T(8,128)(2,1)} %get-tuple-element.141.g_ref), custom_call_target="tpu_custom_call" | custom-call | flops 21532508160 | bytes 60620800 | tf_op jit(solution)/shard_map/attend_back/pallas_call | solution.py:202
  373.0 2.9 convolution_convert_fusion.7
  375.9 2.6 convolution_convert_fusion.8
  382.6 4.3 join.1
  386.9 4.5 add_convert_fusion.5
  391.4 2.4 add_convert_fusion.4
  393.9 4.3 convolution_convert_fusion.1.a_ref
  400.6 4.9 %fusion.8 = f32[1024,384]{1,0:T(8,128)} fusion(bf16[1184,1024]{1,0:T(8,128)(2,1)} %get-tuple-element.148, bf16[1184,1536]{1,0:T(8,128)(2,1)} %get-tuple-element.147), kind=kOutput, calls=%fused_computation.36 | convolution fusion | flops 931135488 | bytes 4907008 | tf_op jit(solution)/shard_map/dot_general | solution.py:34
  405.5 8.9 %last.1 = (f32[1184,256]{1,0:T(8,128)}, bf16[1184,256]{1,0:T(8,128)(2,1)}, f32[2,256]{1,0:T(2,128)}, f32[2,256]{1,0:T(2,128)}) custom-call(s32[4]{0:T(128)} %pad_add_fusion.place_ref, bf16[1184,1024]{1,0:T(8,128)(2,1)} %pad_maximum_fusion.x_ref, f32[1184,1024]{1,0:T(8,128)} %get-tuple-element.153.dh_ref, bf16[1184,1024]{1,0:T(8,128)(2,1)} %copy-done.5, ...), custom_call_target="tpu_custom_call" | custom-call | flops 24248320 | bytes 14548992 | tf_op jit(solution)/shard_map/last/pallas_call | solution.py:437
  415.9 3.0 collective-permute-done.45
  421.9 9.9 %collective-permute-done.54 = f32[12,256]{1,0:T(8,128)S(1)} collective-permute-done((f32[12,256]{1,0:T(8,128)S(1)}, f32[12,256]{1,0:T(8,128)S(1)}, u32[]{:S(2)}, u32[]{:S(2)}) %collective-permute-start.54) | collective-permute-done | bytes 12320 | tf_op jit(solution)/shard_map/ppermute | solution.py:694
  438.0 3.0 collective-permute-start.56
  442.3 11.6 %collective-permute-done.56 = f32[12,256]{1,0:T(8,128)S(1)} collective-permute-done((f32[12,256]{1,0:T(8,128)S(1)}, f32[12,256]{1,0:T(8,128)S(1)}, u32[]{:S(2)}, u32[]{:S(2)}) %collective-permute-start.56) | collective-permute-done | bytes 12320 | tf_op jit(solution)/shard_map/ppermute | solution.py:694
  467.1 11.5 %collective-permute-done.52.other_ref = bf16[256,896]{1,0:T(8,128)(2,1)} collective-permute-done((bf16[256,896]{1,0:T(8,128)(2,1)}, bf16[256,896]{1,0:T(8,128)(2,1)}, u32[]{:S(2)}, u32[]{:S(2)}) %collective-permute-start.52) | collective-permute-done | bytes 458784 | tf_op jit(solution)/shard_map/ppermute | solution.py:694
  478.6 3.0 place_mlp.1
  (281 shorter events, 95.4 us)
Async XLA Ops:
  7.2 117.0 %all-gather.5.cloned.1.call-start = ((), (), s32[]{:S(2)}) async-start(), calls=%async_computation.3 | async-start | bytes 1310720 | tf_op jit(solution)/shard_map/all_gather | solution.py:776
  9.0 16.4 %collective-permute-start = (bf16[1154,256]{1,0:T(8,128)(2,1)S(1)}, bf16[1154,256]{1,0:T(8,128)(2,1)S(1)}, u32[]{:S(2)}, u32[]{:S(2)}) collective-permute-start(bf16[1154,256]{1,0:T(8,128)(2,1)S(1)} %get-tuple-element.200), channel_id=1, source_target_pairs={{0,2},{2,0},{1,3},{3,1},{4,6},{6,4},{5,7},{7,5},{8,10},{10,8},{9,1... | collective-permute-start | bytes 1772552 | tf_op jit(solution)/shard_map/ppermute | solution.py:694
  25.9 29.6 %collective-permute-start.2 = (bf16[1184,512]{1,0:T(8,128)(2,1)S(1)}, bf16[1184,512]{1,0:T(8,128)(2,1)S(1)}, u32[]{:S(2)}, u32[]{:S(2)}) collective-permute-start(bf16[1184,512]{1,0:T(8,128)(2,1)S(1)} %bitcast.51), channel_id=1, source_target_pairs={{0,1},{1,0},{2,3},{3,2},{4,5},{5,4},{6,7},{7,6},{8,9},{9,8},{10,11... | collective-permute-start | bytes 3637256 | tf_op jit(solution)/shard_map/ppermute | solution.py:694
  27.4 24.6 %collective-permute-start.4 = (f32[12,256]{1,0:T(8,128)}, f32[12,256]{1,0:T(8,128)S(1)}, u32[]{:S(2)}, u32[]{:S(2)}) collective-permute-start(f32[12,256]{1,0:T(8,128)} %pack.1.own), channel_id=1, source_target_pairs={{0,1},{1,0},{2,3},{3,2},{4,5},{5,4},{6,7},{7,6},{8,9},{9,8},{10,11... | collective-permute-start | bytes 36872 | tf_op jit(solution)/shard_map/ppermute | solution.py:694
  29.6 20.2 %collective-permute-start.7 = (bf16[256,512]{1,0:T(8,128)(2,1)S(1)}, bf16[256,512]{1,0:T(8,128)(2,1)}, u32[]{:S(2)}, u32[]{:S(2)}) collective-permute-start(bf16[256,512]{1,0:T(8,128)(2,1)S(1)} %pad_maximum_fusion.6.refs_0_), channel_id=1, source_target_pairs={{0,8},{4,12},{8,0},{12,4},{1,9},{5,13},{9,1},{13,5},{2,10},{6,14},... | collective-permute-start | bytes 786440 | tf_op jit(solution)/shard_map/ppermute | solution.py:697
  32.2 19.1 %collective-permute-start.6 = (bf16[256,512]{1,0:T(8,128)(2,1)S(1)}, bf16[256,512]{1,0:T(8,128)(2,1)}, u32[]{:S(2)}, u32[]{:S(2)}) collective-permute-start(bf16[256,512]{1,0:T(8,128)(2,1)S(1)} %pad_maximum_fusion.6.refs_0_), channel_id=1, source_target_pairs={{0,4},{4,8},{8,12},{12,0},{1,5},{5,9},{9,13},{13,1},{2,6},{6,10},{... | collective-permute-start | bytes 786440 | tf_op jit(solution)/shard_map/ppermute | solution.py:697
  37.3 15.2 %collective-permute-start.5 = (f32[12,256]{1,0:T(8,128)S(1)}, f32[12,256]{1,0:T(8,128)S(1)}, u32[]{:S(2)}, u32[]{:S(2)}) collective-permute-start(f32[12,256]{1,0:T(8,128)S(1)} %collective-permute-done.3.far), channel_id=1, source_target_pairs={{0,1},{1,0},{2,3},{3,2},{4,5},{5,4},{6,7},{7,6},{8,9},{9,8},{10,11... | collective-permute-start | bytes 36872 | tf_op jit(solution)/shard_map/ppermute | solution.py:694
  49.8 21.8 %collective-permute-start.12 = (bf16[256,512]{1,0:T(8,128)(2,1)S(1)}, bf16[256,512]{1,0:T(8,128)(2,1)S(1)}, u32[]{:S(2)}, u32[]{:S(2)}) collective-permute-start(bf16[256,512]{1,0:T(8,128)(2,1)S(1)} %pad_maximum_fusion.6.refs_0_), channel_id=1, source_target_pairs={{0,16},{16,0},{1,17},{17,1},{2,18},{18,2},{3,19},{19,3},{4,20},{20... | collective-permute-start | bytes 786440 | tf_op jit(solution)/shard_map/ppermute | solution.py:694
  51.9 75.1 %all-gather.3.cloned.1.call-start = ((), (), s32[]{:S(2)}) async-start(), calls=%async_computation.2 | async-start | bytes 1310720 | tf_op jit(solution)/shard_map/all_gather | solution.py:776
  51.9 27.9 %collective-permute-start.14 = (bf16[256,512]{1,0:T(8,128)(2,1)}, bf16[256,512]{1,0:T(8,128)(2,1)}, u32[]{:S(2)}, u32[]{:S(2)}) collective-permute-start(bf16[256,512]{1,0:T(8,128)(2,1)} %collective-permute-done.7.refs_2_), channel_id=1, source_target_pairs={{0,16},{16,0},{1,17},{17,1},{2,18},{18,2},{3,19},{19,3},{4,20},{20... | collective-permute-start | bytes 786440 | tf_op jit(solution)/shard_map/ppermute | solution.py:694
  52.5 25.3 %collective-permute-start.10 = (bf16[256,512]{1,0:T(8,128)(2,1)}, bf16[256,512]{1,0:T(8,128)(2,1)}, u32[]{:S(2)}, u32[]{:S(2)}) collective-permute-start(bf16[256,512]{1,0:T(8,128)(2,1)} %collective-permute-done.7.refs_2_), channel_id=1, source_target_pairs={{0,2},{2,0},{1,3},{3,1},{4,6},{6,4},{5,7},{7,5},{8,10},{10,8},{9,1... | collective-permute-start | bytes 786440 | tf_op jit(solution)/shard_map/ppermute | solution.py:694
  55.5 12.9 %collective-permute-start.15 = (bf16[256,512]{1,0:T(8,128)(2,1)}, bf16[256,512]{1,0:T(8,128)(2,1)}, u32[]{:S(2)}, u32[]{:S(2)}) collective-permute-start(bf16[256,512]{1,0:T(8,128)(2,1)} %copy-done.38), channel_id=1, source_target_pairs={{0,16},{16,0},{1,17},{17,1},{2,18},{18,2},{3,19},{19,3},{4,20},{20... | collective-permute-start | bytes 786440 | tf_op jit(solution)/shard_map/ppermute | solution.py:694
  60.5 19.1 %collective-permute-start.9 = (bf16[256,512]{1,0:T(8,128)(2,1)}, bf16[256,512]{1,0:T(8,128)(2,1)S(1)}, u32[]{:S(2)}, u32[]{:S(2)}) collective-permute-start(bf16[256,512]{1,0:T(8,128)(2,1)} %collective-permute-done.6.refs_1_), channel_id=1, source_target_pairs={{0,2},{2,0},{1,3},{3,1},{4,6},{6,4},{5,7},{7,5},{8,10},{10,8},{9,1... | collective-permute-start | bytes 786440 | tf_op jit(solution)/shard_map/ppermute | solution.py:694
  71.6 11.1 %collective-permute-start.13 = (bf16[256,512]{1,0:T(8,128)(2,1)}, bf16[256,512]{1,0:T(8,128)(2,1)S(1)}, u32[]{:S(2)}, u32[]{:S(2)}) collective-permute-start(bf16[256,512]{1,0:T(8,128)(2,1)} %collective-permute-done.6.refs_1_), channel_id=1, source_target_pairs={{0,16},{16,0},{1,17},{17,1},{2,18},{18,2},{3,19},{19,3},{4,20},{20... | collective-permute-start | bytes 786440 | tf_op jit(solution)/shard_map/ppermute | solution.py:694
  79.6 12.1 %collective-permute-start.17 = (bf16[256,512]{1,0:T(8,128)(2,1)S(1)}, bf16[256,512]{1,0:T(8,128)(2,1)}, u32[]{:S(2)}, u32[]{:S(2)}) collective-permute-start(bf16[256,512]{1,0:T(8,128)(2,1)S(1)} %collective-permute-done.9.refs_5_), channel_id=1, source_target_pairs={{0,16},{16,0},{1,17},{17,1},{2,18},{18,2},{3,19},{19,3},{4,20},{20... | collective-permute-start | bytes 786440 | tf_op jit(solution)/shard_map/ppermute | solution.py:694
  79.8 12.0 %collective-permute-start.19 = (bf16[256,512]{1,0:T(8,128)(2,1)}, bf16[256,512]{1,0:T(8,128)(2,1)}, u32[]{:S(2)}, u32[]{:S(2)}) collective-permute-start(bf16[256,512]{1,0:T(8,128)(2,1)} %collective-permute-done.15.refs_11_), channel_id=1, source_target_pairs={{0,2},{2,0},{1,3},{3,1},{4,6},{6,4},{5,7},{7,5},{8,10},{10,8},{9,1... | collective-permute-start | bytes 786440 | tf_op jit(solution)/shard_map/ppermute | solution.py:694
  81.5 238.2 %reduce-scatter.3.cloned.1.call-start = ((), (), s32[]{:S(2)}) async-start(), calls=%async_computation.4 | async-start | bytes 2621440 | tf_op jit(solution)/shard_map/reduce_scatter | solution.py:805
  82.7 41.0 %collective-permute-start.21 = (bf16[1154,256]{1,0:T(8,128)(2,1)S(1)}, bf16[1154,256]{1,0:T(8,128)(2,1)S(1)}, u32[]{:S(2)}, u32[]{:S(2)}) collective-permute-start(bf16[1154,256]{1,0:T(8,128)(2,1)S(1)} %get-tuple-element.111), channel_id=1, source_target_pairs={{0,2},{2,0},{1,3},{3,1},{4,6},{6,4},{5,7},{7,5},{8,10},{10,8},{9,1... | collective-permute-start | bytes 1772552 | tf_op jit(solution)/shard_map/ppermute | solution.py:694
  124.1 49.3 %collective-permute-start.22 = (bf16[1184,512]{1,0:T(8,128)(2,1)S(1)}, bf16[1184,512]{1,0:T(8,128)(2,1)S(1)}, u32[]{:S(2)}, u32[]{:S(2)}) collective-permute-start(bf16[1184,512]{1,0:T(8,128)(2,1)S(1)} %bitcast.52), channel_id=1, source_target_pairs={{0,1},{1,0},{2,3},{3,2},{4,5},{5,4},{6,7},{7,6},{8,9},{9,8},{10,11... | collective-permute-start | bytes 3637256 | tf_op jit(solution)/shard_map/ppermute | solution.py:694
  124.3 26.4 %collective-permute-start.27 = (bf16[1024,512]{1,0:T(8,128)(2,1)}, bf16[1024,512]{1,0:T(8,128)(2,1)}, u32[]{:S(2)}, u32[]{:S(2)}) collective-permute-start(bf16[1024,512]{1,0:T(8,128)(2,1)} %all-gather.5.cloned.1.call-done.refs_0_), channel_id=1, source_target_pairs={{0,2},{2,0},{1,3},{3,1},{4,6},{6,4},{5,7},{7,5},{8,10},{10,8},{9,1... | collective-permute-start | bytes 3145736 | tf_op jit(solution)/shard_map/ppermute | solution.py:694
  125.2 28.7 %collective-permute-start.26 = (bf16[1024,512]{1,0:T(8,128)(2,1)}, bf16[1024,512]{1,0:T(8,128)(2,1)}, u32[]{:S(2)}, u32[]{:S(2)}) collective-permute-start(bf16[1024,512]{1,0:T(8,128)(2,1)} %all-gather.5.cloned.1.call-done.refs_0_), channel_id=1, source_target_pairs={{0,16},{16,0},{1,17},{17,1},{2,18},{18,2},{3,19},{19,3},{4,20},{20... | collective-permute-start | bytes 3145736 | tf_op jit(solution)/shard_map/ppermute | solution.py:694
  127.0 45.6 %collective-permute-start.23 = (bf16[1024,512]{1,0:T(8,128)(2,1)}, bf16[1024,512]{1,0:T(8,128)(2,1)}, u32[]{:S(2)}, u32[]{:S(2)}) collective-permute-start(bf16[1024,512]{1,0:T(8,128)(2,1)} %all-gather.3.cloned.1.call-done.refs_0_), channel_id=1, source_target_pairs={{0,2},{2,0},{1,3},{3,1},{4,6},{6,4},{5,7},{7,5},{8,10},{10,8},{9,1... | collective-permute-start | bytes 3145736 | tf_op jit(solution)/shard_map/ppermute | solution.py:694
  128.5 49.2 %collective-permute-start.20 = (bf16[1184,1024]{1,0:T(8,128)(2,1)}, bf16[1184,1024]{1,0:T(8,128)(2,1)}, u32[]{:S(2)}, u32[]{:S(2)}) collective-permute-start(bf16[1184,1024]{1,0:T(8,128)(2,1)} %convolution_convert_fusion.a_ref), channel_id=1, source_target_pairs={{0,1},{1,0},{2,3},{3,2},{4,5},{5,4},{6,7},{7,6},{8,9},{9,8},{10,11... | collective-permute-start | bytes 7274504 | tf_op jit(solution)/shard_map/ppermute | solution.py:694
  150.7 33.7 %collective-permute-start.24 = (bf16[1024,512]{1,0:T(8,128)(2,1)}, bf16[1024,512]{1,0:T(8,128)(2,1)}, u32[]{:S(2)}, u32[]{:S(2)}) collective-permute-start(bf16[1024,512]{1,0:T(8,128)(2,1)} %all-gather.3.cloned.1.call-done.refs_0_), channel_id=1, source_target_pairs={{0,16},{16,0},{1,17},{17,1},{2,18},{18,2},{3,19},{19,3},{4,20},{20... | collective-permute-start | bytes 3145736 | tf_op jit(solution)/shard_map/ppermute | solution.py:694
  153.9 82.7 %collective-permute-start.28 = (bf16[1024,256]{1,0:T(8,128)(2,1)S(1)}, bf16[1024,256]{1,0:T(8,128)(2,1)}, u32[]{:S(2)}, u32[]{:S(2)}) collective-permute-start(bf16[1024,256]{1,0:T(8,128)(2,1)S(1)} %slice.166), channel_id=1, source_target_pairs={{0,16},{16,0},{1,17},{17,1},{2,18},{18,2},{3,19},{19,3},{4,20},{20... | collective-permute-start | bytes 1572872 | tf_op jit(solution)/shard_map/ppermute | solution.py:694
  172.6 64.0 %collective-permute-start.29 = (bf16[1024,256]{1,0:T(8,128)(2,1)}, bf16[1024,256]{1,0:T(8,128)(2,1)}, u32[]{:S(2)}, u32[]{:S(2)}) collective-permute-start(bf16[1024,256]{1,0:T(8,128)(2,1)} %slice.167), channel_id=1, source_target_pairs={{0,2},{2,0},{1,3},{3,1},{4,6},{6,4},{5,7},{7,5},{8,10},{10,8},{9,1... | collective-permute-start | bytes 1572872 | tf_op jit(solution)/shard_map/ppermute | solution.py:694
  173.4 35.7 %collective-permute-start.25 = (bf16[1024,512]{1,0:T(8,128)(2,1)}, bf16[1024,512]{1,0:T(8,128)(2,1)}, u32[]{:S(2)}, u32[]{:S(2)}) collective-permute-start(bf16[1024,512]{1,0:T(8,128)(2,1)} %collective-permute-done.23.refs_1_), channel_id=1, source_target_pairs={{0,16},{16,0},{1,17},{17,1},{2,18},{18,2},{3,19},{19,3},{4,20},{20... | collective-permute-start | bytes 3145736 | tf_op jit(solution)/shard_map/ppermute | solution.py:694
  255.5 206.9 %reduce-scatter.5.cloned.1.call-start = ((), (), s32[]{:S(2)}) async-start(), calls=%async_computation.5 | async-start | bytes 2293760 | tf_op jit(solution)/shard_map/reduce_scatter | solution.py:825
  255.6 29.5 %collective-permute-start.32 = (bf16[1024,512]{1,0:T(8,128)(2,1)}, bf16[1024,512]{1,0:T(8,128)(2,1)}, u32[]{:S(2)}, u32[]{:S(2)}) collective-permute-start(bf16[1024,512]{1,0:T(8,128)(2,1)} %convolution_convert_fusion.6), channel_id=1, source_target_pairs={{0,16},{16,0},{1,17},{17,1},{2,18},{18,2},{3,19},{19,3},{4,20},{20... | collective-permute-start | bytes 3145736 | tf_op jit(solution)/shard_map/ppermute | solution.py:694
  264.9 39.1 %collective-permute-start.34 = (bf16[1024,512]{1,0:T(8,128)(2,1)}, bf16[1024,512]{1,0:T(8,128)(2,1)}, u32[]{:S(2)}, u32[]{:S(2)}) collective-permute-start(bf16[1024,512]{1,0:T(8,128)(2,1)} %convolution_convert_fusion.4), channel_id=1, source_target_pairs={{0,16},{16,0},{1,17},{17,1},{2,18},{18,2},{3,19},{19,3},{4,20},{20... | collective-permute-start | bytes 3145736 | tf_op jit(solution)/shard_map/ppermute | solution.py:694
  265.0 39.0 %collective-permute-start.33 = (bf16[1024,512]{1,0:T(8,128)(2,1)}, bf16[1024,512]{1,0:T(8,128)(2,1)}, u32[]{:S(2)}, u32[]{:S(2)}) collective-permute-start(bf16[1024,512]{1,0:T(8,128)(2,1)} %convolution_convert_fusion.5), channel_id=1, source_target_pairs={{0,2},{2,0},{1,3},{3,1},{4,6},{6,4},{5,7},{7,5},{8,10},{10,8},{9,1... | collective-permute-start | bytes 3145736 | tf_op jit(solution)/shard_map/ppermute | solution.py:694
  304.0 15.6 %collective-permute-start.36 = (bf16[1024,256]{1,0:T(8,128)(2,1)S(1)}, bf16[1024,256]{1,0:T(8,128)(2,1)S(1)}, u32[]{:S(2)}, u32[]{:S(2)}) collective-permute-start(bf16[1024,256]{1,0:T(8,128)(2,1)S(1)} %slice.169), channel_id=1, source_target_pairs={{0,16},{16,0},{1,17},{17,1},{2,18},{18,2},{3,19},{19,3},{4,20},{20... | collective-permute-start | bytes 1572872 | tf_op jit(solution)/shard_map/ppermute | solution.py:694
  317.3 63.4 %collective-permute-start.41 = (bf16[1024,256]{1,0:T(8,128)(2,1)}, bf16[1024,256]{1,0:T(8,128)(2,1)S(1)}, u32[]{:S(2)}, u32[]{:S(2)}) collective-permute-start(bf16[1024,256]{1,0:T(8,128)(2,1)} %slice.172), channel_id=1, source_target_pairs={{0,16},{16,0},{1,17},{17,1},{2,18},{18,2},{3,19},{19,3},{4,20},{20... | collective-permute-start | bytes 1572872 | tf_op jit(solution)/shard_map/ppermute | solution.py:694
  317.6 63.1 %collective-permute-start.40 = (bf16[1024,256]{1,0:T(8,128)(2,1)}, bf16[1024,256]{1,0:T(8,128)(2,1)S(1)}, u32[]{:S(2)}, u32[]{:S(2)}) collective-permute-start(bf16[1024,256]{1,0:T(8,128)(2,1)} %slice.171), channel_id=1, source_target_pairs={{0,2},{2,0},{1,3},{3,1},{4,6},{6,4},{5,7},{7,5},{8,10},{10,8},{9,1... | collective-permute-start | bytes 1572872 | tf_op jit(solution)/shard_map/ppermute | solution.py:694
  318.2 62.6 %collective-permute-start.42 = (bf16[1024,256]{1,0:T(8,128)(2,1)}, bf16[1024,256]{1,0:T(8,128)(2,1)S(1)}, u32[]{:S(2)}, u32[]{:S(2)}) collective-permute-start(bf16[1024,256]{1,0:T(8,128)(2,1)} %slice.173), channel_id=1, source_target_pairs={{0,2},{2,0},{1,3},{3,1},{4,6},{6,4},{5,7},{7,5},{8,10},{10,8},{9,1... | collective-permute-start | bytes 1572872 | tf_op jit(solution)/shard_map/ppermute | solution.py:694
  320.7 28.8 %collective-permute-start.37 = (bf16[256,512]{1,0:T(8,128)(2,1)S(1)}, bf16[256,512]{1,0:T(8,128)(2,1)S(1)}, u32[]{:S(2)}, u32[]{:S(2)}) collective-permute-start(bf16[256,512]{1,0:T(8,128)(2,1)S(1)} %slice.143), channel_id=1, source_target_pairs={{0,2},{2,0},{1,3},{3,1},{4,6},{6,4},{5,7},{7,5},{8,10},{10,8},{9,1... | collective-permute-start | bytes 786440 | tf_op jit(solution)/shard_map/ppermute | solution.py:694
  322.5 56.5 %collective-permute-start.43 = (bf16[1024,128]{1,0:T(8,128)(2,1)S(1)}, bf16[1024,128]{1,0:T(8,128)(2,1)S(1)}, u32[]{:S(2)}, u32[]{:S(2)}) collective-permute-start(bf16[1024,128]{1,0:T(8,128)(2,1)S(1)} %slice.174), channel_id=1, source_target_pairs={{0,2},{2,0},{1,3},{3,1},{4,6},{6,4},{5,7},{7,5},{8,10},{10,8},{9,1... | collective-permute-start | bytes 786440 | tf_op jit(solution)/shard_map/ppermute | solution.py:694
  379.0 12.4 %collective-permute-start.38 = (bf16[1024,256]{1,0:T(8,128)(2,1)S(1)}, bf16[1024,256]{1,0:T(8,128)(2,1)S(1)}, u32[]{:S(2)}, u32[]{:S(2)}) collective-permute-start(bf16[1024,256]{1,0:T(8,128)(2,1)S(1)} %convolution_convert_fusion.7), channel_id=1, source_target_pairs={{0,16},{16,0},{1,17},{17,1},{2,18},{18,2},{3,19},{19,3},{4,20},{20... | collective-permute-start | bytes 1572872 | tf_op jit(solution)/shard_map/ppermute | solution.py:694
  398.2 20.7 %collective-permute-start.45 = (bf16[1024,384]{1,0:T(8,128)(2,1)}, bf16[1024,384]{1,0:T(8,128)(2,1)S(1)}, u32[]{:S(2)}, u32[]{:S(2)}) collective-permute-start(bf16[1024,384]{1,0:T(8,128)(2,1)} %add_convert_fusion.4), channel_id=1, source_target_pairs={{0,2},{2,0},{1,3},{3,1},{4,6},{6,4},{5,7},{7,5},{8,10},{10,8},{9,1... | collective-permute-start | bytes 2359304 | tf_op jit(solution)/shard_map/ppermute | solution.py:694
  399.8 20.0 %collective-permute-start.44 = (bf16[1024,384]{1,0:T(8,128)(2,1)}, bf16[1024,384]{1,0:T(8,128)(2,1)}, u32[]{:S(2)}, u32[]{:S(2)}) collective-permute-start(bf16[1024,384]{1,0:T(8,128)(2,1)} %add_convert_fusion.5), channel_id=1, source_target_pairs={{0,16},{16,0},{1,17},{17,1},{2,18},{18,2},{3,19},{19,3},{4,20},{20... | collective-permute-start | bytes 2359304 | tf_op jit(solution)/shard_map/ppermute | solution.py:694
  400.0 32.7 %collective-permute-start.35 = (bf16[1184,256]{1,0:T(8,128)(2,1)}, bf16[1184,256]{1,0:T(8,128)(2,1)}, u32[]{:S(2)}, u32[]{:S(2)}) collective-permute-start(bf16[1184,256]{1,0:T(8,128)(2,1)} %get-tuple-element.132), channel_id=1, source_target_pairs={{0,2},{2,0},{1,3},{3,1},{4,6},{6,4},{5,7},{7,5},{8,10},{10,8},{9,1... | collective-permute-start | bytes 1818632 | tf_op jit(solution)/shard_map/ppermute | solution.py:694
  432.7 27.0 %collective-permute-start.48 = (bf16[256,384]{1,0:T(8,128)(2,1)}, bf16[256,384]{1,0:T(8,128)(2,1)}, u32[]{:S(2)}, u32[]{:S(2)}) collective-permute-start(bf16[256,384]{1,0:T(8,128)(2,1)} %get-tuple-element.201), channel_id=1, source_target_pairs={{0,4},{4,8},{8,12},{12,0},{1,5},{5,9},{9,13},{13,1},{2,6},{6,10},{... | collective-permute-start | bytes 589832 | tf_op jit(solution)/shard_map/ppermute | solution.py:697
  434.7 25.0 %collective-permute-start.50 = (bf16[256,384]{1,0:T(8,128)(2,1)}, bf16[256,384]{1,0:T(8,128)(2,1)}, u32[]{:S(2)}, u32[]{:S(2)}) collective-permute-start(bf16[256,384]{1,0:T(8,128)(2,1)} %get-tuple-element.202), channel_id=1, source_target_pairs={{0,12},{4,0},{8,4},{12,8},{1,13},{5,1},{9,5},{13,9},{2,14},{6,2},{... | collective-permute-start | bytes 589832 | tf_op jit(solution)/shard_map/ppermute | solution.py:697
  436.5 23.2 %collective-permute-start.49 = (bf16[256,384]{1,0:T(8,128)(2,1)S(1)}, bf16[256,384]{1,0:T(8,128)(2,1)}, u32[]{:S(2)}, u32[]{:S(2)}) collective-permute-start(bf16[256,384]{1,0:T(8,128)(2,1)S(1)} %get-tuple-element.203), channel_id=1, source_target_pairs={{0,8},{4,12},{8,0},{12,4},{1,9},{5,13},{9,1},{13,5},{2,10},{6,14},... | collective-permute-start | bytes 589832 | tf_op jit(solution)/shard_map/ppermute | solution.py:697
  436.5 26.5 %collective-permute-start.47 = (bf16[1184,256]{1,0:T(8,128)(2,1)}, bf16[1184,256]{1,0:T(8,128)(2,1)}, u32[]{:S(2)}, u32[]{:S(2)}) collective-permute-start(bf16[1184,256]{1,0:T(8,128)(2,1)} %get-tuple-element.162), channel_id=1, source_target_pairs={{0,2},{2,0},{1,3},{3,1},{4,6},{6,4},{5,7},{7,5},{8,10},{10,8},{9,1... | collective-permute-start | bytes 1818632 | tf_op jit(solution)/shard_map/ppermute | solution.py:694
  438.0 16.0 %collective-permute-start.56 = (f32[12,256]{1,0:T(8,128)S(1)}, f32[12,256]{1,0:T(8,128)S(1)}, u32[]{:S(2)}, u32[]{:S(2)}) collective-permute-start(f32[12,256]{1,0:T(8,128)S(1)} %add.144), channel_id=1, source_target_pairs={{0,8},{4,12},{8,0},{12,4},{1,9},{5,13},{9,1},{13,5},{2,10},{6,14},... | collective-permute-start | bytes 36872 | tf_op jit(solution)/shard_map/ppermute | solution.py:694
  460.9 20.7 %collective-permute-start.51 = (bf16[256,384]{1,0:T(8,128)(2,1)S(1)}, bf16[256,384]{1,0:T(8,128)(2,1)}, u32[]{:S(2)}, u32[]{:S(2)}) collective-permute-start(bf16[256,384]{1,0:T(8,128)(2,1)S(1)} %add_convert_fusion.8.mine_ref), channel_id=1, source_target_pairs={{0,16},{16,0},{1,17},{17,1},{2,18},{18,2},{3,19},{19,3},{4,20},{20... | collective-permute-start | bytes 589832 | tf_op jit(solution)/shard_map/ppermute | solution.py:694
  462.4 16.2 %collective-permute-start.52 = (bf16[256,896]{1,0:T(8,128)(2,1)}, bf16[256,896]{1,0:T(8,128)(2,1)}, u32[]{:S(2)}, u32[]{:S(2)}) collective-permute-start(bf16[256,896]{1,0:T(8,128)(2,1)} %reduce-scatter.5.cloned.1.call-done.mine_ref), channel_id=1, source_target_pairs={{0,16},{16,0},{1,17},{17,1},{2,18},{18,2},{3,19},{19,3},{4,20},{20... | collective-permute-start | bytes 1376264 | tf_op jit(solution)/shard_map/ppermute | solution.py:694
  (69 other events, 858.4 us)
Sparse Core Ops, SparseCore 0:
  52.0 26.6 all-gather.4
  81.6 26.0 all-gather.2
  255.7 41.2 reduce-scatter.2
  398.4 37.0 reduce-scatter.4

commit v13 on v12

--- a/solution.py
+++ b/solution.py
@@ -912,7 +912,7 @@
     steps += [("dp", n_dp, 1 << bit) for bit in range(n_dp.bit_length() - 1)]
     for step in steps[:-1]:
         sums = sums + swap(sums, *step)
-    sums = hand_out(sums, swap(sums, *steps[-1]))
+    sums_got = swap(sums, *steps[-1])
     outputs = to_feature_blocks(out_mine, after(out_got, near_sum), BF16)
 
     qkv_total = rows_of(near_sum, 0).astype(F32)
@@ -933,8 +933,9 @@
     else:
         parts = (down_x, down_y_got)
     up_grad, down_grad, out_grad = place_mlp(place, up_piece, up_other, *parts, n_dp == 2)
+    sums = hand_out(sums, after(sums_got, up_grad, input_grad))
     query_grad, key_grad, value_grad = place_qkv(
-        place, qkv_piece, after(qkv_other, up_grad)
+        place, qkv_piece, after(qkv_other, up_grad, input_grad)
     )
 
     return (

time: 496 us -> 494 us (level)
  waiting for transfers between devices: 193 us -> 187 us
    ppermute x52, waiting for transfers between devices: 176 us -> 170 us  [swap(): return lax.ppermute(value, axis, [(at, at ^ bit) for at in range(size)])]
  transfers between devices with their start and end apart: 62 -> 62, of which waited for: 23 -> 23; matrix products, arithmetic and copies ran while one was open for 16% -> 16% of each run, Pallas kernels for 22% -> 23%
where the time goes in v13:
time: 494 us; the launch traced here: 488 us
  waiting for transfers between devices  187 us (38%)
  Pallas kernels  131 us (27%)
  starting transfers between devices  64.8 us (13%)
  matrix products  56.3 us (11%)
  local copies, waits for them, and re-layouts  20.8 us (4%)
  between operations  14.9 us (3%)
  other arithmetic  13.5 us (3%)
    ppermute x52, waiting for transfers between devices, swap(): return lax.ppermute(value, axis, [(at, at ^ bit) for at in range(size)])  170 us
    ppermute x52, starting transfers between devices, swap(): return lax.ppermute(value, axis, [(at, at ^ bit) for at in range(size)])  52.8 us
    dot_general x13, matrix products, mm_tn(): lax.dot_general(a, b, (((0,), (0,)), ((), ())), preferred_element_type=F32)  47.6 us
    pallas_call x2, Pallas kernels, mlp(): pl.pallas_call(functools.partial(mlp_kernel, bool(before), split), name='...  35.8 us
    pallas_call x1, Pallas kernels, attend_back(): pl.pallas_call(attend_back_kernel, grid=(pairs, held), name='attend_back'...  22.7 us
    ppermute x6, waiting for transfers between devices, shifted(): lax.ppermute(value, 'row', [(at, (at + shift) % n_row) for at in range(n_...  17.1 us
    pallas_call x2, Pallas kernels, attend(): pl.pallas_call(kernel, grid=(pairs // 2, held), name='attend', in_specs=[...  16.6 us
    pallas_call x1, Pallas kernels, turn(): pl.pallas_call(turn_kernel, name='turn', grid_spec=pltpu.PrefetchScalarGr...  14.2 us
  transfers between devices with their start and end apart: 62, of which 23 were waited for; matrix products, arithmetic and copies ran while one was open for 16% of the time, Pallas kernels for 23%

profile of v13, /device:TPU:0, one launch (start us, length us, event | category | flops | bytes accessed | tf_op | source)
XLA Modules:
  0.0 487.9 jit_solution(15518199530914804141)
XLA Ops:
  9.0 3.0 collective-permute-start
  12.8 3.7 collective-permute-start.1
  16.5 5.3 %collective-permute-done.1.refs_3_ = bf16[256,512]{1,0:T(8,128)(2,1)S(1)} collective-permute-done((bf16[256,512]{1,0:T(8,128)(2,1)S(1)}, bf16[256,512]{1,0:T(8,128)(2,1)S(1)}, u32[]{:S(2)}, u32[]{:S(2)}) %collective-permute-start.1) | collective-permute-done | bytes 262176 | tf_op jit(solution)/shard_map/ppermute | solution.py:697
  21.8 3.6 collective-permute-done
  29.6 2.6 collective-permute-start.7
  38.0 11.8 %collective-permute-done.7.refs_2_ = bf16[256,512]{1,0:T(8,128)(2,1)} collective-permute-done((bf16[256,512]{1,0:T(8,128)(2,1)S(1)}, bf16[256,512]{1,0:T(8,128)(2,1)}, u32[]{:S(2)}, u32[]{:S(2)}) %collective-permute-start.7) | collective-permute-done | bytes 262176 | tf_op jit(solution)/shard_map/ppermute | solution.py:697
  57.4 3.1 collective-permute-done.8.refs_4_
  61.0 7.3 %collective-permute-done.15.refs_11_ = bf16[256,512]{1,0:T(8,128)(2,1)} collective-permute-done((bf16[256,512]{1,0:T(8,128)(2,1)}, bf16[256,512]{1,0:T(8,128)(2,1)}, u32[]{:S(2)}, u32[]{:S(2)}) %collective-permute-start.15) | collective-permute-done | bytes 262176 | tf_op jit(solution)/shard_map/ppermute | solution.py:694
  72.2 4.9 %collective-permute-done.16.refs_12_ = bf16[256,512]{1,0:T(8,128)(2,1)S(1)} collective-permute-done((bf16[256,512]{1,0:T(8,128)(2,1)S(1)}, bf16[256,512]{1,0:T(8,128)(2,1)S(1)}, u32[]{:S(2)}, u32[]{:S(2)}) %collective-permute-start.16) | collective-permute-done | bytes 262176 | tf_op jit(solution)/shard_map/ppermute | solution.py:694
  83.4 2.7 collective-permute-done.11.refs_7_
  88.3 3.4 collective-permute-done.17.refs_13_
  91.9 10.8 %norm_qkv.1 = (bf16[1184,1024]{1,0:T(8,128)(2,1)}, bf16[1184,1536]{1,0:T(8,128)(2,1)}, bf16[1024,2048]{1,0:T(8,128)(2,1)}) custom-call(s32[4]{0:T(128)} %pad_add_fusion.place_ref, bf16[1184,1024]{1,0:T(8,128)(2,1)} %pad_maximum_fusion.x_ref, f32[6,1,1024]{2,1,0:T(1,128)} %get-tuple-element.103.gain_ref.shift_ref.bias_ref, ...), custom_call_target="tpu_custom_call" | custom-call | flops 3724541952 | bytes 19398656 | tf_op jit(solution)/shard_map/norm_qkv/pallas_call | solution.py:114
  102.7 8.3 %attend.2 = (bf16[1184,512]{1,0:T(8,128)(2,1)}, bf16[2,8,592,592]{3,2,1,0:T(8,128)(2,1)}) custom-call(bf16[1184,1536]{1,0:T(8,128)(2,1)} %get-tuple-element.106.refs_0_.qkv_ref), custom_call_target="tpu_custom_call" | custom-call | flops 8613003264 | bytes 24248320 | tf_op jit(solution)/shard_map/attend/pallas_call | solution.py:160
  111.0 8.3 %attend.3 = (bf16[1184,512]{1,0:T(8,128)(2,1)}, bf16[2,8,592,592]{3,2,1,0:T(8,128)(2,1)}) custom-call(bf16[1184,1536]{1,0:T(8,128)(2,1)} %get-tuple-element.106.refs_0_.qkv_ref, bf16[1184,512]{1,0:T(8,128)(2,1)} %get-tuple-element.107.refs_1_, bf16[2,8,592,592]{3,2,1,0:T(8,128)(2,1)} %get-tuple-element.108.refs_2_), custom_call_target="tpu_custom_call", output_to_operand_aliasing={{0}: (1, {}), {1}: (2, {})} | custom-call | flops 8613003264 | bytes 24248320 | tf_op jit(solution)/shard_map/attend/pallas_call | solution.py:160
  119.3 4.4 convolution_convert_fusion.a_ref
  128.5 22.2 %collective-permute-done.27.refs_2_ = bf16[1024,512]{1,0:T(8,128)(2,1)} collective-permute-done((bf16[1024,512]{1,0:T(8,128)(2,1)}, bf16[1024,512]{1,0:T(8,128)(2,1)}, u32[]{:S(2)}, u32[]{:S(2)}) %collective-permute-start.27) | collective-permute-done | bytes 1048608 | tf_op jit(solution)/shard_map/ppermute | solution.py:694
  155.8 16.8 %collective-permute-done.23.refs_1_ = bf16[1024,512]{1,0:T(8,128)(2,1)} collective-permute-done((bf16[1024,512]{1,0:T(8,128)(2,1)}, bf16[1024,512]{1,0:T(8,128)(2,1)}, u32[]{:S(2)}, u32[]{:S(2)}) %collective-permute-start.23) | collective-permute-done | bytes 1048608 | tf_op jit(solution)/shard_map/ppermute | solution.py:694
  177.7 6.8 %middle.1 = (f32[1184,1024]{1,0:T(8,128)}, bf16[1184,1024]{1,0:T(8,128)(2,1)}) custom-call(bf16[1184,1024]{1,0:T(8,128)(2,1)} %pad_maximum_fusion.x_ref, bf16[1184,1024]{1,0:T(8,128)(2,1)} %convolution_convert_fusion.a_ref, bf16[1184,1024]{1,0:T(8,128)(2,1)} %collective-permute-done.20.b_ref, f32[6,1,1024]{2,1,0:T(1,128)} %get-tuple-element.103.gain_ref.shift_ref.bias_ref, ...), custom_call_target="tpu_custom_call" | custom-call | flops 24248320 | bytes 14548992 | tf_op jit(solution)/shard_map/middle/pallas_call | solution.py:227
  184.4 24.7 %collective-permute-done.25.refs_3_.refs_4_ = bf16[1024,512]{1,0:T(8,128)(2,1)} collective-permute-done((bf16[1024,512]{1,0:T(8,128)(2,1)}, bf16[1024,512]{1,0:T(8,128)(2,1)}, u32[]{:S(2)}, u32[]{:S(2)}) %collective-permute-start.25) | collective-permute-done | bytes 1048608 | tf_op jit(solution)/shard_map/ppermute | solution.py:694
  209.1 17.0 %mlp_first.1 = (bf16[1184,1024]{1,0:T(8,128)(2,1)}, bf16[1184,1024]{1,0:T(8,128)(2,1)}, f32[1,1024]{1,0:T(1,128)}, bf16[1184,1024]{1,0:T(8,128)(2,1)}, bf16[1184,1024]{1,0:T(8,128)(2,1)}) custom-call(s32[4]{0:T(128)} %pad_add_fusion.place_ref, bf16[1184,1024]{1,0:T(8,128)(2,1)} %get-tuple-element.119.n_ref, bf16[1184,1024]{1,0:T(8,128)(2,1)} %pad_maximum_fusion.1.dy_ref, ...), custom_call_target="tpu_custom_call" | custom-call | flops 9932111872 | bytes 24248320 | tf_op jit(solution)/shard_map/mlp_first/pallas_call | solution.py:318
  226.1 6.0 %convolution_convert_fusion.2 = bf16[1024,1024]{1,0:T(8,128)(2,1)} fusion(bf16[1184,1024]{1,0:T(8,128)(2,1)} %get-tuple-element.118, bf16[1184,256]{1,0:T(8,128)(2,1)S(1)} %get-tuple-element.194, bf16[1184,256]{1,0:T(8,128)(2,1)S(1)} %get-tuple-element.210, bf16[1184,256]{1,0:T(8,128)(2,1)S(1)} %get-tuple-element.193, ...), kind=kOutput, calls=%fused_computation.9 | convolution fusion | flops 2493775872 | bytes 6946816 | tf_op jit(solution)/shard_map/dot_general | solution.py:34
  232.1 4.5 convolution_convert_fusion.6
  236.6 18.8 %mlp_second.1 = (bf16[1184,1024]{1,0:T(8,128)(2,1)}, bf16[1184,1024]{1,0:T(8,128)(2,1)}, f32[1,1024]{1,0:T(1,128)}, f32[1184,512]{1,0:T(8,128)}, bf16[1184,512]{1,0:T(8,128)(2,1)}, /*index=5*/bf16[1184,1024]{1,0:T(8,128)(2,1)}) custom-call(s32[4]{0:T(128)} %pad_add_fusion.place_ref, bf16[1184,1024]{1,0:T(8,128)(2,1)} %get-tuple-element.119.n_ref, ...), custom_call_target="tpu_custom_call" | custom-call | flops 9932111872 | bytes 24248320 | tf_op jit(solution)/shard_map/mlp_second/pallas_call | solution.py:318
  257.6 4.7 convolution_convert_fusion.4
  262.4 2.5 convolution_convert_fusion.5
  267.0 14.2 %turn.1 = (f32[1184,1024]{1,0:T(8,128)}, bf16[1184,1024]{1,0:T(8,128)(2,1)}, bf16[1184,512]{1,0:T(8,128)(2,1)}, f32[4,1024]{1,0:T(4,128)}, bf16[1184,256]{1,0:T(8,128)(2,1)}, /*index=5*/bf16[1184,256]{1,0:T(8,128)(2,1)}) custom-call(s32[4]{0:T(128)} %pad_add_fusion.place_ref, f32[1184,1024]{1,0:T(8,128)} %get-tuple-element.111.h_ref, ...), custom_call_target="tpu_custom_call" | custom-call | flops 1241513984 | bytes 24248320 | tf_op jit(solution)/shard_map/turn/pallas_call | solution.py:377
  281.2 3.7 convolution_convert_fusion.3
  285.1 18.9 %collective-permute-done.34 = bf16[1024,512]{1,0:T(8,128)(2,1)} collective-permute-done((bf16[1024,512]{1,0:T(8,128)(2,1)}, bf16[1024,512]{1,0:T(8,128)(2,1)}, u32[]{:S(2)}, u32[]{:S(2)}) %collective-permute-start.34) | collective-permute-done | bytes 1048608 | tf_op jit(solution)/shard_map/ppermute | solution.py:694
  305.8 2.8 add_convert_fusion.2.refs_4_
  308.6 3.2 add_convert_fusion.1.refs_0_
  313.6 2.8 add_convert_fusion.refs_2_
  324.0 25.4 %collective-permute-done.37 = bf16[256,512]{1,0:T(8,128)(2,1)S(1)} collective-permute-done((bf16[256,512]{1,0:T(8,128)(2,1)S(1)}, bf16[256,512]{1,0:T(8,128)(2,1)S(1)}, u32[]{:S(2)}, u32[]{:S(2)}) %collective-permute-start.37) | collective-permute-done | bytes 262176 | tf_op jit(solution)/shard_map/ppermute | solution.py:694
  350.2 22.7 %attend_back.1 = (bf16[1184,1536]{1,0:T(8,128)(2,1)}, f32[1,1536]{1,0:T(1,128)}) custom-call(bf16[1184,1536]{1,0:T(8,128)(2,1)} %get-tuple-element.106.refs_0_.qkv_ref, bf16[2,8,592,592]{3,2,1,0:T(8,128)(2,1)} %get-tuple-element.135.p_ref, bf16[1184,512]{1,0:T(8,128)(2,1)} %get-tuple-element.142.g_ref), custom_call_target="tpu_custom_call" | custom-call | flops 21532508160 | bytes 60620800 | tf_op jit(solution)/shard_map/attend_back/pallas_call | solution.py:202
  372.9 2.9 convolution_convert_fusion.7
  375.8 2.6 convolution_convert_fusion.8
  382.5 4.3 join.1
  386.8 4.5 add_convert_fusion.5
  391.3 2.4 add_convert_fusion.4
  393.8 4.3 convolution_convert_fusion.1.a_ref
  400.5 5.0 %fusion.8 = f32[1024,384]{1,0:T(8,128)} fusion(bf16[1184,1024]{1,0:T(8,128)(2,1)} %get-tuple-element.149, bf16[1184,1536]{1,0:T(8,128)(2,1)} %get-tuple-element.148), kind=kOutput, calls=%fused_computation.36 | convolution fusion | flops 931135488 | bytes 4907008 | tf_op jit(solution)/shard_map/dot_general | solution.py:34
  405.5 9.0 %last.1 = (f32[1184,256]{1,0:T(8,128)}, bf16[1184,256]{1,0:T(8,128)(2,1)}, f32[2,256]{1,0:T(2,128)}, f32[2,256]{1,0:T(2,128)}) custom-call(s32[4]{0:T(128)} %pad_add_fusion.place_ref, bf16[1184,1024]{1,0:T(8,128)(2,1)} %pad_maximum_fusion.x_ref, f32[1184,1024]{1,0:T(8,128)} %get-tuple-element.154.dh_ref, bf16[1184,1024]{1,0:T(8,128)(2,1)} %copy-done.4, ...), custom_call_target="tpu_custom_call" | custom-call | flops 24248320 | bytes 14548992 | tf_op jit(solution)/shard_map/last/pallas_call | solution.py:437
  415.9 2.9 collective-permute-done.45
  422.6 9.0 %collective-permute-done.35 = bf16[1184,256]{1,0:T(8,128)(2,1)} collective-permute-done((bf16[1184,256]{1,0:T(8,128)(2,1)}, bf16[1184,256]{1,0:T(8,128)(2,1)}, u32[]{:S(2)}, u32[]{:S(2)}) %collective-permute-start.35) | collective-permute-done | bytes 606240 | tf_op jit(solution)/shard_map/ppermute | solution.py:694
  431.6 3.8 collective-permute-start.50
  438.8 5.9 %collective-permute-done.55 = f32[12,256]{1,0:T(8,128)S(1)} collective-permute-done((f32[12,256]{1,0:T(8,128)S(1)}, f32[12,256]{1,0:T(8,128)S(1)}, u32[]{:S(2)}, u32[]{:S(2)}) %collective-permute-start.55) | collective-permute-done | bytes 12320 | tf_op jit(solution)/shard_map/ppermute | solution.py:694
  444.7 4.6 collective-permute-start.56
  461.1 13.2 %collective-permute-done.52.other_ref = bf16[256,896]{1,0:T(8,128)(2,1)} collective-permute-done((bf16[256,896]{1,0:T(8,128)(2,1)}, bf16[256,896]{1,0:T(8,128)(2,1)}, u32[]{:S(2)}, u32[]{:S(2)}) %collective-permute-start.52) | collective-permute-done | bytes 458784 | tf_op jit(solution)/shard_map/ppermute | solution.py:694
  474.3 3.0 place_mlp.1
  (283 shorter events, 94.8 us)
Async XLA Ops:
  7.2 117.0 %all-gather.5.cloned.1.call-start = ((), (), s32[]{:S(2)}) async-start(), calls=%async_computation.3 | async-start | bytes 1310720 | tf_op jit(solution)/shard_map/all_gather | solution.py:776
  9.0 16.4 %collective-permute-start = (bf16[1154,256]{1,0:T(8,128)(2,1)S(1)}, bf16[1154,256]{1,0:T(8,128)(2,1)S(1)}, u32[]{:S(2)}, u32[]{:S(2)}) collective-permute-start(bf16[1154,256]{1,0:T(8,128)(2,1)S(1)} %get-tuple-element.202), channel_id=1, source_target_pairs={{0,2},{2,0},{1,3},{3,1},{4,6},{6,4},{5,7},{7,5},{8,10},{10,8},{9,1... | collective-permute-start | bytes 1772552 | tf_op jit(solution)/shard_map/ppermute | solution.py:694
  25.9 29.6 %collective-permute-start.2 = (bf16[1184,512]{1,0:T(8,128)(2,1)S(1)}, bf16[1184,512]{1,0:T(8,128)(2,1)S(1)}, u32[]{:S(2)}, u32[]{:S(2)}) collective-permute-start(bf16[1184,512]{1,0:T(8,128)(2,1)S(1)} %bitcast.51), channel_id=1, source_target_pairs={{0,1},{1,0},{2,3},{3,2},{4,5},{5,4},{6,7},{7,6},{8,9},{9,8},{10,11... | collective-permute-start | bytes 3637256 | tf_op jit(solution)/shard_map/ppermute | solution.py:694
  27.4 24.6 %collective-permute-start.4 = (f32[12,256]{1,0:T(8,128)}, f32[12,256]{1,0:T(8,128)S(1)}, u32[]{:S(2)}, u32[]{:S(2)}) collective-permute-start(f32[12,256]{1,0:T(8,128)} %pack.1.own), channel_id=1, source_target_pairs={{0,1},{1,0},{2,3},{3,2},{4,5},{5,4},{6,7},{7,6},{8,9},{9,8},{10,11... | collective-permute-start | bytes 36872 | tf_op jit(solution)/shard_map/ppermute | solution.py:694
  29.6 20.2 %collective-permute-start.7 = (bf16[256,512]{1,0:T(8,128)(2,1)S(1)}, bf16[256,512]{1,0:T(8,128)(2,1)}, u32[]{:S(2)}, u32[]{:S(2)}) collective-permute-start(bf16[256,512]{1,0:T(8,128)(2,1)S(1)} %pad_maximum_fusion.6.refs_0_), channel_id=1, source_target_pairs={{0,8},{4,12},{8,0},{12,4},{1,9},{5,13},{9,1},{13,5},{2,10},{6,14},... | collective-permute-start | bytes 786440 | tf_op jit(solution)/shard_map/ppermute | solution.py:697
  32.2 19.1 %collective-permute-start.6 = (bf16[256,512]{1,0:T(8,128)(2,1)S(1)}, bf16[256,512]{1,0:T(8,128)(2,1)}, u32[]{:S(2)}, u32[]{:S(2)}) collective-permute-start(bf16[256,512]{1,0:T(8,128)(2,1)S(1)} %pad_maximum_fusion.6.refs_0_), channel_id=1, source_target_pairs={{0,4},{4,8},{8,12},{12,0},{1,5},{5,9},{9,13},{13,1},{2,6},{6,10},{... | collective-permute-start | bytes 786440 | tf_op jit(solution)/shard_map/ppermute | solution.py:697
  37.3 15.2 %collective-permute-start.5 = (f32[12,256]{1,0:T(8,128)S(1)}, f32[12,256]{1,0:T(8,128)S(1)}, u32[]{:S(2)}, u32[]{:S(2)}) collective-permute-start(f32[12,256]{1,0:T(8,128)S(1)} %collective-permute-done.3.far), channel_id=1, source_target_pairs={{0,1},{1,0},{2,3},{3,2},{4,5},{5,4},{6,7},{7,6},{8,9},{9,8},{10,11... | collective-permute-start | bytes 36872 | tf_op jit(solution)/shard_map/ppermute | solution.py:694
  49.8 21.8 %collective-permute-start.12 = (bf16[256,512]{1,0:T(8,128)(2,1)S(1)}, bf16[256,512]{1,0:T(8,128)(2,1)S(1)}, u32[]{:S(2)}, u32[]{:S(2)}) collective-permute-start(bf16[256,512]{1,0:T(8,128)(2,1)S(1)} %pad_maximum_fusion.6.refs_0_), channel_id=1, source_target_pairs={{0,16},{16,0},{1,17},{17,1},{2,18},{18,2},{3,19},{19,3},{4,20},{20... | collective-permute-start | bytes 786440 | tf_op jit(solution)/shard_map/ppermute | solution.py:694
  51.9 75.1 %all-gather.3.cloned.1.call-start = ((), (), s32[]{:S(2)}) async-start(), calls=%async_computation.2 | async-start | bytes 1310720 | tf_op jit(solution)/shard_map/all_gather | solution.py:776
  51.9 27.9 %collective-permute-start.14 = (bf16[256,512]{1,0:T(8,128)(2,1)}, bf16[256,512]{1,0:T(8,128)(2,1)}, u32[]{:S(2)}, u32[]{:S(2)}) collective-permute-start(bf16[256,512]{1,0:T(8,128)(2,1)} %collective-permute-done.7.refs_2_), channel_id=1, source_target_pairs={{0,16},{16,0},{1,17},{17,1},{2,18},{18,2},{3,19},{19,3},{4,20},{20... | collective-permute-start | bytes 786440 | tf_op jit(solution)/shard_map/ppermute | solution.py:694
  52.5 25.3 %collective-permute-start.10 = (bf16[256,512]{1,0:T(8,128)(2,1)}, bf16[256,512]{1,0:T(8,128)(2,1)}, u32[]{:S(2)}, u32[]{:S(2)}) collective-permute-start(bf16[256,512]{1,0:T(8,128)(2,1)} %collective-permute-done.7.refs_2_), channel_id=1, source_target_pairs={{0,2},{2,0},{1,3},{3,1},{4,6},{6,4},{5,7},{7,5},{8,10},{10,8},{9,1... | collective-permute-start | bytes 786440 | tf_op jit(solution)/shard_map/ppermute | solution.py:694
  55.5 12.9 %collective-permute-start.15 = (bf16[256,512]{1,0:T(8,128)(2,1)}, bf16[256,512]{1,0:T(8,128)(2,1)}, u32[]{:S(2)}, u32[]{:S(2)}) collective-permute-start(bf16[256,512]{1,0:T(8,128)(2,1)} %copy-done.39), channel_id=1, source_target_pairs={{0,16},{16,0},{1,17},{17,1},{2,18},{18,2},{3,19},{19,3},{4,20},{20... | collective-permute-start | bytes 786440 | tf_op jit(solution)/shard_map/ppermute | solution.py:694
  60.5 19.1 %collective-permute-start.9 = (bf16[256,512]{1,0:T(8,128)(2,1)}, bf16[256,512]{1,0:T(8,128)(2,1)S(1)}, u32[]{:S(2)}, u32[]{:S(2)}) collective-permute-start(bf16[256,512]{1,0:T(8,128)(2,1)} %collective-permute-done.6.refs_1_), channel_id=1, source_target_pairs={{0,2},{2,0},{1,3},{3,1},{4,6},{6,4},{5,7},{7,5},{8,10},{10,8},{9,1... | collective-permute-start | bytes 786440 | tf_op jit(solution)/shard_map/ppermute | solution.py:694
  79.6 12.1 %collective-permute-start.17 = (bf16[256,512]{1,0:T(8,128)(2,1)S(1)}, bf16[256,512]{1,0:T(8,128)(2,1)}, u32[]{:S(2)}, u32[]{:S(2)}) collective-permute-start(bf16[256,512]{1,0:T(8,128)(2,1)S(1)} %collective-permute-done.9.refs_5_), channel_id=1, source_target_pairs={{0,16},{16,0},{1,17},{17,1},{2,18},{18,2},{3,19},{19,3},{4,20},{20... | collective-permute-start | bytes 786440 | tf_op jit(solution)/shard_map/ppermute | solution.py:694
  79.8 12.0 %collective-permute-start.19 = (bf16[256,512]{1,0:T(8,128)(2,1)}, bf16[256,512]{1,0:T(8,128)(2,1)}, u32[]{:S(2)}, u32[]{:S(2)}) collective-permute-start(bf16[256,512]{1,0:T(8,128)(2,1)} %collective-permute-done.15.refs_11_), channel_id=1, source_target_pairs={{0,2},{2,0},{1,3},{3,1},{4,6},{6,4},{5,7},{7,5},{8,10},{10,8},{9,1... | collective-permute-start | bytes 786440 | tf_op jit(solution)/shard_map/ppermute | solution.py:694
  81.5 238.1 %reduce-scatter.3.cloned.1.call-start = ((), (), s32[]{:S(2)}) async-start(), calls=%async_computation.4 | async-start | bytes 2621440 | tf_op jit(solution)/shard_map/reduce_scatter | solution.py:805
  82.7 41.0 %collective-permute-start.21 = (bf16[1154,256]{1,0:T(8,128)(2,1)S(1)}, bf16[1154,256]{1,0:T(8,128)(2,1)S(1)}, u32[]{:S(2)}, u32[]{:S(2)}) collective-permute-start(bf16[1154,256]{1,0:T(8,128)(2,1)S(1)} %get-tuple-element.112), channel_id=1, source_target_pairs={{0,2},{2,0},{1,3},{3,1},{4,6},{6,4},{5,7},{7,5},{8,10},{10,8},{9,1... | collective-permute-start | bytes 1772552 | tf_op jit(solution)/shard_map/ppermute | solution.py:694
  124.2 49.3 %collective-permute-start.22 = (bf16[1184,512]{1,0:T(8,128)(2,1)S(1)}, bf16[1184,512]{1,0:T(8,128)(2,1)S(1)}, u32[]{:S(2)}, u32[]{:S(2)}) collective-permute-start(bf16[1184,512]{1,0:T(8,128)(2,1)S(1)} %bitcast.52), channel_id=1, source_target_pairs={{0,1},{1,0},{2,3},{3,2},{4,5},{5,4},{6,7},{7,6},{8,9},{9,8},{10,11... | collective-permute-start | bytes 3637256 | tf_op jit(solution)/shard_map/ppermute | solution.py:694
  124.3 26.4 %collective-permute-start.27 = (bf16[1024,512]{1,0:T(8,128)(2,1)}, bf16[1024,512]{1,0:T(8,128)(2,1)}, u32[]{:S(2)}, u32[]{:S(2)}) collective-permute-start(bf16[1024,512]{1,0:T(8,128)(2,1)} %all-gather.5.cloned.1.call-done.refs_0_), channel_id=1, source_target_pairs={{0,2},{2,0},{1,3},{3,1},{4,6},{6,4},{5,7},{7,5},{8,10},{10,8},{9,1... | collective-permute-start | bytes 3145736 | tf_op jit(solution)/shard_map/ppermute | solution.py:694
  125.2 28.7 %collective-permute-start.26 = (bf16[1024,512]{1,0:T(8,128)(2,1)}, bf16[1024,512]{1,0:T(8,128)(2,1)}, u32[]{:S(2)}, u32[]{:S(2)}) collective-permute-start(bf16[1024,512]{1,0:T(8,128)(2,1)} %all-gather.5.cloned.1.call-done.refs_0_), channel_id=1, source_target_pairs={{0,16},{16,0},{1,17},{17,1},{2,18},{18,2},{3,19},{19,3},{4,20},{20... | collective-permute-start | bytes 3145736 | tf_op jit(solution)/shard_map/ppermute | solution.py:694
  127.0 45.6 %collective-permute-start.23 = (bf16[1024,512]{1,0:T(8,128)(2,1)}, bf16[1024,512]{1,0:T(8,128)(2,1)}, u32[]{:S(2)}, u32[]{:S(2)}) collective-permute-start(bf16[1024,512]{1,0:T(8,128)(2,1)} %all-gather.3.cloned.1.call-done.refs_0_), channel_id=1, source_target_pairs={{0,2},{2,0},{1,3},{3,1},{4,6},{6,4},{5,7},{7,5},{8,10},{10,8},{9,1... | collective-permute-start | bytes 3145736 | tf_op jit(solution)/shard_map/ppermute | solution.py:694
  128.5 49.2 %collective-permute-start.20 = (bf16[1184,1024]{1,0:T(8,128)(2,1)}, bf16[1184,1024]{1,0:T(8,128)(2,1)}, u32[]{:S(2)}, u32[]{:S(2)}) collective-permute-start(bf16[1184,1024]{1,0:T(8,128)(2,1)} %convolution_convert_fusion.a_ref), channel_id=1, source_target_pairs={{0,1},{1,0},{2,3},{3,2},{4,5},{5,4},{6,7},{7,6},{8,9},{9,8},{10,11... | collective-permute-start | bytes 7274504 | tf_op jit(solution)/shard_map/ppermute | solution.py:694
  150.7 33.7 %collective-permute-start.24 = (bf16[1024,512]{1,0:T(8,128)(2,1)}, bf16[1024,512]{1,0:T(8,128)(2,1)}, u32[]{:S(2)}, u32[]{:S(2)}) collective-permute-start(bf16[1024,512]{1,0:T(8,128)(2,1)} %all-gather.3.cloned.1.call-done.refs_0_), channel_id=1, source_target_pairs={{0,16},{16,0},{1,17},{17,1},{2,18},{18,2},{3,19},{19,3},{4,20},{20... | collective-permute-start | bytes 3145736 | tf_op jit(solution)/shard_map/ppermute | solution.py:694
  153.9 82.7 %collective-permute-start.28 = (bf16[1024,256]{1,0:T(8,128)(2,1)S(1)}, bf16[1024,256]{1,0:T(8,128)(2,1)}, u32[]{:S(2)}, u32[]{:S(2)}) collective-permute-start(bf16[1024,256]{1,0:T(8,128)(2,1)S(1)} %slice.166), channel_id=1, source_target_pairs={{0,16},{16,0},{1,17},{17,1},{2,18},{18,2},{3,19},{19,3},{4,20},{20... | collective-permute-start | bytes 1572872 | tf_op jit(solution)/shard_map/ppermute | solution.py:694
  172.6 64.0 %collective-permute-start.29 = (bf16[1024,256]{1,0:T(8,128)(2,1)}, bf16[1024,256]{1,0:T(8,128)(2,1)}, u32[]{:S(2)}, u32[]{:S(2)}) collective-permute-start(bf16[1024,256]{1,0:T(8,128)(2,1)} %slice.167), channel_id=1, source_target_pairs={{0,2},{2,0},{1,3},{3,1},{4,6},{6,4},{5,7},{7,5},{8,10},{10,8},{9,1... | collective-permute-start | bytes 1572872 | tf_op jit(solution)/shard_map/ppermute | solution.py:694
  173.4 35.7 %collective-permute-start.25 = (bf16[1024,512]{1,0:T(8,128)(2,1)}, bf16[1024,512]{1,0:T(8,128)(2,1)}, u32[]{:S(2)}, u32[]{:S(2)}) collective-permute-start(bf16[1024,512]{1,0:T(8,128)(2,1)} %collective-permute-done.23.refs_1_), channel_id=1, source_target_pairs={{0,16},{16,0},{1,17},{17,1},{2,18},{18,2},{3,19},{19,3},{4,20},{20... | collective-permute-start | bytes 3145736 | tf_op jit(solution)/shard_map/ppermute | solution.py:694
  255.5 201.0 %reduce-scatter.5.cloned.1.call-start = ((), (), s32[]{:S(2)}) async-start(), calls=%async_computation.5 | async-start | bytes 2293760 | tf_op jit(solution)/shard_map/reduce_scatter | solution.py:825
  255.6 29.5 %collective-permute-start.32 = (bf16[1024,512]{1,0:T(8,128)(2,1)}, bf16[1024,512]{1,0:T(8,128)(2,1)}, u32[]{:S(2)}, u32[]{:S(2)}) collective-permute-start(bf16[1024,512]{1,0:T(8,128)(2,1)} %convolution_convert_fusion.6), channel_id=1, source_target_pairs={{0,16},{16,0},{1,17},{17,1},{2,18},{18,2},{3,19},{19,3},{4,20},{20... | collective-permute-start | bytes 3145736 | tf_op jit(solution)/shard_map/ppermute | solution.py:694
  264.9 39.1 %collective-permute-start.34 = (bf16[1024,512]{1,0:T(8,128)(2,1)}, bf16[1024,512]{1,0:T(8,128)(2,1)}, u32[]{:S(2)}, u32[]{:S(2)}) collective-permute-start(bf16[1024,512]{1,0:T(8,128)(2,1)} %convolution_convert_fusion.4), channel_id=1, source_target_pairs={{0,16},{16,0},{1,17},{17,1},{2,18},{18,2},{3,19},{19,3},{4,20},{20... | collective-permute-start | bytes 3145736 | tf_op jit(solution)/shard_map/ppermute | solution.py:694
  265.0 39.0 %collective-permute-start.33 = (bf16[1024,512]{1,0:T(8,128)(2,1)}, bf16[1024,512]{1,0:T(8,128)(2,1)}, u32[]{:S(2)}, u32[]{:S(2)}) collective-permute-start(bf16[1024,512]{1,0:T(8,128)(2,1)} %convolution_convert_fusion.5), channel_id=1, source_target_pairs={{0,2},{2,0},{1,3},{3,1},{4,6},{6,4},{5,7},{7,5},{8,10},{10,8},{9,1... | collective-permute-start | bytes 3145736 | tf_op jit(solution)/shard_map/ppermute | solution.py:694
  304.0 15.6 %collective-permute-start.36 = (bf16[1024,256]{1,0:T(8,128)(2,1)S(1)}, bf16[1024,256]{1,0:T(8,128)(2,1)S(1)}, u32[]{:S(2)}, u32[]{:S(2)}) collective-permute-start(bf16[1024,256]{1,0:T(8,128)(2,1)S(1)} %slice.169), channel_id=1, source_target_pairs={{0,16},{16,0},{1,17},{17,1},{2,18},{18,2},{3,19},{19,3},{4,20},{20... | collective-permute-start | bytes 1572872 | tf_op jit(solution)/shard_map/ppermute | solution.py:694
  317.3 63.4 %collective-permute-start.41 = (bf16[1024,256]{1,0:T(8,128)(2,1)}, bf16[1024,256]{1,0:T(8,128)(2,1)S(1)}, u32[]{:S(2)}, u32[]{:S(2)}) collective-permute-start(bf16[1024,256]{1,0:T(8,128)(2,1)} %slice.172), channel_id=1, source_target_pairs={{0,16},{16,0},{1,17},{17,1},{2,18},{18,2},{3,19},{19,3},{4,20},{20... | collective-permute-start | bytes 1572872 | tf_op jit(solution)/shard_map/ppermute | solution.py:694
  317.6 63.1 %collective-permute-start.40 = (bf16[1024,256]{1,0:T(8,128)(2,1)}, bf16[1024,256]{1,0:T(8,128)(2,1)S(1)}, u32[]{:S(2)}, u32[]{:S(2)}) collective-permute-start(bf16[1024,256]{1,0:T(8,128)(2,1)} %slice.171), channel_id=1, source_target_pairs={{0,2},{2,0},{1,3},{3,1},{4,6},{6,4},{5,7},{7,5},{8,10},{10,8},{9,1... | collective-permute-start | bytes 1572872 | tf_op jit(solution)/shard_map/ppermute | solution.py:694
  318.1 62.6 %collective-permute-start.42 = (bf16[1024,256]{1,0:T(8,128)(2,1)}, bf16[1024,256]{1,0:T(8,128)(2,1)S(1)}, u32[]{:S(2)}, u32[]{:S(2)}) collective-permute-start(bf16[1024,256]{1,0:T(8,128)(2,1)} %slice.173), channel_id=1, source_target_pairs={{0,2},{2,0},{1,3},{3,1},{4,6},{6,4},{5,7},{7,5},{8,10},{10,8},{9,1... | collective-permute-start | bytes 1572872 | tf_op jit(solution)/shard_map/ppermute | solution.py:694
  320.7 28.8 %collective-permute-start.37 = (bf16[256,512]{1,0:T(8,128)(2,1)S(1)}, bf16[256,512]{1,0:T(8,128)(2,1)S(1)}, u32[]{:S(2)}, u32[]{:S(2)}) collective-permute-start(bf16[256,512]{1,0:T(8,128)(2,1)S(1)} %slice.143), channel_id=1, source_target_pairs={{0,2},{2,0},{1,3},{3,1},{4,6},{6,4},{5,7},{7,5},{8,10},{10,8},{9,1... | collective-permute-start | bytes 786440 | tf_op jit(solution)/shard_map/ppermute | solution.py:694
  322.5 56.4 %collective-permute-start.43 = (bf16[1024,128]{1,0:T(8,128)(2,1)S(1)}, bf16[1024,128]{1,0:T(8,128)(2,1)S(1)}, u32[]{:S(2)}, u32[]{:S(2)}) collective-permute-start(bf16[1024,128]{1,0:T(8,128)(2,1)S(1)} %slice.174), channel_id=1, source_target_pairs={{0,2},{2,0},{1,3},{3,1},{4,6},{6,4},{5,7},{7,5},{8,10},{10,8},{9,1... | collective-permute-start | bytes 786440 | tf_op jit(solution)/shard_map/ppermute | solution.py:694
  378.9 12.4 %collective-permute-start.38 = (bf16[1024,256]{1,0:T(8,128)(2,1)S(1)}, bf16[1024,256]{1,0:T(8,128)(2,1)S(1)}, u32[]{:S(2)}, u32[]{:S(2)}) collective-permute-start(bf16[1024,256]{1,0:T(8,128)(2,1)S(1)} %convolution_convert_fusion.7), channel_id=1, source_target_pairs={{0,16},{16,0},{1,17},{17,1},{2,18},{18,2},{3,19},{19,3},{4,20},{20... | collective-permute-start | bytes 1572872 | tf_op jit(solution)/shard_map/ppermute | solution.py:694
  398.1 20.7 %collective-permute-start.45 = (bf16[1024,384]{1,0:T(8,128)(2,1)}, bf16[1024,384]{1,0:T(8,128)(2,1)S(1)}, u32[]{:S(2)}, u32[]{:S(2)}) collective-permute-start(bf16[1024,384]{1,0:T(8,128)(2,1)} %add_convert_fusion.4), channel_id=1, source_target_pairs={{0,2},{2,0},{1,3},{3,1},{4,6},{6,4},{5,7},{7,5},{8,10},{10,8},{9,1... | collective-permute-start | bytes 2359304 | tf_op jit(solution)/shard_map/ppermute | solution.py:694
  399.7 20.0 %collective-permute-start.44 = (bf16[1024,384]{1,0:T(8,128)(2,1)}, bf16[1024,384]{1,0:T(8,128)(2,1)}, u32[]{:S(2)}, u32[]{:S(2)}) collective-permute-start(bf16[1024,384]{1,0:T(8,128)(2,1)} %add_convert_fusion.5), channel_id=1, source_target_pairs={{0,16},{16,0},{1,17},{17,1},{2,18},{18,2},{3,19},{19,3},{4,20},{20... | collective-permute-start | bytes 2359304 | tf_op jit(solution)/shard_map/ppermute | solution.py:694
  400.0 31.7 %collective-permute-start.35 = (bf16[1184,256]{1,0:T(8,128)(2,1)}, bf16[1184,256]{1,0:T(8,128)(2,1)}, u32[]{:S(2)}, u32[]{:S(2)}) collective-permute-start(bf16[1184,256]{1,0:T(8,128)(2,1)} %get-tuple-element.133), channel_id=1, source_target_pairs={{0,2},{2,0},{1,3},{3,1},{4,6},{6,4},{5,7},{7,5},{8,10},{10,8},{9,1... | collective-permute-start | bytes 1818632 | tf_op jit(solution)/shard_map/ppermute | solution.py:694
  421.1 15.9 %collective-permute-start.54 = (f32[12,256]{1,0:T(8,128)S(1)}, f32[12,256]{1,0:T(8,128)S(1)}, u32[]{:S(2)}, u32[]{:S(2)}) collective-permute-start(f32[12,256]{1,0:T(8,128)S(1)} %copy-done.48), channel_id=1, source_target_pairs={{0,2},{2,0},{1,3},{3,1},{4,6},{6,4},{5,7},{7,5},{8,10},{10,8},{9,1... | collective-permute-start | bytes 36872 | tf_op jit(solution)/shard_map/ppermute | solution.py:694
  431.6 21.5 %collective-permute-start.48 = (bf16[256,384]{1,0:T(8,128)(2,1)}, bf16[256,384]{1,0:T(8,128)(2,1)}, u32[]{:S(2)}, u32[]{:S(2)}) collective-permute-start(bf16[256,384]{1,0:T(8,128)(2,1)} %get-tuple-element.203), channel_id=1, source_target_pairs={{0,4},{4,8},{8,12},{12,0},{1,5},{5,9},{9,13},{13,1},{2,6},{6,10},{... | collective-permute-start | bytes 589832 | tf_op jit(solution)/shard_map/ppermute | solution.py:697
  431.6 22.1 %collective-permute-start.50 = (bf16[256,384]{1,0:T(8,128)(2,1)}, bf16[256,384]{1,0:T(8,128)(2,1)}, u32[]{:S(2)}, u32[]{:S(2)}) collective-permute-start(bf16[256,384]{1,0:T(8,128)(2,1)} %get-tuple-element.204), channel_id=1, source_target_pairs={{0,12},{4,0},{8,4},{12,8},{1,13},{5,1},{9,5},{13,9},{2,14},{6,2},{... | collective-permute-start | bytes 589832 | tf_op jit(solution)/shard_map/ppermute | solution.py:697
  435.5 18.3 %collective-permute-start.49 = (bf16[256,384]{1,0:T(8,128)(2,1)S(1)}, bf16[256,384]{1,0:T(8,128)(2,1)}, u32[]{:S(2)}, u32[]{:S(2)}) collective-permute-start(bf16[256,384]{1,0:T(8,128)(2,1)S(1)} %get-tuple-element.205), channel_id=1, source_target_pairs={{0,8},{4,12},{8,0},{12,4},{1,9},{5,13},{9,1},{13,5},{2,10},{6,14},... | collective-permute-start | bytes 589832 | tf_op jit(solution)/shard_map/ppermute | solution.py:697
  435.5 21.6 %collective-permute-start.47 = (bf16[1184,256]{1,0:T(8,128)(2,1)}, bf16[1184,256]{1,0:T(8,128)(2,1)}, u32[]{:S(2)}, u32[]{:S(2)}) collective-permute-start(bf16[1184,256]{1,0:T(8,128)(2,1)} %get-tuple-element.163), channel_id=1, source_target_pairs={{0,2},{2,0},{1,3},{3,1},{4,6},{6,4},{5,7},{7,5},{8,10},{10,8},{9,1... | collective-permute-start | bytes 1818632 | tf_op jit(solution)/shard_map/ppermute | solution.py:694
  453.1 24.2 %collective-permute-start.57 = (f32[12,256]{1,0:T(8,128)S(1)}, f32[12,256]{1,0:T(8,128)S(1)}, u32[]{:S(2)}, u32[]{:S(2)}) collective-permute-start(f32[12,256]{1,0:T(8,128)S(1)} %add.145.a_ref), channel_id=1, source_target_pairs={{0,16},{16,0},{1,17},{17,1},{2,18},{18,2},{3,19},{19,3},{4,20},{20... | collective-permute-start | bytes 36872 | tf_op jit(solution)/shard_map/ppermute | solution.py:694
  454.9 24.3 %collective-permute-start.51 = (bf16[256,384]{1,0:T(8,128)(2,1)S(1)}, bf16[256,384]{1,0:T(8,128)(2,1)}, u32[]{:S(2)}, u32[]{:S(2)}) collective-permute-start(bf16[256,384]{1,0:T(8,128)(2,1)S(1)} %add_convert_fusion.8.mine_ref), channel_id=1, source_target_pairs={{0,16},{16,0},{1,17},{17,1},{2,18},{18,2},{3,19},{19,3},{4,20},{20... | collective-permute-start | bytes 589832 | tf_op jit(solution)/shard_map/ppermute | solution.py:694
  456.5 17.8 %collective-permute-start.52 = (bf16[256,896]{1,0:T(8,128)(2,1)}, bf16[256,896]{1,0:T(8,128)(2,1)}, u32[]{:S(2)}, u32[]{:S(2)}) collective-permute-start(bf16[256,896]{1,0:T(8,128)(2,1)} %reduce-scatter.5.cloned.1.call-done.mine_ref), channel_id=1, source_target_pairs={{0,16},{16,0},{1,17},{17,1},{2,18},{18,2},{3,19},{19,3},{4,20},{20... | collective-permute-start | bytes 1376264 | tf_op jit(solution)/shard_map/ppermute | solution.py:694
  (70 other events, 890.3 us)
Sparse Core Ops, SparseCore 0:
  52.0 26.6 all-gather.4
  81.6 26.0 all-gather.2
  255.6 41.2 reduce-scatter.2
  398.3 36.8 reduce-scatter.4

commit v14 on v13

--- a/solution.py
+++ b/solution.py
@@ -766,8 +766,12 @@
         (vectors, pl.BlockSpec((None, 1, D), lambda i, *_, at=at: (at, 0, 0))) for at in range(6)
     )
     wide_input = wide_tokens(inputs, after(input_got, pieces[-1]))
-    far_oths = [over(far) for far in fars[:-1]]
-    far_oths.append(across(after(oths[-1], wide_input, qkv_bias)))
+    far_oths = [
+        across(after(oths[at], wide_input, qkv_bias))
+        if at % 2
+        else over(fars[at])
+        for at in range(n_row)
+    ]
 
     def gather(part):
         up_part = halves(up_weight, 1)[0][:, quarter * part : quarter * (part + 1)]

time: 494 us -> 503 us (1.018)
  waiting for transfers between devices: 187 us -> 197 us
    ppermute x52, waiting for transfers between devices: 170 us -> 180 us  [swap(): return lax.ppermute(value, axis, [(at, at ^ bit) for at in range(size)])]
  transfers between devices with their start and end apart: 62 -> 62, of which waited for: 23 -> 23; matrix products, arithmetic and copies ran while one was open for 16% -> 16% of each run, Pallas kernels for 23% -> 22%
where the time goes in v14:
time: 503 us; the launch traced here: 498 us
  waiting for transfers between devices  197 us (39%)
  Pallas kernels  131 us (26%)
  starting transfers between devices  64.1 us (13%)
  matrix products  56.3 us (11%)
  local copies, waits for them, and re-layouts  20.8 us (4%)
  between operations  14.9 us (3%)
  other arithmetic  13.5 us (3%)
    ppermute x52, waiting for transfers between devices, swap(): return lax.ppermute(value, axis, [(at, at ^ bit) for at in range(size)])  180 us
    ppermute x52, starting transfers between devices, swap(): return lax.ppermute(value, axis, [(at, at ^ bit) for at in range(size)])  52.1 us
    dot_general x13, matrix products, mm_tn(): lax.dot_general(a, b, (((0,), (0,)), ((), ())), preferred_element_type=F32)  47.6 us
    pallas_call x2, Pallas kernels, mlp(): pl.pallas_call(functools.partial(mlp_kernel, bool(before), split), name='...  35.8 us
    pallas_call x1, Pallas kernels, attend_back(): pl.pallas_call(attend_back_kernel, grid=(pairs, held), name='attend_back'...  22.7 us
    ppermute x6, waiting for transfers between devices, shifted(): lax.ppermute(value, 'row', [(at, (at + shift) % n_row) for at in range(n_...  17.1 us
    pallas_call x2, Pallas kernels, attend(): pl.pallas_call(kernel, grid=(pairs // 2, held), name='attend', in_specs=[...  16.6 us
    pallas_call x1, Pallas kernels, turn(): pl.pallas_call(turn_kernel, name='turn', grid_spec=pltpu.PrefetchScalarGr...  14.2 us
  transfers between devices with their start and end apart: 62, of which 23 were waited for; matrix products, arithmetic and copies ran while one was open for 16% of the time, Pallas kernels for 22%

profile of v14, /device:TPU:0, one launch (start us, length us, event | category | flops | bytes accessed | tf_op | source)
XLA Modules:
  0.0 497.7 jit_solution(16607010984052119288)
XLA Ops:
  9.0 3.0 collective-permute-start
  12.8 3.7 collective-permute-start.1
  16.5 5.3 %collective-permute-done.1.refs_3_ = bf16[256,512]{1,0:T(8,128)(2,1)S(1)} collective-permute-done((bf16[256,512]{1,0:T(8,128)(2,1)S(1)}, bf16[256,512]{1,0:T(8,128)(2,1)S(1)}, u32[]{:S(2)}, u32[]{:S(2)}) %collective-permute-start.1) | collective-permute-done | bytes 262176 | tf_op jit(solution)/shard_map/ppermute | solution.py:697
  21.8 3.6 collective-permute-done
  29.6 2.6 collective-permute-start.7
  38.0 11.8 %collective-permute-done.7.refs_2_ = bf16[256,512]{1,0:T(8,128)(2,1)} collective-permute-done((bf16[256,512]{1,0:T(8,128)(2,1)S(1)}, bf16[256,512]{1,0:T(8,128)(2,1)}, u32[]{:S(2)}, u32[]{:S(2)}) %collective-permute-start.7) | collective-permute-done | bytes 262176 | tf_op jit(solution)/shard_map/ppermute | solution.py:697
  57.4 3.1 collective-permute-done.8.refs_4_
  61.0 9.3 %collective-permute-done.15.refs_11_ = bf16[256,512]{1,0:T(8,128)(2,1)} collective-permute-done((bf16[256,512]{1,0:T(8,128)(2,1)}, bf16[256,512]{1,0:T(8,128)(2,1)}, u32[]{:S(2)}, u32[]{:S(2)}) %collective-permute-start.15) | collective-permute-done | bytes 262176 | tf_op jit(solution)/shard_map/ppermute | solution.py:694
  85.7 5.1 %collective-permute-done.11.refs_7_ = bf16[256,512]{1,0:T(8,128)(2,1)S(1)} collective-permute-done((bf16[256,512]{1,0:T(8,128)(2,1)S(1)}, bf16[256,512]{1,0:T(8,128)(2,1)S(1)}, u32[]{:S(2)}, u32[]{:S(2)}) %collective-permute-start.11) | collective-permute-done | bytes 262176 | tf_op jit(solution)/shard_map/ppermute | solution.py:694
  90.8 5.7 %collective-permute-done.17.refs_13_ = bf16[256,512]{1,0:T(8,128)(2,1)} collective-permute-done((bf16[256,512]{1,0:T(8,128)(2,1)S(1)}, bf16[256,512]{1,0:T(8,128)(2,1)}, u32[]{:S(2)}, u32[]{:S(2)}) %collective-permute-start.17) | collective-permute-done | bytes 262176 | tf_op jit(solution)/shard_map/ppermute | solution.py:694
  96.6 5.6 %collective-permute-done.19.refs_15_ = bf16[256,512]{1,0:T(8,128)(2,1)} collective-permute-done((bf16[256,512]{1,0:T(8,128)(2,1)}, bf16[256,512]{1,0:T(8,128)(2,1)}, u32[]{:S(2)}, u32[]{:S(2)}) %collective-permute-start.19) | collective-permute-done | bytes 262176 | tf_op jit(solution)/shard_map/ppermute | solution.py:694
  102.2 10.8 %norm_qkv.1 = (bf16[1184,1024]{1,0:T(8,128)(2,1)}, bf16[1184,1536]{1,0:T(8,128)(2,1)}, bf16[1024,2048]{1,0:T(8,128)(2,1)}) custom-call(s32[4]{0:T(128)} %pad_add_fusion.place_ref, bf16[1184,1024]{1,0:T(8,128)(2,1)} %pad_maximum_fusion.x_ref, f32[6,1,1024]{2,1,0:T(1,128)} %get-tuple-element.104.gain_ref.shift_ref.bias_ref, ...), custom_call_target="tpu_custom_call" | custom-call | flops 3724541952 | bytes 19398656 | tf_op jit(solution)/shard_map/norm_qkv/pallas_call | solution.py:114
  113.0 8.3 %attend.2 = (bf16[1184,512]{1,0:T(8,128)(2,1)}, bf16[2,8,592,592]{3,2,1,0:T(8,128)(2,1)}) custom-call(bf16[1184,1536]{1,0:T(8,128)(2,1)} %get-tuple-element.108.refs_0_.qkv_ref), custom_call_target="tpu_custom_call" | custom-call | flops 8613003264 | bytes 24248320 | tf_op jit(solution)/shard_map/attend/pallas_call | solution.py:160
  121.3 8.3 %attend.3 = (bf16[1184,512]{1,0:T(8,128)(2,1)}, bf16[2,8,592,592]{3,2,1,0:T(8,128)(2,1)}) custom-call(bf16[1184,1536]{1,0:T(8,128)(2,1)} %get-tuple-element.108.refs_0_.qkv_ref, bf16[1184,512]{1,0:T(8,128)(2,1)} %get-tuple-element.109.refs_1_, bf16[2,8,592,592]{3,2,1,0:T(8,128)(2,1)} %get-tuple-element.110.refs_2_), custom_call_target="tpu_custom_call", output_to_operand_aliasing={{0}: (1, {}), {1}: (2, {})} | custom-call | flops 8613003264 | bytes 24248320 | tf_op jit(solution)/shard_map/attend/pallas_call | solution.py:160
  129.6 4.4 convolution_convert_fusion.a_ref
  138.2 22.8 %collective-permute-done.27.refs_2_ = bf16[1024,512]{1,0:T(8,128)(2,1)} collective-permute-done((bf16[1024,512]{1,0:T(8,128)(2,1)}, bf16[1024,512]{1,0:T(8,128)(2,1)}, u32[]{:S(2)}, u32[]{:S(2)}) %collective-permute-start.27) | collective-permute-done | bytes 1048608 | tf_op jit(solution)/shard_map/ppermute | solution.py:694
  166.1 16.9 %collective-permute-done.23.refs_1_ = bf16[1024,512]{1,0:T(8,128)(2,1)} collective-permute-done((bf16[1024,512]{1,0:T(8,128)(2,1)}, bf16[1024,512]{1,0:T(8,128)(2,1)}, u32[]{:S(2)}, u32[]{:S(2)}) %collective-permute-start.23) | collective-permute-done | bytes 1048608 | tf_op jit(solution)/shard_map/ppermute | solution.py:694
  187.4 6.8 %middle.1 = (f32[1184,1024]{1,0:T(8,128)}, bf16[1184,1024]{1,0:T(8,128)(2,1)}) custom-call(bf16[1184,1024]{1,0:T(8,128)(2,1)} %pad_maximum_fusion.x_ref, bf16[1184,1024]{1,0:T(8,128)(2,1)} %convolution_convert_fusion.a_ref, bf16[1184,1024]{1,0:T(8,128)(2,1)} %collective-permute-done.20.b_ref, f32[6,1,1024]{2,1,0:T(1,128)} %get-tuple-element.104.gain_ref.shift_ref.bias_ref, ...), custom_call_target="tpu_custom_call" | custom-call | flops 24248320 | bytes 14548992 | tf_op jit(solution)/shard_map/middle/pallas_call | solution.py:227
  194.2 24.9 %collective-permute-done.25.refs_3_.refs_4_ = bf16[1024,512]{1,0:T(8,128)(2,1)} collective-permute-done((bf16[1024,512]{1,0:T(8,128)(2,1)}, bf16[1024,512]{1,0:T(8,128)(2,1)}, u32[]{:S(2)}, u32[]{:S(2)}) %collective-permute-start.25) | collective-permute-done | bytes 1048608 | tf_op jit(solution)/shard_map/ppermute | solution.py:694
  219.1 17.0 %mlp_first.1 = (bf16[1184,1024]{1,0:T(8,128)(2,1)}, bf16[1184,1024]{1,0:T(8,128)(2,1)}, f32[1,1024]{1,0:T(1,128)}, bf16[1184,1024]{1,0:T(8,128)(2,1)}, bf16[1184,1024]{1,0:T(8,128)(2,1)}) custom-call(s32[4]{0:T(128)} %pad_add_fusion.place_ref, bf16[1184,1024]{1,0:T(8,128)(2,1)} %get-tuple-element.121.n_ref, bf16[1184,1024]{1,0:T(8,128)(2,1)} %pad_maximum_fusion.1.dy_ref, ...), custom_call_target="tpu_custom_call" | custom-call | flops 9932111872 | bytes 24248320 | tf_op jit(solution)/shard_map/mlp_first/pallas_call | solution.py:318
  236.1 6.0 %convolution_convert_fusion.2 = bf16[1024,1024]{1,0:T(8,128)(2,1)} fusion(bf16[1184,1024]{1,0:T(8,128)(2,1)} %get-tuple-element.120, bf16[1184,256]{1,0:T(8,128)(2,1)S(1)} %get-tuple-element.196, bf16[1184,256]{1,0:T(8,128)(2,1)S(1)} %get-tuple-element.212, bf16[1184,256]{1,0:T(8,128)(2,1)S(1)} %get-tuple-element.195, ...), kind=kOutput, calls=%fused_computation.9 | convolution fusion | flops 2493775872 | bytes 6946816 | tf_op jit(solution)/shard_map/dot_general | solution.py:34
  242.0 4.5 convolution_convert_fusion.6
  246.6 18.8 %mlp_second.1 = (bf16[1184,1024]{1,0:T(8,128)(2,1)}, bf16[1184,1024]{1,0:T(8,128)(2,1)}, f32[1,1024]{1,0:T(1,128)}, f32[1184,512]{1,0:T(8,128)}, bf16[1184,512]{1,0:T(8,128)(2,1)}, /*index=5*/bf16[1184,1024]{1,0:T(8,128)(2,1)}) custom-call(s32[4]{0:T(128)} %pad_add_fusion.place_ref, bf16[1184,1024]{1,0:T(8,128)(2,1)} %get-tuple-element.121.n_ref, ...), custom_call_target="tpu_custom_call" | custom-call | flops 9932111872 | bytes 24248320 | tf_op jit(solution)/shard_map/mlp_second/pallas_call | solution.py:318
  267.4 4.7 convolution_convert_fusion.4
  272.1 2.5 convolution_convert_fusion.5
  276.8 14.2 %turn.1 = (f32[1184,1024]{1,0:T(8,128)}, bf16[1184,1024]{1,0:T(8,128)(2,1)}, bf16[1184,512]{1,0:T(8,128)(2,1)}, f32[4,1024]{1,0:T(4,128)}, bf16[1184,256]{1,0:T(8,128)(2,1)}, /*index=5*/bf16[1184,256]{1,0:T(8,128)(2,1)}) custom-call(s32[4]{0:T(128)} %pad_add_fusion.place_ref, f32[1184,1024]{1,0:T(8,128)} %get-tuple-element.113.h_ref, ...), custom_call_target="tpu_custom_call" | custom-call | flops 1241513984 | bytes 24248320 | tf_op jit(solution)/shard_map/turn/pallas_call | solution.py:377
  291.1 3.7 convolution_convert_fusion.3
  294.9 19.1 %collective-permute-done.34 = bf16[1024,512]{1,0:T(8,128)(2,1)} collective-permute-done((bf16[1024,512]{1,0:T(8,128)(2,1)}, bf16[1024,512]{1,0:T(8,128)(2,1)}, u32[]{:S(2)}, u32[]{:S(2)}) %collective-permute-start.34) | collective-permute-done | bytes 1048608 | tf_op jit(solution)/shard_map/ppermute | solution.py:694
  315.5 2.8 add_convert_fusion.2.refs_4_
  318.3 3.2 add_convert_fusion.1.refs_0_
  323.3 2.8 add_convert_fusion.refs_2_
  334.0 25.4 %collective-permute-done.37 = bf16[256,512]{1,0:T(8,128)(2,1)S(1)} collective-permute-done((bf16[256,512]{1,0:T(8,128)(2,1)S(1)}, bf16[256,512]{1,0:T(8,128)(2,1)S(1)}, u32[]{:S(2)}, u32[]{:S(2)}) %collective-permute-start.37) | collective-permute-done | bytes 262176 | tf_op jit(solution)/shard_map/ppermute | solution.py:694
  360.2 22.7 %attend_back.1 = (bf16[1184,1536]{1,0:T(8,128)(2,1)}, f32[1,1536]{1,0:T(1,128)}) custom-call(bf16[1184,1536]{1,0:T(8,128)(2,1)} %get-tuple-element.108.refs_0_.qkv_ref, bf16[2,8,592,592]{3,2,1,0:T(8,128)(2,1)} %get-tuple-element.137.p_ref, bf16[1184,512]{1,0:T(8,128)(2,1)} %get-tuple-element.144.g_ref), custom_call_target="tpu_custom_call" | custom-call | flops 21532508160 | bytes 60620800 | tf_op jit(solution)/shard_map/attend_back/pallas_call | solution.py:202
  382.9 2.9 convolution_convert_fusion.7
  385.8 2.6 convolution_convert_fusion.8
  392.2 4.3 join.1
  396.6 4.5 add_convert_fusion.5
  401.1 2.4 add_convert_fusion.4
  403.5 4.3 convolution_convert_fusion.1.a_ref
  410.4 4.9 fusion.8
  415.4 9.0 %last.1 = (f32[1184,256]{1,0:T(8,128)}, bf16[1184,256]{1,0:T(8,128)(2,1)}, f32[2,256]{1,0:T(2,128)}, f32[2,256]{1,0:T(2,128)}) custom-call(s32[4]{0:T(128)} %pad_add_fusion.place_ref, bf16[1184,1024]{1,0:T(8,128)(2,1)} %pad_maximum_fusion.x_ref, f32[1184,1024]{1,0:T(8,128)} %get-tuple-element.156.dh_ref, bf16[1184,1024]{1,0:T(8,128)(2,1)} %copy-done.4, ...), custom_call_target="tpu_custom_call" | custom-call | flops 24248320 | bytes 14548992 | tf_op jit(solution)/shard_map/last/pallas_call | solution.py:437
  425.8 2.8 collective-permute-done.45
  432.4 9.0 %collective-permute-done.35 = bf16[1184,256]{1,0:T(8,128)(2,1)} collective-permute-done((bf16[1184,256]{1,0:T(8,128)(2,1)}, bf16[1184,256]{1,0:T(8,128)(2,1)}, u32[]{:S(2)}, u32[]{:S(2)}) %collective-permute-start.35) | collective-permute-done | bytes 606240 | tf_op jit(solution)/shard_map/ppermute | solution.py:694
  441.4 3.8 collective-permute-start.50
  448.6 5.9 %collective-permute-done.55 = f32[12,256]{1,0:T(8,128)S(1)} collective-permute-done((f32[12,256]{1,0:T(8,128)S(1)}, f32[12,256]{1,0:T(8,128)S(1)}, u32[]{:S(2)}, u32[]{:S(2)}) %collective-permute-start.55) | collective-permute-done | bytes 12320 | tf_op jit(solution)/shard_map/ppermute | solution.py:694
  454.5 4.6 collective-permute-start.56
  470.9 13.2 %collective-permute-done.52.other_ref = bf16[256,896]{1,0:T(8,128)(2,1)} collective-permute-done((bf16[256,896]{1,0:T(8,128)(2,1)}, bf16[256,896]{1,0:T(8,128)(2,1)}, u32[]{:S(2)}, u32[]{:S(2)}) %collective-permute-start.52) | collective-permute-done | bytes 458784 | tf_op jit(solution)/shard_map/ppermute | solution.py:694
  484.1 3.0 place_mlp.1
  (283 shorter events, 96.2 us)
Async XLA Ops:
  7.2 127.3 %all-gather.5.cloned.1.call-start = ((), (), s32[]{:S(2)}) async-start(), calls=%async_computation.3 | async-start | bytes 1310720 | tf_op jit(solution)/shard_map/all_gather | solution.py:780
  9.0 16.4 %collective-permute-start = (bf16[1154,256]{1,0:T(8,128)(2,1)S(1)}, bf16[1154,256]{1,0:T(8,128)(2,1)S(1)}, u32[]{:S(2)}, u32[]{:S(2)}) collective-permute-start(bf16[1154,256]{1,0:T(8,128)(2,1)S(1)} %get-tuple-element.204), channel_id=1, source_target_pairs={{0,2},{2,0},{1,3},{3,1},{4,6},{6,4},{5,7},{7,5},{8,10},{10,8},{9,1... | collective-permute-start | bytes 1772552 | tf_op jit(solution)/shard_map/ppermute | solution.py:694
  25.9 29.6 %collective-permute-start.2 = (bf16[1184,512]{1,0:T(8,128)(2,1)S(1)}, bf16[1184,512]{1,0:T(8,128)(2,1)S(1)}, u32[]{:S(2)}, u32[]{:S(2)}) collective-permute-start(bf16[1184,512]{1,0:T(8,128)(2,1)S(1)} %bitcast.51), channel_id=1, source_target_pairs={{0,1},{1,0},{2,3},{3,2},{4,5},{5,4},{6,7},{7,6},{8,9},{9,8},{10,11... | collective-permute-start | bytes 3637256 | tf_op jit(solution)/shard_map/ppermute | solution.py:694
  27.4 24.6 %collective-permute-start.4 = (f32[12,256]{1,0:T(8,128)}, f32[12,256]{1,0:T(8,128)S(1)}, u32[]{:S(2)}, u32[]{:S(2)}) collective-permute-start(f32[12,256]{1,0:T(8,128)} %pack.1.own), channel_id=1, source_target_pairs={{0,1},{1,0},{2,3},{3,2},{4,5},{5,4},{6,7},{7,6},{8,9},{9,8},{10,11... | collective-permute-start | bytes 36872 | tf_op jit(solution)/shard_map/ppermute | solution.py:694
  29.6 20.2 %collective-permute-start.7 = (bf16[256,512]{1,0:T(8,128)(2,1)S(1)}, bf16[256,512]{1,0:T(8,128)(2,1)}, u32[]{:S(2)}, u32[]{:S(2)}) collective-permute-start(bf16[256,512]{1,0:T(8,128)(2,1)S(1)} %pad_maximum_fusion.6.refs_0_), channel_id=1, source_target_pairs={{0,8},{4,12},{8,0},{12,4},{1,9},{5,13},{9,1},{13,5},{2,10},{6,14},... | collective-permute-start | bytes 786440 | tf_op jit(solution)/shard_map/ppermute | solution.py:697
  32.2 19.1 %collective-permute-start.6 = (bf16[256,512]{1,0:T(8,128)(2,1)S(1)}, bf16[256,512]{1,0:T(8,128)(2,1)}, u32[]{:S(2)}, u32[]{:S(2)}) collective-permute-start(bf16[256,512]{1,0:T(8,128)(2,1)S(1)} %pad_maximum_fusion.6.refs_0_), channel_id=1, source_target_pairs={{0,4},{4,8},{8,12},{12,0},{1,5},{5,9},{9,13},{13,1},{2,6},{6,10},{... | collective-permute-start | bytes 786440 | tf_op jit(solution)/shard_map/ppermute | solution.py:697
  37.3 15.2 %collective-permute-start.5 = (f32[12,256]{1,0:T(8,128)S(1)}, f32[12,256]{1,0:T(8,128)S(1)}, u32[]{:S(2)}, u32[]{:S(2)}) collective-permute-start(f32[12,256]{1,0:T(8,128)S(1)} %collective-permute-done.3.far), channel_id=1, source_target_pairs={{0,1},{1,0},{2,3},{3,2},{4,5},{5,4},{6,7},{7,6},{8,9},{9,8},{10,11... | collective-permute-start | bytes 36872 | tf_op jit(solution)/shard_map/ppermute | solution.py:694
  49.8 26.5 %collective-permute-start.12 = (bf16[256,512]{1,0:T(8,128)(2,1)S(1)}, bf16[256,512]{1,0:T(8,128)(2,1)S(1)}, u32[]{:S(2)}, u32[]{:S(2)}) collective-permute-start(bf16[256,512]{1,0:T(8,128)(2,1)S(1)} %pad_maximum_fusion.6.refs_0_), channel_id=1, source_target_pairs={{0,16},{16,0},{1,17},{17,1},{2,18},{18,2},{3,19},{19,3},{4,20},{20... | collective-permute-start | bytes 786440 | tf_op jit(solution)/shard_map/ppermute | solution.py:694
  51.9 84.8 %all-gather.3.cloned.1.call-start = ((), (), s32[]{:S(2)}) async-start(), calls=%async_computation.2 | async-start | bytes 1310720 | tf_op jit(solution)/shard_map/all_gather | solution.py:780
  51.9 30.0 %collective-permute-start.14 = (bf16[256,512]{1,0:T(8,128)(2,1)}, bf16[256,512]{1,0:T(8,128)(2,1)}, u32[]{:S(2)}, u32[]{:S(2)}) collective-permute-start(bf16[256,512]{1,0:T(8,128)(2,1)} %collective-permute-done.7.refs_2_), channel_id=1, source_target_pairs={{0,16},{16,0},{1,17},{17,1},{2,18},{18,2},{3,19},{19,3},{4,20},{20... | collective-permute-start | bytes 786440 | tf_op jit(solution)/shard_map/ppermute | solution.py:694
  52.5 25.4 %collective-permute-start.10 = (bf16[256,512]{1,0:T(8,128)(2,1)}, bf16[256,512]{1,0:T(8,128)(2,1)}, u32[]{:S(2)}, u32[]{:S(2)}) collective-permute-start(bf16[256,512]{1,0:T(8,128)(2,1)} %collective-permute-done.7.refs_2_), channel_id=1, source_target_pairs={{0,2},{2,0},{1,3},{3,1},{4,6},{6,4},{5,7},{7,5},{8,10},{10,8},{9,1... | collective-permute-start | bytes 786440 | tf_op jit(solution)/shard_map/ppermute | solution.py:694
  55.5 14.8 %collective-permute-start.15 = (bf16[256,512]{1,0:T(8,128)(2,1)}, bf16[256,512]{1,0:T(8,128)(2,1)}, u32[]{:S(2)}, u32[]{:S(2)}) collective-permute-start(bf16[256,512]{1,0:T(8,128)(2,1)} %copy-done.39), channel_id=1, source_target_pairs={{0,16},{16,0},{1,17},{17,1},{2,18},{18,2},{3,19},{19,3},{4,20},{20... | collective-permute-start | bytes 786440 | tf_op jit(solution)/shard_map/ppermute | solution.py:694
  60.5 15.3 %collective-permute-start.13 = (bf16[256,512]{1,0:T(8,128)(2,1)}, bf16[256,512]{1,0:T(8,128)(2,1)S(1)}, u32[]{:S(2)}, u32[]{:S(2)}) collective-permute-start(bf16[256,512]{1,0:T(8,128)(2,1)} %collective-permute-done.6.refs_1_), channel_id=1, source_target_pairs={{0,16},{16,0},{1,17},{17,1},{2,18},{18,2},{3,19},{19,3},{4,20},{20... | collective-permute-start | bytes 786440 | tf_op jit(solution)/shard_map/ppermute | solution.py:694
  76.3 14.5 %collective-permute-start.11 = (bf16[256,512]{1,0:T(8,128)(2,1)S(1)}, bf16[256,512]{1,0:T(8,128)(2,1)S(1)}, u32[]{:S(2)}, u32[]{:S(2)}) collective-permute-start(bf16[256,512]{1,0:T(8,128)(2,1)S(1)} %copy-done.40), channel_id=1, source_target_pairs={{0,2},{2,0},{1,3},{3,1},{4,6},{6,4},{5,7},{7,5},{8,10},{10,8},{9,1... | collective-permute-start | bytes 786440 | tf_op jit(solution)/shard_map/ppermute | solution.py:694
  81.4 15.1 %collective-permute-start.17 = (bf16[256,512]{1,0:T(8,128)(2,1)S(1)}, bf16[256,512]{1,0:T(8,128)(2,1)}, u32[]{:S(2)}, u32[]{:S(2)}) collective-permute-start(bf16[256,512]{1,0:T(8,128)(2,1)S(1)} %collective-permute-done.13.refs_9_), channel_id=1, source_target_pairs={{0,2},{2,0},{1,3},{3,1},{4,6},{6,4},{5,7},{7,5},{8,10},{10,8},{9,1... | collective-permute-start | bytes 786440 | tf_op jit(solution)/shard_map/ppermute | solution.py:694
  81.9 20.2 %collective-permute-start.19 = (bf16[256,512]{1,0:T(8,128)(2,1)}, bf16[256,512]{1,0:T(8,128)(2,1)}, u32[]{:S(2)}, u32[]{:S(2)}) collective-permute-start(bf16[256,512]{1,0:T(8,128)(2,1)} %collective-permute-done.15.refs_11_), channel_id=1, source_target_pairs={{0,2},{2,0},{1,3},{3,1},{4,6},{6,4},{5,7},{7,5},{8,10},{10,8},{9,1... | collective-permute-start | bytes 786440 | tf_op jit(solution)/shard_map/ppermute | solution.py:694
  83.8 245.8 %reduce-scatter.3.cloned.1.call-start = ((), (), s32[]{:S(2)}) async-start(), calls=%async_computation.4 | async-start | bytes 2621440 | tf_op jit(solution)/shard_map/reduce_scatter | solution.py:809
  85.2 48.8 %collective-permute-start.21 = (bf16[1154,256]{1,0:T(8,128)(2,1)S(1)}, bf16[1154,256]{1,0:T(8,128)(2,1)S(1)}, u32[]{:S(2)}, u32[]{:S(2)}) collective-permute-start(bf16[1154,256]{1,0:T(8,128)(2,1)S(1)} %get-tuple-element.114), channel_id=1, source_target_pairs={{0,2},{2,0},{1,3},{3,1},{4,6},{6,4},{5,7},{7,5},{8,10},{10,8},{9,1... | collective-permute-start | bytes 1772552 | tf_op jit(solution)/shard_map/ppermute | solution.py:694
  134.5 48.9 %collective-permute-start.22 = (bf16[1184,512]{1,0:T(8,128)(2,1)S(1)}, bf16[1184,512]{1,0:T(8,128)(2,1)S(1)}, u32[]{:S(2)}, u32[]{:S(2)}) collective-permute-start(bf16[1184,512]{1,0:T(8,128)(2,1)S(1)} %bitcast.52), channel_id=1, source_target_pairs={{0,1},{1,0},{2,3},{3,2},{4,5},{5,4},{6,7},{7,6},{8,9},{9,8},{10,11... | collective-permute-start | bytes 3637256 | tf_op jit(solution)/shard_map/ppermute | solution.py:694
  134.6 26.4 %collective-permute-start.27 = (bf16[1024,512]{1,0:T(8,128)(2,1)}, bf16[1024,512]{1,0:T(8,128)(2,1)}, u32[]{:S(2)}, u32[]{:S(2)}) collective-permute-start(bf16[1024,512]{1,0:T(8,128)(2,1)} %all-gather.5.cloned.1.call-done.refs_0_), channel_id=1, source_target_pairs={{0,2},{2,0},{1,3},{3,1},{4,6},{6,4},{5,7},{7,5},{8,10},{10,8},{9,1... | collective-permute-start | bytes 3145736 | tf_op jit(solution)/shard_map/ppermute | solution.py:694
  135.1 28.5 %collective-permute-start.26 = (bf16[1024,512]{1,0:T(8,128)(2,1)}, bf16[1024,512]{1,0:T(8,128)(2,1)}, u32[]{:S(2)}, u32[]{:S(2)}) collective-permute-start(bf16[1024,512]{1,0:T(8,128)(2,1)} %all-gather.5.cloned.1.call-done.refs_0_), channel_id=1, source_target_pairs={{0,16},{16,0},{1,17},{17,1},{2,18},{18,2},{3,19},{19,3},{4,20},{20... | collective-permute-start | bytes 3145736 | tf_op jit(solution)/shard_map/ppermute | solution.py:694
  136.7 46.2 %collective-permute-start.23 = (bf16[1024,512]{1,0:T(8,128)(2,1)}, bf16[1024,512]{1,0:T(8,128)(2,1)}, u32[]{:S(2)}, u32[]{:S(2)}) collective-permute-start(bf16[1024,512]{1,0:T(8,128)(2,1)} %all-gather.3.cloned.1.call-done.refs_0_), channel_id=1, source_target_pairs={{0,2},{2,0},{1,3},{3,1},{4,6},{6,4},{5,7},{7,5},{8,10},{10,8},{9,1... | collective-permute-start | bytes 3145736 | tf_op jit(solution)/shard_map/ppermute | solution.py:694
  138.2 49.2 %collective-permute-start.20 = (bf16[1184,1024]{1,0:T(8,128)(2,1)}, bf16[1184,1024]{1,0:T(8,128)(2,1)}, u32[]{:S(2)}, u32[]{:S(2)}) collective-permute-start(bf16[1184,1024]{1,0:T(8,128)(2,1)} %convolution_convert_fusion.a_ref), channel_id=1, source_target_pairs={{0,1},{1,0},{2,3},{3,2},{4,5},{5,4},{6,7},{7,6},{8,9},{9,8},{10,11... | collective-permute-start | bytes 7274504 | tf_op jit(solution)/shard_map/ppermute | solution.py:694
  161.0 33.1 %collective-permute-start.24 = (bf16[1024,512]{1,0:T(8,128)(2,1)}, bf16[1024,512]{1,0:T(8,128)(2,1)}, u32[]{:S(2)}, u32[]{:S(2)}) collective-permute-start(bf16[1024,512]{1,0:T(8,128)(2,1)} %all-gather.3.cloned.1.call-done.refs_0_), channel_id=1, source_target_pairs={{0,16},{16,0},{1,17},{17,1},{2,18},{18,2},{3,19},{19,3},{4,20},{20... | collective-permute-start | bytes 3145736 | tf_op jit(solution)/shard_map/ppermute | solution.py:694
  163.6 83.0 %collective-permute-start.28 = (bf16[1024,256]{1,0:T(8,128)(2,1)S(1)}, bf16[1024,256]{1,0:T(8,128)(2,1)}, u32[]{:S(2)}, u32[]{:S(2)}) collective-permute-start(bf16[1024,256]{1,0:T(8,128)(2,1)S(1)} %slice.166), channel_id=1, source_target_pairs={{0,16},{16,0},{1,17},{17,1},{2,18},{18,2},{3,19},{19,3},{4,20},{20... | collective-permute-start | bytes 1572872 | tf_op jit(solution)/shard_map/ppermute | solution.py:694
  182.9 63.7 %collective-permute-start.29 = (bf16[1024,256]{1,0:T(8,128)(2,1)}, bf16[1024,256]{1,0:T(8,128)(2,1)}, u32[]{:S(2)}, u32[]{:S(2)}) collective-permute-start(bf16[1024,256]{1,0:T(8,128)(2,1)} %slice.167), channel_id=1, source_target_pairs={{0,2},{2,0},{1,3},{3,1},{4,6},{6,4},{5,7},{7,5},{8,10},{10,8},{9,1... | collective-permute-start | bytes 1572872 | tf_op jit(solution)/shard_map/ppermute | solution.py:694
  183.4 35.7 %collective-permute-start.25 = (bf16[1024,512]{1,0:T(8,128)(2,1)}, bf16[1024,512]{1,0:T(8,128)(2,1)}, u32[]{:S(2)}, u32[]{:S(2)}) collective-permute-start(bf16[1024,512]{1,0:T(8,128)(2,1)} %collective-permute-done.23.refs_1_), channel_id=1, source_target_pairs={{0,16},{16,0},{1,17},{17,1},{2,18},{18,2},{3,19},{19,3},{4,20},{20... | collective-permute-start | bytes 3145736 | tf_op jit(solution)/shard_map/ppermute | solution.py:694
  265.5 200.7 %reduce-scatter.5.cloned.1.call-start = ((), (), s32[]{:S(2)}) async-start(), calls=%async_computation.5 | async-start | bytes 2293760 | tf_op jit(solution)/shard_map/reduce_scatter | solution.py:829
  265.5 29.4 %collective-permute-start.32 = (bf16[1024,512]{1,0:T(8,128)(2,1)}, bf16[1024,512]{1,0:T(8,128)(2,1)}, u32[]{:S(2)}, u32[]{:S(2)}) collective-permute-start(bf16[1024,512]{1,0:T(8,128)(2,1)} %convolution_convert_fusion.6), channel_id=1, source_target_pairs={{0,16},{16,0},{1,17},{17,1},{2,18},{18,2},{3,19},{19,3},{4,20},{20... | collective-permute-start | bytes 3145736 | tf_op jit(solution)/shard_map/ppermute | solution.py:694
  274.6 39.3 %collective-permute-start.34 = (bf16[1024,512]{1,0:T(8,128)(2,1)}, bf16[1024,512]{1,0:T(8,128)(2,1)}, u32[]{:S(2)}, u32[]{:S(2)}) collective-permute-start(bf16[1024,512]{1,0:T(8,128)(2,1)} %convolution_convert_fusion.4), channel_id=1, source_target_pairs={{0,16},{16,0},{1,17},{17,1},{2,18},{18,2},{3,19},{19,3},{4,20},{20... | collective-permute-start | bytes 3145736 | tf_op jit(solution)/shard_map/ppermute | solution.py:694
  274.9 39.1 %collective-permute-start.33 = (bf16[1024,512]{1,0:T(8,128)(2,1)}, bf16[1024,512]{1,0:T(8,128)(2,1)}, u32[]{:S(2)}, u32[]{:S(2)}) collective-permute-start(bf16[1024,512]{1,0:T(8,128)(2,1)} %convolution_convert_fusion.5), channel_id=1, source_target_pairs={{0,2},{2,0},{1,3},{3,1},{4,6},{6,4},{5,7},{7,5},{8,10},{10,8},{9,1... | collective-permute-start | bytes 3145736 | tf_op jit(solution)/shard_map/ppermute | solution.py:694
  314.0 15.6 %collective-permute-start.36 = (bf16[1024,256]{1,0:T(8,128)(2,1)S(1)}, bf16[1024,256]{1,0:T(8,128)(2,1)S(1)}, u32[]{:S(2)}, u32[]{:S(2)}) collective-permute-start(bf16[1024,256]{1,0:T(8,128)(2,1)S(1)} %slice.169), channel_id=1, source_target_pairs={{0,16},{16,0},{1,17},{17,1},{2,18},{18,2},{3,19},{19,3},{4,20},{20... | collective-permute-start | bytes 1572872 | tf_op jit(solution)/shard_map/ppermute | solution.py:694
  327.1 63.4 %collective-permute-start.41 = (bf16[1024,256]{1,0:T(8,128)(2,1)}, bf16[1024,256]{1,0:T(8,128)(2,1)S(1)}, u32[]{:S(2)}, u32[]{:S(2)}) collective-permute-start(bf16[1024,256]{1,0:T(8,128)(2,1)} %slice.172), channel_id=1, source_target_pairs={{0,16},{16,0},{1,17},{17,1},{2,18},{18,2},{3,19},{19,3},{4,20},{20... | collective-permute-start | bytes 1572872 | tf_op jit(solution)/shard_map/ppermute | solution.py:694
  327.6 62.9 %collective-permute-start.40 = (bf16[1024,256]{1,0:T(8,128)(2,1)}, bf16[1024,256]{1,0:T(8,128)(2,1)S(1)}, u32[]{:S(2)}, u32[]{:S(2)}) collective-permute-start(bf16[1024,256]{1,0:T(8,128)(2,1)} %slice.171), channel_id=1, source_target_pairs={{0,2},{2,0},{1,3},{3,1},{4,6},{6,4},{5,7},{7,5},{8,10},{10,8},{9,1... | collective-permute-start | bytes 1572872 | tf_op jit(solution)/shard_map/ppermute | solution.py:694
  328.0 62.4 %collective-permute-start.42 = (bf16[1024,256]{1,0:T(8,128)(2,1)}, bf16[1024,256]{1,0:T(8,128)(2,1)S(1)}, u32[]{:S(2)}, u32[]{:S(2)}) collective-permute-start(bf16[1024,256]{1,0:T(8,128)(2,1)} %slice.173), channel_id=1, source_target_pairs={{0,2},{2,0},{1,3},{3,1},{4,6},{6,4},{5,7},{7,5},{8,10},{10,8},{9,1... | collective-permute-start | bytes 1572872 | tf_op jit(solution)/shard_map/ppermute | solution.py:694
  330.6 28.8 %collective-permute-start.37 = (bf16[256,512]{1,0:T(8,128)(2,1)S(1)}, bf16[256,512]{1,0:T(8,128)(2,1)S(1)}, u32[]{:S(2)}, u32[]{:S(2)}) collective-permute-start(bf16[256,512]{1,0:T(8,128)(2,1)S(1)} %slice.143), channel_id=1, source_target_pairs={{0,2},{2,0},{1,3},{3,1},{4,6},{6,4},{5,7},{7,5},{8,10},{10,8},{9,1... | collective-permute-start | bytes 786440 | tf_op jit(solution)/shard_map/ppermute | solution.py:694
  332.4 56.4 %collective-permute-start.43 = (bf16[1024,128]{1,0:T(8,128)(2,1)S(1)}, bf16[1024,128]{1,0:T(8,128)(2,1)S(1)}, u32[]{:S(2)}, u32[]{:S(2)}) collective-permute-start(bf16[1024,128]{1,0:T(8,128)(2,1)S(1)} %slice.174), channel_id=1, source_target_pairs={{0,2},{2,0},{1,3},{3,1},{4,6},{6,4},{5,7},{7,5},{8,10},{10,8},{9,1... | collective-permute-start | bytes 786440 | tf_op jit(solution)/shard_map/ppermute | solution.py:694
  407.9 20.7 %collective-permute-start.45 = (bf16[1024,384]{1,0:T(8,128)(2,1)}, bf16[1024,384]{1,0:T(8,128)(2,1)S(1)}, u32[]{:S(2)}, u32[]{:S(2)}) collective-permute-start(bf16[1024,384]{1,0:T(8,128)(2,1)} %add_convert_fusion.4), channel_id=1, source_target_pairs={{0,2},{2,0},{1,3},{3,1},{4,6},{6,4},{5,7},{7,5},{8,10},{10,8},{9,1... | collective-permute-start | bytes 2359304 | tf_op jit(solution)/shard_map/ppermute | solution.py:694
  409.4 20.0 %collective-permute-start.44 = (bf16[1024,384]{1,0:T(8,128)(2,1)}, bf16[1024,384]{1,0:T(8,128)(2,1)}, u32[]{:S(2)}, u32[]{:S(2)}) collective-permute-start(bf16[1024,384]{1,0:T(8,128)(2,1)} %add_convert_fusion.5), channel_id=1, source_target_pairs={{0,16},{16,0},{1,17},{17,1},{2,18},{18,2},{3,19},{19,3},{4,20},{20... | collective-permute-start | bytes 2359304 | tf_op jit(solution)/shard_map/ppermute | solution.py:694
  409.9 31.5 %collective-permute-start.35 = (bf16[1184,256]{1,0:T(8,128)(2,1)}, bf16[1184,256]{1,0:T(8,128)(2,1)}, u32[]{:S(2)}, u32[]{:S(2)}) collective-permute-start(bf16[1184,256]{1,0:T(8,128)(2,1)} %get-tuple-element.135), channel_id=1, source_target_pairs={{0,2},{2,0},{1,3},{3,1},{4,6},{6,4},{5,7},{7,5},{8,10},{10,8},{9,1... | collective-permute-start | bytes 1818632 | tf_op jit(solution)/shard_map/ppermute | solution.py:694
  430.8 15.9 %collective-permute-start.54 = (f32[12,256]{1,0:T(8,128)S(1)}, f32[12,256]{1,0:T(8,128)S(1)}, u32[]{:S(2)}, u32[]{:S(2)}) collective-permute-start(f32[12,256]{1,0:T(8,128)S(1)} %copy-done.48), channel_id=1, source_target_pairs={{0,2},{2,0},{1,3},{3,1},{4,6},{6,4},{5,7},{7,5},{8,10},{10,8},{9,1... | collective-permute-start | bytes 36872 | tf_op jit(solution)/shard_map/ppermute | solution.py:694
  441.4 21.5 %collective-permute-start.48 = (bf16[256,384]{1,0:T(8,128)(2,1)}, bf16[256,384]{1,0:T(8,128)(2,1)}, u32[]{:S(2)}, u32[]{:S(2)}) collective-permute-start(bf16[256,384]{1,0:T(8,128)(2,1)} %get-tuple-element.205), channel_id=1, source_target_pairs={{0,4},{4,8},{8,12},{12,0},{1,5},{5,9},{9,13},{13,1},{2,6},{6,10},{... | collective-permute-start | bytes 589832 | tf_op jit(solution)/shard_map/ppermute | solution.py:697
  441.4 22.1 %collective-permute-start.50 = (bf16[256,384]{1,0:T(8,128)(2,1)}, bf16[256,384]{1,0:T(8,128)(2,1)}, u32[]{:S(2)}, u32[]{:S(2)}) collective-permute-start(bf16[256,384]{1,0:T(8,128)(2,1)} %get-tuple-element.206), channel_id=1, source_target_pairs={{0,12},{4,0},{8,4},{12,8},{1,13},{5,1},{9,5},{13,9},{2,14},{6,2},{... | collective-permute-start | bytes 589832 | tf_op jit(solution)/shard_map/ppermute | solution.py:697
  445.2 18.3 %collective-permute-start.49 = (bf16[256,384]{1,0:T(8,128)(2,1)S(1)}, bf16[256,384]{1,0:T(8,128)(2,1)}, u32[]{:S(2)}, u32[]{:S(2)}) collective-permute-start(bf16[256,384]{1,0:T(8,128)(2,1)S(1)} %get-tuple-element.207), channel_id=1, source_target_pairs={{0,8},{4,12},{8,0},{12,4},{1,9},{5,13},{9,1},{13,5},{2,10},{6,14},... | collective-permute-start | bytes 589832 | tf_op jit(solution)/shard_map/ppermute | solution.py:697
  445.2 21.6 %collective-permute-start.47 = (bf16[1184,256]{1,0:T(8,128)(2,1)}, bf16[1184,256]{1,0:T(8,128)(2,1)}, u32[]{:S(2)}, u32[]{:S(2)}) collective-permute-start(bf16[1184,256]{1,0:T(8,128)(2,1)} %get-tuple-element.165), channel_id=1, source_target_pairs={{0,2},{2,0},{1,3},{3,1},{4,6},{6,4},{5,7},{7,5},{8,10},{10,8},{9,1... | collective-permute-start | bytes 1818632 | tf_op jit(solution)/shard_map/ppermute | solution.py:694
  462.8 24.2 %collective-permute-start.57 = (f32[12,256]{1,0:T(8,128)S(1)}, f32[12,256]{1,0:T(8,128)S(1)}, u32[]{:S(2)}, u32[]{:S(2)}) collective-permute-start(f32[12,256]{1,0:T(8,128)S(1)} %add.145.a_ref), channel_id=1, source_target_pairs={{0,16},{16,0},{1,17},{17,1},{2,18},{18,2},{3,19},{19,3},{4,20},{20... | collective-permute-start | bytes 36872 | tf_op jit(solution)/shard_map/ppermute | solution.py:694
  464.7 24.3 %collective-permute-start.51 = (bf16[256,384]{1,0:T(8,128)(2,1)S(1)}, bf16[256,384]{1,0:T(8,128)(2,1)}, u32[]{:S(2)}, u32[]{:S(2)}) collective-permute-start(bf16[256,384]{1,0:T(8,128)(2,1)S(1)} %add_convert_fusion.8.mine_ref), channel_id=1, source_target_pairs={{0,16},{16,0},{1,17},{17,1},{2,18},{18,2},{3,19},{19,3},{4,20},{20... | collective-permute-start | bytes 589832 | tf_op jit(solution)/shard_map/ppermute | solution.py:694
  466.2 17.8 %collective-permute-start.52 = (bf16[256,896]{1,0:T(8,128)(2,1)}, bf16[256,896]{1,0:T(8,128)(2,1)}, u32[]{:S(2)}, u32[]{:S(2)}) collective-permute-start(bf16[256,896]{1,0:T(8,128)(2,1)} %reduce-scatter.5.cloned.1.call-done.mine_ref), channel_id=1, source_target_pairs={{0,16},{16,0},{1,17},{17,1},{2,18},{18,2},{3,19},{19,3},{4,20},{20... | collective-permute-start | bytes 1376264 | tf_op jit(solution)/shard_map/ppermute | solution.py:694
  (70 other events, 935.2 us)
Sparse Core Ops, SparseCore 0:
  52.0 26.6 all-gather.4
  83.9 25.2 all-gather.2
  265.6 41.0 reduce-scatter.2
  408.0 36.9 reduce-scatter.4

commit v15 on v14

--- a/solution.py
+++ b/solution.py
@@ -878,9 +878,14 @@
         up_a, up_a_got, up_b, up_b_got, down_b, down_b_got, out_own, after(out_far_got, far_oth_v)
     )
     up_piece = same_half(scatter(up_sum))
+    lifted_one = mm_nt(
+        after(dqkv, up_sum), attn_weights[:, : 4 * three]
+    ).astype(BF16)
+    lifted_one_other = beside(lifted_one)
+
     near_oth = wide_add(
         mm_tn(wide_one, dqkv[:, 2 * three : 3 * three]),
-        jnp.pad(after(v_got, up_sum), ((0, 0), (cut, 0))),
+        jnp.pad(after(v_got, lifted_one), ((0, 0), (cut, 0))),
     )
     near_oth_got = over(near_oth)
     far_own = wide_add(
@@ -888,12 +893,7 @@
         jnp.pad(after(qk_got, near_oth), ((0, 0), (0, three - cut))),
     )
     far_own_got = across(far_own)
-    lifted_one = mm_nt(
-        after(dqkv, far_own), attn_weights[:, : 4 * three]
-    ).astype(BF16)
-    lifted_one_other = beside(lifted_one)
-
-    near_own = mm_tn(after(wide_one, lifted_one), dqkv[:, :three])
+    near_own = mm_tn(after(wide_one, far_own), dqkv[:, :three])
     input_mine, input_theirs, late_mine, late_theirs = last(
         place, wide_input, middle_grad, lifted_one, after(lifted_one_other, near_own), gain_one
     )

time: 503 us -> 512 us (1.018)
  transfers between devices with their start and end apart: 62 -> 62, of which waited for: 23 -> 24; matrix products, arithmetic and copies ran while one was open for 16% -> 16% of each run, Pallas kernels for 22% -> 21%
where the time goes in v15:
time: 512 us; the launch traced here: 506 us
  waiting for transfers between devices  200 us (39%)
  Pallas kernels  131 us (26%)
  starting transfers between devices  65.9 us (13%)
  matrix products  59.9 us (12%)
  local copies, waits for them, and re-layouts  20.9 us (4%)
  between operations  14.9 us (3%)
  other arithmetic  13.6 us (3%)
    ppermute x52, waiting for transfers between devices, swap(): return lax.ppermute(value, axis, [(at, at ^ bit) for at in range(size)])  183 us
    ppermute x52, starting transfers between devices, swap(): return lax.ppermute(value, axis, [(at, at ^ bit) for at in range(size)])  53.9 us
    dot_general x13, matrix products, mm_tn(): lax.dot_general(a, b, (((0,), (0,)), ((), ())), preferred_element_type=F32)  48.5 us
    pallas_call x2, Pallas kernels, mlp(): pl.pallas_call(functools.partial(mlp_kernel, bool(before), split), name='...  35.8 us
    pallas_call x1, Pallas kernels, attend_back(): pl.pallas_call(attend_back_kernel, grid=(pairs, held), name='attend_back'...  22.7 us
    ppermute x6, waiting for transfers between devices, shifted(): lax.ppermute(value, 'row', [(at, (at + shift) % n_row) for at in range(n_...  17.1 us
    pallas_call x2, Pallas kernels, attend(): pl.pallas_call(kernel, grid=(pairs // 2, held), name='attend', in_specs=[...  16.6 us
    pallas_call x1, Pallas kernels, turn(): pl.pallas_call(turn_kernel, name='turn', grid_spec=pltpu.PrefetchScalarGr...  14.3 us
  transfers between devices with their start and end apart: 62, of which 24 were waited for; matrix products, arithmetic and copies ran while one was open for 16% of the time, Pallas kernels for 21%

profile of v15, /device:TPU:0, one launch (start us, length us, event | category | flops | bytes accessed | tf_op | source)
XLA Modules:
  0.0 505.8 jit_solution(11461006450309547653)
XLA Ops:
  9.0 3.0 collective-permute-start
  12.8 3.7 collective-permute-start.1
  16.5 5.3 %collective-permute-done.1.refs_3_ = bf16[256,512]{1,0:T(8,128)(2,1)S(1)} collective-permute-done((bf16[256,512]{1,0:T(8,128)(2,1)S(1)}, bf16[256,512]{1,0:T(8,128)(2,1)S(1)}, u32[]{:S(2)}, u32[]{:S(2)}) %collective-permute-start.1) | collective-permute-done | bytes 262176 | tf_op jit(solution)/shard_map/ppermute | solution.py:697
  21.8 3.6 collective-permute-done
  29.6 2.6 collective-permute-start.7
  38.0 11.8 %collective-permute-done.7.refs_2_ = bf16[256,512]{1,0:T(8,128)(2,1)} collective-permute-done((bf16[256,512]{1,0:T(8,128)(2,1)S(1)}, bf16[256,512]{1,0:T(8,128)(2,1)}, u32[]{:S(2)}, u32[]{:S(2)}) %collective-permute-start.7) | collective-permute-done | bytes 262176 | tf_op jit(solution)/shard_map/ppermute | solution.py:697
  57.4 3.1 collective-permute-done.8.refs_4_
  61.0 9.3 %collective-permute-done.15.refs_11_ = bf16[256,512]{1,0:T(8,128)(2,1)} collective-permute-done((bf16[256,512]{1,0:T(8,128)(2,1)}, bf16[256,512]{1,0:T(8,128)(2,1)}, u32[]{:S(2)}, u32[]{:S(2)}) %collective-permute-start.15) | collective-permute-done | bytes 262176 | tf_op jit(solution)/shard_map/ppermute | solution.py:694
  73.6 2.2 collective-permute-done.13.refs_9_
  85.7 5.1 %collective-permute-done.11.refs_7_ = bf16[256,512]{1,0:T(8,128)(2,1)S(1)} collective-permute-done((bf16[256,512]{1,0:T(8,128)(2,1)S(1)}, bf16[256,512]{1,0:T(8,128)(2,1)S(1)}, u32[]{:S(2)}, u32[]{:S(2)}) %collective-permute-start.11) | collective-permute-done | bytes 262176 | tf_op jit(solution)/shard_map/ppermute | solution.py:694
  90.8 5.7 %collective-permute-done.17.refs_13_ = bf16[256,512]{1,0:T(8,128)(2,1)} collective-permute-done((bf16[256,512]{1,0:T(8,128)(2,1)S(1)}, bf16[256,512]{1,0:T(8,128)(2,1)}, u32[]{:S(2)}, u32[]{:S(2)}) %collective-permute-start.17) | collective-permute-done | bytes 262176 | tf_op jit(solution)/shard_map/ppermute | solution.py:694
  96.6 5.6 %collective-permute-done.19.refs_15_ = bf16[256,512]{1,0:T(8,128)(2,1)} collective-permute-done((bf16[256,512]{1,0:T(8,128)(2,1)}, bf16[256,512]{1,0:T(8,128)(2,1)}, u32[]{:S(2)}, u32[]{:S(2)}) %collective-permute-start.19) | collective-permute-done | bytes 262176 | tf_op jit(solution)/shard_map/ppermute | solution.py:694
  102.2 10.9 %norm_qkv.1 = (bf16[1184,1024]{1,0:T(8,128)(2,1)}, bf16[1184,1536]{1,0:T(8,128)(2,1)}, bf16[1024,2048]{1,0:T(8,128)(2,1)}) custom-call(s32[4]{0:T(128)} %pad_add_fusion.place_ref, bf16[1184,1024]{1,0:T(8,128)(2,1)} %pad_maximum_fusion.x_ref, f32[6,1,1024]{2,1,0:T(1,128)} %get-tuple-element.104.gain_ref.shift_ref.bias_ref, ...), custom_call_target="tpu_custom_call" | custom-call | flops 3724541952 | bytes 19398656 | tf_op jit(solution)/shard_map/norm_qkv/pallas_call | solution.py:114
  113.1 8.3 %attend.2 = (bf16[1184,512]{1,0:T(8,128)(2,1)}, bf16[2,8,592,592]{3,2,1,0:T(8,128)(2,1)}) custom-call(bf16[1184,1536]{1,0:T(8,128)(2,1)} %get-tuple-element.108.refs_0_.qkv_ref), custom_call_target="tpu_custom_call" | custom-call | flops 8613003264 | bytes 24248320 | tf_op jit(solution)/shard_map/attend/pallas_call | solution.py:160
  121.3 8.3 %attend.3 = (bf16[1184,512]{1,0:T(8,128)(2,1)}, bf16[2,8,592,592]{3,2,1,0:T(8,128)(2,1)}) custom-call(bf16[1184,1536]{1,0:T(8,128)(2,1)} %get-tuple-element.108.refs_0_.qkv_ref, bf16[1184,512]{1,0:T(8,128)(2,1)} %get-tuple-element.109.refs_1_, bf16[2,8,592,592]{3,2,1,0:T(8,128)(2,1)} %get-tuple-element.110.refs_2_), custom_call_target="tpu_custom_call", output_to_operand_aliasing={{0}: (1, {}), {1}: (2, {})} | custom-call | flops 8613003264 | bytes 24248320 | tf_op jit(solution)/shard_map/attend/pallas_call | solution.py:160
  129.6 4.4 convolution_convert_fusion.a_ref
  138.2 22.8 %collective-permute-done.27.refs_2_ = bf16[1024,512]{1,0:T(8,128)(2,1)} collective-permute-done((bf16[1024,512]{1,0:T(8,128)(2,1)}, bf16[1024,512]{1,0:T(8,128)(2,1)}, u32[]{:S(2)}, u32[]{:S(2)}) %collective-permute-start.27) | collective-permute-done | bytes 1048608 | tf_op jit(solution)/shard_map/ppermute | solution.py:694
  166.1 16.9 %collective-permute-done.23.refs_1_ = bf16[1024,512]{1,0:T(8,128)(2,1)} collective-permute-done((bf16[1024,512]{1,0:T(8,128)(2,1)}, bf16[1024,512]{1,0:T(8,128)(2,1)}, u32[]{:S(2)}, u32[]{:S(2)}) %collective-permute-start.23) | collective-permute-done | bytes 1048608 | tf_op jit(solution)/shard_map/ppermute | solution.py:694
  187.4 6.7 %middle.1 = (f32[1184,1024]{1,0:T(8,128)}, bf16[1184,1024]{1,0:T(8,128)(2,1)}) custom-call(bf16[1184,1024]{1,0:T(8,128)(2,1)} %pad_maximum_fusion.x_ref, bf16[1184,1024]{1,0:T(8,128)(2,1)} %convolution_convert_fusion.a_ref, bf16[1184,1024]{1,0:T(8,128)(2,1)} %collective-permute-done.20.b_ref, f32[6,1,1024]{2,1,0:T(1,128)} %get-tuple-element.104.gain_ref.shift_ref.bias_ref, ...), custom_call_target="tpu_custom_call" | custom-call | flops 24248320 | bytes 14548992 | tf_op jit(solution)/shard_map/middle/pallas_call | solution.py:227
  194.1 25.0 %collective-permute-done.25.refs_3_.refs_4_ = bf16[1024,512]{1,0:T(8,128)(2,1)} collective-permute-done((bf16[1024,512]{1,0:T(8,128)(2,1)}, bf16[1024,512]{1,0:T(8,128)(2,1)}, u32[]{:S(2)}, u32[]{:S(2)}) %collective-permute-start.25) | collective-permute-done | bytes 1048608 | tf_op jit(solution)/shard_map/ppermute | solution.py:694
  219.1 17.0 %mlp_first.1 = (bf16[1184,1024]{1,0:T(8,128)(2,1)}, bf16[1184,1024]{1,0:T(8,128)(2,1)}, f32[1,1024]{1,0:T(1,128)}, bf16[1184,1024]{1,0:T(8,128)(2,1)}, bf16[1184,1024]{1,0:T(8,128)(2,1)}) custom-call(s32[4]{0:T(128)} %pad_add_fusion.place_ref, bf16[1184,1024]{1,0:T(8,128)(2,1)} %get-tuple-element.121.n_ref, bf16[1184,1024]{1,0:T(8,128)(2,1)} %pad_maximum_fusion.1.dy_ref, ...), custom_call_target="tpu_custom_call" | custom-call | flops 9932111872 | bytes 24248320 | tf_op jit(solution)/shard_map/mlp_first/pallas_call | solution.py:318
  236.1 6.0 %convolution_convert_fusion.2 = bf16[1024,1024]{1,0:T(8,128)(2,1)} fusion(bf16[1184,1024]{1,0:T(8,128)(2,1)} %get-tuple-element.120, bf16[1184,256]{1,0:T(8,128)(2,1)S(1)} %get-tuple-element.196, bf16[1184,256]{1,0:T(8,128)(2,1)S(1)} %get-tuple-element.212, bf16[1184,256]{1,0:T(8,128)(2,1)S(1)} %get-tuple-element.195, ...), kind=kOutput, calls=%fused_computation.9 | convolution fusion | flops 2493775872 | bytes 6946816 | tf_op jit(solution)/shard_map/dot_general | solution.py:34
  242.0 4.5 convolution_convert_fusion.6
  246.6 18.8 %mlp_second.1 = (bf16[1184,1024]{1,0:T(8,128)(2,1)}, bf16[1184,1024]{1,0:T(8,128)(2,1)}, f32[1,1024]{1,0:T(1,128)}, f32[1184,512]{1,0:T(8,128)}, bf16[1184,512]{1,0:T(8,128)(2,1)}, /*index=5*/bf16[1184,1024]{1,0:T(8,128)(2,1)}) custom-call(s32[4]{0:T(128)} %pad_add_fusion.place_ref, bf16[1184,1024]{1,0:T(8,128)(2,1)} %get-tuple-element.121.n_ref, ...), custom_call_target="tpu_custom_call" | custom-call | flops 9932111872 | bytes 24248320 | tf_op jit(solution)/shard_map/mlp_second/pallas_call | solution.py:318
  267.4 4.7 convolution_convert_fusion.4
  272.1 2.5 convolution_convert_fusion.5
  276.8 14.3 %turn.1 = (f32[1184,1024]{1,0:T(8,128)}, bf16[1184,1024]{1,0:T(8,128)(2,1)}, bf16[1184,512]{1,0:T(8,128)(2,1)}, f32[4,1024]{1,0:T(4,128)}, bf16[1184,256]{1,0:T(8,128)(2,1)}, /*index=5*/bf16[1184,256]{1,0:T(8,128)(2,1)}) custom-call(s32[4]{0:T(128)} %pad_add_fusion.place_ref, f32[1184,1024]{1,0:T(8,128)} %get-tuple-element.113.h_ref, ...), custom_call_target="tpu_custom_call" | custom-call | flops 1241513984 | bytes 24248320 | tf_op jit(solution)/shard_map/turn/pallas_call | solution.py:377
  291.1 3.8 convolution_convert_fusion.3
  295.0 19.0 %collective-permute-done.34 = bf16[1024,512]{1,0:T(8,128)(2,1)} collective-permute-done((bf16[1024,512]{1,0:T(8,128)(2,1)}, bf16[1024,512]{1,0:T(8,128)(2,1)}, u32[]{:S(2)}, u32[]{:S(2)}) %collective-permute-start.34) | collective-permute-done | bytes 1048608 | tf_op jit(solution)/shard_map/ppermute | solution.py:694
  315.5 2.8 add_convert_fusion.2.refs_4_
  318.3 3.2 add_convert_fusion.1.refs_0_
  323.3 2.8 add_convert_fusion.refs_2_
  334.0 25.4 %collective-permute-done.37 = bf16[256,512]{1,0:T(8,128)(2,1)S(1)} collective-permute-done((bf16[256,512]{1,0:T(8,128)(2,1)S(1)}, bf16[256,512]{1,0:T(8,128)(2,1)S(1)}, u32[]{:S(2)}, u32[]{:S(2)}) %collective-permute-start.37) | collective-permute-done | bytes 262176 | tf_op jit(solution)/shard_map/ppermute | solution.py:694
  360.2 22.7 %attend_back.1 = (bf16[1184,1536]{1,0:T(8,128)(2,1)}, f32[1,1536]{1,0:T(1,128)}) custom-call(bf16[1184,1536]{1,0:T(8,128)(2,1)} %get-tuple-element.108.refs_0_.qkv_ref, bf16[2,8,592,592]{3,2,1,0:T(8,128)(2,1)} %get-tuple-element.137.p_ref, bf16[1184,512]{1,0:T(8,128)(2,1)} %get-tuple-element.144.g_ref), custom_call_target="tpu_custom_call" | custom-call | flops 21532508160 | bytes 60620800 | tf_op jit(solution)/shard_map/attend_back/pallas_call | solution.py:202
  383.0 3.6 convolution_convert_fusion.7
  390.4 4.3 join.1
  394.7 7.0 %convolution_convert_fusion.1.a_ref = bf16[1184,1024]{1,0:T(8,128)(2,1)S(1)} fusion(bf16[1184,1536]{1,0:T(8,128)(2,1)} %get-tuple-element.148, bf16[1024,2048]{1,0:T(8,128)(2,1)} %get-tuple-element.112.w_ref), kind=kOutput, calls=%fused_computation.1 | convolution fusion | flops 3725754368 | bytes 9207808 | tf_op jit(solution)/shard_map/dot_general | solution.py:30
  404.0 6.6 %collective-permute-done.39 = bf16[1024,128]{1,0:T(8,128)(2,1)S(1)} collective-permute-done((bf16[1024,128]{1,0:T(8,128)(2,1)S(1)}, bf16[1024,128]{1,0:T(8,128)(2,1)S(1)}, u32[]{:S(2)}, u32[]{:S(2)}) %collective-permute-start.39) | collective-permute-done | bytes 262176 | tf_op jit(solution)/shard_map/ppermute | solution.py:694
  410.6 4.4 add_convert_fusion.5
  416.4 3.6 add_convert_fusion.4
  423.7 4.6 fusion.8
  428.3 8.9 %last.1 = (f32[1184,256]{1,0:T(8,128)}, bf16[1184,256]{1,0:T(8,128)(2,1)}, f32[2,256]{1,0:T(2,128)}, f32[2,256]{1,0:T(2,128)}) custom-call(s32[4]{0:T(128)} %pad_add_fusion.place_ref, bf16[1184,1024]{1,0:T(8,128)(2,1)} %pad_maximum_fusion.x_ref, f32[1184,1024]{1,0:T(8,128)} %get-tuple-element.156.dh_ref, bf16[1184,1024]{1,0:T(8,128)(2,1)} %copy-done.3, ...), custom_call_target="tpu_custom_call" | custom-call | flops 24248320 | bytes 14548992 | tf_op jit(solution)/shard_map/last/pallas_call | solution.py:437
  444.6 7.9 %collective-permute-done.35 = bf16[1184,256]{1,0:T(8,128)(2,1)} collective-permute-done((bf16[1184,256]{1,0:T(8,128)(2,1)}, bf16[1184,256]{1,0:T(8,128)(2,1)}, u32[]{:S(2)}, u32[]{:S(2)}) %collective-permute-start.35) | collective-permute-done | bytes 606240 | tf_op jit(solution)/shard_map/ppermute | solution.py:694
  452.5 3.8 collective-permute-start.50
  459.7 5.0 collective-permute-done.55
  464.7 4.4 collective-permute-start.56
  480.4 11.8 %collective-permute-done.52.other_ref = bf16[256,896]{1,0:T(8,128)(2,1)} collective-permute-done((bf16[256,896]{1,0:T(8,128)(2,1)}, bf16[256,896]{1,0:T(8,128)(2,1)}, u32[]{:S(2)}, u32[]{:S(2)}) %collective-permute-start.52) | collective-permute-done | bytes 458784 | tf_op jit(solution)/shard_map/ppermute | solution.py:694
  492.1 3.0 place_mlp.1
  (281 shorter events, 100.0 us)
Async XLA Ops:
  7.2 127.4 %all-gather.5.cloned.1.call-start = ((), (), s32[]{:S(2)}) async-start(), calls=%async_computation.3 | async-start | bytes 1310720 | tf_op jit(solution)/shard_map/all_gather | solution.py:780
  9.0 16.4 %collective-permute-start = (bf16[1154,256]{1,0:T(8,128)(2,1)S(1)}, bf16[1154,256]{1,0:T(8,128)(2,1)S(1)}, u32[]{:S(2)}, u32[]{:S(2)}) collective-permute-start(bf16[1154,256]{1,0:T(8,128)(2,1)S(1)} %get-tuple-element.204), channel_id=1, source_target_pairs={{0,2},{2,0},{1,3},{3,1},{4,6},{6,4},{5,7},{7,5},{8,10},{10,8},{9,1... | collective-permute-start | bytes 1772552 | tf_op jit(solution)/shard_map/ppermute | solution.py:694
  25.9 29.6 %collective-permute-start.2 = (bf16[1184,512]{1,0:T(8,128)(2,1)S(1)}, bf16[1184,512]{1,0:T(8,128)(2,1)S(1)}, u32[]{:S(2)}, u32[]{:S(2)}) collective-permute-start(bf16[1184,512]{1,0:T(8,128)(2,1)S(1)} %bitcast.51), channel_id=1, source_target_pairs={{0,1},{1,0},{2,3},{3,2},{4,5},{5,4},{6,7},{7,6},{8,9},{9,8},{10,11... | collective-permute-start | bytes 3637256 | tf_op jit(solution)/shard_map/ppermute | solution.py:694
  27.4 24.6 %collective-permute-start.4 = (f32[12,256]{1,0:T(8,128)}, f32[12,256]{1,0:T(8,128)S(1)}, u32[]{:S(2)}, u32[]{:S(2)}) collective-permute-start(f32[12,256]{1,0:T(8,128)} %pack.1.own), channel_id=1, source_target_pairs={{0,1},{1,0},{2,3},{3,2},{4,5},{5,4},{6,7},{7,6},{8,9},{9,8},{10,11... | collective-permute-start | bytes 36872 | tf_op jit(solution)/shard_map/ppermute | solution.py:694
  29.6 20.2 %collective-permute-start.7 = (bf16[256,512]{1,0:T(8,128)(2,1)S(1)}, bf16[256,512]{1,0:T(8,128)(2,1)}, u32[]{:S(2)}, u32[]{:S(2)}) collective-permute-start(bf16[256,512]{1,0:T(8,128)(2,1)S(1)} %pad_maximum_fusion.6.refs_0_), channel_id=1, source_target_pairs={{0,8},{4,12},{8,0},{12,4},{1,9},{5,13},{9,1},{13,5},{2,10},{6,14},... | collective-permute-start | bytes 786440 | tf_op jit(solution)/shard_map/ppermute | solution.py:697
  32.2 19.1 %collective-permute-start.6 = (bf16[256,512]{1,0:T(8,128)(2,1)S(1)}, bf16[256,512]{1,0:T(8,128)(2,1)}, u32[]{:S(2)}, u32[]{:S(2)}) collective-permute-start(bf16[256,512]{1,0:T(8,128)(2,1)S(1)} %pad_maximum_fusion.6.refs_0_), channel_id=1, source_target_pairs={{0,4},{4,8},{8,12},{12,0},{1,5},{5,9},{9,13},{13,1},{2,6},{6,10},{... | collective-permute-start | bytes 786440 | tf_op jit(solution)/shard_map/ppermute | solution.py:697
  37.3 15.2 %collective-permute-start.5 = (f32[12,256]{1,0:T(8,128)S(1)}, f32[12,256]{1,0:T(8,128)S(1)}, u32[]{:S(2)}, u32[]{:S(2)}) collective-permute-start(f32[12,256]{1,0:T(8,128)S(1)} %collective-permute-done.3.far), channel_id=1, source_target_pairs={{0,1},{1,0},{2,3},{3,2},{4,5},{5,4},{6,7},{7,6},{8,9},{9,8},{10,11... | collective-permute-start | bytes 36872 | tf_op jit(solution)/shard_map/ppermute | solution.py:694
  49.8 26.5 %collective-permute-start.12 = (bf16[256,512]{1,0:T(8,128)(2,1)S(1)}, bf16[256,512]{1,0:T(8,128)(2,1)S(1)}, u32[]{:S(2)}, u32[]{:S(2)}) collective-permute-start(bf16[256,512]{1,0:T(8,128)(2,1)S(1)} %pad_maximum_fusion.6.refs_0_), channel_id=1, source_target_pairs={{0,16},{16,0},{1,17},{17,1},{2,18},{18,2},{3,19},{19,3},{4,20},{20... | collective-permute-start | bytes 786440 | tf_op jit(solution)/shard_map/ppermute | solution.py:694
  51.9 84.8 %all-gather.3.cloned.1.call-start = ((), (), s32[]{:S(2)}) async-start(), calls=%async_computation.2 | async-start | bytes 1310720 | tf_op jit(solution)/shard_map/all_gather | solution.py:780
  51.9 30.0 %collective-permute-start.14 = (bf16[256,512]{1,0:T(8,128)(2,1)}, bf16[256,512]{1,0:T(8,128)(2,1)}, u32[]{:S(2)}, u32[]{:S(2)}) collective-permute-start(bf16[256,512]{1,0:T(8,128)(2,1)} %collective-permute-done.7.refs_2_), channel_id=1, source_target_pairs={{0,16},{16,0},{1,17},{17,1},{2,18},{18,2},{3,19},{19,3},{4,20},{20... | collective-permute-start | bytes 786440 | tf_op jit(solution)/shard_map/ppermute | solution.py:694
  52.5 25.4 %collective-permute-start.10 = (bf16[256,512]{1,0:T(8,128)(2,1)}, bf16[256,512]{1,0:T(8,128)(2,1)}, u32[]{:S(2)}, u32[]{:S(2)}) collective-permute-start(bf16[256,512]{1,0:T(8,128)(2,1)} %collective-permute-done.7.refs_2_), channel_id=1, source_target_pairs={{0,2},{2,0},{1,3},{3,1},{4,6},{6,4},{5,7},{7,5},{8,10},{10,8},{9,1... | collective-permute-start | bytes 786440 | tf_op jit(solution)/shard_map/ppermute | solution.py:694
  55.5 14.8 %collective-permute-start.15 = (bf16[256,512]{1,0:T(8,128)(2,1)}, bf16[256,512]{1,0:T(8,128)(2,1)}, u32[]{:S(2)}, u32[]{:S(2)}) collective-permute-start(bf16[256,512]{1,0:T(8,128)(2,1)} %copy-done.39), channel_id=1, source_target_pairs={{0,16},{16,0},{1,17},{17,1},{2,18},{18,2},{3,19},{19,3},{4,20},{20... | collective-permute-start | bytes 786440 | tf_op jit(solution)/shard_map/ppermute | solution.py:694
  60.5 15.3 %collective-permute-start.13 = (bf16[256,512]{1,0:T(8,128)(2,1)}, bf16[256,512]{1,0:T(8,128)(2,1)S(1)}, u32[]{:S(2)}, u32[]{:S(2)}) collective-permute-start(bf16[256,512]{1,0:T(8,128)(2,1)} %collective-permute-done.6.refs_1_), channel_id=1, source_target_pairs={{0,16},{16,0},{1,17},{17,1},{2,18},{18,2},{3,19},{19,3},{4,20},{20... | collective-permute-start | bytes 786440 | tf_op jit(solution)/shard_map/ppermute | solution.py:694
  81.4 15.1 %collective-permute-start.17 = (bf16[256,512]{1,0:T(8,128)(2,1)S(1)}, bf16[256,512]{1,0:T(8,128)(2,1)}, u32[]{:S(2)}, u32[]{:S(2)}) collective-permute-start(bf16[256,512]{1,0:T(8,128)(2,1)S(1)} %collective-permute-done.13.refs_9_), channel_id=1, source_target_pairs={{0,2},{2,0},{1,3},{3,1},{4,6},{6,4},{5,7},{7,5},{8,10},{10,8},{9,1... | collective-permute-start | bytes 786440 | tf_op jit(solution)/shard_map/ppermute | solution.py:694
  81.9 20.2 %collective-permute-start.19 = (bf16[256,512]{1,0:T(8,128)(2,1)}, bf16[256,512]{1,0:T(8,128)(2,1)}, u32[]{:S(2)}, u32[]{:S(2)}) collective-permute-start(bf16[256,512]{1,0:T(8,128)(2,1)} %collective-permute-done.15.refs_11_), channel_id=1, source_target_pairs={{0,2},{2,0},{1,3},{3,1},{4,6},{6,4},{5,7},{7,5},{8,10},{10,8},{9,1... | collective-permute-start | bytes 786440 | tf_op jit(solution)/shard_map/ppermute | solution.py:694
  83.8 245.8 %reduce-scatter.3.cloned.1.call-start = ((), (), s32[]{:S(2)}) async-start(), calls=%async_computation.4 | async-start | bytes 2621440 | tf_op jit(solution)/shard_map/reduce_scatter | solution.py:809
  85.2 48.8 %collective-permute-start.21 = (bf16[1154,256]{1,0:T(8,128)(2,1)S(1)}, bf16[1154,256]{1,0:T(8,128)(2,1)S(1)}, u32[]{:S(2)}, u32[]{:S(2)}) collective-permute-start(bf16[1154,256]{1,0:T(8,128)(2,1)S(1)} %get-tuple-element.114), channel_id=1, source_target_pairs={{0,2},{2,0},{1,3},{3,1},{4,6},{6,4},{5,7},{7,5},{8,10},{10,8},{9,1... | collective-permute-start | bytes 1772552 | tf_op jit(solution)/shard_map/ppermute | solution.py:694
  134.5 48.9 %collective-permute-start.22 = (bf16[1184,512]{1,0:T(8,128)(2,1)S(1)}, bf16[1184,512]{1,0:T(8,128)(2,1)S(1)}, u32[]{:S(2)}, u32[]{:S(2)}) collective-permute-start(bf16[1184,512]{1,0:T(8,128)(2,1)S(1)} %bitcast.52), channel_id=1, source_target_pairs={{0,1},{1,0},{2,3},{3,2},{4,5},{5,4},{6,7},{7,6},{8,9},{9,8},{10,11... | collective-permute-start | bytes 3637256 | tf_op jit(solution)/shard_map/ppermute | solution.py:694
  134.6 26.4 %collective-permute-start.27 = (bf16[1024,512]{1,0:T(8,128)(2,1)}, bf16[1024,512]{1,0:T(8,128)(2,1)}, u32[]{:S(2)}, u32[]{:S(2)}) collective-permute-start(bf16[1024,512]{1,0:T(8,128)(2,1)} %all-gather.5.cloned.1.call-done.refs_0_), channel_id=1, source_target_pairs={{0,2},{2,0},{1,3},{3,1},{4,6},{6,4},{5,7},{7,5},{8,10},{10,8},{9,1... | collective-permute-start | bytes 3145736 | tf_op jit(solution)/shard_map/ppermute | solution.py:694
  135.1 28.5 %collective-permute-start.26 = (bf16[1024,512]{1,0:T(8,128)(2,1)}, bf16[1024,512]{1,0:T(8,128)(2,1)}, u32[]{:S(2)}, u32[]{:S(2)}) collective-permute-start(bf16[1024,512]{1,0:T(8,128)(2,1)} %all-gather.5.cloned.1.call-done.refs_0_), channel_id=1, source_target_pairs={{0,16},{16,0},{1,17},{17,1},{2,18},{18,2},{3,19},{19,3},{4,20},{20... | collective-permute-start | bytes 3145736 | tf_op jit(solution)/shard_map/ppermute | solution.py:694
  136.7 46.2 %collective-permute-start.23 = (bf16[1024,512]{1,0:T(8,128)(2,1)}, bf16[1024,512]{1,0:T(8,128)(2,1)}, u32[]{:S(2)}, u32[]{:S(2)}) collective-permute-start(bf16[1024,512]{1,0:T(8,128)(2,1)} %all-gather.3.cloned.1.call-done.refs_0_), channel_id=1, source_target_pairs={{0,2},{2,0},{1,3},{3,1},{4,6},{6,4},{5,7},{7,5},{8,10},{10,8},{9,1... | collective-permute-start | bytes 3145736 | tf_op jit(solution)/shard_map/ppermute | solution.py:694
  138.2 49.2 %collective-permute-start.20 = (bf16[1184,1024]{1,0:T(8,128)(2,1)}, bf16[1184,1024]{1,0:T(8,128)(2,1)}, u32[]{:S(2)}, u32[]{:S(2)}) collective-permute-start(bf16[1184,1024]{1,0:T(8,128)(2,1)} %convolution_convert_fusion.a_ref), channel_id=1, source_target_pairs={{0,1},{1,0},{2,3},{3,2},{4,5},{5,4},{6,7},{7,6},{8,9},{9,8},{10,11... | collective-permute-start | bytes 7274504 | tf_op jit(solution)/shard_map/ppermute | solution.py:694
  161.0 33.1 %collective-permute-start.24 = (bf16[1024,512]{1,0:T(8,128)(2,1)}, bf16[1024,512]{1,0:T(8,128)(2,1)}, u32[]{:S(2)}, u32[]{:S(2)}) collective-permute-start(bf16[1024,512]{1,0:T(8,128)(2,1)} %all-gather.3.cloned.1.call-done.refs_0_), channel_id=1, source_target_pairs={{0,16},{16,0},{1,17},{17,1},{2,18},{18,2},{3,19},{19,3},{4,20},{20... | collective-permute-start | bytes 3145736 | tf_op jit(solution)/shard_map/ppermute | solution.py:694
  163.6 83.0 %collective-permute-start.28 = (bf16[1024,256]{1,0:T(8,128)(2,1)S(1)}, bf16[1024,256]{1,0:T(8,128)(2,1)}, u32[]{:S(2)}, u32[]{:S(2)}) collective-permute-start(bf16[1024,256]{1,0:T(8,128)(2,1)S(1)} %slice.166), channel_id=1, source_target_pairs={{0,16},{16,0},{1,17},{17,1},{2,18},{18,2},{3,19},{19,3},{4,20},{20... | collective-permute-start | bytes 1572872 | tf_op jit(solution)/shard_map/ppermute | solution.py:694
  182.9 63.7 %collective-permute-start.29 = (bf16[1024,256]{1,0:T(8,128)(2,1)}, bf16[1024,256]{1,0:T(8,128)(2,1)}, u32[]{:S(2)}, u32[]{:S(2)}) collective-permute-start(bf16[1024,256]{1,0:T(8,128)(2,1)} %slice.167), channel_id=1, source_target_pairs={{0,2},{2,0},{1,3},{3,1},{4,6},{6,4},{5,7},{7,5},{8,10},{10,8},{9,1... | collective-permute-start | bytes 1572872 | tf_op jit(solution)/shard_map/ppermute | solution.py:694
  183.4 35.7 %collective-permute-start.25 = (bf16[1024,512]{1,0:T(8,128)(2,1)}, bf16[1024,512]{1,0:T(8,128)(2,1)}, u32[]{:S(2)}, u32[]{:S(2)}) collective-permute-start(bf16[1024,512]{1,0:T(8,128)(2,1)} %collective-permute-done.23.refs_1_), channel_id=1, source_target_pairs={{0,16},{16,0},{1,17},{17,1},{2,18},{18,2},{3,19},{19,3},{4,20},{20... | collective-permute-start | bytes 3145736 | tf_op jit(solution)/shard_map/ppermute | solution.py:694
  265.5 210.3 %reduce-scatter.5.cloned.1.call-start = ((), (), s32[]{:S(2)}) async-start(), calls=%async_computation.5 | async-start | bytes 2293760 | tf_op jit(solution)/shard_map/reduce_scatter | solution.py:829
  265.6 29.4 %collective-permute-start.32 = (bf16[1024,512]{1,0:T(8,128)(2,1)}, bf16[1024,512]{1,0:T(8,128)(2,1)}, u32[]{:S(2)}, u32[]{:S(2)}) collective-permute-start(bf16[1024,512]{1,0:T(8,128)(2,1)} %convolution_convert_fusion.6), channel_id=1, source_target_pairs={{0,16},{16,0},{1,17},{17,1},{2,18},{18,2},{3,19},{19,3},{4,20},{20... | collective-permute-start | bytes 3145736 | tf_op jit(solution)/shard_map/ppermute | solution.py:694
  274.7 39.3 %collective-permute-start.34 = (bf16[1024,512]{1,0:T(8,128)(2,1)}, bf16[1024,512]{1,0:T(8,128)(2,1)}, u32[]{:S(2)}, u32[]{:S(2)}) collective-permute-start(bf16[1024,512]{1,0:T(8,128)(2,1)} %convolution_convert_fusion.4), channel_id=1, source_target_pairs={{0,16},{16,0},{1,17},{17,1},{2,18},{18,2},{3,19},{19,3},{4,20},{20... | collective-permute-start | bytes 3145736 | tf_op jit(solution)/shard_map/ppermute | solution.py:694
  274.9 39.1 %collective-permute-start.33 = (bf16[1024,512]{1,0:T(8,128)(2,1)}, bf16[1024,512]{1,0:T(8,128)(2,1)}, u32[]{:S(2)}, u32[]{:S(2)}) collective-permute-start(bf16[1024,512]{1,0:T(8,128)(2,1)} %convolution_convert_fusion.5), channel_id=1, source_target_pairs={{0,2},{2,0},{1,3},{3,1},{4,6},{6,4},{5,7},{7,5},{8,10},{10,8},{9,1... | collective-permute-start | bytes 3145736 | tf_op jit(solution)/shard_map/ppermute | solution.py:694
  314.0 15.6 %collective-permute-start.36 = (bf16[1024,256]{1,0:T(8,128)(2,1)S(1)}, bf16[1024,256]{1,0:T(8,128)(2,1)S(1)}, u32[]{:S(2)}, u32[]{:S(2)}) collective-permute-start(bf16[1024,256]{1,0:T(8,128)(2,1)S(1)} %slice.169), channel_id=1, source_target_pairs={{0,16},{16,0},{1,17},{17,1},{2,18},{18,2},{3,19},{19,3},{4,20},{20... | collective-permute-start | bytes 1572872 | tf_op jit(solution)/shard_map/ppermute | solution.py:694
  327.1 61.4 %collective-permute-start.41 = (bf16[1024,256]{1,0:T(8,128)(2,1)}, bf16[1024,256]{1,0:T(8,128)(2,1)S(1)}, u32[]{:S(2)}, u32[]{:S(2)}) collective-permute-start(bf16[1024,256]{1,0:T(8,128)(2,1)} %slice.172), channel_id=1, source_target_pairs={{0,16},{16,0},{1,17},{17,1},{2,18},{18,2},{3,19},{19,3},{4,20},{20... | collective-permute-start | bytes 1572872 | tf_op jit(solution)/shard_map/ppermute | solution.py:694
  327.6 60.9 %collective-permute-start.40 = (bf16[1024,256]{1,0:T(8,128)(2,1)}, bf16[1024,256]{1,0:T(8,128)(2,1)S(1)}, u32[]{:S(2)}, u32[]{:S(2)}) collective-permute-start(bf16[1024,256]{1,0:T(8,128)(2,1)} %slice.171), channel_id=1, source_target_pairs={{0,2},{2,0},{1,3},{3,1},{4,6},{6,4},{5,7},{7,5},{8,10},{10,8},{9,1... | collective-permute-start | bytes 1572872 | tf_op jit(solution)/shard_map/ppermute | solution.py:694
  328.1 60.5 %collective-permute-start.42 = (bf16[1024,256]{1,0:T(8,128)(2,1)}, bf16[1024,256]{1,0:T(8,128)(2,1)S(1)}, u32[]{:S(2)}, u32[]{:S(2)}) collective-permute-start(bf16[1024,256]{1,0:T(8,128)(2,1)} %slice.173), channel_id=1, source_target_pairs={{0,2},{2,0},{1,3},{3,1},{4,6},{6,4},{5,7},{7,5},{8,10},{10,8},{9,1... | collective-permute-start | bytes 1572872 | tf_op jit(solution)/shard_map/ppermute | solution.py:694
  330.7 28.8 %collective-permute-start.37 = (bf16[256,512]{1,0:T(8,128)(2,1)S(1)}, bf16[256,512]{1,0:T(8,128)(2,1)S(1)}, u32[]{:S(2)}, u32[]{:S(2)}) collective-permute-start(bf16[256,512]{1,0:T(8,128)(2,1)S(1)} %slice.143), channel_id=1, source_target_pairs={{0,2},{2,0},{1,3},{3,1},{4,6},{6,4},{5,7},{7,5},{8,10},{10,8},{9,1... | collective-permute-start | bytes 786440 | tf_op jit(solution)/shard_map/ppermute | solution.py:694
  332.4 56.0 %collective-permute-start.43 = (bf16[1024,128]{1,0:T(8,128)(2,1)S(1)}, bf16[1024,128]{1,0:T(8,128)(2,1)S(1)}, u32[]{:S(2)}, u32[]{:S(2)}) collective-permute-start(bf16[1024,128]{1,0:T(8,128)(2,1)S(1)} %slice.174), channel_id=1, source_target_pairs={{0,2},{2,0},{1,3},{3,1},{4,6},{6,4},{5,7},{7,5},{8,10},{10,8},{9,1... | collective-permute-start | bytes 786440 | tf_op jit(solution)/shard_map/ppermute | solution.py:694
  401.7 26.6 %collective-permute-start.46 = (bf16[1184,1024]{1,0:T(8,128)(2,1)S(1)}, bf16[1184,1024]{1,0:T(8,128)(2,1)}, u32[]{:S(2)}, u32[]{:S(2)}) collective-permute-start(bf16[1184,1024]{1,0:T(8,128)(2,1)S(1)} %convolution_convert_fusion.1.a_ref), channel_id=1, source_target_pairs={{0,1},{1,0},{2,3},{3,2},{4,5},{5,4},{6,7},{7,6},{8,9},{9,8},{10,11... | collective-permute-start | bytes 7274504 | tf_op jit(solution)/shard_map/ppermute | solution.py:694
  420.1 20.6 %collective-permute-start.45 = (bf16[1024,384]{1,0:T(8,128)(2,1)}, bf16[1024,384]{1,0:T(8,128)(2,1)S(1)}, u32[]{:S(2)}, u32[]{:S(2)}) collective-permute-start(bf16[1024,384]{1,0:T(8,128)(2,1)} %add_convert_fusion.4), channel_id=1, source_target_pairs={{0,2},{2,0},{1,3},{3,1},{4,6},{6,4},{5,7},{7,5},{8,10},{10,8},{9,1... | collective-permute-start | bytes 2359304 | tf_op jit(solution)/shard_map/ppermute | solution.py:694
  421.6 19.1 %collective-permute-start.44 = (bf16[1024,384]{1,0:T(8,128)(2,1)}, bf16[1024,384]{1,0:T(8,128)(2,1)}, u32[]{:S(2)}, u32[]{:S(2)}) collective-permute-start(bf16[1024,384]{1,0:T(8,128)(2,1)} %add_convert_fusion.5), channel_id=1, source_target_pairs={{0,16},{16,0},{1,17},{17,1},{2,18},{18,2},{3,19},{19,3},{4,20},{20... | collective-permute-start | bytes 2359304 | tf_op jit(solution)/shard_map/ppermute | solution.py:694
  423.1 29.3 %collective-permute-start.35 = (bf16[1184,256]{1,0:T(8,128)(2,1)}, bf16[1184,256]{1,0:T(8,128)(2,1)}, u32[]{:S(2)}, u32[]{:S(2)}) collective-permute-start(bf16[1184,256]{1,0:T(8,128)(2,1)} %get-tuple-element.135), channel_id=1, source_target_pairs={{0,2},{2,0},{1,3},{3,1},{4,6},{6,4},{5,7},{7,5},{8,10},{10,8},{9,1... | collective-permute-start | bytes 1818632 | tf_op jit(solution)/shard_map/ppermute | solution.py:694
  442.2 15.7 %collective-permute-start.54 = (f32[12,256]{1,0:T(8,128)S(1)}, f32[12,256]{1,0:T(8,128)S(1)}, u32[]{:S(2)}, u32[]{:S(2)}) collective-permute-start(f32[12,256]{1,0:T(8,128)S(1)} %copy-done.48), channel_id=1, source_target_pairs={{0,2},{2,0},{1,3},{3,1},{4,6},{6,4},{5,7},{7,5},{8,10},{10,8},{9,1... | collective-permute-start | bytes 36872 | tf_op jit(solution)/shard_map/ppermute | solution.py:694
  452.5 20.0 %collective-permute-start.48 = (bf16[256,384]{1,0:T(8,128)(2,1)}, bf16[256,384]{1,0:T(8,128)(2,1)}, u32[]{:S(2)}, u32[]{:S(2)}) collective-permute-start(bf16[256,384]{1,0:T(8,128)(2,1)} %get-tuple-element.205), channel_id=1, source_target_pairs={{0,4},{4,8},{8,12},{12,0},{1,5},{5,9},{9,13},{13,1},{2,6},{6,10},{... | collective-permute-start | bytes 589832 | tf_op jit(solution)/shard_map/ppermute | solution.py:697
  452.5 20.5 %collective-permute-start.50 = (bf16[256,384]{1,0:T(8,128)(2,1)}, bf16[256,384]{1,0:T(8,128)(2,1)}, u32[]{:S(2)}, u32[]{:S(2)}) collective-permute-start(bf16[256,384]{1,0:T(8,128)(2,1)} %get-tuple-element.206), channel_id=1, source_target_pairs={{0,12},{4,0},{8,4},{12,8},{1,13},{5,1},{9,5},{13,9},{2,14},{6,2},{... | collective-permute-start | bytes 589832 | tf_op jit(solution)/shard_map/ppermute | solution.py:697
  456.3 16.7 %collective-permute-start.49 = (bf16[256,384]{1,0:T(8,128)(2,1)S(1)}, bf16[256,384]{1,0:T(8,128)(2,1)}, u32[]{:S(2)}, u32[]{:S(2)}) collective-permute-start(bf16[256,384]{1,0:T(8,128)(2,1)S(1)} %get-tuple-element.207), channel_id=1, source_target_pairs={{0,8},{4,12},{8,0},{12,4},{1,9},{5,13},{9,1},{13,5},{2,10},{6,14},... | collective-permute-start | bytes 589832 | tf_op jit(solution)/shard_map/ppermute | solution.py:697
  456.3 20.0 %collective-permute-start.47 = (bf16[1184,256]{1,0:T(8,128)(2,1)}, bf16[1184,256]{1,0:T(8,128)(2,1)}, u32[]{:S(2)}, u32[]{:S(2)}) collective-permute-start(bf16[1184,256]{1,0:T(8,128)(2,1)} %get-tuple-element.165), channel_id=1, source_target_pairs={{0,2},{2,0},{1,3},{3,1},{4,6},{6,4},{5,7},{7,5},{8,10},{10,8},{9,1... | collective-permute-start | bytes 1818632 | tf_op jit(solution)/shard_map/ppermute | solution.py:694
  472.5 22.7 %collective-permute-start.57 = (f32[12,256]{1,0:T(8,128)S(1)}, f32[12,256]{1,0:T(8,128)S(1)}, u32[]{:S(2)}, u32[]{:S(2)}) collective-permute-start(f32[12,256]{1,0:T(8,128)S(1)} %add.145.a_ref), channel_id=1, source_target_pairs={{0,16},{16,0},{1,17},{17,1},{2,18},{18,2},{3,19},{19,3},{4,20},{20... | collective-permute-start | bytes 36872 | tf_op jit(solution)/shard_map/ppermute | solution.py:694
  474.2 22.9 %collective-permute-start.51 = (bf16[256,384]{1,0:T(8,128)(2,1)S(1)}, bf16[256,384]{1,0:T(8,128)(2,1)}, u32[]{:S(2)}, u32[]{:S(2)}) collective-permute-start(bf16[256,384]{1,0:T(8,128)(2,1)S(1)} %add_convert_fusion.8.mine_ref), channel_id=1, source_target_pairs={{0,16},{16,0},{1,17},{17,1},{2,18},{18,2},{3,19},{19,3},{4,20},{20... | collective-permute-start | bytes 589832 | tf_op jit(solution)/shard_map/ppermute | solution.py:694
  475.9 16.3 %collective-permute-start.52 = (bf16[256,896]{1,0:T(8,128)(2,1)}, bf16[256,896]{1,0:T(8,128)(2,1)}, u32[]{:S(2)}, u32[]{:S(2)}) collective-permute-start(bf16[256,896]{1,0:T(8,128)(2,1)} %reduce-scatter.5.cloned.1.call-done.mine_ref), channel_id=1, source_target_pairs={{0,16},{16,0},{1,17},{17,1},{2,18},{18,2},{3,19},{19,3},{4,20},{20... | collective-permute-start | bytes 1376264 | tf_op jit(solution)/shard_map/ppermute | solution.py:694
  (69 other events, 951.8 us)
Sparse Core Ops, SparseCore 0:
  52.0 26.6 all-gather.4
  83.9 25.2 all-gather.2
  265.6 41.0 reduce-scatter.2
  401.9 36.9 reduce-scatter.4

commit v16 on v14

--- a/solution.py
+++ b/solution.py
@@ -335,16 +335,16 @@
 
 def turn_kernel(
     place_ref, h_ref, dy_ref, a_ref, b_ref, low_ref, other_ref, gain_ref, bias_ref, w_ref,
-    dh_ref, da_ref, do_ref, sums_ref, mine_ref, theirs_ref, held,
+    dh_ref, da_ref, do_ref, sums_ref, mine_ref, theirs_ref,
 ):
     h = h_ref[...]
-    held[...] = h + bias_ref[...]
     core, side = place_ref[0], place_ref[1]
     width = D // 4
     low = low_ref[...] + other_ref[...].astype(F32)
     for far in range(2):
         at = pl.ds(pl.multiple_of((2 * far + core) * width, width), width)
-        out = (held[:, at] + low[:, far * width : (far + 1) * width]).astype(BF16)
+        out = h_ref[:, at] + bias_ref[:, at] + low[:, far * width : (far + 1) * width]
+        out = out.astype(BF16)
 
         @pl.when(side == far)
         def _(out=out):
@@ -392,7 +392,6 @@
                 row_spec(width),
                 row_spec(width),
             ],
-            scratch_shapes=[pltpu.VMEM((TM, D), F32)],
         ),
         out_shape=[
             like((rows, D), F32),

time: 503 us -> 503 us (level)
  no operation moved by 1% of the time
where the time goes in v16:
time: 503 us; the launch traced here: 498 us
  waiting for transfers between devices  197 us (39%)
  Pallas kernels  131 us (26%)
  starting transfers between devices  64.1 us (13%)
  matrix products  56.3 us (11%)
  local copies, waits for them, and re-layouts  20.8 us (4%)
  between operations  14.9 us (3%)
  other arithmetic  13.5 us (3%)
    ppermute x52, waiting for transfers between devices, swap(): return lax.ppermute(value, axis, [(at, at ^ bit) for at in range(size)])  180 us
    ppermute x52, starting transfers between devices, swap(): return lax.ppermute(value, axis, [(at, at ^ bit) for at in range(size)])  52.1 us
    dot_general x13, matrix products, mm_tn(): lax.dot_general(a, b, (((0,), (0,)), ((), ())), preferred_element_type=F32)  47.6 us
    pallas_call x2, Pallas kernels, mlp(): pl.pallas_call(functools.partial(mlp_kernel, bool(before), split), name='...  35.8 us
    pallas_call x1, Pallas kernels, attend_back(): pl.pallas_call(attend_back_kernel, grid=(pairs, held), name='attend_back'...  22.7 us
    ppermute x6, waiting for transfers between devices, shifted(): lax.ppermute(value, 'row', [(at, (at + shift) % n_row) for at in range(n_...  17.1 us
    pallas_call x2, Pallas kernels, attend(): pl.pallas_call(kernel, grid=(pairs // 2, held), name='attend', in_specs=[...  16.6 us
    pallas_call x1, Pallas kernels, turn(): pl.pallas_call(turn_kernel, name='turn', grid_spec=pltpu.PrefetchScalarGr...  14.1 us
  transfers between devices with their start and end apart: 62, of which 23 were waited for; matrix products, arithmetic and copies ran while one was open for 16% of the time, Pallas kernels for 22%

profile of v16, /device:TPU:0, one launch (start us, length us, event | category | flops | bytes accessed | tf_op | source)
XLA Modules:
  0.0 497.7 jit_solution(11253665577445667012)
XLA Ops:
  9.0 3.0 collective-permute-start
  12.8 3.7 collective-permute-start.1
  16.5 5.3 %collective-permute-done.1.refs_3_ = bf16[256,512]{1,0:T(8,128)(2,1)S(1)} collective-permute-done((bf16[256,512]{1,0:T(8,128)(2,1)S(1)}, bf16[256,512]{1,0:T(8,128)(2,1)S(1)}, u32[]{:S(2)}, u32[]{:S(2)}) %collective-permute-start.1) | collective-permute-done | bytes 262176 | tf_op jit(solution)/shard_map/ppermute | solution.py:696
  21.8 3.6 collective-permute-done
  29.6 2.6 collective-permute-start.7
  38.0 11.8 %collective-permute-done.7.refs_2_ = bf16[256,512]{1,0:T(8,128)(2,1)} collective-permute-done((bf16[256,512]{1,0:T(8,128)(2,1)S(1)}, bf16[256,512]{1,0:T(8,128)(2,1)}, u32[]{:S(2)}, u32[]{:S(2)}) %collective-permute-start.7) | collective-permute-done | bytes 262176 | tf_op jit(solution)/shard_map/ppermute | solution.py:696
  57.4 3.1 collective-permute-done.8.refs_4_
  61.0 9.3 %collective-permute-done.15.refs_11_ = bf16[256,512]{1,0:T(8,128)(2,1)} collective-permute-done((bf16[256,512]{1,0:T(8,128)(2,1)}, bf16[256,512]{1,0:T(8,128)(2,1)}, u32[]{:S(2)}, u32[]{:S(2)}) %collective-permute-start.15) | collective-permute-done | bytes 262176 | tf_op jit(solution)/shard_map/ppermute | solution.py:693
  85.7 5.1 %collective-permute-done.11.refs_7_ = bf16[256,512]{1,0:T(8,128)(2,1)S(1)} collective-permute-done((bf16[256,512]{1,0:T(8,128)(2,1)S(1)}, bf16[256,512]{1,0:T(8,128)(2,1)S(1)}, u32[]{:S(2)}, u32[]{:S(2)}) %collective-permute-start.11) | collective-permute-done | bytes 262176 | tf_op jit(solution)/shard_map/ppermute | solution.py:693
  90.8 5.7 %collective-permute-done.17.refs_13_ = bf16[256,512]{1,0:T(8,128)(2,1)} collective-permute-done((bf16[256,512]{1,0:T(8,128)(2,1)S(1)}, bf16[256,512]{1,0:T(8,128)(2,1)}, u32[]{:S(2)}, u32[]{:S(2)}) %collective-permute-start.17) | collective-permute-done | bytes 262176 | tf_op jit(solution)/shard_map/ppermute | solution.py:693
  96.6 5.6 %collective-permute-done.19.refs_15_ = bf16[256,512]{1,0:T(8,128)(2,1)} collective-permute-done((bf16[256,512]{1,0:T(8,128)(2,1)}, bf16[256,512]{1,0:T(8,128)(2,1)}, u32[]{:S(2)}, u32[]{:S(2)}) %collective-permute-start.19) | collective-permute-done | bytes 262176 | tf_op jit(solution)/shard_map/ppermute | solution.py:693
  102.2 10.8 %norm_qkv.1 = (bf16[1184,1024]{1,0:T(8,128)(2,1)}, bf16[1184,1536]{1,0:T(8,128)(2,1)}, bf16[1024,2048]{1,0:T(8,128)(2,1)}) custom-call(s32[4]{0:T(128)} %pad_add_fusion.place_ref, bf16[1184,1024]{1,0:T(8,128)(2,1)} %pad_maximum_fusion.x_ref, f32[6,1,1024]{2,1,0:T(1,128)} %get-tuple-element.104.gain_ref.shift_ref.bias_ref, ...), custom_call_target="tpu_custom_call" | custom-call | flops 3724541952 | bytes 19398656 | tf_op jit(solution)/shard_map/norm_qkv/pallas_call | solution.py:114
  113.0 8.3 %attend.2 = (bf16[1184,512]{1,0:T(8,128)(2,1)}, bf16[2,8,592,592]{3,2,1,0:T(8,128)(2,1)}) custom-call(bf16[1184,1536]{1,0:T(8,128)(2,1)} %get-tuple-element.108.refs_0_.qkv_ref), custom_call_target="tpu_custom_call" | custom-call | flops 8613003264 | bytes 24248320 | tf_op jit(solution)/shard_map/attend/pallas_call | solution.py:160
  121.3 8.3 %attend.3 = (bf16[1184,512]{1,0:T(8,128)(2,1)}, bf16[2,8,592,592]{3,2,1,0:T(8,128)(2,1)}) custom-call(bf16[1184,1536]{1,0:T(8,128)(2,1)} %get-tuple-element.108.refs_0_.qkv_ref, bf16[1184,512]{1,0:T(8,128)(2,1)} %get-tuple-element.109.refs_1_, bf16[2,8,592,592]{3,2,1,0:T(8,128)(2,1)} %get-tuple-element.110.refs_2_), custom_call_target="tpu_custom_call", output_to_operand_aliasing={{0}: (1, {}), {1}: (2, {})} | custom-call | flops 8613003264 | bytes 24248320 | tf_op jit(solution)/shard_map/attend/pallas_call | solution.py:160
  129.6 4.4 convolution_convert_fusion.a_ref
  138.2 22.8 %collective-permute-done.27.refs_2_ = bf16[1024,512]{1,0:T(8,128)(2,1)} collective-permute-done((bf16[1024,512]{1,0:T(8,128)(2,1)}, bf16[1024,512]{1,0:T(8,128)(2,1)}, u32[]{:S(2)}, u32[]{:S(2)}) %collective-permute-start.27) | collective-permute-done | bytes 1048608 | tf_op jit(solution)/shard_map/ppermute | solution.py:693
  166.1 16.9 %collective-permute-done.23.refs_1_ = bf16[1024,512]{1,0:T(8,128)(2,1)} collective-permute-done((bf16[1024,512]{1,0:T(8,128)(2,1)}, bf16[1024,512]{1,0:T(8,128)(2,1)}, u32[]{:S(2)}, u32[]{:S(2)}) %collective-permute-start.23) | collective-permute-done | bytes 1048608 | tf_op jit(solution)/shard_map/ppermute | solution.py:693
  187.4 6.8 %middle.1 = (f32[1184,1024]{1,0:T(8,128)}, bf16[1184,1024]{1,0:T(8,128)(2,1)}) custom-call(bf16[1184,1024]{1,0:T(8,128)(2,1)} %pad_maximum_fusion.x_ref, bf16[1184,1024]{1,0:T(8,128)(2,1)} %convolution_convert_fusion.a_ref, bf16[1184,1024]{1,0:T(8,128)(2,1)} %collective-permute-done.20.b_ref, f32[6,1,1024]{2,1,0:T(1,128)} %get-tuple-element.104.gain_ref.shift_ref.bias_ref, ...), custom_call_target="tpu_custom_call" | custom-call | flops 24248320 | bytes 14548992 | tf_op jit(solution)/shard_map/middle/pallas_call | solution.py:227
  194.2 24.9 %collective-permute-done.25.refs_3_.refs_4_ = bf16[1024,512]{1,0:T(8,128)(2,1)} collective-permute-done((bf16[1024,512]{1,0:T(8,128)(2,1)}, bf16[1024,512]{1,0:T(8,128)(2,1)}, u32[]{:S(2)}, u32[]{:S(2)}) %collective-permute-start.25) | collective-permute-done | bytes 1048608 | tf_op jit(solution)/shard_map/ppermute | solution.py:693
  219.1 17.0 %mlp_first.1 = (bf16[1184,1024]{1,0:T(8,128)(2,1)}, bf16[1184,1024]{1,0:T(8,128)(2,1)}, f32[1,1024]{1,0:T(1,128)}, bf16[1184,1024]{1,0:T(8,128)(2,1)}, bf16[1184,1024]{1,0:T(8,128)(2,1)}) custom-call(s32[4]{0:T(128)} %pad_add_fusion.place_ref, bf16[1184,1024]{1,0:T(8,128)(2,1)} %get-tuple-element.121.n_ref, bf16[1184,1024]{1,0:T(8,128)(2,1)} %pad_maximum_fusion.1.dy_ref, ...), custom_call_target="tpu_custom_call" | custom-call | flops 9932111872 | bytes 24248320 | tf_op jit(solution)/shard_map/mlp_first/pallas_call | solution.py:318
  236.1 6.0 %convolution_convert_fusion.2 = bf16[1024,1024]{1,0:T(8,128)(2,1)} fusion(bf16[1184,1024]{1,0:T(8,128)(2,1)} %get-tuple-element.120, bf16[1184,256]{1,0:T(8,128)(2,1)S(1)} %get-tuple-element.196, bf16[1184,256]{1,0:T(8,128)(2,1)S(1)} %get-tuple-element.212, bf16[1184,256]{1,0:T(8,128)(2,1)S(1)} %get-tuple-element.195, ...), kind=kOutput, calls=%fused_computation.9 | convolution fusion | flops 2493775872 | bytes 6946816 | tf_op jit(solution)/shard_map/dot_general | solution.py:34
  242.0 4.5 convolution_convert_fusion.6
  246.6 18.8 %mlp_second.1 = (bf16[1184,1024]{1,0:T(8,128)(2,1)}, bf16[1184,1024]{1,0:T(8,128)(2,1)}, f32[1,1024]{1,0:T(1,128)}, f32[1184,512]{1,0:T(8,128)}, bf16[1184,512]{1,0:T(8,128)(2,1)}, /*index=5*/bf16[1184,1024]{1,0:T(8,128)(2,1)}) custom-call(s32[4]{0:T(128)} %pad_add_fusion.place_ref, bf16[1184,1024]{1,0:T(8,128)(2,1)} %get-tuple-element.121.n_ref, ...), custom_call_target="tpu_custom_call" | custom-call | flops 9932111872 | bytes 24248320 | tf_op jit(solution)/shard_map/mlp_second/pallas_call | solution.py:318
  267.4 4.7 convolution_convert_fusion.4
  272.1 2.5 convolution_convert_fusion.5
  276.8 14.1 %turn.1 = (f32[1184,1024]{1,0:T(8,128)}, bf16[1184,1024]{1,0:T(8,128)(2,1)}, bf16[1184,512]{1,0:T(8,128)(2,1)}, f32[4,1024]{1,0:T(4,128)}, bf16[1184,256]{1,0:T(8,128)(2,1)}, /*index=5*/bf16[1184,256]{1,0:T(8,128)(2,1)}) custom-call(s32[4]{0:T(128)} %pad_add_fusion.place_ref, f32[1184,1024]{1,0:T(8,128)} %get-tuple-element.113.h_ref, ...), custom_call_target="tpu_custom_call" | custom-call | flops 1241513984 | bytes 24248320 | tf_op jit(solution)/shard_map/turn/pallas_call | solution.py:377
  290.9 3.7 convolution_convert_fusion.3
  294.7 19.2 %collective-permute-done.34 = bf16[1024,512]{1,0:T(8,128)(2,1)} collective-permute-done((bf16[1024,512]{1,0:T(8,128)(2,1)}, bf16[1024,512]{1,0:T(8,128)(2,1)}, u32[]{:S(2)}, u32[]{:S(2)}) %collective-permute-start.34) | collective-permute-done | bytes 1048608 | tf_op jit(solution)/shard_map/ppermute | solution.py:693
  315.5 2.8 add_convert_fusion.2.refs_4_
  318.3 3.2 add_convert_fusion.1.refs_0_
  323.3 2.8 add_convert_fusion.refs_2_
  334.0 25.4 %collective-permute-done.37 = bf16[256,512]{1,0:T(8,128)(2,1)S(1)} collective-permute-done((bf16[256,512]{1,0:T(8,128)(2,1)S(1)}, bf16[256,512]{1,0:T(8,128)(2,1)S(1)}, u32[]{:S(2)}, u32[]{:S(2)}) %collective-permute-start.37) | collective-permute-done | bytes 262176 | tf_op jit(solution)/shard_map/ppermute | solution.py:693
  360.2 22.7 %attend_back.1 = (bf16[1184,1536]{1,0:T(8,128)(2,1)}, f32[1,1536]{1,0:T(1,128)}) custom-call(bf16[1184,1536]{1,0:T(8,128)(2,1)} %get-tuple-element.108.refs_0_.qkv_ref, bf16[2,8,592,592]{3,2,1,0:T(8,128)(2,1)} %get-tuple-element.137.p_ref, bf16[1184,512]{1,0:T(8,128)(2,1)} %get-tuple-element.144.g_ref), custom_call_target="tpu_custom_call" | custom-call | flops 21532508160 | bytes 60620800 | tf_op jit(solution)/shard_map/attend_back/pallas_call | solution.py:202
  382.9 2.9 convolution_convert_fusion.7
  385.8 2.6 convolution_convert_fusion.8
  392.2 4.3 join.1
  396.6 4.5 add_convert_fusion.5
  401.1 2.4 add_convert_fusion.4
  403.5 4.3 convolution_convert_fusion.1.a_ref
  410.4 4.9 fusion.8
  415.4 9.0 %last.1 = (f32[1184,256]{1,0:T(8,128)}, bf16[1184,256]{1,0:T(8,128)(2,1)}, f32[2,256]{1,0:T(2,128)}, f32[2,256]{1,0:T(2,128)}) custom-call(s32[4]{0:T(128)} %pad_add_fusion.place_ref, bf16[1184,1024]{1,0:T(8,128)(2,1)} %pad_maximum_fusion.x_ref, f32[1184,1024]{1,0:T(8,128)} %get-tuple-element.156.dh_ref, bf16[1184,1024]{1,0:T(8,128)(2,1)} %copy-done.4, ...), custom_call_target="tpu_custom_call" | custom-call | flops 24248320 | bytes 14548992 | tf_op jit(solution)/shard_map/last/pallas_call | solution.py:436
  425.8 2.8 collective-permute-done.45
  432.4 9.0 %collective-permute-done.35 = bf16[1184,256]{1,0:T(8,128)(2,1)} collective-permute-done((bf16[1184,256]{1,0:T(8,128)(2,1)}, bf16[1184,256]{1,0:T(8,128)(2,1)}, u32[]{:S(2)}, u32[]{:S(2)}) %collective-permute-start.35) | collective-permute-done | bytes 606240 | tf_op jit(solution)/shard_map/ppermute | solution.py:693
  441.4 3.8 collective-permute-start.50
  448.6 5.9 %collective-permute-done.55 = f32[12,256]{1,0:T(8,128)S(1)} collective-permute-done((f32[12,256]{1,0:T(8,128)S(1)}, f32[12,256]{1,0:T(8,128)S(1)}, u32[]{:S(2)}, u32[]{:S(2)}) %collective-permute-start.55) | collective-permute-done | bytes 12320 | tf_op jit(solution)/shard_map/ppermute | solution.py:693
  454.5 4.6 collective-permute-start.56
  470.9 13.2 %collective-permute-done.52.other_ref = bf16[256,896]{1,0:T(8,128)(2,1)} collective-permute-done((bf16[256,896]{1,0:T(8,128)(2,1)}, bf16[256,896]{1,0:T(8,128)(2,1)}, u32[]{:S(2)}, u32[]{:S(2)}) %collective-permute-start.52) | collective-permute-done | bytes 458784 | tf_op jit(solution)/shard_map/ppermute | solution.py:693
  484.1 3.0 place_mlp.1
  (283 shorter events, 96.2 us)
Async XLA Ops:
  7.2 127.3 %all-gather.5.cloned.1.call-start = ((), (), s32[]{:S(2)}) async-start(), calls=%async_computation.3 | async-start | bytes 1310720 | tf_op jit(solution)/shard_map/all_gather | solution.py:779
  9.0 16.4 %collective-permute-start = (bf16[1154,256]{1,0:T(8,128)(2,1)S(1)}, bf16[1154,256]{1,0:T(8,128)(2,1)S(1)}, u32[]{:S(2)}, u32[]{:S(2)}) collective-permute-start(bf16[1154,256]{1,0:T(8,128)(2,1)S(1)} %get-tuple-element.204), channel_id=1, source_target_pairs={{0,2},{2,0},{1,3},{3,1},{4,6},{6,4},{5,7},{7,5},{8,10},{10,8},{9,1... | collective-permute-start | bytes 1772552 | tf_op jit(solution)/shard_map/ppermute | solution.py:693
  25.9 29.6 %collective-permute-start.2 = (bf16[1184,512]{1,0:T(8,128)(2,1)S(1)}, bf16[1184,512]{1,0:T(8,128)(2,1)S(1)}, u32[]{:S(2)}, u32[]{:S(2)}) collective-permute-start(bf16[1184,512]{1,0:T(8,128)(2,1)S(1)} %bitcast.51), channel_id=1, source_target_pairs={{0,1},{1,0},{2,3},{3,2},{4,5},{5,4},{6,7},{7,6},{8,9},{9,8},{10,11... | collective-permute-start | bytes 3637256 | tf_op jit(solution)/shard_map/ppermute | solution.py:693
  27.4 24.6 %collective-permute-start.4 = (f32[12,256]{1,0:T(8,128)}, f32[12,256]{1,0:T(8,128)S(1)}, u32[]{:S(2)}, u32[]{:S(2)}) collective-permute-start(f32[12,256]{1,0:T(8,128)} %pack.1.own), channel_id=1, source_target_pairs={{0,1},{1,0},{2,3},{3,2},{4,5},{5,4},{6,7},{7,6},{8,9},{9,8},{10,11... | collective-permute-start | bytes 36872 | tf_op jit(solution)/shard_map/ppermute | solution.py:693
  29.6 20.2 %collective-permute-start.7 = (bf16[256,512]{1,0:T(8,128)(2,1)S(1)}, bf16[256,512]{1,0:T(8,128)(2,1)}, u32[]{:S(2)}, u32[]{:S(2)}) collective-permute-start(bf16[256,512]{1,0:T(8,128)(2,1)S(1)} %pad_maximum_fusion.6.refs_0_), channel_id=1, source_target_pairs={{0,8},{4,12},{8,0},{12,4},{1,9},{5,13},{9,1},{13,5},{2,10},{6,14},... | collective-permute-start | bytes 786440 | tf_op jit(solution)/shard_map/ppermute | solution.py:696
  32.2 19.1 %collective-permute-start.6 = (bf16[256,512]{1,0:T(8,128)(2,1)S(1)}, bf16[256,512]{1,0:T(8,128)(2,1)}, u32[]{:S(2)}, u32[]{:S(2)}) collective-permute-start(bf16[256,512]{1,0:T(8,128)(2,1)S(1)} %pad_maximum_fusion.6.refs_0_), channel_id=1, source_target_pairs={{0,4},{4,8},{8,12},{12,0},{1,5},{5,9},{9,13},{13,1},{2,6},{6,10},{... | collective-permute-start | bytes 786440 | tf_op jit(solution)/shard_map/ppermute | solution.py:696
  37.3 15.2 %collective-permute-start.5 = (f32[12,256]{1,0:T(8,128)S(1)}, f32[12,256]{1,0:T(8,128)S(1)}, u32[]{:S(2)}, u32[]{:S(2)}) collective-permute-start(f32[12,256]{1,0:T(8,128)S(1)} %collective-permute-done.3.far), channel_id=1, source_target_pairs={{0,1},{1,0},{2,3},{3,2},{4,5},{5,4},{6,7},{7,6},{8,9},{9,8},{10,11... | collective-permute-start | bytes 36872 | tf_op jit(solution)/shard_map/ppermute | solution.py:693
  49.8 26.5 %collective-permute-start.12 = (bf16[256,512]{1,0:T(8,128)(2,1)S(1)}, bf16[256,512]{1,0:T(8,128)(2,1)S(1)}, u32[]{:S(2)}, u32[]{:S(2)}) collective-permute-start(bf16[256,512]{1,0:T(8,128)(2,1)S(1)} %pad_maximum_fusion.6.refs_0_), channel_id=1, source_target_pairs={{0,16},{16,0},{1,17},{17,1},{2,18},{18,2},{3,19},{19,3},{4,20},{20... | collective-permute-start | bytes 786440 | tf_op jit(solution)/shard_map/ppermute | solution.py:693
  51.9 84.8 %all-gather.3.cloned.1.call-start = ((), (), s32[]{:S(2)}) async-start(), calls=%async_computation.2 | async-start | bytes 1310720 | tf_op jit(solution)/shard_map/all_gather | solution.py:779
  51.9 30.0 %collective-permute-start.14 = (bf16[256,512]{1,0:T(8,128)(2,1)}, bf16[256,512]{1,0:T(8,128)(2,1)}, u32[]{:S(2)}, u32[]{:S(2)}) collective-permute-start(bf16[256,512]{1,0:T(8,128)(2,1)} %collective-permute-done.7.refs_2_), channel_id=1, source_target_pairs={{0,16},{16,0},{1,17},{17,1},{2,18},{18,2},{3,19},{19,3},{4,20},{20... | collective-permute-start | bytes 786440 | tf_op jit(solution)/shard_map/ppermute | solution.py:693
  52.5 25.4 %collective-permute-start.10 = (bf16[256,512]{1,0:T(8,128)(2,1)}, bf16[256,512]{1,0:T(8,128)(2,1)}, u32[]{:S(2)}, u32[]{:S(2)}) collective-permute-start(bf16[256,512]{1,0:T(8,128)(2,1)} %collective-permute-done.7.refs_2_), channel_id=1, source_target_pairs={{0,2},{2,0},{1,3},{3,1},{4,6},{6,4},{5,7},{7,5},{8,10},{10,8},{9,1... | collective-permute-start | bytes 786440 | tf_op jit(solution)/shard_map/ppermute | solution.py:693
  55.5 14.8 %collective-permute-start.15 = (bf16[256,512]{1,0:T(8,128)(2,1)}, bf16[256,512]{1,0:T(8,128)(2,1)}, u32[]{:S(2)}, u32[]{:S(2)}) collective-permute-start(bf16[256,512]{1,0:T(8,128)(2,1)} %copy-done.39), channel_id=1, source_target_pairs={{0,16},{16,0},{1,17},{17,1},{2,18},{18,2},{3,19},{19,3},{4,20},{20... | collective-permute-start | bytes 786440 | tf_op jit(solution)/shard_map/ppermute | solution.py:693
  60.5 15.3 %collective-permute-start.13 = (bf16[256,512]{1,0:T(8,128)(2,1)}, bf16[256,512]{1,0:T(8,128)(2,1)S(1)}, u32[]{:S(2)}, u32[]{:S(2)}) collective-permute-start(bf16[256,512]{1,0:T(8,128)(2,1)} %collective-permute-done.6.refs_1_), channel_id=1, source_target_pairs={{0,16},{16,0},{1,17},{17,1},{2,18},{18,2},{3,19},{19,3},{4,20},{20... | collective-permute-start | bytes 786440 | tf_op jit(solution)/shard_map/ppermute | solution.py:693
  76.3 14.5 %collective-permute-start.11 = (bf16[256,512]{1,0:T(8,128)(2,1)S(1)}, bf16[256,512]{1,0:T(8,128)(2,1)S(1)}, u32[]{:S(2)}, u32[]{:S(2)}) collective-permute-start(bf16[256,512]{1,0:T(8,128)(2,1)S(1)} %copy-done.40), channel_id=1, source_target_pairs={{0,2},{2,0},{1,3},{3,1},{4,6},{6,4},{5,7},{7,5},{8,10},{10,8},{9,1... | collective-permute-start | bytes 786440 | tf_op jit(solution)/shard_map/ppermute | solution.py:693
  81.4 15.1 %collective-permute-start.17 = (bf16[256,512]{1,0:T(8,128)(2,1)S(1)}, bf16[256,512]{1,0:T(8,128)(2,1)}, u32[]{:S(2)}, u32[]{:S(2)}) collective-permute-start(bf16[256,512]{1,0:T(8,128)(2,1)S(1)} %collective-permute-done.13.refs_9_), channel_id=1, source_target_pairs={{0,2},{2,0},{1,3},{3,1},{4,6},{6,4},{5,7},{7,5},{8,10},{10,8},{9,1... | collective-permute-start | bytes 786440 | tf_op jit(solution)/shard_map/ppermute | solution.py:693
  81.9 20.2 %collective-permute-start.19 = (bf16[256,512]{1,0:T(8,128)(2,1)}, bf16[256,512]{1,0:T(8,128)(2,1)}, u32[]{:S(2)}, u32[]{:S(2)}) collective-permute-start(bf16[256,512]{1,0:T(8,128)(2,1)} %collective-permute-done.15.refs_11_), channel_id=1, source_target_pairs={{0,2},{2,0},{1,3},{3,1},{4,6},{6,4},{5,7},{7,5},{8,10},{10,8},{9,1... | collective-permute-start | bytes 786440 | tf_op jit(solution)/shard_map/ppermute | solution.py:693
  83.8 245.8 %reduce-scatter.3.cloned.1.call-start = ((), (), s32[]{:S(2)}) async-start(), calls=%async_computation.4 | async-start | bytes 2621440 | tf_op jit(solution)/shard_map/reduce_scatter | solution.py:808
  85.2 48.8 %collective-permute-start.21 = (bf16[1154,256]{1,0:T(8,128)(2,1)S(1)}, bf16[1154,256]{1,0:T(8,128)(2,1)S(1)}, u32[]{:S(2)}, u32[]{:S(2)}) collective-permute-start(bf16[1154,256]{1,0:T(8,128)(2,1)S(1)} %get-tuple-element.114), channel_id=1, source_target_pairs={{0,2},{2,0},{1,3},{3,1},{4,6},{6,4},{5,7},{7,5},{8,10},{10,8},{9,1... | collective-permute-start | bytes 1772552 | tf_op jit(solution)/shard_map/ppermute | solution.py:693
  134.5 48.9 %collective-permute-start.22 = (bf16[1184,512]{1,0:T(8,128)(2,1)S(1)}, bf16[1184,512]{1,0:T(8,128)(2,1)S(1)}, u32[]{:S(2)}, u32[]{:S(2)}) collective-permute-start(bf16[1184,512]{1,0:T(8,128)(2,1)S(1)} %bitcast.52), channel_id=1, source_target_pairs={{0,1},{1,0},{2,3},{3,2},{4,5},{5,4},{6,7},{7,6},{8,9},{9,8},{10,11... | collective-permute-start | bytes 3637256 | tf_op jit(solution)/shard_map/ppermute | solution.py:693
  134.6 26.4 %collective-permute-start.27 = (bf16[1024,512]{1,0:T(8,128)(2,1)}, bf16[1024,512]{1,0:T(8,128)(2,1)}, u32[]{:S(2)}, u32[]{:S(2)}) collective-permute-start(bf16[1024,512]{1,0:T(8,128)(2,1)} %all-gather.5.cloned.1.call-done.refs_0_), channel_id=1, source_target_pairs={{0,2},{2,0},{1,3},{3,1},{4,6},{6,4},{5,7},{7,5},{8,10},{10,8},{9,1... | collective-permute-start | bytes 3145736 | tf_op jit(solution)/shard_map/ppermute | solution.py:693
  135.1 28.5 %collective-permute-start.26 = (bf16[1024,512]{1,0:T(8,128)(2,1)}, bf16[1024,512]{1,0:T(8,128)(2,1)}, u32[]{:S(2)}, u32[]{:S(2)}) collective-permute-start(bf16[1024,512]{1,0:T(8,128)(2,1)} %all-gather.5.cloned.1.call-done.refs_0_), channel_id=1, source_target_pairs={{0,16},{16,0},{1,17},{17,1},{2,18},{18,2},{3,19},{19,3},{4,20},{20... | collective-permute-start | bytes 3145736 | tf_op jit(solution)/shard_map/ppermute | solution.py:693
  136.7 46.2 %collective-permute-start.23 = (bf16[1024,512]{1,0:T(8,128)(2,1)}, bf16[1024,512]{1,0:T(8,128)(2,1)}, u32[]{:S(2)}, u32[]{:S(2)}) collective-permute-start(bf16[1024,512]{1,0:T(8,128)(2,1)} %all-gather.3.cloned.1.call-done.refs_0_), channel_id=1, source_target_pairs={{0,2},{2,0},{1,3},{3,1},{4,6},{6,4},{5,7},{7,5},{8,10},{10,8},{9,1... | collective-permute-start | bytes 3145736 | tf_op jit(solution)/shard_map/ppermute | solution.py:693
  138.2 49.2 %collective-permute-start.20 = (bf16[1184,1024]{1,0:T(8,128)(2,1)}, bf16[1184,1024]{1,0:T(8,128)(2,1)}, u32[]{:S(2)}, u32[]{:S(2)}) collective-permute-start(bf16[1184,1024]{1,0:T(8,128)(2,1)} %convolution_convert_fusion.a_ref), channel_id=1, source_target_pairs={{0,1},{1,0},{2,3},{3,2},{4,5},{5,4},{6,7},{7,6},{8,9},{9,8},{10,11... | collective-permute-start | bytes 7274504 | tf_op jit(solution)/shard_map/ppermute | solution.py:693
  161.0 33.1 %collective-permute-start.24 = (bf16[1024,512]{1,0:T(8,128)(2,1)}, bf16[1024,512]{1,0:T(8,128)(2,1)}, u32[]{:S(2)}, u32[]{:S(2)}) collective-permute-start(bf16[1024,512]{1,0:T(8,128)(2,1)} %all-gather.3.cloned.1.call-done.refs_0_), channel_id=1, source_target_pairs={{0,16},{16,0},{1,17},{17,1},{2,18},{18,2},{3,19},{19,3},{4,20},{20... | collective-permute-start | bytes 3145736 | tf_op jit(solution)/shard_map/ppermute | solution.py:693
  163.6 83.0 %collective-permute-start.28 = (bf16[1024,256]{1,0:T(8,128)(2,1)S(1)}, bf16[1024,256]{1,0:T(8,128)(2,1)}, u32[]{:S(2)}, u32[]{:S(2)}) collective-permute-start(bf16[1024,256]{1,0:T(8,128)(2,1)S(1)} %slice.166), channel_id=1, source_target_pairs={{0,16},{16,0},{1,17},{17,1},{2,18},{18,2},{3,19},{19,3},{4,20},{20... | collective-permute-start | bytes 1572872 | tf_op jit(solution)/shard_map/ppermute | solution.py:693
  182.9 63.7 %collective-permute-start.29 = (bf16[1024,256]{1,0:T(8,128)(2,1)}, bf16[1024,256]{1,0:T(8,128)(2,1)}, u32[]{:S(2)}, u32[]{:S(2)}) collective-permute-start(bf16[1024,256]{1,0:T(8,128)(2,1)} %slice.167), channel_id=1, source_target_pairs={{0,2},{2,0},{1,3},{3,1},{4,6},{6,4},{5,7},{7,5},{8,10},{10,8},{9,1... | collective-permute-start | bytes 1572872 | tf_op jit(solution)/shard_map/ppermute | solution.py:693
  183.4 35.7 %collective-permute-start.25 = (bf16[1024,512]{1,0:T(8,128)(2,1)}, bf16[1024,512]{1,0:T(8,128)(2,1)}, u32[]{:S(2)}, u32[]{:S(2)}) collective-permute-start(bf16[1024,512]{1,0:T(8,128)(2,1)} %collective-permute-done.23.refs_1_), channel_id=1, source_target_pairs={{0,16},{16,0},{1,17},{17,1},{2,18},{18,2},{3,19},{19,3},{4,20},{20... | collective-permute-start | bytes 3145736 | tf_op jit(solution)/shard_map/ppermute | solution.py:693
  265.5 200.7 %reduce-scatter.5.cloned.1.call-start = ((), (), s32[]{:S(2)}) async-start(), calls=%async_computation.5 | async-start | bytes 2293760 | tf_op jit(solution)/shard_map/reduce_scatter | solution.py:828
  265.5 29.2 %collective-permute-start.32 = (bf16[1024,512]{1,0:T(8,128)(2,1)}, bf16[1024,512]{1,0:T(8,128)(2,1)}, u32[]{:S(2)}, u32[]{:S(2)}) collective-permute-start(bf16[1024,512]{1,0:T(8,128)(2,1)} %convolution_convert_fusion.6), channel_id=1, source_target_pairs={{0,16},{16,0},{1,17},{17,1},{2,18},{18,2},{3,19},{19,3},{4,20},{20... | collective-permute-start | bytes 3145736 | tf_op jit(solution)/shard_map/ppermute | solution.py:693
  274.6 39.3 %collective-permute-start.34 = (bf16[1024,512]{1,0:T(8,128)(2,1)}, bf16[1024,512]{1,0:T(8,128)(2,1)}, u32[]{:S(2)}, u32[]{:S(2)}) collective-permute-start(bf16[1024,512]{1,0:T(8,128)(2,1)} %convolution_convert_fusion.4), channel_id=1, source_target_pairs={{0,16},{16,0},{1,17},{17,1},{2,18},{18,2},{3,19},{19,3},{4,20},{20... | collective-permute-start | bytes 3145736 | tf_op jit(solution)/shard_map/ppermute | solution.py:693
  274.9 39.1 %collective-permute-start.33 = (bf16[1024,512]{1,0:T(8,128)(2,1)}, bf16[1024,512]{1,0:T(8,128)(2,1)}, u32[]{:S(2)}, u32[]{:S(2)}) collective-permute-start(bf16[1024,512]{1,0:T(8,128)(2,1)} %convolution_convert_fusion.5), channel_id=1, source_target_pairs={{0,2},{2,0},{1,3},{3,1},{4,6},{6,4},{5,7},{7,5},{8,10},{10,8},{9,1... | collective-permute-start | bytes 3145736 | tf_op jit(solution)/shard_map/ppermute | solution.py:693
  314.0 15.6 %collective-permute-start.36 = (bf16[1024,256]{1,0:T(8,128)(2,1)S(1)}, bf16[1024,256]{1,0:T(8,128)(2,1)S(1)}, u32[]{:S(2)}, u32[]{:S(2)}) collective-permute-start(bf16[1024,256]{1,0:T(8,128)(2,1)S(1)} %slice.169), channel_id=1, source_target_pairs={{0,16},{16,0},{1,17},{17,1},{2,18},{18,2},{3,19},{19,3},{4,20},{20... | collective-permute-start | bytes 1572872 | tf_op jit(solution)/shard_map/ppermute | solution.py:693
  327.1 63.4 %collective-permute-start.41 = (bf16[1024,256]{1,0:T(8,128)(2,1)}, bf16[1024,256]{1,0:T(8,128)(2,1)S(1)}, u32[]{:S(2)}, u32[]{:S(2)}) collective-permute-start(bf16[1024,256]{1,0:T(8,128)(2,1)} %slice.172), channel_id=1, source_target_pairs={{0,16},{16,0},{1,17},{17,1},{2,18},{18,2},{3,19},{19,3},{4,20},{20... | collective-permute-start | bytes 1572872 | tf_op jit(solution)/shard_map/ppermute | solution.py:693
  327.6 62.9 %collective-permute-start.40 = (bf16[1024,256]{1,0:T(8,128)(2,1)}, bf16[1024,256]{1,0:T(8,128)(2,1)S(1)}, u32[]{:S(2)}, u32[]{:S(2)}) collective-permute-start(bf16[1024,256]{1,0:T(8,128)(2,1)} %slice.171), channel_id=1, source_target_pairs={{0,2},{2,0},{1,3},{3,1},{4,6},{6,4},{5,7},{7,5},{8,10},{10,8},{9,1... | collective-permute-start | bytes 1572872 | tf_op jit(solution)/shard_map/ppermute | solution.py:693
  328.0 62.4 %collective-permute-start.42 = (bf16[1024,256]{1,0:T(8,128)(2,1)}, bf16[1024,256]{1,0:T(8,128)(2,1)S(1)}, u32[]{:S(2)}, u32[]{:S(2)}) collective-permute-start(bf16[1024,256]{1,0:T(8,128)(2,1)} %slice.173), channel_id=1, source_target_pairs={{0,2},{2,0},{1,3},{3,1},{4,6},{6,4},{5,7},{7,5},{8,10},{10,8},{9,1... | collective-permute-start | bytes 1572872 | tf_op jit(solution)/shard_map/ppermute | solution.py:693
  330.6 28.8 %collective-permute-start.37 = (bf16[256,512]{1,0:T(8,128)(2,1)S(1)}, bf16[256,512]{1,0:T(8,128)(2,1)S(1)}, u32[]{:S(2)}, u32[]{:S(2)}) collective-permute-start(bf16[256,512]{1,0:T(8,128)(2,1)S(1)} %slice.143), channel_id=1, source_target_pairs={{0,2},{2,0},{1,3},{3,1},{4,6},{6,4},{5,7},{7,5},{8,10},{10,8},{9,1... | collective-permute-start | bytes 786440 | tf_op jit(solution)/shard_map/ppermute | solution.py:693
  332.4 56.4 %collective-permute-start.43 = (bf16[1024,128]{1,0:T(8,128)(2,1)S(1)}, bf16[1024,128]{1,0:T(8,128)(2,1)S(1)}, u32[]{:S(2)}, u32[]{:S(2)}) collective-permute-start(bf16[1024,128]{1,0:T(8,128)(2,1)S(1)} %slice.174), channel_id=1, source_target_pairs={{0,2},{2,0},{1,3},{3,1},{4,6},{6,4},{5,7},{7,5},{8,10},{10,8},{9,1... | collective-permute-start | bytes 786440 | tf_op jit(solution)/shard_map/ppermute | solution.py:693
  407.9 20.7 %collective-permute-start.45 = (bf16[1024,384]{1,0:T(8,128)(2,1)}, bf16[1024,384]{1,0:T(8,128)(2,1)S(1)}, u32[]{:S(2)}, u32[]{:S(2)}) collective-permute-start(bf16[1024,384]{1,0:T(8,128)(2,1)} %add_convert_fusion.4), channel_id=1, source_target_pairs={{0,2},{2,0},{1,3},{3,1},{4,6},{6,4},{5,7},{7,5},{8,10},{10,8},{9,1... | collective-permute-start | bytes 2359304 | tf_op jit(solution)/shard_map/ppermute | solution.py:693
  409.4 20.0 %collective-permute-start.44 = (bf16[1024,384]{1,0:T(8,128)(2,1)}, bf16[1024,384]{1,0:T(8,128)(2,1)}, u32[]{:S(2)}, u32[]{:S(2)}) collective-permute-start(bf16[1024,384]{1,0:T(8,128)(2,1)} %add_convert_fusion.5), channel_id=1, source_target_pairs={{0,16},{16,0},{1,17},{17,1},{2,18},{18,2},{3,19},{19,3},{4,20},{20... | collective-permute-start | bytes 2359304 | tf_op jit(solution)/shard_map/ppermute | solution.py:693
  409.9 31.5 %collective-permute-start.35 = (bf16[1184,256]{1,0:T(8,128)(2,1)}, bf16[1184,256]{1,0:T(8,128)(2,1)}, u32[]{:S(2)}, u32[]{:S(2)}) collective-permute-start(bf16[1184,256]{1,0:T(8,128)(2,1)} %get-tuple-element.135), channel_id=1, source_target_pairs={{0,2},{2,0},{1,3},{3,1},{4,6},{6,4},{5,7},{7,5},{8,10},{10,8},{9,1... | collective-permute-start | bytes 1818632 | tf_op jit(solution)/shard_map/ppermute | solution.py:693
  430.8 15.9 %collective-permute-start.54 = (f32[12,256]{1,0:T(8,128)S(1)}, f32[12,256]{1,0:T(8,128)S(1)}, u32[]{:S(2)}, u32[]{:S(2)}) collective-permute-start(f32[12,256]{1,0:T(8,128)S(1)} %copy-done.48), channel_id=1, source_target_pairs={{0,2},{2,0},{1,3},{3,1},{4,6},{6,4},{5,7},{7,5},{8,10},{10,8},{9,1... | collective-permute-start | bytes 36872 | tf_op jit(solution)/shard_map/ppermute | solution.py:693
  441.4 21.5 %collective-permute-start.48 = (bf16[256,384]{1,0:T(8,128)(2,1)}, bf16[256,384]{1,0:T(8,128)(2,1)}, u32[]{:S(2)}, u32[]{:S(2)}) collective-permute-start(bf16[256,384]{1,0:T(8,128)(2,1)} %get-tuple-element.205), channel_id=1, source_target_pairs={{0,4},{4,8},{8,12},{12,0},{1,5},{5,9},{9,13},{13,1},{2,6},{6,10},{... | collective-permute-start | bytes 589832 | tf_op jit(solution)/shard_map/ppermute | solution.py:696
  441.4 22.1 %collective-permute-start.50 = (bf16[256,384]{1,0:T(8,128)(2,1)}, bf16[256,384]{1,0:T(8,128)(2,1)}, u32[]{:S(2)}, u32[]{:S(2)}) collective-permute-start(bf16[256,384]{1,0:T(8,128)(2,1)} %get-tuple-element.206), channel_id=1, source_target_pairs={{0,12},{4,0},{8,4},{12,8},{1,13},{5,1},{9,5},{13,9},{2,14},{6,2},{... | collective-permute-start | bytes 589832 | tf_op jit(solution)/shard_map/ppermute | solution.py:696
  445.2 18.3 %collective-permute-start.49 = (bf16[256,384]{1,0:T(8,128)(2,1)S(1)}, bf16[256,384]{1,0:T(8,128)(2,1)}, u32[]{:S(2)}, u32[]{:S(2)}) collective-permute-start(bf16[256,384]{1,0:T(8,128)(2,1)S(1)} %get-tuple-element.207), channel_id=1, source_target_pairs={{0,8},{4,12},{8,0},{12,4},{1,9},{5,13},{9,1},{13,5},{2,10},{6,14},... | collective-permute-start | bytes 589832 | tf_op jit(solution)/shard_map/ppermute | solution.py:696
  445.2 21.6 %collective-permute-start.47 = (bf16[1184,256]{1,0:T(8,128)(2,1)}, bf16[1184,256]{1,0:T(8,128)(2,1)}, u32[]{:S(2)}, u32[]{:S(2)}) collective-permute-start(bf16[1184,256]{1,0:T(8,128)(2,1)} %get-tuple-element.165), channel_id=1, source_target_pairs={{0,2},{2,0},{1,3},{3,1},{4,6},{6,4},{5,7},{7,5},{8,10},{10,8},{9,1... | collective-permute-start | bytes 1818632 | tf_op jit(solution)/shard_map/ppermute | solution.py:693
  462.8 24.2 %collective-permute-start.57 = (f32[12,256]{1,0:T(8,128)S(1)}, f32[12,256]{1,0:T(8,128)S(1)}, u32[]{:S(2)}, u32[]{:S(2)}) collective-permute-start(f32[12,256]{1,0:T(8,128)S(1)} %add.145.a_ref), channel_id=1, source_target_pairs={{0,16},{16,0},{1,17},{17,1},{2,18},{18,2},{3,19},{19,3},{4,20},{20... | collective-permute-start | bytes 36872 | tf_op jit(solution)/shard_map/ppermute | solution.py:693
  464.7 24.3 %collective-permute-start.51 = (bf16[256,384]{1,0:T(8,128)(2,1)S(1)}, bf16[256,384]{1,0:T(8,128)(2,1)}, u32[]{:S(2)}, u32[]{:S(2)}) collective-permute-start(bf16[256,384]{1,0:T(8,128)(2,1)S(1)} %add_convert_fusion.8.mine_ref), channel_id=1, source_target_pairs={{0,16},{16,0},{1,17},{17,1},{2,18},{18,2},{3,19},{19,3},{4,20},{20... | collective-permute-start | bytes 589832 | tf_op jit(solution)/shard_map/ppermute | solution.py:693
  466.2 17.8 %collective-permute-start.52 = (bf16[256,896]{1,0:T(8,128)(2,1)}, bf16[256,896]{1,0:T(8,128)(2,1)}, u32[]{:S(2)}, u32[]{:S(2)}) collective-permute-start(bf16[256,896]{1,0:T(8,128)(2,1)} %reduce-scatter.5.cloned.1.call-done.mine_ref), channel_id=1, source_target_pairs={{0,16},{16,0},{1,17},{17,1},{2,18},{18,2},{3,19},{19,3},{4,20},{20... | collective-permute-start | bytes 1376264 | tf_op jit(solution)/shard_map/ppermute | solution.py:693
  (70 other events, 936.3 us)
Sparse Core Ops, SparseCore 0:
  52.0 26.6 all-gather.4
  83.9 25.2 all-gather.2
  265.6 41.0 reduce-scatter.2
  408.0 36.9 reduce-scatter.4
